TPU v7x, 32 devices: a whole 2x2x4 slice. The times are simulated.
32 devices in a mesh: heads: 4 (over z), rows: 8 (over y, x, core).
Axes of the slice: x: 2, y: 2, z: 4, core: 2. Of those that a mesh axis runs over, the one named last changes fastest.
Arguments:
- tokens: bfloat16 [4, 2048, 1024], P(None, 'rows'), may hold values from -6 to 6
- cam_index: int32 [4, 2048], P(None, 'rows'), may hold values from 0 to 31
- patches: bfloat16 [4, 2048, 768], P(None, 'rows'), may hold values from -6 to 6
- patch_len: int32 [4], replicated, may hold values from 512 to 2048, as said below
- camera_table: bfloat16 [32, 2, 1024], replicated, may hold values from -3 to 3
- self_weights: bfloat16 [3, 1024, 1024], P(None, None, 'heads'), may hold values from -0.1875 to 0.1875
- self_output: bfloat16 [1024, 1024], P('heads'), may hold values from -4 to 4
- cross_gain: bfloat16 [1024], replicated, may hold values from 0.5 to 1.5
- cross_query: bfloat16 [1024, 1024], P(None, 'heads'), may hold values from -0.1875 to 0.1875
- cross_pair: bfloat16 [2, 1024, 1024], P(None, None, 'heads'), may hold values from -0.1875 to 0.1875
- cross_output: bfloat16 [1024, 1024], P('heads'), may hold values from -4 to 4
- patch_weights: bfloat16 [768, 1024], replicated, may hold values from -0.21875 to 0.21875
- hidden_gain: bfloat16 [1024], replicated, may hold values from 0.5 to 1.5
- widen_weights: bfloat16 [1024, 4096], P(None, 'heads'), may hold values from -0.1875 to 0.1875
- narrow_weights: bfloat16 [4096, 1024], P('heads'), may hold values from -0.09375 to 0.09375
- cotangent: bfloat16 [4, 2048, 1024], P(None, 'rows'), may hold values from -6 to 6
Outputs:
- tokens_out: bfloat16 [4, 2048, 1024], P(None, 'rows')
- input_grad: float32 [4, 2048, 1024], P(None, 'rows')
- patch_grad: float32 [4, 2048, 768], P(None, 'rows')
- grad_camera_table: float32 [32, 2, 1024], P(None, None, 'heads')
- grad_self_weights: float32 [3, 1024, 1024], P(None, None, 'heads')
- grad_self_output: float32 [1024, 1024], P('heads')
- grad_cross_gain: float32 [1024], P('heads')
- grad_cross_query: float32 [1024, 1024], P(None, 'heads')
- grad_cross_pair: float32 [2, 1024, 1024], P(None, None, 'heads')
- grad_cross_output: float32 [1024, 1024], P('heads')
- grad_patch_weights: float32 [768, 1024], P(None, 'heads')
- grad_hidden_gain: float32 [1024], P('heads')
- grad_widen_weights: float32 [1024, 4096], P(None, 'heads')
- grad_narrow_weights: float32 [4096, 1024], P('heads')
Inputs may be any that keep to these rules, and one draw needn't show every extreme that they name: `patch_len`: each entry is 2048 or a quarter of 2048; both values occur in every draw. Live patch tokens are the first ones of the object.
All inputs are finite; a program needn't handle non-finite values.
Results may differ from a plain program's by a relative error of at most 0.028.
The roundings to bfloat16 on the way count: a program that leaves them out, or rounds other values in their place, can miss the bound.
Values may be sent and summed in bfloat16 or wider, within the bound.
No kernel may reach another device: no remote copies, remote signals or barrier semaphores. Data moves between devices by JAX's collectives and lax.ppermute only.
A program may use at most 448 MiB of HBM per device.

v0:
```python
from functools import reduce

import jax
import jax.numpy as jnp
from jax import lax
from jax.sharding import PartitionSpec as P

HEAD_DIM = 64


EPSILON = 1e-05


def layer_norm(inputs):
    centred = inputs - jnp.mean(inputs, axis=-1, keepdims=True)
    return centred * lax.rsqrt(jnp.mean(centred * centred, axis=-1, keepdims=True) + EPSILON)


def modulated(inputs, shift_scale):
    return layer_norm(inputs) * (1.0 + shift_scale[:, 0]) + shift_scale[:, 1]


def gained(inputs, gain_row):
    return layer_norm(inputs) * gain_row


def gelu_tanh(pre_act):
    return jax.nn.gelu(pre_act, approximate=True)


def by_heads(matrix):
    return matrix.reshape(matrix.shape[0], -1, HEAD_DIM)


def scaled_scores(queries, key_rows):
    return jnp.einsum(
        "qhe,khe->hqk", queries, key_rows, preferred_element_type=jnp.float32
    ) * HEAD_DIM ** (-0.5)


def attend_forward(queries, key_rows, value_rows, mask_add):
    scores = scaled_scores(queries, key_rows) + mask_add
    row_peak = jnp.max(scores, axis=-1, keepdims=True)
    raised = jnp.exp(scores - row_peak)
    row_total = jnp.sum(raised, axis=-1, keepdims=True)
    attn_probs = (raised / row_total).astype(jnp.bfloat16)
    mixed_out = jnp.einsum(
        "hqk,khe->qhe", attn_probs, value_rows, preferred_element_type=jnp.float32
    )
    return (mixed_out.reshape(mixed_out.shape[0], -1).astype(jnp.bfloat16), row_peak, row_total)


def attend_queries_back(queries, key_rows, value_rows, mask_add, row_peak, row_total, grad_mixed):
    score_scale = HEAD_DIM ** (-0.5)
    scores = scaled_scores(queries, key_rows) + mask_add
    attn_probs = jnp.exp(scores - row_peak) / row_total
    grad_probs = jnp.einsum(
        "qhe,khe->hqk", grad_mixed, value_rows, preferred_element_type=jnp.float32
    )
    spread = jnp.sum(attn_probs * grad_probs, axis=-1, keepdims=True)
    grad_scores = (attn_probs * (grad_probs - spread)).astype(jnp.bfloat16)
    grad_queries = (
        jnp.einsum("hqk,khe->qhe", grad_scores, key_rows, preferred_element_type=jnp.float32)
        * score_scale
    )
    return (grad_queries, spread)


def attend_keys_back(
    all_queries, key_rows, value_rows, mask_add, all_peak, all_total, all_spread, all_grad
):
    score_scale = HEAD_DIM ** (-0.5)
    scores = scaled_scores(all_queries, key_rows) + mask_add
    attn_probs = jnp.exp(scores - all_peak) / all_total
    grad_probs = jnp.einsum(
        "qhe,khe->hqk", all_grad, value_rows, preferred_element_type=jnp.float32
    )
    grad_scores = (attn_probs * (grad_probs - all_spread)).astype(jnp.bfloat16)
    grad_keys = (
        jnp.einsum("hqk,qhe->khe", grad_scores, all_queries, preferred_element_type=jnp.float32)
        * score_scale
    )
    grad_values = jnp.einsum(
        "hqk,qhe->khe",
        attn_probs.astype(jnp.bfloat16),
        all_grad,
        preferred_element_type=jnp.float32,
    )
    return (grad_keys, grad_values)


def owner_key_grads(
    queries, grad_mixed, row_peak, row_total, spread, own_keys, own_values, own_mask
):
    gathered_queries, gathered_grads = (
        lax.all_gather(queries, "rows", axis=0, tiled=True),
        lax.all_gather(grad_mixed, "rows", axis=0, tiled=True),
    )
    gathered_peak, gathered_total, gathered_spread = (
        lax.all_gather(row_peak[:, :, 0].T, "rows", axis=0, tiled=True),
        lax.all_gather(row_total[:, :, 0].T, "rows", axis=0, tiled=True),
        lax.all_gather(spread[:, :, 0].T, "rows", axis=0, tiled=True),
    )
    grad_keys, grad_values = attend_keys_back(
        by_heads(gathered_queries),
        by_heads(own_keys),
        by_heads(own_values),
        own_mask,
        gathered_peak.T[:, :, None],
        gathered_total.T[:, :, None],
        gathered_spread.T[:, :, None],
        by_heads(gathered_grads),
    )
    return (grad_keys.reshape(own_keys.shape[0], -1), grad_values.reshape(own_keys.shape[0], -1))


def add_trees(former, latter):
    return jax.tree.map(jnp.add, former, latter)


def per_device(
    tokens,
    cam_index,
    patches,
    patch_len,
    camera_table,
    self_weights,
    self_output,
    cross_gain,
    cross_query,
    cross_pair,
    cross_output,
    patch_weights,
    hidden_gain,
    widen_weights,
    narrow_weights,
    cotangent,
):
    batches = tokens.shape[0]
    row_count = tokens.shape[1]
    model_width = tokens.shape[2]
    local_cols = self_weights.shape[2]
    code_count = camera_table.shape[0]
    patch_rows = patches.shape[1]
    row_rank = lax.axis_index("rows")
    head_rank = lax.axis_index("heads")
    all_patches = patch_rows * lax.axis_size("rows")
    table_flat = camera_table.reshape(code_count, -1).astype(jnp.float32)
    patch_index = jnp.arange(all_patches)
    own_index = row_rank * patch_rows + jnp.arange(patch_rows)
    cross_gain_f = cross_gain.astype(jnp.float32)
    hidden_gain_f = hidden_gain.astype(jnp.float32)
    outputs = []
    input_grads = []
    patch_grads = []
    contributions = []
    for microbatch in range(batches):
        inputs = tokens[microbatch].astype(jnp.float32)
        onehot = (cam_index[microbatch][:, None] == jnp.arange(code_count)[None, :]).astype(
            jnp.float32
        )
        shift_scale = jnp.dot(onehot, table_flat, precision=lax.Precision.HIGHEST).reshape(
            row_count, 2, model_width
        )
        normed_one, norm_one_back = jax.vjp(modulated, inputs, shift_scale)
        normed_one_low = normed_one.astype(jnp.bfloat16)
        projected = jnp.einsum(
            "rd,tdc->trc", normed_one_low, self_weights, preferred_element_type=jnp.float32
        ).astype(jnp.bfloat16)
        queries = projected[0]
        all_keys, all_values = (
            lax.all_gather(projected[1], "rows", axis=0, tiled=True),
            lax.all_gather(projected[2], "rows", axis=0, tiled=True),
        )
        self_mixed, self_peak, self_total = attend_forward(
            by_heads(queries), by_heads(all_keys), by_heads(all_values), 0.0
        )
        attn_sum = lax.psum(
            jnp.dot(self_mixed, self_output, preferred_element_type=jnp.float32), "heads"
        )
        after_self = inputs + attn_sum
        normed_two, norm_two_back = jax.vjp(gained, after_self, cross_gain_f)
        normed_two_low = normed_two.astype(jnp.bfloat16)
        cross_queries = jnp.dot(
            normed_two_low, cross_query, preferred_element_type=jnp.float32
        ).astype(jnp.bfloat16)
        patch_mid = jnp.dot(
            patches[microbatch], patch_weights, preferred_element_type=jnp.float32
        ).astype(jnp.bfloat16)
        patch_pair = jnp.einsum(
            "pd,tdc->tpc", patch_mid, cross_pair, preferred_element_type=jnp.float32
        ).astype(jnp.bfloat16)
        own_keys = patch_pair[0]
        own_values = patch_pair[1]
        cross_keys_all, cross_values_all = (
            lax.all_gather(own_keys, "rows", axis=0, tiled=True),
            lax.all_gather(own_values, "rows", axis=0, tiled=True),
        )
        mask_add = jnp.where(patch_index < patch_len[microbatch], 0.0, -1e30).astype(jnp.float32)
        cross_mixed, cross_peak, cross_total = attend_forward(
            by_heads(cross_queries), by_heads(cross_keys_all), by_heads(cross_values_all), mask_add
        )
        cross_sum = lax.psum(
            jnp.dot(cross_mixed, cross_output, preferred_element_type=jnp.float32).astype(
                jnp.bfloat16
            ),
            "heads",
        ).astype(jnp.float32)
        after_cross = after_self + cross_sum
        normed_three, norm_three_back = jax.vjp(gained, after_cross, hidden_gain_f)
        normed_three_low = normed_three.astype(jnp.bfloat16)
        pre_act = jnp.dot(normed_three_low, widen_weights, preferred_element_type=jnp.float32)
        activated, act_back = jax.vjp(gelu_tanh, pre_act)
        activated_low = activated.astype(jnp.bfloat16)
        hidden_sum = lax.psum(
            jnp.dot(activated_low, narrow_weights, preferred_element_type=jnp.float32).astype(
                jnp.bfloat16
            ),
            "heads",
        ).astype(jnp.float32)
        outputs.append((after_cross + hidden_sum).astype(jnp.bfloat16))
        grad_low = cotangent[microbatch]
        grad_top = grad_low.astype(jnp.float32)
        narrow_term = jnp.einsum(
            "rf,rd->fd", activated_low, grad_low, preferred_element_type=jnp.float32
        )
        grad_act = jnp.einsum(
            "rd,fd->rf", grad_low, narrow_weights, preferred_element_type=jnp.float32
        )
        grad_pre = act_back(grad_act)[0].astype(jnp.bfloat16)
        widen_term = jnp.einsum(
            "rd,rf->df", normed_three_low, grad_pre, preferred_element_type=jnp.float32
        )
        grad_normed_three = lax.psum(
            jnp.einsum(
                "rf,df->rd", grad_pre, widen_weights, preferred_element_type=jnp.float32
            ).astype(jnp.bfloat16),
            "heads",
        ).astype(jnp.float32)
        grad_mid, hidden_gain_term = norm_three_back(grad_normed_three)
        grad_cross = grad_top + grad_mid
        grad_cross_low = grad_cross.astype(jnp.bfloat16)
        cross_output_term = jnp.einsum(
            "rc,rd->cd", cross_mixed, grad_cross_low, preferred_element_type=jnp.float32
        )
        grad_cross_mixed = jnp.einsum(
            "rd,cd->rc", grad_cross_low, cross_output, preferred_element_type=jnp.float32
        ).astype(jnp.bfloat16)
        grad_cq, cross_spread = attend_queries_back(
            by_heads(cross_queries),
            by_heads(cross_keys_all),
            by_heads(cross_values_all),
            mask_add,
            cross_peak,
            cross_total,
            by_heads(grad_cross_mixed),
        )
        own_mask = jnp.where(own_index < patch_len[microbatch], 0.0, -1e30).astype(jnp.float32)
        grad_ck, grad_cv = owner_key_grads(
            cross_queries,
            grad_cross_mixed,
            cross_peak,
            cross_total,
            cross_spread,
            own_keys,
            own_values,
            own_mask,
        )
        grad_pair_low = jnp.stack([grad_ck, grad_cv]).astype(jnp.bfloat16)
        pair_term = jnp.einsum(
            "pd,tpc->tdc", patch_mid, grad_pair_low, preferred_element_type=jnp.float32
        )
        grad_cq_low = grad_cq.reshape(row_count, -1).astype(jnp.bfloat16)
        query_term = jnp.einsum(
            "rd,rc->dc", normed_two_low, grad_cq_low, preferred_element_type=jnp.float32
        )
        grad_normed_two, grad_patch_mid = (
            lax.psum(
                jnp.einsum(
                    "rc,dc->rd", grad_cq_low, cross_query, preferred_element_type=jnp.float32
                ).astype(jnp.bfloat16),
                "heads",
            ).astype(jnp.float32),
            lax.psum(
                jnp.einsum(
                    "tpc,tdc->pd", grad_pair_low, cross_pair, preferred_element_type=jnp.float32
                ).astype(jnp.bfloat16),
                "heads",
            ).astype(jnp.float32),
        )
        grad_mid_low = grad_patch_mid.astype(jnp.bfloat16)
        own_columns = lax.dynamic_slice_in_dim(grad_mid_low, head_rank * local_cols, local_cols, 1)
        patch_term = jnp.einsum(
            "pe,pc->ec", patches[microbatch], own_columns, preferred_element_type=jnp.float32
        )
        patch_grads.append(
            jnp.einsum("pd,ed->pe", grad_mid_low, patch_weights, preferred_element_type=jnp.float32)
        )
        grad_after_self, cross_gain_term = norm_two_back(grad_normed_two)
        grad_self = grad_cross + grad_after_self
        grad_self_low = grad_self.astype(jnp.bfloat16)
        self_output_term = jnp.einsum(
            "rc,rd->cd", self_mixed, grad_self_low, preferred_element_type=jnp.float32
        )
        grad_self_mixed = jnp.einsum(
            "rd,cd->rc", grad_self_low, self_output, preferred_element_type=jnp.float32
        ).astype(jnp.bfloat16)
        grad_q, self_spread = attend_queries_back(
            by_heads(queries),
            by_heads(all_keys),
            by_heads(all_values),
            0.0,
            self_peak,
            self_total,
            by_heads(grad_self_mixed),
        )
        grad_k, grad_v = owner_key_grads(
            queries,
            grad_self_mixed,
            self_peak,
            self_total,
            self_spread,
            projected[1],
            projected[2],
            0.0,
        )
        grad_proj = jnp.stack([grad_q.reshape(row_count, -1), grad_k, grad_v]).astype(jnp.bfloat16)
        self_term = jnp.einsum(
            "rd,trc->tdc", normed_one_low, grad_proj, preferred_element_type=jnp.float32
        )
        grad_normed_one = lax.psum(
            jnp.einsum(
                "trc,tdc->rd", grad_proj, self_weights, preferred_element_type=jnp.float32
            ).astype(jnp.bfloat16),
            "heads",
        ).astype(jnp.float32)
        grad_inputs, grad_shift_scale = norm_one_back(grad_normed_one)
        table_term = jnp.dot(
            onehot.T, grad_shift_scale.reshape(row_count, -1), precision=lax.Precision.HIGHEST
        )
        input_grads.append(grad_self + grad_inputs)
        contributions.append(
            (
                table_term,
                self_term,
                self_output_term,
                cross_gain_term,
                query_term,
                pair_term,
                cross_output_term,
                patch_term,
                hidden_gain_term,
                widen_term,
                narrow_term,
            )
        )
    summed = reduce(add_trees, contributions)
    table_part = lax.dynamic_slice_in_dim(
        summed[0].reshape(code_count, 2, model_width), head_rank * local_cols, local_cols, 2
    )
    cross_gain_part = lax.dynamic_slice_in_dim(summed[3], head_rank * local_cols, local_cols, 0)
    hidden_gain_part = lax.dynamic_slice_in_dim(summed[8], head_rank * local_cols, local_cols, 0)
    totals = (
        lax.psum(table_part.astype(jnp.bfloat16), "rows").astype(jnp.float32),
        lax.psum(summed[1].astype(jnp.bfloat16), "rows").astype(jnp.float32),
        lax.psum(summed[2].astype(jnp.bfloat16), "rows").astype(jnp.float32),
        lax.psum(cross_gain_part.astype(jnp.bfloat16), "rows").astype(jnp.float32),
        lax.psum(summed[4].astype(jnp.bfloat16), "rows").astype(jnp.float32),
        lax.psum(summed[5].astype(jnp.bfloat16), "rows").astype(jnp.float32),
        lax.psum(summed[6].astype(jnp.bfloat16), "rows").astype(jnp.float32),
        lax.psum(summed[7].astype(jnp.bfloat16), "rows").astype(jnp.float32),
        lax.psum(hidden_gain_part.astype(jnp.bfloat16), "rows").astype(jnp.float32),
        lax.psum(summed[9].astype(jnp.bfloat16), "rows").astype(jnp.float32),
        lax.psum(summed[10].astype(jnp.bfloat16), "rows").astype(jnp.float32),
    )
    return (jnp.stack(outputs), jnp.stack(input_grads), jnp.stack(patch_grads)) + tuple(totals)


def solution(mesh):
    in_specs = (
        P(None, "rows", None),
        P(None, "rows"),
        P(None, "rows", None),
        P(),
        P(),
        P(None, None, "heads"),
        P("heads", None),
        P(),
        P(None, "heads"),
        P(None, None, "heads"),
        P("heads", None),
        P(),
        P(),
        P(None, "heads"),
        P("heads", None),
        P(None, "rows", None),
    )
    out_specs = (
        P(None, "rows", None),
        P(None, "rows", None),
        P(None, "rows", None),
        P(None, None, "heads"),
        P(None, None, "heads"),
        P("heads", None),
        P("heads"),
        P(None, "heads"),
        P(None, None, "heads"),
        P("heads", None),
        P(None, "heads"),
        P("heads"),
        P(None, "heads"),
        P("heads", None),
    )
    return jax.shard_map(
        per_device, mesh=mesh, in_specs=in_specs, out_specs=out_specs, check_vma=False
    )
```

profile of v0, /device:TPU:0, one launch (start us, length us, event | category | flops | bytes accessed | tf_op | source)
XLA Modules:
  0.0 1912.8 jit_solution(12267981073876656317)
XLA Ops:
  36.8 9.2 all-gather.87.cloned.1.call-done
  54.1 17.4 all-gather.85.cloned.1.call-done
  78.5 19.1 all-gather.103.cloned.1.call-done
  105.1 17.8 all-gather.101.cloned.1.call-done
  128.6 20.3 %all-gather.95.cloned.1.call-done = bf16[1,2048,256]{1,2,0:T(8,128)(2,1)} async-done(((bf16[1,256,256]{1,2,0:T(8,128)(2,1)}), bf16[1,2048,256]{1,2,0:T(8,128)(2,1)}) %all-gather.95.cloned.1.call-update) | async-done | bytes 1048592 | tf_op jit(solution)/shard_map/all_gather | solution.py:172
  156.3 17.9 all-gather.93.cloned.1.call-done
  179.8 19.8 %all-gather.79.cloned.1.call-done = bf16[1,2048,256]{1,2,0:T(8,128)(2,1)} async-done(((bf16[1,256,256]{1,2,0:T(8,128)(2,1)}), bf16[1,2048,256]{1,2,0:T(8,128)(2,1)}) %all-gather.79.cloned.1.call-update) | async-done | bytes 1048592 | tf_op jit(solution)/shard_map/all_gather | solution.py:172
  210.0 15.2 all-gather.77.cloned.1.call-done
  262.0 9.0 all_gather.196
  271.0 8.1 all_gather.195
  279.1 9.0 all_gather.191
  288.1 8.1 all_gather.190
  296.3 9.0 all_gather.186
  305.3 8.1 all_gather.185
  331.7 9.1 all_gather.201
  340.8 8.1 all_gather.200
  348.9 112.9 %all-reduce.22.cloned.1.call-done = (f32[256,1024]{1,0:T(8,128)}, f32[256,1024]{1,0:T(8,128)}, f32[256,1024]{1,0:T(8,128)}, f32[256,1024]{1,0:T(8,128)}) async-done(((f32[256,1024]{1,0:T(8,128)}, f32[256,1024]{1,0:T(8,128)}, f32[256,1024]{1,0:T(8,128)}, f32[256,1024]{1,0:T(8,128)}), (f32[256,1024]{1,0:T(8,128)}, f32[256,1024]{1,0:T(8,128)}, f32[256,1024]{1,0:T(8,128)}, ...) | async-done | bytes 4194320 | tf_op jit(solution)/shard_map/psum | solution.py:178
  469.0 17.5 all-gather.115.cloned.1.call-done
  494.1 17.8 all-gather.107.cloned.1.call-done
  516.7 10.0 all_gather.221
  526.7 9.1 all_gather.220
  547.8 15.2 all-gather.89.cloned.1.call-done
  568.9 19.6 %all-gather.83.cloned.1.call-done = bf16[1,2048,256]{1,2,0:T(8,128)(2,1)} async-done(((bf16[1,256,256]{1,2,0:T(8,128)(2,1)}), bf16[1,2048,256]{1,2,0:T(8,128)(2,1)}) %all-gather.83.cloned.1.call-update) | async-done | bytes 1048592 | tf_op jit(solution)/shard_map/all_gather | solution.py:196
  596.9 17.1 all-gather.81.cloned.1.call-done
  619.9 19.8 %all-gather.99.cloned.1.call-done = bf16[1,2048,256]{1,2,0:T(8,128)(2,1)} async-done(((bf16[1,256,256]{1,2,0:T(8,128)(2,1)}), bf16[1,2048,256]{1,2,0:T(8,128)(2,1)}) %all-gather.99.cloned.1.call-update) | async-done | bytes 1048592 | tf_op jit(solution)/shard_map/all_gather | solution.py:196
  647.5 10.0 all_gather.216
  657.5 9.1 all_gather.215
  666.6 10.1 all_gather.211
  684.9 9.1 all_gather.210
  694.0 9.9 all_gather.206
  704.0 9.1 all_gather.205
  729.2 13.1 all-gather.69.cloned.1.call-done
  748.5 19.4 %all-gather.65.cloned.1.call-done = bf16[2048,256]{0,1:T(8,128)(2,1)} async-done(((bf16[256,256]{0,1:T(8,128)(2,1)}), bf16[2048,256]{0,1:T(8,128)(2,1)}) %all-gather.65.cloned.1.call-update) | async-done | bytes 1048592 | tf_op jit(solution)/shard_map/all_gather | solution.py:96
  774.1 19.4 %all-gather.61.cloned.1.call-done = bf16[2048,256]{0,1:T(8,128)(2,1)} async-done(((bf16[256,256]{0,1:T(8,128)(2,1)}), bf16[2048,256]{0,1:T(8,128)(2,1)}) %all-gather.61.cloned.1.call-update) | async-done | bytes 1048592 | tf_op jit(solution)/shard_map/all_gather | solution.py:96
  799.7 85.7 %all-reduce.32.cloned.1.call-done = (bf16[256,1024]{1,0:T(8,128)(2,1)}, bf16[256,1024]{1,0:T(8,128)(2,1)}, bf16[256,1024]{1,0:T(8,128)(2,1)}, bf16[256,1024]{1,0:T(8,128)(2,1)}) async-done(((bf16[256,1024]{1,0:T(8,128)(2,1)}, bf16[256,1024]{1,0:T(8,128)(2,1)}, bf16[256,1024]{1,0:T(8,128)(2,1)}, bf16[256,1024]{1,0:T(8,128)(2,1)}), (bf16[256,1024]{1,0:T(8,128)(2,1)}, bf16[256,1024]{1,0:T(8,128)(2,1)}, ...) | async-done | bytes 2097168 | tf_op jit(solution)/shard_map/psum | solution.py:203
  940.3 68.7 %all-reduce.30.cloned.1.call-done = (bf16[256,1024]{1,0:T(8,128)(2,1)}, bf16[256,1024]{1,0:T(8,128)(2,1)}, bf16[256,1024]{1,0:T(8,128)(2,1)}, bf16[256,1024]{1,0:T(8,128)(2,1)}) async-done(((bf16[256,1024]{1,0:T(8,128)(2,1)}, bf16[256,1024]{1,0:T(8,128)(2,1)}, bf16[256,1024]{1,0:T(8,128)(2,1)}, bf16[256,1024]{1,0:T(8,128)(2,1)}), (bf16[256,1024]{1,0:T(8,128)(2,1)}, bf16[256,1024]{1,0:T(8,128)(2,1)}, ...) | async-done | bytes 2097168 | tf_op jit(solution)/shard_map/psum | solution.py:234
  1026.3 7.7 multiply_reduce_fusion.3
  1035.1 7.3 multiply_reduce_fusion.1
  1042.4 9.1 all_gather.223
  1051.4 9.0 all_gather.218
  1060.4 7.5 fusion.173
  1076.5 8.6 all_gather.213
  1085.1 7.7 fusion.171
  1094.0 9.0 all_gather.208
  1103.0 7.5 fusion.177
  1111.8 7.9 fusion.175
  1179.4 61.5 %all-reduce.28.cloned.1.call-done = (bf16[256,1024]{1,0:T(8,128)(2,1)}, bf16[256,1024]{1,0:T(8,128)(2,1)}, bf16[256,1024]{1,0:T(8,128)(2,1)}, bf16[256,1024]{1,0:T(8,128)(2,1)}) async-done(((bf16[256,1024]{1,0:T(8,128)(2,1)}, bf16[256,1024]{1,0:T(8,128)(2,1)}, bf16[256,1024]{1,0:T(8,128)(2,1)}, bf16[256,1024]{1,0:T(8,128)(2,1)}), (bf16[256,1024]{1,0:T(8,128)(2,1)}, bf16[256,1024]{1,0:T(8,128)(2,1)}, ...) | async-done | bytes 2097168 | tf_op jit(solution)/shard_map/psum | solution.py:278
  1264.2 8.1 multiply_reduce_fusion.2
  1272.4 10.3 multiply_reduce_fusion.4
  1283.1 8.1 multiply_reduce_fusion.6
  1293.2 9.3 fusion.176
  1302.5 8.1 fusion.174
  1326.5 8.5 fusion.178
  1335.8 10.7 all_gather.198
  1346.5 9.3 all_gather.193
  1355.8 10.2 all_gather.188
  1366.0 9.3 all_gather.203
  1381.0 7.1 fusion.165
  1391.4 7.1 fusion.164
  1407.1 7.1 fusion.163
  1428.0 7.1 fusion.166
  1471.1 204.0 %all-reduce.26.cloned.1.call-done = (bf16[256,1024]{1,0:T(8,128)(2,1)}, bf16[256,1024]{1,0:T(8,128)(2,1)}, bf16[256,1024]{1,0:T(8,128)(2,1)}, bf16[256,1024]{1,0...) async-done(((bf16[256,1024]{1,0:T(8,128)(2,1)}, ...) | async-done | bytes 6291472 | tf_op jit(solution)/shard_map/psum | solution.py:284
  1722.4 24.8 %all-reduce.9 = (bf16[32,2,256]{2,1,0:T(2,128)(2,1)S(1)}, bf16[256]{0:T(256)(128)(2,1)S(1)}, bf16[256]{0:T(256)(128)(2,1)S(1)}) all-reduce(bf16[32,2,256]{2,1,0:T(2,128)(2,1)S(1)} %dynamic-slice_convert_fusion, bf16[256]{0:T(256)(128)(2,1)S(1)} %dynamic_slice.40, ...), channel_id=1, replica_groups=mesh['heads'=4,'rows'=8] {'rows'}, use_global_device_ids=true, to_apply=%region_100.101 | all-reduce | flops 16896 | bytes 67584 | tf_op jit(solution)/shard_map/psum | solution.py:364
  1769.3 116.2 %all-reduce.24.cloned.1.call-done = (bf16[3,1024,256]{1,2,0:T(8,128)(2,1)}, bf16[2,1024,256]{1,2,0:T(8,128)(2,1)}, bf16[768,256]{0,1:T(8,128)(2,1)}, bf16[256,10...) async-done(((bf16[3,1024,256]{1,2,0:T(8,128)(2,1)}, ...) | async-done | bytes 8781840 | tf_op jit(solution)/shard_map/psum | solution.py:365
  (1070 shorter events, 578.0 us)
Async XLA Ops:
  7.2 881.0 %copy-start = (bf16[1024,1024]{1,0:T(8,128)(2,1)S(1)}, bf16[1024,1024]{1,0:T(8,128)(2,1)}, u32[]{:S(2)}) copy-start(bf16[1024,1024]{1,0:T(8,128)(2,1)} %param.29) | copy-start | bytes 6291460
  7.2 38.9 %all-gather.87.cloned.1.call-start = ((), (), s32[]{:S(2)}) async-start(), calls=%async_computation.17 | async-start | bytes 1179648 | tf_op jit(solution)/shard_map/all_gather | solution.py:172
  19.6 51.9 %all-gather.85.cloned.1.call-start = ((), (), s32[]{:S(2)}) async-start(), calls=%async_computation.16 | async-start | bytes 1179648 | tf_op jit(solution)/shard_map/all_gather | solution.py:173
  20.4 77.2 %all-gather.103.cloned.1.call-start = ((), (), s32[]{:S(2)}) async-start(), calls=%async_computation.25 | async-start | bytes 1179648 | tf_op jit(solution)/shard_map/all_gather | solution.py:172
  23.4 99.6 %all-gather.101.cloned.1.call-start = ((), (), s32[]{:S(2)}) async-start(), calls=%async_computation.24 | async-start | bytes 1179648 | tf_op jit(solution)/shard_map/all_gather | solution.py:173
  24.0 124.9 %all-gather.95.cloned.1.call-start = ((), (), s32[]{:S(2)}) async-start(), calls=%async_computation.21 | async-start | bytes 1179648 | tf_op jit(solution)/shard_map/all_gather | solution.py:172
  26.9 147.3 %all-gather.93.cloned.1.call-start = ((), (), s32[]{:S(2)}) async-start(), calls=%async_computation.20 | async-start | bytes 1179648 | tf_op jit(solution)/shard_map/all_gather | solution.py:173
  27.5 172.2 %all-gather.79.cloned.1.call-start = ((), (), s32[]{:S(2)}) async-start(), calls=%async_computation.13 | async-start | bytes 1179648 | tf_op jit(solution)/shard_map/all_gather | solution.py:172
  34.0 191.2 %all-gather.77.cloned.1.call-start = ((), (), s32[]{:S(2)}) async-start(), calls=%async_computation.12 | async-start | bytes 1179648 | tf_op jit(solution)/shard_map/all_gather | solution.py:173
  34.7 278.7 %all-gather.113.cloned.1.call-start = ((), (), s32[]{:S(2)}) async-start(), calls=%async_computation.30 | async-start | bytes 1179648 | tf_op jit(solution)/shard_map/all_gather | solution.py:96
  35.5 284.1 %all-gather.111.cloned.1.call-start = ((), (), s32[]{:S(2)}) async-start(), calls=%async_computation.29 | async-start | bytes 1179648 | tf_op jit(solution)/shard_map/all_gather | solution.py:96
  36.0 289.6 %all-gather.109.cloned.1.call-start = ((), (), s32[]{:S(2)}) async-start(), calls=%async_computation.28 | async-start | bytes 1179648 | tf_op jit(solution)/shard_map/all_gather | solution.py:96
  36.8 425.0 %all-reduce.22.cloned.1.call-start = ((), (), s32[]{:S(2)}) async-start(), calls=%async_computation.32 | async-start | bytes 8388608 | tf_op jit(solution)/shard_map/psum | solution.py:178
  54.1 225.0 %copy-start.262 = (f32[4,256]{1,0:T(4,128)}, f32[4,256]{1,0:T(4,128)S(1)}, u32[]{:S(2)}) copy-start(f32[4,256]{1,0:T(4,128)S(1)} %fusion.7) | copy-start | bytes 12292
  100.2 240.6 %copy-start.224 = (f32[4,256]{1,0:T(4,128)}, f32[4,256]{1,0:T(4,128)S(1)}, u32[]{:S(2)}) copy-start(f32[4,256]{1,0:T(4,128)S(1)} %get-tuple-element.215) | copy-start | bytes 12292
  105.1 226.5 %copy-start.260 = (f32[4,256]{1,0:T(4,128)}, f32[4,256]{1,0:T(4,128)S(1)}, u32[]{:S(2)}) copy-start(f32[4,256]{1,0:T(4,128)S(1)} %fusion.11) | copy-start | bytes 12292
  151.5 119.6 %copy-start.231 = (f32[4,256]{1,0:T(4,128)}, f32[4,256]{1,0:T(4,128)S(1)}, u32[]{:S(2)}) copy-start(f32[4,256]{1,0:T(4,128)S(1)} %get-tuple-element.213) | copy-start | bytes 12292
  156.3 105.7 %copy-start.266 = (f32[4,256]{1,0:T(4,128)}, f32[4,256]{1,0:T(4,128)S(1)}, u32[]{:S(2)}) copy-start(f32[4,256]{1,0:T(4,128)S(1)} %fusion.9) | copy-start | bytes 12292
  202.3 103.0 %copy-start.229 = (f32[4,256]{1,0:T(4,128)}, f32[4,256]{1,0:T(4,128)S(1)}, u32[]{:S(2)}) copy-start(f32[4,256]{1,0:T(4,128)S(1)} %get-tuple-element.217) | copy-start | bytes 12292
  207.3 88.9 %copy-start.264 = (f32[4,256]{1,0:T(4,128)}, f32[4,256]{1,0:T(4,128)S(1)}, u32[]{:S(2)}) copy-start(f32[4,256]{1,0:T(4,128)S(1)} %fusion.5) | copy-start | bytes 12292
  232.8 253.7 %all-gather.115.cloned.1.call-start = ((), (), s32[]{:S(2)}) async-start(), calls=%async_computation.31 | async-start | bytes 1179648 | tf_op jit(solution)/shard_map/all_gather | solution.py:96
  233.5 278.4 %all-gather.107.cloned.1.call-start = ((), (), s32[]{:S(2)}) async-start(), calls=%async_computation.27 | async-start | bytes 1179648 | tf_op jit(solution)/shard_map/all_gather | solution.py:196
  237.9 302.0 %all-gather.91.cloned.1.call-start = ((), (), s32[]{:S(2)}) async-start(), calls=%async_computation.19 | async-start | bytes 1179648 | tf_op jit(solution)/shard_map/all_gather | solution.py:196
  242.2 320.8 %all-gather.89.cloned.1.call-start = ((), (), s32[]{:S(2)}) async-start(), calls=%async_computation.18 | async-start | bytes 1179648 | tf_op jit(solution)/shard_map/all_gather | solution.py:197
  242.8 345.7 %all-gather.83.cloned.1.call-start = ((), (), s32[]{:S(2)}) async-start(), calls=%async_computation.15 | async-start | bytes 1179648 | tf_op jit(solution)/shard_map/all_gather | solution.py:196
  247.0 367.0 %all-gather.81.cloned.1.call-start = ((), (), s32[]{:S(2)}) async-start(), calls=%async_computation.14 | async-start | bytes 1179648 | tf_op jit(solution)/shard_map/all_gather | solution.py:197
  247.6 392.0 %all-gather.99.cloned.1.call-start = ((), (), s32[]{:S(2)}) async-start(), calls=%async_computation.23 | async-start | bytes 1179648 | tf_op jit(solution)/shard_map/all_gather | solution.py:196
  251.3 427.6 %all-gather.105.cloned.1.call-start = ((), (), s32[]{:S(2)}) async-start(), calls=%async_computation.26 | async-start | bytes 1179648 | tf_op jit(solution)/shard_map/all_gather | solution.py:197
  251.9 463.3 %all-gather.97.cloned.1.call-start = ((), (), s32[]{:S(2)}) async-start(), calls=%async_computation.22 | async-start | bytes 1179648 | tf_op jit(solution)/shard_map/all_gather | solution.py:197
  252.7 470.4 %all-gather.73.cloned.1.call-start = ((), (), s32[]{:S(2)}) async-start(), calls=%async_computation.10 | async-start | bytes 1179648 | tf_op jit(solution)/shard_map/all_gather | solution.py:96
  257.7 284.9 %copy-start.215 = (f32[2048]{0:T(1024)}, f32[2048]{0:T(1024)S(1)}, u32[]{:S(2)}) copy-start(f32[2048]{0:T(1024)S(1)} %fusion.404) | copy-start | bytes 24580
  261.4 276.1 %copy-start.155 = (f32[1024]{0:T(1024)}, f32[1024]{0:T(1024)S(1)}, u32[]{:S(2)}) copy-start(f32[1024]{0:T(1024)S(1)} %convert_element_type.678) | copy-start | bytes 12292
  331.7 154.8 %copy-start.188 = (bf16[1,256,256]{1,2,0:T(8,128)(2,1)S(1)}, bf16[1,256,256]{1,2,0:T(8,128)(2,1)}, u32[]{:S(2)}) copy-start(bf16[1,256,256]{1,2,0:T(8,128)(2,1)} %get-tuple-element.177) | copy-start | bytes 393220
  466.4 431.7 %copy-start.7 = (f32[256,1024]{1,0:T(8,128)}, f32[256,1024]{1,0:T(8,128)S(1)}, u32[]{:S(2)}) copy-start(f32[256,1024]{1,0:T(8,128)S(1)} %get-tuple-element.167) | copy-start | bytes 3145732
  468.9 273.5 %all-gather.69.cloned.1.call-start = ((), (), s32[]{:S(2)}) async-start(), calls=%async_computation.8 | async-start | bytes 1179648 | tf_op jit(solution)/shard_map/all_gather | solution.py:96
  494.1 273.8 %all-gather.65.cloned.1.call-start = ((), (), s32[]{:S(2)}) async-start(), calls=%async_computation.6 | async-start | bytes 1179648 | tf_op jit(solution)/shard_map/all_gather | solution.py:96
  539.4 254.1 %all-gather.61.cloned.1.call-start = ((), (), s32[]{:S(2)}) async-start(), calls=%async_computation.4 | async-start | bytes 1179648 | tf_op jit(solution)/shard_map/all_gather | solution.py:96
  568.9 107.8 %copy-start.208 = (bf16[4,64,256]{2,1,0:T(8,128)(2,1)}, bf16[4,64,256]{2,1,0:T(8,128)(2,1)S(1)}, u32[]{:S(2)}) copy-start(bf16[4,64,256]{2,1,0:T(8,128)(2,1)S(1)} %fusion.188) | copy-start | bytes 393220
  684.9 200.5 %all-reduce.32.cloned.1.call-start = ((), (), s32[]{:S(2)}) async-start(), calls=%async_computation.37 | async-start | bytes 4194304 | tf_op jit(solution)/shard_map/psum | solution.py:203
  723.0 285.9 %all-reduce.30.cloned.1.call-start = ((), (), s32[]{:S(2)}) async-start(), calls=%async_computation.36 | async-start | bytes 4194304 | tf_op jit(solution)/shard_map/psum | solution.py:234
  793.5 94.7 %copy-start.142 = (f32[1024]{0:T(1024)S(1)}, f32[1024]{0:T(1024)}, u32[]{:S(2)}) copy-start(f32[1024]{0:T(1024)} %convert_element_type.687) | copy-start | bytes 12292
  921.8 200.4 %all-gather.75.cloned.1.call-start = ((), (), s32[]{:S(2)}) async-start(), calls=%async_computation.11 | async-start | bytes 1179648 | tf_op jit(solution)/shard_map/all_gather | solution.py:97
  1035.0 98.1 %all-gather.71.cloned.1.call-start = ((), (), s32[]{:S(2)}) async-start(), calls=%async_computation.9 | async-start | bytes 1179648 | tf_op jit(solution)/shard_map/all_gather | solution.py:97
  1076.4 68.1 %all-gather.67.cloned.1.call-start = ((), (), s32[]{:S(2)}) async-start(), calls=%async_computation.7 | async-start | bytes 1179648 | tf_op jit(solution)/shard_map/all_gather | solution.py:97
  1093.9 62.6 %all-gather.63.cloned.1.call-start = ((), (), s32[]{:S(2)}) async-start(), calls=%async_computation.5 | async-start | bytes 1179648 | tf_op jit(solution)/shard_map/all_gather | solution.py:97
  1111.7 129.2 %all-reduce.28.cloned.1.call-start = ((), (), s32[]{:S(2)}) async-start(), calls=%async_computation.35 | async-start | bytes 4194304 | tf_op jit(solution)/shard_map/psum | solution.py:278
  1122.1 253.7 %all-gather.57.cloned.1.call-start = ((), (), s32[]{:S(2)}) async-start(), calls=%async_computation.2 | async-start | bytes 1179648 | tf_op jit(solution)/shard_map/all_gather | solution.py:97
  1164.2 79.4 %copy-start.11 = (f32[256,1024]{1,0:T(8,128)S(1)}, f32[256,1024]{1,0:T(8,128)}, u32[]{:S(2)}) copy-start(f32[256,1024]{1,0:T(8,128)} %get-tuple-element.163) | copy-start | bytes 3145732
  1164.2 79.4 %copy-start.220 = (f32[256]{0:T(256)S(1)}, f32[256]{0:T(256)}, u32[]{:S(2)}) copy-start(f32[256]{0:T(256)} %copy-done.219) | copy-start | bytes 3076
  1164.2 79.4 %copy-start.222 = (f32[256]{0:T(256)S(1)}, f32[256]{0:T(256)}, u32[]{:S(2)}) copy-start(f32[256]{0:T(256)} %copy-done.221) | copy-start | bytes 3076
  1258.3 133.1 %all-gather.55.cloned.1.call-start = ((), (), s32[]{:S(2)}) async-start(), calls=%async_computation.1 | async-start | bytes 1179648 | tf_op jit(solution)/shard_map/all_gather | solution.py:97
  1272.3 134.8 %all-gather.53.cloned.1.call-start = ((), (), s32[]{:S(2)}) async-start(), calls=%async_computation | async-start | bytes 1179648 | tf_op jit(solution)/shard_map/all_gather | solution.py:97
  1291.1 131.6 %all-gather.59.cloned.1.call-start = ((), (), s32[]{:S(2)}) async-start(), calls=%async_computation.3 | async-start | bytes 1179648 | tf_op jit(solution)/shard_map/all_gather | solution.py:97
  1375.3 299.8 %all-reduce.26.cloned.1.call-start = ((), (), s32[]{:S(2)}) async-start(), calls=%async_computation.34 | async-start | bytes 12582912 | tf_op jit(solution)/shard_map/psum | solution.py:284
  1449.3 436.2 %all-reduce.24.cloned.1.call-start = ((), (), s32[]{:S(2)}) async-start(), calls=%async_computation.33 | async-start | bytes 17563648 | tf_op jit(solution)/shard_map/psum | solution.py:365
  1469.1 212.1 %copy-start.4 = (bf16[4,256,1024]{2,1,0:T(8,128)(2,1)S(1)}, bf16[4,256,1024]{2,1,0:T(8,128)(2,1)}, u32[]{:S(2)}) copy-start(bf16[4,256,1024]{2,1,0:T(8,128)(2,1)} %param.16) | copy-start | bytes 6291460
  1469.2 212.1 %copy-start.246 = (f32[256]{0:T(256)S(1)}, f32[256]{0:T(256)}, u32[]{:S(2)}) copy-start(f32[256]{0:T(256)} %copy-done.245) | copy-start | bytes 3076
  1469.2 212.1 %copy-start.248 = (f32[256]{0:T(256)S(1)}, f32[256]{0:T(256)}, u32[]{:S(2)}) copy-start(f32[256]{0:T(256)} %copy-done.247) | copy-start | bytes 3076
  1469.2 212.1 %copy-start.250 = (f32[256]{0:T(256)S(1)}, f32[256]{0:T(256)}, u32[]{:S(2)}) copy-start(f32[256]{0:T(256)} %copy-done.249) | copy-start | bytes 3076
  1469.2 212.1 %copy-start.252 = (f32[256]{0:T(256)S(1)}, f32[256]{0:T(256)}, u32[]{:S(2)}) copy-start(f32[256]{0:T(256)} %copy-done.251) | copy-start | bytes 3076
  1471.1 217.4 %copy-start.305 = (f32[256]{0:T(256)S(1)}, f32[256]{0:T(256)}, u32[]{:S(2)}) copy-start(f32[256]{0:T(256)} %copy-done.304) | copy-start | bytes 3076
  1471.1 217.4 %copy-start.303 = (f32[256]{0:T(256)S(1)}, f32[256]{0:T(256)}, u32[]{:S(2)}) copy-start(f32[256]{0:T(256)} %copy-done.302) | copy-start | bytes 3076
  1471.1 217.5 %copy-start.285 = (f32[256]{0:T(256)S(1)}, f32[256]{0:T(256)}, u32[]{:S(2)}) copy-start(f32[256]{0:T(256)} %copy-done.284) | copy-start | bytes 3076
  1471.1 217.5 %copy-start.287 = (f32[256]{0:T(256)S(1)}, f32[256]{0:T(256)}, u32[]{:S(2)}) copy-start(f32[256]{0:T(256)} %copy-done.286) | copy-start | bytes 3076
  (309 other events, 4190.0 us)
Sparse Core Ops, SparseCore 0:
  19.8 26.2 all-gather.86
  47.9 23.5 all-gather.84
  74.0 23.5 all-gather.102
  99.3 23.5 all-gather.100
  125.3 23.5 all-gather.94
  150.6 23.5 all-gather.92
  176.1 23.5 all-gather.78
  201.6 23.5 all-gather.76
  227.6 23.5 all-gather.112
  252.9 23.6 all-gather.110
  278.5 23.6 all-gather.108
  305.7 156.0 all-reduce.21
  463.8 22.6 all-gather.114
  488.4 23.5 all-gather.106
  513.9 23.6 all-gather.90
  539.4 23.5 all-gather.88
  564.9 23.5 all-gather.82
  590.4 23.5 all-gather.80
  616.0 23.5 all-gather.98
  641.5 23.7 all-gather.104
  667.3 23.6 all-gather.96
  693.1 23.6 all-gather.72
  718.8 23.5 all-gather.68
  744.3 23.5 all-gather.64
  769.9 23.5 all-gather.60
  797.3 88.0 all-reduce.31
  921.9 86.9 all-reduce.29
  1035.1 22.6 all-gather.74
  1076.6 21.5 all-gather.70
  1100.1 23.6 all-gather.66
  1126.3 23.6 all-gather.62
  1152.9 87.9 all-reduce.27
  1258.4 22.4 all-gather.56
  1282.8 23.5 all-gather.54
  1308.9 23.6 all-gather.52
  1375.4 22.0 all-gather.58
  1449.4 225.6 all-reduce.25
  1755.1 130.3 all-reduce.23
where the time goes:
time: 1920 us; the launch traced here: 1910 us
  waiting for transfers between devices  953 us (50%)
  matrix products  489 us (25%)
  blocking collectives  245 us (13%)
  other arithmetic  120 us (6%)
  local copies, waits for them, and re-layouts  84.7 us (4%)
    psum x1, waiting for transfers between devices, per_device(): lax.psum(jnp.einsum('tpc,tdc->pd', grad_pair_low, cross_pair, preferred_e...  204 us
    psum x1, waiting for transfers between devices, per_device(): lax.psum(summed[1].astype(jnp.bfloat16), 'rows').astype(jnp.float32)  116 us
    psum x1, waiting for transfers between devices, per_device(): lax.psum(jnp.dot(self_mixed, self_output, preferred_element_type=jnp.floa...  113 us
    psum x1, waiting for transfers between devices, per_device(): lax.psum(jnp.dot(cross_mixed, cross_output, preferred_element_type=jnp.fl...  85.7 us
    all_gather x8, blocking collectives, owner_key_grads(): lax.all_gather(row_total[:, :, 0].T, 'rows', axis=0, tiled=True)  76.2 us
    all_gather x8, blocking collectives, owner_key_grads(): lax.all_gather(spread[:, :, 0].T, 'rows', axis=0, tiled=True)  75.1 us
    dot_general x16, matrix products, scaled_scores(): jnp.einsum('qhe,khe->hqk', queries, key_rows, preferred_element_type=jnp....  70 us
    all_gather x8, waiting for transfers between devices, owner_key_grads(): lax.all_gather(queries, 'rows', axis=0, tiled=True)  69.5 us
  transfers between devices with their start and end apart: 38, of which 23 were waited for; matrix products, arithmetic and copies ran while one was open for 24% of the time, Pallas kernels for 0%

commit v1 on v0

v1 whole, which is shorter than its diff:
```python
import jax
import jax.numpy as jnp
from jax import lax
from jax.experimental import pallas as pl
from jax.experimental.pallas import tpu as pltpu
from jax.sharding import PartitionSpec as P

HEAD_DIM = 64
EPSILON = 1e-05
SCALE = HEAD_DIM ** (-0.5)
LOW = jnp.bfloat16
WIDE = jnp.float32

NN = (((1,), (0,)), ((), ()))
NT = (((1,), (1,)), ((), ()))
TN = (((0,), (0,)), ((), ()))


def mul(left, right, dims=NN):
    return lax.dot_general(left, right, dims, preferred_element_type=WIDE)


def attend_block(scaled_q, keys, values_t, live):
    peak = None
    for c in range(live):
        top = jnp.max(mul(keys(c), scaled_q), axis=0, keepdims=True)
        peak = top if peak is None else jnp.maximum(peak, top)
    total = 0.0
    mixed = 0.0
    for c in range(live):
        raised = jnp.exp(mul(keys(c), scaled_q) - peak)
        total = total + jnp.sum(raised, axis=0, keepdims=True)
        mixed = mixed + mul(values_t(c), raised.astype(LOW))
    return mixed / total, peak + jnp.log(total)


def attend_block_back(scaled_q, queries, grad_t, grad, keys, keys_t, values, log_total, spread):
    probs = jnp.exp(mul(keys, scaled_q) - log_total)
    grad_scores = (probs * (mul(values, grad_t) - spread)).astype(LOW)
    return (mul(keys_t, grad_scores), mul(grad_scores, queries), mul(probs.astype(LOW), grad))


def estimate(rows, cols, passes):
    return pl.CostEstimate(
        flops=int(rows * cols * 1200 * passes), transcendentals=int(rows * cols), bytes_accessed=int(rows * 2048)
    )


VMEM_LIMIT = 48 << 20


def self_forward(qkv):
    blocks, pairs, _, width, rows = qkv.shape

    def kernel(q_ref, k_ref, v_ref, mixed_ref, wide_ref, log_ref, keys):
        @pl.when(pl.program_id(1) == 0)
        def _():
            for c in range(blocks):
                keys[c] = k_ref[c].T

        mixed, log_total = attend_block(
            q_ref[...] * LOW(SCALE), lambda c: keys[c], lambda c: v_ref[c], blocks
        )
        mixed_ref[...] = mixed.astype(LOW)
        wide_ref[...] = mixed
        log_ref[...] = log_total

    block = pl.BlockSpec((None, None, width, rows), lambda p, i: (i, p, 0, 0))
    return pl.pallas_call(
        kernel,
        grid=(pairs, blocks),
        in_specs=[
            pl.BlockSpec((None, None, None, width, rows), lambda p, i: (i, p, 0, 0, 0)),
            pl.BlockSpec((blocks, None, None, width, rows), lambda p, i: (0, p, 1, 0, 0)),
            pl.BlockSpec((blocks, None, None, width, rows), lambda p, i: (0, p, 2, 0, 0)),
        ],
        out_specs=[block, block, pl.BlockSpec((None, None, 1, rows), lambda p, i: (i, p, 0, 0))],
        out_shape=[
            jax.ShapeDtypeStruct((blocks, pairs, width, rows), LOW),
            jax.ShapeDtypeStruct((blocks, pairs, width, rows), WIDE),
            jax.ShapeDtypeStruct((blocks, pairs, 1, rows), WIDE),
        ],
        scratch_shapes=[pltpu.VMEM((blocks, rows, width), LOW)],
        name="self_forward",
        cost_estimate=estimate(blocks * rows, blocks * rows * pairs, 2),
        compiler_params=pltpu.CompilerParams(vmem_limit_bytes=VMEM_LIMIT),
    )(qkv, qkv, qkv)


def self_backward(qkv, grad_mixed, wide, log_total):
    blocks, pairs, _, width, rows = qkv.shape

    def kernel(q_ref, k_ref, v_ref, g_ref, wide_ref, log_ref, out_ref, keys, values, grad_k, grad_v):
        i = pl.program_id(1)

        @pl.when(i == 0)
        def _():
            for c in range(blocks):
                keys[c] = k_ref[c].T
                values[c] = v_ref[c].T
            grad_k[...] = jnp.zeros_like(grad_k)
            grad_v[...] = jnp.zeros_like(grad_v)

        scaled_q = q_ref[...] * LOW(SCALE)
        grad_t = g_ref[...]
        spread = jnp.sum(grad_t.astype(WIDE) * wide_ref[...], axis=0, keepdims=True)
        logs = log_ref[...]
        queries, grad = scaled_q.T, grad_t.T
        grad_q = jnp.zeros((width, rows), WIDE)
        for c in range(blocks):
            term_q, term_k, term_v = attend_block_back(
                scaled_q, queries, grad_t, grad, keys[c], k_ref[c], values[c], logs, spread
            )
            grad_q += term_q
            grad_k[c] += term_k
            grad_v[c] += term_v
        out_ref[i, 0] = (grad_q * SCALE).astype(LOW)

        @pl.when(i == blocks - 1)
        def _():
            for c in range(blocks):
                out_ref[c, 1] = grad_k[c].T.astype(LOW)
                out_ref[c, 2] = grad_v[c].T.astype(LOW)

    block = pl.BlockSpec((None, None, width, rows), lambda p, i: (i, p, 0, 0))
    return pl.pallas_call(
        kernel,
        grid=(pairs, blocks),
        in_specs=[
            pl.BlockSpec((None, None, None, width, rows), lambda p, i: (i, p, 0, 0, 0)),
            pl.BlockSpec((blocks, None, None, width, rows), lambda p, i: (0, p, 1, 0, 0)),
            pl.BlockSpec((blocks, None, None, width, rows), lambda p, i: (0, p, 2, 0, 0)),
            block,
            block,
            pl.BlockSpec((None, None, 1, rows), lambda p, i: (i, p, 0, 0)),
        ],
        out_specs=pl.BlockSpec((blocks, None, 3, width, rows), lambda p, i: (0, p, 0, 0, 0)),
        out_shape=jax.ShapeDtypeStruct((blocks, pairs, 3, width, rows), LOW),
        scratch_shapes=[pltpu.VMEM((blocks, rows, width), LOW)] * 2
        + [pltpu.VMEM((blocks, rows, width), WIDE)] * 2,
        name="self_backward",
        cost_estimate=estimate(blocks * rows, blocks * rows * pairs, 4),
        compiler_params=pltpu.CompilerParams(vmem_limit_bytes=VMEM_LIMIT),
    )(qkv, qkv, qkv, grad_mixed, wide, log_total)


def by_length(length, full, blocks, run):
    @pl.when(length * 4 > full)
    def _():
        run(blocks)

    @pl.when(length * 4 <= full)
    def _():
        run(blocks // 4)


def cross_forward(queries_t, pair_t, lengths):
    blocks, _, cols, all_patches = pair_t.shape
    objects = lengths.shape[0]
    heads = cols // HEAD_DIM
    rows, patch_rows = queries_t.shape[1] // objects, all_patches // objects

    def kernel(len_ref, q_ref, pair_ref, mixed_ref, wide_ref, log_ref, keys):
        scaled_q = q_ref[...] * LOW(SCALE)

        def run(live):
            for c in range(live):
                keys[c] = pair_ref[c, 0].T
            mixed, log_total = attend_block(
                scaled_q, lambda c: keys[c], lambda c: pair_ref[c, 1], live
            )
            mixed_ref[...] = mixed.astype(LOW)
            wide_ref[...] = mixed
            log_ref[...] = log_total

        by_length(len_ref[pl.program_id(0)], blocks * patch_rows, blocks, run)

    block = pl.BlockSpec((HEAD_DIM, rows), lambda b, j, lens: (j, b))
    return pl.pallas_call(
        kernel,
        grid_spec=pltpu.PrefetchScalarGridSpec(
            num_scalar_prefetch=1,
            grid=(objects, heads),
            in_specs=[
                block,
                pl.BlockSpec((blocks, 2, HEAD_DIM, patch_rows), lambda b, j, lens: (0, 0, j, b)),
            ],
            out_specs=[block, block, pl.BlockSpec((None, 1, rows), lambda b, j, lens: (j, 0, b))],
            scratch_shapes=[pltpu.VMEM((blocks, patch_rows, HEAD_DIM), LOW)],
        ),
        out_shape=[
            jax.ShapeDtypeStruct(queries_t.shape, LOW),
            jax.ShapeDtypeStruct(queries_t.shape, WIDE),
            jax.ShapeDtypeStruct((heads, 1, queries_t.shape[1]), WIDE),
        ],
        name="cross_forward",
        cost_estimate=estimate(objects * rows, blocks * patch_rows * heads, 1.4),
        compiler_params=pltpu.CompilerParams(vmem_limit_bytes=VMEM_LIMIT),
    )(lengths, queries_t, pair_t)


def cross_backward(queries_t, pair_t, lengths, grad_t_all, wide, log_total):
    blocks, _, cols, all_patches = pair_t.shape
    objects = lengths.shape[0]
    heads = cols // HEAD_DIM
    rows, patch_rows = queries_t.shape[1] // objects, all_patches // objects

    def kernel(len_ref, q_ref, pair_ref, g_ref, wide_ref, log_ref, out_q, out_pair):
        scaled_q = q_ref[...] * LOW(SCALE)
        grad_t = g_ref[...]
        spread = jnp.sum(grad_t.astype(WIDE) * wide_ref[...], axis=0, keepdims=True)
        logs = log_ref[...]
        queries, grad = scaled_q.T, grad_t.T

        def run(live):
            grad_q = jnp.zeros((HEAD_DIM, rows), WIDE)
            for c in range(live):
                keys_t = pair_ref[c, 0]
                term_q, term_k, term_v = attend_block_back(
                    scaled_q, queries, grad_t, grad, keys_t.T, keys_t, pair_ref[c, 1].T, logs, spread
                )
                grad_q += term_q
                out_pair[c, 0] = term_k.T.astype(LOW)
                out_pair[c, 1] = term_v.T.astype(LOW)
            for c in range(live, blocks):
                out_pair[c] = jnp.zeros_like(out_pair[c])
            out_q[...] = (grad_q * SCALE).astype(LOW)

        by_length(len_ref[pl.program_id(0)], blocks * patch_rows, blocks, run)

    block = pl.BlockSpec((HEAD_DIM, rows), lambda b, j, lens: (j, b))
    pair_block = pl.BlockSpec((blocks, 2, HEAD_DIM, patch_rows), lambda b, j, lens: (0, 0, j, b))
    return pl.pallas_call(
        kernel,
        grid_spec=pltpu.PrefetchScalarGridSpec(
            num_scalar_prefetch=1,
            grid=(objects, heads),
            in_specs=[
                block,
                pair_block,
                block,
                block,
                pl.BlockSpec((None, 1, rows), lambda b, j, lens: (j, 0, b)),
            ],
            out_specs=[block, pair_block],
        ),
        out_shape=[
            jax.ShapeDtypeStruct(queries_t.shape, LOW),
            jax.ShapeDtypeStruct(pair_t.shape, LOW),
        ],
        name="cross_backward",
        cost_estimate=estimate(objects * rows, blocks * patch_rows * heads, 2.5),
        compiler_params=pltpu.CompilerParams(vmem_limit_bytes=VMEM_LIMIT),
    )(lengths, queries_t, pair_t, grad_t_all, wide, log_total)


def shift(value, step, pairs=None):
    size = lax.axis_size("heads")
    return lax.ppermute(value, "heads", [((i + step) % size, i) for i in range(size)])


def gather_heads(value):
    size = lax.axis_size("heads")
    if size != 4:
        return [value] + [shift(value, step) for step in range(1, size)]
    after, before = shift(value, 1), shift(value, -1)
    inner = lax.ppermute(after, "heads", [(1, 0), (2, 1)]) + lax.ppermute(before, "heads", [(1, 2), (2, 3)])
    return [value, after, inner, before]


def scatter_heads(partial):
    size, me = lax.axis_size("heads"), lax.axis_index("heads")

    def part(step):
        return lax.dynamic_index_in_dim(partial, (me + step) % size, 0, keepdims=False)

    if size != 4:
        total = part(0)
        for step in range(1, size):
            total = total + shift(part(step).astype(LOW), -step).astype(WIDE)
        return total
    far = part(2).astype(LOW)
    up = lax.ppermute(far, "heads", [(0, 1), (1, 2)]).astype(WIDE)
    down = lax.ppermute(far, "heads", [(2, 1), (3, 2)]).astype(WIDE)
    from_below = shift((part(1) + up).astype(LOW), -1)
    from_above = shift((part(3) + down).astype(LOW), 1)
    return part(0) + from_below.astype(WIDE) + from_above.astype(WIDE)


def in_order(parts):
    size, me = lax.axis_size("heads"), lax.axis_index("heads")
    out = jnp.zeros((size,) + parts[0].shape, parts[0].dtype)
    for step, value in enumerate(parts):
        out = lax.dynamic_update_index_in_dim(out, value, (me + step) % size, 0)
    return out.reshape((-1,) + parts[0].shape[1:])


def sum_heads(partial):
    size = lax.axis_size("heads")
    split = partial.reshape((size, -1) + partial.shape[1:])
    return in_order(gather_heads(scatter_heads(split).astype(LOW)))


def exchange_rows(value):
    return lax.all_to_all(value, "rows", 0, 0, tiled=True)


def normed(value):
    centred = value - jnp.mean(value, axis=-1, keepdims=True)
    rate = lax.rsqrt(jnp.mean(centred * centred, axis=-1, keepdims=True) + EPSILON)
    return centred * rate, rate


def normed_back(grad, unit, rate):
    return rate * (
        grad
        - jnp.mean(grad, axis=-1, keepdims=True)
        - unit * jnp.mean(grad * unit, axis=-1, keepdims=True)
    )


def gelu_tanh(pre_act):
    return jax.nn.gelu(pre_act, approximate=True)


def add_trees(former, latter):
    return jax.tree.map(jnp.add, former, latter)


def per_device(
    tokens,
    cam_index,
    patches,
    patch_len,
    camera_table,
    self_weights,
    self_output,
    cross_gain,
    cross_query,
    cross_pair,
    cross_output,
    patch_weights,
    hidden_gain,
    widen_weights,
    narrow_weights,
    cotangent,
):
    batches, rows, width = tokens.shape
    cols = self_weights.shape[2]
    heads = cols // HEAD_DIM
    codes = camera_table.shape[0]
    patch_rows, patch_width = patches.shape[1:]
    n_rows, n_heads = lax.axis_size("rows"), lax.axis_size("heads")
    row_rank, head_rank = lax.axis_index("rows"), lax.axis_index("heads")
    groups = 2 if batches % 2 == 0 and heads * (batches // 2) % n_rows == 0 else 1
    objects = batches // groups
    pairs, left_over = divmod(heads * objects, n_rows)
    whole_pairs = left_over == 0
    full_lengths = jnp.full((objects,), n_rows * rows, jnp.int32)
    count = objects * rows

    def own_columns(value):
        return lax.dynamic_slice_in_dim(value, head_rank * cols, cols, value.ndim - 1)

    table_flat = camera_table.reshape(codes, -1)
    cross_gain_f = cross_gain.astype(WIDE)
    hidden_gain_f = hidden_gain.astype(WIDE)

    qkv_rows = (
        self_weights.reshape(3, width, heads, HEAD_DIM).transpose(2, 0, 3, 1).reshape(3 * cols, width)
    )
    pair_rows = cross_pair.transpose(0, 2, 1).reshape(2 * cols, width)
    query_rows = cross_query.T

    local = jnp.stack([self_output, cross_output, query_rows])
    piece = cols // n_rows
    local = lax.dynamic_slice_in_dim(local, row_rank * piece, piece, 1)
    whole = lax.all_gather(lax.all_gather(local, "heads", axis=0), "rows", axis=0)
    whole = whole.transpose(2, 1, 0, 3, 4).reshape(3, n_heads, cols, width)
    whole = lax.dynamic_slice_in_dim(
        jnp.concatenate([whole, whole], axis=1), head_rank, n_heads, 1
    ).reshape(3, n_heads * cols, width)
    self_whole, cross_whole, query_whole = whole[0], whole[1], whole[2]

    def over_all_columns(value_t, weight):
        return mul(jnp.concatenate(gather_heads(value_t), axis=0), weight, TN)

    def to_pairs(value_t, depth):
        value = value_t.reshape(heads, depth, objects, rows).transpose(2, 0, 1, 3)
        return value.reshape(n_rows, pairs, depth, rows)

    def from_pairs(value, depth):
        value = value.reshape(objects, heads, depth, rows).transpose(1, 2, 0, 3)
        return value.reshape(heads * depth, objects * rows)

    def one_group(group):
        part = slice(group * objects, (group + 1) * objects)
        inputs = tokens[part].reshape(count, width).astype(WIDE)
        patch_in = patches[part].reshape(objects * patch_rows, patch_width)
        lengths = patch_len[part]
        grad_low = cotangent[part].reshape(count, width)
        onehot = (cam_index[part].reshape(count)[:, None] == jnp.arange(codes)[None, :]).astype(LOW)
        shift_scale = mul(onehot, table_flat)
        gain_one = 1.0 + shift_scale[:, :width]
        unit_one, rate_one = normed(inputs)
        normed_one = (unit_one * gain_one + shift_scale[:, width:]).astype(LOW)
        qkv_t = mul(qkv_rows, normed_one, NT).astype(LOW)
        if whole_pairs:
            qkv = exchange_rows(to_pairs(qkv_t, 3 * HEAD_DIM))
            qkv = qkv.reshape(n_rows, pairs, 3, HEAD_DIM, rows)
        else:
            by_kind = qkv_t.reshape(heads, 3, HEAD_DIM, count).transpose(1, 0, 2, 3)
            by_kind = by_kind.reshape(3, cols, count)
            self_pair = lax.all_gather(by_kind[1:], "rows", axis=0)
        patch_mid = mul(patch_in, patch_weights).astype(LOW)
        own_pair = mul(pair_rows, patch_mid, NT).astype(LOW).reshape(2, cols, -1)
        pair_t = lax.all_gather(own_pair, "rows", axis=0)
        yield
        if whole_pairs:
            mixed, self_wide, self_log = self_forward(qkv)
            self_mixed_t = from_pairs(exchange_rows(mixed), HEAD_DIM)
        else:
            self_mixed_t, self_wide, self_log = cross_forward(by_kind[0], self_pair, full_lengths)
        after_self = inputs + over_all_columns(self_mixed_t, self_whole)
        yield
        unit_two, rate_two = normed(after_self)
        normed_two = (unit_two * cross_gain_f).astype(LOW)
        cross_q_t = mul(query_rows, normed_two, NT).astype(LOW)
        cross_mixed_t, cross_wide, cross_log = cross_forward(cross_q_t, pair_t, lengths)
        after_cross = after_self + over_all_columns(cross_mixed_t, cross_whole)
        yield
        unit_three, rate_three = normed(after_cross)
        normed_three = (unit_three * hidden_gain_f).astype(LOW)
        pre_act = mul(normed_three, widen_weights)
        activated, act_back = jax.vjp(gelu_tanh, pre_act)
        activated = activated.astype(LOW)
        grad_pre = act_back(mul(grad_low, narrow_weights, NT))[0].astype(LOW)
        grad_three = sum_heads(mul(grad_pre, widen_weights, NT)).astype(WIDE)
        hidden_sum = sum_heads(mul(activated, narrow_weights)).astype(WIDE)
        result = (after_cross + hidden_sum).astype(LOW)
        narrow_term = mul(activated, grad_low, TN)
        widen_term = mul(normed_three, grad_pre, TN)
        yield
        hidden_gain_term = jnp.sum(own_columns(grad_three * unit_three), axis=0)
        grad_cross = grad_low.astype(WIDE) + normed_back(
            grad_three * hidden_gain_f, unit_three, rate_three
        )
        grad_cross_low = grad_cross.astype(LOW)
        cross_output_term = mul(cross_mixed_t, grad_cross_low)
        grad_mixed_t = mul(cross_output, grad_cross_low, NT).astype(LOW)
        grad_cq_t, grad_pair_t = cross_backward(
            cross_q_t, pair_t, lengths, grad_mixed_t, cross_wide, cross_log
        )
        grad_two = over_all_columns(grad_cq_t, query_whole)
        grad_pair_t = lax.psum_scatter(grad_pair_t, "rows", scatter_dimension=0, tiled=False)
        grad_pair_t = grad_pair_t.reshape(2 * cols, -1)
        query_term = mul(normed_two, grad_cq_t, (((0,), (1,)), ((), ())))
        yield
        cross_gain_term = jnp.sum(own_columns(grad_two * unit_two), axis=0)
        grad_self = grad_cross + normed_back(grad_two * cross_gain_f, unit_two, rate_two)
        grad_self_low = grad_self.astype(LOW)
        self_output_term = mul(self_mixed_t, grad_self_low)
        grad_self_mixed_t = mul(self_output, grad_self_low, NT).astype(LOW)
        if whole_pairs:
            grad_mixed = exchange_rows(to_pairs(grad_self_mixed_t, HEAD_DIM))
            grad_qkv = self_backward(qkv, grad_mixed, self_wide, self_log)
            grad_qkv = exchange_rows(grad_qkv.reshape(n_rows, pairs, 3 * HEAD_DIM, rows))
            grad_qkv_t = from_pairs(grad_qkv, 3 * HEAD_DIM)
        else:
            grad_q_t, grad_kv_t = cross_backward(
                by_kind[0], self_pair, full_lengths, grad_self_mixed_t, self_wide, self_log
            )
            grad_kv_t = lax.psum_scatter(grad_kv_t, "rows", scatter_dimension=0, tiled=False)
            grad_qkv_t = jnp.concatenate([grad_q_t[None], grad_kv_t]).reshape(3, heads, HEAD_DIM, count)
            grad_qkv_t = grad_qkv_t.transpose(1, 0, 2, 3).reshape(3 * cols, count)
        yield
        pair_term = mul(patch_mid, grad_pair_t, (((0,), (1,)), ((), ())))
        grad_mid = sum_heads(mul(grad_pair_t, pair_rows, TN))
        patch_term = mul(patch_in, own_columns(grad_mid), TN)
        patch_grad = mul(grad_mid, patch_weights, NT)
        yield
        grad_one = sum_heads(mul(grad_qkv_t, qkv_rows, TN)).astype(WIDE)
        self_term = mul(normed_one, grad_qkv_t, (((0,), (1,)), ((), ())))
        input_grad = grad_self + normed_back(grad_one * gain_one, unit_one, rate_one)
        own_grad = own_columns(grad_one)
        table_term = jnp.stack(
            [
                lax.dot_general(onehot.astype(WIDE), v, TN, precision=lax.Precision.HIGHEST)
                for v in (own_grad * own_columns(unit_one), own_grad)
            ],
            axis=1,
        )
        yield (
            result.reshape(objects, rows, width),
            input_grad.reshape(objects, rows, width),
            patch_grad.reshape(objects, patch_rows, patch_width),
            (narrow_term, widen_term),
            (
                table_term,
                self_term,
                self_output_term,
                cross_gain_term,
                query_term,
                pair_term,
                cross_output_term,
                patch_term,
                hidden_gain_term,
            ),
        )

    steps = [one_group(group) for group in range(groups)]
    done = [None] * groups
    while done[-1] is None:
        for index, step in enumerate(steps):
            done[index] = next(step)
    outputs, input_grads, patch_grads = (
        jnp.concatenate([values[i] for values in done], axis=0) for i in range(3)
    )
    hidden = done[0][3]
    rest = done[0][4]
    for values in done[1:]:
        hidden, rest = add_trees(hidden, values[3]), add_trees(rest, values[4])

    def reduce_rows(value):
        return lax.psum(value.astype(LOW), "rows")

    narrow_total, widen_total = (reduce_rows(value) for value in hidden)
    (narrow_total, widen_total), rest = lax.optimization_barrier(((narrow_total, widen_total), rest))
    rest = list(rest)
    rest[1] = (
        rest[1].reshape(width, heads, 3, HEAD_DIM).transpose(2, 0, 1, 3).reshape(3, width, cols)
    )
    rest[5] = rest[5].reshape(width, 2, cols).transpose(1, 0, 2)
    totals = [reduce_rows(value) for value in rest]
    totals = [value.astype(WIDE) for value in totals + [widen_total, narrow_total]]
    return (outputs, input_grads, patch_grads) + tuple(totals)


def solution(mesh):
    in_specs = (
        P(None, "rows", None),
        P(None, "rows"),
        P(None, "rows", None),
        P(),
        P(),
        P(None, None, "heads"),
        P("heads", None),
        P(),
        P(None, "heads"),
        P(None, None, "heads"),
        P("heads", None),
        P(),
        P(),
        P(None, "heads"),
        P("heads", None),
        P(None, "rows", None),
    )
    out_specs = (
        P(None, "rows", None),
        P(None, "rows", None),
        P(None, "rows", None),
        P(None, None, "heads"),
        P(None, None, "heads"),
        P("heads", None),
        P("heads"),
        P(None, "heads"),
        P(None, None, "heads"),
        P("heads", None),
        P(None, "heads"),
        P("heads"),
        P(None, "heads"),
        P("heads", None),
    )
    return jax.shard_map(
        per_device, mesh=mesh, in_specs=in_specs, out_specs=out_specs, check_vma=False
    )
```

time: 1920 us -> 863 us (0.45)
  waiting for transfers between devices: 953 us -> 190 us
  matrix products: 489 us -> 94.3 us
  starting transfers between devices: 2.62 us -> 233 us
  blocking collectives: 245 us -> 46.1 us
  Pallas kernels: 0 us -> 113 us
  other arithmetic: 120 us -> 64.2 us
    psum x6 -> x2, waiting for transfers between devices: 649 us -> 44.7 us  [reduce_rows(): return lax.psum(value.astype(LOW), 'rows')]
    dot_general x160 -> x54, matrix products: 489 us -> 94.3 us  [the longest x50 90.6 us: mul(): return lax.dot_general(left, right, dims, preferred_element_type=WIDE)]
    all_gather x32 -> x3, waiting for transfers between devices: 296 us -> 0.06 us  [the longest x2 0.04 us: one_group(): pair_t = lax.all_gather(own_pair, 'rows', axis=0)]
    ppermute x0 -> x88, starting transfers between devices: none -> 202 us  [the longest x44 127 us: shift(): lax.ppermute(value, 'heads', [((i + step) % size, i) for i in range(size)])]
    all_gather x24 -> x1, blocking collectives: 220 us -> 21.7 us  [per_device(): lax.all_gather(local, 'heads', axis=0)]
    ppermute x0 -> x88, waiting for transfers between devices: none -> 132 us  [the longest x44 90.6 us: shift(): lax.ppermute(value, 'heads', [((i + step) % size, i) for i in range(size)])]
    pallas_call x0 -> x8, Pallas kernels: none -> 113 us  [the longest x2 42 us: self_backward(): pl.pallas_call(kernel, grid=(pairs, blocks), in_specs=[pl.BlockSpec((None...]
    reduce_sum x30 -> x13, other arithmetic: 55.3 us -> 12.2 us  [the longest x2 3.06 us: normed_back(): jnp.mean(grad, axis=-1, keepdims=True)]
  transfers between devices with their start and end apart: 38 -> 103, of which waited for: 23 -> 42; matrix products, arithmetic and copies ran while one was open for 24% -> 23% of each run, Pallas kernels for 0% -> 12%
where the time goes in v1:
time: 863 us; the launch traced here: 851 us
  starting transfers between devices  233 us (27%)
  waiting for transfers between devices  190 us (22%)
  Pallas kernels  113 us (13%)
  matrix products  94.3 us (11%)
  local copies, waits for them, and re-layouts  92 us (11%)
  other arithmetic  64.2 us (7%)
  blocking collectives  46.1 us (5%)
  between operations  17.3 us (2%)
    ppermute x44, starting transfers between devices, shift(): lax.ppermute(value, 'heads', [((i + step) % size, i) for i in range(size)])  127 us
    dot_general x50, matrix products, mul(): return lax.dot_general(left, right, dims, preferred_element_type=WIDE)  90.6 us
    ppermute x44, waiting for transfers between devices, shift(): lax.ppermute(value, 'heads', [((i + step) % size, i) for i in range(size)])  90.6 us
    psum x2, waiting for transfers between devices, reduce_rows(): return lax.psum(value.astype(LOW), 'rows')  44.7 us
    unnamed x312, local copies, waits for them, and re-layouts  43.2 us
    pallas_call x2, Pallas kernels, self_backward(): pl.pallas_call(kernel, grid=(pairs, blocks), in_specs=[pl.BlockSpec((None...  42 us
    ppermute x14, waiting for transfers between devices, gather_heads(): lax.ppermute(after, 'heads', [(1, 0), (2, 1)])  40.9 us
    ppermute x8, starting transfers between devices, scatter_heads(): up = lax.ppermute(far, 'heads', [(0, 1), (1, 2)]).astype(WIDE)  39.1 us
  transfers between devices with their start and end apart: 103, of which 42 were waited for; matrix products, arithmetic and copies ran while one was open for 23% of the time, Pallas kernels for 12%

profile of v1, /device:TPU:0, one launch (start us, length us, event | category | flops | bytes accessed | tf_op | source)
XLA Modules:
  0.0 850.5 jit_solution(13258139083661023939)
XLA Ops:
  9.5 21.7 %all-gather = bf16[12,32,1024]{2,1,0:T(8,128)(2,1)} all-gather(bf16[3,32,1024]{2,1,0:T(8,128)(2,1)S(1)} %fusion.158), channel_id=2, replica_groups=mesh['heads'=4,'rows'=8] {'heads'}, dimensions={0}, use_global_device_ids=true | all-gather | bytes 983040 | tf_op jit(solution)/shard_map/all_gather | solution.py:378
  60.5 3.7 all-to-all-start
  68.6 3.6 fusion.32
  79.5 4.6 all-to-all-done
  84.1 4.4 all-to-all-start.2
  88.5 11.0 %self_forward.2 = (bf16[8,1,64,256]{3,2,1,0:T(8,128)(2,1)}, f32[8,1,64,256]{3,2,1,0:T(8,128)S(1)}, f32[8,1,1,256]{3,2,1,0:T(1,128)S(1)}) custom-call(bf16[8,1,3,64,256]{4,3,2,1,0:T(8,128)(2,1)S(1)} %bitcast.486, bf16[8,1,3,64,256]{4,3,2,1,0:T(8,128)(2,1)S(1)} %bitcast.487, bf16[8,1,3,64,256]{4,3,2,1,0:T(8,128)(2,1)S(1)} %bitcast.488), custom_call_target="tpu_custom_call" | custom-call | flops 10066329600 | bytes 4194304 | tf_op jit(solution)/shard_map/self_forward/pallas_call | solution.py:69
  100.3 4.1 all-to-all-done.2
  107.8 12.1 %self_forward.3 = (bf16[8,1,64,256]{3,2,1,0:T(8,128)(2,1)}, f32[8,1,64,256]{3,2,1,0:T(8,128)S(1)}, f32[8,1,1,256]{3,2,1,0:T(1,128)S(1)}) custom-call(bf16[8,1,3,64,256]{4,3,2,1,0:T(8,128)(2,1)} %bitcast.43.q_ref.k_ref.v_ref, bf16[8,1,3,64,256]{4,3,2,1,0:T(8,128)(2,1)} %bitcast.43.q_ref.k_ref.v_ref, bf16[8,1,3,64,256]{4,3,2,1,0:T(8,128)(2,1)} %bitcast.43.q_ref.k_ref.v_ref), custom_call_target="tpu_custom_call" | custom-call | flops 10066329600 | bytes 4194304 | tf_op jit(solution)/shard_map/self_forward/pallas_call | solution.py:69
  120.7 4.1 all-to-all-start.3
  132.1 3.7 collective-permute-start.16
  135.8 4.5 fusion.199
  145.6 4.1 collective-permute-done.16
  151.0 4.9 collective-permute-done.18
  161.2 4.5 collective-permute-done.17
  165.8 3.5 copy.111
  183.0 8.6 %cross_forward.2 = (bf16[256,512]{1,0:T(8,128)(2,1)S(1)}, f32[256,512]{1,0:T(8,128)S(1)}, f32[4,1,512]{2,1,0:T(1,128)S(1)}) custom-call(s32[2]{0:T(128)S(1)} %get-tuple-element.214.len_ref, bf16[256,512]{1,0:T(8,128)(2,1)S(1)} %fusion.34.q_ref, bf16[8,2,256,512]{3,2,1,0:T(8,128)(2,1)S(1)} %copy-done.6), custom_call_target="tpu_custom_call" | custom-call | flops 7046430720 | bytes 1048576 | tf_op jit(solution)/shard_map/cross_forward/pallas_call | solution.py:179
  202.6 8.6 %cross_forward.3 = (bf16[256,512]{1,0:T(8,128)(2,1)S(1)}, f32[256,512]{1,0:T(8,128)S(1)}, f32[4,1,512]{2,1,0:T(1,128)S(1)}) custom-call(s32[2]{0:T(128)S(1)} %get-tuple-element.215.len_ref, bf16[256,512]{1,0:T(8,128)(2,1)S(1)} %fusion.35.q_ref, bf16[8,2,256,512]{3,2,1,0:T(8,128)(2,1)S(1)} %copy-done.7), custom_call_target="tpu_custom_call" | custom-call | flops 7046430720 | bytes 1048576 | tf_op jit(solution)/shard_map/cross_forward/pallas_call | solution.py:179
  211.2 3.8 collective-permute-start.20
  226.6 4.1 collective-permute-done.5
  235.5 3.7 fusion.7
  248.8 3.7 fusion.14
  255.2 4.4 collective-permute-start.52
  269.1 11.3 %collective-permute-start.53 = (bf16[128,1024]{1,0:T(8,128)(2,1)}, bf16[128,1024]{1,0:T(8,128)(2,1)}, u32[]{:S(2)}, u32[]{:S(2)}) collective-permute-start(bf16[128,1024]{1,0:T(8,128)(2,1)} %get-tuple-element.190), channel_id=1, source_target_pairs={{24,0},{0,8},{8,16},{16,24},{25,1},{1,9},{9,17},{17,25},{26,2},{2,... | collective-permute-start | bytes 786440 | tf_op jit(solution)/shard_map/ppermute | solution.py:259
  283.9 3.8 collective-permute-start.38
  288.0 5.2 collective-permute-done.55
  294.5 4.4 collective-permute-start.56
  300.2 4.7 collective-permute-done.38
  305.6 7.8 collective-permute-done.56
  317.5 4.2 collective-permute-done.57
  328.1 15.5 %cross_backward.2 = (bf16[256,512]{1,0:T(8,128)(2,1)S(1)}, bf16[8,2,256,512]{3,2,1,0:T(8,128)(2,1)S(1)}) custom-call(s32[2]{0:T(128)S(1)} %get-tuple-element.214.len_ref, bf16[256,512]{1,0:T(8,128)(2,1)S(1)} %fusion.34.q_ref, bf16[8,2,256,512]{3,2,1,0:T(8,128)(2,1)} %all-gather.6.cloned.1.call-done.pair_ref, bf16[256,512]{1,0:T(8,128)(2,1)S(1)} %fusion.36.g_ref, ...), custom_call_target="tpu_custom_call" | custom-call | flops 12582912000 | bytes 1048576 | tf_op jit(solution)/shard_map/cross_backward/pallas_call | solution.py:233
  348.7 15.6 %cross_backward.3 = (bf16[256,512]{1,0:T(8,128)(2,1)S(1)}, bf16[8,2,256,512]{3,2,1,0:T(8,128)(2,1)S(1)}) custom-call(s32[2]{0:T(128)S(1)} %get-tuple-element.215.len_ref, bf16[256,512]{1,0:T(8,128)(2,1)S(1)} %fusion.35.q_ref, bf16[8,2,256,512]{3,2,1,0:T(8,128)(2,1)} %all-gather.8.cloned.1.call-done.pair_ref, bf16[256,512]{1,0:T(8,128)(2,1)S(1)} %fusion.38.g_ref, ...), custom_call_target="tpu_custom_call" | custom-call | flops 12582912000 | bytes 1048576 | tf_op jit(solution)/shard_map/cross_backward/pallas_call | solution.py:233
  366.4 3.8 fusion.180
  371.0 5.9 collective-permute-start.8
  378.4 5.6 collective-permute-start.24
  391.9 7.9 collective-permute-start.25
  407.0 4.5 collective-permute-start.14
  416.9 3.6 collective-permute-start.28
  430.0 7.8 collective-permute-done.28
  444.3 4.7 collective-permute-done.13
  455.9 3.9 collective-permute-start.62
  475.0 5.4 collective-permute-done.61
  497.5 4.7 all-to-all-done.6.g_ref
  505.6 21.6 %self_backward.3 = bf16[8,1,3,64,256]{4,3,2,1,0:T(8,128)(2,1)} custom-call(bf16[8,1,3,64,256]{4,3,2,1,0:T(8,128)(2,1)} %bitcast.43.q_ref.k_ref.v_ref, bf16[8,1,3,64,256]{4,3,2,1,0:T(8,128)(2,1)} %bitcast.43.q_ref.k_ref.v_ref, bf16[8,1,3,64,256]{4,3,2,1,0:T(8,128)(2,1)} %bitcast.43.q_ref.k_ref.v_ref, bf16[8,1,64,256]{3,2,1,0:T(8,128)(2,1)S(1)} %all-to-all-done.6.g_ref, ...), custom_call_target="tpu_custom_call" | custom-call | flops 20132659200 | bytes 4194304 | tf_op jit(solution)/shard_map/self_backward/pallas_call | solution.py:126
  527.3 4.2 all-to-all-start.7
  532.6 20.4 %self_backward.2 = bf16[8,1,3,64,256]{4,3,2,1,0:T(8,128)(2,1)} custom-call(bf16[8,1,3,64,256]{4,3,2,1,0:T(8,128)(2,1)S(1)} %bitcast.489, bf16[8,1,3,64,256]{4,3,2,1,0:T(8,128)(2,1)S(1)} %bitcast.490, bf16[8,1,3,64,256]{4,3,2,1,0:T(8,128)(2,1)S(1)} %bitcast.491, bf16[8,1,64,256]{3,2,1,0:T(8,128)(2,1)S(1)} %all-to-all-done.4.g_ref, ...), custom_call_target="tpu_custom_call" | custom-call | flops 20132659200 | bytes 4194304 | tf_op jit(solution)/shard_map/self_backward/pallas_call | solution.py:126
  552.9 4.1 all-to-all-start.5
  564.9 5.0 collective-permute-start.64
  574.5 5.0 collective-permute-start.44
  586.7 12.4 %collective-permute-start.45 = (bf16[128,1024]{1,0:T(8,128)(2,1)S(1)}, bf16[128,1024]{1,0:T(8,128)(2,1)S(1)}, u32[]{:S(2)}, u32[]{:S(2)}) collective-permute-start(bf16[128,1024]{1,0:T(8,128)(2,1)S(1)} %get-tuple-element.186), channel_id=1, source_target_pairs={{24,0},{0,8},{8,16},{16,24},{25,1},{1,9},{9,17},{17,25},{26,2},{2,... | collective-permute-start | bytes 786440 | tf_op jit(solution)/shard_map/ppermute | solution.py:259
  602.6 7.9 collective-permute-start.70
  619.9 5.4 collective-permute-done.70
  626.0 3.7 collective-permute-done.48
  631.0 4.6 collective-permute-done.50
  636.6 4.3 collective-permute-done.69
  657.4 6.2 collective-permute-start.72
  669.3 3.6 collective-permute-start.80
  680.0 12.5 %collective-permute-start.81 = (bf16[128,1024]{1,0:T(8,128)(2,1)S(1)}, bf16[128,1024]{1,0:T(8,128)(2,1)S(1)}, u32[]{:S(2)}, u32[]{:S(2)}) collective-permute-start(bf16[128,1024]{1,0:T(8,128)(2,1)S(1)} %get-tuple-element.180), channel_id=1, source_target_pairs={{24,0},{0,8},{8,16},{16,24},{25,1},{1,9},{9,17},{17,25},{26,2},{2,... | collective-permute-start | bytes 786440 | tf_op jit(solution)/shard_map/ppermute | solution.py:259
  696.1 3.6 collective-permute-start.78
  705.2 4.3 collective-permute-start.84
  719.6 8.3 collective-permute-done.84
  732.4 3.7 collective-permute-done.85
  745.5 4.6 multiply_add_fusion.3
  758.0 24.3 %all-reduce = (bf16[32,2,256]{2,0,1:T(8,128)(2,1)S(1)}, bf16[256]{0:T(256)(128)(2,1)S(1)}, bf16[256]{0:T(256)(128)(2,1)S(1)}) all-reduce(bf16[32,2,256]{2,0,1:T(8,128)(2,1)S(1)} %copy-done.116, bf16[256]{0:T(256)(128)(2,1)S(1)} %copy-done.136, bf16[256]{0:T(256)(128)(2,1)S(1)} %copy-done.135), channel_id=1, replica_groups=mesh['heads'=4,'rows'=8] {'rows'}, use_global_device_ids=true, to_apply=%region_32.33 | all-reduce | flops 16896 | bytes 67584 | tf_op jit(solution)/shard_map/psum | solution.py:525
  789.7 44.7 %all-reduce.6.cloned.1.call-done = (bf16[3,1024,256]{1,2,0:T(8,128)(2,1)}, bf16[768,256]{0,1:T(8,128)(2,1)}, bf16[256,1024]{1,0:T(8,128)(2,1)}, bf16[1024,256]{1...) async-done(((bf16[3,1024,256]{1,2,0:T(8,128)(2,1)}, bf16[768,256]{0,1:T(8,128)(2,1)}, bf16[256,1024]{1,0:T(8,128)(2,1)}, ...) | async-done | bytes 4587536 | tf_op jit(solution)/shard_map/psum | solution.py:525
  (685 shorter events, 357.0 us)
Async XLA Ops:
  7.2 158.6 %all-gather.10.cloned.1.call-start = ((), (), s32[]{:S(2)}) async-start(), calls=%async_computation.14 | async-start | bytes 7077888 | tf_op jit(solution)/shard_map/all_gather | solution.py:378
  31.3 149.5 %all-gather.6.cloned.1.call-start = ((), (), s32[]{:S(2)}) async-start(), calls=%async_computation.10 | async-start | bytes 4718592 | tf_op jit(solution)/shard_map/all_gather | solution.py:417
  60.5 23.7 %all-to-all-start = ((bf16[8,1,192,256]{3,2,1,0:T(8,128)(2,1)}), bf16[8,1,192,256]{3,2,1,0:T(8,128)(2,1)S(1)}, u32[]{:S(2)}, u32[]{:S(2)}) async-start(bf16[8,1,192,256]{3,2,1,0:T(8,128)(2,1)} %bitcast.524), calls=%async_computation | async-start | bytes 1572864 | tf_op jit(solution)/shard_map/all_to_all | solution.py:305
  64.2 136.3 %all-gather.8.cloned.1.call-start = ((), (), s32[]{:S(2)}) async-start(), calls=%async_computation.11 | async-start | bytes 4718592 | tf_op jit(solution)/shard_map/all_gather | solution.py:417
  84.1 20.3 %all-to-all-start.2 = ((bf16[8,1,192,256]{3,2,1,0:T(8,128)(2,1)}), bf16[8,1,192,256]{3,2,1,0:T(8,128)(2,1)}, u32[]{:S(2)}, u32[]{:S(2)}) async-start(bf16[8,1,192,256]{3,2,1,0:T(8,128)(2,1)} %bitcast.525), calls=%async_computation.2 | async-start | bytes 1572864 | tf_op jit(solution)/shard_map/all_to_all | solution.py:305
  104.4 16.3 %all-to-all-start.1 = ((bf16[8,1,64,256]{3,2,1,0:T(8,128)(2,1)}), bf16[8,1,64,256]{3,2,1,0:T(8,128)(2,1)S(1)}, u32[]{:S(2)}, u32[]{:S(2)}) async-start(bf16[8,1,64,256]{3,2,1,0:T(8,128)(2,1)} %get-tuple-element.41), calls=%async_computation.1 | async-start | bytes 524288 | tf_op jit(solution)/shard_map/all_to_all | solution.py:305
  124.8 527.1 %reduce-scatter.3.cloned.1.call-start = ((), (), s32[]{:S(2)}) async-start(), calls=%async_computation.12 | async-start | bytes 4718592 | tf_op jit(solution)/shard_map/reduce_scatter | solution.py:455
  132.1 17.7 %collective-permute-start.16 = (bf16[256,512]{1,0:T(8,128)(2,1)S(1)}, bf16[256,512]{1,0:T(8,128)(2,1)}, u32[]{:S(2)}, u32[]{:S(2)}) collective-permute-start(bf16[256,512]{1,0:T(8,128)(2,1)S(1)} %bitcast.572), channel_id=1, source_target_pairs={{8,0},{16,8},{24,16},{0,24},{9,1},{17,9},{25,17},{1,25},{10,2},{18... | collective-permute-start | bytes 786440 | tf_op jit(solution)/shard_map/ppermute | solution.py:259
  135.8 20.1 %collective-permute-start.18 = (bf16[256,512]{1,0:T(8,128)(2,1)S(1)}, bf16[256,512]{1,0:T(8,128)(2,1)}, u32[]{:S(2)}, u32[]{:S(2)}) collective-permute-start(bf16[256,512]{1,0:T(8,128)(2,1)S(1)} %bitcast.573), channel_id=1, source_target_pairs={{24,0},{0,8},{8,16},{16,24},{25,1},{1,9},{9,17},{17,25},{26,2},{2,... | collective-permute-start | bytes 786440 | tf_op jit(solution)/shard_map/ppermute | solution.py:259
  140.3 20.2 %collective-permute-start.1 = (bf16[256,512]{1,0:T(8,128)(2,1)}, bf16[256,512]{1,0:T(8,128)(2,1)S(1)}, u32[]{:S(2)}, u32[]{:S(2)}) collective-permute-start(bf16[256,512]{1,0:T(8,128)(2,1)} %collective-permute-done), channel_id=1, source_target_pairs={{8,0},{16,8},{9,1},{17,9},{10,2},{18,10},{11,3},{19,11},{12,4},{20... | collective-permute-start | bytes 786440 | tf_op jit(solution)/shard_map/ppermute | solution.py:267
  149.7 16.0 %collective-permute-start.17 = (bf16[256,512]{1,0:T(8,128)(2,1)}, bf16[256,512]{1,0:T(8,128)(2,1)S(1)}, u32[]{:S(2)}, u32[]{:S(2)}) collective-permute-start(bf16[256,512]{1,0:T(8,128)(2,1)} %collective-permute-done.16), channel_id=1, source_target_pairs={{8,0},{16,8},{9,1},{17,9},{10,2},{18,10},{11,3},{19,11},{12,4},{20... | collective-permute-start | bytes 786440 | tf_op jit(solution)/shard_map/ppermute | solution.py:267
  191.6 23.5 %collective-permute-start.4 = (bf16[256,512]{1,0:T(8,128)(2,1)S(1)}, bf16[256,512]{1,0:T(8,128)(2,1)}, u32[]{:S(2)}, u32[]{:S(2)}) collective-permute-start(bf16[256,512]{1,0:T(8,128)(2,1)S(1)} %get-tuple-element.42), channel_id=1, source_target_pairs={{8,0},{16,8},{24,16},{0,24},{9,1},{17,9},{25,17},{1,25},{10,2},{18... | collective-permute-start | bytes 786440 | tf_op jit(solution)/shard_map/ppermute | solution.py:259
  194.5 21.9 %collective-permute-start.6 = (bf16[256,512]{1,0:T(8,128)(2,1)S(1)}, bf16[256,512]{1,0:T(8,128)(2,1)}, u32[]{:S(2)}, u32[]{:S(2)}) collective-permute-start(bf16[256,512]{1,0:T(8,128)(2,1)S(1)} %get-tuple-element.42), channel_id=1, source_target_pairs={{24,0},{0,8},{8,16},{16,24},{25,1},{1,9},{9,17},{17,25},{26,2},{2,... | collective-permute-start | bytes 786440 | tf_op jit(solution)/shard_map/ppermute | solution.py:259
  215.1 15.6 %collective-permute-start.5 = (bf16[256,512]{1,0:T(8,128)(2,1)}, bf16[256,512]{1,0:T(8,128)(2,1)S(1)}, u32[]{:S(2)}, u32[]{:S(2)}) collective-permute-start(bf16[256,512]{1,0:T(8,128)(2,1)} %collective-permute-done.4), channel_id=1, source_target_pairs={{8,0},{16,8},{9,1},{17,9},{10,2},{18,10},{11,3},{19,11},{12,4},{20... | collective-permute-start | bytes 786440 | tf_op jit(solution)/shard_map/ppermute | solution.py:267
  221.8 24.2 %collective-permute-start.21 = (bf16[256,512]{1,0:T(8,128)(2,1)S(1)}, bf16[256,512]{1,0:T(8,128)(2,1)S(1)}, u32[]{:S(2)}, u32[]{:S(2)}) collective-permute-start(bf16[256,512]{1,0:T(8,128)(2,1)S(1)} %collective-permute-done.20), channel_id=1, source_target_pairs={{8,0},{16,8},{9,1},{17,9},{10,2},{18,10},{11,3},{19,11},{12,4},{20... | collective-permute-start | bytes 786440 | tf_op jit(solution)/shard_map/ppermute | solution.py:267
  225.9 20.1 %collective-permute-start.23 = (bf16[256,512]{1,0:T(8,128)(2,1)S(1)}, bf16[256,512]{1,0:T(8,128)(2,1)S(1)}, u32[]{:S(2)}, u32[]{:S(2)}) collective-permute-start(bf16[256,512]{1,0:T(8,128)(2,1)S(1)} %collective-permute-done.22), channel_id=1, source_target_pairs={{8,16},{16,24},{9,17},{17,25},{10,18},{18,26},{11,19},{19,27},{12,... | collective-permute-start | bytes 786440 | tf_op jit(solution)/shard_map/ppermute | solution.py:267
  241.3 19.7 %collective-permute-start.32 = (bf16[128,1024]{1,0:T(8,128)(2,1)}, bf16[128,1024]{1,0:T(8,128)(2,1)}, u32[]{:S(2)}, u32[]{:S(2)}) collective-permute-start(bf16[128,1024]{1,0:T(8,128)(2,1)} %fusion.144), channel_id=1, source_target_pairs={{0,8},{8,16},{1,9},{9,17},{2,10},{10,18},{3,11},{11,19},{4,12},{12... | collective-permute-start | bytes 786440 | tf_op jit(solution)/shard_map/ppermute | solution.py:283
  244.7 16.3 %collective-permute-start.34 = (bf16[128,1024]{1,0:T(8,128)(2,1)}, bf16[128,1024]{1,0:T(8,128)(2,1)}, u32[]{:S(2)}, u32[]{:S(2)}) collective-permute-start(bf16[128,1024]{1,0:T(8,128)(2,1)} %fusion.144), channel_id=1, source_target_pairs={{16,8},{24,16},{17,9},{25,17},{18,10},{26,18},{19,11},{27,19},{20,... | collective-permute-start | bytes 786440 | tf_op jit(solution)/shard_map/ppermute | solution.py:284
  263.3 17.2 %collective-permute-start.33 = (bf16[128,1024]{1,0:T(8,128)(2,1)}, bf16[128,1024]{1,0:T(8,128)(2,1)}, u32[]{:S(2)}, u32[]{:S(2)}) collective-permute-start(bf16[128,1024]{1,0:T(8,128)(2,1)} %get-tuple-element.194), channel_id=1, source_target_pairs={{24,0},{0,8},{8,16},{16,24},{25,1},{1,9},{9,17},{17,25},{26,2},{2,... | collective-permute-start | bytes 786440 | tf_op jit(solution)/shard_map/ppermute | solution.py:259
  269.1 18.9 %collective-permute-start.53 = (bf16[128,1024]{1,0:T(8,128)(2,1)}, bf16[128,1024]{1,0:T(8,128)(2,1)}, u32[]{:S(2)}, u32[]{:S(2)}) collective-permute-start(bf16[128,1024]{1,0:T(8,128)(2,1)} %get-tuple-element.190), channel_id=1, source_target_pairs={{24,0},{0,8},{8,16},{16,24},{25,1},{1,9},{9,17},{17,25},{26,2},{2,... | collective-permute-start | bytes 786440 | tf_op jit(solution)/shard_map/ppermute | solution.py:259
  281.9 17.0 %collective-permute-start.36 = (bf16[128,1024]{1,0:T(8,128)(2,1)S(1)}, bf16[128,1024]{1,0:T(8,128)(2,1)S(1)}, u32[]{:S(2)}, u32[]{:S(2)}) collective-permute-start(bf16[128,1024]{1,0:T(8,128)(2,1)S(1)} %get-tuple-element.164), channel_id=1, source_target_pairs={{8,0},{16,8},{24,16},{0,24},{9,1},{17,9},{25,17},{1,25},{10,2},{18... | collective-permute-start | bytes 786440 | tf_op jit(solution)/shard_map/ppermute | solution.py:259
  283.9 21.0 %collective-permute-start.38 = (bf16[128,1024]{1,0:T(8,128)(2,1)S(1)}, bf16[128,1024]{1,0:T(8,128)(2,1)S(1)}, u32[]{:S(2)}, u32[]{:S(2)}) collective-permute-start(bf16[128,1024]{1,0:T(8,128)(2,1)S(1)} %get-tuple-element.164), channel_id=1, source_target_pairs={{24,0},{0,8},{8,16},{16,24},{25,1},{1,9},{9,17},{17,25},{26,2},{2,... | collective-permute-start | bytes 786440 | tf_op jit(solution)/shard_map/ppermute | solution.py:259
  294.5 18.9 %collective-permute-start.56 = (bf16[128,1024]{1,0:T(8,128)(2,1)S(1)}, bf16[128,1024]{1,0:T(8,128)(2,1)S(1)}, u32[]{:S(2)}, u32[]{:S(2)}) collective-permute-start(bf16[128,1024]{1,0:T(8,128)(2,1)S(1)} %get-tuple-element.162), channel_id=1, source_target_pairs={{8,0},{16,8},{24,16},{0,24},{9,1},{17,9},{25,17},{1,25},{10,2},{18... | collective-permute-start | bytes 786440 | tf_op jit(solution)/shard_map/ppermute | solution.py:259
  298.9 15.8 %collective-permute-start.58 = (bf16[128,1024]{1,0:T(8,128)(2,1)S(1)}, bf16[128,1024]{1,0:T(8,128)(2,1)S(1)}, u32[]{:S(2)}, u32[]{:S(2)}) collective-permute-start(bf16[128,1024]{1,0:T(8,128)(2,1)S(1)} %get-tuple-element.162), channel_id=1, source_target_pairs={{24,0},{0,8},{8,16},{16,24},{25,1},{1,9},{9,17},{17,25},{26,2},{2,... | collective-permute-start | bytes 786440 | tf_op jit(solution)/shard_map/ppermute | solution.py:259
  298.9 18.5 %collective-permute-start.37 = (bf16[128,1024]{1,0:T(8,128)(2,1)S(1)}, bf16[128,1024]{1,0:T(8,128)(2,1)S(1)}, u32[]{:S(2)}, u32[]{:S(2)}) collective-permute-start(bf16[128,1024]{1,0:T(8,128)(2,1)S(1)} %collective-permute-done.36), channel_id=1, source_target_pairs={{8,0},{16,8},{9,1},{17,9},{10,2},{18,10},{11,3},{19,11},{12,4},{20... | collective-permute-start | bytes 786440 | tf_op jit(solution)/shard_map/ppermute | solution.py:267
  345.6 319.4 %reduce-scatter.5.cloned.1.call-start = ((), (), s32[]{:S(2)}) async-start(), calls=%async_computation.13 | async-start | bytes 4718592 | tf_op jit(solution)/shard_map/reduce_scatter | solution.py:455
  366.4 372.0 %all-reduce.8.cloned.1.call-start = ((), (), s32[]{:S(2)}) async-start(), calls=%async_computation.16 | async-start | bytes 8388608 | tf_op jit(solution)/shard_map/psum | solution.py:525
  370.3 19.2 %collective-permute-start.10 = (bf16[128,1024]{1,0:T(8,128)(2,1)S(1)}, bf16[128,1024]{1,0:T(8,128)(2,1)S(1)}, u32[]{:S(2)}, u32[]{:S(2)}) collective-permute-start(bf16[128,1024]{1,0:T(8,128)(2,1)S(1)} %fusion.142), channel_id=1, source_target_pairs={{16,8},{24,16},{17,9},{25,17},{18,10},{26,18},{19,11},{27,19},{20,... | collective-permute-start | bytes 786440 | tf_op jit(solution)/shard_map/ppermute | solution.py:284
  371.0 18.5 %collective-permute-start.8 = (bf16[128,1024]{1,0:T(8,128)(2,1)S(1)}, bf16[128,1024]{1,0:T(8,128)(2,1)S(1)}, u32[]{:S(2)}, u32[]{:S(2)}) collective-permute-start(bf16[128,1024]{1,0:T(8,128)(2,1)S(1)} %fusion.142), channel_id=1, source_target_pairs={{0,8},{8,16},{1,9},{9,17},{2,10},{10,18},{3,11},{11,19},{4,12},{12... | collective-permute-start | bytes 786440 | tf_op jit(solution)/shard_map/ppermute | solution.py:283
  390.5 16.1 %collective-permute-start.9 = (bf16[128,1024]{1,0:T(8,128)(2,1)S(1)}, bf16[128,1024]{1,0:T(8,128)(2,1)S(1)}, u32[]{:S(2)}, u32[]{:S(2)}) collective-permute-start(bf16[128,1024]{1,0:T(8,128)(2,1)S(1)} %get-tuple-element.196), channel_id=1, source_target_pairs={{24,0},{0,8},{8,16},{16,24},{25,1},{1,9},{9,17},{17,25},{26,2},{2,... | collective-permute-start | bytes 786440 | tf_op jit(solution)/shard_map/ppermute | solution.py:259
  391.9 20.4 %collective-permute-start.25 = (bf16[128,1024]{1,0:T(8,128)(2,1)S(1)}, bf16[128,1024]{1,0:T(8,128)(2,1)S(1)}, u32[]{:S(2)}, u32[]{:S(2)}) collective-permute-start(bf16[128,1024]{1,0:T(8,128)(2,1)S(1)} %get-tuple-element.200), channel_id=1, source_target_pairs={{24,0},{0,8},{8,16},{16,24},{25,1},{1,9},{9,17},{17,25},{26,2},{2,... | collective-permute-start | bytes 786440 | tf_op jit(solution)/shard_map/ppermute | solution.py:259
  407.0 18.3 %collective-permute-start.12 = (bf16[128,1024]{1,0:T(8,128)(2,1)S(1)}, bf16[128,1024]{1,0:T(8,128)(2,1)S(1)}, u32[]{:S(2)}, u32[]{:S(2)}) collective-permute-start(bf16[128,1024]{1,0:T(8,128)(2,1)S(1)} %get-tuple-element.166), channel_id=1, source_target_pairs={{8,0},{16,8},{24,16},{0,24},{9,1},{17,9},{25,17},{1,25},{10,2},{18... | collective-permute-start | bytes 786440 | tf_op jit(solution)/shard_map/ppermute | solution.py:259
  407.0 22.3 %collective-permute-start.14 = (bf16[128,1024]{1,0:T(8,128)(2,1)S(1)}, bf16[128,1024]{1,0:T(8,128)(2,1)S(1)}, u32[]{:S(2)}, u32[]{:S(2)}) collective-permute-start(bf16[128,1024]{1,0:T(8,128)(2,1)S(1)} %get-tuple-element.166), channel_id=1, source_target_pairs={{24,0},{0,8},{8,16},{16,24},{25,1},{1,9},{9,17},{17,25},{26,2},{2,... | collective-permute-start | bytes 786440 | tf_op jit(solution)/shard_map/ppermute | solution.py:259
  416.9 20.9 %collective-permute-start.28 = (bf16[128,1024]{1,0:T(8,128)(2,1)}, bf16[128,1024]{1,0:T(8,128)(2,1)S(1)}, u32[]{:S(2)}, u32[]{:S(2)}) collective-permute-start(bf16[128,1024]{1,0:T(8,128)(2,1)} %get-tuple-element.168), channel_id=1, source_target_pairs={{8,0},{16,8},{24,16},{0,24},{9,1},{17,9},{25,17},{1,25},{10,2},{18... | collective-permute-start | bytes 786440 | tf_op jit(solution)/shard_map/ppermute | solution.py:259
  423.2 16.6 %collective-permute-start.30 = (bf16[128,1024]{1,0:T(8,128)(2,1)}, bf16[128,1024]{1,0:T(8,128)(2,1)S(1)}, u32[]{:S(2)}, u32[]{:S(2)}) collective-permute-start(bf16[128,1024]{1,0:T(8,128)(2,1)} %get-tuple-element.168), channel_id=1, source_target_pairs={{24,0},{0,8},{8,16},{16,24},{25,1},{1,9},{9,17},{17,25},{26,2},{2,... | collective-permute-start | bytes 786440 | tf_op jit(solution)/shard_map/ppermute | solution.py:259
  425.2 23.8 %collective-permute-start.13 = (bf16[128,1024]{1,0:T(8,128)(2,1)S(1)}, bf16[128,1024]{1,0:T(8,128)(2,1)S(1)}, u32[]{:S(2)}, u32[]{:S(2)}) collective-permute-start(bf16[128,1024]{1,0:T(8,128)(2,1)S(1)} %collective-permute-done.12), channel_id=1, source_target_pairs={{8,0},{16,8},{9,1},{17,9},{10,2},{18,10},{11,3},{19,11},{12,4},{20... | collective-permute-start | bytes 786440 | tf_op jit(solution)/shard_map/ppermute | solution.py:267
  429.3 22.0 %collective-permute-start.15 = (bf16[128,1024]{1,0:T(8,128)(2,1)S(1)}, bf16[128,1024]{1,0:T(8,128)(2,1)S(1)}, u32[]{:S(2)}, u32[]{:S(2)}) collective-permute-start(bf16[128,1024]{1,0:T(8,128)(2,1)S(1)} %collective-permute-done.14), channel_id=1, source_target_pairs={{8,16},{16,24},{9,17},{17,25},{10,18},{18,26},{11,19},{19,27},{12,... | collective-permute-start | bytes 786440 | tf_op jit(solution)/shard_map/ppermute | solution.py:267
  437.8 18.1 %collective-permute-start.29 = (bf16[128,1024]{1,0:T(8,128)(2,1)S(1)}, bf16[128,1024]{1,0:T(8,128)(2,1)S(1)}, u32[]{:S(2)}, u32[]{:S(2)}) collective-permute-start(bf16[128,1024]{1,0:T(8,128)(2,1)S(1)} %collective-permute-done.28), channel_id=1, source_target_pairs={{8,0},{16,8},{9,1},{17,9},{10,2},{18,10},{11,3},{19,11},{12,4},{20... | collective-permute-start | bytes 786440 | tf_op jit(solution)/shard_map/ppermute | solution.py:267
  439.8 20.0 %collective-permute-start.31 = (bf16[128,1024]{1,0:T(8,128)(2,1)S(1)}, bf16[128,1024]{1,0:T(8,128)(2,1)S(1)}, u32[]{:S(2)}, u32[]{:S(2)}) collective-permute-start(bf16[128,1024]{1,0:T(8,128)(2,1)S(1)} %collective-permute-done.30), channel_id=1, source_target_pairs={{8,16},{16,24},{9,17},{17,25},{10,18},{18,26},{11,19},{19,27},{12,... | collective-permute-start | bytes 786440 | tf_op jit(solution)/shard_map/ppermute | solution.py:267
  443.7 22.7 %collective-permute-start.40 = (bf16[256,512]{1,0:T(8,128)(2,1)S(1)}, bf16[256,512]{1,0:T(8,128)(2,1)S(1)}, u32[]{:S(2)}, u32[]{:S(2)}) collective-permute-start(bf16[256,512]{1,0:T(8,128)(2,1)S(1)} %get-tuple-element.47), channel_id=1, source_target_pairs={{8,0},{16,8},{24,16},{0,24},{9,1},{17,9},{25,17},{1,25},{10,2},{18... | collective-permute-start | bytes 786440 | tf_op jit(solution)/shard_map/ppermute | solution.py:259
  449.0 18.9 %collective-permute-start.42 = (bf16[256,512]{1,0:T(8,128)(2,1)S(1)}, bf16[256,512]{1,0:T(8,128)(2,1)S(1)}, u32[]{:S(2)}, u32[]{:S(2)}) collective-permute-start(bf16[256,512]{1,0:T(8,128)(2,1)S(1)} %get-tuple-element.47), channel_id=1, source_target_pairs={{24,0},{0,8},{8,16},{16,24},{25,1},{1,9},{9,17},{17,25},{26,2},{2,... | collective-permute-start | bytes 786440 | tf_op jit(solution)/shard_map/ppermute | solution.py:259
  451.3 19.5 %collective-permute-start.60 = (bf16[256,512]{1,0:T(8,128)(2,1)S(1)}, bf16[256,512]{1,0:T(8,128)(2,1)S(1)}, u32[]{:S(2)}, u32[]{:S(2)}) collective-permute-start(bf16[256,512]{1,0:T(8,128)(2,1)S(1)} %get-tuple-element.52), channel_id=1, source_target_pairs={{8,0},{16,8},{24,16},{0,24},{9,1},{17,9},{25,17},{1,25},{10,2},{18... | collective-permute-start | bytes 786440 | tf_op jit(solution)/shard_map/ppermute | solution.py:259
  455.9 16.2 %collective-permute-start.62 = (bf16[256,512]{1,0:T(8,128)(2,1)S(1)}, bf16[256,512]{1,0:T(8,128)(2,1)S(1)}, u32[]{:S(2)}, u32[]{:S(2)}) collective-permute-start(bf16[256,512]{1,0:T(8,128)(2,1)S(1)} %get-tuple-element.52), channel_id=1, source_target_pairs={{24,0},{0,8},{8,16},{16,24},{25,1},{1,9},{9,17},{17,25},{26,2},{2,... | collective-permute-start | bytes 786440 | tf_op jit(solution)/shard_map/ppermute | solution.py:259
  502.2 25.1 %all-to-all-start.4 = ((bf16[8,1,64,256]{3,2,1,0:T(8,128)(2,1)}), bf16[8,1,64,256]{3,2,1,0:T(8,128)(2,1)S(1)}, u32[]{:S(2)}, u32[]{:S(2)}) async-start(bf16[8,1,64,256]{3,2,1,0:T(8,128)(2,1)} %bitcast.78), calls=%async_computation.4 | async-start | bytes 524288 | tf_op jit(solution)/shard_map/all_to_all | solution.py:305
  527.3 25.7 %all-to-all-start.7 = ((bf16[8,1,192,256]{3,2,1,0:T(8,128)(2,1)}), bf16[8,1,192,256]{3,2,1,0:T(8,128)(2,1)}, u32[]{:S(2)}, u32[]{:S(2)}) async-start(bf16[8,1,192,256]{3,2,1,0:T(8,128)(2,1)} %bitcast.113), calls=%async_computation.7 | async-start | bytes 1572864 | tf_op jit(solution)/shard_map/all_to_all | solution.py:305
  552.9 17.7 %all-to-all-start.5 = ((bf16[8,1,192,256]{3,2,1,0:T(8,128)(2,1)}), bf16[8,1,192,256]{3,2,1,0:T(8,128)(2,1)S(1)}, u32[]{:S(2)}, u32[]{:S(2)}) async-start(bf16[8,1,192,256]{3,2,1,0:T(8,128)(2,1)} %bitcast.80), calls=%async_computation.5 | async-start | bytes 1572864 | tf_op jit(solution)/shard_map/all_to_all | solution.py:305
  557.0 277.5 %all-reduce.6.cloned.1.call-start = ((), (), s32[]{:S(2)}) async-start(), calls=%async_computation.15 | async-start | bytes 9175040 | tf_op jit(solution)/shard_map/psum | solution.py:525
  564.9 17.1 %collective-permute-start.64 = (bf16[128,1024]{1,0:T(8,128)(2,1)S(1)}, bf16[128,1024]{1,0:T(8,128)(2,1)S(1)}, u32[]{:S(2)}, u32[]{:S(2)}) collective-permute-start(bf16[128,1024]{1,0:T(8,128)(2,1)S(1)} %fusion.147), channel_id=1, source_target_pairs={{0,8},{8,16},{1,9},{9,17},{2,10},{10,18},{3,11},{11,19},{4,12},{12... | collective-permute-start | bytes 786440 | tf_op jit(solution)/shard_map/ppermute | solution.py:283
  582.2 17.9 %collective-permute-start.65 = (bf16[128,1024]{1,0:T(8,128)(2,1)S(1)}, bf16[128,1024]{1,0:T(8,128)(2,1)S(1)}, u32[]{:S(2)}, u32[]{:S(2)}) collective-permute-start(bf16[128,1024]{1,0:T(8,128)(2,1)S(1)} %get-tuple-element.188), channel_id=1, source_target_pairs={{24,0},{0,8},{8,16},{16,24},{25,1},{1,9},{9,17},{17,25},{26,2},{2,... | collective-permute-start | bytes 786440 | tf_op jit(solution)/shard_map/ppermute | solution.py:259
  586.7 23.8 %collective-permute-start.45 = (bf16[128,1024]{1,0:T(8,128)(2,1)S(1)}, bf16[128,1024]{1,0:T(8,128)(2,1)S(1)}, u32[]{:S(2)}, u32[]{:S(2)}) collective-permute-start(bf16[128,1024]{1,0:T(8,128)(2,1)S(1)} %get-tuple-element.186), channel_id=1, source_target_pairs={{24,0},{0,8},{8,16},{16,24},{25,1},{1,9},{9,17},{17,25},{26,2},{2,... | collective-permute-start | bytes 786440 | tf_op jit(solution)/shard_map/ppermute | solution.py:259
  601.3 17.3 %collective-permute-start.68 = (bf16[128,1024]{1,0:T(8,128)(2,1)S(1)}, bf16[128,1024]{1,0:T(8,128)(2,1)S(1)}, u32[]{:S(2)}, u32[]{:S(2)}) collective-permute-start(bf16[128,1024]{1,0:T(8,128)(2,1)S(1)} %get-tuple-element.160), channel_id=1, source_target_pairs={{8,0},{16,8},{24,16},{0,24},{9,1},{17,9},{25,17},{1,25},{10,2},{18... | collective-permute-start | bytes 786440 | tf_op jit(solution)/shard_map/ppermute | solution.py:259
  602.6 22.7 %collective-permute-start.70 = (bf16[128,1024]{1,0:T(8,128)(2,1)S(1)}, bf16[128,1024]{1,0:T(8,128)(2,1)S(1)}, u32[]{:S(2)}, u32[]{:S(2)}) collective-permute-start(bf16[128,1024]{1,0:T(8,128)(2,1)S(1)} %get-tuple-element.160), channel_id=1, source_target_pairs={{24,0},{0,8},{8,16},{16,24},{25,1},{1,9},{9,17},{17,25},{26,2},{2,... | collective-permute-start | bytes 786440 | tf_op jit(solution)/shard_map/ppermute | solution.py:259
  613.2 16.6 %collective-permute-start.48 = (bf16[128,1024]{1,0:T(8,128)(2,1)S(1)}, bf16[128,1024]{1,0:T(8,128)(2,1)S(1)}, u32[]{:S(2)}, u32[]{:S(2)}) collective-permute-start(bf16[128,1024]{1,0:T(8,128)(2,1)S(1)} %get-tuple-element.158), channel_id=1, source_target_pairs={{8,0},{16,8},{24,16},{0,24},{9,1},{17,9},{25,17},{1,25},{10,2},{18... | collective-permute-start | bytes 786440 | tf_op jit(solution)/shard_map/ppermute | solution.py:259
  616.4 19.2 %collective-permute-start.50 = (bf16[128,1024]{1,0:T(8,128)(2,1)S(1)}, bf16[128,1024]{1,0:T(8,128)(2,1)S(1)}, u32[]{:S(2)}, u32[]{:S(2)}) collective-permute-start(bf16[128,1024]{1,0:T(8,128)(2,1)S(1)} %get-tuple-element.158), channel_id=1, source_target_pairs={{24,0},{0,8},{8,16},{16,24},{25,1},{1,9},{9,17},{17,25},{26,2},{2,... | collective-permute-start | bytes 786440 | tf_op jit(solution)/shard_map/ppermute | solution.py:259
  618.6 22.3 %collective-permute-start.69 = (bf16[128,1024]{1,0:T(8,128)(2,1)S(1)}, bf16[128,1024]{1,0:T(8,128)(2,1)S(1)}, u32[]{:S(2)}, u32[]{:S(2)}) collective-permute-start(bf16[128,1024]{1,0:T(8,128)(2,1)S(1)} %collective-permute-done.68), channel_id=1, source_target_pairs={{8,0},{16,8},{9,1},{17,9},{10,2},{18,10},{11,3},{19,11},{12,4},{20... | collective-permute-start | bytes 786440 | tf_op jit(solution)/shard_map/ppermute | solution.py:267
  625.3 15.6 %collective-permute-start.71 = (bf16[128,1024]{1,0:T(8,128)(2,1)S(1)}, bf16[128,1024]{1,0:T(8,128)(2,1)S(1)}, u32[]{:S(2)}, u32[]{:S(2)}) collective-permute-start(bf16[128,1024]{1,0:T(8,128)(2,1)S(1)} %collective-permute-done.70), channel_id=1, source_target_pairs={{8,16},{16,24},{9,17},{17,25},{10,18},{18,26},{11,19},{19,27},{12,... | collective-permute-start | bytes 786440 | tf_op jit(solution)/shard_map/ppermute | solution.py:267
  657.4 16.8 %collective-permute-start.72 = (bf16[128,1024]{1,0:T(8,128)(2,1)S(1)}, bf16[128,1024]{1,0:T(8,128)(2,1)}, u32[]{:S(2)}, u32[]{:S(2)}) collective-permute-start(bf16[128,1024]{1,0:T(8,128)(2,1)S(1)} %fusion.148), channel_id=1, source_target_pairs={{0,8},{8,16},{1,9},{9,17},{2,10},{10,18},{3,11},{11,19},{4,12},{12... | collective-permute-start | bytes 786440 | tf_op jit(solution)/shard_map/ppermute | solution.py:283
  675.6 17.7 %collective-permute-start.73 = (bf16[128,1024]{1,0:T(8,128)(2,1)S(1)}, bf16[128,1024]{1,0:T(8,128)(2,1)S(1)}, u32[]{:S(2)}, u32[]{:S(2)}) collective-permute-start(bf16[128,1024]{1,0:T(8,128)(2,1)S(1)} %get-tuple-element.178), channel_id=1, source_target_pairs={{24,0},{0,8},{8,16},{16,24},{25,1},{1,9},{9,17},{17,25},{26,2},{2,... | collective-permute-start | bytes 786440 | tf_op jit(solution)/shard_map/ppermute | solution.py:259
  680.0 21.8 %collective-permute-start.81 = (bf16[128,1024]{1,0:T(8,128)(2,1)S(1)}, bf16[128,1024]{1,0:T(8,128)(2,1)S(1)}, u32[]{:S(2)}, u32[]{:S(2)}) collective-permute-start(bf16[128,1024]{1,0:T(8,128)(2,1)S(1)} %get-tuple-element.180), channel_id=1, source_target_pairs={{24,0},{0,8},{8,16},{16,24},{25,1},{1,9},{9,17},{17,25},{26,2},{2,... | collective-permute-start | bytes 786440 | tf_op jit(solution)/shard_map/ppermute | solution.py:259
  693.6 21.0 %collective-permute-start.76 = (bf16[128,1024]{1,0:T(8,128)(2,1)S(1)}, bf16[128,1024]{1,0:T(8,128)(2,1)S(1)}, u32[]{:S(2)}, u32[]{:S(2)}) collective-permute-start(bf16[128,1024]{1,0:T(8,128)(2,1)S(1)} %get-tuple-element.154), channel_id=1, source_target_pairs={{8,0},{16,8},{24,16},{0,24},{9,1},{17,9},{25,17},{1,25},{10,2},{18... | collective-permute-start | bytes 786440 | tf_op jit(solution)/shard_map/ppermute | solution.py:259
  696.1 22.8 %collective-permute-start.78 = (bf16[128,1024]{1,0:T(8,128)(2,1)S(1)}, bf16[128,1024]{1,0:T(8,128)(2,1)S(1)}, u32[]{:S(2)}, u32[]{:S(2)}) collective-permute-start(bf16[128,1024]{1,0:T(8,128)(2,1)S(1)} %get-tuple-element.154), channel_id=1, source_target_pairs={{24,0},{0,8},{8,16},{16,24},{25,1},{1,9},{9,17},{17,25},{26,2},{2,... | collective-permute-start | bytes 786440 | tf_op jit(solution)/shard_map/ppermute | solution.py:259
  705.2 22.7 %collective-permute-start.84 = (bf16[128,1024]{1,0:T(8,128)(2,1)S(1)}, bf16[128,1024]{1,0:T(8,128)(2,1)S(1)}, u32[]{:S(2)}, u32[]{:S(2)}) collective-permute-start(bf16[128,1024]{1,0:T(8,128)(2,1)S(1)} %get-tuple-element.156), channel_id=1, source_target_pairs={{8,0},{16,8},{24,16},{0,24},{9,1},{17,9},{25,17},{1,25},{10,2},{18... | collective-permute-start | bytes 786440 | tf_op jit(solution)/shard_map/ppermute | solution.py:259
  709.5 19.6 %collective-permute-start.86 = (bf16[128,1024]{1,0:T(8,128)(2,1)S(1)}, bf16[128,1024]{1,0:T(8,128)(2,1)S(1)}, u32[]{:S(2)}, u32[]{:S(2)}) collective-permute-start(bf16[128,1024]{1,0:T(8,128)(2,1)S(1)} %get-tuple-element.156), channel_id=1, source_target_pairs={{24,0},{0,8},{8,16},{16,24},{25,1},{1,9},{9,17},{17,25},{26,2},{2,... | collective-permute-start | bytes 786440 | tf_op jit(solution)/shard_map/ppermute | solution.py:259
  714.7 17.6 %collective-permute-start.77 = (bf16[128,1024]{1,0:T(8,128)(2,1)S(1)}, bf16[128,1024]{1,0:T(8,128)(2,1)S(1)}, u32[]{:S(2)}, u32[]{:S(2)}) collective-permute-start(bf16[128,1024]{1,0:T(8,128)(2,1)S(1)} %collective-permute-done.76), channel_id=1, source_target_pairs={{8,0},{16,8},{9,1},{17,9},{10,2},{18,10},{11,3},{19,11},{12,4},{20... | collective-permute-start | bytes 786440 | tf_op jit(solution)/shard_map/ppermute | solution.py:267
  (186 other events, 1660.5 us)
Sparse Core Ops, SparseCore 0:
  31.4 52.3 all-gather.9
  85.7 41.3 all-gather.5
  129.1 35.8 all-gather.7
  345.7 54.0 reduce-scatter.2
  404.0 51.3 reduce-scatter.4
  458.5 91.3 all-reduce.7
  744.9 89.5 all-reduce.5

commit v2 on v1

v2 whole, which is shorter than its diff:
```python
import jax
import jax.numpy as jnp
from jax import lax
from jax.experimental import pallas as pl
from jax.experimental.pallas import tpu as pltpu
from jax.sharding import PartitionSpec as P

HEAD_DIM = 64
EPSILON = 1e-05
SCALE = HEAD_DIM ** (-0.5)
LOW = jnp.bfloat16
WIDE = jnp.float32

NN = (((1,), (0,)), ((), ()))
NT = (((1,), (1,)), ((), ()))
TN = (((0,), (0,)), ((), ()))
T_LAST = (((0,), (1,)), ((), ()))


def mul(left, right, dims=NN):
    return lax.dot_general(left, right, dims, preferred_element_type=WIDE)


def load_values(values, block, values_t):
    rows = values_t.shape[1]
    at = slice(block * rows, (block + 1) * rows)
    values[at, :HEAD_DIM] = values_t.T
    values[at, HEAD_DIM:] = jnp.ones((rows, HEAD_DIM), values.dtype)


def attend_block(queries, keys_t, values):
    scores = mul(queries, keys_t)
    peak = jnp.max(scores, axis=1, keepdims=True)
    both = mul(jnp.exp(scores - peak).astype(LOW), values).T
    total = both[HEAD_DIM : HEAD_DIM + 1]
    return both[:HEAD_DIM] / total, peak.T + jnp.log(total)


def attend_block_back(scaled_q, grad_t, keys, keys_t, values, log_total, spread):
    probs = jnp.exp(mul(keys, scaled_q) - log_total)
    grad_scores = (probs * (mul(values, grad_t) - spread)).astype(LOW)
    return (
        (mul(keys_t, grad_scores) * SCALE).astype(LOW),
        mul(grad_scores, scaled_q.T),
        mul(probs.astype(LOW), grad_t.T),
    )


def estimate(rows, cols, passes):
    return pl.CostEstimate(
        flops=int(rows * cols * 1200 * passes), transcendentals=int(rows * cols), bytes_accessed=int(rows * 2048)
    )


VMEM_LIMIT = 48 << 20


def by_length(length, full, blocks, run):
    @pl.when(length * 4 > full)
    def _():
        run(blocks)

    @pl.when(length * 4 <= full)
    def _():
        run(blocks // 4)


def cross_forward(queries_t, pair_t, lengths):
    blocks, _, cols, all_patches = pair_t.shape
    objects = lengths.shape[0]
    heads = cols // HEAD_DIM
    rows, patch_rows = queries_t.shape[1] // objects, all_patches // objects

    def kernel(len_ref, q_ref, pair_ref, mixed_ref, wide_ref, log_ref, keys_t, values):
        queries = (q_ref[...] * LOW(SCALE)).T

        def run(live):
            for c in range(live):
                keys_t[:, c * patch_rows : (c + 1) * patch_rows] = pair_ref[c, 0]
                load_values(values, c, pair_ref[c, 1])
            size = live * patch_rows
            mixed, log_total = attend_block(queries, keys_t[:, :size], values[:size])
            mixed_ref[...] = mixed.astype(LOW)
            wide_ref[...] = mixed
            log_ref[...] = log_total

        by_length(len_ref[pl.program_id(0)], blocks * patch_rows, blocks, run)

    block = pl.BlockSpec((HEAD_DIM, rows), lambda b, j, lens: (j, b))
    return pl.pallas_call(
        kernel,
        grid_spec=pltpu.PrefetchScalarGridSpec(
            num_scalar_prefetch=1,
            grid=(objects, heads),
            in_specs=[
                block,
                pl.BlockSpec((blocks, 2, HEAD_DIM, patch_rows), lambda b, j, lens: (0, 0, j, b)),
            ],
            out_specs=[block, block, pl.BlockSpec((None, 1, rows), lambda b, j, lens: (j, 0, b))],
            scratch_shapes=[
                pltpu.VMEM((HEAD_DIM, blocks * patch_rows), LOW),
                pltpu.VMEM((blocks * patch_rows, 2 * HEAD_DIM), LOW),
            ],
        ),
        out_shape=[
            jax.ShapeDtypeStruct(queries_t.shape, LOW),
            jax.ShapeDtypeStruct(queries_t.shape, WIDE),
            jax.ShapeDtypeStruct((heads, 1, queries_t.shape[1]), WIDE),
        ],
        name="cross_forward",
        cost_estimate=estimate(objects * rows, blocks * patch_rows * heads, 1.4),
        compiler_params=pltpu.CompilerParams(vmem_limit_bytes=VMEM_LIMIT),
    )(lengths, queries_t, pair_t)


def cross_backward(queries_t, pair_t, lengths, grad_t_all, wide, log_total):
    blocks, _, cols, all_patches = pair_t.shape
    objects = lengths.shape[0]
    heads = cols // HEAD_DIM
    rows, patch_rows = queries_t.shape[1] // objects, all_patches // objects

    def kernel(len_ref, q_ref, pair_ref, g_ref, wide_ref, log_ref, out_q, out_pair, keys, keys_t, values):
        grad_t = g_ref[...]
        spread = jnp.sum(grad_t.astype(WIDE) * wide_ref[...], axis=0, keepdims=True)

        def run(live):
            for c in range(live):
                at = slice(c * patch_rows, (c + 1) * patch_rows)
                keys[at] = pair_ref[c, 0].T
                keys_t[:, at] = pair_ref[c, 0]
                values[at] = pair_ref[c, 1].T
            size = live * patch_rows
            out_q[...], grad_k, grad_v = attend_block_back(
                q_ref[...] * LOW(SCALE),
                grad_t,
                keys[:size],
                keys_t[:, :size],
                values[:size],
                log_ref[...],
                spread,
            )
            for c in range(live):
                at = slice(c * patch_rows, (c + 1) * patch_rows)
                out_pair[c, 0] = grad_k[at].T.astype(LOW)
                out_pair[c, 1] = grad_v[at].T.astype(LOW)
            for c in range(live, blocks):
                out_pair[c] = jnp.zeros_like(out_pair[c])

        by_length(len_ref[pl.program_id(0)], blocks * patch_rows, blocks, run)

    block = pl.BlockSpec((HEAD_DIM, rows), lambda b, j, lens: (j, b))
    pair_block = pl.BlockSpec((blocks, 2, HEAD_DIM, patch_rows), lambda b, j, lens: (0, 0, j, b))
    return pl.pallas_call(
        kernel,
        grid_spec=pltpu.PrefetchScalarGridSpec(
            num_scalar_prefetch=1,
            grid=(objects, heads),
            in_specs=[
                block,
                pair_block,
                block,
                block,
                pl.BlockSpec((None, 1, rows), lambda b, j, lens: (j, 0, b)),
            ],
            out_specs=[block, pair_block],
            scratch_shapes=[
                pltpu.VMEM((blocks * patch_rows, HEAD_DIM), LOW),
                pltpu.VMEM((HEAD_DIM, blocks * patch_rows), LOW),
                pltpu.VMEM((blocks * patch_rows, HEAD_DIM), LOW),
            ],
        ),
        out_shape=[
            jax.ShapeDtypeStruct(queries_t.shape, LOW),
            jax.ShapeDtypeStruct(pair_t.shape, LOW),
        ],
        name="cross_backward",
        cost_estimate=estimate(objects * rows, blocks * patch_rows * heads, 2.5),
        compiler_params=pltpu.CompilerParams(vmem_limit_bytes=VMEM_LIMIT),
    )(lengths, queries_t, pair_t, grad_t_all, wide, log_total)


def shift(value, step):
    size = lax.axis_size("heads")
    return lax.ppermute(value, "heads", [((i + step) % size, i) for i in range(size)])


def gather_heads(value):
    size = lax.axis_size("heads")
    if size != 4:
        return [value] + [shift(value, step) for step in range(1, size)]
    after, before = shift(value, 1), shift(value, -1)
    inner = lax.ppermute(after, "heads", [(1, 0), (2, 1)]) + lax.ppermute(before, "heads", [(1, 2), (2, 3)])
    return [value, after, inner, before]


def scatter_heads(partial):
    size, me = lax.axis_size("heads"), lax.axis_index("heads")

    def part(step):
        return lax.dynamic_index_in_dim(partial, (me + step) % size, 0, keepdims=False)

    if size != 4:
        total = part(0)
        for step in range(1, size):
            total = total + shift(part(step).astype(LOW), -step).astype(WIDE)
        return total
    far = part(2).astype(LOW)
    up = lax.ppermute(far, "heads", [(0, 1), (1, 2)]).astype(WIDE)
    down = lax.ppermute(far, "heads", [(2, 1), (3, 2)]).astype(WIDE)
    from_below = shift((part(1) + up).astype(LOW), -1)
    from_above = shift((part(3) + down).astype(LOW), 1)
    return part(0) + from_below.astype(WIDE) + from_above.astype(WIDE)


def in_order(parts):
    size, me = lax.axis_size("heads"), lax.axis_index("heads")
    out = jnp.zeros((size,) + parts[0].shape, parts[0].dtype)
    for step, value in enumerate(parts):
        out = lax.dynamic_update_index_in_dim(out, value, (me + step) % size, 0)
    return out.reshape((-1,) + parts[0].shape[1:])


def sum_heads(partial):
    size = lax.axis_size("heads")
    split = partial.reshape((size, -1) + partial.shape[1:])
    return in_order(gather_heads(scatter_heads(split).astype(LOW)))


def exchange_rows(value):
    return lax.all_to_all(value, "rows", 0, 0, tiled=True)


def normed(value):
    centred = value - jnp.mean(value, axis=-1, keepdims=True)
    rate = lax.rsqrt(jnp.mean(centred * centred, axis=-1, keepdims=True) + EPSILON)
    return centred * rate, rate


def normed_back(grad, unit, rate):
    return rate * (
        grad
        - jnp.mean(grad, axis=-1, keepdims=True)
        - unit * jnp.mean(grad * unit, axis=-1, keepdims=True)
    )


def gelu_tanh(pre_act):
    return jax.nn.gelu(pre_act, approximate=True)


def add_trees(former, latter):
    return jax.tree.map(jnp.add, former, latter)


def pair_forward(queries, pair, key_at, length=None):
    blocks, _, width, rows = queries.shape
    pair_rows = pair.shape[3]
    lengths = jnp.full((1,), blocks * pair_rows, jnp.int32) if length is None else length

    def kernel(len_ref, q_ref, k_ref, v_ref, mixed_ref, wide_ref, log_ref, keys_t, values):
        def run(live):
            @pl.when(pl.program_id(0) == 0)
            def _():
                for c in range(live):
                    keys_t[:, c * pair_rows : (c + 1) * pair_rows] = k_ref[c]
                    load_values(values, c, v_ref[c])

            size = live * pair_rows
            mixed, log_total = attend_block(
                (q_ref[...] * LOW(SCALE)).T, keys_t[:, :size], values[:size]
            )
            mixed_ref[...] = mixed.astype(LOW)
            wide_ref[...] = mixed
            log_ref[...] = log_total

        if length is None:
            run(blocks)
        else:
            by_length(len_ref[0], blocks * pair_rows, blocks, run)

    block = pl.BlockSpec((None, width, rows), lambda i, lens: (i, 0, 0))
    return pl.pallas_call(
        kernel,
        grid_spec=pltpu.PrefetchScalarGridSpec(
            num_scalar_prefetch=1,
            grid=(blocks,),
            in_specs=[
                pl.BlockSpec((None, None, width, rows), lambda i, lens: (i, 0, 0, 0)),
                pl.BlockSpec((blocks, None, width, pair_rows), lambda i, lens: (0, key_at, 0, 0)),
                pl.BlockSpec((blocks, None, width, pair_rows), lambda i, lens: (0, key_at + 1, 0, 0)),
            ],
            out_specs=[block, block, pl.BlockSpec((None, 1, rows), lambda i, lens: (i, 0, 0))],
            scratch_shapes=[
                pltpu.VMEM((width, blocks * pair_rows), LOW),
                pltpu.VMEM((blocks * pair_rows, 2 * width), LOW),
            ],
        ),
        out_shape=[
            jax.ShapeDtypeStruct((blocks, width, rows), LOW),
            jax.ShapeDtypeStruct((blocks, width, rows), WIDE),
            jax.ShapeDtypeStruct((blocks, 1, rows), WIDE),
        ],
        name="pair_forward",
        cost_estimate=estimate(blocks * rows, blocks * pair_rows, 2 if length is None else 1.4),
        compiler_params=pltpu.CompilerParams(vmem_limit_bytes=VMEM_LIMIT),
    )(lengths, queries, pair, pair)


def pair_backward(queries, pair, key_at, length, grad_mixed, wide, log_total):
    blocks, _, width, rows = queries.shape
    lengths = jnp.full((1,), blocks * rows, jnp.int32) if length is None else length

    def kernel(len_ref, q_ref, k_ref, v_ref, g_ref, wide_ref, log_ref, out_ref, keys, keys_t, values, grad_k, grad_v):
        i = pl.program_id(0)

        def run(live):
            size = live * rows

            @pl.when(i == 0)
            def _():
                for c in range(live):
                    at = slice(c * rows, (c + 1) * rows)
                    keys[at] = k_ref[c].T
                    keys_t[:, at] = k_ref[c]
                    values[at] = v_ref[c].T

            grad_t = g_ref[...]
            spread = jnp.sum(grad_t.astype(WIDE) * wide_ref[...], axis=0, keepdims=True)
            out_ref[i, 0], term_k, term_v = attend_block_back(
                q_ref[...] * LOW(SCALE),
                grad_t,
                keys[:size],
                keys_t[:, :size],
                values[:size],
                log_ref[...],
                spread,
            )

            @pl.when(i == 0)
            def _():
                grad_k[:size] = term_k
                grad_v[:size] = term_v

            @pl.when(i > 0)
            def _():
                grad_k[:size] += term_k
                grad_v[:size] += term_v

            @pl.when(i == blocks - 1)
            def _():
                for c in range(live):
                    at = slice(c * rows, (c + 1) * rows)
                    out_ref[c, 1] = grad_k[at].T.astype(LOW)
                    out_ref[c, 2] = grad_v[at].T.astype(LOW)
                for c in range(live, blocks):
                    out_ref[c, 1:] = jnp.zeros_like(out_ref[c, 1:])

        if length is None:
            run(blocks)
        else:
            by_length(len_ref[0], blocks * rows, blocks, run)

    block = pl.BlockSpec((None, width, rows), lambda i, lens: (i, 0, 0))
    return pl.pallas_call(
        kernel,
        grid_spec=pltpu.PrefetchScalarGridSpec(
            num_scalar_prefetch=1,
            grid=(blocks,),
            in_specs=[
                pl.BlockSpec((None, None, width, rows), lambda i, lens: (i, 0, 0, 0)),
                pl.BlockSpec((blocks, None, width, rows), lambda i, lens: (0, key_at, 0, 0)),
                pl.BlockSpec((blocks, None, width, rows), lambda i, lens: (0, key_at + 1, 0, 0)),
                block,
                block,
                pl.BlockSpec((None, 1, rows), lambda i, lens: (i, 0, 0)),
            ],
            out_specs=pl.BlockSpec((blocks, 3, width, rows), lambda i, lens: (0, 0, 0, 0)),
            scratch_shapes=[
                pltpu.VMEM((blocks * rows, width), LOW),
                pltpu.VMEM((width, blocks * rows), LOW),
                pltpu.VMEM((blocks * rows, width), LOW),
                pltpu.VMEM((blocks * rows, width), WIDE),
                pltpu.VMEM((blocks * rows, width), WIDE),
            ],
        ),
        out_shape=jax.ShapeDtypeStruct((blocks, 3, width, rows), LOW),
        name="pair_backward",
        cost_estimate=estimate(blocks * rows, blocks * rows, 3 if length is None else 2),
        compiler_params=pltpu.CompilerParams(vmem_limit_bytes=VMEM_LIMIT),
    )(lengths, queries, pair, pair, grad_mixed, wide, log_total)


def swap(value, axis):
    return lax.ppermute(value, axis, [(0, 1), (1, 0)])


def sum_near(partial):
    low = partial.astype(LOW)
    return low.astype(WIDE) + swap(low, "near").astype(WIDE)


def halves(value):
    size = value.shape[0] // 2
    near = lax.axis_index("near")
    return (
        lax.dynamic_slice_in_dim(value, near * size, size, 0),
        lax.dynamic_slice_in_dim(value, (1 - near) * size, size, 0),
    )


def half_sum_near(partial):
    mine, other = halves(partial)
    return mine + swap(other.astype(LOW), "near").astype(WIDE)


def over_heads(value):
    far, near = lax.axis_index("far"), lax.axis_index("near")
    value = jnp.stack([value, swap(value, "far")])
    value = jnp.stack([value, swap(value, "near")])
    value = jnp.where(far == 0, value, jnp.flip(value, 1))
    value = jnp.where(near == 0, value, jnp.flip(value, 0))
    value = value.transpose(1, 2, 0, 3, 4)
    return value.reshape(2 * value.shape[1], 2 * value.shape[3], -1)


def paired_device(
    tokens,
    cam_index,
    patches,
    patch_len,
    camera_table,
    self_weights,
    self_output,
    cross_gain,
    cross_query,
    cross_pair,
    cross_output,
    patch_weights,
    hidden_gain,
    widen_weights,
    narrow_weights,
    cotangent,
):
    _, rows, width = tokens.shape
    cols = self_weights.shape[2]
    hidden = widen_weights.shape[1]
    heads = cols // HEAD_DIM
    codes = camera_table.shape[0]
    patch_width = patches.shape[2]
    n_rows = lax.axis_size("rows")
    row_rank = lax.axis_index("rows")
    far, near = lax.axis_index("far"), lax.axis_index("near")
    own = 2 * far + near
    other = 2 * (1 - far) + near
    groups = tokens.shape[0] // 2

    def piece(value):
        size = value.shape[0] // n_rows
        return lax.dynamic_slice_in_dim(value, row_rank * size, size, 0)

    def shard_columns(value):
        return [
            lax.dynamic_slice_in_dim(value, index * cols, cols, value.ndim - 1)
            for index in (own, other)
        ]

    qkv_rows = self_weights.reshape(3, width, heads, HEAD_DIM).transpose(2, 0, 3, 1)
    qkv_rows = qkv_rows.reshape(3 * cols, width)
    pair_rows = cross_pair.reshape(2, width, heads, HEAD_DIM).transpose(2, 0, 3, 1)
    pair_rows = pair_rows.reshape(2 * cols, width)
    query_rows = cross_query.T

    first = swap(piece(qkv_rows), "far")
    qkv_other = lax.all_gather(first, "rows", axis=0, tiled=True)
    mine = [piece(v) for v in (self_output, query_rows, cross_output, pair_rows, widen_weights, narrow_weights)]
    across = swap(jnp.concatenate(mine, axis=0), "far")
    sizes = [v.shape[0] for v in mine]
    starts = [sum(sizes[:i]) for i in range(len(sizes) + 1)]
    across = [across[a:b] for a, b in zip(starts[:-1], starts[1:])]
    two = jnp.stack([jnp.stack(mine[:3]), jnp.stack(across[:3])])
    four = jnp.concatenate([two, swap(two, "near")])

    def put_together(value):
        whole = lax.all_gather(value, "rows", axis=1)
        return whole.reshape(value.shape[0] * cols, width)

    self_whole = put_together(four[:, 0])
    query_whole = put_together(four[:, 1])
    cross_whole = put_together(four[:, 2])
    pair_other = lax.all_gather(across[3], "rows", axis=0, tiled=True)
    widen_other = lax.all_gather(across[4], "rows", axis=0, tiled=True)
    narrow_other = lax.all_gather(across[5], "rows", axis=0, tiled=True)

    table_flat = camera_table.reshape(codes, -1)
    cross_gain_f = cross_gain.astype(WIDE)
    hidden_gain_f = hidden_gain.astype(WIDE)

    def two_rows(weight, weight_other, value):
        return jnp.concatenate(
            [mul(weight, value, NT).astype(LOW), mul(weight_other, value, NT).astype(LOW)]
        )

    def over_all_columns(value_t, weight):
        return mul(jnp.concatenate([value_t, swap(value_t, "near")]), weight, TN)

    def one_group(group):
        def object_of(value):
            return lax.dynamic_index_in_dim(value, groups * far + group, 0, keepdims=False)

        inputs = object_of(tokens).astype(WIDE)
        patch_in = object_of(patches)
        length = object_of(patch_len)[None]
        grad_low = object_of(cotangent)
        onehot = (object_of(cam_index)[:, None] == jnp.arange(codes)[None, :]).astype(LOW)
        shift_scale = mul(onehot, table_flat)
        gain_one = 1.0 + shift_scale[:, :width]
        unit_one, rate_one = normed(inputs)
        normed_one = (unit_one * gain_one + shift_scale[:, width:]).astype(LOW)
        qkv_t = two_rows(qkv_rows, qkv_other, normed_one)
        qkv = exchange_rows(qkv_t.reshape(n_rows, 3, HEAD_DIM, rows))
        patch_mid = mul(patch_in, patch_weights).astype(LOW)
        pair_t = two_rows(pair_rows, pair_other, patch_mid)
        pair = exchange_rows(pair_t.reshape(n_rows, 2, HEAD_DIM, rows))
        mixed, self_wide, self_log = pair_forward(qkv, qkv, 1)
        self_mixed_t = exchange_rows(mixed).reshape(2 * cols, rows)
        after_self = inputs + over_all_columns(self_mixed_t, self_whole)
        unit_two, rate_two = normed(after_self)
        normed_two = (unit_two * cross_gain_f).astype(LOW)
        cross_q = mul(query_whole[: 2 * cols], normed_two, NT).astype(LOW)
        cross_q = exchange_rows(cross_q.reshape(n_rows, 1, HEAD_DIM, rows))
        mixed, cross_wide, cross_log = pair_forward(cross_q, pair, 0, length)
        cross_mixed_t = exchange_rows(mixed).reshape(2 * cols, rows)
        after_cross = after_self + over_all_columns(cross_mixed_t, cross_whole)
        unit_three, rate_three = normed(after_cross)
        normed_three = (unit_three * hidden_gain_f).astype(LOW)
        activated, grad_pre = [], []
        for widen, narrow in ((widen_weights, narrow_weights), (widen_other, narrow_other)):
            result, act_back = jax.vjp(gelu_tanh, mul(normed_three, widen))
            activated.append(result.astype(LOW))
            grad_pre.append(act_back(mul(grad_low, narrow, NT))[0].astype(LOW))
        grad_three = sum_near(
            mul(grad_pre[0], widen_weights, NT) + mul(grad_pre[1], widen_other, NT)
        )
        hidden_half = half_sum_near(
            mul(activated[0], narrow_weights) + mul(activated[1], narrow_other)
        )
        result = (halves(after_cross)[0] + hidden_half).astype(LOW)
        yield (
            "hidden",
            {
                "widen": [(normed_three, value, TN) for value in grad_pre],
                "narrow": [(value, grad_low, TN) for value in activated],
            },
        )
        hidden_gain_term = jnp.sum(grad_three * unit_three, axis=0)
        grad_cross = grad_low.astype(WIDE) + normed_back(
            grad_three * hidden_gain_f, unit_three, rate_three
        )
        grad_cross_low = grad_cross.astype(LOW)
        grad_mixed = mul(cross_whole[: 2 * cols], grad_cross_low, NT).astype(LOW)
        grad_mixed = exchange_rows(grad_mixed.reshape(n_rows, HEAD_DIM, rows))
        grads = pair_backward(cross_q, pair, 0, length, grad_mixed, cross_wide, cross_log)
        grads = exchange_rows(grads)
        grad_cq_t = grads[:, 0].reshape(2 * cols, rows)
        grad_pair = grads[:, 1:].reshape(2, heads, 2, HEAD_DIM, rows)
        grad_two = over_all_columns(grad_cq_t, query_whole)
        cross_gain_term = jnp.sum(grad_two * unit_two, axis=0)
        grad_self = grad_cross + normed_back(grad_two * cross_gain_f, unit_two, rate_two)
        grad_self_low = grad_self.astype(LOW)
        grad_mixed = mul(self_whole[: 2 * cols], grad_self_low, NT).astype(LOW)
        grad_mixed = exchange_rows(grad_mixed.reshape(n_rows, HEAD_DIM, rows))
        grads = pair_backward(qkv, qkv, 1, None, grad_mixed, self_wide, self_log)
        grads = exchange_rows(grads)
        grad_pair_t = grad_pair.reshape(2, 2 * cols, rows)
        grad_mid = sum_near(
            mul(grad_pair_t[0], pair_rows, TN) + mul(grad_pair_t[1], pair_other, TN)
        ).astype(LOW)
        patch_half = mul(halves(grad_mid)[0], patch_weights, NT).astype(LOW)
        by_kind = grad_pair.transpose(0, 2, 1, 3, 4).reshape(2, 2, cols, rows)
        yield (
            "middle",
            {
                "query": [(normed_two, grad_cq_t[i : i + cols], T_LAST) for i in (0, cols)],
                "pair": [[(patch_mid, by_kind[s, k], T_LAST) for k in range(2)] for s in range(2)],
                "patch": [(patch_in, value, TN) for value in shard_columns(grad_mid)],
                "cross_output": [
                    (cross_mixed_t[i : i + cols], grad_cross_low, NN) for i in (0, cols)
                ],
                "self_output": [(self_mixed_t[i : i + cols], grad_self_low, NN) for i in (0, cols)],
            },
        )
        grad_qkv_t = grads.reshape(2, 3 * cols, rows)
        grad_one = half_sum_near(
            mul(grad_qkv_t[0], qkv_rows, TN) + mul(grad_qkv_t[1], qkv_other, TN)
        )
        by_kind = grads.reshape(2, heads, 3, HEAD_DIM, rows).transpose(0, 2, 1, 3, 4)
        by_kind = by_kind.reshape(2, 3, cols, rows)
        gain_half, unit_half, rate_half, self_half = (
            halves(value)[0] for value in (gain_one, unit_one, rate_one, grad_self)
        )
        input_half = self_half + normed_back(grad_one * gain_half, unit_half, rate_half)
        onehot_half = halves(onehot)[0].astype(WIDE)
        table_term = jnp.concatenate(
            [
                lax.dot_general(onehot_half, value, TN, precision=lax.Precision.HIGHEST)
                for value in (grad_one * unit_half, grad_one)
            ],
            axis=0,
        )
        yield (
            "last",
            {
                "self": [[(normed_one, by_kind[s, k], T_LAST) for k in range(3)] for s in range(2)],
            },
        )
        yield "done", (result, input_half.astype(LOW), patch_half, table_term, hidden_gain_term, cross_gain_term)

    def product(*terms):
        dims = terms[0][2]
        left = jnp.concatenate([term[0] for term in terms], axis=dims[0][0][0])
        right = jnp.concatenate([term[1] for term in terms], axis=dims[0][1][0])
        return mul(left, right, dims).astype(LOW)

    def is_term(value):
        return isinstance(value, tuple)

    def sum_rows(both):
        part = lax.psum_scatter(both, "rows", scatter_dimension=1, tiled=True)
        total = part[0].astype(WIDE) + swap(part[1], "far").astype(WIDE)
        return lax.all_gather(total.astype(LOW), "rows", axis=0, tiled=True)

    steps = [one_group(group) for group in range(groups)]
    asked = [next(step) for step in steps]
    terms = {}
    while asked[0][0] != "done":
        gathered = [value for _, value in asked]
        terms.update(jax.tree.map(product, *gathered, is_leaf=is_term))
        if asked[0][0] == "hidden":
            hidden_total = sum_rows(
                jnp.stack([jnp.concatenate([terms["widen"][s], terms["narrow"][s]]) for s in range(2)])
            )
        elif asked[0][0] == "middle":
            output_total = sum_rows(
                jnp.stack(
                    [jnp.concatenate([terms["cross_output"][s], terms["self_output"][s]]) for s in range(2)]
                )
            )
            cross_total = sum_rows(
                jnp.stack(
                    [jnp.concatenate([terms["query"][s], *terms["pair"][s], terms["patch"][s]]) for s in range(2)]
                )
            )
        asked = [next(step) for step in steps]
    results, input_halves, patch_halves, tables, *gains = zip(*[value for _, value in asked])
    table = sum_near(sum(tables[1:], tables[0]))
    gain_terms = [sum(values[1:], values[0])[None] for values in gains]
    small = jnp.concatenate([table] + gain_terms + [jnp.zeros((62, width), WIDE)], axis=0).astype(LOW)
    last_total = sum_rows(
        jnp.stack(
            [jnp.concatenate([*terms["self"][s], value]) for s, value in enumerate(shard_columns(small))]
        )
    )
    outputs = over_heads(jnp.stack(results))
    input_grads = over_heads(jnp.stack(input_halves))
    patch_grads = over_heads(jnp.stack(patch_halves))
    kinds = last_total[: 3 * width].reshape(3, width, cols)
    table_total = last_total[3 * width : 3 * width + 2 * codes].reshape(2, codes, cols)
    gain_total = last_total[3 * width + 2 * codes :]
    gradients = (
        table_total.transpose(1, 0, 2),
        kinds,
        output_total[cols:],
        gain_total[1],
        cross_total[:width],
        cross_total[width : 3 * width].reshape(2, width, cols),
        output_total[:cols],
        cross_total[3 * width :],
        gain_total[0],
        hidden_total[:width],
        hidden_total[width:],
    )
    return (outputs, input_grads.astype(WIDE), patch_grads.astype(WIDE)) + tuple(
        value.astype(WIDE) for value in gradients
    )


def per_device(
    tokens,
    cam_index,
    patches,
    patch_len,
    camera_table,
    self_weights,
    self_output,
    cross_gain,
    cross_query,
    cross_pair,
    cross_output,
    patch_weights,
    hidden_gain,
    widen_weights,
    narrow_weights,
    cotangent,
):
    batches, rows, width = tokens.shape
    cols = self_weights.shape[2]
    heads = cols // HEAD_DIM
    codes = camera_table.shape[0]
    patch_rows, patch_width = patches.shape[1:]
    n_rows, n_heads = lax.axis_size("rows"), lax.axis_size("heads")
    row_rank, head_rank = lax.axis_index("rows"), lax.axis_index("heads")
    groups = 1
    objects = batches // groups
    full_lengths = jnp.full((objects,), n_rows * rows, jnp.int32)
    count = objects * rows

    def own_columns(value):
        return lax.dynamic_slice_in_dim(value, head_rank * cols, cols, value.ndim - 1)

    table_flat = camera_table.reshape(codes, -1)
    cross_gain_f = cross_gain.astype(WIDE)
    hidden_gain_f = hidden_gain.astype(WIDE)

    qkv_rows = (
        self_weights.reshape(3, width, heads, HEAD_DIM).transpose(2, 0, 3, 1).reshape(3 * cols, width)
    )
    qkv_rows_back = self_weights.transpose(0, 2, 1).reshape(3 * cols, width)
    pair_rows = cross_pair.transpose(0, 2, 1).reshape(2 * cols, width)
    query_rows = cross_query.T

    local = jnp.stack([self_output, cross_output, query_rows])
    piece = cols // n_rows
    local = lax.dynamic_slice_in_dim(local, row_rank * piece, piece, 1)
    whole = lax.all_gather(jnp.stack(gather_heads(local)), "rows", axis=0)
    whole = whole.transpose(2, 1, 0, 3, 4).reshape(3, n_heads * cols, width)
    self_whole, cross_whole, query_whole = whole[0], whole[1], whole[2]

    def over_all_columns(value_t, weight):
        return mul(jnp.concatenate(gather_heads(value_t), axis=0), weight, TN)

    def by_object(weight, value):
        return jnp.stack(
            [mul(weight, value[i * rows : (i + 1) * rows], NT).astype(LOW) for i in range(objects)]
        )

    def column_terms(value, grads_t):
        return [
            mul(value, grads_t[i : i + cols], (((0,), (1,)), ((), ())))
            for i in range(0, grads_t.shape[0], cols)
        ]

    def one_group(group):
        part = slice(group * objects, (group + 1) * objects)
        inputs = tokens[part].reshape(count, width).astype(WIDE)
        patch_in = patches[part].reshape(objects * patch_rows, patch_width)
        lengths = patch_len[part]
        grad_low = cotangent[part].reshape(count, width)
        onehot = (cam_index[part].reshape(count)[:, None] == jnp.arange(codes)[None, :]).astype(LOW)
        shift_scale = mul(onehot, table_flat)
        gain_one = 1.0 + shift_scale[:, :width]
        unit_one, rate_one = normed(inputs)
        normed_one = (unit_one * gain_one + shift_scale[:, width:]).astype(LOW)
        qkv_t = by_object(qkv_rows, normed_one)
        by_kind = qkv_t.reshape(objects, heads, 3, HEAD_DIM, rows).transpose(2, 1, 3, 0, 4)
        by_kind = by_kind.reshape(3, cols, count)
        self_pair = lax.all_gather(by_kind[1:], "rows", axis=0)
        patch_mid = mul(patch_in, patch_weights).astype(LOW)
        own_pair = mul(pair_rows, patch_mid, NT).astype(LOW).reshape(2, cols, -1)
        pair_t = lax.all_gather(own_pair, "rows", axis=0)
        self_mixed_t, self_wide, self_log = cross_forward(by_kind[0], self_pair, full_lengths)
        after_self = inputs + over_all_columns(self_mixed_t, self_whole)
        unit_two, rate_two = normed(after_self)
        normed_two = (unit_two * cross_gain_f).astype(LOW)
        cross_q_t = mul(query_rows, normed_two, NT).astype(LOW)
        cross_mixed_t, cross_wide, cross_log = cross_forward(cross_q_t, pair_t, lengths)
        after_cross = after_self + over_all_columns(cross_mixed_t, cross_whole)
        unit_three, rate_three = normed(after_cross)
        normed_three = (unit_three * hidden_gain_f).astype(LOW)
        pre_act = mul(normed_three, widen_weights)
        activated, act_back = jax.vjp(gelu_tanh, pre_act)
        activated = activated.astype(LOW)
        grad_pre = act_back(mul(grad_low, narrow_weights, NT))[0].astype(LOW)
        grad_three = sum_heads(mul(grad_pre, widen_weights, NT)).astype(WIDE)
        yield "heads", {"hidden": mul(activated, narrow_weights)}
        yield "rows", {
            "narrow": mul(activated, grad_low, TN),
            "widen": mul(normed_three, grad_pre, TN),
        }
        hidden_gain_term = jnp.sum(own_columns(grad_three * unit_three), axis=0)
        grad_cross = grad_low.astype(WIDE) + normed_back(
            grad_three * hidden_gain_f, unit_three, rate_three
        )
        grad_cross_low = grad_cross.astype(LOW)
        cross_output_term = mul(cross_mixed_t, grad_cross_low)
        grad_mixed_t = mul(cross_output, grad_cross_low, NT).astype(LOW)
        grad_cq_t, grad_pair_t = cross_backward(
            cross_q_t, pair_t, lengths, grad_mixed_t, cross_wide, cross_log
        )
        grad_two = over_all_columns(grad_cq_t, query_whole)
        grad_pair_t = lax.psum_scatter(grad_pair_t, "rows", scatter_dimension=0, tiled=False)
        grad_pair_t = grad_pair_t.reshape(2 * cols, -1)
        query_term = mul(normed_two, grad_cq_t, (((0,), (1,)), ((), ())))
        cross_gain_term = jnp.sum(own_columns(grad_two * unit_two), axis=0)
        grad_self = grad_cross + normed_back(grad_two * cross_gain_f, unit_two, rate_two)
        grad_self_low = grad_self.astype(LOW)
        self_output_term = mul(self_mixed_t, grad_self_low)
        yield "heads", {"patch": mul(grad_pair_t, pair_rows, TN)}
        yield "rows", {
            "query": query_term,
            "pair": column_terms(patch_mid, grad_pair_t),
            "cross_output": cross_output_term,
            "self_output": self_output_term,
        }
        grad_self_mixed_t = mul(self_output, grad_self_low, NT).astype(LOW)
        grad_q_t, grad_kv_t = cross_backward(
            by_kind[0], self_pair, full_lengths, grad_self_mixed_t, self_wide, self_log
        )
        grad_kv_t = lax.psum_scatter(grad_kv_t, "rows", scatter_dimension=0, tiled=False)
        grad_qkv_t = jnp.concatenate([grad_q_t[None], grad_kv_t]).reshape(3 * cols, count)
        grad_qkv_t = yield "after", (grad_qkv_t, ["patch", "narrow", "widen"])
        grad_mid = yield "take", "patch"
        patch_term = mul(patch_in, own_columns(grad_mid), TN)
        patch_grad = mul(grad_mid, patch_weights, NT)
        grad_one = sum_heads(mul(grad_qkv_t, qkv_rows_back, TN))
        grad_one = yield "after", (grad_one, ["query", "pair", "cross_output", "self_output"])
        grad_one = grad_one.astype(WIDE)
        input_grad = grad_self + normed_back(grad_one * gain_one, unit_one, rate_one)
        own_grad = own_columns(grad_one)
        table_term = jnp.stack(
            [
                lax.dot_general(onehot.astype(WIDE), v, TN, precision=lax.Precision.HIGHEST)
                for v in (own_grad * own_columns(unit_one), own_grad)
            ],
            axis=1,
        )
        small = [patch_term, table_term.reshape(2 * codes, cols)]
        small += [hidden_gain_term[None], cross_gain_term[None], jnp.zeros((14, cols), WIDE)]
        yield "rows", {
            "self": column_terms(normed_one, grad_qkv_t),
            "small": jnp.concatenate(small, axis=0),
        }
        hidden_sum = yield "take", "hidden"
        result = (after_cross + hidden_sum.astype(WIDE)).astype(LOW)
        yield (
            "done",
            (
                result.reshape(objects, rows, width),
                input_grad.reshape(objects, rows, width),
                patch_grad.reshape(objects, patch_rows, patch_width),
            ),
        )

    steps = [one_group(group) for group in range(groups)]
    asked = [next(step) for step in steps]
    totals, ahead = {}, []
    while asked[0][0] != "done":
        kind, what = asked[0]
        answers = [None] * groups
        if kind == "take":
            answers = jnp.split(totals[what], groups)
        elif kind == "after":
            early = {name: totals[name] for name in what[1]}
            answers = [value for _, (value, _) in asked]
            answers[-1], early = lax.optimization_barrier((answers[-1], early))
            totals.update(early)
        else:
            terms = [value for _, value in asked]
            if kind == "heads":
                terms = jax.tree.map(lambda *parts: jnp.concatenate(parts, axis=0), *terms)
            else:
                for value in terms[1:]:
                    terms[0] = add_trees(terms[0], value)
                terms = terms[0]
            if kind == "rows":
                terms = jax.tree.map(lambda value: value.astype(LOW), terms)
            if kind == "heads":
                totals.update({name: sum_heads(value) for name, value in terms.items()})
            else:
                before = {name: totals[name] for name in ahead}
                terms, before = lax.optimization_barrier((terms, before))
                totals.update(before)
                totals.update(lax.psum(terms, kind))
                ahead = list(terms)
        asked = [step.send(value) for step, value in zip(steps, answers)]
    outputs, input_grads, patch_grads = (
        jnp.concatenate([value[i] for _, value in asked], axis=0) for i in range(3)
    )
    patch_total, table_total, gains = jnp.split(
        totals["small"], [patch_width, patch_width + 2 * codes]
    )
    gradients = (
        table_total.reshape(codes, 2, cols),
        jnp.stack(totals["self"]),
        totals["self_output"],
        gains[1],
        totals["query"],
        jnp.stack(totals["pair"]),
        totals["cross_output"],
        patch_total,
        gains[0],
        totals["widen"],
        totals["narrow"],
    )
    return (outputs, input_grads, patch_grads) + tuple(value.astype(WIDE) for value in gradients)


def solution(mesh):
    sizes = mesh.shape
    paired = sizes["heads"] == 4 and sizes["rows"] == 8
    heads = ("far", "near") if paired else "heads"
    if paired:
        names = (*heads, "rows")
        mesh = jax.sharding.Mesh(mesh.devices.reshape(2, 2, sizes["rows"]), names)
    in_specs = (
        P(None, "rows", None),
        P(None, "rows"),
        P(None, "rows", None),
        P(),
        P(),
        P(None, None, heads),
        P(heads, None),
        P(),
        P(None, heads),
        P(None, None, heads),
        P(heads, None),
        P(),
        P(),
        P(None, heads),
        P(heads, None),
        P(None, "rows", None),
    )
    out_specs = (
        P(None, "rows", None),
        P(None, "rows", None),
        P(None, "rows", None),
        P(None, None, heads),
        P(None, None, heads),
        P(heads, None),
        P(heads),
        P(None, heads),
        P(None, None, heads),
        P(heads, None),
        P(None, heads),
        P(heads),
        P(None, heads),
        P(heads, None),
    )
    return jax.shard_map(
        paired_device if paired else per_device,
        mesh=mesh,
        in_specs=in_specs,
        out_specs=out_specs,
        check_vma=False,
    )
```

time: 863 us -> 966 us (1.12)
  waiting for transfers between devices: 190 us -> 435 us
  starting transfers between devices: 233 us -> 123 us
  blocking collectives: 46.1 us -> 0 us
  Pallas kernels: 113 us -> 86.9 us
  matrix products: 94.3 us -> 118 us
    ppermute x88 -> x28, starting transfers between devices: 202 us -> 49.6 us  [swap(): return lax.ppermute(value, axis, [(0, 1), (1, 0)])]
    reduce_scatter x2 -> x4, waiting for transfers between devices: 0.02 us -> 108 us  [sum_rows(): part = lax.psum_scatter(both, 'rows', scatter_dimension=1, tiled=True)]
    ppermute x88 -> x28, waiting for transfers between devices: 132 us -> 229 us  [swap(): return lax.ppermute(value, axis, [(0, 1), (1, 0)])]
    all_to_all x8 -> x18, waiting for transfers between devices: 13.5 us -> 66.3 us  [exchange_rows(): return lax.all_to_all(value, 'rows', 0, 0, tiled=True)]
    psum x2 -> x0, waiting for transfers between devices: 44.7 us -> none  [reduce_rows(): return lax.psum(value.astype(LOW), 'rows')]
    all_to_all x8 -> x18, starting transfers between devices: 30.7 us -> 72 us  [exchange_rows(): return lax.all_to_all(value, 'rows', 0, 0, tiled=True)]
    all_gather x3 -> x11, waiting for transfers between devices: 0.06 us -> 31.8 us  [the longest x1 19.8 us: paired_device(): widen_other = lax.all_gather(across[4], 'rows', axis=0, tiled=True)]
    pallas_call x8, Pallas kernels: 113 us -> 86.9 us  [the longest x4 54.7 us: pair_backward(): pl.pallas_call(kernel, grid_spec=pltpu.PrefetchScalarGridSpec(num_scalar_...]
  transfers between devices with their start and end apart: 103 -> 61, of which waited for: 42 -> 40; matrix products, arithmetic and copies ran while one was open for 23% -> 25% of each run, Pallas kernels for 12% -> 7%
where the time goes in v2:
time: 966 us; the launch traced here: 949 us
  waiting for transfers between devices  435 us (45%)
  starting transfers between devices  123 us (13%)
  matrix products  118 us (12%)
  local copies, waits for them, and re-layouts  97 us (10%)
  Pallas kernels  86.9 us (9%)
  other arithmetic  72.4 us (7%)
  between operations  16.8 us (2%)
    ppermute x28, waiting for transfers between devices, swap(): return lax.ppermute(value, axis, [(0, 1), (1, 0)])  229 us
    dot_general x72, matrix products, mul(): return lax.dot_general(left, right, dims, preferred_element_type=WIDE)  114 us
    reduce_scatter x4, waiting for transfers between devices, sum_rows(): part = lax.psum_scatter(both, 'rows', scatter_dimension=1, tiled=True)  108 us
    all_to_all x18, starting transfers between devices, exchange_rows(): return lax.all_to_all(value, 'rows', 0, 0, tiled=True)  72 us
    all_to_all x18, waiting for transfers between devices, exchange_rows(): return lax.all_to_all(value, 'rows', 0, 0, tiled=True)  66.3 us
    pallas_call x4, Pallas kernels, pair_backward(): pl.pallas_call(kernel, grid_spec=pltpu.PrefetchScalarGridSpec(num_scalar_...  54.7 us
    ppermute x28, starting transfers between devices, swap(): return lax.ppermute(value, axis, [(0, 1), (1, 0)])  49.6 us
    pallas_call x4, Pallas kernels, pair_forward(): pl.pallas_call(kernel, grid_spec=pltpu.PrefetchScalarGridSpec(num_scalar_...  32.2 us
  transfers between devices with their start and end apart: 61, of which 40 were waited for; matrix products, arithmetic and copies ran while one was open for 25% of the time, Pallas kernels for 7%

profile of v2, /device:TPU:0, one launch (start us, length us, event | category | flops | bytes accessed | tf_op | source)
XLA Modules:
  0.0 948.9 jit_solution(4987814329422531883)
XLA Ops:
  11.5 4.1 collective-permute-start
  15.6 9.1 collective-permute-done
  35.4 39.3 %collective-permute-done.2 = bf16[416,1024]{1,0:T(8,128)(2,1)S(1)} collective-permute-done((bf16[416,1024]{1,0:T(8,128)(2,1)S(1)}, bf16[416,1024]{1,0:T(8,128)(2,1)S(1)}, u32[]{:S(2)}, u32[]{:S(2)}) %collective-permute-start.2) | collective-permute-done | bytes 852000 | tf_op jit(solution)/shard_map/ppermute | solution.py:394
  76.6 9.4 collective-permute-done.3
  110.4 3.7 all-to-all-start
  120.2 11.6 %all-to-all-done.q_ref.k_ref.v_ref = bf16[8,3,64,256]{3,2,1,0:T(8,128)(2,1)S(1)} async-done(((bf16[8,3,64,256]{3,2,1,0:T(8,128)(2,1)}), bf16[8,3,64,256]{3,2,1,0:T(8,128)(2,1)S(1)}, u32[]{:S(2)}, u32[]{:S(2)}) %all-to-all-start) | async-done | bytes 786464 | tf_op jit(solution)/shard_map/all_to_all | solution.py:230
  131.7 8.8 pair_forward.4
  141.3 3.5 all-to-all-start.1
  147.7 4.0 all-to-all-done.1
  151.7 3.9 all-to-all-start.3
  164.3 3.3 all-gather.14.cloned.1.call-done
  173.1 4.1 all-to-all-start.2
  181.7 5.3 all-to-all-done.2.q_ref
  187.0 3.5 all-to-all-start.5
  193.6 8.8 pair_forward.5
  204.0 4.7 all-to-all-done.5.q_ref.k_ref.v_ref
  208.7 4.0 all-to-all-start.4
  212.7 8.2 pair_forward.6
  222.4 4.1 all-to-all-start.6
  228.0 3.5 fusion.231
  231.5 8.6 all-gather.20.cloned.1.call-done
  249.8 19.8 %all-gather.22.cloned.1.call-done = bf16[1024,1024]{1,0:T(8,128)(2,1)} async-done(((bf16[128,1024]{1,0:T(8,128)(2,1)}), bf16[1024,1024]{1,0:T(8,128)(2,1)}) %all-gather.22.cloned.1.call-update) | async-done | bytes 2097168 | tf_op jit(solution)/shard_map/all_gather | solution.py:491
  269.6 4.4 fusion.32
  284.1 6.5 collective-permute-done.11
  296.8 4.0 all-to-all-start.10
  302.5 5.3 all-to-all-done.10.g_ref
  309.9 16.0 %pair_backward.4 = bf16[8,3,64,256]{3,2,1,0:T(8,128)(2,1)S(1)} custom-call(s32[1]{0:T(128)} %get-tuple-element.160.len_ref, bf16[8,1,64,256]{3,2,1,0:T(8,128)(2,1)S(1)} %all-to-all-done.2.q_ref, bf16[8,2,64,256]{3,2,1,0:T(8,128)(2,1)S(1)} %copy-done.5, bf16[8,2,64,256]{3,2,1,0:T(8,128)(2,1)S(1)} %copy-done.5, bf16[8,64,256]{2,1,0:T(8,128)(2,1)} %all-to-all-done.10.g_ref, ...), custom_call_target="tpu_custom_call" | custom-call | flops 10066329600 | bytes 4194304 | tf_op jit(solution)/shard_map/pair_backward/pallas_call | solution.py:364
  326.8 4.4 all-to-all-start.11
  331.2 3.6 fusion.234
  337.7 6.0 all-to-all-done.11
  343.8 4.1 all-to-all-start.8
  362.9 3.9 all-to-all-start.7
  370.1 3.6 all-to-all-done.7.q_ref
  373.7 6.4 pair_forward.7
  381.6 4.0 all-to-all-start.9
  388.2 4.4 all-to-all-done.9
  392.6 4.1 all-to-all-start.12
  404.6 15.3 %pair_backward.5 = bf16[8,3,64,256]{3,2,1,0:T(8,128)(2,1)S(1)} custom-call(s32[1]{0:T(128)} %constant.95.clone.1.len_ref, bf16[8,3,64,256]{3,2,1,0:T(8,128)(2,1)S(1)} %all-to-all-done.q_ref.k_ref.v_ref, bf16[8,3,64,256]{3,2,1,0:T(8,128)(2,1)S(1)} %all-to-all-done.q_ref.k_ref.v_ref, bf16[8,3,64,256]{3,2,1,0:T(8,128)(2,1)S(1)} %all-to-all-done.q_ref.k_ref.v_ref, ...), custom_call_target="tpu_custom_call" | custom-call | flops 15099494400 | bytes 4194304 | tf_op jit(solution)/shard_map/pair_backward/pallas_call | solution.py:364
  420.8 3.8 all-to-all-start.13
  443.5 7.4 collective-permute-done.14
  457.2 3.9 all-to-all-start.14
  470.7 7.9 pair_backward.6
  478.6 4.7 all-to-all-start.15
  489.0 7.0 all-to-all-done.15
  508.5 3.8 all-to-all-start.16
  519.2 15.5 %pair_backward.7 = bf16[8,3,64,256]{3,2,1,0:T(8,128)(2,1)} custom-call(s32[1]{0:T(128)} %constant.95.clone.1.len_ref, bf16[8,3,64,256]{3,2,1,0:T(8,128)(2,1)S(1)} %all-to-all-done.5.q_ref.k_ref.v_ref, bf16[8,3,64,256]{3,2,1,0:T(8,128)(2,1)S(1)} %all-to-all-done.5.q_ref.k_ref.v_ref, bf16[8,3,64,256]{3,2,1,0:T(8,128)(2,1)S(1)} %all-to-all-done.5.q_ref.k_ref.v_ref, ...), custom_call_target="tpu_custom_call" | custom-call | flops 15099494400 | bytes 4194304 | tf_op jit(solution)/shard_map/pair_backward/pallas_call | solution.py:364
  534.7 4.4 all-to-all-start.17
  544.3 7.4 all-to-all-done.17
  577.4 5.3 collective-permute-done.19
  610.1 6.2 pad_maximum_fusion
  617.4 6.6 collective-permute-start.25
  628.6 13.2 %reduce-scatter.5.cloned.1.call-done = bf16[2,400,256]{2,1,0:T(8,128)(2,1)} async-done(((bf16[2,3200,256]{2,1,0:T(8,128)(2,1)}), bf16[2,400,256]{2,1,0:T(8,128)(2,1)}) %reduce-scatter.5.cloned.1.call-update) | async-done | bytes 409616 | tf_op jit(solution)/shard_map/reduce_scatter | solution.py:628
  645.3 9.7 %collective-permute-done.24 = bf16[400,256]{1,0:T(8,128)(2,1)S(1)} collective-permute-done((bf16[400,256]{1,0:T(8,128)(2,1)S(1)}, bf16[400,256]{1,0:T(8,128)(2,1)S(1)}, u32[]{:S(2)}, u32[]{:S(2)}) %collective-permute-start.24) | collective-permute-done | bytes 204832 | tf_op jit(solution)/shard_map/ppermute | solution.py:394
  656.7 39.6 %reduce-scatter.9.cloned.1.call-done = bf16[2,480,256]{2,1,0:T(8,128)(2,1)} async-done(((bf16[2,3840,256]{2,1,0:T(8,128)(2,1)}), bf16[2,480,256]{2,1,0:T(8,128)(2,1)}) %reduce-scatter.9.cloned.1.call-update) | async-done | bytes 491536 | tf_op jit(solution)/shard_map/reduce_scatter | solution.py:628
  699.7 11.5 %collective-permute-done.26 = bf16[480,256]{1,0:T(8,128)(2,1)S(1)} collective-permute-done((bf16[480,256]{1,0:T(8,128)(2,1)S(1)}, bf16[480,256]{1,0:T(8,128)(2,1)S(1)}, u32[]{:S(2)}, u32[]{:S(2)}) %collective-permute-start.26) | collective-permute-done | bytes 245792 | tf_op jit(solution)/shard_map/ppermute | solution.py:394
  716.3 54.7 %reduce-scatter.11.cloned.1.call-done = bf16[2,256,1024]{2,1,0:T(8,128)(2,1)} async-done(((bf16[2,2048,1024]{2,1,0:T(8,128)(2,1)}), bf16[2,256,1024]{2,1,0:T(8,128)(2,1)}) %reduce-scatter.11.cloned.1.call-update) | async-done | bytes 1048592 | tf_op jit(solution)/shard_map/reduce_scatter | solution.py:628
  780.1 17.9 %collective-permute-done.27 = bf16[256,1024]{1,0:T(8,128)(2,1)S(1)} collective-permute-done((bf16[256,1024]{1,0:T(8,128)(2,1)S(1)}, bf16[256,1024]{1,0:T(8,128)(2,1)S(1)}, u32[]{:S(2)}, u32[]{:S(2)}) %collective-permute-start.27) | collective-permute-done | bytes 524320 | tf_op jit(solution)/shard_map/ppermute | solution.py:394
  804.0 5.0 collective-permute-done.8
  813.8 21.5 %collective-permute-done.9 = bf16[2,128,1024]{2,1,0:T(8,128)(2,1)S(1)} collective-permute-done((bf16[2,128,1024]{2,1,0:T(8,128)(2,1)S(1)}, bf16[2,128,1024]{2,1,0:T(8,128)(2,1)S(1)}, u32[]{:S(2)}, u32[]{:S(2)}) %collective-permute-start.9) | collective-permute-done | bytes 524320 | tf_op jit(solution)/shard_map/ppermute | solution.py:394
  837.0 3.4 collective-permute-start.21
  841.9 37.6 %collective-permute-done.10 = bf16[2,2,128,1024]{3,2,1,0:T(8,128)(2,1)S(1)} collective-permute-done((bf16[2,2,128,1024]{3,2,1,0:T(8,128)(2,1)S(1)}, bf16[2,2,128,1024]{3,2,1,0:T(8,128)(2,1)S(1)}, u32[]{:S(2)}, u32[]{:S(2)}) %collective-permute-start.10) | collective-permute-done | bytes 1048608 | tf_op jit(solution)/shard_map/ppermute | solution.py:394
  884.9 15.4 %collective-permute-done.22 = bf16[2,2,128,768]{3,2,1,0:T(8,128)(2,1)S(1)} collective-permute-done((bf16[2,2,128,768]{3,2,1,0:T(8,128)(2,1)S(1)}, bf16[2,2,128,768]{3,2,1,0:T(8,128)(2,1)S(1)}, u32[]{:S(2)}, u32[]{:S(2)}) %collective-permute-start.22) | collective-permute-done | bytes 786464 | tf_op jit(solution)/shard_map/ppermute | solution.py:394
  903.0 17.0 %collective-permute-done.18 = bf16[2,2,128,1024]{3,2,1,0:T(8,128)(2,1)S(1)} collective-permute-done((bf16[2,2,128,1024]{3,2,1,0:T(8,128)(2,1)S(1)}, bf16[2,2,128,1024]{3,2,1,0:T(8,128)(2,1)S(1)}, u32[]{:S(2)}, u32[]{:S(2)}) %collective-permute-start.18) | collective-permute-done | bytes 1048608 | tf_op jit(solution)/shard_map/ppermute | solution.py:394
  935.2 6.7 slice_convert_fusion
  (672 shorter events, 323.6 us)
Async XLA Ops:
  7.2 99.9 %all-gather.12.cloned.1.call-start = ((), (), s32[]{:S(2)}) async-start(), calls=%async_computation.22 | async-start | bytes 1769472 | tf_op jit(solution)/shard_map/all_gather | solution.py:474
  11.5 13.2 %collective-permute-start = (bf16[96,1024]{1,0:T(8,128)(2,1)S(1)}, bf16[96,1024]{1,0:T(8,128)(2,1)S(1)}, u32[]{:S(2)}, u32[]{:S(2)}) collective-permute-start(bf16[96,1024]{1,0:T(8,128)(2,1)S(1)} %constant_dynamic-slice_fusion.8), channel_id=1, source_target_pairs={{0,16},{16,0},{1,17},{17,1},{2,18},{18,2},{3,19},{19,3},{4,20},{20... | collective-permute-start | bytes 589832 | tf_op jit(solution)/shard_map/ppermute | solution.py:394
  25.4 119.4 %all-gather.18.cloned.1.call-start = ((), (), s32[]{:S(2)}) async-start(), calls=%async_computation.25 | async-start | bytes 1179648 | tf_op jit(solution)/shard_map/all_gather | solution.py:490
  35.4 39.4 %collective-permute-start.2 = (bf16[416,1024]{1,0:T(8,128)(2,1)S(1)}, bf16[416,1024]{1,0:T(8,128)(2,1)S(1)}, u32[]{:S(2)}, u32[]{:S(2)}) collective-permute-start(bf16[416,1024]{1,0:T(8,128)(2,1)S(1)} %dynamic-slice_dynamic-update-slice_fusion), channel_id=1, source_target_pairs={{0,16},{16,0},{1,17},{17,1},{2,18},{18,2},{3,19},{19,3},{4,20},{20... | collective-permute-start | bytes 2555912 | tf_op jit(solution)/shard_map/ppermute | solution.py:394
  75.4 83.6 %all-gather.16.cloned.1.call-start = ((), (), s32[]{:S(2)}) async-start(), calls=%async_computation.24 | async-start | bytes 2359296 | tf_op jit(solution)/shard_map/all_gather | solution.py:484
  76.5 9.5 collective-permute-start.3
  87.0 80.7 %all-gather.14.cloned.1.call-start = ((), (), s32[]{:S(2)}) async-start(), calls=%async_computation.23 | async-start | bytes 2359296 | tf_op jit(solution)/shard_map/all_gather | solution.py:484
  87.5 140.5 %all-gather.24.cloned.1.call-start = ((), (), s32[]{:S(2)}) async-start(), calls=%async_computation.28 | async-start | bytes 2359296 | tf_op jit(solution)/shard_map/all_gather | solution.py:492
  95.7 263.5 %copy-start.135 = (f32[1024]{0:T(1024)}, f32[1024]{0:T(1024)S(1)}, u32[]{:S(2)}) copy-start(f32[1024]{0:T(1024)S(1)} %convert_element_type.425) | copy-start | bytes 12292
  110.4 21.4 %all-to-all-start = ((bf16[8,3,64,256]{3,2,1,0:T(8,128)(2,1)}), bf16[8,3,64,256]{3,2,1,0:T(8,128)(2,1)S(1)}, u32[]{:S(2)}, u32[]{:S(2)}) async-start(bf16[8,3,64,256]{3,2,1,0:T(8,128)(2,1)} %bitcast.387), calls=%async_computation | async-start | bytes 1572864 | tf_op jit(solution)/shard_map/all_to_all | solution.py:230
  114.1 126.0 %all-gather.20.cloned.1.call-start = ((), (), s32[]{:S(2)}) async-start(), calls=%async_computation.26 | async-start | bytes 2359296 | tf_op jit(solution)/shard_map/all_gather | solution.py:484
  120.1 365.5 %copy-start.139 = (pred[256,32]{1,0:T(32,128)(4,1)}, pred[256,32]{1,0:T(32,128)(4,1)S(1)}, u32[]{:S(2)}) copy-start(pred[256,32]{1,0:T(32,128)(4,1)S(1)} %iota_compare_fusion.1) | copy-start | bytes 24580
  141.3 10.4 %all-to-all-start.1 = ((bf16[8,64,256]{2,1,0:T(8,128)(2,1)}), bf16[8,64,256]{2,1,0:T(8,128)(2,1)S(1)}, u32[]{:S(2)}, u32[]{:S(2)}) async-start(bf16[8,64,256]{2,1,0:T(8,128)(2,1)} %get-tuple-element.26), calls=%async_computation.1 | async-start | bytes 524288 | tf_op jit(solution)/shard_map/all_to_all | solution.py:230
  151.7 21.4 %all-to-all-start.3 = ((bf16[8,2,64,256]{3,2,1,0:T(8,128)(2,1)}), bf16[8,2,64,256]{3,2,1,0:T(8,128)(2,1)S(1)}, u32[]{:S(2)}, u32[]{:S(2)}) async-start(bf16[8,2,64,256]{3,2,1,0:T(8,128)(2,1)} %bitcast.393), calls=%async_computation.3 | async-start | bytes 1048576 | tf_op jit(solution)/shard_map/all_to_all | solution.py:230
  155.6 8.7 collective-permute-start.1
  173.1 13.9 %all-to-all-start.2 = ((bf16[8,1,64,256]{3,2,1,0:T(8,128)(2,1)}), bf16[8,1,64,256]{3,2,1,0:T(8,128)(2,1)S(1)}, u32[]{:S(2)}, u32[]{:S(2)}) async-start(bf16[8,1,64,256]{3,2,1,0:T(8,128)(2,1)} %bitcast.22), calls=%async_computation.2 | async-start | bytes 524288 | tf_op jit(solution)/shard_map/all_to_all | solution.py:230
  187.0 21.7 %all-to-all-start.5 = ((bf16[8,3,64,256]{3,2,1,0:T(8,128)(2,1)}), bf16[8,3,64,256]{3,2,1,0:T(8,128)(2,1)S(1)}, u32[]{:S(2)}, u32[]{:S(2)}) async-start(bf16[8,3,64,256]{3,2,1,0:T(8,128)(2,1)} %bitcast.385), calls=%async_computation.5 | async-start | bytes 1572864 | tf_op jit(solution)/shard_map/all_to_all | solution.py:230
  190.6 79.0 %all-gather.22.cloned.1.call-start = ((), (), s32[]{:S(2)}) async-start(), calls=%async_computation.27 | async-start | bytes 2359296 | tf_op jit(solution)/shard_map/all_gather | solution.py:491
  208.7 13.7 %all-to-all-start.4 = ((bf16[8,64,256]{2,1,0:T(8,128)(2,1)}), bf16[8,64,256]{2,1,0:T(8,128)(2,1)}, u32[]{:S(2)}, u32[]{:S(2)}) async-start(bf16[8,64,256]{2,1,0:T(8,128)(2,1)} %copy-done.9), calls=%async_computation.4 | async-start | bytes 524288 | tf_op jit(solution)/shard_map/all_to_all | solution.py:230
  222.4 58.0 %all-to-all-start.6 = ((bf16[8,64,256]{2,1,0:T(8,128)(2,1)}), bf16[8,64,256]{2,1,0:T(8,128)(2,1)}, u32[]{:S(2)}, u32[]{:S(2)}) async-start(bf16[8,64,256]{2,1,0:T(8,128)(2,1)} %copy-done.6), calls=%async_computation.6 | async-start | bytes 524288 | tf_op jit(solution)/shard_map/all_to_all | solution.py:230
  226.5 13.6 %collective-permute-start.4 = (bf16[512,256]{1,0:T(8,128)(2,1)}, bf16[512,256]{1,0:T(8,128)(2,1)}, u32[]{:S(2)}, u32[]{:S(2)}) collective-permute-start(bf16[512,256]{1,0:T(8,128)(2,1)} %bitcast.26), channel_id=1, source_target_pairs={{0,8},{8,0},{1,9},{9,1},{2,10},{10,2},{3,11},{11,3},{4,12},{12,4},... | collective-permute-start | bytes 786440 | tf_op jit(solution)/shard_map/ppermute | solution.py:394
  275.5 15.1 %collective-permute-start.11 = (bf16[256,1024]{1,0:T(8,128)(2,1)}, bf16[256,1024]{1,0:T(8,128)(2,1)}, u32[]{:S(2)}, u32[]{:S(2)}) collective-permute-start(bf16[256,1024]{1,0:T(8,128)(2,1)} %fusion.5), channel_id=1, source_target_pairs={{0,8},{8,0},{1,9},{9,1},{2,10},{10,2},{3,11},{11,3},{4,12},{12,4},... | collective-permute-start | bytes 1572872 | tf_op jit(solution)/shard_map/ppermute | solution.py:394
  280.4 54.4 %collective-permute-start.6 = (bf16[512,256]{1,0:T(8,128)(2,1)}, bf16[512,256]{1,0:T(8,128)(2,1)}, u32[]{:S(2)}, u32[]{:S(2)}) collective-permute-start(bf16[512,256]{1,0:T(8,128)(2,1)} %bitcast.33), channel_id=1, source_target_pairs={{0,8},{8,0},{1,9},{9,1},{2,10},{10,2},{3,11},{11,3},{4,12},{12,4},... | collective-permute-start | bytes 786440 | tf_op jit(solution)/shard_map/ppermute | solution.py:394
  296.8 11.0 %all-to-all-start.10 = ((bf16[8,64,256]{2,1,0:T(8,128)(2,1)}), bf16[8,64,256]{2,1,0:T(8,128)(2,1)}, u32[]{:S(2)}, u32[]{:S(2)}) async-start(bf16[8,64,256]{2,1,0:T(8,128)(2,1)} %bitcast.426), calls=%async_computation.10 | async-start | bytes 524288 | tf_op jit(solution)/shard_map/all_to_all | solution.py:230
  326.8 17.0 %all-to-all-start.11 = ((bf16[8,3,64,256]{3,2,1,0:T(8,128)(2,1)}), bf16[8,3,64,256]{3,2,1,0:T(8,128)(2,1)}, u32[]{:S(2)}, u32[]{:S(2)}) async-start(bf16[8,3,64,256]{3,2,1,0:T(8,128)(2,1)} %copy-done.2), calls=%async_computation.11 | async-start | bytes 1572864 | tf_op jit(solution)/shard_map/all_to_all | solution.py:230
  343.8 19.1 %all-to-all-start.8 = ((bf16[8,2,64,256]{3,2,1,0:T(8,128)(2,1)}), bf16[8,2,64,256]{3,2,1,0:T(8,128)(2,1)}, u32[]{:S(2)}, u32[]{:S(2)}) async-start(bf16[8,2,64,256]{3,2,1,0:T(8,128)(2,1)} %bitcast.392), calls=%async_computation.8 | async-start | bytes 1048576 | tf_op jit(solution)/shard_map/all_to_all | solution.py:230
  349.1 8.6 collective-permute-start.12
  362.9 10.8 %all-to-all-start.7 = ((bf16[8,1,64,256]{3,2,1,0:T(8,128)(2,1)}), bf16[8,1,64,256]{3,2,1,0:T(8,128)(2,1)S(1)}, u32[]{:S(2)}, u32[]{:S(2)}) async-start(bf16[8,1,64,256]{3,2,1,0:T(8,128)(2,1)} %bitcast.423), calls=%async_computation.7 | async-start | bytes 524288 | tf_op jit(solution)/shard_map/all_to_all | solution.py:230
  381.6 11.0 %all-to-all-start.9 = ((bf16[8,64,256]{2,1,0:T(8,128)(2,1)}), bf16[8,64,256]{2,1,0:T(8,128)(2,1)}, u32[]{:S(2)}, u32[]{:S(2)}) async-start(bf16[8,64,256]{2,1,0:T(8,128)(2,1)} %copy-done.10), calls=%async_computation.9 | async-start | bytes 524288 | tf_op jit(solution)/shard_map/all_to_all | solution.py:230
  392.6 11.0 %all-to-all-start.12 = ((bf16[8,64,256]{2,1,0:T(8,128)(2,1)}), bf16[8,64,256]{2,1,0:T(8,128)(2,1)}, u32[]{:S(2)}, u32[]{:S(2)}) async-start(bf16[8,64,256]{2,1,0:T(8,128)(2,1)} %bitcast.425), calls=%async_computation.12 | async-start | bytes 524288 | tf_op jit(solution)/shard_map/all_to_all | solution.py:230
  399.4 25.2 %collective-permute-start.7 = (bf16[512,256]{1,0:T(8,128)(2,1)}, bf16[512,256]{1,0:T(8,128)(2,1)}, u32[]{:S(2)}, u32[]{:S(2)}) collective-permute-start(bf16[512,256]{1,0:T(8,128)(2,1)} %bitcast.38), channel_id=1, source_target_pairs={{0,8},{8,0},{1,9},{9,1},{2,10},{10,2},{3,11},{11,3},{4,12},{12,4},... | collective-permute-start | bytes 786440 | tf_op jit(solution)/shard_map/ppermute | solution.py:394
  420.8 18.7 %all-to-all-start.13 = ((bf16[8,3,64,256]{3,2,1,0:T(8,128)(2,1)}), bf16[8,3,64,256]{3,2,1,0:T(8,128)(2,1)S(1)}, u32[]{:S(2)}, u32[]{:S(2)}) async-start(bf16[8,3,64,256]{3,2,1,0:T(8,128)(2,1)} %copy-done.1), calls=%async_computation.13 | async-start | bytes 1572864 | tf_op jit(solution)/shard_map/all_to_all | solution.py:230
  436.3 14.6 %collective-permute-start.14 = (bf16[256,1024]{1,0:T(8,128)(2,1)}, bf16[256,1024]{1,0:T(8,128)(2,1)}, u32[]{:S(2)}, u32[]{:S(2)}) collective-permute-start(bf16[256,1024]{1,0:T(8,128)(2,1)} %fusion.6), channel_id=1, source_target_pairs={{0,8},{8,0},{1,9},{9,1},{2,10},{10,2},{3,11},{11,3},{4,12},{12,4},... | collective-permute-start | bytes 1572872 | tf_op jit(solution)/shard_map/ppermute | solution.py:394
  457.2 10.8 %all-to-all-start.14 = ((bf16[8,64,256]{2,1,0:T(8,128)(2,1)}), bf16[8,64,256]{2,1,0:T(8,128)(2,1)S(1)}, u32[]{:S(2)}, u32[]{:S(2)}) async-start(bf16[8,64,256]{2,1,0:T(8,128)(2,1)} %bitcast.424), calls=%async_computation.14 | async-start | bytes 524288 | tf_op jit(solution)/shard_map/all_to_all | solution.py:230
  464.3 21.3 %collective-permute-start.13 = (bf16[128,1024]{1,0:T(8,128)(2,1)}, bf16[128,1024]{1,0:T(8,128)(2,1)}, u32[]{:S(2)}, u32[]{:S(2)}) collective-permute-start(bf16[128,1024]{1,0:T(8,128)(2,1)} %dynamic-slice_convert_fusion.1), channel_id=1, source_target_pairs={{0,8},{8,0},{1,9},{9,1},{2,10},{10,2},{3,11},{11,3},{4,12},{12,4},... | collective-permute-start | bytes 786440 | tf_op jit(solution)/shard_map/ppermute | solution.py:394
  478.6 17.4 %all-to-all-start.15 = ((bf16[8,3,64,256]{3,2,1,0:T(8,128)(2,1)}), bf16[8,3,64,256]{3,2,1,0:T(8,128)(2,1)}, u32[]{:S(2)}, u32[]{:S(2)}) async-start(bf16[8,3,64,256]{3,2,1,0:T(8,128)(2,1)} %pair_backward.6), calls=%async_computation.15 | async-start | bytes 1572864 | tf_op jit(solution)/shard_map/all_to_all | solution.py:230
  497.1 6.4 collective-permute-start.15
  508.5 10.7 %all-to-all-start.16 = ((bf16[8,64,256]{2,1,0:T(8,128)(2,1)}), bf16[8,64,256]{2,1,0:T(8,128)(2,1)S(1)}, u32[]{:S(2)}, u32[]{:S(2)}) async-start(bf16[8,64,256]{2,1,0:T(8,128)(2,1)} %bitcast.61), calls=%async_computation.16 | async-start | bytes 524288 | tf_op jit(solution)/shard_map/all_to_all | solution.py:230
  534.7 17.0 %all-to-all-start.17 = ((bf16[8,3,64,256]{3,2,1,0:T(8,128)(2,1)}), bf16[8,3,64,256]{3,2,1,0:T(8,128)(2,1)}, u32[]{:S(2)}, u32[]{:S(2)}) async-start(bf16[8,3,64,256]{3,2,1,0:T(8,128)(2,1)} %pair_backward.7), calls=%async_computation.17 | async-start | bytes 1572864 | tf_op jit(solution)/shard_map/all_to_all | solution.py:230
  539.1 77.4 %reduce-scatter.7.cloned.1.call-start = ((), (), s32[]{:S(2)}) async-start(), calls=%async_computation.31 | async-start | bytes 2359296 | tf_op jit(solution)/shard_map/reduce_scatter | solution.py:628
  544.0 97.8 %reduce-scatter.5.cloned.1.call-start = ((), (), s32[]{:S(2)}) async-start(), calls=%async_computation.29 | async-start | bytes 3686400 | tf_op jit(solution)/shard_map/reduce_scatter | solution.py:628
  555.1 7.0 collective-permute-start.16
  562.9 5.0 collective-permute-start.23
  570.4 125.9 %reduce-scatter.9.cloned.1.call-start = ((), (), s32[]{:S(2)}) async-start(), calls=%async_computation.33 | async-start | bytes 4423680 | tf_op jit(solution)/shard_map/reduce_scatter | solution.py:628
  573.3 9.3 collective-permute-start.19
  585.8 9.2 collective-permute-start.20
  599.1 172.0 %reduce-scatter.11.cloned.1.call-start = ((), (), s32[]{:S(2)}) async-start(), calls=%async_computation.35 | async-start | bytes 9437184 | tf_op jit(solution)/shard_map/reduce_scatter | solution.py:628
  616.4 97.0 %copy-start.161 = (f32[256]{0:T(256)S(1)}, f32[256]{0:T(256)}, u32[]{:S(2)}) copy-start(f32[256]{0:T(256)} %add_rsqrt_fusion.5) | copy-start | bytes 3076
  616.4 307.4 %all-gather.28.cloned.1.call-start = ((), (), s32[]{:S(2)}) async-start(), calls=%async_computation.32 | async-start | bytes 1179648 | tf_op jit(solution)/shard_map/all_gather | solution.py:630
  617.4 9.5 %collective-permute-start.25 = (bf16[64,1024]{1,0:T(8,128)(2,1)S(1)}, bf16[64,1024]{1,0:T(8,128)(2,1)S(1)}, u32[]{:S(2)}, u32[]{:S(2)}) collective-permute-start(bf16[64,1024]{1,0:T(8,128)(2,1)S(1)} %slice_bitcast_fusion.14), channel_id=1, source_target_pairs={{0,16},{16,0},{1,17},{17,1},{2,18},{18,2},{3,19},{19,3},{4,20},{20... | collective-permute-start | bytes 393224 | tf_op jit(solution)/shard_map/ppermute | solution.py:394
  628.6 297.9 %all-gather.26.cloned.1.call-start = ((), (), s32[]{:S(2)}) async-start(), calls=%async_computation.30 | async-start | bytes 1843200 | tf_op jit(solution)/shard_map/all_gather | solution.py:630
  642.8 12.2 %collective-permute-start.24 = (bf16[400,256]{1,0:T(8,128)(2,1)S(1)}, bf16[400,256]{1,0:T(8,128)(2,1)S(1)}, u32[]{:S(2)}, u32[]{:S(2)}) collective-permute-start(bf16[400,256]{1,0:T(8,128)(2,1)S(1)} %slice_bitcast_fusion.4), channel_id=1, source_target_pairs={{0,16},{16,0},{1,17},{17,1},{2,18},{18,2},{3,19},{19,3},{4,20},{20... | collective-permute-start | bytes 614408 | tf_op jit(solution)/shard_map/ppermute | solution.py:394
  656.7 273.9 %all-gather.30.cloned.1.call-start = ((), (), s32[]{:S(2)}) async-start(), calls=%async_computation.34 | async-start | bytes 2211840 | tf_op jit(solution)/shard_map/all_gather | solution.py:630
  697.2 13.9 %collective-permute-start.26 = (bf16[480,256]{1,0:T(8,128)(2,1)S(1)}, bf16[480,256]{1,0:T(8,128)(2,1)S(1)}, u32[]{:S(2)}, u32[]{:S(2)}) collective-permute-start(bf16[480,256]{1,0:T(8,128)(2,1)S(1)} %slice_bitcast_fusion.2), channel_id=1, source_target_pairs={{0,16},{16,0},{1,17},{17,1},{2,18},{18,2},{3,19},{19,3},{4,20},{20... | collective-permute-start | bytes 737288 | tf_op jit(solution)/shard_map/ppermute | solution.py:394
  712.9 222.3 %all-gather.32.cloned.1.call-start = ((), (), s32[]{:S(2)}) async-start(), calls=%async_computation.36 | async-start | bytes 4718592 | tf_op jit(solution)/shard_map/all_gather | solution.py:630
  772.2 25.9 %collective-permute-start.27 = (bf16[256,1024]{1,0:T(8,128)(2,1)S(1)}, bf16[256,1024]{1,0:T(8,128)(2,1)S(1)}, u32[]{:S(2)}, u32[]{:S(2)}) collective-permute-start(bf16[256,1024]{1,0:T(8,128)(2,1)S(1)} %slice_bitcast_fusion), channel_id=1, source_target_pairs={{0,16},{16,0},{1,17},{17,1},{2,18},{18,2},{3,19},{19,3},{4,20},{20... | collective-permute-start | bytes 1572872 | tf_op jit(solution)/shard_map/ppermute | solution.py:394
  777.9 24.4 %collective-permute-start.5 = (bf16[128,1024]{1,0:T(8,128)(2,1)}, bf16[128,1024]{1,0:T(8,128)(2,1)}, u32[]{:S(2)}, u32[]{:S(2)}) collective-permute-start(bf16[128,1024]{1,0:T(8,128)(2,1)} %dynamic-slice_convert_fusion.3), channel_id=1, source_target_pairs={{0,8},{8,0},{1,9},{9,1},{2,10},{10,2},{3,11},{11,3},{4,12},{12,4},... | collective-permute-start | bytes 786440 | tf_op jit(solution)/shard_map/ppermute | solution.py:394
  801.7 7.4 collective-permute-start.8
  809.3 26.1 %collective-permute-start.9 = (bf16[2,128,1024]{2,1,0:T(8,128)(2,1)S(1)}, bf16[2,128,1024]{2,1,0:T(8,128)(2,1)S(1)}, u32[]{:S(2)}, u32[]{:S(2)}) collective-permute-start(bf16[2,128,1024]{2,1,0:T(8,128)(2,1)S(1)} %get-tuple-element.140), channel_id=1, source_target_pairs={{0,16},{16,0},{1,17},{17,1},{2,18},{18,2},{3,19},{19,3},{4,20},{20... | collective-permute-start | bytes 1572872 | tf_op jit(solution)/shard_map/ppermute | solution.py:394
  835.5 43.9 %collective-permute-start.10 = (bf16[2,2,128,1024]{3,2,1,0:T(8,128)(2,1)S(1)}, bf16[2,2,128,1024]{3,2,1,0:T(8,128)(2,1)S(1)}, u32[]{:S(2)}, u32[]{:S(2)}) collective-permute-start(bf16[2,2,128,1024]{3,2,1,0:T(8,128)(2,1)S(1)} %get-tuple-element.98), channel_id=1, source_target_pairs={{0,8},{8,0},{1,9},{9,1},{2,10},{10,2},{3,11},{11,3},{4,12},{12,4},... | collective-permute-start | bytes 3145736 | tf_op jit(solution)/shard_map/ppermute | solution.py:394
  837.0 42.6 %collective-permute-start.21 = (bf16[2,128,768]{2,1,0:T(8,128)(2,1)S(1)}, bf16[2,128,768]{2,1,0:T(8,128)(2,1)S(1)}, u32[]{:S(2)}, u32[]{:S(2)}) collective-permute-start(bf16[2,128,768]{2,1,0:T(8,128)(2,1)S(1)} %get-tuple-element.146), channel_id=1, source_target_pairs={{0,16},{16,0},{1,17},{17,1},{2,18},{18,2},{3,19},{19,3},{4,20},{20... | collective-permute-start | bytes 1179656 | tf_op jit(solution)/shard_map/ppermute | solution.py:394
  840.9 39.5 %collective-permute-start.17 = (bf16[2,128,1024]{2,1,0:T(8,128)(2,1)S(1)}, bf16[2,128,1024]{2,1,0:T(8,128)(2,1)S(1)}, u32[]{:S(2)}, u32[]{:S(2)}) collective-permute-start(bf16[2,128,1024]{2,1,0:T(8,128)(2,1)S(1)} %get-tuple-element.138), channel_id=1, source_target_pairs={{0,16},{16,0},{1,17},{17,1},{2,18},{18,2},{3,19},{19,3},{4,20},{20... | collective-permute-start | bytes 1572872 | tf_op jit(solution)/shard_map/ppermute | solution.py:394
  879.8 20.5 %collective-permute-start.22 = (bf16[2,2,128,768]{3,2,1,0:T(8,128)(2,1)S(1)}, bf16[2,2,128,768]{3,2,1,0:T(8,128)(2,1)S(1)}, u32[]{:S(2)}, u32[]{:S(2)}) collective-permute-start(bf16[2,2,128,768]{3,2,1,0:T(8,128)(2,1)S(1)} %get-tuple-element.121), channel_id=1, source_target_pairs={{0,8},{8,0},{1,9},{9,1},{2,10},{10,2},{3,11},{11,3},{4,12},{12,4},... | collective-permute-start | bytes 2359304 | tf_op jit(solution)/shard_map/ppermute | solution.py:394
  880.6 39.3 %collective-permute-start.18 = (bf16[2,2,128,1024]{3,2,1,0:T(8,128)(2,1)S(1)}, bf16[2,2,128,1024]{3,2,1,0:T(8,128)(2,1)S(1)}, u32[]{:S(2)}, u32[]{:S(2)}) collective-permute-start(bf16[2,2,128,1024]{3,2,1,0:T(8,128)(2,1)S(1)} %get-tuple-element.88), channel_id=1, source_target_pairs={{0,8},{8,0},{1,9},{9,1},{2,10},{10,2},{3,11},{11,3},{4,12},{12,4},... | collective-permute-start | bytes 3145736 | tf_op jit(solution)/shard_map/ppermute | solution.py:394
  (168 other events, 1016.0 us)
Sparse Core Ops, SparseCore 0:
  25.6 26.8 all-gather.11
  75.6 22.0 all-gather.17
  100.1 32.6 all-gather.15
  134.6 33.0 all-gather.13
  169.4 37.8 all-gather.23
  209.0 31.0 all-gather.19
  242.0 27.5 all-gather.21
  544.2 46.3 reduce-scatter.6
  594.9 46.8 reduce-scatter.4
  646.2 50.0 reduce-scatter.8
  699.7 71.2 reduce-scatter.10
  773.0 23.4 all-gather.27
  798.5 25.9 all-gather.25
  827.0 27.3 all-gather.29
  856.8 36.7 all-gather.31

commit v3 on v2

--- a/solution.py
+++ b/solution.py
@@ -253,13 +253,13 @@
 
 
 def pair_forward(queries, pair, key_at, length=None):
-    blocks, _, width, rows = queries.shape
-    pair_rows = pair.shape[3]
-    lengths = jnp.full((1,), blocks * pair_rows, jnp.int32) if length is None else length
+    blocks, objects, _, width, rows = queries.shape
+    pair_rows = pair.shape[4]
+    lengths = jnp.full((objects,), blocks * pair_rows, jnp.int32) if length is None else length
 
     def kernel(len_ref, q_ref, k_ref, v_ref, mixed_ref, wide_ref, log_ref, keys_t, values):
         def run(live):
-            @pl.when(pl.program_id(0) == 0)
+            @pl.when(pl.program_id(1) == 0)
             def _():
                 for c in range(live):
                     keys_t[:, c * pair_rows : (c + 1) * pair_rows] = k_ref[c]
@@ -276,42 +276,42 @@
         if length is None:
             run(blocks)
         else:
-            by_length(len_ref[0], blocks * pair_rows, blocks, run)
-
-    block = pl.BlockSpec((None, width, rows), lambda i, lens: (i, 0, 0))
+            by_length(len_ref[pl.program_id(0)], blocks * pair_rows, blocks, run)
+
+    block = pl.BlockSpec((None, None, width, rows), lambda o, i, lens: (i, o, 0, 0))
     return pl.pallas_call(
         kernel,
         grid_spec=pltpu.PrefetchScalarGridSpec(
             num_scalar_prefetch=1,
-            grid=(blocks,),
+            grid=(objects, blocks),
             in_specs=[
-                pl.BlockSpec((None, None, width, rows), lambda i, lens: (i, 0, 0, 0)),
-                pl.BlockSpec((blocks, None, width, pair_rows), lambda i, lens: (0, key_at, 0, 0)),
-                pl.BlockSpec((blocks, None, width, pair_rows), lambda i, lens: (0, key_at + 1, 0, 0)),
-            ],
-            out_specs=[block, block, pl.BlockSpec((None, 1, rows), lambda i, lens: (i, 0, 0))],
+                pl.BlockSpec((None, None, None, width, rows), lambda o, i, lens: (i, o, 0, 0, 0)),
+                pl.BlockSpec((blocks, None, None, width, pair_rows), lambda o, i, lens: (0, o, key_at, 0, 0)),
+                pl.BlockSpec((blocks, None, None, width, pair_rows), lambda o, i, lens: (0, o, key_at + 1, 0, 0)),
+            ],
+            out_specs=[block, block, pl.BlockSpec((None, None, 1, rows), lambda o, i, lens: (i, o, 0, 0))],
             scratch_shapes=[
                 pltpu.VMEM((width, blocks * pair_rows), LOW),
                 pltpu.VMEM((blocks * pair_rows, 2 * width), LOW),
             ],
         ),
         out_shape=[
-            jax.ShapeDtypeStruct((blocks, width, rows), LOW),
-            jax.ShapeDtypeStruct((blocks, width, rows), WIDE),
-            jax.ShapeDtypeStruct((blocks, 1, rows), WIDE),
+            jax.ShapeDtypeStruct((blocks, objects, width, rows), LOW),
+            jax.ShapeDtypeStruct((blocks, objects, width, rows), WIDE),
+            jax.ShapeDtypeStruct((blocks, objects, 1, rows), WIDE),
         ],
         name="pair_forward",
-        cost_estimate=estimate(blocks * rows, blocks * pair_rows, 2 if length is None else 1.4),
+        cost_estimate=estimate(objects * blocks * rows, blocks * pair_rows, 2 if length is None else 1.4),
         compiler_params=pltpu.CompilerParams(vmem_limit_bytes=VMEM_LIMIT),
     )(lengths, queries, pair, pair)
 
 
 def pair_backward(queries, pair, key_at, length, grad_mixed, wide, log_total):
-    blocks, _, width, rows = queries.shape
-    lengths = jnp.full((1,), blocks * rows, jnp.int32) if length is None else length
+    blocks, objects, _, width, rows = queries.shape
+    lengths = jnp.full((objects,), blocks * rows, jnp.int32) if length is None else length
 
     def kernel(len_ref, q_ref, k_ref, v_ref, g_ref, wide_ref, log_ref, out_ref, keys, keys_t, values, grad_k, grad_v):
-        i = pl.program_id(0)
+        i = pl.program_id(1)
 
         def run(live):
             size = live * rows
@@ -358,23 +358,23 @@
         if length is None:
             run(blocks)
         else:
-            by_length(len_ref[0], blocks * rows, blocks, run)
-
-    block = pl.BlockSpec((None, width, rows), lambda i, lens: (i, 0, 0))
+            by_length(len_ref[pl.program_id(0)], blocks * rows, blocks, run)
+
+    block = pl.BlockSpec((None, None, width, rows), lambda o, i, lens: (i, o, 0, 0))
     return pl.pallas_call(
         kernel,
         grid_spec=pltpu.PrefetchScalarGridSpec(
             num_scalar_prefetch=1,
-            grid=(blocks,),
+            grid=(objects, blocks),
             in_specs=[
-                pl.BlockSpec((None, None, width, rows), lambda i, lens: (i, 0, 0, 0)),
-                pl.BlockSpec((blocks, None, width, rows), lambda i, lens: (0, key_at, 0, 0)),
-                pl.BlockSpec((blocks, None, width, rows), lambda i, lens: (0, key_at + 1, 0, 0)),
+                pl.BlockSpec((None, None, None, width, rows), lambda o, i, lens: (i, o, 0, 0, 0)),
+                pl.BlockSpec((blocks, None, None, width, rows), lambda o, i, lens: (0, o, key_at, 0, 0)),
+                pl.BlockSpec((blocks, None, None, width, rows), lambda o, i, lens: (0, o, key_at + 1, 0, 0)),
                 block,
                 block,
-                pl.BlockSpec((None, 1, rows), lambda i, lens: (i, 0, 0)),
-            ],
-            out_specs=pl.BlockSpec((blocks, 3, width, rows), lambda i, lens: (0, 0, 0, 0)),
+                pl.BlockSpec((None, None, 1, rows), lambda o, i, lens: (i, o, 0, 0)),
+            ],
+            out_specs=pl.BlockSpec((blocks, None, 3, width, rows), lambda o, i, lens: (0, o, 0, 0, 0)),
             scratch_shapes=[
                 pltpu.VMEM((blocks * rows, width), LOW),
                 pltpu.VMEM((width, blocks * rows), LOW),
@@ -383,9 +383,9 @@
                 pltpu.VMEM((blocks * rows, width), WIDE),
             ],
         ),
-        out_shape=jax.ShapeDtypeStruct((blocks, 3, width, rows), LOW),
+        out_shape=jax.ShapeDtypeStruct((blocks, objects, 3, width, rows), LOW),
         name="pair_backward",
-        cost_estimate=estimate(blocks * rows, blocks * rows, 3 if length is None else 2),
+        cost_estimate=estimate(objects * blocks * rows, blocks * rows, 3 if length is None else 2),
         compiler_params=pltpu.CompilerParams(vmem_limit_bytes=VMEM_LIMIT),
     )(lengths, queries, pair, pair, grad_mixed, wide, log_total)
 
@@ -399,28 +399,8 @@
     return low.astype(WIDE) + swap(low, "near").astype(WIDE)
 
 
-def halves(value):
-    size = value.shape[0] // 2
-    near = lax.axis_index("near")
-    return (
-        lax.dynamic_slice_in_dim(value, near * size, size, 0),
-        lax.dynamic_slice_in_dim(value, (1 - near) * size, size, 0),
-    )
-
-
-def half_sum_near(partial):
-    mine, other = halves(partial)
-    return mine + swap(other.astype(LOW), "near").astype(WIDE)
-
-
-def over_heads(value):
-    far, near = lax.axis_index("far"), lax.axis_index("near")
-    value = jnp.stack([value, swap(value, "far")])
-    value = jnp.stack([value, swap(value, "near")])
-    value = jnp.where(far == 0, value, jnp.flip(value, 1))
-    value = jnp.where(near == 0, value, jnp.flip(value, 0))
-    value = value.transpose(1, 2, 0, 3, 4)
-    return value.reshape(2 * value.shape[1], 2 * value.shape[3], -1)
+def tie(value, *others):
+    return lax.optimization_barrier((value, *others))
 
 
 def paired_device(
@@ -441,28 +421,73 @@
     narrow_weights,
     cotangent,
 ):
+    objects = tokens.shape[0] // 2
     _, rows, width = tokens.shape
     cols = self_weights.shape[2]
     hidden = widen_weights.shape[1]
     heads = cols // HEAD_DIM
     codes = camera_table.shape[0]
     patch_width = patches.shape[2]
+    count = objects * rows
     n_rows = lax.axis_size("rows")
     row_rank = lax.axis_index("rows")
     far, near = lax.axis_index("far"), lax.axis_index("near")
     own = 2 * far + near
     other = 2 * (1 - far) + near
-    groups = tokens.shape[0] // 2
+
+    def objects_of(value):
+        return lax.dynamic_slice_in_dim(value, objects * far, objects, 0)
 
     def piece(value):
         size = value.shape[0] // n_rows
         return lax.dynamic_slice_in_dim(value, row_rank * size, size, 0)
 
-    def shard_columns(value):
+    def join_rows(value):
+        return lax.all_gather(value, "rows", axis=0, tiled=True)
+
+    def put_together(value):
+        whole = lax.all_gather(value, "rows", axis=1)
+        return whole.reshape(value.shape[0] * cols, width)
+
+    def both_columns(value):
         return [
             lax.dynamic_slice_in_dim(value, index * cols, cols, value.ndim - 1)
             for index in (own, other)
         ]
+
+    def halves(value):
+        value = value.reshape(objects, 2, rows // 2, -1)
+        return [
+            lax.dynamic_index_in_dim(value, index, 1, keepdims=False).reshape(count // 2, -1)
+            for index in (near, 1 - near)
+        ]
+
+    def half_sum_near(partial):
+        mine, away = halves(partial)
+        return mine + swap(away.astype(LOW), "near").astype(WIDE)
+
+    def over_heads(value):
+        value = value.reshape(objects, rows // 2, -1)
+        value = jnp.stack([value, swap(value, "far")])
+        value = jnp.stack([value, swap(value, "near")])
+        value = jnp.where(far == 0, value, jnp.flip(value, 1))
+        value = jnp.where(near == 0, value, jnp.flip(value, 0))
+        return value.transpose(1, 2, 0, 3, 4).reshape(2 * objects, rows, -1)
+
+    def to_pairs(weights, value, slots):
+        parts = [
+            jnp.concatenate(
+                [mul(weight, value[i * rows : (i + 1) * rows], NT).astype(LOW) for weight in weights]
+            ).reshape(n_rows, slots, HEAD_DIM, rows)
+            for i in range(objects)
+        ]
+        return exchange_rows(jnp.stack(parts, axis=1))
+
+    def from_pairs(value):
+        return value.transpose(0, 2, 3, 1, 4).reshape(-1, count)
+
+    def over_all_columns(value_t, weight):
+        return mul(jnp.concatenate([value_t, swap(value_t, "near")]), weight, TN)
 
     qkv_rows = self_weights.reshape(3, width, heads, HEAD_DIM).transpose(2, 0, 3, 1)
     qkv_rows = qkv_rows.reshape(3 * cols, width)
@@ -470,214 +495,164 @@
     pair_rows = pair_rows.reshape(2 * cols, width)
     query_rows = cross_query.T
 
-    first = swap(piece(qkv_rows), "far")
-    qkv_other = lax.all_gather(first, "rows", axis=0, tiled=True)
-    mine = [piece(v) for v in (self_output, query_rows, cross_output, pair_rows, widen_weights, narrow_weights)]
-    across = swap(jnp.concatenate(mine, axis=0), "far")
-    sizes = [v.shape[0] for v in mine]
-    starts = [sum(sizes[:i]) for i in range(len(sizes) + 1)]
-    across = [across[a:b] for a, b in zip(starts[:-1], starts[1:])]
-    two = jnp.stack([jnp.stack(mine[:3]), jnp.stack(across[:3])])
-    four = jnp.concatenate([two, swap(two, "near")])
-
-    def put_together(value):
-        whole = lax.all_gather(value, "rows", axis=1)
-        return whole.reshape(value.shape[0] * cols, width)
-
-    self_whole = put_together(four[:, 0])
-    query_whole = put_together(four[:, 1])
-    cross_whole = put_together(four[:, 2])
-    pair_other = lax.all_gather(across[3], "rows", axis=0, tiled=True)
-    widen_other = lax.all_gather(across[4], "rows", axis=0, tiled=True)
-    narrow_other = lax.all_gather(across[5], "rows", axis=0, tiled=True)
+    qkv_other = join_rows(swap(piece(qkv_rows), "far"))
 
     table_flat = camera_table.reshape(codes, -1)
     cross_gain_f = cross_gain.astype(WIDE)
     hidden_gain_f = hidden_gain.astype(WIDE)
 
-    def two_rows(weight, weight_other, value):
-        return jnp.concatenate(
-            [mul(weight, value, NT).astype(LOW), mul(weight_other, value, NT).astype(LOW)]
+    inputs = objects_of(tokens).reshape(count, width).astype(WIDE)
+    patch_in = objects_of(patches).reshape(count, patch_width)
+    length = objects_of(patch_len)
+    grad_low = objects_of(cotangent).reshape(count, width)
+    codes_of = objects_of(cam_index).reshape(count)
+    onehot = (codes_of[:, None] == jnp.arange(codes)[None, :]).astype(LOW)
+    shift_scale = mul(onehot, table_flat)
+    gain_one = 1.0 + shift_scale[:, :width]
+    unit_one, rate_one = normed(inputs)
+    normed_one = (unit_one * gain_one + shift_scale[:, width:]).astype(LOW)
+
+    mine = [piece(v) for v in (self_output, query_rows, cross_output, pair_rows)]
+    normed_one, *mine = tie(normed_one, *mine)
+    across = swap(jnp.concatenate(mine, axis=0), "far")
+    size = cols // n_rows
+    two = jnp.stack([jnp.concatenate(mine[:3]), across[: 3 * size]])
+    four = jnp.concatenate([two, swap(two, "near")])
+    pair_other = join_rows(across[3 * size :])
+    self_whole, query_whole, cross_whole = (
+        put_together(four[:, i * size : (i + 1) * size]) for i in range(3)
+    )
+
+    qkv = to_pairs((qkv_rows, qkv_other), normed_one, 3)
+    patch_mid = mul(patch_in, patch_weights).astype(LOW)
+    pair = to_pairs((pair_rows, pair_other), patch_mid, 2)
+
+    mine = [piece(widen_weights), piece(narrow_weights)]
+    qkv, *mine = tie(qkv, *mine)
+    across = swap(jnp.concatenate(mine, axis=0), "far")
+    size = width // n_rows
+    widen = jnp.concatenate([widen_weights, join_rows(across[:size])], axis=1)
+    narrow = jnp.concatenate([narrow_weights, join_rows(across[size:])], axis=0)
+
+    mixed, self_wide, self_log = pair_forward(qkv, qkv, 1)
+    self_mixed_t = from_pairs(exchange_rows(mixed)[:, :, None])
+    after_self = inputs + over_all_columns(self_mixed_t, self_whole)
+    unit_two, rate_two = normed(after_self)
+    normed_two = (unit_two * cross_gain_f).astype(LOW)
+    cross_q = to_pairs((query_whole[: 2 * cols],), normed_two, 1)
+    mixed, cross_wide, cross_log = pair_forward(cross_q, pair, 0, length)
+    cross_mixed_t = from_pairs(exchange_rows(mixed)[:, :, None])
+    after_cross = after_self + over_all_columns(cross_mixed_t, cross_whole)
+    unit_three, rate_three = normed(after_cross)
+    normed_three = (unit_three * hidden_gain_f).astype(LOW)
+    activated, act_back = jax.vjp(gelu_tanh, mul(normed_three, widen))
+    activated = activated.astype(LOW)
+    grad_pre = act_back(mul(grad_low, narrow, NT))[0].astype(LOW)
+    grad_three = sum_near(mul(grad_pre, widen, NT))
+    hidden_half = half_sum_near(mul(activated, narrow))
+    result = (halves(after_cross)[0] + hidden_half).astype(LOW)
+
+    def part_rows(both):
+        return lax.psum_scatter(both, "rows", scatter_dimension=1, tiled=True)
+
+    def total_rows(part):
+        return join_rows((part[0].astype(WIDE) + swap(part[1], "far").astype(WIDE)).astype(LOW))
+
+    def by_shard(left, right):
+        return mul(left, right, NN).astype(LOW).reshape(2, -1, right.shape[1])
+
+    hidden_part = part_rows(
+        jnp.concatenate(
+            [
+                mul(value, against, TN).astype(LOW).reshape(2, hidden, width)
+                for value, against in ((activated, grad_low), (grad_pre, normed_three))
+            ],
+            axis=1,
         )
-
-    def over_all_columns(value_t, weight):
-        return mul(jnp.concatenate([value_t, swap(value_t, "near")]), weight, TN)
-
-    def one_group(group):
-        def object_of(value):
-            return lax.dynamic_index_in_dim(value, groups * far + group, 0, keepdims=False)
-
-        inputs = object_of(tokens).astype(WIDE)
-        patch_in = object_of(patches)
-        length = object_of(patch_len)[None]
-        grad_low = object_of(cotangent)
-        onehot = (object_of(cam_index)[:, None] == jnp.arange(codes)[None, :]).astype(LOW)
-        shift_scale = mul(onehot, table_flat)
-        gain_one = 1.0 + shift_scale[:, :width]
-        unit_one, rate_one = normed(inputs)
-        normed_one = (unit_one * gain_one + shift_scale[:, width:]).astype(LOW)
-        qkv_t = two_rows(qkv_rows, qkv_other, normed_one)
-        qkv = exchange_rows(qkv_t.reshape(n_rows, 3, HEAD_DIM, rows))
-        patch_mid = mul(patch_in, patch_weights).astype(LOW)
-        pair_t = two_rows(pair_rows, pair_other, patch_mid)
-        pair = exchange_rows(pair_t.reshape(n_rows, 2, HEAD_DIM, rows))
-        mixed, self_wide, self_log = pair_forward(qkv, qkv, 1)
-        self_mixed_t = exchange_rows(mixed).reshape(2 * cols, rows)
-        after_self = inputs + over_all_columns(self_mixed_t, self_whole)
-        unit_two, rate_two = normed(after_self)
-        normed_two = (unit_two * cross_gain_f).astype(LOW)
-        cross_q = mul(query_whole[: 2 * cols], normed_two, NT).astype(LOW)
-        cross_q = exchange_rows(cross_q.reshape(n_rows, 1, HEAD_DIM, rows))
-        mixed, cross_wide, cross_log = pair_forward(cross_q, pair, 0, length)
-        cross_mixed_t = exchange_rows(mixed).reshape(2 * cols, rows)
-        after_cross = after_self + over_all_columns(cross_mixed_t, cross_whole)
-        unit_three, rate_three = normed(after_cross)
-        normed_three = (unit_three * hidden_gain_f).astype(LOW)
-        activated, grad_pre = [], []
-        for widen, narrow in ((widen_weights, narrow_weights), (widen_other, narrow_other)):
-            result, act_back = jax.vjp(gelu_tanh, mul(normed_three, widen))
-            activated.append(result.astype(LOW))
-            grad_pre.append(act_back(mul(grad_low, narrow, NT))[0].astype(LOW))
-        grad_three = sum_near(
-            mul(grad_pre[0], widen_weights, NT) + mul(grad_pre[1], widen_other, NT)
+    )
+
+    hidden_gain_term = jnp.sum(grad_three * unit_three, axis=0)
+    grad_cross = grad_low.astype(WIDE) + normed_back(
+        grad_three * hidden_gain_f, unit_three, rate_three
+    )
+    grad_cross_low = grad_cross.astype(LOW)
+    grad_mixed = to_pairs((cross_whole[: 2 * cols],), grad_cross_low, 1)[:, :, 0]
+    grads = pair_backward(cross_q, pair, 0, length, grad_mixed, cross_wide, cross_log)
+    grads = exchange_rows(grads)
+    grads, hidden_part = tie(grads, hidden_part)
+    hidden_total = total_rows(hidden_part)
+    outputs = over_heads(result)
+    grad_cq_t = from_pairs(grads[:, :, :1])
+    grad_pair_t = from_pairs(grads[:, :, 1:])
+    grad_two = over_all_columns(grad_cq_t, query_whole)
+    cross_gain_term = jnp.sum(grad_two * unit_two, axis=0)
+    grad_self = grad_cross + normed_back(grad_two * cross_gain_f, unit_two, rate_two)
+    grad_self_low = grad_self.astype(LOW)
+    grad_mid = sum_near(
+        mul(grad_pair_t, jnp.concatenate([pair_rows, pair_other]), TN)
+    ).astype(LOW)
+    patch_half = mul(halves(grad_mid)[0], patch_weights, NT).astype(LOW)
+    patch_terms = jnp.stack([mul(value, patch_in, TN).astype(LOW) for value in both_columns(grad_mid)])
+    patch_terms = jnp.pad(patch_terms, ((0, 0), (0, 0), (0, width - patch_width)))
+    middle_part = part_rows(
+        jnp.concatenate(
+            [
+                by_shard(cross_mixed_t, grad_cross_low),
+                by_shard(self_mixed_t, grad_self_low),
+                by_shard(grad_cq_t, normed_two),
+                by_shard(grad_pair_t, patch_mid),
+                patch_terms,
+            ],
+            axis=1,
         )
-        hidden_half = half_sum_near(
-            mul(activated[0], narrow_weights) + mul(activated[1], narrow_other)
-        )
-        result = (halves(after_cross)[0] + hidden_half).astype(LOW)
-        yield (
-            "hidden",
-            {
-                "widen": [(normed_three, value, TN) for value in grad_pre],
-                "narrow": [(value, grad_low, TN) for value in activated],
-            },
-        )
-        hidden_gain_term = jnp.sum(grad_three * unit_three, axis=0)
-        grad_cross = grad_low.astype(WIDE) + normed_back(
-            grad_three * hidden_gain_f, unit_three, rate_three
-        )
-        grad_cross_low = grad_cross.astype(LOW)
-        grad_mixed = mul(cross_whole[: 2 * cols], grad_cross_low, NT).astype(LOW)
-        grad_mixed = exchange_rows(grad_mixed.reshape(n_rows, HEAD_DIM, rows))
-        grads = pair_backward(cross_q, pair, 0, length, grad_mixed, cross_wide, cross_log)
-        grads = exchange_rows(grads)
-        grad_cq_t = grads[:, 0].reshape(2 * cols, rows)
-        grad_pair = grads[:, 1:].reshape(2, heads, 2, HEAD_DIM, rows)
-        grad_two = over_all_columns(grad_cq_t, query_whole)
-        cross_gain_term = jnp.sum(grad_two * unit_two, axis=0)
-        grad_self = grad_cross + normed_back(grad_two * cross_gain_f, unit_two, rate_two)
-        grad_self_low = grad_self.astype(LOW)
-        grad_mixed = mul(self_whole[: 2 * cols], grad_self_low, NT).astype(LOW)
-        grad_mixed = exchange_rows(grad_mixed.reshape(n_rows, HEAD_DIM, rows))
-        grads = pair_backward(qkv, qkv, 1, None, grad_mixed, self_wide, self_log)
-        grads = exchange_rows(grads)
-        grad_pair_t = grad_pair.reshape(2, 2 * cols, rows)
-        grad_mid = sum_near(
-            mul(grad_pair_t[0], pair_rows, TN) + mul(grad_pair_t[1], pair_other, TN)
-        ).astype(LOW)
-        patch_half = mul(halves(grad_mid)[0], patch_weights, NT).astype(LOW)
-        by_kind = grad_pair.transpose(0, 2, 1, 3, 4).reshape(2, 2, cols, rows)
-        yield (
-            "middle",
-            {
-                "query": [(normed_two, grad_cq_t[i : i + cols], T_LAST) for i in (0, cols)],
-                "pair": [[(patch_mid, by_kind[s, k], T_LAST) for k in range(2)] for s in range(2)],
-                "patch": [(patch_in, value, TN) for value in shard_columns(grad_mid)],
-                "cross_output": [
-                    (cross_mixed_t[i : i + cols], grad_cross_low, NN) for i in (0, cols)
-                ],
-                "self_output": [(self_mixed_t[i : i + cols], grad_self_low, NN) for i in (0, cols)],
-            },
-        )
-        grad_qkv_t = grads.reshape(2, 3 * cols, rows)
-        grad_one = half_sum_near(
-            mul(grad_qkv_t[0], qkv_rows, TN) + mul(grad_qkv_t[1], qkv_other, TN)
-        )
-        by_kind = grads.reshape(2, heads, 3, HEAD_DIM, rows).transpose(0, 2, 1, 3, 4)
-        by_kind = by_kind.reshape(2, 3, cols, rows)
-        gain_half, unit_half, rate_half, self_half = (
-            halves(value)[0] for value in (gain_one, unit_one, rate_one, grad_self)
-        )
-        input_half = self_half + normed_back(grad_one * gain_half, unit_half, rate_half)
-        onehot_half = halves(onehot)[0].astype(WIDE)
-        table_term = jnp.concatenate(
-            [
-                lax.dot_general(onehot_half, value, TN, precision=lax.Precision.HIGHEST)
-                for value in (grad_one * unit_half, grad_one)
-            ],
-            axis=0,
-        )
-        yield (
-            "last",
-            {
-                "self": [[(normed_one, by_kind[s, k], T_LAST) for k in range(3)] for s in range(2)],
-            },
-        )
-        yield "done", (result, input_half.astype(LOW), patch_half, table_term, hidden_gain_term, cross_gain_term)
-
-    def product(*terms):
-        dims = terms[0][2]
-        left = jnp.concatenate([term[0] for term in terms], axis=dims[0][0][0])
-        right = jnp.concatenate([term[1] for term in terms], axis=dims[0][1][0])
-        return mul(left, right, dims).astype(LOW)
-
-    def is_term(value):
-        return isinstance(value, tuple)
-
-    def sum_rows(both):
-        part = lax.psum_scatter(both, "rows", scatter_dimension=1, tiled=True)
-        total = part[0].astype(WIDE) + swap(part[1], "far").astype(WIDE)
-        return lax.all_gather(total.astype(LOW), "rows", axis=0, tiled=True)
-
-    steps = [one_group(group) for group in range(groups)]
-    asked = [next(step) for step in steps]
-    terms = {}
-    while asked[0][0] != "done":
-        gathered = [value for _, value in asked]
-        terms.update(jax.tree.map(product, *gathered, is_leaf=is_term))
-        if asked[0][0] == "hidden":
-            hidden_total = sum_rows(
-                jnp.stack([jnp.concatenate([terms["widen"][s], terms["narrow"][s]]) for s in range(2)])
-            )
-        elif asked[0][0] == "middle":
-            output_total = sum_rows(
-                jnp.stack(
-                    [jnp.concatenate([terms["cross_output"][s], terms["self_output"][s]]) for s in range(2)]
-                )
-            )
-            cross_total = sum_rows(
-                jnp.stack(
-                    [jnp.concatenate([terms["query"][s], *terms["pair"][s], terms["patch"][s]]) for s in range(2)]
-                )
-            )
-        asked = [next(step) for step in steps]
-    results, input_halves, patch_halves, tables, *gains = zip(*[value for _, value in asked])
-    table = sum_near(sum(tables[1:], tables[0]))
-    gain_terms = [sum(values[1:], values[0])[None] for values in gains]
-    small = jnp.concatenate([table] + gain_terms + [jnp.zeros((62, width), WIDE)], axis=0).astype(LOW)
-    last_total = sum_rows(
-        jnp.stack(
-            [jnp.concatenate([*terms["self"][s], value]) for s, value in enumerate(shard_columns(small))]
-        )
-    )
-    outputs = over_heads(jnp.stack(results))
-    input_grads = over_heads(jnp.stack(input_halves))
-    patch_grads = over_heads(jnp.stack(patch_halves))
-    kinds = last_total[: 3 * width].reshape(3, width, cols)
-    table_total = last_total[3 * width : 3 * width + 2 * codes].reshape(2, codes, cols)
-    gain_total = last_total[3 * width + 2 * codes :]
+    )
+    grad_mixed = to_pairs((self_whole[: 2 * cols],), grad_self_low, 1)[:, :, 0]
+    grad_mixed, hidden_total, outputs = tie(grad_mixed, hidden_total, outputs)
+    grads = exchange_rows(pair_backward(qkv, qkv, 1, None, grad_mixed, self_wide, self_log))
+    patch_grads = over_heads(patch_half)
+    grads, middle_part, patch_grads = tie(grads, middle_part, patch_grads)
+    middle_total = total_rows(middle_part)
+    grad_qkv_t = from_pairs(grads)
+    last_part = part_rows(by_shard(grad_qkv_t, normed_one))
+    grad_one = half_sum_near(mul(grad_qkv_t, jnp.concatenate([qkv_rows, qkv_other]), TN))
+    gain_half, unit_half, rate_half, self_half = (
+        halves(value)[0] for value in (gain_one, unit_one, rate_one, grad_self)
+    )
+    input_half = self_half + normed_back(grad_one * gain_half, unit_half, rate_half)
+    input_half = input_half.astype(LOW)
+    onehot_half = halves(onehot)[0].astype(WIDE)
+    table_term = jnp.concatenate(
+        [
+            lax.dot_general(onehot_half, value, TN, precision=lax.Precision.HIGHEST)
+            for value in (grad_one * unit_half, grad_one)
+        ],
+        axis=0,
+    )
+    small = [sum_near(table_term), hidden_gain_term[None], cross_gain_term[None], jnp.zeros((14, width), WIDE)]
+    small = jnp.stack(both_columns(jnp.concatenate(small, axis=0).astype(LOW)))
+    small = jnp.sum(lax.all_gather(small, "rows", axis=0).astype(WIDE), axis=0)
+    small = small[0] + swap(small[1].astype(LOW), "far").astype(WIDE)
+    input_half, middle_total = tie(input_half, middle_total)
+    input_grads = over_heads(input_half)
+    last_total = total_rows(last_part)
+
+    output_total = middle_total[: 2 * cols]
+    query_total = middle_total[2 * cols : 3 * cols]
+    pair_total = middle_total[3 * cols : 5 * cols].reshape(heads, 2, HEAD_DIM, width)
+    patch_total = middle_total[5 * cols :, :patch_width]
+    self_total = last_total.reshape(heads, 3, HEAD_DIM, width)
     gradients = (
-        table_total.transpose(1, 0, 2),
-        kinds,
+        small[: 2 * codes].reshape(2, codes, cols).transpose(1, 0, 2),
+        self_total.transpose(1, 3, 0, 2).reshape(3, width, cols),
         output_total[cols:],
-        gain_total[1],
-        cross_total[:width],
-        cross_total[width : 3 * width].reshape(2, width, cols),
+        small[2 * codes + 1],
+        query_total.T,
+        pair_total.transpose(1, 3, 0, 2).reshape(2, width, cols),
         output_total[:cols],
-        cross_total[3 * width :],
-        gain_total[0],
-        hidden_total[:width],
-        hidden_total[width:],
+        patch_total.T,
+        small[2 * codes],
+        hidden_total[hidden:].T,
+        hidden_total[:hidden],
     )
     return (outputs, input_grads.astype(WIDE), patch_grads.astype(WIDE)) + tuple(
         value.astype(WIDE) for value in gradients

time: 966 us -> 817 us (0.85)
  waiting for transfers between devices: 435 us -> 319 us
  blocking collectives: 0 us -> 74.7 us
  starting transfers between devices: 123 us -> 50.9 us
  matrix products: 118 us -> 79.6 us
  Pallas kernels: 86.9 us -> 100 us
    reduce_scatter x4 -> x3, waiting for transfers between devices: 108 us -> 0.02 us  [part_rows(): return lax.psum_scatter(both, 'rows', scatter_dimension=1, tiled=True)]
    all_to_all x0 -> x3, blocking collectives: none -> 60.5 us  [exchange_rows(): return lax.all_to_all(value, 'rows', 0, 0, tiled=True)]
    all_to_all x18 -> x6, starting transfers between devices: 72 us -> 24.6 us  [exchange_rows(): return lax.all_to_all(value, 'rows', 0, 0, tiled=True)]
    dot_general x72 -> x35, matrix products: 114 us -> 78.6 us  [mul(): return lax.dot_general(left, right, dims, preferred_element_type=WIDE)]
    ppermute x28 -> x22, waiting for transfers between devices: 229 us -> 254 us  [swap(): return lax.ppermute(value, axis, [(0, 1), (1, 0)])]
    ppermute x28 -> x22, starting transfers between devices: 49.6 us -> 25.4 us  [swap(): return lax.ppermute(value, axis, [(0, 1), (1, 0)])]
    slice x26 -> x10, local copies, waits for them, and re-layouts: 27.6 us -> 5.36 us  [the longest x1 2.26 us: paired_device(): cross_q = to_pairs((query_whole[:2 * cols],), normed_two, 1)]
    all_gather x8 -> x7, waiting for transfers between devices: 19.8 us -> 2.02 us  [join_rows(): return lax.all_gather(value, 'rows', axis=0, tiled=True)]
  transfers between devices with their start and end apart: 61 -> 41, of which waited for: 40 -> 26; matrix products, arithmetic and copies ran while one was open for 25% -> 23% of each run, Pallas kernels for 7% -> 12%
where the time goes in v3:
time: 817 us; the launch traced here: 805 us
  waiting for transfers between devices  319 us (39%)
  Pallas kernels  100 us (12%)
  local copies, waits for them, and re-layouts  90.2 us (11%)
  matrix products  79.6 us (10%)
  other arithmetic  74.9 us (9%)
  blocking collectives  74.7 us (9%)
  starting transfers between devices  50.9 us (6%)
  between operations  15.7 us (2%)
    ppermute x22, waiting for transfers between devices, swap(): return lax.ppermute(value, axis, [(0, 1), (1, 0)])  254 us
    dot_general x35, matrix products, mul(): return lax.dot_general(left, right, dims, preferred_element_type=WIDE)  78.6 us
    pallas_call x2, Pallas kernels, pair_backward(): pl.pallas_call(kernel, grid_spec=pltpu.PrefetchScalarGridSpec(num_scalar_...  63.1 us
    all_to_all x6, waiting for transfers between devices, exchange_rows(): return lax.all_to_all(value, 'rows', 0, 0, tiled=True)  61.6 us
    all_to_all x3, blocking collectives, exchange_rows(): return lax.all_to_all(value, 'rows', 0, 0, tiled=True)  60.5 us
    unnamed x163, local copies, waits for them, and re-layouts  46.6 us
    pallas_call x2, Pallas kernels, pair_forward(): pl.pallas_call(kernel, grid_spec=pltpu.PrefetchScalarGridSpec(num_scalar_...  37 us
    ppermute x22, starting transfers between devices, swap(): return lax.ppermute(value, axis, [(0, 1), (1, 0)])  25.4 us
  transfers between devices with their start and end apart: 41, of which 26 were waited for; matrix products, arithmetic and copies ran while one was open for 23% of the time, Pallas kernels for 12%

profile of v3, /device:TPU:0, one launch (start us, length us, event | category | flops | bytes accessed | tf_op | source)
XLA Modules:
  0.0 804.6 jit_solution(258504289278254439)
XLA Ops:
  7.2 2.7 copy.115
  10.0 2.7 copy.116
  13.7 4.1 collective-permute-start.2
  17.8 9.1 %collective-permute-done.2 = bf16[96,1024]{1,0:T(8,128)(2,1)S(1)} collective-permute-done((bf16[96,1024]{1,0:T(8,128)(2,1)S(1)}, bf16[96,1024]{1,0:T(8,128)(2,1)S(1)}, u32[]{:S(2)}, u32[]{:S(2)}) %collective-permute-start.2) | collective-permute-done | bytes 196640 | tf_op jit(solution)/shard_map/ppermute | solution.py:394
  39.7 16.8 %collective-permute-done = bf16[160,1024]{1,0:T(8,128)(2,1)S(1)} collective-permute-done((bf16[160,1024]{1,0:T(8,128)(2,1)S(1)}, bf16[160,1024]{1,0:T(8,128)(2,1)S(1)}, u32[]{:S(2)}, u32[]{:S(2)}) %collective-permute-start) | collective-permute-done | bytes 327712 | tf_op jit(solution)/shard_map/ppermute | solution.py:394
  59.0 9.4 %collective-permute-done.1 = bf16[2,96,1024]{2,1,0:T(8,128)(2,1)S(1)} collective-permute-done((bf16[2,96,1024]{2,1,0:T(8,128)(2,1)S(1)}, bf16[2,96,1024]{2,1,0:T(8,128)(2,1)S(1)}, u32[]{:S(2)}, u32[]{:S(2)}) %collective-permute-start.1) | collective-permute-done | bytes 393248 | tf_op jit(solution)/shard_map/ppermute | solution.py:394
  72.1 2.8 fusion.28
  84.2 4.3 all-to-all-start
  94.5 19.8 %all-to-all-done.q_ref.k_ref.v_ref = bf16[8,2,3,64,256]{4,3,2,1,0:T(8,128)(2,1)} async-done(((bf16[8,2,3,64,256]{4,3,2,1,0:T(8,128)(2,1)}), bf16[8,2,3,64,256]{4,3,2,1,0:T(8,128)(2,1)}, u32[]{:S(2)}, u32[]{:S(2)}) %all-to-all-start) | async-done | bytes 1572896 | tf_op jit(solution)/shard_map/all_to_all | solution.py:230
  119.0 18.1 %collective-permute-done.5 = bf16[256,1024]{1,0:T(8,128)(2,1)S(1)} collective-permute-done((bf16[256,1024]{1,0:T(8,128)(2,1)S(1)}, bf16[256,1024]{1,0:T(8,128)(2,1)S(1)}, u32[]{:S(2)}, u32[]{:S(2)}) %collective-permute-start.5) | collective-permute-done | bytes 524320 | tf_op jit(solution)/shard_map/ppermute | solution.py:394
  138.0 19.0 %pair_forward.2 = (bf16[8,2,64,256]{3,2,1,0:T(8,128)(2,1)}, f32[8,2,64,256]{3,2,1,0:T(8,128)S(1)}, f32[8,2,1,256]{3,2,1,0:T(1,128)S(1)}) custom-call(s32[2]{0:T(128)S(1)} %broadcast_13_len_ref.2.len_ref, bf16[8,2,3,64,256]{4,3,2,1,0:T(8,128)(2,1)} %all-to-all-done.q_ref.k_ref.v_ref, bf16[8,2,3,64,256]{4,3,2,1,0:T(8,128)(2,1)} %all-to-all-done.q_ref.k_ref.v_ref, ...), custom_call_target="tpu_custom_call" | custom-call | flops 20132659200 | bytes 8388608 | tf_op jit(solution)/shard_map/pair_forward/pallas_call | solution.py:282
  158.0 5.5 all-to-all-start.1
  163.5 3.2 dynamic-slice_convert_fusion.2
  170.6 5.1 all-to-all-done.1
  180.9 3.6 all-to-all-start.3
  187.7 3.6 fusion.97
  195.1 7.4 all-to-all-done.3.k_ref.v_ref
  202.5 4.2 all-to-all-start.2
  207.5 11.6 %all-to-all-done.2.q_ref = bf16[8,2,1,64,256]{4,3,2,1,0:T(8,128)(2,1)} async-done(((bf16[8,2,1,64,256]{4,3,2,1,0:T(8,128)(2,1)}), bf16[8,2,1,64,256]{4,3,2,1,0:T(8,128)(2,1)}, u32[]{:S(2)}, u32[]{:S(2)}) %all-to-all-start.2) | async-done | bytes 524320 | tf_op jit(solution)/shard_map/all_to_all | solution.py:230
  219.1 18.0 %pair_forward.3 = (bf16[8,2,64,256]{3,2,1,0:T(8,128)(2,1)S(1)}, f32[8,2,64,256]{3,2,1,0:T(8,128)S(1)}, f32[8,2,1,256]{3,2,1,0:T(1,128)S(1)}) custom-call(s32[2]{0:T(128)S(1)} %dynamic_slice.95.len_ref, bf16[8,2,1,64,256]{4,3,2,1,0:T(8,128)(2,1)} %all-to-all-done.2.q_ref, bf16[8,2,2,64,256]{4,3,2,1,0:T(8,128)(2,1)S(1)} %all-to-all-done.3.k_ref.v_ref, ...), custom_call_target="tpu_custom_call" | custom-call | flops 14092861440 | bytes 8388608 | tf_op jit(solution)/shard_map/pair_forward/pallas_call | solution.py:282
  237.1 17.3 %all_to_all.45 = bf16[8,2,64,256]{3,2,1,0:T(8,128)(2,1)S(1)} all-to-all(bf16[8,2,64,256]{3,2,1,0:T(8,128)(2,1)S(1)} %get-tuple-element.45), channel_id=1, replica_groups=mesh['far'=2,'near'=2,'rows'=8] {'rows'}, dimensions={0} | all-to-all | bytes 1048576 | tf_op jit(solution)/shard_map/all_to_all | solution.py:230
  262.3 5.8 collective-permute-done.4
  268.1 3.3 fusion.98
  273.1 3.2 constant_dynamic-update-slice_fusion.2
  276.3 4.7 fusion.90
  283.1 5.0 convolution_convert_fusion.2
  288.1 3.2 constant_dynamic-update-slice_fusion
  291.3 8.0 fusion.6
  299.3 4.5 convolution_convert_fusion.1
  303.8 7.8 pad_maximum_fusion
  311.7 5.3 convolution_convert_fusion.8
  318.7 20.6 %collective-permute-done.6 = bf16[512,1024]{1,0:T(8,128)(2,1)S(1)} collective-permute-done((bf16[512,1024]{1,0:T(8,128)(2,1)S(1)}, bf16[512,1024]{1,0:T(8,128)(2,1)S(1)}, u32[]{:S(2)}, u32[]{:S(2)}) %collective-permute-start.6) | collective-permute-done | bytes 1048608 | tf_op jit(solution)/shard_map/ppermute | solution.py:394
  343.6 19.1 %all_to_all.46 = bf16[8,2,1,64,256]{4,3,1,2,0:T(8,128)(2,1)S(1)} all-to-all(bf16[8,2,1,64,256]{4,3,1,2,0:T(8,128)(2,1)S(1)} %pad_maximum_fusion.16), channel_id=1, replica_groups=mesh['far'=2,'near'=2,'rows'=8] {'rows'}, dimensions={0} | all-to-all | bytes 1048576 | tf_op jit(solution)/shard_map/all_to_all | solution.py:230
  362.7 31.0 %pair_backward.2 = bf16[8,2,3,64,256]{4,3,2,1,0:T(8,128)(2,1)S(1)} custom-call(s32[2]{0:T(128)S(1)} %dynamic_slice.95.len_ref, bf16[8,2,1,64,256]{4,3,2,1,0:T(8,128)(2,1)} %all-to-all-done.2.q_ref, bf16[8,2,2,64,256]{4,3,2,1,0:T(8,128)(2,1)S(1)} %all-to-all-done.3.k_ref.v_ref, bf16[8,2,2,64,256]{4,3,2,1,0:T(8,128)(2,1)S(1)} %all-to-all-done.3.k_ref.v_ref, ...), custom_call_target="tpu_custom_call" | custom-call | flops 20132659200 | bytes 8388608 | tf_op jit(solution)/shard_map/pair_backward/pallas_call | solution.py:364
  393.6 24.1 %all_to_all.47 = bf16[8,2,3,64,256]{4,3,2,1,0:T(8,128)(2,1)} all-to-all(bf16[8,2,3,64,256]{4,3,2,1,0:T(8,128)(2,1)S(1)} %pair_backward.2), channel_id=1, replica_groups=mesh['far'=2,'near'=2,'rows'=8] {'rows'}, dimensions={0} | all-to-all | bytes 3145728 | tf_op jit(solution)/shard_map/all_to_all | solution.py:230
  419.0 25.1 %collective-permute-done.8 = bf16[256,1024]{1,0:T(8,128)(2,1)S(1)} collective-permute-done((bf16[256,1024]{1,0:T(8,128)(2,1)S(1)}, bf16[256,1024]{1,0:T(8,128)(2,1)S(1)}, u32[]{:S(2)}, u32[]{:S(2)}) %collective-permute-start.8) | collective-permute-done | bytes 524320 | tf_op jit(solution)/shard_map/ppermute | solution.py:394
  457.1 9.5 %collective-permute-done.7 = bf16[512,512]{1,0:T(8,128)(2,1)S(1)} collective-permute-done((bf16[512,512]{1,0:T(8,128)(2,1)S(1)}, bf16[512,512]{1,0:T(8,128)(2,1)S(1)}, u32[]{:S(2)}, u32[]{:S(2)}) %collective-permute-start.7) | collective-permute-done | bytes 524320 | tf_op jit(solution)/shard_map/ppermute | solution.py:394
  476.1 10.9 %collective-permute-done.12 = bf16[512,1024]{1,0:T(8,128)(2,1)S(1)} collective-permute-done((bf16[512,1024]{1,0:T(8,128)(2,1)S(1)}, bf16[512,1024]{1,0:T(8,128)(2,1)S(1)}, u32[]{:S(2)}, u32[]{:S(2)}) %collective-permute-start.12) | collective-permute-done | bytes 1048608 | tf_op jit(solution)/shard_map/ppermute | solution.py:394
  489.4 6.2 fusion.91
  500.1 9.9 %collective-permute-done.9 = bf16[256,1024]{1,0:T(8,128)(2,1)} collective-permute-done((bf16[256,1024]{1,0:T(8,128)(2,1)}, bf16[256,1024]{1,0:T(8,128)(2,1)}, u32[]{:S(2)}, u32[]{:S(2)}) %collective-permute-start.9) | collective-permute-done | bytes 524320 | tf_op jit(solution)/shard_map/ppermute | solution.py:394
  514.2 21.9 %collective-permute-done.10 = bf16[2,128,1024]{2,1,0:T(8,128)(2,1)S(1)} collective-permute-done((bf16[2,128,1024]{2,1,0:T(8,128)(2,1)S(1)}, bf16[2,128,1024]{2,1,0:T(8,128)(2,1)S(1)}, u32[]{:S(2)}, u32[]{:S(2)}) %collective-permute-start.10) | collective-permute-done | bytes 524320 | tf_op jit(solution)/shard_map/ppermute | solution.py:394
  537.9 24.4 %collective-permute-done.11 = bf16[2,2,128,1024]{3,2,1,0:T(8,128)(2,1)} collective-permute-done((bf16[2,2,128,1024]{3,2,1,0:T(8,128)(2,1)}, bf16[2,2,128,1024]{3,2,1,0:T(8,128)(2,1)}, u32[]{:S(2)}, u32[]{:S(2)}) %collective-permute-start.11) | collective-permute-done | bytes 1048608 | tf_op jit(solution)/shard_map/ppermute | solution.py:394
  571.3 3.5 all-to-all-start.7
  574.8 4.5 reverse_select_fusion.2
  579.4 7.8 collective-permute-done.13
  588.8 32.1 %pair_backward.3 = bf16[8,2,3,64,256]{4,3,2,1,0:T(8,128)(2,1)} custom-call(s32[2]{0:T(128)S(1)} %broadcast_13_len_ref.2.len_ref, bf16[8,2,3,64,256]{4,3,2,1,0:T(8,128)(2,1)} %all-to-all-done.q_ref.k_ref.v_ref, bf16[8,2,3,64,256]{4,3,2,1,0:T(8,128)(2,1)} %all-to-all-done.q_ref.k_ref.v_ref, bf16[8,2,3,64,256]{4,3,2,1,0:T(8,128)(2,1)} %all-to-all-done.q_ref.k_ref.v_ref, ...), custom_call_target="tpu_custom_call" | custom-call | flops 30198988800 | bytes 8388608 | tf_op jit(solution)/shard_map/pair_backward/pallas_call | solution.py:364
  621.0 3.6 all-to-all-start.8
  627.8 17.7 %all-to-all-done.8 = bf16[8,2,3,64,256]{4,3,2,1,0:T(8,128)(2,1)S(1)} async-done(((bf16[8,2,3,64,256]{4,3,2,1,0:T(8,128)(2,1)}), bf16[8,2,3,64,256]{4,3,2,1,0:T(8,128)(2,1)S(1)}, u32[]{:S(2)}, u32[]{:S(2)}) %all-to-all-start.8) | async-done | bytes 1572896 | tf_op jit(solution)/shard_map/all_to_all | solution.py:230
  648.4 3.5 convolution_convert_fusion
  653.0 3.4 collective-permute-start.16
  656.5 14.6 %collective-permute-done.16 = bf16[192,1024]{1,0:T(8,128)(2,1)S(1)} collective-permute-done((bf16[192,1024]{1,0:T(8,128)(2,1)S(1)}, bf16[192,1024]{1,0:T(8,128)(2,1)S(1)}, u32[]{:S(2)}, u32[]{:S(2)}) %collective-permute-start.16) | collective-permute-done | bytes 393248 | tf_op jit(solution)/shard_map/ppermute | solution.py:394
  677.2 4.4 fusion.7
  682.2 13.5 %collective-permute-done.15 = bf16[256,1024]{1,0:T(8,128)(2,1)S(1)} collective-permute-done((bf16[256,1024]{1,0:T(8,128)(2,1)S(1)}, bf16[256,1024]{1,0:T(8,128)(2,1)S(1)}, u32[]{:S(2)}, u32[]{:S(2)}) %collective-permute-start.15) | collective-permute-done | bytes 524320 | tf_op jit(solution)/shard_map/ppermute | solution.py:394
  698.1 4.0 collective-permute-done.19
  702.3 14.1 %all-gather.3 = bf16[16,80,256]{2,1,0:T(8,128)(2,1)S(1)} all-gather(bf16[2,80,256]{2,1,0:T(8,128)(2,1)S(1)} %pad_maximum_fusion.21), channel_id=5, replica_groups=mesh['far'=2,'near'=2,'rows'=8] {'rows'}, dimensions={0}, use_global_device_ids=true | all-gather | bytes 737280 | tf_op jit(solution)/shard_map/all_gather | solution.py:633
  717.6 2.9 collective-permute-start.20
  720.5 9.1 %collective-permute-done.21 = bf16[96,1024]{1,0:T(8,128)(2,1)S(1)} collective-permute-done((bf16[96,1024]{1,0:T(8,128)(2,1)S(1)}, bf16[96,1024]{1,0:T(8,128)(2,1)S(1)}, u32[]{:S(2)}, u32[]{:S(2)}) %collective-permute-start.21) | collective-permute-done | bytes 196640 | tf_op jit(solution)/shard_map/ppermute | solution.py:394
  735.6 6.7 slice_convert_fusion
  742.2 5.5 copy.145
  750.4 9.0 %collective-permute-done.17 = bf16[2,128,1024]{2,1,0:T(8,128)(2,1)S(1)} collective-permute-done((bf16[2,128,1024]{2,1,0:T(8,128)(2,1)S(1)}, bf16[2,128,1024]{2,1,0:T(8,128)(2,1)S(1)}, u32[]{:S(2)}, u32[]{:S(2)}) %collective-permute-start.17) | collective-permute-done | bytes 524320 | tf_op jit(solution)/shard_map/ppermute | solution.py:394
  763.3 3.1 slice_convert_fusion.1
  769.5 3.0 copy.143
  772.4 13.3 %collective-permute-done.18 = bf16[2,2,128,1024]{3,2,1,0:T(8,128)(2,1)} collective-permute-done((bf16[2,2,128,1024]{3,2,1,0:T(8,128)(2,1)}, bf16[2,2,128,1024]{3,2,1,0:T(8,128)(2,1)}, u32[]{:S(2)}, u32[]{:S(2)}) %collective-permute-start.18) | collective-permute-done | bytes 1048608 | tf_op jit(solution)/shard_map/ppermute | solution.py:394
  794.0 3.7 copy.141
  (377 shorter events, 164.3 us)
Async XLA Ops:
  7.2 250.2 %copy-start = (bf16[4,256,1024]{2,1,0:T(8,128)(2,1)S(1)}, bf16[4,256,1024]{2,1,0:T(8,128)(2,1)}, u32[]{:S(2)}) copy-start(bf16[4,256,1024]{2,1,0:T(8,128)(2,1)} %param.31) | copy-start | bytes 6291460
  7.2 67.7 %all-gather.15.cloned.1.call-start = ((), (), s32[]{:S(2)}) async-start(), calls=%async_computation.12 | async-start | bytes 1769472 | tf_op jit(solution)/shard_map/all_gather | solution.py:446
  10.0 17.7 %copy-start.55 = (s32[4,256]{1,0:T(4,128)S(1)}, s32[4,256]{1,0:T(4,128)}, u32[]{:S(2)}) copy-start(s32[4,256]{1,0:T(4,128)} %param.17) | copy-start | bytes 12292
  12.6 18.7 %copy-start.51 = (bf16[32,2,1024]{2,1,0:T(2,128)(2,1)S(1)}, bf16[32,2,1024]{2,1,0:T(2,128)(2,1)}, u32[]{:S(2)}) copy-start(bf16[32,2,1024]{2,1,0:T(2,128)(2,1)} %param.20) | copy-start | bytes 393220
  12.6 18.8 %copy-start.50 = (bf16[1024,256]{1,0:T(8,128)(2,1)S(1)}, bf16[1024,256]{1,0:T(8,128)(2,1)}, u32[]{:S(2)}) copy-start(bf16[1024,256]{1,0:T(8,128)(2,1)} %param.24) | copy-start | bytes 1572868
  13.7 13.2 %collective-permute-start.2 = (bf16[96,1024]{1,0:T(8,128)(2,1)S(1)}, bf16[96,1024]{1,0:T(8,128)(2,1)S(1)}, u32[]{:S(2)}, u32[]{:S(2)}) collective-permute-start(bf16[96,1024]{1,0:T(8,128)(2,1)S(1)} %constant_dynamic-slice_fusion.13), channel_id=1, source_target_pairs={{0,16},{16,0},{1,17},{17,1},{2,18},{18,2},{3,19},{19,3},{4,20},{20... | collective-permute-start | bytes 589832 | tf_op jit(solution)/shard_map/ppermute | solution.py:394
  27.6 139.2 %all-gather.17.cloned.1.call-start = ((), (), s32[]{:S(2)}) async-start(), calls=%async_computation.13 | async-start | bytes 1179648 | tf_op jit(solution)/shard_map/all_gather | solution.py:446
  39.6 35.3 %copy-start.42 = (bf16[512,1024]{1,0:T(8,128)(2,1)}, bf16[512,1024]{1,0:T(8,128)(2,1)S(1)}, u32[]{:S(2)}) copy-start(bf16[512,1024]{1,0:T(8,128)(2,1)S(1)} %get-tuple-element.42) | copy-start | bytes 3145732
  39.6 16.9 %collective-permute-start = (bf16[160,1024]{1,0:T(8,128)(2,1)S(1)}, bf16[160,1024]{1,0:T(8,128)(2,1)S(1)}, u32[]{:S(2)}, u32[]{:S(2)}) collective-permute-start(bf16[160,1024]{1,0:T(8,128)(2,1)S(1)} %pad_maximum_fusion.19), channel_id=1, source_target_pairs={{0,16},{16,0},{1,17},{17,1},{2,18},{18,2},{3,19},{19,3},{4,20},{20... | collective-permute-start | bytes 983048 | tf_op jit(solution)/shard_map/ppermute | solution.py:394
  57.9 126.6 %all-gather.31.cloned.1.call-start = ((), (), s32[]{:S(2)}) async-start(), calls=%async_computation.23 | async-start | bytes 2359296 | tf_op jit(solution)/shard_map/all_gather | solution.py:449
  59.0 9.4 %collective-permute-start.1 = (bf16[2,96,1024]{2,1,0:T(8,128)(2,1)S(1)}, bf16[2,96,1024]{2,1,0:T(8,128)(2,1)S(1)}, u32[]{:S(2)}, u32[]{:S(2)}) collective-permute-start(bf16[2,96,1024]{2,1,0:T(8,128)(2,1)S(1)} %pad_maximum_fusion.18), channel_id=1, source_target_pairs={{0,8},{8,0},{1,9},{9,1},{2,10},{10,2},{3,11},{11,3},{4,12},{12,4},... | collective-permute-start | bytes 1179656 | tf_op jit(solution)/shard_map/ppermute | solution.py:394
  69.4 117.3 %all-gather.29.cloned.1.call-start = ((), (), s32[]{:S(2)}) async-start(), calls=%async_computation.22 | async-start | bytes 2359296 | tf_op jit(solution)/shard_map/all_gather | solution.py:449
  70.0 192.3 %all-gather.33.cloned.1.call-start = ((), (), s32[]{:S(2)}) async-start(), calls=%async_computation.24 | async-start | bytes 2359296 | tf_op jit(solution)/shard_map/all_gather | solution.py:449
  84.2 30.2 %all-to-all-start = ((bf16[8,2,3,64,256]{4,3,2,1,0:T(8,128)(2,1)}), bf16[8,2,3,64,256]{4,3,2,1,0:T(8,128)(2,1)}, u32[]{:S(2)}, u32[]{:S(2)}) async-start(bf16[8,2,3,64,256]{4,3,2,1,0:T(8,128)(2,1)} %pad_maximum_fusion.3), calls=%async_computation | async-start | bytes 3145728 | tf_op jit(solution)/shard_map/all_to_all | solution.py:230
  88.5 184.6 %all-gather.21.cloned.1.call-start = ((), (), s32[]{:S(2)}) async-start(), calls=%async_computation.15 | async-start | bytes 2359296 | tf_op jit(solution)/shard_map/all_gather | solution.py:446
  92.5 23.8 %copy-start.31 = (bf16[4,2,64,1024]{3,2,1,0:T(8,128)(2,1)S(1)}, bf16[4,2,64,1024]{3,2,1,0:T(8,128)(2,1)}, u32[]{:S(2)}) copy-start(bf16[4,2,64,1024]{3,2,1,0:T(8,128)(2,1)} %copy.114) | copy-start | bytes 3145732
  115.4 21.7 %collective-permute-start.5 = (bf16[256,1024]{1,0:T(8,128)(2,1)S(1)}, bf16[256,1024]{1,0:T(8,128)(2,1)S(1)}, u32[]{:S(2)}, u32[]{:S(2)}) collective-permute-start(bf16[256,1024]{1,0:T(8,128)(2,1)S(1)} %pad_maximum_fusion.15), channel_id=1, source_target_pairs={{0,16},{16,0},{1,17},{17,1},{2,18},{18,2},{3,19},{19,3},{4,20},{20... | collective-permute-start | bytes 1572872 | tf_op jit(solution)/shard_map/ppermute | solution.py:394
  158.0 17.7 %all-to-all-start.1 = ((bf16[8,2,64,256]{3,2,1,0:T(8,128)(2,1)}), bf16[8,2,64,256]{3,2,1,0:T(8,128)(2,1)S(1)}, u32[]{:S(2)}, u32[]{:S(2)}) async-start(bf16[8,2,64,256]{3,2,1,0:T(8,128)(2,1)} %get-tuple-element.44), calls=%async_computation.1 | async-start | bytes 1048576 | tf_op jit(solution)/shard_map/all_to_all | solution.py:230
  177.1 10.6 %collective-permute-start.3 = (bf16[512,512]{1,0:T(8,128)(2,1)}, bf16[512,512]{1,0:T(8,128)(2,1)}, u32[]{:S(2)}, u32[]{:S(2)}) collective-permute-start(bf16[512,512]{1,0:T(8,128)(2,1)} %bitcast.153), channel_id=1, source_target_pairs={{0,8},{8,0},{1,9},{9,1},{2,10},{10,2},{3,11},{11,3},{4,12},{12,4},... | collective-permute-start | bytes 1572872 | tf_op jit(solution)/shard_map/ppermute | solution.py:394
  180.9 21.7 %all-to-all-start.3 = ((bf16[8,2,2,64,256]{4,3,2,1,0:T(8,128)(2,1)}), bf16[8,2,2,64,256]{4,3,2,1,0:T(8,128)(2,1)S(1)}, u32[]{:S(2)}, u32[]{:S(2)}) async-start(bf16[8,2,2,64,256]{4,3,2,1,0:T(8,128)(2,1)} %pad_maximum_fusion.5), calls=%async_computation.3 | async-start | bytes 2097152 | tf_op jit(solution)/shard_map/all_to_all | solution.py:230
  193.8 13.0 %copy-start.63 = (s32[4]{0:T(128)S(1)}, s32[4]{0:T(128)}, u32[]{:S(2)}) copy-start(s32[4]{0:T(128)} %param.19) | copy-start | bytes 52
  202.5 16.6 %all-to-all-start.2 = ((bf16[8,2,1,64,256]{4,3,2,1,0:T(8,128)(2,1)}), bf16[8,2,1,64,256]{4,3,2,1,0:T(8,128)(2,1)}, u32[]{:S(2)}, u32[]{:S(2)}) async-start(bf16[8,2,1,64,256]{4,3,2,1,0:T(8,128)(2,1)} %pad_maximum_fusion.12), calls=%async_computation.2 | async-start | bytes 1048576 | tf_op jit(solution)/shard_map/all_to_all | solution.py:230
  206.7 81.4 %all-gather.19.cloned.1.call-start = ((), (), s32[]{:S(2)}) async-start(), calls=%async_computation.14 | async-start | bytes 2359296 | tf_op jit(solution)/shard_map/all_gather | solution.py:446
  207.5 210.3 %reduce-scatter.4.cloned.1.call-start = ((), (), s32[]{:S(2)}) async-start(), calls=%async_computation.16 | async-start | bytes 9437184 | tf_op jit(solution)/shard_map/reduce_scatter | solution.py:556
  237.1 21.3 %copy-start.2 = (f32[8,2,64,256]{3,2,1,0:T(8,128)}, f32[8,2,64,256]{3,2,1,0:T(8,128)S(1)}, u32[]{:S(2)}) copy-start(f32[8,2,64,256]{3,2,1,0:T(8,128)S(1)} %get-tuple-element.48.wide_ref) | copy-start | bytes 3145732
  237.1 20.3 %copy-start.58 = (bf16[1024]{0:T(1024)(128)(2,1)S(1)}, bf16[1024]{0:T(1024)(128)(2,1)}, u32[]{:S(2)}) copy-start(bf16[1024]{0:T(1024)(128)(2,1)} %param.28) | copy-start | bytes 6148
  255.9 12.2 %collective-permute-start.4 = (bf16[512,512]{1,0:T(8,128)(2,1)}, bf16[512,512]{1,0:T(8,128)(2,1)}, u32[]{:S(2)}, u32[]{:S(2)}) collective-permute-start(bf16[512,512]{1,0:T(8,128)(2,1)} %bitcast.157), channel_id=1, source_target_pairs={{0,8},{8,0},{1,9},{9,1},{2,10},{10,2},{3,11},{11,3},{4,12},{12,4},... | collective-permute-start | bytes 1572872 | tf_op jit(solution)/shard_map/ppermute | solution.py:394
  260.8 7.3 copy-start.7
  291.3 8.0 copy-start.10
  311.6 277.2 %all-gather.23.cloned.1.call-start = ((), (), s32[]{:S(2)}) async-start(), calls=%async_computation.17 | async-start | bytes 4718592 | tf_op jit(solution)/shard_map/all_gather | solution.py:446
  317.0 22.3 %copy-start.11 = (f32[512,1024]{1,0:T(8,128)S(1)}, f32[512,1024]{1,0:T(8,128)}, u32[]{:S(2)}) copy-start(f32[512,1024]{1,0:T(8,128)} %copy-done.8) | copy-start | bytes 6291460
  317.1 22.2 %collective-permute-start.6 = (bf16[512,1024]{1,0:T(8,128)(2,1)S(1)}, bf16[512,1024]{1,0:T(8,128)(2,1)S(1)}, u32[]{:S(2)}, u32[]{:S(2)}) collective-permute-start(bf16[512,1024]{1,0:T(8,128)(2,1)S(1)} %convolution_convert_fusion.8), channel_id=1, source_target_pairs={{0,8},{8,0},{1,9},{9,1},{2,10},{10,2},{3,11},{11,3},{4,12},{12,4},... | collective-permute-start | bytes 3145736 | tf_op jit(solution)/shard_map/ppermute | solution.py:394
  318.7 21.6 %copy-start.24 = (bf16[2,256,1024]{2,1,0:T(8,128)(2,1)S(1)}, bf16[2,256,1024]{2,1,0:T(8,128)(2,1)}, u32[]{:S(2)}) copy-start(bf16[2,256,1024]{2,1,0:T(8,128)(2,1)} %constant_dynamic-slice_fusion.14) | copy-start | bytes 3145732
  343.0 19.6 %copy-start.3 = (f32[8,2,64,256]{3,2,1,0:T(8,128)S(1)}, f32[8,2,64,256]{3,2,1,0:T(8,128)}, u32[]{:S(2)}) copy-start(f32[8,2,64,256]{3,2,1,0:T(8,128)} %copy-done.2) | copy-start | bytes 3145732
  417.8 28.7 %copy-start.40 = (bf16[512,1024]{1,0:T(8,128)(2,1)S(1)}, bf16[512,1024]{1,0:T(8,128)(2,1)}, u32[]{:S(2)}) copy-start(bf16[512,1024]{1,0:T(8,128)(2,1)} %copy-done.39) | copy-start | bytes 3145732
  419.0 25.2 %collective-permute-start.8 = (bf16[256,1024]{1,0:T(8,128)(2,1)S(1)}, bf16[256,1024]{1,0:T(8,128)(2,1)S(1)}, u32[]{:S(2)}, u32[]{:S(2)}) collective-permute-start(bf16[256,1024]{1,0:T(8,128)(2,1)S(1)} %slice_bitcast_fusion.1), channel_id=1, source_target_pairs={{0,16},{16,0},{1,17},{17,1},{2,18},{18,2},{3,19},{19,3},{4,20},{20... | collective-permute-start | bytes 1572872 | tf_op jit(solution)/shard_map/ppermute | solution.py:394
  446.2 199.3 %reduce-scatter.6.cloned.1.call-start = ((), (), s32[]{:S(2)}) async-start(), calls=%async_computation.18 | async-start | bytes 7077888 | tf_op jit(solution)/shard_map/reduce_scatter | solution.py:556
  451.6 14.9 %collective-permute-start.7 = (bf16[512,512]{1,0:T(8,128)(2,1)S(1)}, bf16[512,512]{1,0:T(8,128)(2,1)S(1)}, u32[]{:S(2)}, u32[]{:S(2)}) collective-permute-start(bf16[512,512]{1,0:T(8,128)(2,1)S(1)} %bitcast.366), channel_id=1, source_target_pairs={{0,8},{8,0},{1,9},{9,1},{2,10},{10,2},{3,11},{11,3},{4,12},{12,4},... | collective-permute-start | bytes 1572872 | tf_op jit(solution)/shard_map/ppermute | solution.py:394
  453.9 33.1 %collective-permute-start.12 = (bf16[512,1024]{1,0:T(8,128)(2,1)S(1)}, bf16[512,1024]{1,0:T(8,128)(2,1)S(1)}, u32[]{:S(2)}, u32[]{:S(2)}) collective-permute-start(bf16[512,1024]{1,0:T(8,128)(2,1)S(1)} %fusion.25), channel_id=1, source_target_pairs={{0,8},{8,0},{1,9},{9,1},{2,10},{10,2},{3,11},{11,3},{4,12},{12,4},... | collective-permute-start | bytes 3145736 | tf_op jit(solution)/shard_map/ppermute | solution.py:394
  455.8 10.7 %copy-start.45 = (bf16[4,256,1024]{2,1,0:T(8,128)(2,1)S(1)}, bf16[4,256,1024]{2,1,0:T(8,128)(2,1)}, u32[]{:S(2)}) copy-start(bf16[4,256,1024]{2,1,0:T(8,128)(2,1)} %all-gather.31.cloned.1.call-done) | copy-start | bytes 6291460
  476.1 11.3 %copy-start.16 = (bf16[2,256,768]{2,1,0:T(8,128)(2,1)S(1)}, bf16[2,256,768]{2,1,0:T(8,128)(2,1)}, u32[]{:S(2)}) copy-start(bf16[2,256,768]{2,1,0:T(8,128)(2,1)} %copy-done.15) | copy-start | bytes 2359300
  489.4 8.7 %copy-start.12 = (f32[512,1024]{1,0:T(8,128)S(1)}, f32[512,1024]{1,0:T(8,128)}, u32[]{:S(2)}) copy-start(f32[512,1024]{1,0:T(8,128)} %copy-done.8) | copy-start | bytes 6291460
  497.8 12.2 %collective-permute-start.9 = (bf16[256,1024]{1,0:T(8,128)(2,1)}, bf16[256,1024]{1,0:T(8,128)(2,1)}, u32[]{:S(2)}, u32[]{:S(2)}) collective-permute-start(bf16[256,1024]{1,0:T(8,128)(2,1)} %bitcast.51), channel_id=1, source_target_pairs={{0,8},{8,0},{1,9},{9,1},{2,10},{10,2},{3,11},{11,3},{4,12},{12,4},... | collective-permute-start | bytes 1572872 | tf_op jit(solution)/shard_map/ppermute | solution.py:394
  511.6 26.3 %copy-start.21 = (bf16[4,256,1024]{2,1,0:T(8,128)(2,1)S(1)}, bf16[4,256,1024]{2,1,0:T(8,128)(2,1)}, u32[]{:S(2)}) copy-start(bf16[4,256,1024]{2,1,0:T(8,128)(2,1)} %all-gather.29.cloned.1.call-done) | copy-start | bytes 6291460
  511.6 24.4 %collective-permute-start.10 = (bf16[2,128,1024]{2,1,0:T(8,128)(2,1)S(1)}, bf16[2,128,1024]{2,1,0:T(8,128)(2,1)S(1)}, u32[]{:S(2)}, u32[]{:S(2)}) collective-permute-start(bf16[2,128,1024]{2,1,0:T(8,128)(2,1)S(1)} %bitcast.336), channel_id=1, source_target_pairs={{0,16},{16,0},{1,17},{17,1},{2,18},{18,2},{3,19},{19,3},{4,20},{20... | collective-permute-start | bytes 1572872 | tf_op jit(solution)/shard_map/ppermute | solution.py:394
  537.5 24.8 %collective-permute-start.11 = (bf16[2,2,128,1024]{3,2,1,0:T(8,128)(2,1)}, bf16[2,2,128,1024]{3,2,1,0:T(8,128)(2,1)}, u32[]{:S(2)}, u32[]{:S(2)}) collective-permute-start(bf16[2,2,128,1024]{3,2,1,0:T(8,128)(2,1)} %get-tuple-element.144), channel_id=1, source_target_pairs={{0,8},{8,0},{1,9},{9,1},{2,10},{10,2},{3,11},{11,3},{4,12},{12,4},... | collective-permute-start | bytes 3145736 | tf_op jit(solution)/shard_map/ppermute | solution.py:394
  537.9 24.4 %copy-start.27 = (bf16[1,2,2,128,1024]{4,3,0,2,1:T(8,128)(2,1)S(1)}, bf16[1,2,2,128,1024]{4,3,0,2,1:T(8,128)(2,1)}, u32[]{:S(2)}) copy-start(bf16[1,2,2,128,1024]{4,3,0,2,1:T(8,128)(2,1)} %get-tuple-element.143) | copy-start | bytes 3145732
  568.2 18.9 %collective-permute-start.13 = (bf16[2,128,768]{2,1,0:T(8,128)(2,1)S(1)}, bf16[2,128,768]{2,1,0:T(8,128)(2,1)S(1)}, u32[]{:S(2)}, u32[]{:S(2)}) collective-permute-start(bf16[2,128,768]{2,1,0:T(8,128)(2,1)S(1)} %bitcast.373), channel_id=1, source_target_pairs={{0,16},{16,0},{1,17},{17,1},{2,18},{18,2},{3,19},{19,3},{4,20},{20... | collective-permute-start | bytes 1179656 | tf_op jit(solution)/shard_map/ppermute | solution.py:394
  571.3 17.5 %all-to-all-start.7 = ((bf16[8,2,1,64,256]{4,3,1,2,0:T(8,128)(2,1)}), bf16[8,2,1,64,256]{4,3,1,2,0:T(8,128)(2,1)S(1)}, u32[]{:S(2)}, u32[]{:S(2)}) async-start(bf16[8,2,1,64,256]{4,3,1,2,0:T(8,128)(2,1)} %pad_maximum_fusion.17), calls=%async_computation.8 | async-start | bytes 1048576 | tf_op jit(solution)/shard_map/all_to_all | solution.py:230
  579.3 9.5 %copy-start.5 = (f32[8,2,64,256]{3,2,1,0:T(8,128)S(1)}, f32[8,2,64,256]{3,2,1,0:T(8,128)}, u32[]{:S(2)}) copy-start(f32[8,2,64,256]{3,2,1,0:T(8,128)} %copy-done.4) | copy-start | bytes 3145732
  588.1 36.5 %collective-permute-start.14 = (bf16[2,2,128,768]{3,2,1,0:T(8,128)(2,1)}, bf16[2,2,128,768]{3,2,1,0:T(8,128)(2,1)}, u32[]{:S(2)}, u32[]{:S(2)}) collective-permute-start(bf16[2,2,128,768]{3,2,1,0:T(8,128)(2,1)} %get-tuple-element.146), channel_id=1, source_target_pairs={{0,8},{8,0},{1,9},{9,1},{2,10},{10,2},{3,11},{11,3},{4,12},{12,4},... | collective-permute-start | bytes 2359304 | tf_op jit(solution)/shard_map/ppermute | solution.py:394
  621.0 24.5 %all-to-all-start.8 = ((bf16[8,2,3,64,256]{4,3,2,1,0:T(8,128)(2,1)}), bf16[8,2,3,64,256]{4,3,2,1,0:T(8,128)(2,1)S(1)}, u32[]{:S(2)}, u32[]{:S(2)}) async-start(bf16[8,2,3,64,256]{4,3,2,1,0:T(8,128)(2,1)} %pair_backward.3), calls=%async_computation.9 | async-start | bytes 3145728 | tf_op jit(solution)/shard_map/all_to_all | solution.py:230
  624.6 91.9 %reduce-scatter.8.cloned.1.call-start = ((), (), s32[]{:S(2)}) async-start(), calls=%async_computation.20 | async-start | bytes 3538944 | tf_op jit(solution)/shard_map/reduce_scatter | solution.py:556
  651.9 20.5 %copy-start.56 = (s32[4,256]{1,0:T(4,128)S(1)}, s32[4,256]{1,0:T(4,128)}, u32[]{:S(2)}) copy-start(s32[4,256]{1,0:T(4,128)} %param.17) | copy-start | bytes 12292
  651.9 81.2 %all-gather.25.cloned.1.call-start = ((), (), s32[]{:S(2)}) async-start(), calls=%async_computation.19 | async-start | bytes 3538944 | tf_op jit(solution)/shard_map/all_gather | solution.py:446
  653.0 18.1 %collective-permute-start.16 = (bf16[192,1024]{1,0:T(8,128)(2,1)S(1)}, bf16[192,1024]{1,0:T(8,128)(2,1)S(1)}, u32[]{:S(2)}, u32[]{:S(2)}) collective-permute-start(bf16[192,1024]{1,0:T(8,128)(2,1)S(1)} %slice_bitcast_fusion.3), channel_id=1, source_target_pairs={{0,16},{16,0},{1,17},{17,1},{2,18},{18,2},{3,19},{19,3},{4,20},{20... | collective-permute-start | bytes 1179656 | tf_op jit(solution)/shard_map/ppermute | solution.py:394
  672.1 118.2 %all-gather.27.cloned.1.call-start = ((), (), s32[]{:S(2)}) async-start(), calls=%async_computation.21 | async-start | bytes 1769472 | tf_op jit(solution)/shard_map/all_gather | solution.py:446
  681.6 14.1 %collective-permute-start.15 = (bf16[256,1024]{1,0:T(8,128)(2,1)S(1)}, bf16[256,1024]{1,0:T(8,128)(2,1)S(1)}, u32[]{:S(2)}, u32[]{:S(2)}) collective-permute-start(bf16[256,1024]{1,0:T(8,128)(2,1)S(1)} %bitcast.369), channel_id=1, source_target_pairs={{0,8},{8,0},{1,9},{9,1},{2,10},{10,2},{3,11},{11,3},{4,12},{12,4},... | collective-permute-start | bytes 1572872 | tf_op jit(solution)/shard_map/ppermute | solution.py:394
  697.0 5.0 collective-permute-start.19
  717.5 12.0 %collective-permute-start.21 = (bf16[96,1024]{1,0:T(8,128)(2,1)S(1)}, bf16[96,1024]{1,0:T(8,128)(2,1)S(1)}, u32[]{:S(2)}, u32[]{:S(2)}) collective-permute-start(bf16[96,1024]{1,0:T(8,128)(2,1)S(1)} %slice_bitcast_fusion.4), channel_id=1, source_target_pairs={{0,16},{16,0},{1,17},{17,1},{2,18},{18,2},{3,19},{19,3},{4,20},{20... | collective-permute-start | bytes 589832 | tf_op jit(solution)/shard_map/ppermute | solution.py:394
  717.6 32.1 %collective-permute-start.20 = (bf16[80,256]{1,0:T(8,128)(2,1)S(1)}, bf16[80,256]{1,0:T(8,128)(2,1)S(1)}, u32[]{:S(2)}, u32[]{:S(2)}) collective-permute-start(bf16[80,256]{1,0:T(8,128)(2,1)S(1)} %fusion.76), channel_id=1, source_target_pairs={{0,16},{16,0},{1,17},{17,1},{2,18},{18,2},{3,19},{19,3},{4,20},{20... | collective-permute-start | bytes 122888 | tf_op jit(solution)/shard_map/ppermute | solution.py:394
  733.2 26.2 %collective-permute-start.17 = (bf16[2,128,1024]{2,1,0:T(8,128)(2,1)S(1)}, bf16[2,128,1024]{2,1,0:T(8,128)(2,1)S(1)}, u32[]{:S(2)}, u32[]{:S(2)}) collective-permute-start(bf16[2,128,1024]{2,1,0:T(8,128)(2,1)S(1)} %bitcast.327), channel_id=1, source_target_pairs={{0,16},{16,0},{1,17},{17,1},{2,18},{18,2},{3,19},{19,3},{4,20},{20... | collective-permute-start | bytes 1572872 | tf_op jit(solution)/shard_map/ppermute | solution.py:394
  760.8 24.8 %collective-permute-start.18 = (bf16[2,2,128,1024]{3,2,1,0:T(8,128)(2,1)}, bf16[2,2,128,1024]{3,2,1,0:T(8,128)(2,1)}, u32[]{:S(2)}, u32[]{:S(2)}) collective-permute-start(bf16[2,2,128,1024]{3,2,1,0:T(8,128)(2,1)} %get-tuple-element.142), channel_id=1, source_target_pairs={{0,8},{8,0},{1,9},{9,1},{2,10},{10,2},{3,11},{11,3},{4,12},{12,4},... | collective-permute-start | bytes 3145736 | tf_op jit(solution)/shard_map/ppermute | solution.py:394
  769.4 16.2 %copy-start.26 = (bf16[1,2,2,128,1024]{4,3,0,2,1:T(8,128)(2,1)S(1)}, bf16[1,2,2,128,1024]{4,3,0,2,1:T(8,128)(2,1)}, u32[]{:S(2)}) copy-start(bf16[1,2,2,128,1024]{4,3,0,2,1:T(8,128)(2,1)} %get-tuple-element.141) | copy-start | bytes 3145732
  (47 other events, 122.3 us)
Sparse Core Ops, SparseCore 0:
  27.7 26.8 all-gather.14
  58.0 22.5 all-gather.16
  83.1 36.3 all-gather.30
  121.2 26.4 all-gather.28
  149.4 30.0 all-gather.32
  181.8 36.2 all-gather.20
  220.0 34.6 all-gather.18
  311.8 74.9 reduce-scatter.3
  446.4 34.3 all-gather.22
  489.5 60.4 reduce-scatter.5
  652.0 45.4 reduce-scatter.7
  700.0 33.1 all-gather.24
  735.2 25.6 all-gather.26

commit v4 on v3

--- a/solution.py
+++ b/solution.py
@@ -432,8 +432,6 @@
     n_rows = lax.axis_size("rows")
     row_rank = lax.axis_index("rows")
     far, near = lax.axis_index("far"), lax.axis_index("near")
-    own = 2 * far + near
-    other = 2 * (1 - far) + near
 
     def objects_of(value):
         return lax.dynamic_slice_in_dim(value, objects * far, objects, 0)
@@ -445,15 +443,18 @@
     def join_rows(value):
         return lax.all_gather(value, "rows", axis=0, tiled=True)
 
-    def put_together(value):
-        whole = lax.all_gather(value, "rows", axis=1)
-        return whole.reshape(value.shape[0] * cols, width)
-
     def both_columns(value):
         return [
-            lax.dynamic_slice_in_dim(value, index * cols, cols, value.ndim - 1)
-            for index in (own, other)
+            lax.dynamic_slice_in_dim(value, (2 * index + near) * cols, cols, value.ndim - 1)
+            for index in range(2)
         ]
+
+    def in_order(mine, away, axis=0):
+        size = mine.shape[axis]
+        shape = list(mine.shape)
+        shape[axis] *= 2
+        out = lax.dynamic_update_slice_in_dim(jnp.zeros(shape, mine.dtype), mine, far * size, axis)
+        return lax.dynamic_update_slice_in_dim(out, away, (1 - far) * size, axis)
 
     def halves(value):
         value = value.reshape(objects, 2, rows // 2, -1)
@@ -466,7 +467,7 @@
         mine, away = halves(partial)
         return mine + swap(away.astype(LOW), "near").astype(WIDE)
 
-    def over_heads(value):
+    def swap_over_heads(value):
         value = value.reshape(objects, rows // 2, -1)
         value = jnp.stack([value, swap(value, "far")])
         value = jnp.stack([value, swap(value, "near")])
@@ -474,11 +475,16 @@
         value = jnp.where(near == 0, value, jnp.flip(value, 0))
         return value.transpose(1, 2, 0, 3, 4).reshape(2 * objects, rows, -1)
 
+    def over_heads(value):
+        value = lax.all_gather(value.reshape(objects, rows // 2, -1), ("far", "near"), axis=0)
+        value = value.reshape(2, 2, objects, rows // 2, -1).transpose(0, 2, 1, 3, 4)
+        return value.reshape(2 * objects, rows, -1)
+
     def to_pairs(weights, value, slots):
         parts = [
-            jnp.concatenate(
-                [mul(weight, value[i * rows : (i + 1) * rows], NT).astype(LOW) for weight in weights]
-            ).reshape(n_rows, slots, HEAD_DIM, rows)
+            mul(weights, value[i * rows : (i + 1) * rows], NT)
+            .astype(LOW)
+            .reshape(n_rows, slots, HEAD_DIM, rows)
             for i in range(objects)
         ]
         return exchange_rows(jnp.stack(parts, axis=1))
@@ -495,7 +501,7 @@
     pair_rows = pair_rows.reshape(2 * cols, width)
     query_rows = cross_query.T
 
-    qkv_other = join_rows(swap(piece(qkv_rows), "far"))
+    qkv_away = join_rows(swap(piece(qkv_rows), "far"))
 
     table_flat = camera_table.reshape(codes, -1)
     cross_gain_f = cross_gain.astype(WIDE)
@@ -514,32 +520,37 @@
 
     mine = [piece(v) for v in (self_output, query_rows, cross_output, pair_rows)]
     normed_one, *mine = tie(normed_one, *mine)
-    across = swap(jnp.concatenate(mine, axis=0), "far")
+    mine = jnp.concatenate(mine, axis=0)
+    across = swap(mine, "far")
     size = cols // n_rows
-    two = jnp.stack([jnp.concatenate(mine[:3]), across[: 3 * size]])
+    two = in_order(mine[None, : 3 * size], across[None, : 3 * size])
     four = jnp.concatenate([two, swap(two, "near")])
-    pair_other = join_rows(across[3 * size :])
-    self_whole, query_whole, cross_whole = (
-        put_together(four[:, i * size : (i + 1) * size]) for i in range(3)
-    )
-
-    qkv = to_pairs((qkv_rows, qkv_other), normed_one, 3)
+    sent = jnp.concatenate([four.reshape(-1, width), across[3 * size :]])
+    sent = lax.all_gather(sent, "rows", axis=0)
+    pair_away = sent[:, 12 * size :].reshape(2 * cols, width)
+    whole = sent[:, : 12 * size].reshape(n_rows, 4, 3, size, width).transpose(2, 1, 0, 3, 4)
+    self_whole, query_whole, cross_whole = whole.reshape(3, 4 * cols, width)
+
+    qkv_both = in_order(qkv_rows, qkv_away)
+    qkv = to_pairs(qkv_both, normed_one, 3)
     patch_mid = mul(patch_in, patch_weights).astype(LOW)
-    pair = to_pairs((pair_rows, pair_other), patch_mid, 2)
+    pair_both = in_order(pair_rows, pair_away)
+    pair = to_pairs(pair_both, patch_mid, 2)
 
     mine = [piece(widen_weights), piece(narrow_weights)]
     qkv, *mine = tie(qkv, *mine)
     across = swap(jnp.concatenate(mine, axis=0), "far")
+    sent = lax.all_gather(across, "rows", axis=0)
     size = width // n_rows
-    widen = jnp.concatenate([widen_weights, join_rows(across[:size])], axis=1)
-    narrow = jnp.concatenate([narrow_weights, join_rows(across[size:])], axis=0)
+    widen = in_order(widen_weights, sent[:, :size].reshape(width, hidden), axis=1)
+    narrow = in_order(narrow_weights, sent[:, size:].reshape(hidden, width))
 
     mixed, self_wide, self_log = pair_forward(qkv, qkv, 1)
     self_mixed_t = from_pairs(exchange_rows(mixed)[:, :, None])
     after_self = inputs + over_all_columns(self_mixed_t, self_whole)
     unit_two, rate_two = normed(after_self)
     normed_two = (unit_two * cross_gain_f).astype(LOW)
-    cross_q = to_pairs((query_whole[: 2 * cols],), normed_two, 1)
+    cross_q = to_pairs(query_whole[: 2 * cols], normed_two, 1)
     mixed, cross_wide, cross_log = pair_forward(cross_q, pair, 0, length)
     cross_mixed_t = from_pairs(exchange_rows(mixed)[:, :, None])
     after_cross = after_self + over_all_columns(cross_mixed_t, cross_whole)
@@ -553,10 +564,8 @@
     result = (halves(after_cross)[0] + hidden_half).astype(LOW)
 
     def part_rows(both):
-        return lax.psum_scatter(both, "rows", scatter_dimension=1, tiled=True)
-
-    def total_rows(part):
-        return join_rows((part[0].astype(WIDE) + swap(part[1], "far").astype(WIDE)).astype(LOW))
+        both = both.reshape(-1, both.shape[-1])
+        return lax.psum_scatter(both, ("far", "rows"), scatter_dimension=0, tiled=True)
 
     def by_shard(left, right):
         return mul(left, right, NN).astype(LOW).reshape(2, -1, right.shape[1])
@@ -576,11 +585,10 @@
         grad_three * hidden_gain_f, unit_three, rate_three
     )
     grad_cross_low = grad_cross.astype(LOW)
-    grad_mixed = to_pairs((cross_whole[: 2 * cols],), grad_cross_low, 1)[:, :, 0]
+    grad_mixed = to_pairs(cross_whole[: 2 * cols], grad_cross_low, 1)[:, :, 0]
     grads = pair_backward(cross_q, pair, 0, length, grad_mixed, cross_wide, cross_log)
     grads = exchange_rows(grads)
-    grads, hidden_part = tie(grads, hidden_part)
-    hidden_total = total_rows(hidden_part)
+    hidden_total = join_rows(hidden_part)
     outputs = over_heads(result)
     grad_cq_t = from_pairs(grads[:, :, :1])
     grad_pair_t = from_pairs(grads[:, :, 1:])
@@ -589,7 +597,7 @@
     grad_self = grad_cross + normed_back(grad_two * cross_gain_f, unit_two, rate_two)
     grad_self_low = grad_self.astype(LOW)
     grad_mid = sum_near(
-        mul(grad_pair_t, jnp.concatenate([pair_rows, pair_other]), TN)
+        mul(grad_pair_t, pair_both, TN)
     ).astype(LOW)
     patch_half = mul(halves(grad_mid)[0], patch_weights, NT).astype(LOW)
     patch_terms = jnp.stack([mul(value, patch_in, TN).astype(LOW) for value in both_columns(grad_mid)])
@@ -606,15 +614,15 @@
             axis=1,
         )
     )
-    grad_mixed = to_pairs((self_whole[: 2 * cols],), grad_self_low, 1)[:, :, 0]
+    grad_mixed = to_pairs(self_whole[: 2 * cols], grad_self_low, 1)[:, :, 0]
     grad_mixed, hidden_total, outputs = tie(grad_mixed, hidden_total, outputs)
     grads = exchange_rows(pair_backward(qkv, qkv, 1, None, grad_mixed, self_wide, self_log))
     patch_grads = over_heads(patch_half)
     grads, middle_part, patch_grads = tie(grads, middle_part, patch_grads)
-    middle_total = total_rows(middle_part)
+    middle_total = join_rows(middle_part)
     grad_qkv_t = from_pairs(grads)
     last_part = part_rows(by_shard(grad_qkv_t, normed_one))
-    grad_one = half_sum_near(mul(grad_qkv_t, jnp.concatenate([qkv_rows, qkv_other]), TN))
+    grad_one = half_sum_near(mul(grad_qkv_t, qkv_both, TN))
     gain_half, unit_half, rate_half, self_half = (
         halves(value)[0] for value in (gain_one, unit_one, rate_one, grad_self)
     )
@@ -630,11 +638,14 @@
     )
     small = [sum_near(table_term), hidden_gain_term[None], cross_gain_term[None], jnp.zeros((14, width), WIDE)]
     small = jnp.stack(both_columns(jnp.concatenate(small, axis=0).astype(LOW)))
-    small = jnp.sum(lax.all_gather(small, "rows", axis=0).astype(WIDE), axis=0)
-    small = small[0] + swap(small[1].astype(LOW), "far").astype(WIDE)
+    small = jnp.sum(lax.all_gather(small, "rows", axis=0).astype(WIDE), axis=0).astype(LOW)
+    small_own, small_away = (
+        lax.dynamic_index_in_dim(small, index, 0, keepdims=False) for index in (far, 1 - far)
+    )
+    small = small_own.astype(WIDE) + swap(small_away, "far").astype(WIDE)
     input_half, middle_total = tie(input_half, middle_total)
-    input_grads = over_heads(input_half)
-    last_total = total_rows(last_part)
+    input_grads = swap_over_heads(input_half)
+    last_total = join_rows(last_part)
 
     output_total = middle_total[: 2 * cols]
     query_total = middle_total[2 * cols : 3 * cols]

time: 817 us -> 836 us (1.023)
  waiting for transfers between devices: 319 us -> 395 us
  blocking collectives: 74.7 us -> 22.4 us
  local copies, waits for them, and re-layouts: 90.2 us -> 117 us
  other arithmetic: 74.9 us -> 56.6 us
  Pallas kernels: 100 us -> 87.3 us
    reduce_scatter x3, waiting for transfers between devices: 0.02 us -> 144 us  [part_rows(): lax.psum_scatter(both, ('far', 'rows'), scatter_dimension=0, tiled=True)]
    ppermute x22 -> x15, waiting for transfers between devices: 254 us -> 154 us  [swap(): return lax.ppermute(value, axis, [(0, 1), (1, 0)])]
    all_to_all x3 -> x1, blocking collectives: 60.5 us -> 12.3 us  [exchange_rows(): return lax.all_to_all(value, 'rows', 0, 0, tiled=True)]
    all_gather x7 -> x4, waiting for transfers between devices: 2.02 us -> 22.5 us  [join_rows(): return lax.all_gather(value, 'rows', axis=0, tiled=True)]
    all_to_all x6 -> x8, waiting for transfers between devices: 61.6 us -> 74.7 us  [exchange_rows(): return lax.all_to_all(value, 'rows', 0, 0, tiled=True)]
    dynamic_update_slice x0 -> x9, local copies, waits for them, and re-layouts: none -> 11.8 us  [the longest x5 7.75 us: in_order(): return lax.dynamic_update_slice_in_dim(out, away, (1 - far) * size, axis)]
    concatenate x6 -> x0, local copies, waits for them, and re-layouts: 10.7 us -> none  [the longest x4 4.31 us: to_pairs(): jnp.concatenate([mul(weight, value[i * rows:(i + 1) * rows], NT).astype(L...]
    pallas_call x2, Pallas kernels: 63.1 us -> 53.9 us  [pair_backward(): pl.pallas_call(kernel, grid_spec=pltpu.PrefetchScalarGridSpec(num_scalar_...]
  transfers between devices with their start and end apart: 41 -> 34, of which waited for: 26 -> 23; matrix products, arithmetic and copies ran while one was open for 23% -> 23% of each run, Pallas kernels for 12% -> 11%
where the time goes in v4:
time: 836 us; the launch traced here: 823 us
  waiting for transfers between devices  395 us (47%)
  local copies, waits for them, and re-layouts  117 us (14%)
  Pallas kernels  87.3 us (10%)
  matrix products  74.8 us (9%)
  other arithmetic  56.6 us (7%)
  starting transfers between devices  53.6 us (6%)
  blocking collectives  22.4 us (3%)
  between operations  15.7 us (2%)
    ppermute x15, waiting for transfers between devices, swap(): return lax.ppermute(value, axis, [(0, 1), (1, 0)])  154 us
    reduce_scatter x3, waiting for transfers between devices, part_rows(): lax.psum_scatter(both, ('far', 'rows'), scatter_dimension=0, tiled=True)  144 us
    all_to_all x8, waiting for transfers between devices, exchange_rows(): return lax.all_to_all(value, 'rows', 0, 0, tiled=True)  74.7 us
    dot_general x31, matrix products, mul(): return lax.dot_general(left, right, dims, preferred_element_type=WIDE)  73.8 us
    pallas_call x2, Pallas kernels, pair_backward(): pl.pallas_call(kernel, grid_spec=pltpu.PrefetchScalarGridSpec(num_scalar_...  53.9 us
    unnamed x175, local copies, waits for them, and re-layouts  43.5 us
    pallas_call x2, Pallas kernels, pair_forward(): pl.pallas_call(kernel, grid_spec=pltpu.PrefetchScalarGridSpec(num_scalar_...  33.4 us
    all_to_all x8, starting transfers between devices, exchange_rows(): return lax.all_to_all(value, 'rows', 0, 0, tiled=True)  32.8 us
  transfers between devices with their start and end apart: 34, of which 23 were waited for; matrix products, arithmetic and copies ran while one was open for 23% of the time, Pallas kernels for 11%

profile of v4, /device:TPU:0, one launch (start us, length us, event | category | flops | bytes accessed | tf_op | source)
XLA Modules:
  0.0 822.8 jit_solution(9048305076921453396)
XLA Ops:
  14.4 4.0 collective-permute-start.2
  19.9 7.8 collective-permute-done.2
  40.8 17.1 %collective-permute-done = bf16[160,1024]{1,0:T(8,128)(2,1)} collective-permute-done((bf16[160,1024]{1,0:T(8,128)(2,1)}, bf16[160,1024]{1,0:T(8,128)(2,1)}, u32[]{:S(2)}, u32[]{:S(2)}) %collective-permute-start) | collective-permute-done | bytes 327712 | tf_op jit(solution)/shard_map/ppermute | solution.py:394
  59.8 8.5 %collective-permute-done.1 = bf16[2,96,1024]{2,1,0:T(8,128)(2,1)S(1)} collective-permute-done((bf16[2,96,1024]{2,1,0:T(8,128)(2,1)S(1)}, bf16[2,96,1024]{2,1,0:T(8,128)(2,1)S(1)}, u32[]{:S(2)}, u32[]{:S(2)}) %collective-permute-start.1) | collective-permute-done | bytes 393248 | tf_op jit(solution)/shard_map/ppermute | solution.py:394
  75.3 3.2 convolution_convert_fusion.3
  78.6 2.9 convolution_convert_fusion.4
  82.8 4.3 all-to-all-start
  88.3 24.3 %all-to-all-done.q_ref.k_ref.v_ref = bf16[8,2,3,64,256]{4,3,2,1,0:T(8,128)(2,1)} async-done(((bf16[8,2,3,64,256]{4,3,2,1,0:T(8,128)(2,1)}), bf16[8,2,3,64,256]{4,3,2,1,0:T(8,128)(2,1)}, u32[]{:S(2)}, u32[]{:S(2)}) %all-to-all-start) | async-done | bytes 1572896 | tf_op jit(solution)/shard_map/all_to_all | solution.py:230
  114.0 3.3 dynamic-slice_convert_fusion.2
  117.3 17.6 %collective-permute-done.5 = bf16[256,1024]{1,0:T(8,128)(2,1)S(1)} collective-permute-done((bf16[256,1024]{1,0:T(8,128)(2,1)S(1)}, bf16[256,1024]{1,0:T(8,128)(2,1)S(1)}, u32[]{:S(2)}, u32[]{:S(2)}) %collective-permute-start.5) | collective-permute-done | bytes 524320 | tf_op jit(solution)/shard_map/ppermute | solution.py:394
  135.7 19.0 %pair_forward.2 = (bf16[8,2,64,256]{3,2,1,0:T(8,128)(2,1)}, f32[8,2,64,256]{3,2,1,0:T(8,128)S(1)}, f32[8,2,1,256]{3,2,1,0:T(1,128)S(1)}) custom-call(s32[2]{0:T(128)S(1)} %broadcast_13_len_ref.2.len_ref, bf16[8,2,3,64,256]{4,3,2,1,0:T(8,128)(2,1)} %all-to-all-done.q_ref.k_ref.v_ref, bf16[8,2,3,64,256]{4,3,2,1,0:T(8,128)(2,1)} %all-to-all-done.q_ref.k_ref.v_ref, ...), custom_call_target="tpu_custom_call" | custom-call | flops 20132659200 | bytes 8388608 | tf_op jit(solution)/shard_map/pair_forward/pallas_call | solution.py:282
  155.7 5.7 all-to-all-start.1
  167.8 9.4 %all-to-all-done.1 = bf16[8,2,64,256]{3,2,1,0:T(8,128)(2,1)S(1)} async-done(((bf16[8,2,64,256]{3,2,1,0:T(8,128)(2,1)}), bf16[8,2,64,256]{3,2,1,0:T(8,128)(2,1)S(1)}, u32[]{:S(2)}, u32[]{:S(2)}) %all-to-all-start.1) | async-done | bytes 524320 | tf_op jit(solution)/shard_map/all_to_all | solution.py:230
  178.1 3.6 slice.159
  185.7 2.7 fusion.71
  194.1 3.5 all-to-all-start.2
  208.1 3.6 all-to-all-start.3
  219.6 7.4 all-to-all-done.3.k_ref.v_ref
  227.0 14.4 %pair_forward.3 = (bf16[8,2,64,256]{3,2,1,0:T(8,128)(2,1)}, f32[8,2,64,256]{3,2,1,0:T(8,128)S(1)}, f32[8,2,1,256]{3,2,1,0:T(1,128)S(1)}) custom-call(s32[2]{0:T(128)S(1)} %dynamic_slice.102.len_ref, bf16[8,2,1,64,256]{4,3,2,1,0:T(8,128)(2,1)S(1)} %copy-done.3, bf16[8,2,2,64,256]{4,3,2,1,0:T(8,128)(2,1)S(1)} %all-to-all-done.3.k_ref.v_ref, ...), custom_call_target="tpu_custom_call" | custom-call | flops 14092861440 | bytes 8388608 | tf_op jit(solution)/shard_map/pair_forward/pallas_call | solution.py:282
  241.4 4.1 all-to-all-start.4
  245.9 2.9 fusion.72
  259.0 4.7 fusion.76
  263.9 5.3 collective-permute-done.4
  271.4 4.9 fusion.6
  276.3 4.7 convolution_convert_fusion.1
  280.9 5.3 convolution_convert_fusion.2
  286.2 7.8 pad_maximum_fusion
  294.1 6.1 fusion.67
  306.2 15.4 %collective-permute-done.8 = bf16[256,1024]{1,0:T(8,128)(2,1)} collective-permute-done((bf16[256,1024]{1,0:T(8,128)(2,1)}, bf16[256,1024]{1,0:T(8,128)(2,1)}, u32[]{:S(2)}, u32[]{:S(2)}) %collective-permute-start.8) | collective-permute-done | bytes 524320 | tf_op jit(solution)/shard_map/ppermute | solution.py:394
  323.9 5.3 convolution_convert_fusion.11
  330.7 35.8 %collective-permute-done.6 = bf16[512,1024]{1,0:T(8,128)(2,1)S(1)} collective-permute-done((bf16[512,1024]{1,0:T(8,128)(2,1)S(1)}, bf16[512,1024]{1,0:T(8,128)(2,1)S(1)}, u32[]{:S(2)}, u32[]{:S(2)}) %collective-permute-start.6) | collective-permute-done | bytes 1048608 | tf_op jit(solution)/shard_map/ppermute | solution.py:394
  367.5 34.1 %reduce-scatter.4.cloned.1.call-done = bf16[256,1024]{1,0:T(8,128)(2,1)} async-done(((bf16[4096,1024]{1,0:T(8,128)(2,1)}), bf16[256,1024]{1,0:T(8,128)(2,1)}) %reduce-scatter.4.cloned.1.call-update) | async-done | bytes 524304 | tf_op jit(solution)/shard_map/reduce_scatter | solution.py:568
  401.7 4.9 fusion.69
  407.6 12.3 %all_to_all.45 = bf16[8,2,1,64,256]{4,3,1,2,0:T(8,128)(2,1)S(1)} all-to-all(bf16[8,2,1,64,256]{4,3,1,2,0:T(8,128)(2,1)S(1)} %pad_maximum_fusion.9), channel_id=1, replica_groups=mesh['far'=2,'near'=2,'rows'=8] {'rows'}, dimensions={0} | all-to-all | bytes 1048576 | tf_op jit(solution)/shard_map/all_to_all | solution.py:230
  419.9 21.8 %pair_backward.2 = bf16[8,2,3,64,256]{4,3,2,1,0:T(8,128)(2,1)} custom-call(s32[2]{0:T(128)S(1)} %dynamic_slice.102.len_ref, bf16[8,2,1,64,256]{4,3,2,1,0:T(8,128)(2,1)S(1)} %copy-done.3, bf16[8,2,2,64,256]{4,3,2,1,0:T(8,128)(2,1)S(1)} %all-to-all-done.3.k_ref.v_ref, bf16[8,2,2,64,256]{4,3,2,1,0:T(8,128)(2,1)S(1)} %all-to-all-done.3.k_ref.v_ref, ...), custom_call_target="tpu_custom_call" | custom-call | flops 20132659200 | bytes 8388608 | tf_op jit(solution)/shard_map/pair_backward/pallas_call | solution.py:364
  441.6 4.4 all-to-all-start.6
  447.8 23.4 %all-to-all-done.6 = bf16[8,2,3,64,256]{4,3,2,1,0:T(8,128)(2,1)} async-done(((bf16[8,2,3,64,256]{4,3,2,1,0:T(8,128)(2,1)}), bf16[8,2,3,64,256]{4,3,2,1,0:T(8,128)(2,1)}, u32[]{:S(2)}, u32[]{:S(2)}) %all-to-all-start.6) | async-done | bytes 1572896 | tf_op jit(solution)/shard_map/all_to_all | solution.py:230
  473.9 3.0 convolution_convert_fusion.7
  476.8 6.2 collective-permute-start.9
  487.5 2.8 convolution_convert_fusion.8
  492.8 14.3 %collective-permute-done.9 = bf16[512,1024]{1,0:T(8,128)(2,1)S(1)} collective-permute-done((bf16[512,1024]{1,0:T(8,128)(2,1)S(1)}, bf16[512,1024]{1,0:T(8,128)(2,1)S(1)}, u32[]{:S(2)}, u32[]{:S(2)}) %collective-permute-start.9) | collective-permute-done | bytes 1048608 | tf_op jit(solution)/shard_map/ppermute | solution.py:394
  509.3 5.3 collective-permute-done.7
  514.6 3.9 multiply_reduce_fusion
  530.4 3.6 all-to-all-start.7
  534.0 3.2 copy.106
  537.2 6.5 all-to-all-done.7
  543.7 32.1 %pair_backward.3 = bf16[8,2,3,64,256]{4,3,2,1,0:T(8,128)(2,1)} custom-call(s32[2]{0:T(128)S(1)} %copy-done.5, bf16[8,2,3,64,256]{4,3,2,1,0:T(8,128)(2,1)} %all-to-all-done.q_ref.k_ref.v_ref, bf16[8,2,3,64,256]{4,3,2,1,0:T(8,128)(2,1)} %all-to-all-done.q_ref.k_ref.v_ref, bf16[8,2,3,64,256]{4,3,2,1,0:T(8,128)(2,1)} %all-to-all-done.q_ref.k_ref.v_ref, ...), custom_call_target="tpu_custom_call" | custom-call | flops 30198988800 | bytes 8388608 | tf_op jit(solution)/shard_map/pair_backward/pallas_call | solution.py:364
  575.9 3.6 all-to-all-start.8
  579.5 2.8 copy.108
  582.3 65.4 %reduce-scatter.6.cloned.1.call-done = bf16[192,1024]{1,0:T(8,128)(2,1)} async-done(((bf16[3072,1024]{1,0:T(8,128)(2,1)}), bf16[192,1024]{1,0:T(8,128)(2,1)}) %reduce-scatter.6.cloned.1.call-update) | async-done | bytes 393232 | tf_op jit(solution)/shard_map/reduce_scatter | solution.py:568
  650.5 3.5 convolution_convert_fusion
  659.6 4.3 fusion.7
  667.5 11.5 %collective-permute-done.10 = bf16[256,1024]{1,0:T(8,128)(2,1)S(1)} collective-permute-done((bf16[256,1024]{1,0:T(8,128)(2,1)S(1)}, bf16[256,1024]{1,0:T(8,128)(2,1)S(1)}, u32[]{:S(2)}, u32[]{:S(2)}) %collective-permute-start.10) | collective-permute-done | bytes 524320 | tf_op jit(solution)/shard_map/ppermute | solution.py:394
  681.4 44.1 %reduce-scatter.8.cloned.1.call-done = bf16[96,1024]{1,0:T(8,128)(2,1)} async-done(((bf16[1536,1024]{1,0:T(8,128)(2,1)}), bf16[96,1024]{1,0:T(8,128)(2,1)}) %reduce-scatter.8.cloned.1.call-update) | async-done | bytes 196624 | tf_op jit(solution)/shard_map/reduce_scatter | solution.py:568
  725.7 10.1 %all-gather.2 = bf16[16,80,256]{2,1,0:T(8,128)(2,1)S(1)} all-gather(bf16[2,80,256]{2,1,0:T(8,128)(2,1)S(1)} %pad_maximum_fusion.13), channel_id=4, replica_groups=mesh['far'=2,'near'=2,'rows'=8] {'rows'}, dimensions={0}, use_global_device_ids=true | all-gather | bytes 737280 | tf_op jit(solution)/shard_map/all_gather | solution.py:641
  736.1 22.5 %all-gather.20.cloned.1.call-done = bf16[1536,1024]{1,0:T(8,128)(2,1)} async-done(((bf16[192,1024]{1,0:T(8,128)(2,1)}), bf16[1536,1024]{1,0:T(8,128)(2,1)}) %all-gather.20.cloned.1.call-update) | async-done | bytes 3145744 | tf_op jit(solution)/shard_map/all_gather | solution.py:444
  761.0 6.7 slice_convert_fusion
  767.7 5.5 copy.119
  775.8 9.0 %collective-permute-done.11 = bf16[2,128,1024]{2,1,0:T(8,128)(2,1)S(1)} collective-permute-done((bf16[2,128,1024]{2,1,0:T(8,128)(2,1)S(1)}, bf16[2,128,1024]{2,1,0:T(8,128)(2,1)S(1)}, u32[]{:S(2)}, u32[]{:S(2)}) %collective-permute-start.11) | collective-permute-done | bytes 524320 | tf_op jit(solution)/shard_map/ppermute | solution.py:394
  788.7 3.1 slice_convert_fusion.1
  794.9 2.9 copy.117
  797.8 3.5 copy.112
  801.2 3.6 copy.115
  804.9 6.3 collective-permute-done.12
  (362 shorter events, 152.5 us)
Async XLA Ops:
  7.2 204.6 %copy-start = (bf16[4,256,1024]{2,1,0:T(8,128)(2,1)S(1)}, bf16[4,256,1024]{2,1,0:T(8,128)(2,1)}, u32[]{:S(2)}) copy-start(bf16[4,256,1024]{2,1,0:T(8,128)(2,1)} %param.31) | copy-start | bytes 6291460
  7.2 65.5 %all-gather.12.cloned.1.call-start = ((), (), s32[]{:S(2)}) async-start(), calls=%async_computation.12 | async-start | bytes 1769472 | tf_op jit(solution)/shard_map/all_gather | solution.py:444
  10.0 8.4 %copy-start.65 = (s32[4,256]{1,0:T(4,128)S(1)}, s32[4,256]{1,0:T(4,128)}, u32[]{:S(2)}) copy-start(s32[4,256]{1,0:T(4,128)} %param.17) | copy-start | bytes 12292
  12.7 18.1 %copy-start.61 = (bf16[32,2,1024]{2,1,0:T(2,128)(2,1)S(1)}, bf16[32,2,1024]{2,1,0:T(2,128)(2,1)}, u32[]{:S(2)}) copy-start(bf16[32,2,1024]{2,1,0:T(2,128)(2,1)} %param.20) | copy-start | bytes 393220
  12.7 20.0 %copy-start.51 = (bf16[2,1024,256]{2,1,0:T(8,128)(2,1)S(1)}, bf16[2,1024,256]{2,1,0:T(8,128)(2,1)}, u32[]{:S(2)}) copy-start(bf16[2,1024,256]{2,1,0:T(8,128)(2,1)} %param.25) | copy-start | bytes 3145732
  14.4 13.4 %collective-permute-start.2 = (bf16[96,1024]{1,0:T(8,128)(2,1)}, bf16[96,1024]{1,0:T(8,128)(2,1)S(1)}, u32[]{:S(2)}, u32[]{:S(2)}) collective-permute-start(bf16[96,1024]{1,0:T(8,128)(2,1)} %constant_dynamic-slice_fusion.13), channel_id=1, source_target_pairs={{0,16},{16,0},{1,17},{17,1},{2,18},{18,2},{3,19},{19,3},{4,20},{20... | collective-permute-start | bytes 589832 | tf_op jit(solution)/shard_map/ppermute | solution.py:394
  19.9 11.5 %copy-start.62 = (f32[2,256]{1,0:T(2,128)}, f32[2,256]{1,0:T(2,128)S(1)}, u32[]{:S(2)}) copy-start(f32[2,256]{1,0:T(2,128)S(1)} %get-tuple-element.154) | copy-start | bytes 6148
  28.4 149.6 %all-gather.24.cloned.1.call-start = ((), (), s32[]{:S(2)}) async-start(), calls=%async_computation.21 | async-start | bytes 8257536 | tf_op jit(solution)/shard_map/all_gather | solution.py:529
  39.9 38.7 %copy-start.54 = (bf16[512,1024]{1,0:T(8,128)(2,1)}, bf16[512,1024]{1,0:T(8,128)(2,1)S(1)}, u32[]{:S(2)}) copy-start(bf16[512,1024]{1,0:T(8,128)(2,1)S(1)} %get-tuple-element.40) | copy-start | bytes 3145732
  40.7 17.1 %collective-permute-start = (bf16[160,1024]{1,0:T(8,128)(2,1)}, bf16[160,1024]{1,0:T(8,128)(2,1)}, u32[]{:S(2)}, u32[]{:S(2)}) collective-permute-start(bf16[160,1024]{1,0:T(8,128)(2,1)} %pad_maximum_fusion.11), channel_id=1, source_target_pairs={{0,16},{16,0},{1,17},{17,1},{2,18},{18,2},{3,19},{19,3},{4,20},{20... | collective-permute-start | bytes 983048 | tf_op jit(solution)/shard_map/ppermute | solution.py:394
  58.8 9.5 %collective-permute-start.1 = (bf16[2,96,1024]{2,1,0:T(8,128)(2,1)S(1)}, bf16[2,96,1024]{2,1,0:T(8,128)(2,1)S(1)}, u32[]{:S(2)}, u32[]{:S(2)}) collective-permute-start(bf16[2,96,1024]{2,1,0:T(8,128)(2,1)S(1)} %fusion.54), channel_id=1, source_target_pairs={{0,8},{8,0},{1,9},{9,1},{2,10},{10,2},{3,11},{11,3},{4,12},{12,4},... | collective-permute-start | bytes 1179656 | tf_op jit(solution)/shard_map/ppermute | solution.py:394
  82.8 29.8 %all-to-all-start = ((bf16[8,2,3,64,256]{4,3,2,1,0:T(8,128)(2,1)}), bf16[8,2,3,64,256]{4,3,2,1,0:T(8,128)(2,1)}, u32[]{:S(2)}, u32[]{:S(2)}) async-start(bf16[8,2,3,64,256]{4,3,2,1,0:T(8,128)(2,1)} %pad_maximum_fusion.2), calls=%async_computation | async-start | bytes 3145728 | tf_op jit(solution)/shard_map/all_to_all | solution.py:230
  87.2 158.7 %all-gather.26.cloned.1.call-start = ((), (), s32[]{:S(2)}) async-start(), calls=%async_computation.22 | async-start | bytes 4718592 | tf_op jit(solution)/shard_map/all_gather | solution.py:543
  112.6 22.2 %collective-permute-start.5 = (bf16[256,1024]{1,0:T(8,128)(2,1)S(1)}, bf16[256,1024]{1,0:T(8,128)(2,1)S(1)}, u32[]{:S(2)}, u32[]{:S(2)}) collective-permute-start(bf16[256,1024]{1,0:T(8,128)(2,1)S(1)} %pad_maximum_fusion.8), channel_id=1, source_target_pairs={{0,16},{16,0},{1,17},{17,1},{2,18},{18,2},{3,19},{19,3},{4,20},{20... | collective-permute-start | bytes 1572872 | tf_op jit(solution)/shard_map/ppermute | solution.py:394
  135.7 19.0 %copy-start.4 = (s32[2]{0:T(128)}, s32[2]{0:T(128)S(1)}, u32[]{:S(2)}) copy-start(s32[2]{0:T(128)S(1)} %broadcast_13_len_ref.2.len_ref) | copy-start | bytes 28
  155.7 7.0 copy-start.67
  155.7 21.4 %all-to-all-start.1 = ((bf16[8,2,64,256]{3,2,1,0:T(8,128)(2,1)}), bf16[8,2,64,256]{3,2,1,0:T(8,128)(2,1)S(1)}, u32[]{:S(2)}, u32[]{:S(2)}) async-start(bf16[8,2,64,256]{3,2,1,0:T(8,128)(2,1)} %get-tuple-element.42), calls=%async_computation.1 | async-start | bytes 1048576 | tf_op jit(solution)/shard_map/all_to_all | solution.py:230
  177.8 10.8 %copy-start.39 = (bf16[64,8,2,256]{3,1,2,0:T(8,128)(2,1)}, bf16[64,8,2,256]{3,1,2,0:T(8,128)(2,1)S(1)}, u32[]{:S(2)}) copy-start(bf16[64,8,2,256]{3,1,2,0:T(8,128)(2,1)S(1)} %copy.127) | copy-start | bytes 1572868
  177.8 10.8 %collective-permute-start.3 = (bf16[512,512]{1,0:T(8,128)(2,1)S(1)}, bf16[512,512]{1,0:T(8,128)(2,1)S(1)}, u32[]{:S(2)}, u32[]{:S(2)}) collective-permute-start(bf16[512,512]{1,0:T(8,128)(2,1)S(1)} %bitcast.312), channel_id=1, source_target_pairs={{0,8},{8,0},{1,9},{9,1},{2,10},{10,2},{3,11},{11,3},{4,12},{12,4},... | collective-permute-start | bytes 1572872 | tf_op jit(solution)/shard_map/ppermute | solution.py:394
  194.1 13.2 %all-to-all-start.2 = ((bf16[8,2,1,64,256]{4,3,2,1,0:T(8,128)(2,1)}), bf16[8,2,1,64,256]{4,3,2,1,0:T(8,128)(2,1)S(1)}, u32[]{:S(2)}, u32[]{:S(2)}) async-start(bf16[8,2,1,64,256]{4,3,2,1,0:T(8,128)(2,1)} %pad_maximum_fusion.7), calls=%async_computation.2 | async-start | bytes 1048576 | tf_op jit(solution)/shard_map/all_to_all | solution.py:230
  204.7 7.0 copy-start.71
  204.7 7.1 copy-start.68
  208.1 18.9 %all-to-all-start.3 = ((bf16[8,2,2,64,256]{4,3,2,1,0:T(8,128)(2,1)}), bf16[8,2,2,64,256]{4,3,2,1,0:T(8,128)(2,1)S(1)}, u32[]{:S(2)}, u32[]{:S(2)}) async-start(bf16[8,2,2,64,256]{4,3,2,1,0:T(8,128)(2,1)} %pad_maximum_fusion.3), calls=%async_computation.3 | async-start | bytes 2097152 | tf_op jit(solution)/shard_map/all_to_all | solution.py:230
  218.1 8.9 %copy-start.3 = (bf16[8,2,1,64,256]{4,3,2,1,0:T(8,128)(2,1)S(1)}, bf16[8,2,1,64,256]{4,3,2,1,0:T(8,128)(2,1)}, u32[]{:S(2)}) copy-start(bf16[8,2,1,64,256]{4,3,2,1,0:T(8,128)(2,1)} %copy-done.2) | copy-start | bytes 1572868
  241.4 13.9 %all-to-all-start.4 = ((bf16[8,2,64,256]{3,2,1,0:T(8,128)(2,1)}), bf16[8,2,64,256]{3,2,1,0:T(8,128)(2,1)}, u32[]{:S(2)}, u32[]{:S(2)}) async-start(bf16[8,2,64,256]{3,2,1,0:T(8,128)(2,1)} %get-tuple-element.43), calls=%async_computation.4 | async-start | bytes 1048576 | tf_op jit(solution)/shard_map/all_to_all | solution.py:230
  245.6 156.0 %reduce-scatter.4.cloned.1.call-start = ((), (), s32[]{:S(2)}) async-start(), calls=%async_computation.13 | async-start | bytes 8912896 | tf_op jit(solution)/shard_map/reduce_scatter | solution.py:568
  257.1 12.1 %copy-start.57 = (bf16[64,8,2,256]{3,1,2,0:T(8,128)(2,1)}, bf16[64,8,2,256]{3,1,2,0:T(8,128)(2,1)S(1)}, u32[]{:S(2)}) copy-start(bf16[64,8,2,256]{3,1,2,0:T(8,128)(2,1)S(1)} %copy.128) | copy-start | bytes 1572868
  257.1 12.1 %collective-permute-start.4 = (bf16[512,512]{1,0:T(8,128)(2,1)S(1)}, bf16[512,512]{1,0:T(8,128)(2,1)S(1)}, u32[]{:S(2)}, u32[]{:S(2)}) collective-permute-start(bf16[512,512]{1,0:T(8,128)(2,1)S(1)} %bitcast.346), channel_id=1, source_target_pairs={{0,8},{8,0},{1,9},{9,1},{2,10},{10,2},{3,11},{11,3},{4,12},{12,4},... | collective-permute-start | bytes 1572872 | tf_op jit(solution)/shard_map/ppermute | solution.py:394
  259.0 4.7 copy-start.17
  263.7 5.5 copy-start.9
  270.6 5.7 copy-start.11
  276.2 4.7 copy-start.74
  276.3 4.7 copy-start.75
  294.1 239.9 %all-gather.16.cloned.1.call-start = ((), (), s32[]{:S(2)}) async-start(), calls=%async_computation.15 | async-start | bytes 2621440 | tf_op jit(solution)/shard_map/all_gather | solution.py:479
  302.4 19.2 %collective-permute-start.8 = (bf16[256,1024]{1,0:T(8,128)(2,1)}, bf16[256,1024]{1,0:T(8,128)(2,1)}, u32[]{:S(2)}, u32[]{:S(2)}) collective-permute-start(bf16[256,1024]{1,0:T(8,128)(2,1)} %bitcast.55), channel_id=1, source_target_pairs={{0,8},{8,0},{1,9},{9,1},{2,10},{10,2},{3,11},{11,3},{4,12},{12,4},... | collective-permute-start | bytes 1572872 | tf_op jit(solution)/shard_map/ppermute | solution.py:394
  323.8 219.9 %all-gather.14.cloned.1.call-start = ((), (), s32[]{:S(2)}) async-start(), calls=%async_computation.14 | async-start | bytes 4718592 | tf_op jit(solution)/shard_map/all_gather | solution.py:444
  323.8 5.8 copy-start.36
  329.2 38.3 %copy-start.25 = (bf16[512,1024]{1,0:T(8,128)(2,1)}, bf16[512,1024]{1,0:T(8,128)(2,1)S(1)}, u32[]{:S(2)}) copy-start(bf16[512,1024]{1,0:T(8,128)(2,1)S(1)} %convolution_convert_fusion.11) | copy-start | bytes 3145732
  329.2 37.3 %copy-start.13 = (f32[512,1024]{1,0:T(8,128)S(1)}, f32[512,1024]{1,0:T(8,128)}, u32[]{:S(2)}) copy-start(f32[512,1024]{1,0:T(8,128)} %copy-done.11) | copy-start | bytes 6291460
  329.2 37.3 %collective-permute-start.6 = (bf16[512,1024]{1,0:T(8,128)(2,1)S(1)}, bf16[512,1024]{1,0:T(8,128)(2,1)S(1)}, u32[]{:S(2)}, u32[]{:S(2)}) collective-permute-start(bf16[512,1024]{1,0:T(8,128)(2,1)S(1)} %convolution_convert_fusion.11), channel_id=1, source_target_pairs={{0,8},{8,0},{1,9},{9,1},{2,10},{10,2},{3,11},{11,3},{4,12},{12,4},... | collective-permute-start | bytes 3145736 | tf_op jit(solution)/shard_map/ppermute | solution.py:394
  401.6 4.9 copy-start.53
  441.6 29.5 %all-to-all-start.6 = ((bf16[8,2,3,64,256]{4,3,2,1,0:T(8,128)(2,1)}), bf16[8,2,3,64,256]{4,3,2,1,0:T(8,128)(2,1)}, u32[]{:S(2)}, u32[]{:S(2)}) async-start(bf16[8,2,3,64,256]{4,3,2,1,0:T(8,128)(2,1)} %pair_backward.2), calls=%async_computation.6 | async-start | bytes 3145728 | tf_op jit(solution)/shard_map/all_to_all | solution.py:230
  446.1 133.4 %all-gather.18.cloned.1.call-start = ((), (), s32[]{:S(2)}) async-start(), calls=%async_computation.17 | async-start | bytes 1966080 | tf_op jit(solution)/shard_map/all_gather | solution.py:479
  473.8 9.2 %copy-start.48 = (bf16[512,1024]{1,0:T(8,128)(2,1)S(1)}, bf16[512,1024]{1,0:T(8,128)(2,1)}, u32[]{:S(2)}) copy-start(bf16[512,1024]{1,0:T(8,128)(2,1)} %copy-done.47) | copy-start | bytes 3145732
  473.8 9.2 %copy-start.58 = (bf16[64,8,2,256]{3,1,2,0:T(8,128)(2,1)S(1)}, bf16[64,8,2,256]{3,1,2,0:T(8,128)(2,1)}, u32[]{:S(2)}) copy-start(bf16[64,8,2,256]{3,1,2,0:T(8,128)(2,1)} %copy-done.57) | copy-start | bytes 1572868
  476.8 30.3 %collective-permute-start.9 = (bf16[512,1024]{1,0:T(8,128)(2,1)S(1)}, bf16[512,1024]{1,0:T(8,128)(2,1)S(1)}, u32[]{:S(2)}, u32[]{:S(2)}) collective-permute-start(bf16[512,1024]{1,0:T(8,128)(2,1)S(1)} %convolution_convert_fusion.7), channel_id=1, source_target_pairs={{0,8},{8,0},{1,9},{9,1},{2,10},{10,2},{3,11},{11,3},{4,12},{12,4},... | collective-permute-start | bytes 3145736 | tf_op jit(solution)/shard_map/ppermute | solution.py:394
  487.5 27.1 %collective-permute-start.7 = (bf16[512,512]{1,0:T(8,128)(2,1)}, bf16[512,512]{1,0:T(8,128)(2,1)}, u32[]{:S(2)}, u32[]{:S(2)}) collective-permute-start(bf16[512,512]{1,0:T(8,128)(2,1)} %bitcast.152), channel_id=1, source_target_pairs={{0,8},{8,0},{1,9},{9,1},{2,10},{10,2},{3,11},{11,3},{4,12},{12,4},... | collective-permute-start | bytes 1572872 | tf_op jit(solution)/shard_map/ppermute | solution.py:394
  492.8 14.8 %copy-start.70 = (bf16[768,1024]{1,0:T(8,128)(2,1)S(1)}, bf16[768,1024]{1,0:T(8,128)(2,1)}, u32[]{:S(2)}) copy-start(bf16[768,1024]{1,0:T(8,128)(2,1)} %param.27) | copy-start | bytes 4718596
  507.6 7.1 copy-start.10
  509.0 138.6 %reduce-scatter.6.cloned.1.call-start = ((), (), s32[]{:S(2)}) async-start(), calls=%async_computation.16 | async-start | bytes 6684672 | tf_op jit(solution)/shard_map/reduce_scatter | solution.py:568
  530.4 13.3 %all-to-all-start.7 = ((bf16[8,2,1,64,256]{4,3,1,2,0:T(8,128)(2,1)}), bf16[8,2,1,64,256]{4,3,1,2,0:T(8,128)(2,1)S(1)}, u32[]{:S(2)}, u32[]{:S(2)}) async-start(bf16[8,2,1,64,256]{4,3,1,2,0:T(8,128)(2,1)} %pad_maximum_fusion.10), calls=%async_computation.7 | async-start | bytes 1048576 | tf_op jit(solution)/shard_map/all_to_all | solution.py:230
  534.0 9.7 %copy-start.5 = (s32[2]{0:T(128)S(1)}, s32[2]{0:T(128)}, u32[]{:S(2)}) copy-start(s32[2]{0:T(128)} %copy-done.4) | copy-start | bytes 28
  534.0 9.7 %copy-start.7 = (f32[8,2,64,256]{3,2,1,0:T(8,128)S(1)}, f32[8,2,64,256]{3,2,1,0:T(8,128)}, u32[]{:S(2)}) copy-start(f32[8,2,64,256]{3,2,1,0:T(8,128)} %copy-done.6) | copy-start | bytes 3145732
  575.9 71.8 %all-to-all-start.8 = ((bf16[8,2,3,64,256]{4,3,2,1,0:T(8,128)(2,1)}), bf16[8,2,3,64,256]{4,3,2,1,0:T(8,128)(2,1)S(1)}, u32[]{:S(2)}, u32[]{:S(2)}) async-start(bf16[8,2,3,64,256]{4,3,2,1,0:T(8,128)(2,1)} %pair_backward.3), calls=%async_computation.9 | async-start | bytes 3145728 | tf_op jit(solution)/shard_map/all_to_all | solution.py:230
  579.5 146.0 %reduce-scatter.8.cloned.1.call-start = ((), (), s32[]{:S(2)}) async-start(), calls=%async_computation.19 | async-start | bytes 3342336 | tf_op jit(solution)/shard_map/reduce_scatter | solution.py:568
  654.1 104.5 %all-gather.20.cloned.1.call-start = ((), (), s32[]{:S(2)}) async-start(), calls=%async_computation.18 | async-start | bytes 3538944 | tf_op jit(solution)/shard_map/all_gather | solution.py:444
  654.6 143.1 %all-gather.22.cloned.1.call-start = ((), (), s32[]{:S(2)}) async-start(), calls=%async_computation.20 | async-start | bytes 1769472 | tf_op jit(solution)/shard_map/all_gather | solution.py:444
  665.3 13.7 %collective-permute-start.10 = (bf16[256,1024]{1,0:T(8,128)(2,1)S(1)}, bf16[256,1024]{1,0:T(8,128)(2,1)S(1)}, u32[]{:S(2)}, u32[]{:S(2)}) collective-permute-start(bf16[256,1024]{1,0:T(8,128)(2,1)S(1)} %bitcast.349), channel_id=1, source_target_pairs={{0,8},{8,0},{1,9},{9,1},{2,10},{10,2},{3,11},{11,3},{4,12},{12,4},... | collective-permute-start | bytes 1572872 | tf_op jit(solution)/shard_map/ppermute | solution.py:394
  680.3 45.2 %collective-permute-start.13 = (bf16[64,1024]{1,0:T(8,128)(2,1)S(1)}, bf16[64,1024]{1,0:T(8,128)(2,1)S(1)}, u32[]{:S(2)}, u32[]{:S(2)}) collective-permute-start(bf16[64,1024]{1,0:T(8,128)(2,1)S(1)} %pad_maximum_fusion.12), channel_id=1, source_target_pairs={{0,8},{8,0},{1,9},{9,1},{2,10},{10,2},{3,11},{11,3},{4,12},{12,4},... | collective-permute-start | bytes 393224 | tf_op jit(solution)/shard_map/ppermute | solution.py:394
  735.9 39.2 %collective-permute-start.14 = (bf16[80,256]{1,0:T(8,128)(2,1)S(1)}, bf16[80,256]{1,0:T(8,128)(2,1)S(1)}, u32[]{:S(2)}, u32[]{:S(2)}) collective-permute-start(bf16[80,256]{1,0:T(8,128)(2,1)S(1)} %dynamic-slice_bitcast_fusion), channel_id=1, source_target_pairs={{0,16},{16,0},{1,17},{17,1},{2,18},{18,2},{3,19},{19,3},{4,20},{20... | collective-permute-start | bytes 122888 | tf_op jit(solution)/shard_map/ppermute | solution.py:394
  758.6 26.2 %collective-permute-start.11 = (bf16[2,128,1024]{2,1,0:T(8,128)(2,1)S(1)}, bf16[2,128,1024]{2,1,0:T(8,128)(2,1)S(1)}, u32[]{:S(2)}, u32[]{:S(2)}) collective-permute-start(bf16[2,128,1024]{2,1,0:T(8,128)(2,1)S(1)} %bitcast.320), channel_id=1, source_target_pairs={{0,16},{16,0},{1,17},{17,1},{2,18},{18,2},{3,19},{19,3},{4,20},{20... | collective-permute-start | bytes 1572872 | tf_op jit(solution)/shard_map/ppermute | solution.py:394
  767.7 5.5 copy-start.22
  786.3 24.8 %collective-permute-start.12 = (bf16[2,2,128,1024]{3,2,1,0:T(8,128)(2,1)}, bf16[2,2,128,1024]{3,2,1,0:T(8,128)(2,1)}, u32[]{:S(2)}, u32[]{:S(2)}) collective-permute-start(bf16[2,2,128,1024]{3,2,1,0:T(8,128)(2,1)} %get-tuple-element.146), channel_id=1, source_target_pairs={{0,8},{8,0},{1,9},{9,1},{2,10},{10,2},{3,11},{11,3},{4,12},{12,4},... | collective-permute-start | bytes 3145736 | tf_op jit(solution)/shard_map/ppermute | solution.py:394
  801.2 9.9 %copy-start.34 = (bf16[1,2,2,128,1024]{4,3,0,2,1:T(8,128)(2,1)S(1)}, bf16[1,2,2,128,1024]{4,3,0,2,1:T(8,128)(2,1)}, u32[]{:S(2)}) copy-start(bf16[1,2,2,128,1024]{4,3,0,2,1:T(8,128)(2,1)} %get-tuple-element.145) | copy-start | bytes 3145732
  (47 other events, 96.3 us)
Sparse Core Ops, SparseCore 0:
  28.5 26.8 all-gather.11
  69.4 59.4 all-gather.23
  135.8 44.7 all-gather.25
  294.2 107.4 reduce-scatter.3
  403.6 48.0 all-gather.15
  453.5 41.9 all-gather.13
  509.1 36.7 all-gather.17
  550.3 97.2 reduce-scatter.5
  654.2 71.2 reduce-scatter.7
  727.4 31.1 all-gather.19
  760.6 25.6 all-gather.21

commit v5 on v4

--- a/solution.py
+++ b/solution.py
@@ -467,18 +467,13 @@
         mine, away = halves(partial)
         return mine + swap(away.astype(LOW), "near").astype(WIDE)
 
-    def swap_over_heads(value):
+    def over_heads(value):
         value = value.reshape(objects, rows // 2, -1)
         value = jnp.stack([value, swap(value, "far")])
         value = jnp.stack([value, swap(value, "near")])
         value = jnp.where(far == 0, value, jnp.flip(value, 1))
         value = jnp.where(near == 0, value, jnp.flip(value, 0))
         return value.transpose(1, 2, 0, 3, 4).reshape(2 * objects, rows, -1)
-
-    def over_heads(value):
-        value = lax.all_gather(value.reshape(objects, rows // 2, -1), ("far", "near"), axis=0)
-        value = value.reshape(2, 2, objects, rows // 2, -1).transpose(0, 2, 1, 3, 4)
-        return value.reshape(2 * objects, rows, -1)
 
     def to_pairs(weights, value, slots):
         parts = [
@@ -539,11 +534,12 @@
 
     mine = [piece(widen_weights), piece(narrow_weights)]
     qkv, *mine = tie(qkv, *mine)
-    across = swap(jnp.concatenate(mine, axis=0), "far")
-    sent = lax.all_gather(across, "rows", axis=0)
     size = width // n_rows
-    widen = in_order(widen_weights, sent[:, :size].reshape(width, hidden), axis=1)
-    narrow = in_order(narrow_weights, sent[:, size:].reshape(hidden, width))
+    sent = lax.all_gather(jnp.concatenate(mine, axis=0), ("far", "rows"), axis=0)
+    sent = sent.reshape(2, n_rows, 2, size, width)
+    widen = sent[:, :, 0].reshape(2, width, hidden)
+    widen = jnp.concatenate([widen[0], widen[1]], axis=1)
+    narrow = sent[:, :, 1].reshape(2 * hidden, width)
 
     mixed, self_wide, self_log = pair_forward(qkv, qkv, 1)
     self_mixed_t = from_pairs(exchange_rows(mixed)[:, :, None])
@@ -564,20 +560,26 @@
     result = (halves(after_cross)[0] + hidden_half).astype(LOW)
 
     def part_rows(both):
-        both = both.reshape(-1, both.shape[-1])
-        return lax.psum_scatter(both, ("far", "rows"), scatter_dimension=0, tiled=True)
+        return lax.psum_scatter(both, "rows", scatter_dimension=1, tiled=True)
+
+    def own_and_away(value):
+        return [lax.dynamic_index_in_dim(value, index, 0, keepdims=False) for index in (far, 1 - far)]
+
+    def add_far(mine, away):
+        return (mine.astype(WIDE) + away.astype(WIDE)).astype(LOW)
 
     def by_shard(left, right):
         return mul(left, right, NN).astype(LOW).reshape(2, -1, right.shape[1])
 
-    hidden_part = part_rows(
-        jnp.concatenate(
-            [
-                mul(value, against, TN).astype(LOW).reshape(2, hidden, width)
-                for value, against in ((activated, grad_low), (grad_pre, normed_three))
-            ],
-            axis=1,
-        )
+    hidden_terms = jnp.concatenate(
+        [
+            mul(value, against, TN).astype(LOW).reshape(2, hidden, width)
+            for value, against in ((activated, grad_low), (grad_pre, normed_three))
+        ],
+        axis=1,
+    )
+    hidden_part = lax.psum_scatter(
+        hidden_terms.reshape(-1, width), ("far", "rows"), scatter_dimension=0, tiled=True
     )
 
     hidden_gain_term = jnp.sum(grad_three * unit_three, axis=0)
@@ -587,9 +589,9 @@
     grad_cross_low = grad_cross.astype(LOW)
     grad_mixed = to_pairs(cross_whole[: 2 * cols], grad_cross_low, 1)[:, :, 0]
     grads = pair_backward(cross_q, pair, 0, length, grad_mixed, cross_wide, cross_log)
+    grads, hidden_part = tie(grads, hidden_part)
     grads = exchange_rows(grads)
     hidden_total = join_rows(hidden_part)
-    outputs = over_heads(result)
     grad_cq_t = from_pairs(grads[:, :, :1])
     grad_pair_t = from_pairs(grads[:, :, 1:])
     grad_two = over_all_columns(grad_cq_t, query_whole)
@@ -615,11 +617,11 @@
         )
     )
     grad_mixed = to_pairs(self_whole[: 2 * cols], grad_self_low, 1)[:, :, 0]
-    grad_mixed, hidden_total, outputs = tie(grad_mixed, hidden_total, outputs)
-    grads = exchange_rows(pair_backward(qkv, qkv, 1, None, grad_mixed, self_wide, self_log))
-    patch_grads = over_heads(patch_half)
-    grads, middle_part, patch_grads = tie(grads, middle_part, patch_grads)
-    middle_total = join_rows(middle_part)
+    grads = pair_backward(qkv, qkv, 1, None, grad_mixed, self_wide, self_log)
+    grads, hidden_total, middle_part = tie(grads, hidden_total, middle_part)
+    grads = exchange_rows(grads)
+    middle_own, middle_away = own_and_away(middle_part)
+    middle_total = join_rows(add_far(middle_own, swap(middle_away, "far")))
     grad_qkv_t = from_pairs(grads)
     last_part = part_rows(by_shard(grad_qkv_t, normed_one))
     grad_one = half_sum_near(mul(grad_qkv_t, qkv_both, TN))
@@ -644,8 +646,11 @@
     )
     small = small_own.astype(WIDE) + swap(small_away, "far").astype(WIDE)
     input_half, middle_total = tie(input_half, middle_total)
-    input_grads = swap_over_heads(input_half)
-    last_total = join_rows(last_part)
+    input_grads = over_heads(input_half)
+    outputs = over_heads(result)
+    patch_grads = over_heads(patch_half)
+    last_own, last_away = own_and_away(last_part)
+    last_total = join_rows(add_far(last_own, swap(last_away, "far")))
 
     output_total = middle_total[: 2 * cols]
     query_total = middle_total[2 * cols : 3 * cols]

time: 836 us -> 804 us (0.962)
  waiting for transfers between devices: 395 us -> 315 us
  blocking collectives: 22.4 us -> 87.7 us
  local copies, waits for them, and re-layouts: 117 us -> 105 us
  other arithmetic: 56.6 us -> 66 us
    reduce_scatter x3, waiting for transfers between devices: 144 us -> 25.8 us  [the longest x2 15.2 us: part_rows(): return lax.psum_scatter(both, 'rows', scatter_dimension=1, tiled=True)]
    all_to_all x1 -> x4, blocking collectives: 12.3 us -> 77 us  [exchange_rows(): return lax.all_to_all(value, 'rows', 0, 0, tiled=True)]
    ppermute x15 -> x20, waiting for transfers between devices: 154 us -> 215 us  [swap(): return lax.ppermute(value, axis, [(0, 1), (1, 0)])]
    all_gather x4, waiting for transfers between devices: 22.5 us -> 0.03 us  [join_rows(): return lax.all_gather(value, 'rows', axis=0, tiled=True)]
    all_to_all x8 -> x5, starting transfers between devices: 32.8 us -> 23.3 us  [exchange_rows(): return lax.all_to_all(value, 'rows', 0, 0, tiled=True)]
    ppermute x15 -> x20, starting transfers between devices: 19.7 us -> 28.9 us  [swap(): return lax.ppermute(value, axis, [(0, 1), (1, 0)])]
    unnamed x175 -> x169, local copies, waits for them, and re-layouts: 43.5 us -> 45.4 us
    all_to_all x8 -> x5, waiting for transfers between devices: 74.7 us -> 73.9 us  [exchange_rows(): return lax.all_to_all(value, 'rows', 0, 0, tiled=True)]
  transfers between devices with their start and end apart: 34 -> 34, of which waited for: 23 -> 24; matrix products, arithmetic and copies ran while one was open for 23% -> 22% of each run, Pallas kernels for 11% -> 11%
where the time goes in v5:
time: 804 us; the launch traced here: 796 us
  waiting for transfers between devices  315 us (39%)
  local copies, waits for them, and re-layouts  105 us (13%)
  blocking collectives  87.7 us (11%)
  Pallas kernels  85.8 us (11%)
  matrix products  67.6 us (8%)
  other arithmetic  66 us (8%)
  starting transfers between devices  52.9 us (7%)
  between operations  15.7 us (2%)
    ppermute x20, waiting for transfers between devices, swap(): return lax.ppermute(value, axis, [(0, 1), (1, 0)])  215 us
    all_to_all x4, blocking collectives, exchange_rows(): return lax.all_to_all(value, 'rows', 0, 0, tiled=True)  77 us
    all_to_all x5, waiting for transfers between devices, exchange_rows(): return lax.all_to_all(value, 'rows', 0, 0, tiled=True)  73.9 us
    dot_general x31, matrix products, mul(): return lax.dot_general(left, right, dims, preferred_element_type=WIDE)  66.5 us
    pallas_call x2, Pallas kernels, pair_backward(): pl.pallas_call(kernel, grid_spec=pltpu.PrefetchScalarGridSpec(num_scalar_...  53.2 us
    unnamed x169, local copies, waits for them, and re-layouts  45.4 us
    pallas_call x2, Pallas kernels, pair_forward(): pl.pallas_call(kernel, grid_spec=pltpu.PrefetchScalarGridSpec(num_scalar_...  32.6 us
    ppermute x20, starting transfers between devices, swap(): return lax.ppermute(value, axis, [(0, 1), (1, 0)])  28.9 us
  transfers between devices with their start and end apart: 34, of which 24 were waited for; matrix products, arithmetic and copies ran while one was open for 22% of the time, Pallas kernels for 11%

profile of v5, /device:TPU:0, one launch (start us, length us, event | category | flops | bytes accessed | tf_op | source)
XLA Modules:
  0.0 795.9 jit_solution(3631161899195425072)
XLA Ops:
  7.2 2.7 copy.96
  10.0 2.7 copy.97
  14.4 4.0 collective-permute-start
  19.9 7.8 collective-permute-done
  40.8 17.1 %collective-permute-done.2 = bf16[160,1024]{1,0:T(8,128)(2,1)} collective-permute-done((bf16[160,1024]{1,0:T(8,128)(2,1)}, bf16[160,1024]{1,0:T(8,128)(2,1)}, u32[]{:S(2)}, u32[]{:S(2)}) %collective-permute-start.2) | collective-permute-done | bytes 327712 | tf_op jit(solution)/shard_map/ppermute | solution.py:394
  59.8 8.5 %collective-permute-done.3 = bf16[2,96,1024]{2,1,0:T(8,128)(2,1)S(1)} collective-permute-done((bf16[2,96,1024]{2,1,0:T(8,128)(2,1)S(1)}, bf16[2,96,1024]{2,1,0:T(8,128)(2,1)S(1)}, u32[]{:S(2)}, u32[]{:S(2)}) %collective-permute-start.3) | collective-permute-done | bytes 393248 | tf_op jit(solution)/shard_map/ppermute | solution.py:394
  75.3 3.2 convolution_convert_fusion.3
  78.6 2.9 convolution_convert_fusion.4
  82.8 4.3 all-to-all-start
  88.3 24.2 %all-to-all-done.q_ref.k_ref.v_ref = bf16[8,2,3,64,256]{4,3,2,1,0:T(8,128)(2,1)} async-done(((bf16[8,2,3,64,256]{4,3,2,1,0:T(8,128)(2,1)}), bf16[8,2,3,64,256]{4,3,2,1,0:T(8,128)(2,1)}, u32[]{:S(2)}, u32[]{:S(2)}) %all-to-all-start) | async-done | bytes 1572896 | tf_op jit(solution)/shard_map/all_to_all | solution.py:230
  113.4 3.3 dynamic-slice_convert_fusion.2
  116.6 19.0 %pair_forward.2 = (bf16[8,2,64,256]{3,2,1,0:T(8,128)(2,1)}, f32[8,2,64,256]{3,2,1,0:T(8,128)S(1)}, f32[8,2,1,256]{3,2,1,0:T(1,128)S(1)}) custom-call(s32[2]{0:T(128)S(1)} %broadcast_13_len_ref.2.len_ref, bf16[8,2,3,64,256]{4,3,2,1,0:T(8,128)(2,1)} %all-to-all-done.q_ref.k_ref.v_ref, bf16[8,2,3,64,256]{4,3,2,1,0:T(8,128)(2,1)} %all-to-all-done.q_ref.k_ref.v_ref, ...), custom_call_target="tpu_custom_call" | custom-call | flops 20132659200 | bytes 8388608 | tf_op jit(solution)/shard_map/pair_forward/pallas_call | solution.py:282
  136.6 4.5 all-to-all-start.1
  147.3 5.6 all-to-all-done.1
  156.9 3.8 slice.168
  164.7 2.7 fusion.79
  167.6 5.7 collective-permute-done.1
  179.0 5.7 all-to-all-start.2
  192.9 7.5 all-to-all-done.2.q_ref
  201.2 3.6 all-to-all-start.3
  204.9 15.2 %all-to-all-done.3.k_ref.v_ref = bf16[8,2,2,64,256]{4,3,2,1,0:T(8,128)(2,1)S(1)} async-done(((bf16[8,2,2,64,256]{4,3,2,1,0:T(8,128)(2,1)}), bf16[8,2,2,64,256]{4,3,2,1,0:T(8,128)(2,1)S(1)}, u32[]{:S(2)}, u32[]{:S(2)}) %all-to-all-start.3) | async-done | bytes 1048608 | tf_op jit(solution)/shard_map/all_to_all | solution.py:230
  221.1 13.7 %pair_forward.3 = (bf16[8,2,64,256]{3,2,1,0:T(8,128)(2,1)S(1)}, f32[8,2,64,256]{3,2,1,0:T(8,128)S(1)}, f32[8,2,1,256]{3,2,1,0:T(1,128)S(1)}) custom-call(s32[2]{0:T(128)S(1)} %dynamic_slice.115.len_ref, bf16[8,2,1,64,256]{4,3,2,1,0:T(8,128)(2,1)S(1)} %copy-done.3, bf16[8,2,2,64,256]{4,3,2,1,0:T(8,128)(2,1)S(1)} %all-to-all-done.3.k_ref.v_ref, ...), custom_call_target="tpu_custom_call" | custom-call | flops 14092861440 | bytes 8388608 | tf_op jit(solution)/shard_map/pair_forward/pallas_call | solution.py:282
  234.9 12.3 %all_to_all.45 = bf16[8,2,64,256]{3,2,1,0:T(8,128)(2,1)S(1)} all-to-all(bf16[8,2,64,256]{3,2,1,0:T(8,128)(2,1)S(1)} %get-tuple-element.42), channel_id=1, replica_groups=mesh['far'=2,'near'=2,'rows'=8] {'rows'}, dimensions={0} | all-to-all | bytes 1048576 | tf_op jit(solution)/shard_map/all_to_all | solution.py:230
  250.1 10.8 %collective-permute-done.4 = bf16[512,512]{1,0:T(8,128)(2,1)S(1)} collective-permute-done((bf16[512,512]{1,0:T(8,128)(2,1)S(1)}, bf16[512,512]{1,0:T(8,128)(2,1)S(1)}, u32[]{:S(2)}, u32[]{:S(2)}) %collective-permute-start.4) | collective-permute-done | bytes 524320 | tf_op jit(solution)/shard_map/ppermute | solution.py:394
  263.9 2.8 slice.177
  273.3 5.2 fusion.6
  278.5 5.0 convolution_convert_fusion.1
  283.5 4.4 convolution_convert_fusion.2
  287.9 7.8 pad_maximum_fusion
  295.8 5.3 fusion.21
  302.2 33.8 %collective-permute-done.8 = bf16[512,1024]{1,0:T(8,128)(2,1)S(1)} collective-permute-done((bf16[512,1024]{1,0:T(8,128)(2,1)S(1)}, bf16[512,1024]{1,0:T(8,128)(2,1)S(1)}, u32[]{:S(2)}, u32[]{:S(2)}) %collective-permute-start.8) | collective-permute-done | bytes 1048608 | tf_op jit(solution)/shard_map/ppermute | solution.py:394
  340.3 26.8 %all_to_all.46 = bf16[8,2,1,64,256]{4,3,1,2,0:T(8,128)(2,1)S(1)} all-to-all(bf16[8,2,1,64,256]{4,3,1,2,0:T(8,128)(2,1)S(1)} %pad_maximum_fusion.18), channel_id=1, replica_groups=mesh['far'=2,'near'=2,'rows'=8] {'rows'}, dimensions={0} | all-to-all | bytes 1048576 | tf_op jit(solution)/shard_map/all_to_all | solution.py:230
  367.1 21.8 %pair_backward.2 = bf16[8,2,3,64,256]{4,3,2,1,0:T(8,128)(2,1)} custom-call(s32[2]{0:T(128)S(1)} %dynamic_slice.115.len_ref, bf16[8,2,1,64,256]{4,3,2,1,0:T(8,128)(2,1)S(1)} %copy-done.4, bf16[8,2,2,64,256]{4,3,2,1,0:T(8,128)(2,1)S(1)} %all-to-all-done.3.k_ref.v_ref, bf16[8,2,2,64,256]{4,3,2,1,0:T(8,128)(2,1)S(1)} %all-to-all-done.3.k_ref.v_ref, ...), custom_call_target="tpu_custom_call" | custom-call | flops 20132659200 | bytes 8388608 | tf_op jit(solution)/shard_map/pair_backward/pallas_call | solution.py:364
  388.9 10.6 %reduce-scatter.4.cloned.1.call-done = bf16[256,1024]{1,0:T(8,128)(2,1)} async-done(((bf16[4096,1024]{1,0:T(8,128)(2,1)}), bf16[256,1024]{1,0:T(8,128)(2,1)}) %reduce-scatter.4.cloned.1.call-update) | async-done | bytes 524304 | tf_op jit(solution)/shard_map/reduce_scatter | solution.py:581
  399.5 5.3 all-to-all-start.6
  405.0 3.3 copy.112
  410.1 21.4 %all-to-all-done.6 = bf16[8,2,3,64,256]{4,3,2,1,0:T(8,128)(2,1)} async-done(((bf16[8,2,3,64,256]{4,3,2,1,0:T(8,128)(2,1)}), bf16[8,2,3,64,256]{4,3,2,1,0:T(8,128)(2,1)}, u32[]{:S(2)}, u32[]{:S(2)}) %all-to-all-start.6) | async-done | bytes 1572896 | tf_op jit(solution)/shard_map/all_to_all | solution.py:230
  437.5 3.0 convolution_convert_fusion.7
  443.0 7.8 collective-permute-done.9
  460.4 9.2 %collective-permute-done.10 = bf16[512,1024]{1,0:T(8,128)(2,1)S(1)} collective-permute-done((bf16[512,1024]{1,0:T(8,128)(2,1)S(1)}, bf16[512,1024]{1,0:T(8,128)(2,1)S(1)}, u32[]{:S(2)}, u32[]{:S(2)}) %collective-permute-start.10) | collective-permute-done | bytes 1048608 | tf_op jit(solution)/shard_map/ppermute | solution.py:394
  474.5 14.3 %all_to_all.47 = bf16[8,2,1,64,256]{4,3,1,2,0:T(8,128)(2,1)S(1)} all-to-all(bf16[8,2,1,64,256]{4,3,1,2,0:T(8,128)(2,1)S(1)} %pad_maximum_fusion.19), channel_id=1, replica_groups=mesh['far'=2,'near'=2,'rows'=8] {'rows'}, dimensions={0} | all-to-all | bytes 1048576 | tf_op jit(solution)/shard_map/all_to_all | solution.py:230
  488.8 31.4 %pair_backward.3 = bf16[8,2,3,64,256]{4,3,2,1,0:T(8,128)(2,1)S(1)} custom-call(s32[2]{0:T(128)S(1)} %broadcast_13_len_ref.2.len_ref, bf16[8,2,3,64,256]{4,3,2,1,0:T(8,128)(2,1)} %all-to-all-done.q_ref.k_ref.v_ref, bf16[8,2,3,64,256]{4,3,2,1,0:T(8,128)(2,1)} %all-to-all-done.q_ref.k_ref.v_ref, bf16[8,2,3,64,256]{4,3,2,1,0:T(8,128)(2,1)} %all-to-all-done.q_ref.k_ref.v_ref, ...), custom_call_target="tpu_custom_call" | custom-call | flops 30198988800 | bytes 8388608 | tf_op jit(solution)/shard_map/pair_backward/pallas_call | solution.py:364
  520.2 15.2 %reduce-scatter.6.cloned.1.call-done = bf16[2,192,1024]{2,1,0:T(8,128)(2,1)} async-done(((bf16[2,1536,1024]{2,1,0:T(8,128)(2,1)}), bf16[2,192,1024]{2,1,0:T(8,128)(2,1)}) %reduce-scatter.6.cloned.1.call-update) | async-done | bytes 786448 | tf_op jit(solution)/shard_map/reduce_scatter | solution.py:563
  535.4 23.5 %all_to_all.48 = bf16[8,2,3,64,256]{4,3,2,1,0:T(8,128)(2,1)S(1)} all-to-all(bf16[8,2,3,64,256]{4,3,2,1,0:T(8,128)(2,1)S(1)} %pair_backward.3), channel_id=1, replica_groups=mesh['far'=2,'near'=2,'rows'=8] {'rows'}, dimensions={0} | all-to-all | bytes 3145728 | tf_op jit(solution)/shard_map/all_to_all | solution.py:230
  561.8 3.5 convolution_convert_fusion
  565.4 5.3 fusion.83
  576.2 9.9 %collective-permute-done.5 = bf16[256,1024]{1,0:T(8,128)(2,1)} collective-permute-done((bf16[256,1024]{1,0:T(8,128)(2,1)}, bf16[256,1024]{1,0:T(8,128)(2,1)}, u32[]{:S(2)}, u32[]{:S(2)}) %collective-permute-start.5) | collective-permute-done | bytes 524320 | tf_op jit(solution)/shard_map/ppermute | solution.py:394
  590.2 21.6 %collective-permute-done.6 = bf16[2,128,1024]{2,1,0:T(8,128)(2,1)S(1)} collective-permute-done((bf16[2,128,1024]{2,1,0:T(8,128)(2,1)S(1)}, bf16[2,128,1024]{2,1,0:T(8,128)(2,1)S(1)}, u32[]{:S(2)}, u32[]{:S(2)}) %collective-permute-start.6) | collective-permute-done | bytes 524320 | tf_op jit(solution)/shard_map/ppermute | solution.py:394
  616.1 3.4 collective-permute-start.12
  620.3 34.2 %collective-permute-done.7 = bf16[2,2,128,1024]{3,2,1,0:T(8,128)(2,1)} collective-permute-done((bf16[2,2,128,1024]{3,2,1,0:T(8,128)(2,1)}, bf16[2,2,128,1024]{3,2,1,0:T(8,128)(2,1)}, u32[]{:S(2)}, u32[]{:S(2)}) %collective-permute-start.7) | collective-permute-done | bytes 1048608 | tf_op jit(solution)/shard_map/ppermute | solution.py:394
  654.5 2.7 pad_maximum_fusion.4
  662.7 13.5 %collective-permute-done.16 = bf16[2,2,128,768]{3,2,1,0:T(8,128)(2,1)S(1)} collective-permute-done((bf16[2,2,128,768]{3,2,1,0:T(8,128)(2,1)S(1)}, bf16[2,2,128,768]{3,2,1,0:T(8,128)(2,1)S(1)}, u32[]{:S(2)}, u32[]{:S(2)}) %collective-permute-start.16) | collective-permute-done | bytes 786464 | tf_op jit(solution)/shard_map/ppermute | solution.py:394
  680.1 4.3 fusion.7
  688.1 7.5 collective-permute-done.11
  699.4 2.7 collective-permute-done.17
  703.2 6.1 collective-permute-start.19
  709.3 10.7 %all-gather.2 = bf16[16,80,256]{2,1,0:T(8,128)(2,1)S(1)} all-gather(bf16[2,80,256]{2,1,0:T(8,128)(2,1)S(1)} %pad_maximum_fusion.22), channel_id=4, replica_groups=mesh['far'=2,'near'=2,'rows'=8] {'rows'}, dimensions={0}, use_global_device_ids=true | all-gather | bytes 737280 | tf_op jit(solution)/shard_map/all_gather | solution.py:643
  720.2 2.9 collective-permute-start.13
  724.8 6.7 slice_convert_fusion
  731.5 5.3 copy.128
  738.3 10.0 %collective-permute-done.13 = bf16[2,128,1024]{2,1,0:T(8,128)(2,1)S(1)} collective-permute-done((bf16[2,128,1024]{2,1,0:T(8,128)(2,1)S(1)}, bf16[2,128,1024]{2,1,0:T(8,128)(2,1)S(1)}, u32[]{:S(2)}, u32[]{:S(2)}) %collective-permute-start.13) | collective-permute-done | bytes 524320 | tf_op jit(solution)/shard_map/ppermute | solution.py:394
  749.1 2.8 fusion.73
  762.4 14.4 %collective-permute-done.14 = bf16[2,2,128,1024]{3,2,1,0:T(8,128)(2,1)} collective-permute-done((bf16[2,2,128,1024]{3,2,1,0:T(8,128)(2,1)}, bf16[2,2,128,1024]{3,2,1,0:T(8,128)(2,1)}, u32[]{:S(2)}, u32[]{:S(2)}) %collective-permute-start.14) | collective-permute-done | bytes 1048608 | tf_op jit(solution)/shard_map/ppermute | solution.py:394
  785.1 3.7 copy.124
  (363 shorter events, 160.3 us)
Async XLA Ops:
  7.2 241.6 %copy-start = (bf16[4,256,1024]{2,1,0:T(8,128)(2,1)S(1)}, bf16[4,256,1024]{2,1,0:T(8,128)(2,1)}, u32[]{:S(2)}) copy-start(bf16[4,256,1024]{2,1,0:T(8,128)(2,1)} %param.31) | copy-start | bytes 6291460
  7.2 65.5 %all-gather.10.cloned.1.call-start = ((), (), s32[]{:S(2)}) async-start(), calls=%async_computation.12 | async-start | bytes 1769472 | tf_op jit(solution)/shard_map/all_gather | solution.py:444
  10.0 8.4 %copy-start.62 = (s32[4,256]{1,0:T(4,128)S(1)}, s32[4,256]{1,0:T(4,128)}, u32[]{:S(2)}) copy-start(s32[4,256]{1,0:T(4,128)} %param.17) | copy-start | bytes 12292
  12.7 18.1 %copy-start.58 = (bf16[32,2,1024]{2,1,0:T(2,128)(2,1)S(1)}, bf16[32,2,1024]{2,1,0:T(2,128)(2,1)}, u32[]{:S(2)}) copy-start(bf16[32,2,1024]{2,1,0:T(2,128)(2,1)} %param.20) | copy-start | bytes 393220
  12.7 20.0 %copy-start.49 = (bf16[2,1024,256]{2,1,0:T(8,128)(2,1)S(1)}, bf16[2,1024,256]{2,1,0:T(8,128)(2,1)}, u32[]{:S(2)}) copy-start(bf16[2,1024,256]{2,1,0:T(8,128)(2,1)} %param.25) | copy-start | bytes 3145732
  14.4 13.4 %collective-permute-start = (bf16[96,1024]{1,0:T(8,128)(2,1)}, bf16[96,1024]{1,0:T(8,128)(2,1)S(1)}, u32[]{:S(2)}, u32[]{:S(2)}) collective-permute-start(bf16[96,1024]{1,0:T(8,128)(2,1)} %constant_dynamic-slice_fusion.19), channel_id=1, source_target_pairs={{0,16},{16,0},{1,17},{17,1},{2,18},{18,2},{3,19},{19,3},{4,20},{20... | collective-permute-start | bytes 589832 | tf_op jit(solution)/shard_map/ppermute | solution.py:394
  19.9 11.5 %copy-start.59 = (f32[2,256]{1,0:T(2,128)}, f32[2,256]{1,0:T(2,128)S(1)}, u32[]{:S(2)}) copy-start(f32[2,256]{1,0:T(2,128)S(1)} %get-tuple-element.158) | copy-start | bytes 6148
  28.4 128.4 %all-gather.18.cloned.1.call-start = ((), (), s32[]{:S(2)}) async-start(), calls=%async_computation.19 | async-start | bytes 8257536 | tf_op jit(solution)/shard_map/all_gather | solution.py:524
  39.9 38.7 %copy-start.50 = (bf16[512,1024]{1,0:T(8,128)(2,1)}, bf16[512,1024]{1,0:T(8,128)(2,1)S(1)}, u32[]{:S(2)}) copy-start(bf16[512,1024]{1,0:T(8,128)(2,1)S(1)} %get-tuple-element.35) | copy-start | bytes 3145732
  40.7 17.1 %collective-permute-start.2 = (bf16[160,1024]{1,0:T(8,128)(2,1)}, bf16[160,1024]{1,0:T(8,128)(2,1)}, u32[]{:S(2)}, u32[]{:S(2)}) collective-permute-start(bf16[160,1024]{1,0:T(8,128)(2,1)} %pad_maximum_fusion.20), channel_id=1, source_target_pairs={{0,16},{16,0},{1,17},{17,1},{2,18},{18,2},{3,19},{19,3},{4,20},{20... | collective-permute-start | bytes 983048 | tf_op jit(solution)/shard_map/ppermute | solution.py:394
  58.8 9.5 %collective-permute-start.3 = (bf16[2,96,1024]{2,1,0:T(8,128)(2,1)S(1)}, bf16[2,96,1024]{2,1,0:T(8,128)(2,1)S(1)}, u32[]{:S(2)}, u32[]{:S(2)}) collective-permute-start(bf16[2,96,1024]{2,1,0:T(8,128)(2,1)S(1)} %fusion.59), channel_id=1, source_target_pairs={{0,8},{8,0},{1,9},{9,1},{2,10},{10,2},{3,11},{11,3},{4,12},{12,4},... | collective-permute-start | bytes 1179656 | tf_op jit(solution)/shard_map/ppermute | solution.py:394
  82.8 29.7 %all-to-all-start = ((bf16[8,2,3,64,256]{4,3,2,1,0:T(8,128)(2,1)}), bf16[8,2,3,64,256]{4,3,2,1,0:T(8,128)(2,1)}, u32[]{:S(2)}, u32[]{:S(2)}) async-start(bf16[8,2,3,64,256]{4,3,2,1,0:T(8,128)(2,1)} %pad_maximum_fusion.6), calls=%async_computation | async-start | bytes 3145728 | tf_op jit(solution)/shard_map/all_to_all | solution.py:230
  87.1 176.8 %all-gather.20.cloned.1.call-start = ((), (), s32[]{:S(2)}) async-start(), calls=%async_computation.20 | async-start | bytes 8912896 | tf_op jit(solution)/shard_map/all_gather | solution.py:538
  136.6 5.7 copy-start.64
  136.6 16.3 %all-to-all-start.1 = ((bf16[8,2,64,256]{3,2,1,0:T(8,128)(2,1)}), bf16[8,2,64,256]{3,2,1,0:T(8,128)(2,1)}, u32[]{:S(2)}, u32[]{:S(2)}) async-start(bf16[8,2,64,256]{3,2,1,0:T(8,128)(2,1)} %get-tuple-element.37), calls=%async_computation.1 | async-start | bytes 1048576 | tf_op jit(solution)/shard_map/all_to_all | solution.py:230
  155.4 17.9 %collective-permute-start.1 = (bf16[512,512]{1,0:T(8,128)(2,1)}, bf16[512,512]{1,0:T(8,128)(2,1)}, u32[]{:S(2)}, u32[]{:S(2)}) collective-permute-start(bf16[512,512]{1,0:T(8,128)(2,1)} %bitcast.164), channel_id=1, source_target_pairs={{0,8},{8,0},{1,9},{9,1},{2,10},{10,2},{3,11},{11,3},{4,12},{12,4},... | collective-permute-start | bytes 1572872 | tf_op jit(solution)/shard_map/ppermute | solution.py:394
  167.4 5.9 copy-start.32
  179.0 21.4 %all-to-all-start.2 = ((bf16[8,2,1,64,256]{4,3,2,1,0:T(8,128)(2,1)}), bf16[8,2,1,64,256]{4,3,2,1,0:T(8,128)(2,1)S(1)}, u32[]{:S(2)}, u32[]{:S(2)}) async-start(bf16[8,2,1,64,256]{4,3,2,1,0:T(8,128)(2,1)} %pad_maximum_fusion.16), calls=%async_computation.2 | async-start | bytes 1048576 | tf_op jit(solution)/shard_map/all_to_all | solution.py:230
  191.8 13.0 %copy-start.68 = (s32[4]{0:T(128)S(1)}, s32[4]{0:T(128)}, u32[]{:S(2)}) copy-start(s32[4]{0:T(128)} %param.19) | copy-start | bytes 52
  201.2 18.9 %all-to-all-start.3 = ((bf16[8,2,2,64,256]{4,3,2,1,0:T(8,128)(2,1)}), bf16[8,2,2,64,256]{4,3,2,1,0:T(8,128)(2,1)S(1)}, u32[]{:S(2)}, u32[]{:S(2)}) async-start(bf16[8,2,2,64,256]{4,3,2,1,0:T(8,128)(2,1)} %pad_maximum_fusion.10), calls=%async_computation.3 | async-start | bytes 2097152 | tf_op jit(solution)/shard_map/all_to_all | solution.py:230
  204.8 194.7 %reduce-scatter.4.cloned.1.call-start = ((), (), s32[]{:S(2)}) async-start(), calls=%async_computation.13 | async-start | bytes 8912896 | tf_op jit(solution)/shard_map/reduce_scatter | solution.py:581
  234.8 15.0 %copy-start.5 = (f32[8,2,64,256]{3,2,1,0:T(8,128)}, f32[8,2,64,256]{3,2,1,0:T(8,128)S(1)}, u32[]{:S(2)}) copy-start(f32[8,2,64,256]{3,2,1,0:T(8,128)S(1)} %get-tuple-element.45.wide_ref) | copy-start | bytes 3145732
  234.8 13.9 %copy-start.65 = (bf16[1024]{0:T(1024)(128)(2,1)S(1)}, bf16[1024]{0:T(1024)(128)(2,1)}, u32[]{:S(2)}) copy-start(bf16[1024]{0:T(1024)(128)(2,1)} %param.28) | copy-start | bytes 6148
  247.8 13.1 %copy-start.54 = (bf16[64,8,2,256]{3,1,2,0:T(8,128)(2,1)}, bf16[64,8,2,256]{3,1,2,0:T(8,128)(2,1)S(1)}, u32[]{:S(2)}) copy-start(bf16[64,8,2,256]{3,1,2,0:T(8,128)(2,1)S(1)} %copy.138) | copy-start | bytes 1572868
  247.8 13.1 %collective-permute-start.4 = (bf16[512,512]{1,0:T(8,128)(2,1)S(1)}, bf16[512,512]{1,0:T(8,128)(2,1)S(1)}, u32[]{:S(2)}, u32[]{:S(2)}) collective-permute-start(bf16[512,512]{1,0:T(8,128)(2,1)S(1)} %bitcast.375), channel_id=1, source_target_pairs={{0,8},{8,0},{1,9},{9,1},{2,10},{10,2},{3,11},{11,3},{4,12},{12,4},... | collective-permute-start | bytes 1572872 | tf_op jit(solution)/shard_map/ppermute | solution.py:394
  249.8 11.0 %copy-start.10 = (f32[512,1024]{1,0:T(8,128)S(1)}, f32[512,1024]{1,0:T(8,128)}, u32[]{:S(2)}) copy-start(f32[512,1024]{1,0:T(8,128)} %copy-done.9) | copy-start | bytes 6291460
  295.7 224.5 %all-gather.12.cloned.1.call-start = ((), (), s32[]{:S(2)}) async-start(), calls=%async_computation.14 | async-start | bytes 4718592 | tf_op jit(solution)/shard_map/all_gather | solution.py:444
  295.7 6.3 copy-start.36
  301.1 35.0 %copy-start.13 = (f32[512,1024]{1,0:T(8,128)S(1)}, f32[512,1024]{1,0:T(8,128)}, u32[]{:S(2)}) copy-start(f32[512,1024]{1,0:T(8,128)} %copy-done.11) | copy-start | bytes 6291460
  301.1 34.9 %collective-permute-start.8 = (bf16[512,1024]{1,0:T(8,128)(2,1)S(1)}, bf16[512,1024]{1,0:T(8,128)(2,1)S(1)}, u32[]{:S(2)}, u32[]{:S(2)}) collective-permute-start(bf16[512,1024]{1,0:T(8,128)(2,1)S(1)} %fusion.21), channel_id=1, source_target_pairs={{0,8},{8,0},{1,9},{9,1},{2,10},{10,2},{3,11},{11,3},{4,12},{12,4},... | collective-permute-start | bytes 3145736 | tf_op jit(solution)/shard_map/ppermute | solution.py:394
  302.2 34.8 %copy-start.29 = (bf16[2,256,1024]{2,1,0:T(8,128)(2,1)S(1)}, bf16[2,256,1024]{2,1,0:T(8,128)(2,1)}, u32[]{:S(2)}) copy-start(bf16[2,256,1024]{2,1,0:T(8,128)(2,1)} %constant_dynamic-slice_fusion.8) | copy-start | bytes 3145732
  339.7 27.4 %copy-start.4 = (bf16[8,2,1,64,256]{4,3,2,1,0:T(8,128)(2,1)S(1)}, bf16[8,2,1,64,256]{4,3,2,1,0:T(8,128)(2,1)}, u32[]{:S(2)}) copy-start(bf16[8,2,1,64,256]{4,3,2,1,0:T(8,128)(2,1)} %copy-done.2) | copy-start | bytes 1572868
  339.7 27.4 %copy-start.6 = (f32[8,2,64,256]{3,2,1,0:T(8,128)S(1)}, f32[8,2,64,256]{3,2,1,0:T(8,128)}, u32[]{:S(2)}) copy-start(f32[8,2,64,256]{3,2,1,0:T(8,128)} %copy-done.5) | copy-start | bytes 3145732
  399.5 32.0 %all-to-all-start.6 = ((bf16[8,2,3,64,256]{4,3,2,1,0:T(8,128)(2,1)}), bf16[8,2,3,64,256]{4,3,2,1,0:T(8,128)(2,1)}, u32[]{:S(2)}, u32[]{:S(2)}) async-start(bf16[8,2,3,64,256]{4,3,2,1,0:T(8,128)(2,1)} %pair_backward.2), calls=%async_computation.7 | async-start | bytes 3145728 | tf_op jit(solution)/shard_map/all_to_all | solution.py:230
  404.8 130.6 %reduce-scatter.6.cloned.1.call-start = ((), (), s32[]{:S(2)}) async-start(), calls=%async_computation.15 | async-start | bytes 7077888 | tf_op jit(solution)/shard_map/reduce_scatter | solution.py:563
  435.9 14.9 %collective-permute-start.9 = (bf16[512,512]{1,0:T(8,128)(2,1)S(1)}, bf16[512,512]{1,0:T(8,128)(2,1)S(1)}, u32[]{:S(2)}, u32[]{:S(2)}) collective-permute-start(bf16[512,512]{1,0:T(8,128)(2,1)S(1)} %bitcast.378), channel_id=1, source_target_pairs={{0,8},{8,0},{1,9},{9,1},{2,10},{10,2},{3,11},{11,3},{4,12},{12,4},... | collective-permute-start | bytes 1572872 | tf_op jit(solution)/shard_map/ppermute | solution.py:394
  440.5 29.0 %collective-permute-start.10 = (bf16[512,1024]{1,0:T(8,128)(2,1)S(1)}, bf16[512,1024]{1,0:T(8,128)(2,1)S(1)}, u32[]{:S(2)}, u32[]{:S(2)}) collective-permute-start(bf16[512,1024]{1,0:T(8,128)(2,1)S(1)} %convolution_convert_fusion.7), channel_id=1, source_target_pairs={{0,8},{8,0},{1,9},{9,1},{2,10},{10,2},{3,11},{11,3},{4,12},{12,4},... | collective-permute-start | bytes 3145736 | tf_op jit(solution)/shard_map/ppermute | solution.py:394
  441.8 9.0 %copy-start.37 = (bf16[1,4,8,32,1024]{4,3,2,1,0:T(8,128)(2,1)S(1)}, bf16[1,4,8,32,1024]{4,3,2,1,0:T(8,128)(2,1)}, u32[]{:S(2)}) copy-start(bf16[1,4,8,32,1024]{4,3,2,1,0:T(8,128)(2,1)} %copy.112) | copy-start | bytes 6291460
  460.4 9.6 %copy-start.22 = (bf16[2,256,768]{2,1,0:T(8,128)(2,1)S(1)}, bf16[2,256,768]{2,1,0:T(8,128)(2,1)}, u32[]{:S(2)}) copy-start(bf16[2,256,768]{2,1,0:T(8,128)(2,1)} %copy-done.21) | copy-start | bytes 2359300
  471.9 230.3 %reduce-scatter.8.cloned.1.call-start = ((), (), s32[]{:S(2)}) async-start(), calls=%async_computation.17 | async-start | bytes 3538944 | tf_op jit(solution)/shard_map/reduce_scatter | solution.py:563
  473.9 14.9 %copy-start.8 = (f32[8,2,64,256]{3,2,1,0:T(8,128)S(1)}, f32[8,2,64,256]{3,2,1,0:T(8,128)}, u32[]{:S(2)}) copy-start(f32[8,2,64,256]{3,2,1,0:T(8,128)} %copy-done.7) | copy-start | bytes 3145732
  565.3 154.9 %all-gather.14.cloned.1.call-start = ((), (), s32[]{:S(2)}) async-start(), calls=%async_computation.16 | async-start | bytes 3538944 | tf_op jit(solution)/shard_map/all_gather | solution.py:444
  565.3 9.0 %copy-start.14 = (f32[512,1024]{1,0:T(8,128)S(1)}, f32[512,1024]{1,0:T(8,128)}, u32[]{:S(2)}) copy-start(f32[512,1024]{1,0:T(8,128)} %copy-done.11) | copy-start | bytes 6291460
  572.8 13.3 %collective-permute-start.5 = (bf16[256,1024]{1,0:T(8,128)(2,1)}, bf16[256,1024]{1,0:T(8,128)(2,1)}, u32[]{:S(2)}, u32[]{:S(2)}) collective-permute-start(bf16[256,1024]{1,0:T(8,128)(2,1)} %bitcast.40), channel_id=1, source_target_pairs={{0,8},{8,0},{1,9},{9,1},{2,10},{10,2},{3,11},{11,3},{4,12},{12,4},... | collective-permute-start | bytes 1572872 | tf_op jit(solution)/shard_map/ppermute | solution.py:394
  576.2 13.9 %copy-start.60 = (f32[2,256]{1,0:T(2,128)S(1)}, f32[2,256]{1,0:T(2,128)}, u32[]{:S(2)}) copy-start(f32[2,256]{1,0:T(2,128)} %copy-done.59) | copy-start | bytes 6148
  576.2 13.9 %copy-start.61 = (f32[2,256]{1,0:T(2,128)S(1)}, f32[2,256]{1,0:T(2,128)}, u32[]{:S(2)}) copy-start(f32[2,256]{1,0:T(2,128)} %get-tuple-element.155) | copy-start | bytes 6148
  576.2 13.9 %copy-start.63 = (s32[4,256]{1,0:T(4,128)S(1)}, s32[4,256]{1,0:T(4,128)}, u32[]{:S(2)}) copy-start(s32[4,256]{1,0:T(4,128)} %param.17) | copy-start | bytes 12292
  587.5 24.3 %collective-permute-start.6 = (bf16[2,128,1024]{2,1,0:T(8,128)(2,1)S(1)}, bf16[2,128,1024]{2,1,0:T(8,128)(2,1)S(1)}, u32[]{:S(2)}, u32[]{:S(2)}) collective-permute-start(bf16[2,128,1024]{2,1,0:T(8,128)(2,1)S(1)} %bitcast.356), channel_id=1, source_target_pairs={{0,16},{16,0},{1,17},{17,1},{2,18},{18,2},{3,19},{19,3},{4,20},{20... | collective-permute-start | bytes 1572872 | tf_op jit(solution)/shard_map/ppermute | solution.py:394
  613.3 41.3 %collective-permute-start.7 = (bf16[2,2,128,1024]{3,2,1,0:T(8,128)(2,1)}, bf16[2,2,128,1024]{3,2,1,0:T(8,128)(2,1)}, u32[]{:S(2)}, u32[]{:S(2)}) collective-permute-start(bf16[2,2,128,1024]{3,2,1,0:T(8,128)(2,1)} %get-tuple-element.148), channel_id=1, source_target_pairs={{0,8},{8,0},{1,9},{9,1},{2,10},{10,2},{3,11},{11,3},{4,12},{12,4},... | collective-permute-start | bytes 3145736 | tf_op jit(solution)/shard_map/ppermute | solution.py:394
  614.0 5.6 copy-start.67
  616.0 38.6 %copy-start.33 = (bf16[1,2,2,128,1024]{4,3,0,2,1:T(8,128)(2,1)S(1)}, bf16[1,2,2,128,1024]{4,3,0,2,1:T(8,128)(2,1)}, u32[]{:S(2)}) copy-start(bf16[1,2,2,128,1024]{4,3,0,2,1:T(8,128)(2,1)} %get-tuple-element.147) | copy-start | bytes 3145732
  616.1 41.2 %collective-permute-start.12 = (bf16[192,1024]{1,0:T(8,128)(2,1)S(1)}, bf16[192,1024]{1,0:T(8,128)(2,1)S(1)}, u32[]{:S(2)}, u32[]{:S(2)}) collective-permute-start(bf16[192,1024]{1,0:T(8,128)(2,1)S(1)} %dynamic-slice_bitcast_fusion), channel_id=1, source_target_pairs={{0,16},{16,0},{1,17},{17,1},{2,18},{18,2},{3,19},{19,3},{4,20},{20... | collective-permute-start | bytes 1179656 | tf_op jit(solution)/shard_map/ppermute | solution.py:394
  620.2 38.3 %collective-permute-start.15 = (bf16[2,128,768]{2,1,0:T(8,128)(2,1)S(1)}, bf16[2,128,768]{2,1,0:T(8,128)(2,1)S(1)}, u32[]{:S(2)}, u32[]{:S(2)}) collective-permute-start(bf16[2,128,768]{2,1,0:T(8,128)(2,1)S(1)} %bitcast.387), channel_id=1, source_target_pairs={{0,16},{16,0},{1,17},{17,1},{2,18},{18,2},{3,19},{19,3},{4,20},{20... | collective-permute-start | bytes 1179656 | tf_op jit(solution)/shard_map/ppermute | solution.py:394
  658.2 123.3 %all-gather.16.cloned.1.call-start = ((), (), s32[]{:S(2)}) async-start(), calls=%async_computation.18 | async-start | bytes 1769472 | tf_op jit(solution)/shard_map/all_gather | solution.py:444
  658.6 17.6 %collective-permute-start.16 = (bf16[2,2,128,768]{3,2,1,0:T(8,128)(2,1)S(1)}, bf16[2,2,128,768]{3,2,1,0:T(8,128)(2,1)S(1)}, u32[]{:S(2)}, u32[]{:S(2)}) collective-permute-start(bf16[2,2,128,768]{3,2,1,0:T(8,128)(2,1)S(1)} %get-tuple-element.150), channel_id=1, source_target_pairs={{0,8},{8,0},{1,9},{9,1},{2,10},{10,2},{3,11},{11,3},{4,12},{12,4},... | collective-permute-start | bytes 2359304 | tf_op jit(solution)/shard_map/ppermute | solution.py:394
  680.1 5.4 copy-start.24
  684.5 11.2 %collective-permute-start.11 = (bf16[256,1024]{1,0:T(8,128)(2,1)S(1)}, bf16[256,1024]{1,0:T(8,128)(2,1)S(1)}, u32[]{:S(2)}, u32[]{:S(2)}) collective-permute-start(bf16[256,1024]{1,0:T(8,128)(2,1)S(1)} %bitcast.381), channel_id=1, source_target_pairs={{0,8},{8,0},{1,9},{9,1},{2,10},{10,2},{3,11},{11,3},{4,12},{12,4},... | collective-permute-start | bytes 1572872 | tf_op jit(solution)/shard_map/ppermute | solution.py:394
  697.0 5.0 collective-permute-start.17
  699.4 20.9 %copy-start.38 = (bf16[256,1024]{1,0:T(8,128)(2,1)S(1)}, bf16[256,1024]{1,0:T(8,128)(2,1)}, u32[]{:S(2)}) copy-start(bf16[256,1024]{1,0:T(8,128)(2,1)} %fusion.41) | copy-start | bytes 1572868
  703.2 19.9 %collective-permute-start.19 = (bf16[96,1024]{1,0:T(8,128)(2,1)S(1)}, bf16[96,1024]{1,0:T(8,128)(2,1)S(1)}, u32[]{:S(2)}, u32[]{:S(2)}) collective-permute-start(bf16[96,1024]{1,0:T(8,128)(2,1)S(1)} %dynamic-slice_bitcast_fusion.1), channel_id=1, source_target_pairs={{0,16},{16,0},{1,17},{17,1},{2,18},{18,2},{3,19},{19,3},{4,20},{20... | collective-permute-start | bytes 589832 | tf_op jit(solution)/shard_map/ppermute | solution.py:394
  720.1 17.5 %collective-permute-start.18 = (bf16[80,256]{1,0:T(8,128)(2,1)S(1)}, bf16[80,256]{1,0:T(8,128)(2,1)S(1)}, u32[]{:S(2)}, u32[]{:S(2)}) collective-permute-start(bf16[80,256]{1,0:T(8,128)(2,1)S(1)} %dynamic-slice_bitcast_fusion.2), channel_id=1, source_target_pairs={{0,16},{16,0},{1,17},{17,1},{2,18},{18,2},{3,19},{19,3},{4,20},{20... | collective-permute-start | bytes 122888 | tf_op jit(solution)/shard_map/ppermute | solution.py:394
  720.2 28.0 %collective-permute-start.13 = (bf16[2,128,1024]{2,1,0:T(8,128)(2,1)S(1)}, bf16[2,128,1024]{2,1,0:T(8,128)(2,1)S(1)}, u32[]{:S(2)}, u32[]{:S(2)}) collective-permute-start(bf16[2,128,1024]{2,1,0:T(8,128)(2,1)S(1)} %bitcast.347), channel_id=1, source_target_pairs={{0,16},{16,0},{1,17},{17,1},{2,18},{18,2},{3,19},{19,3},{4,20},{20... | collective-permute-start | bytes 1572872 | tf_op jit(solution)/shard_map/ppermute | solution.py:394
  751.9 24.9 %collective-permute-start.14 = (bf16[2,2,128,1024]{3,2,1,0:T(8,128)(2,1)}, bf16[2,2,128,1024]{3,2,1,0:T(8,128)(2,1)}, u32[]{:S(2)}, u32[]{:S(2)}) collective-permute-start(bf16[2,2,128,1024]{3,2,1,0:T(8,128)(2,1)} %get-tuple-element.146), channel_id=1, source_target_pairs={{0,8},{8,0},{1,9},{9,1},{2,10},{10,2},{3,11},{11,3},{4,12},{12,4},... | collective-permute-start | bytes 3145736 | tf_op jit(solution)/shard_map/ppermute | solution.py:394
  760.5 16.3 %copy-start.34 = (bf16[1,2,2,128,1024]{4,3,0,2,1:T(8,128)(2,1)S(1)}, bf16[1,2,2,128,1024]{4,3,0,2,1:T(8,128)(2,1)}, u32[]{:S(2)}) copy-start(bf16[1,2,2,128,1024]{4,3,0,2,1:T(8,128)(2,1)} %get-tuple-element.145) | copy-start | bytes 3145732
  (44 other events, 102.5 us)
Sparse Core Ops, SparseCore 0:
  28.5 26.8 all-gather.9
  69.5 59.4 all-gather.17
  131.9 83.6 all-gather.19
  295.8 103.6 reduce-scatter.3
  401.2 49.1 all-gather.11
  472.0 63.3 reduce-scatter.5
  565.4 45.3 reduce-scatter.7
  658.3 33.9 all-gather.13
  724.9 23.4 all-gather.15

commit v6 on v5

--- a/solution.py
+++ b/solution.py
@@ -468,9 +468,7 @@
         return mine + swap(away.astype(LOW), "near").astype(WIDE)
 
     def over_heads(value):
-        value = value.reshape(objects, rows // 2, -1)
-        value = jnp.stack([value, swap(value, "far")])
-        value = jnp.stack([value, swap(value, "near")])
+        value = value.reshape(2, 2, objects, rows // 2, -1)
         value = jnp.where(far == 0, value, jnp.flip(value, 1))
         value = jnp.where(near == 0, value, jnp.flip(value, 0))
         return value.transpose(1, 2, 0, 3, 4).reshape(2 * objects, rows, -1)
@@ -482,7 +480,7 @@
             .reshape(n_rows, slots, HEAD_DIM, rows)
             for i in range(objects)
         ]
-        return exchange_rows(jnp.stack(parts, axis=1))
+        return jnp.stack(parts, axis=1)
 
     def from_pairs(value):
         return value.transpose(0, 2, 3, 1, 4).reshape(-1, count)
@@ -527,10 +525,10 @@
     self_whole, query_whole, cross_whole = whole.reshape(3, 4 * cols, width)
 
     qkv_both = in_order(qkv_rows, qkv_away)
-    qkv = to_pairs(qkv_both, normed_one, 3)
+    qkv = exchange_rows(to_pairs(qkv_both, normed_one, 3))
     patch_mid = mul(patch_in, patch_weights).astype(LOW)
     pair_both = in_order(pair_rows, pair_away)
-    pair = to_pairs(pair_both, patch_mid, 2)
+    pair = exchange_rows(to_pairs(pair_both, patch_mid, 2))
 
     mine = [piece(widen_weights), piece(narrow_weights)]
     qkv, *mine = tie(qkv, *mine)
@@ -546,7 +544,7 @@
     after_self = inputs + over_all_columns(self_mixed_t, self_whole)
     unit_two, rate_two = normed(after_self)
     normed_two = (unit_two * cross_gain_f).astype(LOW)
-    cross_q = to_pairs(query_whole[: 2 * cols], normed_two, 1)
+    cross_q = exchange_rows(to_pairs(query_whole[: 2 * cols], normed_two, 1))
     mixed, cross_wide, cross_log = pair_forward(cross_q, pair, 0, length)
     cross_mixed_t = from_pairs(exchange_rows(mixed)[:, :, None])
     after_cross = after_self + over_all_columns(cross_mixed_t, cross_whole)
@@ -555,7 +553,8 @@
     activated, act_back = jax.vjp(gelu_tanh, mul(normed_three, widen))
     activated = activated.astype(LOW)
     grad_pre = act_back(mul(grad_low, narrow, NT))[0].astype(LOW)
-    grad_three = sum_near(mul(grad_pre, widen, NT))
+    third, activated, grad_pre = tie(mul(grad_pre, widen, NT).astype(LOW), activated, grad_pre)
+    grad_three = third.astype(WIDE) + swap(third, "near").astype(WIDE)
     hidden_half = half_sum_near(mul(activated, narrow))
     result = (halves(after_cross)[0] + hidden_half).astype(LOW)
 
@@ -587,9 +586,11 @@
         grad_three * hidden_gain_f, unit_three, rate_three
     )
     grad_cross_low = grad_cross.astype(LOW)
-    grad_mixed = to_pairs(cross_whole[: 2 * cols], grad_cross_low, 1)[:, :, 0]
-    grads = pair_backward(cross_q, pair, 0, length, grad_mixed, cross_wide, cross_log)
-    grads, hidden_part = tie(grads, hidden_part)
+    grad_mixed, result = tie(to_pairs(cross_whole[: 2 * cols], grad_cross_low, 1)[:, :, 0], result)
+    result_two = jnp.stack([result, swap(result, "far")])
+    grads = pair_backward(cross_q, pair, 0, length, exchange_rows(grad_mixed), cross_wide, cross_log)
+    grads, result_two, hidden_part = tie(grads, result_two, hidden_part)
+    result_four = jnp.stack([result_two, swap(result_two, "near")])
     grads = exchange_rows(grads)
     hidden_total = join_rows(hidden_part)
     grad_cq_t = from_pairs(grads[:, :, :1])
@@ -611,19 +612,22 @@
                 by_shard(self_mixed_t, grad_self_low),
                 by_shard(grad_cq_t, normed_two),
                 by_shard(grad_pair_t, patch_mid),
-                patch_terms,
             ],
             axis=1,
         )
     )
-    grad_mixed = to_pairs(self_whole[: 2 * cols], grad_self_low, 1)[:, :, 0]
-    grads = pair_backward(qkv, qkv, 1, None, grad_mixed, self_wide, self_log)
-    grads, hidden_total, middle_part = tie(grads, hidden_total, middle_part)
-    grads = exchange_rows(grads)
+    grad_mixed, patch_half = tie(to_pairs(self_whole[: 2 * cols], grad_self_low, 1)[:, :, 0], patch_half)
+    patch_two = jnp.stack([patch_half, swap(patch_half, "far")])
+    grads = pair_backward(qkv, qkv, 1, None, exchange_rows(grad_mixed), self_wide, self_log)
+    grads, patch_two, result_four, hidden_total, middle_part = tie(
+        grads, patch_two, result_four, hidden_total, middle_part
+    )
     middle_own, middle_away = own_and_away(middle_part)
-    middle_total = join_rows(add_far(middle_own, swap(middle_away, "far")))
+    patch_four = jnp.stack([patch_two, swap(patch_two, "near")])
+    grads, patch_four, middle_away = tie(exchange_rows(grads), patch_four, swap(middle_away, "far"))
+    middle_total = join_rows(add_far(middle_own, middle_away))
     grad_qkv_t = from_pairs(grads)
-    last_part = part_rows(by_shard(grad_qkv_t, normed_one))
+    last_part = part_rows(jnp.concatenate([by_shard(grad_qkv_t, normed_one), patch_terms], axis=1))
     grad_one = half_sum_near(mul(grad_qkv_t, qkv_both, TN))
     gain_half, unit_half, rate_half, self_half = (
         halves(value)[0] for value in (gain_one, unit_one, rate_one, grad_self)
@@ -646,17 +650,18 @@
     )
     small = small_own.astype(WIDE) + swap(small_away, "far").astype(WIDE)
     input_half, middle_total = tie(input_half, middle_total)
-    input_grads = over_heads(input_half)
-    outputs = over_heads(result)
-    patch_grads = over_heads(patch_half)
+    input_two = jnp.stack([input_half, swap(input_half, "far")])
+    last_part, input_two = tie(last_part, input_two)
+    input_grads = over_heads(jnp.stack([input_two, swap(input_two, "near")]))
+    outputs, patch_grads = over_heads(result_four), over_heads(patch_four)
     last_own, last_away = own_and_away(last_part)
     last_total = join_rows(add_far(last_own, swap(last_away, "far")))
 
     output_total = middle_total[: 2 * cols]
     query_total = middle_total[2 * cols : 3 * cols]
     pair_total = middle_total[3 * cols : 5 * cols].reshape(heads, 2, HEAD_DIM, width)
-    patch_total = middle_total[5 * cols :, :patch_width]
-    self_total = last_total.reshape(heads, 3, HEAD_DIM, width)
+    patch_total = last_total[3 * cols :, :patch_width]
+    self_total = last_total[: 3 * cols].reshape(heads, 3, HEAD_DIM, width)
     gradients = (
         small[: 2 * codes].reshape(2, codes, cols).transpose(1, 0, 2),
         self_total.transpose(1, 3, 0, 2).reshape(3, width, cols),

time: 804 us -> 795 us (0.989)
  blocking collectives: 87.7 us -> 23.3 us
  other arithmetic: 66 us -> 87.7 us
  waiting for transfers between devices: 315 us -> 331 us
  Pallas kernels: 85.8 us -> 99.5 us
  starting transfers between devices: 52.9 us -> 63.1 us
    all_to_all x4 -> x1, blocking collectives: 77 us -> 12.3 us  [exchange_rows(): return lax.all_to_all(value, 'rows', 0, 0, tiled=True)]
    all_to_all x5 -> x8, waiting for transfers between devices: 73.9 us -> 90.3 us  [exchange_rows(): return lax.all_to_all(value, 'rows', 0, 0, tiled=True)]
    all_to_all x5 -> x8, starting transfers between devices: 23.3 us -> 36.5 us  [exchange_rows(): return lax.all_to_all(value, 'rows', 0, 0, tiled=True)]
    pallas_call x2, Pallas kernels: 53.2 us -> 63.3 us  [pair_backward(): pl.pallas_call(kernel, grid_spec=pltpu.PrefetchScalarGridSpec(num_scalar_...]
  transfers between devices with their start and end apart: 34 -> 37, of which waited for: 24 -> 23; matrix products, arithmetic and copies ran while one was open for 22% -> 23% of each run, Pallas kernels for 11% -> 13%
where the time goes in v6:
time: 795 us; the launch traced here: 787 us
  waiting for transfers between devices  331 us (42%)
  local copies, waits for them, and re-layouts  103 us (13%)
  Pallas kernels  99.5 us (13%)
  other arithmetic  87.7 us (11%)
  matrix products  63.2 us (8%)
  starting transfers between devices  63.1 us (8%)
  blocking collectives  23.3 us (3%)
  between operations  15.4 us (2%)
    ppermute x20, waiting for transfers between devices, swap(): return lax.ppermute(value, axis, [(0, 1), (1, 0)])  209 us
    all_to_all x8, waiting for transfers between devices, exchange_rows(): return lax.all_to_all(value, 'rows', 0, 0, tiled=True)  90.3 us
    pallas_call x2, Pallas kernels, pair_backward(): pl.pallas_call(kernel, grid_spec=pltpu.PrefetchScalarGridSpec(num_scalar_...  63.3 us
    dot_general x31, matrix products, mul(): return lax.dot_general(left, right, dims, preferred_element_type=WIDE)  62.2 us
    unnamed x169, local copies, waits for them, and re-layouts  38.6 us
    all_to_all x8, starting transfers between devices, exchange_rows(): return lax.all_to_all(value, 'rows', 0, 0, tiled=True)  36.5 us
    pallas_call x2, Pallas kernels, pair_forward(): pl.pallas_call(kernel, grid_spec=pltpu.PrefetchScalarGridSpec(num_scalar_...  36.1 us
    ppermute x20, starting transfers between devices, swap(): return lax.ppermute(value, axis, [(0, 1), (1, 0)])  25.9 us
  transfers between devices with their start and end apart: 37, of which 23 were waited for; matrix products, arithmetic and copies ran while one was open for 23% of the time, Pallas kernels for 13%

profile of v6, /device:TPU:0, one launch (start us, length us, event | category | flops | bytes accessed | tf_op | source)
XLA Modules:
  0.0 786.6 jit_solution(8144868971354209745)
XLA Ops:
  7.2 2.7 copy.98
  10.0 2.7 copy.99
  14.4 4.0 collective-permute-start
  19.9 7.8 collective-permute-done
  40.8 17.1 %collective-permute-done.1 = bf16[160,1024]{1,0:T(8,128)(2,1)} collective-permute-done((bf16[160,1024]{1,0:T(8,128)(2,1)}, bf16[160,1024]{1,0:T(8,128)(2,1)}, u32[]{:S(2)}, u32[]{:S(2)}) %collective-permute-start.1) | collective-permute-done | bytes 327712 | tf_op jit(solution)/shard_map/ppermute | solution.py:394
  59.8 8.5 %collective-permute-done.2 = bf16[2,96,1024]{2,1,0:T(8,128)(2,1)S(1)} collective-permute-done((bf16[2,96,1024]{2,1,0:T(8,128)(2,1)S(1)}, bf16[2,96,1024]{2,1,0:T(8,128)(2,1)S(1)}, u32[]{:S(2)}, u32[]{:S(2)}) %collective-permute-start.2) | collective-permute-done | bytes 393248 | tf_op jit(solution)/shard_map/ppermute | solution.py:394
  75.3 3.2 convolution_convert_fusion.3
  78.6 2.9 convolution_convert_fusion.4
  82.8 4.3 all-to-all-start
  88.3 24.3 %all-to-all-done.q_ref.k_ref.v_ref = bf16[8,2,3,64,256]{4,3,2,1,0:T(8,128)(2,1)} async-done(((bf16[8,2,3,64,256]{4,3,2,1,0:T(8,128)(2,1)}), bf16[8,2,3,64,256]{4,3,2,1,0:T(8,128)(2,1)}, u32[]{:S(2)}, u32[]{:S(2)}) %all-to-all-start) | async-done | bytes 1572896 | tf_op jit(solution)/shard_map/all_to_all | solution.py:230
  113.4 3.2 dynamic-slice_convert_fusion.2
  116.6 19.0 %pair_forward.2 = (bf16[8,2,64,256]{3,2,1,0:T(8,128)(2,1)}, f32[8,2,64,256]{3,2,1,0:T(8,128)S(1)}, f32[8,2,1,256]{3,2,1,0:T(1,128)S(1)}) custom-call(s32[2]{0:T(128)S(1)} %broadcast_13_len_ref.2.len_ref, bf16[8,2,3,64,256]{4,3,2,1,0:T(8,128)(2,1)} %all-to-all-done.q_ref.k_ref.v_ref, bf16[8,2,3,64,256]{4,3,2,1,0:T(8,128)(2,1)} %all-to-all-done.q_ref.k_ref.v_ref, ...), custom_call_target="tpu_custom_call" | custom-call | flops 20132659200 | bytes 8388608 | tf_op jit(solution)/shard_map/pair_forward/pallas_call | solution.py:282
  136.6 3.8 all-to-all-start.1
  146.8 5.9 all-to-all-done.1
  155.0 3.5 slice.172
  162.5 2.7 fusion.75
  165.4 5.5 collective-permute-done.3
  175.5 4.4 all-to-all-start.2
  179.9 2.7 constant_dynamic-update-slice_fusion
  188.3 6.9 all-to-all-done.2.q_ref
  196.0 3.6 all-to-all-start.3
  199.7 15.6 %all-to-all-done.3.k_ref.v_ref = bf16[8,2,2,64,256]{4,3,2,1,0:T(8,128)(2,1)S(1)} async-done(((bf16[8,2,2,64,256]{4,3,2,1,0:T(8,128)(2,1)}), bf16[8,2,2,64,256]{4,3,2,1,0:T(8,128)(2,1)S(1)}, u32[]{:S(2)}, u32[]{:S(2)}) %all-to-all-start.3) | async-done | bytes 1048608 | tf_op jit(solution)/shard_map/all_to_all | solution.py:230
  216.3 17.2 %pair_forward.3 = (bf16[8,2,64,256]{3,2,1,0:T(8,128)(2,1)S(1)}, f32[8,2,64,256]{3,2,1,0:T(8,128)S(1)}, f32[8,2,1,256]{3,2,1,0:T(1,128)S(1)}) custom-call(s32[2]{0:T(128)S(1)} %dynamic_slice.116.len_ref, bf16[8,2,1,64,256]{4,3,2,1,0:T(8,128)(2,1)S(1)} %copy-done.3, bf16[8,2,2,64,256]{4,3,2,1,0:T(8,128)(2,1)S(1)} %all-to-all-done.3.k_ref.v_ref, ...), custom_call_target="tpu_custom_call" | custom-call | flops 14092861440 | bytes 8388608 | tf_op jit(solution)/shard_map/pair_forward/pallas_call | solution.py:282
  233.6 12.3 %all_to_all.45 = bf16[8,2,64,256]{3,2,1,0:T(8,128)(2,1)S(1)} all-to-all(bf16[8,2,64,256]{3,2,1,0:T(8,128)(2,1)S(1)} %get-tuple-element.57), channel_id=1, replica_groups=mesh['far'=2,'near'=2,'rows'=8] {'rows'}, dimensions={0} | all-to-all | bytes 1048576 | tf_op jit(solution)/shard_map/all_to_all | solution.py:230
  249.8 9.9 %collective-permute-done.4 = bf16[512,512]{1,0:T(8,128)(2,1)S(1)} collective-permute-done((bf16[512,512]{1,0:T(8,128)(2,1)S(1)}, bf16[512,512]{1,0:T(8,128)(2,1)S(1)}, u32[]{:S(2)}, u32[]{:S(2)}) %collective-permute-start.4) | collective-permute-done | bytes 524320 | tf_op jit(solution)/shard_map/ppermute | solution.py:394
  261.5 2.8 slice.180
  270.6 5.1 multiply_convert_fusion
  275.7 3.4 fusion.21
  279.1 5.0 convolution_convert_fusion.1
  284.0 4.4 convolution_convert_fusion.2
  288.5 7.8 pad_maximum_fusion
  298.1 5.4 fusion.80
  307.7 39.0 %collective-permute-done.6 = bf16[256,1024]{1,0:T(8,128)(2,1)} collective-permute-done((bf16[256,1024]{1,0:T(8,128)(2,1)}, bf16[256,1024]{1,0:T(8,128)(2,1)}, u32[]{:S(2)}, u32[]{:S(2)}) %collective-permute-start.6) | collective-permute-done | bytes 524320 | tf_op jit(solution)/shard_map/ppermute | solution.py:394
  351.2 3.5 fusion.72
  356.6 3.6 all-to-all-start.5
  360.3 14.1 %all-to-all-done.5.g_ref = bf16[8,2,64,256]{3,2,1,0:T(8,128)(2,1)S(1)} async-done(((bf16[8,2,64,256]{3,2,1,0:T(8,128)(2,1)}), bf16[8,2,64,256]{3,2,1,0:T(8,128)(2,1)S(1)}, u32[]{:S(2)}, u32[]{:S(2)}) %all-to-all-start.5) | async-done | bytes 524320 | tf_op jit(solution)/shard_map/all_to_all | solution.py:230
  374.4 31.2 %pair_backward.2 = bf16[8,2,3,64,256]{4,3,2,1,0:T(8,128)(2,1)} custom-call(s32[2]{0:T(128)S(1)} %dynamic_slice.116.len_ref, bf16[8,2,1,64,256]{4,3,2,1,0:T(8,128)(2,1)S(1)} %copy-done.4, bf16[8,2,2,64,256]{4,3,2,1,0:T(8,128)(2,1)S(1)} %all-to-all-done.3.k_ref.v_ref, bf16[8,2,2,64,256]{4,3,2,1,0:T(8,128)(2,1)S(1)} %all-to-all-done.3.k_ref.v_ref, ...), custom_call_target="tpu_custom_call" | custom-call | flops 20132659200 | bytes 8388608 | tf_op jit(solution)/shard_map/pair_backward/pallas_call | solution.py:364
  407.8 12.2 %reduce-scatter.4.cloned.1.call-done = bf16[256,1024]{1,0:T(8,128)(2,1)} async-done(((bf16[4096,1024]{1,0:T(8,128)(2,1)}), bf16[256,1024]{1,0:T(8,128)(2,1)}) %reduce-scatter.4.cloned.1.call-update) | async-done | bytes 524304 | tf_op jit(solution)/shard_map/reduce_scatter | solution.py:580
  420.0 4.7 all-to-all-start.6
  428.2 23.5 %all-to-all-done.6 = bf16[8,2,3,64,256]{4,3,2,1,0:T(8,128)(2,1)} async-done(((bf16[8,2,3,64,256]{4,3,2,1,0:T(8,128)(2,1)}), bf16[8,2,3,64,256]{4,3,2,1,0:T(8,128)(2,1)}, u32[]{:S(2)}, u32[]{:S(2)}) %all-to-all-start.6) | async-done | bytes 1572896 | tf_op jit(solution)/shard_map/all_to_all | solution.py:230
  456.2 5.6 collective-permute-start.8
  463.8 6.7 collective-permute-done.8
  475.9 9.1 %pad_maximum_fusion.1 = bf16[2,1280,1024]{2,1,0:T(8,128)(2,1)} fusion(bf16[2,512,1024]{2,1,0:T(8,128)(2,1)S(1)} %bitcast.333, bf16[2,256,1024]{2,1,0:T(8,128)(2,1)S(1)} %bitcast.353, bf16[2,256,1024]{2,1,0:T(8,128)(2,1)S(1)} %bitcast.354, bf16[2,256,1024]{2,1,0:T(8,128)(2,1)S(1)} %bitcast.352), kind=kLoop, calls=%fused_computation.3 | loop fusion | flops 20971520 | bytes 10485760 | tf_op jit(solution)/shard_map/concatenate | solution.py:609
  485.0 3.0 convolution_convert_fusion.7
  492.1 26.3 %collective-permute-done.9 = bf16[512,1024]{1,0:T(8,128)(2,1)S(1)} collective-permute-done((bf16[512,1024]{1,0:T(8,128)(2,1)S(1)}, bf16[512,1024]{1,0:T(8,128)(2,1)S(1)}, u32[]{:S(2)}, u32[]{:S(2)}) %collective-permute-start.9) | collective-permute-done | bytes 1048608 | tf_op jit(solution)/shard_map/ppermute | solution.py:394
  520.3 3.5 all-to-all-start.7
  523.8 16.3 %collective-permute-done.11 = bf16[2,256,1024]{2,1,0:T(8,128)(2,1)S(1)} collective-permute-done((bf16[2,256,1024]{2,1,0:T(8,128)(2,1)}, bf16[2,256,1024]{2,1,0:T(8,128)(2,1)S(1)}, u32[]{:S(2)}, u32[]{:S(2)}) %collective-permute-start.11) | collective-permute-done | bytes 1048608 | tf_op jit(solution)/shard_map/ppermute | solution.py:394
  541.1 3.2 pad_maximum_fusion.6
  546.3 32.1 %pair_backward.3 = bf16[8,2,3,64,256]{4,3,2,1,0:T(8,128)(2,1)} custom-call(s32[2]{0:T(128)S(1)} %broadcast_13_len_ref.2.len_ref, bf16[8,2,3,64,256]{4,3,2,1,0:T(8,128)(2,1)} %all-to-all-done.q_ref.k_ref.v_ref, bf16[8,2,3,64,256]{4,3,2,1,0:T(8,128)(2,1)} %all-to-all-done.q_ref.k_ref.v_ref, bf16[8,2,3,64,256]{4,3,2,1,0:T(8,128)(2,1)} %all-to-all-done.q_ref.k_ref.v_ref, ...), custom_call_target="tpu_custom_call" | custom-call | flops 30198988800 | bytes 8388608 | tf_op jit(solution)/shard_map/pair_backward/pallas_call | solution.py:364
  578.5 8.6 %all-to-all-start.8 = ((bf16[8,2,3,64,256]{4,3,2,1,0:T(8,128)(2,1)}), bf16[8,2,3,64,256]{4,3,2,1,0:T(8,128)(2,1)}, u32[]{:S(2)}, u32[]{:S(2)}) async-start(bf16[8,2,3,64,256]{4,3,2,1,0:T(8,128)(2,1)} %pair_backward.3), calls=%async_computation.10 | async-start | bytes 3145728 | tf_op jit(solution)/shard_map/all_to_all | solution.py:230
  588.4 25.7 %collective-permute-done.12 = bf16[2,256,768]{2,1,0:T(8,128)(2,1)S(1)} collective-permute-done((bf16[2,256,768]{2,1,0:T(8,128)(2,1)S(1)}, bf16[2,256,768]{2,1,0:T(8,128)(2,1)S(1)}, u32[]{:S(2)}, u32[]{:S(2)}) %collective-permute-start.12) | collective-permute-done | bytes 786464 | tf_op jit(solution)/shard_map/ppermute | solution.py:394
  618.7 3.0 copy.116
  632.5 4.2 fusion.7
  642.6 9.0 %collective-permute-done.14 = bf16[256,1024]{1,0:T(8,128)(2,1)S(1)} collective-permute-done((bf16[256,1024]{1,0:T(8,128)(2,1)S(1)}, bf16[256,1024]{1,0:T(8,128)(2,1)S(1)}, u32[]{:S(2)}, u32[]{:S(2)}) %collective-permute-start.14) | collective-permute-done | bytes 524320 | tf_op jit(solution)/shard_map/ppermute | solution.py:394
  656.3 3.8 reverse_select_fusion.3
  660.5 4.4 slice_convert_fusion
  665.0 16.2 %collective-permute-done.15 = bf16[256,1024]{1,0:T(8,128)(2,1)S(1)} collective-permute-done((bf16[256,1024]{1,0:T(8,128)(2,1)}, bf16[256,1024]{1,0:T(8,128)(2,1)S(1)}, u32[]{:S(2)}, u32[]{:S(2)}) %collective-permute-start.15) | collective-permute-done | bytes 524320 | tf_op jit(solution)/shard_map/ppermute | solution.py:394
  682.3 19.3 %reduce-scatter.8.cloned.1.call-done = bf16[2,128,1024]{2,1,0:T(8,128)(2,1)} async-done(((bf16[2,1024,1024]{2,1,0:T(8,128)(2,1)}), bf16[2,128,1024]{2,1,0:T(8,128)(2,1)}) %reduce-scatter.8.cloned.1.call-update) | async-done | bytes 524304 | tf_op jit(solution)/shard_map/reduce_scatter | solution.py:562
  707.0 5.4 copy.128
  712.9 4.4 collective-permute-done.19
  724.8 11.0 %all-gather.2 = bf16[16,80,256]{2,1,0:T(8,128)(2,1)S(1)} all-gather(bf16[2,80,256]{2,1,0:T(8,128)(2,1)S(1)} %pad_maximum_fusion.22), channel_id=4, replica_groups=mesh['far'=2,'near'=2,'rows'=8] {'rows'}, dimensions={0}, use_global_device_ids=true | all-gather | bytes 737280 | tf_op jit(solution)/shard_map/all_gather | solution.py:647
  748.7 2.9 copy.126
  751.6 14.7 %collective-permute-done.16 = bf16[2,256,1024]{2,1,0:T(8,128)(2,1)} collective-permute-done((bf16[2,256,1024]{2,1,0:T(8,128)(2,1)}, bf16[2,256,1024]{2,1,0:T(8,128)(2,1)}, u32[]{:S(2)}, u32[]{:S(2)}) %collective-permute-start.16) | collective-permute-done | bytes 1048608 | tf_op jit(solution)/shard_map/ppermute | solution.py:394
  776.2 3.7 copy.124
  (371 shorter events, 169.8 us)
Async XLA Ops:
  7.2 241.3 %copy-start = (bf16[4,256,1024]{2,1,0:T(8,128)(2,1)S(1)}, bf16[4,256,1024]{2,1,0:T(8,128)(2,1)}, u32[]{:S(2)}) copy-start(bf16[4,256,1024]{2,1,0:T(8,128)(2,1)} %param.31) | copy-start | bytes 6291460
  7.2 65.5 %all-gather.10.cloned.1.call-start = ((), (), s32[]{:S(2)}) async-start(), calls=%async_computation.12 | async-start | bytes 1769472 | tf_op jit(solution)/shard_map/all_gather | solution.py:444
  10.0 8.4 %copy-start.65 = (s32[4,256]{1,0:T(4,128)S(1)}, s32[4,256]{1,0:T(4,128)}, u32[]{:S(2)}) copy-start(s32[4,256]{1,0:T(4,128)} %param.17) | copy-start | bytes 12292
  12.7 18.1 %copy-start.61 = (bf16[32,2,1024]{2,1,0:T(2,128)(2,1)S(1)}, bf16[32,2,1024]{2,1,0:T(2,128)(2,1)}, u32[]{:S(2)}) copy-start(bf16[32,2,1024]{2,1,0:T(2,128)(2,1)} %param.20) | copy-start | bytes 393220
  12.7 20.0 %copy-start.50 = (bf16[2,1024,256]{2,1,0:T(8,128)(2,1)S(1)}, bf16[2,1024,256]{2,1,0:T(8,128)(2,1)}, u32[]{:S(2)}) copy-start(bf16[2,1024,256]{2,1,0:T(8,128)(2,1)} %param.25) | copy-start | bytes 3145732
  14.4 13.4 %collective-permute-start = (bf16[96,1024]{1,0:T(8,128)(2,1)}, bf16[96,1024]{1,0:T(8,128)(2,1)S(1)}, u32[]{:S(2)}, u32[]{:S(2)}) collective-permute-start(bf16[96,1024]{1,0:T(8,128)(2,1)} %constant_dynamic-slice_fusion.20), channel_id=1, source_target_pairs={{0,16},{16,0},{1,17},{17,1},{2,18},{18,2},{3,19},{19,3},{4,20},{20... | collective-permute-start | bytes 589832 | tf_op jit(solution)/shard_map/ppermute | solution.py:394
  19.9 11.5 %copy-start.62 = (f32[2,256]{1,0:T(2,128)}, f32[2,256]{1,0:T(2,128)S(1)}, u32[]{:S(2)}) copy-start(f32[2,256]{1,0:T(2,128)S(1)} %get-tuple-element.182) | copy-start | bytes 6148
  28.4 126.6 %all-gather.18.cloned.1.call-start = ((), (), s32[]{:S(2)}) async-start(), calls=%async_computation.19 | async-start | bytes 8257536 | tf_op jit(solution)/shard_map/all_gather | solution.py:522
  39.9 38.7 %copy-start.52 = (bf16[512,1024]{1,0:T(8,128)(2,1)}, bf16[512,1024]{1,0:T(8,128)(2,1)S(1)}, u32[]{:S(2)}) copy-start(bf16[512,1024]{1,0:T(8,128)(2,1)S(1)} %get-tuple-element.50) | copy-start | bytes 3145732
  40.7 17.1 %collective-permute-start.1 = (bf16[160,1024]{1,0:T(8,128)(2,1)}, bf16[160,1024]{1,0:T(8,128)(2,1)}, u32[]{:S(2)}, u32[]{:S(2)}) collective-permute-start(bf16[160,1024]{1,0:T(8,128)(2,1)} %pad_maximum_fusion.20), channel_id=1, source_target_pairs={{0,16},{16,0},{1,17},{17,1},{2,18},{18,2},{3,19},{19,3},{4,20},{20... | collective-permute-start | bytes 983048 | tf_op jit(solution)/shard_map/ppermute | solution.py:394
  58.8 9.5 %collective-permute-start.2 = (bf16[2,96,1024]{2,1,0:T(8,128)(2,1)S(1)}, bf16[2,96,1024]{2,1,0:T(8,128)(2,1)S(1)}, u32[]{:S(2)}, u32[]{:S(2)}) collective-permute-start(bf16[2,96,1024]{2,1,0:T(8,128)(2,1)S(1)} %fusion.58), channel_id=1, source_target_pairs={{0,8},{8,0},{1,9},{9,1},{2,10},{10,2},{3,11},{11,3},{4,12},{12,4},... | collective-permute-start | bytes 1179656 | tf_op jit(solution)/shard_map/ppermute | solution.py:394
  82.8 29.7 %all-to-all-start = ((bf16[8,2,3,64,256]{4,3,2,1,0:T(8,128)(2,1)}), bf16[8,2,3,64,256]{4,3,2,1,0:T(8,128)(2,1)}, u32[]{:S(2)}, u32[]{:S(2)}) async-start(bf16[8,2,3,64,256]{4,3,2,1,0:T(8,128)(2,1)} %pad_maximum_fusion.8), calls=%async_computation | async-start | bytes 3145728 | tf_op jit(solution)/shard_map/all_to_all | solution.py:230
  87.1 174.3 %all-gather.20.cloned.1.call-start = ((), (), s32[]{:S(2)}) async-start(), calls=%async_computation.20 | async-start | bytes 8912896 | tf_op jit(solution)/shard_map/all_gather | solution.py:536
  136.6 16.1 %all-to-all-start.1 = ((bf16[8,2,64,256]{3,2,1,0:T(8,128)(2,1)}), bf16[8,2,64,256]{3,2,1,0:T(8,128)(2,1)S(1)}, u32[]{:S(2)}, u32[]{:S(2)}) async-start(bf16[8,2,64,256]{3,2,1,0:T(8,128)(2,1)} %get-tuple-element.56), calls=%async_computation.1 | async-start | bytes 1048576 | tf_op jit(solution)/shard_map/all_to_all | solution.py:230
  153.4 17.4 %copy-start.34 = (bf16[64,8,2,256]{3,1,2,0:T(8,128)(2,1)}, bf16[64,8,2,256]{3,1,2,0:T(8,128)(2,1)S(1)}, u32[]{:S(2)}) copy-start(bf16[64,8,2,256]{3,1,2,0:T(8,128)(2,1)S(1)} %copy.138) | copy-start | bytes 1572868
  153.4 17.4 %collective-permute-start.3 = (bf16[512,512]{1,0:T(8,128)(2,1)S(1)}, bf16[512,512]{1,0:T(8,128)(2,1)S(1)}, u32[]{:S(2)}, u32[]{:S(2)}) collective-permute-start(bf16[512,512]{1,0:T(8,128)(2,1)S(1)} %bitcast.334), channel_id=1, source_target_pairs={{0,8},{8,0},{1,9},{9,1},{2,10},{10,2},{3,11},{11,3},{4,12},{12,4},... | collective-permute-start | bytes 1572872 | tf_op jit(solution)/shard_map/ppermute | solution.py:394
  175.5 19.7 %all-to-all-start.2 = ((bf16[8,2,1,64,256]{4,3,2,1,0:T(8,128)(2,1)}), bf16[8,2,1,64,256]{4,3,2,1,0:T(8,128)(2,1)S(1)}, u32[]{:S(2)}, u32[]{:S(2)}) async-start(bf16[8,2,1,64,256]{4,3,2,1,0:T(8,128)(2,1)} %pad_maximum_fusion.18), calls=%async_computation.2 | async-start | bytes 1048576 | tf_op jit(solution)/shard_map/all_to_all | solution.py:230
  187.3 12.4 %copy-start.71 = (s32[4]{0:T(128)S(1)}, s32[4]{0:T(128)}, u32[]{:S(2)}) copy-start(s32[4]{0:T(128)} %param.19) | copy-start | bytes 52
  196.0 19.3 %all-to-all-start.3 = ((bf16[8,2,2,64,256]{4,3,2,1,0:T(8,128)(2,1)}), bf16[8,2,2,64,256]{4,3,2,1,0:T(8,128)(2,1)S(1)}, u32[]{:S(2)}, u32[]{:S(2)}) async-start(bf16[8,2,2,64,256]{4,3,2,1,0:T(8,128)(2,1)} %pad_maximum_fusion.12), calls=%async_computation.3 | async-start | bytes 2097152 | tf_op jit(solution)/shard_map/all_to_all | solution.py:230
  199.6 220.4 %reduce-scatter.4.cloned.1.call-start = ((), (), s32[]{:S(2)}) async-start(), calls=%async_computation.13 | async-start | bytes 8912896 | tf_op jit(solution)/shard_map/reduce_scatter | solution.py:580
  233.5 16.0 %copy-start.5 = (f32[8,2,64,256]{3,2,1,0:T(8,128)}, f32[8,2,64,256]{3,2,1,0:T(8,128)S(1)}, u32[]{:S(2)}) copy-start(f32[8,2,64,256]{3,2,1,0:T(8,128)S(1)} %get-tuple-element.63.wide_ref) | copy-start | bytes 3145732
  233.5 14.9 %copy-start.68 = (bf16[1024]{0:T(1024)(128)(2,1)S(1)}, bf16[1024]{0:T(1024)(128)(2,1)}, u32[]{:S(2)}) copy-start(bf16[1024]{0:T(1024)(128)(2,1)} %param.28) | copy-start | bytes 6148
  246.5 13.3 %copy-start.57 = (bf16[64,8,2,256]{3,1,2,0:T(8,128)(2,1)}, bf16[64,8,2,256]{3,1,2,0:T(8,128)(2,1)S(1)}, u32[]{:S(2)}) copy-start(bf16[64,8,2,256]{3,1,2,0:T(8,128)(2,1)S(1)} %copy.139) | copy-start | bytes 1572868
  246.5 13.2 %collective-permute-start.4 = (bf16[512,512]{1,0:T(8,128)(2,1)S(1)}, bf16[512,512]{1,0:T(8,128)(2,1)S(1)}, u32[]{:S(2)}, u32[]{:S(2)}) collective-permute-start(bf16[512,512]{1,0:T(8,128)(2,1)S(1)} %bitcast.368), channel_id=1, source_target_pairs={{0,8},{8,0},{1,9},{9,1},{2,10},{10,2},{3,11},{11,3},{4,12},{12,4},... | collective-permute-start | bytes 1572872 | tf_op jit(solution)/shard_map/ppermute | solution.py:394
  249.5 10.2 %copy-start.10 = (f32[512,1024]{1,0:T(8,128)S(1)}, f32[512,1024]{1,0:T(8,128)}, u32[]{:S(2)}) copy-start(f32[512,1024]{1,0:T(8,128)} %copy-done.9) | copy-start | bytes 6291460
  275.7 8.3 %copy-start.72 = (bf16[512,2048]{1,0:T(8,128)(2,1)}, bf16[512,2048]{1,0:T(8,128)(2,1)S(1)}, u32[]{:S(2)}) copy-start(bf16[512,2048]{1,0:T(8,128)(2,1)S(1)} %get-tuple-element.61) | copy-start | bytes 6291460
  296.3 52.6 %collective-permute-start.5 = (bf16[512,1024]{1,0:T(8,128)(2,1)}, bf16[512,1024]{1,0:T(8,128)(2,1)}, u32[]{:S(2)}, u32[]{:S(2)}) collective-permute-start(bf16[512,1024]{1,0:T(8,128)(2,1)} %fusion.21), channel_id=1, source_target_pairs={{0,8},{8,0},{1,9},{9,1},{2,10},{10,2},{3,11},{11,3},{4,12},{12,4},... | collective-permute-start | bytes 3145736 | tf_op jit(solution)/shard_map/ppermute | solution.py:394
  305.7 41.1 %collective-permute-start.6 = (bf16[256,1024]{1,0:T(8,128)(2,1)}, bf16[256,1024]{1,0:T(8,128)(2,1)}, u32[]{:S(2)}, u32[]{:S(2)}) collective-permute-start(bf16[256,1024]{1,0:T(8,128)(2,1)} %bitcast.46), channel_id=1, source_target_pairs={{0,8},{8,0},{1,9},{9,1},{2,10},{10,2},{3,11},{11,3},{4,12},{12,4},... | collective-permute-start | bytes 1572872 | tf_op jit(solution)/shard_map/ppermute | solution.py:394
  307.7 41.2 %copy-start.25 = (bf16[512,1024]{1,0:T(8,128)(2,1)S(1)}, bf16[512,1024]{1,0:T(8,128)(2,1)}, u32[]{:S(2)}) copy-start(bf16[512,1024]{1,0:T(8,128)(2,1)} %fusion.21) | copy-start | bytes 3145732
  355.2 19.2 %copy-start.4 = (bf16[8,2,1,64,256]{4,3,2,1,0:T(8,128)(2,1)S(1)}, bf16[8,2,1,64,256]{4,3,2,1,0:T(8,128)(2,1)}, u32[]{:S(2)}) copy-start(bf16[8,2,1,64,256]{4,3,2,1,0:T(8,128)(2,1)} %copy-done.2) | copy-start | bytes 1572868
  355.2 19.2 %copy-start.6 = (f32[8,2,64,256]{3,2,1,0:T(8,128)S(1)}, f32[8,2,64,256]{3,2,1,0:T(8,128)}, u32[]{:S(2)}) copy-start(f32[8,2,64,256]{3,2,1,0:T(8,128)} %copy-done.5) | copy-start | bytes 3145732
  356.6 17.8 %all-to-all-start.5 = ((bf16[8,2,64,256]{3,2,1,0:T(8,128)(2,1)}), bf16[8,2,64,256]{3,2,1,0:T(8,128)(2,1)S(1)}, u32[]{:S(2)}, u32[]{:S(2)}) async-start(bf16[8,2,64,256]{3,2,1,0:T(8,128)(2,1)} %maximum_bitcast_fusion), calls=%async_computation.5 | async-start | bytes 1048576 | tf_op jit(solution)/shard_map/all_to_all | solution.py:230
  360.2 218.3 %all-gather.12.cloned.1.call-start = ((), (), s32[]{:S(2)}) async-start(), calls=%async_computation.14 | async-start | bytes 4718592 | tf_op jit(solution)/shard_map/all_gather | solution.py:444
  360.2 45.4 %collective-permute-start.7 = (bf16[256,1024]{1,0:T(8,128)(2,1)}, bf16[256,1024]{1,0:T(8,128)(2,1)}, u32[]{:S(2)}, u32[]{:S(2)}) collective-permute-start(bf16[256,1024]{1,0:T(8,128)(2,1)} %fusion.42), channel_id=1, source_target_pairs={{0,16},{16,0},{1,17},{17,1},{2,18},{18,2},{3,19},{19,3},{4,20},{20... | collective-permute-start | bytes 1572872 | tf_op jit(solution)/shard_map/ppermute | solution.py:394
  374.4 31.2 %copy-start.38 = (bf16[256,1024]{1,0:T(8,128)(2,1)S(1)}, bf16[256,1024]{1,0:T(8,128)(2,1)}, u32[]{:S(2)}) copy-start(bf16[256,1024]{1,0:T(8,128)(2,1)} %fusion.42) | copy-start | bytes 1572868
  407.8 17.0 %copy-start.16 = (bf16[1,4,8,32,1024]{4,3,0,1,2:T(8,128)(2,1)S(1)}, bf16[1,4,8,32,1024]{4,3,0,1,2:T(8,128)(2,1)}, u32[]{:S(2)}) copy-start(bf16[1,4,8,32,1024]{4,3,0,1,2:T(8,128)(2,1)} %get-tuple-element.161) | copy-start | bytes 6291460
  420.0 31.7 %all-to-all-start.6 = ((bf16[8,2,3,64,256]{4,3,2,1,0:T(8,128)(2,1)}), bf16[8,2,3,64,256]{4,3,2,1,0:T(8,128)(2,1)}, u32[]{:S(2)}, u32[]{:S(2)}) async-start(bf16[8,2,3,64,256]{4,3,2,1,0:T(8,128)(2,1)} %pair_backward.2), calls=%async_computation.7 | async-start | bytes 3145728 | tf_op jit(solution)/shard_map/all_to_all | solution.py:230
  424.7 153.8 %reduce-scatter.6.cloned.1.call-start = ((), (), s32[]{:S(2)}) async-start(), calls=%async_computation.15 | async-start | bytes 5898240 | tf_op jit(solution)/shard_map/reduce_scatter | solution.py:562
  454.3 7.4 copy-start.44
  456.2 14.3 %collective-permute-start.8 = (bf16[512,512]{1,0:T(8,128)(2,1)S(1)}, bf16[512,512]{1,0:T(8,128)(2,1)S(1)}, u32[]{:S(2)}, u32[]{:S(2)}) collective-permute-start(bf16[512,512]{1,0:T(8,128)(2,1)S(1)} %bitcast.371), channel_id=1, source_target_pairs={{0,8},{8,0},{1,9},{9,1},{2,10},{10,2},{3,11},{11,3},{4,12},{12,4},... | collective-permute-start | bytes 1572872 | tf_op jit(solution)/shard_map/ppermute | solution.py:394
  462.5 7.9 %copy-start.11 = (f32[512,1024]{1,0:T(8,128)S(1)}, f32[512,1024]{1,0:T(8,128)}, u32[]{:S(2)}) copy-start(f32[512,1024]{1,0:T(8,128)} %copy-done.9) | copy-start | bytes 6291460
  462.5 7.9 %copy-start.36 = (bf16[1,4,8,32,1024]{4,3,2,1,0:T(8,128)(2,1)S(1)}, bf16[1,4,8,32,1024]{4,3,2,1,0:T(8,128)(2,1)}, u32[]{:S(2)}) copy-start(bf16[1,4,8,32,1024]{4,3,2,1,0:T(8,128)(2,1)} %copy.112) | copy-start | bytes 6291460
  488.0 30.4 %collective-permute-start.9 = (bf16[512,1024]{1,0:T(8,128)(2,1)S(1)}, bf16[512,1024]{1,0:T(8,128)(2,1)S(1)}, u32[]{:S(2)}, u32[]{:S(2)}) collective-permute-start(bf16[512,1024]{1,0:T(8,128)(2,1)S(1)} %convolution_convert_fusion.7), channel_id=1, source_target_pairs={{0,8},{8,0},{1,9},{9,1},{2,10},{10,2},{3,11},{11,3},{4,12},{12,4},... | collective-permute-start | bytes 3145736 | tf_op jit(solution)/shard_map/ppermute | solution.py:394
  489.9 50.2 %collective-permute-start.11 = (bf16[2,256,1024]{2,1,0:T(8,128)(2,1)}, bf16[2,256,1024]{2,1,0:T(8,128)(2,1)S(1)}, u32[]{:S(2)}, u32[]{:S(2)}) collective-permute-start(bf16[2,256,1024]{2,1,0:T(8,128)(2,1)} %pad_maximum_fusion.13), channel_id=1, source_target_pairs={{0,8},{8,0},{1,9},{9,1},{2,10},{10,2},{3,11},{11,3},{4,12},{12,4},... | collective-permute-start | bytes 3145736 | tf_op jit(solution)/shard_map/ppermute | solution.py:394
  492.1 26.8 %copy-start.70 = (bf16[768,1024]{1,0:T(8,128)(2,1)S(1)}, bf16[768,1024]{1,0:T(8,128)(2,1)}, u32[]{:S(2)}) copy-start(bf16[768,1024]{1,0:T(8,128)(2,1)} %param.27) | copy-start | bytes 4718596
  520.3 24.0 %collective-permute-start.10 = (bf16[256,768]{1,0:T(8,128)(2,1)}, bf16[256,768]{1,0:T(8,128)(2,1)}, u32[]{:S(2)}, u32[]{:S(2)}) collective-permute-start(bf16[256,768]{1,0:T(8,128)(2,1)} %convolution_convert_fusion.15), channel_id=1, source_target_pairs={{0,16},{16,0},{1,17},{17,1},{2,18},{18,2},{3,19},{19,3},{4,20},{20... | collective-permute-start | bytes 1179656 | tf_op jit(solution)/shard_map/ppermute | solution.py:394
  520.3 26.0 %all-to-all-start.7 = ((bf16[8,2,64,256]{3,2,1,0:T(8,128)(2,1)}), bf16[8,2,64,256]{3,2,1,0:T(8,128)(2,1)S(1)}, u32[]{:S(2)}, u32[]{:S(2)}) async-start(bf16[8,2,64,256]{3,2,1,0:T(8,128)(2,1)} %maximum_bitcast_fusion.1), calls=%async_computation.8 | async-start | bytes 1048576 | tf_op jit(solution)/shard_map/all_to_all | solution.py:230
  578.4 8.7 %copy-start.33 = (bf16[2,256,768]{2,1,0:T(8,128)(2,1)S(1)}, bf16[2,256,768]{2,1,0:T(8,128)(2,1)}, u32[]{:S(2)}) copy-start(bf16[2,256,768]{2,1,0:T(8,128)(2,1)} %pad_maximum_fusion.17) | copy-start | bytes 2359300
  578.5 8.7 %copy-start.54 = (bf16[2,160,1024]{2,1,0:T(8,128)(2,1)S(1)}, bf16[2,160,1024]{2,1,0:T(8,128)(2,1)}, u32[]{:S(2)}) copy-start(bf16[2,160,1024]{2,1,0:T(8,128)(2,1)} %reduce-scatter.6.cloned.1.call-done) | copy-start | bytes 1966084
  578.5 36.9 %all-to-all-start.8 = ((bf16[8,2,3,64,256]{4,3,2,1,0:T(8,128)(2,1)}), bf16[8,2,3,64,256]{4,3,2,1,0:T(8,128)(2,1)}, u32[]{:S(2)}, u32[]{:S(2)}) async-start(bf16[8,2,3,64,256]{4,3,2,1,0:T(8,128)(2,1)} %pair_backward.3), calls=%async_computation.10 | async-start | bytes 3145728 | tf_op jit(solution)/shard_map/all_to_all | solution.py:230
  587.1 69.2 %all-gather.14.cloned.1.call-start = ((), (), s32[]{:S(2)}) async-start(), calls=%async_computation.17 | async-start | bytes 2949120 | tf_op jit(solution)/shard_map/all_gather | solution.py:444
  587.1 27.0 %collective-permute-start.12 = (bf16[2,256,768]{2,1,0:T(8,128)(2,1)S(1)}, bf16[2,256,768]{2,1,0:T(8,128)(2,1)S(1)}, u32[]{:S(2)}, u32[]{:S(2)}) collective-permute-start(bf16[2,256,768]{2,1,0:T(8,128)(2,1)S(1)} %copy-done.33), channel_id=1, source_target_pairs={{0,8},{8,0},{1,9},{9,1},{2,10},{10,2},{3,11},{11,3},{4,12},{12,4},... | collective-permute-start | bytes 2359304 | tf_op jit(solution)/shard_map/ppermute | solution.py:394
  587.2 28.2 %collective-permute-start.13 = (bf16[160,1024]{1,0:T(8,128)(2,1)S(1)}, bf16[160,1024]{1,0:T(8,128)(2,1)S(1)}, u32[]{:S(2)}, u32[]{:S(2)}) collective-permute-start(bf16[160,1024]{1,0:T(8,128)(2,1)S(1)} %dynamic-slice_bitcast_fusion), channel_id=1, source_target_pairs={{0,16},{16,0},{1,17},{17,1},{2,18},{18,2},{3,19},{19,3},{4,20},{20... | collective-permute-start | bytes 983048 | tf_op jit(solution)/shard_map/ppermute | solution.py:394
  617.2 84.3 %reduce-scatter.8.cloned.1.call-start = ((), (), s32[]{:S(2)}) async-start(), calls=%async_computation.16 | async-start | bytes 4718592 | tf_op jit(solution)/shard_map/reduce_scatter | solution.py:562
  627.3 143.9 %all-gather.16.cloned.1.call-start = ((), (), s32[]{:S(2)}) async-start(), calls=%async_computation.18 | async-start | bytes 2359296 | tf_op jit(solution)/shard_map/all_gather | solution.py:444
  638.1 13.6 %collective-permute-start.14 = (bf16[256,1024]{1,0:T(8,128)(2,1)S(1)}, bf16[256,1024]{1,0:T(8,128)(2,1)S(1)}, u32[]{:S(2)}, u32[]{:S(2)}) collective-permute-start(bf16[256,1024]{1,0:T(8,128)(2,1)S(1)} %bitcast.374), channel_id=1, source_target_pairs={{0,8},{8,0},{1,9},{9,1},{2,10},{10,2},{3,11},{11,3},{4,12},{12,4},... | collective-permute-start | bytes 1572872 | tf_op jit(solution)/shard_map/ppermute | solution.py:394
  656.2 24.9 %collective-permute-start.15 = (bf16[256,1024]{1,0:T(8,128)(2,1)}, bf16[256,1024]{1,0:T(8,128)(2,1)S(1)}, u32[]{:S(2)}, u32[]{:S(2)}) collective-permute-start(bf16[256,1024]{1,0:T(8,128)(2,1)} %fusion.40), channel_id=1, source_target_pairs={{0,16},{16,0},{1,17},{17,1},{2,18},{18,2},{3,19},{19,3},{4,20},{20... | collective-permute-start | bytes 1572872 | tf_op jit(solution)/shard_map/ppermute | solution.py:394
  660.5 20.7 %copy-start.37 = (bf16[256,1024]{1,0:T(8,128)(2,1)S(1)}, bf16[256,1024]{1,0:T(8,128)(2,1)}, u32[]{:S(2)}) copy-start(bf16[256,1024]{1,0:T(8,128)(2,1)} %fusion.40) | copy-start | bytes 1572868
  702.5 14.7 %collective-permute-start.19 = (bf16[128,1024]{1,0:T(8,128)(2,1)S(1)}, bf16[128,1024]{1,0:T(8,128)(2,1)}, u32[]{:S(2)}, u32[]{:S(2)}) collective-permute-start(bf16[128,1024]{1,0:T(8,128)(2,1)S(1)} %dynamic-slice_bitcast_fusion.1), channel_id=1, source_target_pairs={{0,16},{16,0},{1,17},{17,1},{2,18},{18,2},{3,19},{19,3},{4,20},{20... | collective-permute-start | bytes 786440 | tf_op jit(solution)/shard_map/ppermute | solution.py:394
  707.0 10.3 %copy-start.59 = (bf16[2,128,1024]{2,1,0:T(8,128)(2,1)S(1)}, bf16[2,128,1024]{2,1,0:T(8,128)(2,1)}, u32[]{:S(2)}) copy-start(bf16[2,128,1024]{2,1,0:T(8,128)(2,1)} %reduce-scatter.8.cloned.1.call-done) | copy-start | bytes 1572868
  712.4 6.7 copy-start.32
  719.6 5.0 collective-permute-start.17
  735.9 6.7 collective-permute-start.18
  740.8 25.5 %collective-permute-start.16 = (bf16[2,256,1024]{2,1,0:T(8,128)(2,1)}, bf16[2,256,1024]{2,1,0:T(8,128)(2,1)}, u32[]{:S(2)}, u32[]{:S(2)}) collective-permute-start(bf16[2,256,1024]{2,1,0:T(8,128)(2,1)} %pad_maximum_fusion.14), channel_id=1, source_target_pairs={{0,8},{8,0},{1,9},{9,1},{2,10},{10,2},{3,11},{11,3},{4,12},{12,4},... | collective-permute-start | bytes 3145736 | tf_op jit(solution)/shard_map/ppermute | solution.py:394
  (50 other events, 116.2 us)
Sparse Core Ops, SparseCore 0:
  28.5 26.8 all-gather.9
  69.4 59.4 all-gather.17
  131.8 83.6 all-gather.19
  296.4 123.4 reduce-scatter.3
  421.7 48.9 all-gather.11
  485.1 57.2 reduce-scatter.5
  617.4 28.4 all-gather.13
  650.2 51.3 reduce-scatter.7
  719.1 29.1 all-gather.15

commit v7 on v6

--- a/solution.py
+++ b/solution.py
@@ -555,7 +555,9 @@
     grad_pre = act_back(mul(grad_low, narrow, NT))[0].astype(LOW)
     third, activated, grad_pre = tie(mul(grad_pre, widen, NT).astype(LOW), activated, grad_pre)
     grad_three = third.astype(WIDE) + swap(third, "near").astype(WIDE)
-    hidden_half = half_sum_near(mul(activated, narrow))
+    hidden_mine, hidden_away = halves(mul(activated, narrow))
+    hidden_away, grad_three = tie(hidden_away.astype(LOW), grad_three)
+    hidden_half = hidden_mine + swap(hidden_away, "near").astype(WIDE)
     result = (halves(after_cross)[0] + hidden_half).astype(LOW)
 
     def part_rows(both):
@@ -586,12 +588,13 @@
         grad_three * hidden_gain_f, unit_three, rate_three
     )
     grad_cross_low = grad_cross.astype(LOW)
-    grad_mixed, result = tie(to_pairs(cross_whole[: 2 * cols], grad_cross_low, 1)[:, :, 0], result)
+    grad_mixed = exchange_rows(to_pairs(cross_whole[: 2 * cols], grad_cross_low, 1)[:, :, 0])
+    grad_mixed, result = tie(grad_mixed, result)
     result_two = jnp.stack([result, swap(result, "far")])
-    grads = pair_backward(cross_q, pair, 0, length, exchange_rows(grad_mixed), cross_wide, cross_log)
-    grads, result_two, hidden_part = tie(grads, result_two, hidden_part)
+    grads = pair_backward(cross_q, pair, 0, length, grad_mixed, cross_wide, cross_log)
+    grads, result_two = tie(grads, result_two)
     result_four = jnp.stack([result_two, swap(result_two, "near")])
-    grads = exchange_rows(grads)
+    grads, result_four, hidden_part = tie(exchange_rows(grads), result_four, hidden_part)
     hidden_total = join_rows(hidden_part)
     grad_cq_t = from_pairs(grads[:, :, :1])
     grad_pair_t = from_pairs(grads[:, :, 1:])
@@ -605,6 +608,7 @@
     patch_half = mul(halves(grad_mid)[0], patch_weights, NT).astype(LOW)
     patch_terms = jnp.stack([mul(value, patch_in, TN).astype(LOW) for value in both_columns(grad_mid)])
     patch_terms = jnp.pad(patch_terms, ((0, 0), (0, 0), (0, width - patch_width)))
+    grad_mixed, grad_self_low = tie(to_pairs(self_whole[: 2 * cols], grad_self_low, 1)[:, :, 0], grad_self_low)
     middle_part = part_rows(
         jnp.concatenate(
             [
@@ -616,19 +620,19 @@
             axis=1,
         )
     )
-    grad_mixed, patch_half = tie(to_pairs(self_whole[: 2 * cols], grad_self_low, 1)[:, :, 0], patch_half)
+    grad_mixed, patch_half = tie(exchange_rows(grad_mixed), patch_half)
     patch_two = jnp.stack([patch_half, swap(patch_half, "far")])
-    grads = pair_backward(qkv, qkv, 1, None, exchange_rows(grad_mixed), self_wide, self_log)
-    grads, patch_two, result_four, hidden_total, middle_part = tie(
-        grads, patch_two, result_four, hidden_total, middle_part
-    )
+    grads = pair_backward(qkv, qkv, 1, None, grad_mixed, self_wide, self_log)
+    grads, patch_two, hidden_total, middle_part = tie(grads, patch_two, hidden_total, middle_part)
     middle_own, middle_away = own_and_away(middle_part)
     patch_four = jnp.stack([patch_two, swap(patch_two, "near")])
     grads, patch_four, middle_away = tie(exchange_rows(grads), patch_four, swap(middle_away, "far"))
+    grad_qkv_t = from_pairs(grads)
+    last_terms = jnp.concatenate([by_shard(grad_qkv_t, normed_one), patch_terms], axis=1)
+    last_part = part_rows(last_terms)
+    grad_one = half_sum_near(mul(grad_qkv_t, qkv_both, TN))
+    grad_one, middle_own = tie(grad_one, middle_own)
     middle_total = join_rows(add_far(middle_own, middle_away))
-    grad_qkv_t = from_pairs(grads)
-    last_part = part_rows(jnp.concatenate([by_shard(grad_qkv_t, normed_one), patch_terms], axis=1))
-    grad_one = half_sum_near(mul(grad_qkv_t, qkv_both, TN))
     gain_half, unit_half, rate_half, self_half = (
         halves(value)[0] for value in (gain_one, unit_one, rate_one, grad_self)
     )
@@ -649,7 +653,6 @@
         lax.dynamic_index_in_dim(small, index, 0, keepdims=False) for index in (far, 1 - far)
     )
     small = small_own.astype(WIDE) + swap(small_away, "far").astype(WIDE)
-    input_half, middle_total = tie(input_half, middle_total)
     input_two = jnp.stack([input_half, swap(input_half, "far")])
     last_part, input_two = tie(last_part, input_two)
     input_grads = over_heads(jnp.stack([input_two, swap(input_two, "near")]))

time: 795 us -> 722 us (0.908)
  waiting for transfers between devices: 331 us -> 289 us
  Pallas kernels: 99.5 us -> 86.5 us
    all_to_all x8, waiting for transfers between devices: 90.3 us -> 62.5 us  [exchange_rows(): return lax.all_to_all(value, 'rows', 0, 0, tiled=True)]
    reduce_scatter x2, waiting for transfers between devices: 19.3 us -> 0.02 us  [part_rows(): return lax.psum_scatter(both, 'rows', scatter_dimension=1, tiled=True)]
    ppermute x20, waiting for transfers between devices: 209 us -> 227 us  [swap(): return lax.ppermute(value, axis, [(0, 1), (1, 0)])]
    reduce_scatter x1, waiting for transfers between devices: 12.2 us -> 0.01 us  [paired_device(): lax.psum_scatter(hidden_terms.reshape(-1, width), ('far', 'rows'), scatte...]
    pallas_call x2, Pallas kernels: 63.3 us -> 53.9 us  [pair_backward(): pl.pallas_call(kernel, grid_spec=pltpu.PrefetchScalarGridSpec(num_scalar_...]
    unnamed x169 -> x149, local copies, waits for them, and re-layouts: 38.6 us -> 37.2 us
  transfers between devices with their start and end apart: 37 -> 37, of which waited for: 23 -> 22; matrix products, arithmetic and copies ran while one was open for 23% -> 24% of each run, Pallas kernels for 13% -> 12%
where the time goes in v7:
time: 722 us; the launch traced here: 714 us
  waiting for transfers between devices  289 us (40%)
  local copies, waits for them, and re-layouts  99.2 us (14%)
  Pallas kernels  86.5 us (12%)
  other arithmetic  79.8 us (11%)
  matrix products  61.4 us (9%)
  starting transfers between devices  59.1 us (8%)
  blocking collectives  23.3 us (3%)
  between operations  15.4 us (2%)
    ppermute x20, waiting for transfers between devices, swap(): return lax.ppermute(value, axis, [(0, 1), (1, 0)])  227 us
    all_to_all x8, waiting for transfers between devices, exchange_rows(): return lax.all_to_all(value, 'rows', 0, 0, tiled=True)  62.5 us
    dot_general x31, matrix products, mul(): return lax.dot_general(left, right, dims, preferred_element_type=WIDE)  60.4 us
    pallas_call x2, Pallas kernels, pair_backward(): pl.pallas_call(kernel, grid_spec=pltpu.PrefetchScalarGridSpec(num_scalar_...  53.9 us
    unnamed x149, local copies, waits for them, and re-layouts  37.2 us
    pallas_call x2, Pallas kernels, pair_forward(): pl.pallas_call(kernel, grid_spec=pltpu.PrefetchScalarGridSpec(num_scalar_...  32.6 us
    all_to_all x8, starting transfers between devices, exchange_rows(): return lax.all_to_all(value, 'rows', 0, 0, tiled=True)  32.3 us
    ppermute x20, starting transfers between devices, swap(): return lax.ppermute(value, axis, [(0, 1), (1, 0)])  25.8 us
  transfers between devices with their start and end apart: 37, of which 22 were waited for; matrix products, arithmetic and copies ran while one was open for 24% of the time, Pallas kernels for 12%

profile of v7, /device:TPU:0, one launch (start us, length us, event | category | flops | bytes accessed | tf_op | source)
XLA Modules:
  0.0 713.9 jit_solution(1722612762963752102)
XLA Ops:
  7.2 2.7 copy.102
  10.0 2.7 copy.103
  14.4 4.0 collective-permute-start.2
  19.9 7.8 %collective-permute-done.2 = bf16[96,1024]{1,0:T(8,128)(2,1)S(1)} collective-permute-done((bf16[96,1024]{1,0:T(8,128)(2,1)}, bf16[96,1024]{1,0:T(8,128)(2,1)S(1)}, u32[]{:S(2)}, u32[]{:S(2)}) %collective-permute-start.2) | collective-permute-done | bytes 196640 | tf_op jit(solution)/shard_map/ppermute | solution.py:394
  40.8 17.1 %collective-permute-done = bf16[160,1024]{1,0:T(8,128)(2,1)} collective-permute-done((bf16[160,1024]{1,0:T(8,128)(2,1)}, bf16[160,1024]{1,0:T(8,128)(2,1)}, u32[]{:S(2)}, u32[]{:S(2)}) %collective-permute-start) | collective-permute-done | bytes 327712 | tf_op jit(solution)/shard_map/ppermute | solution.py:394
  59.8 8.5 %collective-permute-done.1 = bf16[2,96,1024]{2,1,0:T(8,128)(2,1)S(1)} collective-permute-done((bf16[2,96,1024]{2,1,0:T(8,128)(2,1)S(1)}, bf16[2,96,1024]{2,1,0:T(8,128)(2,1)S(1)}, u32[]{:S(2)}, u32[]{:S(2)}) %collective-permute-start.1) | collective-permute-done | bytes 393248 | tf_op jit(solution)/shard_map/ppermute | solution.py:394
  72.7 2.7 constant_dynamic-update-slice_fusion.2
  75.3 3.2 convolution_convert_fusion.3
  78.6 2.9 convolution_convert_fusion.4
  82.8 4.3 all-to-all-start
  88.3 24.3 %all-to-all-done.q_ref.k_ref.v_ref = bf16[8,2,3,64,256]{4,3,2,1,0:T(8,128)(2,1)} async-done(((bf16[8,2,3,64,256]{4,3,2,1,0:T(8,128)(2,1)}), bf16[8,2,3,64,256]{4,3,2,1,0:T(8,128)(2,1)}, u32[]{:S(2)}, u32[]{:S(2)}) %all-to-all-start) | async-done | bytes 1572896 | tf_op jit(solution)/shard_map/all_to_all | solution.py:230
  113.5 3.3 dynamic-slice_convert_fusion.2
  116.7 19.0 %pair_forward.2 = (bf16[8,2,64,256]{3,2,1,0:T(8,128)(2,1)}, f32[8,2,64,256]{3,2,1,0:T(8,128)S(1)}, f32[8,2,1,256]{3,2,1,0:T(1,128)S(1)}) custom-call(s32[2]{0:T(128)S(1)} %broadcast_13_len_ref.2.len_ref, bf16[8,2,3,64,256]{4,3,2,1,0:T(8,128)(2,1)} %all-to-all-done.q_ref.k_ref.v_ref, bf16[8,2,3,64,256]{4,3,2,1,0:T(8,128)(2,1)} %all-to-all-done.q_ref.k_ref.v_ref, ...), custom_call_target="tpu_custom_call" | custom-call | flops 20132659200 | bytes 8388608 | tf_op jit(solution)/shard_map/pair_forward/pallas_call | solution.py:282
  136.7 3.8 all-to-all-start.1
  146.9 5.8 all-to-all-done.1
  155.0 3.5 slice.172
  162.5 2.7 fusion.71
  165.4 5.5 collective-permute-done.3
  175.5 4.7 all-to-all-start.2
  180.2 2.7 constant_dynamic-update-slice_fusion
  188.6 6.9 all-to-all-done.2.q_ref
  196.4 3.6 all-to-all-start.3
  200.1 15.2 %all-to-all-done.3.k_ref.v_ref = bf16[8,2,2,64,256]{4,3,2,1,0:T(8,128)(2,1)S(1)} async-done(((bf16[8,2,2,64,256]{4,3,2,1,0:T(8,128)(2,1)}), bf16[8,2,2,64,256]{4,3,2,1,0:T(8,128)(2,1)S(1)}, u32[]{:S(2)}, u32[]{:S(2)}) %all-to-all-start.3) | async-done | bytes 1048608 | tf_op jit(solution)/shard_map/all_to_all | solution.py:230
  216.3 13.7 %pair_forward.3 = (bf16[8,2,64,256]{3,2,1,0:T(8,128)(2,1)S(1)}, f32[8,2,64,256]{3,2,1,0:T(8,128)S(1)}, f32[8,2,1,256]{3,2,1,0:T(1,128)S(1)}) custom-call(s32[2]{0:T(128)S(1)} %dynamic_slice.106.len_ref, bf16[8,2,1,64,256]{4,3,2,1,0:T(8,128)(2,1)S(1)} %copy-done.3, bf16[8,2,2,64,256]{4,3,2,1,0:T(8,128)(2,1)S(1)} %all-to-all-done.3.k_ref.v_ref, ...), custom_call_target="tpu_custom_call" | custom-call | flops 14092861440 | bytes 8388608 | tf_op jit(solution)/shard_map/pair_forward/pallas_call | solution.py:282
  230.0 12.3 %all_to_all.45 = bf16[8,2,64,256]{3,2,1,0:T(8,128)(2,1)S(1)} all-to-all(bf16[8,2,64,256]{3,2,1,0:T(8,128)(2,1)S(1)} %get-tuple-element.62), channel_id=1, replica_groups=mesh['far'=2,'near'=2,'rows'=8] {'rows'}, dimensions={0} | all-to-all | bytes 1048576 | tf_op jit(solution)/shard_map/all_to_all | solution.py:230
  246.2 9.9 %collective-permute-done.4 = bf16[512,512]{1,0:T(8,128)(2,1)S(1)} collective-permute-done((bf16[512,512]{1,0:T(8,128)(2,1)S(1)}, bf16[512,512]{1,0:T(8,128)(2,1)S(1)}, u32[]{:S(2)}, u32[]{:S(2)}) %collective-permute-start.4) | collective-permute-done | bytes 524320 | tf_op jit(solution)/shard_map/ppermute | solution.py:394
  259.2 2.8 slice.180
  268.3 5.1 multiply_convert_fusion
  273.5 3.4 fusion.19
  276.8 4.7 convolution_convert_fusion.1
  281.6 4.4 convolution_convert_fusion.2
  286.0 7.8 %pad_maximum_fusion = bf16[2,2048,1024]{2,1,0:T(8,128)(2,1)} fusion(bf16[2,1024,1024]{2,1,0:T(8,128)(2,1)} %bitcast.325, bf16[2,1024,1024]{2,1,0:T(8,128)(2,1)} %bitcast.326), kind=kLoop, calls=%fused_computation | loop fusion | flops 16777216 | bytes 16777216 | tf_op jit(solution)/shard_map/concatenate | solution.py:575
  297.5 4.8 fusion.77
  303.3 23.6 %collective-permute-done.5 = bf16[512,1024]{1,0:T(8,128)(2,1)} collective-permute-done((bf16[512,1024]{1,0:T(8,128)(2,1)}, bf16[512,1024]{1,0:T(8,128)(2,1)}, u32[]{:S(2)}, u32[]{:S(2)}) %collective-permute-start.5) | collective-permute-done | bytes 1048608 | tf_op jit(solution)/shard_map/ppermute | solution.py:394
  328.5 2.5 collective-permute-start.6
  335.9 3.5 all-to-all-start.5
  341.5 5.9 collective-permute-done.6
  349.5 10.2 %all-to-all-done.5.g_ref = bf16[8,2,64,256]{3,2,1,0:T(8,128)(2,1)S(1)} async-done(((bf16[8,2,64,256]{3,2,1,0:T(8,128)(2,1)}), bf16[8,2,64,256]{3,2,1,0:T(8,128)(2,1)S(1)}, u32[]{:S(2)}, u32[]{:S(2)}) %all-to-all-start.5) | async-done | bytes 524320 | tf_op jit(solution)/shard_map/all_to_all | solution.py:230
  359.7 3.5 collective-permute-start.7
  363.2 21.7 %pair_backward.2 = bf16[8,2,3,64,256]{4,3,2,1,0:T(8,128)(2,1)} custom-call(s32[2]{0:T(128)S(1)} %dynamic_slice.106.len_ref, bf16[8,2,1,64,256]{4,3,2,1,0:T(8,128)(2,1)S(1)} %copy-done.4, bf16[8,2,2,64,256]{4,3,2,1,0:T(8,128)(2,1)S(1)} %all-to-all-done.3.k_ref.v_ref, bf16[8,2,2,64,256]{4,3,2,1,0:T(8,128)(2,1)S(1)} %all-to-all-done.3.k_ref.v_ref, ...), custom_call_target="tpu_custom_call" | custom-call | flops 20132659200 | bytes 8388608 | tf_op jit(solution)/shard_map/pair_backward/pallas_call | solution.py:364
  384.9 8.6 %collective-permute-done.7 = bf16[256,1024]{1,0:T(8,128)(2,1)S(1)} collective-permute-done((bf16[256,1024]{1,0:T(8,128)(2,1)}, bf16[256,1024]{1,0:T(8,128)(2,1)S(1)}, u32[]{:S(2)}, u32[]{:S(2)}) %collective-permute-start.7) | collective-permute-done | bytes 524320 | tf_op jit(solution)/shard_map/ppermute | solution.py:394
  393.6 4.3 all-to-all-start.6
  398.0 34.3 %collective-permute-done.8 = bf16[2,256,1024]{2,1,0:T(8,128)(2,1)S(1)} collective-permute-done((bf16[2,256,1024]{2,1,0:T(8,128)(2,1)S(1)}, bf16[2,256,1024]{2,1,0:T(8,128)(2,1)S(1)}, u32[]{:S(2)}, u32[]{:S(2)}) %collective-permute-start.8) | collective-permute-done | bytes 1048608 | tf_op jit(solution)/shard_map/ppermute | solution.py:394
  444.5 11.1 %collective-permute-done.9 = bf16[512,512]{1,0:T(8,128)(2,1)S(1)} collective-permute-done((bf16[512,512]{1,0:T(8,128)(2,1)S(1)}, bf16[512,512]{1,0:T(8,128)(2,1)S(1)}, u32[]{:S(2)}, u32[]{:S(2)}) %collective-permute-start.9) | collective-permute-done | bytes 524320 | tf_op jit(solution)/shard_map/ppermute | solution.py:394
  462.1 9.0 %pad_maximum_fusion.1 = bf16[2,1280,1024]{2,1,0:T(8,128)(2,1)} fusion(bf16[2,512,1024]{2,1,0:T(8,128)(2,1)S(1)} %bitcast.332, bf16[2,256,1024]{2,1,0:T(8,128)(2,1)S(1)} %bitcast.352, bf16[2,256,1024]{2,1,0:T(8,128)(2,1)S(1)} %bitcast.353, bf16[2,256,1024]{2,1,0:T(8,128)(2,1)S(1)} %bitcast.351), kind=kLoop, calls=%fused_computation.3 | loop fusion | flops 20971520 | bytes 10485760 | tf_op jit(solution)/shard_map/concatenate | solution.py:613
  471.1 2.9 convolution_convert_fusion.7
  474.3 3.7 all-to-all-start.7
  478.0 19.9 %collective-permute-done.10 = bf16[512,1024]{1,0:T(8,128)(2,1)} collective-permute-done((bf16[512,1024]{1,0:T(8,128)(2,1)S(1)}, bf16[512,1024]{1,0:T(8,128)(2,1)}, u32[]{:S(2)}, u32[]{:S(2)}) %collective-permute-start.10) | collective-permute-done | bytes 1048608 | tf_op jit(solution)/shard_map/ppermute | solution.py:394
  501.0 2.9 collective-permute-start.11
  503.9 32.1 %pair_backward.3 = bf16[8,2,3,64,256]{4,3,2,1,0:T(8,128)(2,1)} custom-call(s32[2]{0:T(128)S(1)} %broadcast_13_len_ref.2.len_ref, bf16[8,2,3,64,256]{4,3,2,1,0:T(8,128)(2,1)} %all-to-all-done.q_ref.k_ref.v_ref, bf16[8,2,3,64,256]{4,3,2,1,0:T(8,128)(2,1)} %all-to-all-done.q_ref.k_ref.v_ref, bf16[8,2,3,64,256]{4,3,2,1,0:T(8,128)(2,1)} %all-to-all-done.q_ref.k_ref.v_ref, ...), custom_call_target="tpu_custom_call" | custom-call | flops 30198988800 | bytes 8388608 | tf_op jit(solution)/shard_map/pair_backward/pallas_call | solution.py:364
  536.2 4.4 all-to-all-start.8
  544.3 23.2 %collective-permute-done.12 = bf16[2,256,768]{2,1,0:T(8,128)(2,1)} collective-permute-done((bf16[2,256,768]{2,1,0:T(8,128)(2,1)S(1)}, bf16[2,256,768]{2,1,0:T(8,128)(2,1)}, u32[]{:S(2)}, u32[]{:S(2)}) %collective-permute-start.12) | collective-permute-done | bytes 786464 | tf_op jit(solution)/shard_map/ppermute | solution.py:394
  570.0 3.0 copy.116
  580.2 4.2 fusion.7
  584.7 13.1 %collective-permute-done.14 = bf16[256,1024]{1,0:T(8,128)(2,1)S(1)} collective-permute-done((bf16[256,1024]{1,0:T(8,128)(2,1)S(1)}, bf16[256,1024]{1,0:T(8,128)(2,1)S(1)}, u32[]{:S(2)}, u32[]{:S(2)}) %collective-permute-start.14) | collective-permute-done | bytes 524320 | tf_op jit(solution)/shard_map/ppermute | solution.py:394
  607.7 22.1 %collective-permute-done.15 = bf16[256,1024]{1,0:T(8,128)(2,1)S(1)} collective-permute-done((bf16[256,1024]{1,0:T(8,128)(2,1)S(1)}, bf16[256,1024]{1,0:T(8,128)(2,1)S(1)}, u32[]{:S(2)}, u32[]{:S(2)}) %collective-permute-start.15) | collective-permute-done | bytes 524320 | tf_op jit(solution)/shard_map/ppermute | solution.py:394
  632.2 6.7 slice_convert_fusion
  638.8 5.5 copy.128
  652.2 11.0 %all-gather.2 = bf16[16,80,256]{2,1,0:T(8,128)(2,1)S(1)} all-gather(bf16[2,80,256]{2,1,0:T(8,128)(2,1)S(1)} %pad_maximum_fusion.22), channel_id=4, replica_groups=mesh['far'=2,'near'=2,'rows'=8] {'rows'}, dimensions={0}, use_global_device_ids=true | all-gather | bytes 737280 | tf_op jit(solution)/shard_map/all_gather | solution.py:651
  670.8 3.1 slice_convert_fusion.1
  677.0 2.9 copy.126
  679.9 13.6 %collective-permute-done.16 = bf16[2,256,1024]{2,1,0:T(8,128)(2,1)} collective-permute-done((bf16[2,256,1024]{2,1,0:T(8,128)(2,1)}, bf16[2,256,1024]{2,1,0:T(8,128)(2,1)}, u32[]{:S(2)}, u32[]{:S(2)}) %collective-permute-start.16) | collective-permute-done | bytes 1048608 | tf_op jit(solution)/shard_map/ppermute | solution.py:394
  695.8 2.6 fusion.11
  703.5 3.7 copy.124
  (352 shorter events, 153.9 us)
Async XLA Ops:
  7.2 237.7 %copy-start = (bf16[4,256,1024]{2,1,0:T(8,128)(2,1)S(1)}, bf16[4,256,1024]{2,1,0:T(8,128)(2,1)}, u32[]{:S(2)}) copy-start(bf16[4,256,1024]{2,1,0:T(8,128)(2,1)} %param.31) | copy-start | bytes 6291460
  7.2 65.5 %all-gather.10.cloned.1.call-start = ((), (), s32[]{:S(2)}) async-start(), calls=%async_computation.12 | async-start | bytes 1769472 | tf_op jit(solution)/shard_map/all_gather | solution.py:444
  10.0 8.4 %copy-start.54 = (s32[4,256]{1,0:T(4,128)S(1)}, s32[4,256]{1,0:T(4,128)}, u32[]{:S(2)}) copy-start(s32[4,256]{1,0:T(4,128)} %param.17) | copy-start | bytes 12292
  12.7 18.1 %copy-start.50 = (bf16[32,2,1024]{2,1,0:T(2,128)(2,1)S(1)}, bf16[32,2,1024]{2,1,0:T(2,128)(2,1)}, u32[]{:S(2)}) copy-start(bf16[32,2,1024]{2,1,0:T(2,128)(2,1)} %param.20) | copy-start | bytes 393220
  12.7 20.0 %copy-start.40 = (bf16[2,1024,256]{2,1,0:T(8,128)(2,1)S(1)}, bf16[2,1024,256]{2,1,0:T(8,128)(2,1)}, u32[]{:S(2)}) copy-start(bf16[2,1024,256]{2,1,0:T(8,128)(2,1)} %param.25) | copy-start | bytes 3145732
  14.4 13.4 %collective-permute-start.2 = (bf16[96,1024]{1,0:T(8,128)(2,1)}, bf16[96,1024]{1,0:T(8,128)(2,1)S(1)}, u32[]{:S(2)}, u32[]{:S(2)}) collective-permute-start(bf16[96,1024]{1,0:T(8,128)(2,1)} %constant_dynamic-slice_fusion.14), channel_id=1, source_target_pairs={{0,16},{16,0},{1,17},{17,1},{2,18},{18,2},{3,19},{19,3},{4,20},{20... | collective-permute-start | bytes 589832 | tf_op jit(solution)/shard_map/ppermute | solution.py:394
  19.9 11.5 %copy-start.51 = (f32[2,256]{1,0:T(2,128)}, f32[2,256]{1,0:T(2,128)S(1)}, u32[]{:S(2)}) copy-start(f32[2,256]{1,0:T(2,128)S(1)} %get-tuple-element.194) | copy-start | bytes 6148
  28.4 126.5 %all-gather.18.cloned.1.call-start = ((), (), s32[]{:S(2)}) async-start(), calls=%async_computation.19 | async-start | bytes 8257536 | tf_op jit(solution)/shard_map/all_gather | solution.py:522
  39.9 38.7 %copy-start.42 = (bf16[512,1024]{1,0:T(8,128)(2,1)}, bf16[512,1024]{1,0:T(8,128)(2,1)S(1)}, u32[]{:S(2)}) copy-start(bf16[512,1024]{1,0:T(8,128)(2,1)S(1)} %get-tuple-element.59) | copy-start | bytes 3145732
  40.7 17.1 %collective-permute-start = (bf16[160,1024]{1,0:T(8,128)(2,1)}, bf16[160,1024]{1,0:T(8,128)(2,1)}, u32[]{:S(2)}, u32[]{:S(2)}) collective-permute-start(bf16[160,1024]{1,0:T(8,128)(2,1)} %pad_maximum_fusion.20), channel_id=1, source_target_pairs={{0,16},{16,0},{1,17},{17,1},{2,18},{18,2},{3,19},{19,3},{4,20},{20... | collective-permute-start | bytes 983048 | tf_op jit(solution)/shard_map/ppermute | solution.py:394
  58.8 9.5 %collective-permute-start.1 = (bf16[2,96,1024]{2,1,0:T(8,128)(2,1)S(1)}, bf16[2,96,1024]{2,1,0:T(8,128)(2,1)S(1)}, u32[]{:S(2)}, u32[]{:S(2)}) collective-permute-start(bf16[2,96,1024]{2,1,0:T(8,128)(2,1)S(1)} %fusion.55), channel_id=1, source_target_pairs={{0,8},{8,0},{1,9},{9,1},{2,10},{10,2},{3,11},{11,3},{4,12},{12,4},... | collective-permute-start | bytes 1179656 | tf_op jit(solution)/shard_map/ppermute | solution.py:394
  82.8 29.8 %all-to-all-start = ((bf16[8,2,3,64,256]{4,3,2,1,0:T(8,128)(2,1)}), bf16[8,2,3,64,256]{4,3,2,1,0:T(8,128)(2,1)}, u32[]{:S(2)}, u32[]{:S(2)}) async-start(bf16[8,2,3,64,256]{4,3,2,1,0:T(8,128)(2,1)} %pad_maximum_fusion.8), calls=%async_computation | async-start | bytes 3145728 | tf_op jit(solution)/shard_map/all_to_all | solution.py:230
  87.2 172.1 %all-gather.20.cloned.1.call-start = ((), (), s32[]{:S(2)}) async-start(), calls=%async_computation.20 | async-start | bytes 8912896 | tf_op jit(solution)/shard_map/all_gather | solution.py:536
  136.7 16.0 %all-to-all-start.1 = ((bf16[8,2,64,256]{3,2,1,0:T(8,128)(2,1)}), bf16[8,2,64,256]{3,2,1,0:T(8,128)(2,1)S(1)}, u32[]{:S(2)}, u32[]{:S(2)}) async-start(bf16[8,2,64,256]{3,2,1,0:T(8,128)(2,1)} %get-tuple-element.61), calls=%async_computation.1 | async-start | bytes 1048576 | tf_op jit(solution)/shard_map/all_to_all | solution.py:230
  153.4 17.5 %copy-start.31 = (bf16[64,8,2,256]{3,1,2,0:T(8,128)(2,1)}, bf16[64,8,2,256]{3,1,2,0:T(8,128)(2,1)S(1)}, u32[]{:S(2)}) copy-start(bf16[64,8,2,256]{3,1,2,0:T(8,128)(2,1)S(1)} %copy.138) | copy-start | bytes 1572868
  153.4 17.5 %collective-permute-start.3 = (bf16[512,512]{1,0:T(8,128)(2,1)S(1)}, bf16[512,512]{1,0:T(8,128)(2,1)S(1)}, u32[]{:S(2)}, u32[]{:S(2)}) collective-permute-start(bf16[512,512]{1,0:T(8,128)(2,1)S(1)} %bitcast.333), channel_id=1, source_target_pairs={{0,8},{8,0},{1,9},{9,1},{2,10},{10,2},{3,11},{11,3},{4,12},{12,4},... | collective-permute-start | bytes 1572872 | tf_op jit(solution)/shard_map/ppermute | solution.py:394
  165.2 5.7 copy-start.29
  175.5 20.1 %all-to-all-start.2 = ((bf16[8,2,1,64,256]{4,3,2,1,0:T(8,128)(2,1)}), bf16[8,2,1,64,256]{4,3,2,1,0:T(8,128)(2,1)S(1)}, u32[]{:S(2)}, u32[]{:S(2)}) async-start(bf16[8,2,1,64,256]{4,3,2,1,0:T(8,128)(2,1)} %pad_maximum_fusion.18), calls=%async_computation.2 | async-start | bytes 1048576 | tf_op jit(solution)/shard_map/all_to_all | solution.py:230
  187.5 12.4 %copy-start.60 = (s32[4]{0:T(128)S(1)}, s32[4]{0:T(128)}, u32[]{:S(2)}) copy-start(s32[4]{0:T(128)} %param.19) | copy-start | bytes 52
  196.4 18.9 %all-to-all-start.3 = ((bf16[8,2,2,64,256]{4,3,2,1,0:T(8,128)(2,1)}), bf16[8,2,2,64,256]{4,3,2,1,0:T(8,128)(2,1)S(1)}, u32[]{:S(2)}, u32[]{:S(2)}) async-start(bf16[8,2,2,64,256]{4,3,2,1,0:T(8,128)(2,1)} %pad_maximum_fusion.12), calls=%async_computation.3 | async-start | bytes 2097152 | tf_op jit(solution)/shard_map/all_to_all | solution.py:230
  199.9 233.9 %reduce-scatter.4.cloned.1.call-start = ((), (), s32[]{:S(2)}) async-start(), calls=%async_computation.13 | async-start | bytes 8912896 | tf_op jit(solution)/shard_map/reduce_scatter | solution.py:582
  230.0 15.9 %copy-start.5 = (f32[8,2,64,256]{3,2,1,0:T(8,128)}, f32[8,2,64,256]{3,2,1,0:T(8,128)S(1)}, u32[]{:S(2)}) copy-start(f32[8,2,64,256]{3,2,1,0:T(8,128)S(1)} %get-tuple-element.70.wide_ref) | copy-start | bytes 3145732
  230.0 14.9 %copy-start.57 = (bf16[1024]{0:T(1024)(128)(2,1)S(1)}, bf16[1024]{0:T(1024)(128)(2,1)}, u32[]{:S(2)}) copy-start(bf16[1024]{0:T(1024)(128)(2,1)} %param.28) | copy-start | bytes 6148
  243.0 13.2 %copy-start.45 = (bf16[64,8,2,256]{3,1,2,0:T(8,128)(2,1)}, bf16[64,8,2,256]{3,1,2,0:T(8,128)(2,1)S(1)}, u32[]{:S(2)}) copy-start(bf16[64,8,2,256]{3,1,2,0:T(8,128)(2,1)S(1)} %copy.139) | copy-start | bytes 1572868
  243.0 13.2 %collective-permute-start.4 = (bf16[512,512]{1,0:T(8,128)(2,1)S(1)}, bf16[512,512]{1,0:T(8,128)(2,1)S(1)}, u32[]{:S(2)}, u32[]{:S(2)}) collective-permute-start(bf16[512,512]{1,0:T(8,128)(2,1)S(1)} %bitcast.366), channel_id=1, source_target_pairs={{0,8},{8,0},{1,9},{9,1},{2,10},{10,2},{3,11},{11,3},{4,12},{12,4},... | collective-permute-start | bytes 1572872 | tf_op jit(solution)/shard_map/ppermute | solution.py:394
  246.0 10.2 %copy-start.10 = (f32[512,1024]{1,0:T(8,128)S(1)}, f32[512,1024]{1,0:T(8,128)}, u32[]{:S(2)}) copy-start(f32[512,1024]{1,0:T(8,128)} %copy-done.9) | copy-start | bytes 6291460
  273.5 8.1 %copy-start.61 = (bf16[512,2048]{1,0:T(8,128)(2,1)}, bf16[512,2048]{1,0:T(8,128)(2,1)S(1)}, u32[]{:S(2)}) copy-start(bf16[512,2048]{1,0:T(8,128)(2,1)S(1)} %get-tuple-element.65) | copy-start | bytes 6291460
  293.8 33.1 %collective-permute-start.5 = (bf16[512,1024]{1,0:T(8,128)(2,1)}, bf16[512,1024]{1,0:T(8,128)(2,1)}, u32[]{:S(2)}, u32[]{:S(2)}) collective-permute-start(bf16[512,1024]{1,0:T(8,128)(2,1)} %fusion.19), channel_id=1, source_target_pairs={{0,8},{8,0},{1,9},{9,1},{2,10},{10,2},{3,11},{11,3},{4,12},{12,4},... | collective-permute-start | bytes 3145736 | tf_op jit(solution)/shard_map/ppermute | solution.py:394
  297.5 29.4 %copy-start.41 = (bf16[512,1024]{1,0:T(8,128)(2,1)S(1)}, bf16[512,1024]{1,0:T(8,128)(2,1)}, u32[]{:S(2)}) copy-start(bf16[512,1024]{1,0:T(8,128)(2,1)} %fusion.19) | copy-start | bytes 3145732
  302.3 26.2 %copy-start.34 = (f32[2,2,128,1024]{3,2,1,0:T(8,128)}, f32[2,2,128,1024]{3,2,1,0:T(8,128)S(1)}, u32[]{:S(2)}) copy-start(f32[2,2,128,1024]{3,2,1,0:T(8,128)S(1)} %fusion.77) | copy-start | bytes 6291460
  328.5 18.8 %collective-permute-start.6 = (bf16[256,1024]{1,0:T(8,128)(2,1)}, bf16[256,1024]{1,0:T(8,128)(2,1)}, u32[]{:S(2)}, u32[]{:S(2)}) collective-permute-start(bf16[256,1024]{1,0:T(8,128)(2,1)} %bitcast.39), channel_id=1, source_target_pairs={{0,8},{8,0},{1,9},{9,1},{2,10},{10,2},{3,11},{11,3},{4,12},{12,4},... | collective-permute-start | bytes 1572872 | tf_op jit(solution)/shard_map/ppermute | solution.py:394
  335.9 23.8 %all-to-all-start.5 = ((bf16[8,2,64,256]{3,2,1,0:T(8,128)(2,1)}), bf16[8,2,64,256]{3,2,1,0:T(8,128)(2,1)S(1)}, u32[]{:S(2)}, u32[]{:S(2)}) async-start(bf16[8,2,64,256]{3,2,1,0:T(8,128)(2,1)} %maximum_bitcast_fusion), calls=%async_computation.5 | async-start | bytes 1048576 | tf_op jit(solution)/shard_map/all_to_all | solution.py:230
  341.4 21.7 %copy-start.4 = (bf16[8,2,1,64,256]{4,3,2,1,0:T(8,128)(2,1)S(1)}, bf16[8,2,1,64,256]{4,3,2,1,0:T(8,128)(2,1)}, u32[]{:S(2)}) copy-start(bf16[8,2,1,64,256]{4,3,2,1,0:T(8,128)(2,1)} %copy-done.2) | copy-start | bytes 1572868
  341.4 21.7 %copy-start.6 = (f32[8,2,64,256]{3,2,1,0:T(8,128)S(1)}, f32[8,2,64,256]{3,2,1,0:T(8,128)}, u32[]{:S(2)}) copy-start(f32[8,2,64,256]{3,2,1,0:T(8,128)} %copy-done.5) | copy-start | bytes 3145732
  359.7 33.8 %collective-permute-start.7 = (bf16[256,1024]{1,0:T(8,128)(2,1)}, bf16[256,1024]{1,0:T(8,128)(2,1)S(1)}, u32[]{:S(2)}, u32[]{:S(2)}) collective-permute-start(bf16[256,1024]{1,0:T(8,128)(2,1)} %fusion.40), channel_id=1, source_target_pairs={{0,16},{16,0},{1,17},{17,1},{2,18},{18,2},{3,19},{19,3},{4,20},{20... | collective-permute-start | bytes 1572872 | tf_op jit(solution)/shard_map/ppermute | solution.py:394
  363.2 30.3 %copy-start.33 = (bf16[256,1024]{1,0:T(8,128)(2,1)S(1)}, bf16[256,1024]{1,0:T(8,128)(2,1)}, u32[]{:S(2)}) copy-start(bf16[256,1024]{1,0:T(8,128)(2,1)} %fusion.40) | copy-start | bytes 1572868
  393.6 40.2 %all-to-all-start.6 = ((bf16[8,2,3,64,256]{4,3,2,1,0:T(8,128)(2,1)}), bf16[8,2,3,64,256]{4,3,2,1,0:T(8,128)(2,1)}, u32[]{:S(2)}, u32[]{:S(2)}) async-start(bf16[8,2,3,64,256]{4,3,2,1,0:T(8,128)(2,1)} %pair_backward.2), calls=%async_computation.6 | async-start | bytes 3145728 | tf_op jit(solution)/shard_map/all_to_all | solution.py:230
  397.9 138.3 %all-gather.12.cloned.1.call-start = ((), (), s32[]{:S(2)}) async-start(), calls=%async_computation.14 | async-start | bytes 4718592 | tf_op jit(solution)/shard_map/all_gather | solution.py:444
  397.9 34.4 %collective-permute-start.8 = (bf16[2,256,1024]{2,1,0:T(8,128)(2,1)S(1)}, bf16[2,256,1024]{2,1,0:T(8,128)(2,1)S(1)}, u32[]{:S(2)}, u32[]{:S(2)}) collective-permute-start(bf16[2,256,1024]{2,1,0:T(8,128)(2,1)S(1)} %pad_maximum_fusion.13), channel_id=1, source_target_pairs={{0,8},{8,0},{1,9},{9,1},{2,10},{10,2},{3,11},{11,3},{4,12},{12,4},... | collective-permute-start | bytes 3145736 | tf_op jit(solution)/shard_map/ppermute | solution.py:394
  433.8 102.3 %reduce-scatter.6.cloned.1.call-start = ((), (), s32[]{:S(2)}) async-start(), calls=%async_computation.15 | async-start | bytes 5898240 | tf_op jit(solution)/shard_map/reduce_scatter | solution.py:564
  442.0 13.5 %collective-permute-start.9 = (bf16[512,512]{1,0:T(8,128)(2,1)S(1)}, bf16[512,512]{1,0:T(8,128)(2,1)S(1)}, u32[]{:S(2)}, u32[]{:S(2)}) collective-permute-start(bf16[512,512]{1,0:T(8,128)(2,1)S(1)} %bitcast.369), channel_id=1, source_target_pairs={{0,8},{8,0},{1,9},{9,1},{2,10},{10,2},{3,11},{11,3},{4,12},{12,4},... | collective-permute-start | bytes 1572872 | tf_op jit(solution)/shard_map/ppermute | solution.py:394
  443.2 12.3 %copy-start.11 = (f32[512,1024]{1,0:T(8,128)S(1)}, f32[512,1024]{1,0:T(8,128)}, u32[]{:S(2)}) copy-start(f32[512,1024]{1,0:T(8,128)} %copy-done.9) | copy-start | bytes 6291460
  474.0 23.8 %collective-permute-start.10 = (bf16[512,1024]{1,0:T(8,128)(2,1)S(1)}, bf16[512,1024]{1,0:T(8,128)(2,1)}, u32[]{:S(2)}, u32[]{:S(2)}) collective-permute-start(bf16[512,1024]{1,0:T(8,128)(2,1)S(1)} %convolution_convert_fusion.7), channel_id=1, source_target_pairs={{0,8},{8,0},{1,9},{9,1},{2,10},{10,2},{3,11},{11,3},{4,12},{12,4},... | collective-permute-start | bytes 3145736 | tf_op jit(solution)/shard_map/ppermute | solution.py:394
  474.3 26.7 %all-to-all-start.7 = ((bf16[8,2,64,256]{3,2,1,0:T(8,128)(2,1)}), bf16[8,2,64,256]{3,2,1,0:T(8,128)(2,1)S(1)}, u32[]{:S(2)}, u32[]{:S(2)}) async-start(bf16[8,2,64,256]{3,2,1,0:T(8,128)(2,1)} %maximum_bitcast_fusion.1), calls=%async_computation.8 | async-start | bytes 1048576 | tf_op jit(solution)/shard_map/all_to_all | solution.py:230
  477.9 21.6 %copy-start.59 = (bf16[768,1024]{1,0:T(8,128)(2,1)S(1)}, bf16[768,1024]{1,0:T(8,128)(2,1)}, u32[]{:S(2)}) copy-start(bf16[768,1024]{1,0:T(8,128)(2,1)} %param.27) | copy-start | bytes 4718596
  501.0 35.0 %collective-permute-start.11 = (bf16[256,768]{1,0:T(8,128)(2,1)}, bf16[256,768]{1,0:T(8,128)(2,1)S(1)}, u32[]{:S(2)}, u32[]{:S(2)}) collective-permute-start(bf16[256,768]{1,0:T(8,128)(2,1)} %convolution_convert_fusion.15), channel_id=1, source_target_pairs={{0,16},{16,0},{1,17},{17,1},{2,18},{18,2},{3,19},{19,3},{4,20},{20... | collective-permute-start | bytes 1179656 | tf_op jit(solution)/shard_map/ppermute | solution.py:394
  503.9 32.2 %copy-start.48 = (bf16[256,768]{1,0:T(8,128)(2,1)S(1)}, bf16[256,768]{1,0:T(8,128)(2,1)}, u32[]{:S(2)}) copy-start(bf16[256,768]{1,0:T(8,128)(2,1)} %convolution_convert_fusion.15) | copy-start | bytes 1179652
  536.0 6.2 copy-start.22
  536.2 33.8 %all-to-all-start.8 = ((bf16[8,2,3,64,256]{4,3,2,1,0:T(8,128)(2,1)}), bf16[8,2,3,64,256]{4,3,2,1,0:T(8,128)(2,1)}, u32[]{:S(2)}, u32[]{:S(2)}) async-start(bf16[8,2,3,64,256]{4,3,2,1,0:T(8,128)(2,1)} %pair_backward.3), calls=%async_computation.10 | async-start | bytes 3145728 | tf_op jit(solution)/shard_map/all_to_all | solution.py:230
  540.6 90.3 %reduce-scatter.8.cloned.1.call-start = ((), (), s32[]{:S(2)}) async-start(), calls=%async_computation.16 | async-start | bytes 4718592 | tf_op jit(solution)/shard_map/reduce_scatter | solution.py:564
  540.7 26.9 %collective-permute-start.12 = (bf16[2,256,768]{2,1,0:T(8,128)(2,1)S(1)}, bf16[2,256,768]{2,1,0:T(8,128)(2,1)}, u32[]{:S(2)}, u32[]{:S(2)}) collective-permute-start(bf16[2,256,768]{2,1,0:T(8,128)(2,1)S(1)} %pad_maximum_fusion.17), channel_id=1, source_target_pairs={{0,8},{8,0},{1,9},{9,1},{2,10},{10,2},{3,11},{11,3},{4,12},{12,4},... | collective-permute-start | bytes 2359304 | tf_op jit(solution)/shard_map/ppermute | solution.py:394
  543.7 26.3 %collective-permute-start.13 = (bf16[160,1024]{1,0:T(8,128)(2,1)S(1)}, bf16[160,1024]{1,0:T(8,128)(2,1)}, u32[]{:S(2)}, u32[]{:S(2)}) collective-permute-start(bf16[160,1024]{1,0:T(8,128)(2,1)S(1)} %get-tuple-element.186), channel_id=1, source_target_pairs={{0,16},{16,0},{1,17},{17,1},{2,18},{18,2},{3,19},{19,3},{4,20},{20... | collective-permute-start | bytes 983048 | tf_op jit(solution)/shard_map/ppermute | solution.py:394
  578.6 92.2 %all-gather.16.cloned.1.call-start = ((), (), s32[]{:S(2)}) async-start(), calls=%async_computation.18 | async-start | bytes 2949120 | tf_op jit(solution)/shard_map/all_gather | solution.py:444
  584.5 13.3 %collective-permute-start.14 = (bf16[256,1024]{1,0:T(8,128)(2,1)S(1)}, bf16[256,1024]{1,0:T(8,128)(2,1)S(1)}, u32[]{:S(2)}, u32[]{:S(2)}) collective-permute-start(bf16[256,1024]{1,0:T(8,128)(2,1)S(1)} %bitcast.372), channel_id=1, source_target_pairs={{0,8},{8,0},{1,9},{9,1},{2,10},{10,2},{3,11},{11,3},{4,12},{12,4},... | collective-permute-start | bytes 1572872 | tf_op jit(solution)/shard_map/ppermute | solution.py:394
  584.6 15.5 %copy-start.52 = (f32[2,256]{1,0:T(2,128)S(1)}, f32[2,256]{1,0:T(2,128)}, u32[]{:S(2)}) copy-start(f32[2,256]{1,0:T(2,128)} %copy-done.51) | copy-start | bytes 6148
  584.6 15.5 %copy-start.53 = (f32[2,256]{1,0:T(2,128)S(1)}, f32[2,256]{1,0:T(2,128)}, u32[]{:S(2)}) copy-start(f32[2,256]{1,0:T(2,128)} %get-tuple-element.191) | copy-start | bytes 6148
  584.7 15.5 %copy-start.55 = (s32[4,256]{1,0:T(4,128)S(1)}, s32[4,256]{1,0:T(4,128)}, u32[]{:S(2)}) copy-start(s32[4,256]{1,0:T(4,128)} %param.17) | copy-start | bytes 12292
  599.8 98.6 %all-gather.14.cloned.1.call-start = ((), (), s32[]{:S(2)}) async-start(), calls=%async_computation.17 | async-start | bytes 2359296 | tf_op jit(solution)/shard_map/all_gather | solution.py:444
  605.1 24.7 %collective-permute-start.15 = (bf16[256,1024]{1,0:T(8,128)(2,1)S(1)}, bf16[256,1024]{1,0:T(8,128)(2,1)S(1)}, u32[]{:S(2)}, u32[]{:S(2)}) collective-permute-start(bf16[256,1024]{1,0:T(8,128)(2,1)S(1)} %get-tuple-element.182), channel_id=1, source_target_pairs={{0,16},{16,0},{1,17},{17,1},{2,18},{18,2},{3,19},{19,3},{4,20},{20... | collective-permute-start | bytes 1572872 | tf_op jit(solution)/shard_map/ppermute | solution.py:394
  631.9 13.4 %collective-permute-start.19 = (bf16[128,1024]{1,0:T(8,128)(2,1)S(1)}, bf16[128,1024]{1,0:T(8,128)(2,1)S(1)}, u32[]{:S(2)}, u32[]{:S(2)}) collective-permute-start(bf16[128,1024]{1,0:T(8,128)(2,1)S(1)} %dynamic-slice_bitcast_fusion.2), channel_id=1, source_target_pairs={{0,16},{16,0},{1,17},{17,1},{2,18},{18,2},{3,19},{19,3},{4,20},{20... | collective-permute-start | bytes 786440 | tf_op jit(solution)/shard_map/ppermute | solution.py:394
  638.8 6.4 copy-start.47
  646.6 5.5 collective-permute-start.17
  663.3 6.2 collective-permute-start.18
  668.0 25.5 %collective-permute-start.16 = (bf16[2,256,1024]{2,1,0:T(8,128)(2,1)}, bf16[2,256,1024]{2,1,0:T(8,128)(2,1)}, u32[]{:S(2)}, u32[]{:S(2)}) collective-permute-start(bf16[2,256,1024]{2,1,0:T(8,128)(2,1)} %pad_maximum_fusion.14), channel_id=1, source_target_pairs={{0,8},{8,0},{1,9},{9,1},{2,10},{10,2},{3,11},{11,3},{4,12},{12,4},... | collective-permute-start | bytes 3145736 | tf_op jit(solution)/shard_map/ppermute | solution.py:394
  (40 other events, 83.1 us)
Sparse Core Ops, SparseCore 0:
  28.5 26.8 all-gather.9
  69.4 59.4 all-gather.17
  131.8 83.6 all-gather.19
  293.9 130.4 reduce-scatter.3
  434.0 37.0 all-gather.11
  474.3 56.5 reduce-scatter.5
  578.7 49.9 reduce-scatter.7
  631.2 31.6 all-gather.15
  664.8 28.8 all-gather.13

commit v8 on v7

--- a/solution.py
+++ b/solution.py
@@ -528,7 +528,7 @@
     qkv = exchange_rows(to_pairs(qkv_both, normed_one, 3))
     patch_mid = mul(patch_in, patch_weights).astype(LOW)
     pair_both = in_order(pair_rows, pair_away)
-    pair = exchange_rows(to_pairs(pair_both, patch_mid, 2))
+    pair = to_pairs(pair_both, patch_mid, 2)
 
     mine = [piece(widen_weights), piece(narrow_weights)]
     qkv, *mine = tie(qkv, *mine)
@@ -540,11 +540,14 @@
     narrow = sent[:, :, 1].reshape(2 * hidden, width)
 
     mixed, self_wide, self_log = pair_forward(qkv, qkv, 1)
-    self_mixed_t = from_pairs(exchange_rows(mixed)[:, :, None])
+    mixed, pair = tie(exchange_rows(mixed), pair)
+    pair = exchange_rows(pair)
+    self_mixed_t = from_pairs(mixed[:, :, None])
     after_self = inputs + over_all_columns(self_mixed_t, self_whole)
     unit_two, rate_two = normed(after_self)
     normed_two = (unit_two * cross_gain_f).astype(LOW)
-    cross_q = exchange_rows(to_pairs(query_whole[: 2 * cols], normed_two, 1))
+    cross_q, pair = tie(to_pairs(query_whole[: 2 * cols], normed_two, 1), pair)
+    cross_q = exchange_rows(cross_q)
     mixed, cross_wide, cross_log = pair_forward(cross_q, pair, 0, length)
     cross_mixed_t = from_pairs(exchange_rows(mixed)[:, :, None])
     after_cross = after_self + over_all_columns(cross_mixed_t, cross_whole)
@@ -593,12 +596,23 @@
     result_two = jnp.stack([result, swap(result, "far")])
     grads = pair_backward(cross_q, pair, 0, length, grad_mixed, cross_wide, cross_log)
     grads, result_two = tie(grads, result_two)
-    result_four = jnp.stack([result_two, swap(result_two, "near")])
-    grads, result_four, hidden_part = tie(exchange_rows(grads), result_four, hidden_part)
-    hidden_total = join_rows(hidden_part)
+    grads = exchange_rows(grads)
     grad_cq_t = from_pairs(grads[:, :, :1])
     grad_pair_t = from_pairs(grads[:, :, 1:])
-    grad_two = over_all_columns(grad_cq_t, query_whole)
+    middle_terms = jnp.concatenate(
+        [
+            by_shard(cross_mixed_t, grad_cross_low),
+            by_shard(grad_cq_t, normed_two),
+            by_shard(grad_pair_t, patch_mid),
+        ],
+        axis=1,
+    )
+    grad_cq_away, middle_terms = tie(swap(grad_cq_t, "near"), middle_terms)
+    middle_part = part_rows(middle_terms)
+    grad_two = mul(jnp.concatenate([grad_cq_t, grad_cq_away]), query_whole, TN)
+    grad_two, result_two, hidden_part = tie(grad_two, result_two, hidden_part)
+    result_four = jnp.stack([result_two, swap(result_two, "near")])
+    hidden_total = join_rows(hidden_part)
     cross_gain_term = jnp.sum(grad_two * unit_two, axis=0)
     grad_self = grad_cross + normed_back(grad_two * cross_gain_f, unit_two, rate_two)
     grad_self_low = grad_self.astype(LOW)
@@ -609,30 +623,22 @@
     patch_terms = jnp.stack([mul(value, patch_in, TN).astype(LOW) for value in both_columns(grad_mid)])
     patch_terms = jnp.pad(patch_terms, ((0, 0), (0, 0), (0, width - patch_width)))
     grad_mixed, grad_self_low = tie(to_pairs(self_whole[: 2 * cols], grad_self_low, 1)[:, :, 0], grad_self_low)
-    middle_part = part_rows(
-        jnp.concatenate(
-            [
-                by_shard(cross_mixed_t, grad_cross_low),
-                by_shard(self_mixed_t, grad_self_low),
-                by_shard(grad_cq_t, normed_two),
-                by_shard(grad_pair_t, patch_mid),
-            ],
-            axis=1,
-        )
-    )
-    grad_mixed, patch_half = tie(exchange_rows(grad_mixed), patch_half)
+    output_terms = by_shard(self_mixed_t, grad_self_low)
+    grad_mixed, patch_half, middle_part = tie(exchange_rows(grad_mixed), patch_half, middle_part)
     patch_two = jnp.stack([patch_half, swap(patch_half, "far")])
+    middle_own, middle_away = own_and_away(middle_part)
+    middle_away = swap(middle_away, "far")
     grads = pair_backward(qkv, qkv, 1, None, grad_mixed, self_wide, self_log)
-    grads, patch_two, hidden_total, middle_part = tie(grads, patch_two, hidden_total, middle_part)
-    middle_own, middle_away = own_and_away(middle_part)
+    grads, patch_two, hidden_total, middle_away, result_four = tie(
+        grads, patch_two, hidden_total, middle_away, result_four
+    )
     patch_four = jnp.stack([patch_two, swap(patch_two, "near")])
-    grads, patch_four, middle_away = tie(exchange_rows(grads), patch_four, swap(middle_away, "far"))
+    middle_total = join_rows(add_far(middle_own, middle_away))
+    grads, patch_four = tie(exchange_rows(grads), patch_four)
     grad_qkv_t = from_pairs(grads)
-    last_terms = jnp.concatenate([by_shard(grad_qkv_t, normed_one), patch_terms], axis=1)
+    last_terms = jnp.concatenate([by_shard(grad_qkv_t, normed_one), output_terms, patch_terms], axis=1)
     last_part = part_rows(last_terms)
     grad_one = half_sum_near(mul(grad_qkv_t, qkv_both, TN))
-    grad_one, middle_own = tie(grad_one, middle_own)
-    middle_total = join_rows(add_far(middle_own, middle_away))
     gain_half, unit_half, rate_half, self_half = (
         halves(value)[0] for value in (gain_one, unit_one, rate_one, grad_self)
     )
@@ -646,6 +652,8 @@
         ],
         axis=0,
     )
+    input_two = jnp.stack([input_half, swap(input_half, "far")])
+    last_part, input_two, table_term = tie(last_part, input_two, table_term)
     small = [sum_near(table_term), hidden_gain_term[None], cross_gain_term[None], jnp.zeros((14, width), WIDE)]
     small = jnp.stack(both_columns(jnp.concatenate(small, axis=0).astype(LOW)))
     small = jnp.sum(lax.all_gather(small, "rows", axis=0).astype(WIDE), axis=0).astype(LOW)
@@ -653,26 +661,24 @@
         lax.dynamic_index_in_dim(small, index, 0, keepdims=False) for index in (far, 1 - far)
     )
     small = small_own.astype(WIDE) + swap(small_away, "far").astype(WIDE)
-    input_two = jnp.stack([input_half, swap(input_half, "far")])
-    last_part, input_two = tie(last_part, input_two)
     input_grads = over_heads(jnp.stack([input_two, swap(input_two, "near")]))
     outputs, patch_grads = over_heads(result_four), over_heads(patch_four)
     last_own, last_away = own_and_away(last_part)
     last_total = join_rows(add_far(last_own, swap(last_away, "far")))
 
-    output_total = middle_total[: 2 * cols]
-    query_total = middle_total[2 * cols : 3 * cols]
-    pair_total = middle_total[3 * cols : 5 * cols].reshape(heads, 2, HEAD_DIM, width)
-    patch_total = last_total[3 * cols :, :patch_width]
+    cross_output_total, query_total = middle_total[:cols], middle_total[cols : 2 * cols]
+    pair_total = middle_total[2 * cols :].reshape(heads, 2, HEAD_DIM, width)
     self_total = last_total[: 3 * cols].reshape(heads, 3, HEAD_DIM, width)
+    self_output_total = last_total[3 * cols : 4 * cols]
+    patch_total = last_total[4 * cols :, :patch_width]
     gradients = (
         small[: 2 * codes].reshape(2, codes, cols).transpose(1, 0, 2),
         self_total.transpose(1, 3, 0, 2).reshape(3, width, cols),
-        output_total[cols:],
+        self_output_total,
         small[2 * codes + 1],
         query_total.T,
         pair_total.transpose(1, 3, 0, 2).reshape(2, width, cols),
-        output_total[:cols],
+        cross_output_total,
         patch_total.T,
         small[2 * codes],
         hidden_total[hidden:].T,

time: 722 us -> 726 us (level)
  waiting for transfers between devices: 289 us -> 279 us
    ppermute x20, waiting for transfers between devices: 227 us -> 181 us  [swap(): return lax.ppermute(value, axis, [(0, 1), (1, 0)])]
    reduce_scatter x2, waiting for transfers between devices: 0.02 us -> 24.3 us  [part_rows(): return lax.psum_scatter(both, 'rows', scatter_dimension=1, tiled=True)]
    all_to_all x8, waiting for transfers between devices: 62.5 us -> 74 us  [exchange_rows(): return lax.all_to_all(value, 'rows', 0, 0, tiled=True)]
    unnamed x149 -> x177, local copies, waits for them, and re-layouts: 37.2 us -> 39.5 us
  transfers between devices with their start and end apart: 37 -> 37, of which waited for: 22 -> 22; matrix products, arithmetic and copies ran while one was open for 24% -> 23% of each run, Pallas kernels for 12% -> 12%
where the time goes in v8:
time: 726 us; the launch traced here: 715 us
  waiting for transfers between devices  279 us (38%)
  local copies, waits for them, and re-layouts  104 us (14%)
  Pallas kernels  88.8 us (12%)
  other arithmetic  81.3 us (11%)
  starting transfers between devices  62.7 us (9%)
  matrix products  61.6 us (8%)
  blocking collectives  22.1 us (3%)
  between operations  15.5 us (2%)
    ppermute x20, waiting for transfers between devices, swap(): return lax.ppermute(value, axis, [(0, 1), (1, 0)])  181 us
    all_to_all x8, waiting for transfers between devices, exchange_rows(): return lax.all_to_all(value, 'rows', 0, 0, tiled=True)  74 us
    dot_general x31, matrix products, mul(): return lax.dot_general(left, right, dims, preferred_element_type=WIDE)  60.6 us
    pallas_call x2, Pallas kernels, pair_backward(): pl.pallas_call(kernel, grid_spec=pltpu.PrefetchScalarGridSpec(num_scalar_...  54.9 us
    unnamed x177, local copies, waits for them, and re-layouts  39.5 us
    pallas_call x2, Pallas kernels, pair_forward(): pl.pallas_call(kernel, grid_spec=pltpu.PrefetchScalarGridSpec(num_scalar_...  34 us
    all_to_all x8, starting transfers between devices, exchange_rows(): return lax.all_to_all(value, 'rows', 0, 0, tiled=True)  31.6 us
    ppermute x20, starting transfers between devices, swap(): return lax.ppermute(value, axis, [(0, 1), (1, 0)])  29.8 us
  transfers between devices with their start and end apart: 37, of which 22 were waited for; matrix products, arithmetic and copies ran while one was open for 23% of the time, Pallas kernels for 12%

profile of v8, /device:TPU:0, one launch (start us, length us, event | category | flops | bytes accessed | tf_op | source)
XLA Modules:
  0.0 715.4 jit_solution(17779524010354047352)
XLA Ops:
  7.2 2.7 copy.100
  10.0 2.7 copy.101
  14.4 4.0 collective-permute-start
  19.9 7.8 %collective-permute-done = bf16[96,1024]{1,0:T(8,128)(2,1)S(1)} collective-permute-done((bf16[96,1024]{1,0:T(8,128)(2,1)}, bf16[96,1024]{1,0:T(8,128)(2,1)S(1)}, u32[]{:S(2)}, u32[]{:S(2)}) %collective-permute-start) | collective-permute-done | bytes 196640 | tf_op jit(solution)/shard_map/ppermute | solution.py:394
  40.9 17.1 %collective-permute-done.1 = bf16[160,1024]{1,0:T(8,128)(2,1)} collective-permute-done((bf16[160,1024]{1,0:T(8,128)(2,1)}, bf16[160,1024]{1,0:T(8,128)(2,1)}, u32[]{:S(2)}, u32[]{:S(2)}) %collective-permute-start.1) | collective-permute-done | bytes 327712 | tf_op jit(solution)/shard_map/ppermute | solution.py:394
  59.9 8.5 %collective-permute-done.2 = bf16[2,96,1024]{2,1,0:T(8,128)(2,1)S(1)} collective-permute-done((bf16[2,96,1024]{2,1,0:T(8,128)(2,1)S(1)}, bf16[2,96,1024]{2,1,0:T(8,128)(2,1)S(1)}, u32[]{:S(2)}, u32[]{:S(2)}) %collective-permute-start.2) | collective-permute-done | bytes 393248 | tf_op jit(solution)/shard_map/ppermute | solution.py:394
  72.8 2.8 constant_dynamic-update-slice_fusion.2
  75.5 3.3 convolution_convert_fusion.3
  78.8 2.9 convolution_convert_fusion.4
  83.0 4.3 all-to-all-start
  89.1 23.7 %all-to-all-done.q_ref.k_ref.v_ref = bf16[8,2,3,64,256]{4,3,2,1,0:T(8,128)(2,1)} async-done(((bf16[8,2,3,64,256]{4,3,2,1,0:T(8,128)(2,1)}), bf16[8,2,3,64,256]{4,3,2,1,0:T(8,128)(2,1)}, u32[]{:S(2)}, u32[]{:S(2)}) %all-to-all-start) | async-done | bytes 1572896 | tf_op jit(solution)/shard_map/all_to_all | solution.py:230
  122.4 19.0 %pair_forward.2 = (bf16[8,2,64,256]{3,2,1,0:T(8,128)(2,1)}, f32[8,2,64,256]{3,2,1,0:T(8,128)S(1)}, f32[8,2,1,256]{3,2,1,0:T(1,128)S(1)}) custom-call(s32[2]{0:T(128)S(1)} %broadcast_13_len_ref.2.len_ref, bf16[8,2,3,64,256]{4,3,2,1,0:T(8,128)(2,1)} %all-to-all-done.q_ref.k_ref.v_ref, bf16[8,2,3,64,256]{4,3,2,1,0:T(8,128)(2,1)} %all-to-all-done.q_ref.k_ref.v_ref, ...), custom_call_target="tpu_custom_call" | custom-call | flops 20132659200 | bytes 8388608 | tf_op jit(solution)/shard_map/pair_forward/pallas_call | solution.py:282
  142.4 3.7 all-to-all-start.1
  149.0 2.9 copy-done.22
  151.9 3.3 slice.169
  158.5 4.2 all-to-all-start.2
  162.9 3.7 fusion.72
  166.7 6.2 fusion.73
  173.1 11.6 %collective-permute-done.3 = bf16[512,512]{1,0:T(8,128)(2,1)S(1)} collective-permute-done((bf16[512,512]{1,0:T(8,128)(2,1)}, bf16[512,512]{1,0:T(8,128)(2,1)S(1)}, u32[]{:S(2)}, u32[]{:S(2)}) %collective-permute-start.3) | collective-permute-done | bytes 524320 | tf_op jit(solution)/shard_map/ppermute | solution.py:394
  189.3 4.1 all-to-all-start.3
  193.6 9.6 %all-to-all-done.3.q_ref = bf16[8,2,1,64,256]{4,3,2,1,0:T(8,128)(2,1)} async-done(((bf16[8,2,1,64,256]{4,3,2,1,0:T(8,128)(2,1)}), bf16[8,2,1,64,256]{4,3,2,1,0:T(8,128)(2,1)}, u32[]{:S(2)}, u32[]{:S(2)}) %all-to-all-start.3) | async-done | bytes 524320 | tf_op jit(solution)/shard_map/all_to_all | solution.py:230
  203.2 15.0 %pair_forward.3 = (bf16[8,2,64,256]{3,2,1,0:T(8,128)(2,1)S(1)}, f32[8,2,64,256]{3,2,1,0:T(8,128)S(1)}, f32[8,2,1,256]{3,2,1,0:T(1,128)S(1)}) custom-call(s32[2]{0:T(128)S(1)} %dynamic_slice.117.len_ref, bf16[8,2,1,64,256]{4,3,2,1,0:T(8,128)(2,1)} %all-to-all-done.3.q_ref, bf16[8,2,2,64,256]{4,3,2,1,0:T(8,128)(2,1)S(1)} %all-to-all-done.2.k_ref.v_ref, ...), custom_call_target="tpu_custom_call" | custom-call | flops 14092861440 | bytes 8388608 | tf_op jit(solution)/shard_map/pair_forward/pallas_call | solution.py:282
  218.3 12.3 %all_to_all.45 = bf16[8,2,64,256]{3,2,1,0:T(8,128)(2,1)S(1)} all-to-all(bf16[8,2,64,256]{3,2,1,0:T(8,128)(2,1)S(1)} %get-tuple-element.72), channel_id=1, replica_groups=mesh['far'=2,'near'=2,'rows'=8] {'rows'}, dimensions={0} | all-to-all | bytes 1048576 | tf_op jit(solution)/shard_map/all_to_all | solution.py:230
  233.4 10.9 %collective-permute-done.4 = bf16[512,512]{1,0:T(8,128)(2,1)S(1)} collective-permute-done((bf16[512,512]{1,0:T(8,128)(2,1)S(1)}, bf16[512,512]{1,0:T(8,128)(2,1)S(1)}, u32[]{:S(2)}, u32[]{:S(2)}) %collective-permute-start.4) | collective-permute-done | bytes 524320 | tf_op jit(solution)/shard_map/ppermute | solution.py:394
  247.4 2.8 slice.177
  256.5 5.1 multiply_convert_fusion
  261.6 3.4 fusion.19
  265.1 4.7 convolution_convert_fusion.1
  269.8 4.4 convolution_convert_fusion.2
  274.2 7.8 %pad_maximum_fusion = bf16[2,2048,1024]{2,1,0:T(8,128)(2,1)} fusion(bf16[2,1024,1024]{2,1,0:T(8,128)(2,1)} %bitcast.327, bf16[2,1024,1024]{2,1,0:T(8,128)(2,1)} %bitcast.328), kind=kLoop, calls=%fused_computation | loop fusion | flops 16777216 | bytes 16777216 | tf_op jit(solution)/shard_map/concatenate | solution.py:578
  284.8 4.6 fusion.78
  290.5 24.4 %collective-permute-done.5 = bf16[512,1024]{1,0:T(8,128)(2,1)} collective-permute-done((bf16[512,1024]{1,0:T(8,128)(2,1)}, bf16[512,1024]{1,0:T(8,128)(2,1)}, u32[]{:S(2)}, u32[]{:S(2)}) %collective-permute-start.5) | collective-permute-done | bytes 1048608 | tf_op jit(solution)/shard_map/ppermute | solution.py:394
  322.8 3.7 all-to-all-start.5
  328.6 7.0 collective-permute-done.6
  337.7 9.3 %all-to-all-done.5.g_ref = bf16[8,2,64,256]{3,2,1,0:T(8,128)(2,1)S(1)} async-done(((bf16[8,2,64,256]{3,2,1,0:T(8,128)(2,1)}), bf16[8,2,64,256]{3,2,1,0:T(8,128)(2,1)S(1)}, u32[]{:S(2)}, u32[]{:S(2)}) %all-to-all-start.5) | async-done | bytes 524320 | tf_op jit(solution)/shard_map/all_to_all | solution.py:230
  347.0 3.7 collective-permute-start.7
  350.7 22.7 %pair_backward.2 = bf16[8,2,3,64,256]{4,3,2,1,0:T(8,128)(2,1)} custom-call(s32[2]{0:T(128)S(1)} %dynamic_slice.117.len_ref, bf16[8,2,1,64,256]{4,3,2,1,0:T(8,128)(2,1)} %all-to-all-done.3.q_ref, bf16[8,2,2,64,256]{4,3,2,1,0:T(8,128)(2,1)S(1)} %all-to-all-done.2.k_ref.v_ref, bf16[8,2,2,64,256]{4,3,2,1,0:T(8,128)(2,1)S(1)} %all-to-all-done.2.k_ref.v_ref, ...), custom_call_target="tpu_custom_call" | custom-call | flops 20132659200 | bytes 8388608 | tf_op jit(solution)/shard_map/pair_backward/pallas_call | solution.py:364
  373.4 8.8 %collective-permute-done.7 = bf16[256,1024]{1,0:T(8,128)(2,1)S(1)} collective-permute-done((bf16[256,1024]{1,0:T(8,128)(2,1)}, bf16[256,1024]{1,0:T(8,128)(2,1)S(1)}, u32[]{:S(2)}, u32[]{:S(2)}) %collective-permute-start.7) | collective-permute-done | bytes 524320 | tf_op jit(solution)/shard_map/ppermute | solution.py:394
  384.3 3.7 all-to-all-start.6
  389.8 31.4 %all-to-all-done.6 = bf16[8,2,3,64,256]{4,3,2,1,0:T(8,128)(2,1)S(1)} async-done(((bf16[8,2,3,64,256]{4,3,2,1,0:T(8,128)(2,1)}), bf16[8,2,3,64,256]{4,3,2,1,0:T(8,128)(2,1)S(1)}, u32[]{:S(2)}, u32[]{:S(2)}) %all-to-all-start.6) | async-done | bytes 1572896 | tf_op jit(solution)/shard_map/all_to_all | solution.py:230
  429.3 6.0 collective-permute-done.8
  438.3 2.6 fusion.30
  441.1 3.5 convolution_convert_fusion.7
  451.0 3.5 all-to-all-start.7
  454.5 12.4 %collective-permute-done.9 = bf16[512,1024]{1,0:T(8,128)(2,1)} collective-permute-done((bf16[512,1024]{1,0:T(8,128)(2,1)S(1)}, bf16[512,1024]{1,0:T(8,128)(2,1)}, u32[]{:S(2)}, u32[]{:S(2)}) %collective-permute-start.9) | collective-permute-done | bytes 1048608 | tf_op jit(solution)/shard_map/ppermute | solution.py:394
  471.7 17.9 %reduce-scatter.6.cloned.1.call-done = bf16[2,128,1024]{2,1,0:T(8,128)(2,1)} async-done(((bf16[2,1024,1024]{2,1,0:T(8,128)(2,1)}), bf16[2,128,1024]{2,1,0:T(8,128)(2,1)}) %reduce-scatter.6.cloned.1.call-update) | async-done | bytes 524304 | tf_op jit(solution)/shard_map/reduce_scatter | solution.py:567
  493.6 32.1 %pair_backward.3 = bf16[8,2,3,64,256]{4,3,2,1,0:T(8,128)(2,1)} custom-call(s32[2]{0:T(128)S(1)} %broadcast_13_len_ref.2.len_ref, bf16[8,2,3,64,256]{4,3,2,1,0:T(8,128)(2,1)} %all-to-all-done.q_ref.k_ref.v_ref, bf16[8,2,3,64,256]{4,3,2,1,0:T(8,128)(2,1)} %all-to-all-done.q_ref.k_ref.v_ref, bf16[8,2,3,64,256]{4,3,2,1,0:T(8,128)(2,1)} %all-to-all-done.q_ref.k_ref.v_ref, ...), custom_call_target="tpu_custom_call" | custom-call | flops 30198988800 | bytes 8388608 | tf_op jit(solution)/shard_map/pair_backward/pallas_call | solution.py:364
  525.8 3.1 pad_maximum_fusion.6
  528.9 4.4 all-to-all-start.8
  538.5 15.3 %collective-permute-done.13 = bf16[2,256,768]{2,1,0:T(8,128)(2,1)} collective-permute-done((bf16[2,256,768]{2,1,0:T(8,128)(2,1)S(1)}, bf16[2,256,768]{2,1,0:T(8,128)(2,1)}, u32[]{:S(2)}, u32[]{:S(2)}) %collective-permute-start.13) | collective-permute-done | bytes 786464 | tf_op jit(solution)/shard_map/ppermute | solution.py:394
  556.2 3.0 copy.118
  562.4 7.8 %pad_maximum_fusion.1 = bf16[2,1280,1024]{2,1,0:T(8,128)(2,1)} fusion(bf16[2,256,1024]{2,1,0:T(8,128)(2,1)S(1)} %fusion.22, bf16[2,256,1024]{2,1,0:T(8,128)(2,1)S(1)} %bitcast.354, bf16[2,768,1024]{2,1,0:T(8,128)(2,1)S(1)} %bitcast.332), kind=kLoop, calls=%fused_computation.3 | loop fusion | flops 15728640 | bytes 10485760 | tf_op jit(solution)/shard_map/concatenate | solution.py:639
  576.5 4.4 fusion.7
  583.1 11.7 %collective-permute-done.14 = bf16[256,1024]{1,0:T(8,128)(2,1)S(1)} collective-permute-done((bf16[256,1024]{1,0:T(8,128)(2,1)S(1)}, bf16[256,1024]{1,0:T(8,128)(2,1)S(1)}, u32[]{:S(2)}, u32[]{:S(2)}) %collective-permute-start.14) | collective-permute-done | bytes 524320 | tf_op jit(solution)/shard_map/ppermute | solution.py:394
  599.2 21.5 %collective-permute-done.15 = bf16[256,1024]{1,0:T(8,128)(2,1)S(1)} collective-permute-done((bf16[256,1024]{1,0:T(8,128)(2,1)S(1)}, bf16[256,1024]{1,0:T(8,128)(2,1)S(1)}, u32[]{:S(2)}, u32[]{:S(2)}) %collective-permute-start.15) | collective-permute-done | bytes 524320 | tf_op jit(solution)/shard_map/ppermute | solution.py:394
  621.7 6.3 reduce-scatter.8.cloned.1.call-done
  633.2 13.4 %collective-permute-done.19 = bf16[160,1024]{1,0:T(8,128)(2,1)S(1)} collective-permute-done((bf16[160,1024]{1,0:T(8,128)(2,1)S(1)}, bf16[160,1024]{1,0:T(8,128)(2,1)S(1)}, u32[]{:S(2)}, u32[]{:S(2)}) %collective-permute-start.19) | collective-permute-done | bytes 327712 | tf_op jit(solution)/shard_map/ppermute | solution.py:394
  647.4 6.9 slice_convert_fusion
  654.3 5.5 copy.130
  667.2 3.9 collective-permute-done.17
  671.4 9.9 %all-gather.2 = bf16[16,80,256]{2,1,0:T(8,128)(2,1)S(1)} all-gather(bf16[2,80,256]{2,1,0:T(8,128)(2,1)S(1)} %pad_maximum_fusion.22), channel_id=4, replica_groups=mesh['far'=2,'near'=2,'rows'=8] {'rows'}, dimensions={0}, use_global_device_ids=true | all-gather | bytes 737280 | tf_op jit(solution)/shard_map/all_gather | solution.py:659
  688.5 2.9 copy.128
  695.2 2.6 fusion.11
  702.9 3.7 copy.126
  (382 shorter events, 161.6 us)
Async XLA Ops:
  7.2 224.9 %copy-start = (bf16[4,256,1024]{2,1,0:T(8,128)(2,1)S(1)}, bf16[4,256,1024]{2,1,0:T(8,128)(2,1)}, u32[]{:S(2)}) copy-start(bf16[4,256,1024]{2,1,0:T(8,128)(2,1)} %param.31) | copy-start | bytes 6291460
  7.2 65.6 %all-gather.10.cloned.1.call-start = ((), (), s32[]{:S(2)}) async-start(), calls=%async_computation.12 | async-start | bytes 1769472 | tf_op jit(solution)/shard_map/all_gather | solution.py:444
  10.0 8.4 %copy-start.68 = (s32[4,256]{1,0:T(4,128)S(1)}, s32[4,256]{1,0:T(4,128)}, u32[]{:S(2)}) copy-start(s32[4,256]{1,0:T(4,128)} %param.17) | copy-start | bytes 12292
  12.7 18.1 %copy-start.64 = (bf16[32,2,1024]{2,1,0:T(2,128)(2,1)S(1)}, bf16[32,2,1024]{2,1,0:T(2,128)(2,1)}, u32[]{:S(2)}) copy-start(bf16[32,2,1024]{2,1,0:T(2,128)(2,1)} %param.20) | copy-start | bytes 393220
  12.7 20.0 %copy-start.50 = (bf16[2,1024,256]{2,1,0:T(8,128)(2,1)S(1)}, bf16[2,1024,256]{2,1,0:T(8,128)(2,1)}, u32[]{:S(2)}) copy-start(bf16[2,1024,256]{2,1,0:T(8,128)(2,1)} %param.25) | copy-start | bytes 3145732
  14.4 13.4 %collective-permute-start = (bf16[96,1024]{1,0:T(8,128)(2,1)}, bf16[96,1024]{1,0:T(8,128)(2,1)S(1)}, u32[]{:S(2)}, u32[]{:S(2)}) collective-permute-start(bf16[96,1024]{1,0:T(8,128)(2,1)} %constant_dynamic-slice_fusion.20), channel_id=1, source_target_pairs={{0,16},{16,0},{1,17},{17,1},{2,18},{18,2},{3,19},{19,3},{4,20},{20... | collective-permute-start | bytes 589832 | tf_op jit(solution)/shard_map/ppermute | solution.py:394
  19.9 11.5 %copy-start.65 = (f32[2,256]{1,0:T(2,128)}, f32[2,256]{1,0:T(2,128)S(1)}, u32[]{:S(2)}) copy-start(f32[2,256]{1,0:T(2,128)S(1)} %get-tuple-element.203) | copy-start | bytes 6148
  28.4 117.7 %all-gather.18.cloned.1.call-start = ((), (), s32[]{:S(2)}) async-start(), calls=%async_computation.19 | async-start | bytes 8257536 | tf_op jit(solution)/shard_map/all_gather | solution.py:522
  40.8 17.1 %collective-permute-start.1 = (bf16[160,1024]{1,0:T(8,128)(2,1)}, bf16[160,1024]{1,0:T(8,128)(2,1)}, u32[]{:S(2)}, u32[]{:S(2)}) collective-permute-start(bf16[160,1024]{1,0:T(8,128)(2,1)} %pad_maximum_fusion.20), channel_id=1, source_target_pairs={{0,16},{16,0},{1,17},{17,1},{2,18},{18,2},{3,19},{19,3},{4,20},{20... | collective-permute-start | bytes 983048 | tf_op jit(solution)/shard_map/ppermute | solution.py:394
  58.9 9.4 %collective-permute-start.2 = (bf16[2,96,1024]{2,1,0:T(8,128)(2,1)S(1)}, bf16[2,96,1024]{2,1,0:T(8,128)(2,1)S(1)}, u32[]{:S(2)}, u32[]{:S(2)}) collective-permute-start(bf16[2,96,1024]{2,1,0:T(8,128)(2,1)S(1)} %fusion.56), channel_id=1, source_target_pairs={{0,8},{8,0},{1,9},{9,1},{2,10},{10,2},{3,11},{11,3},{4,12},{12,4},... | collective-permute-start | bytes 1179656 | tf_op jit(solution)/shard_map/ppermute | solution.py:394
  83.0 29.8 %all-to-all-start = ((bf16[8,2,3,64,256]{4,3,2,1,0:T(8,128)(2,1)}), bf16[8,2,3,64,256]{4,3,2,1,0:T(8,128)(2,1)}, u32[]{:S(2)}, u32[]{:S(2)}) async-start(bf16[8,2,3,64,256]{4,3,2,1,0:T(8,128)(2,1)} %pad_maximum_fusion.8), calls=%async_computation | async-start | bytes 3145728 | tf_op jit(solution)/shard_map/all_to_all | solution.py:230
  87.3 27.4 %copy-start.70 = (bf16[1024]{0:T(1024)(128)(2,1)S(1)}, bf16[1024]{0:T(1024)(128)(2,1)}, u32[]{:S(2)}) copy-start(bf16[1024]{0:T(1024)(128)(2,1)} %param.23) | copy-start | bytes 6148
  87.3 160.0 %all-gather.20.cloned.1.call-start = ((), (), s32[]{:S(2)}) async-start(), calls=%async_computation.20 | async-start | bytes 8912896 | tf_op jit(solution)/shard_map/all_gather | solution.py:536
  142.4 14.7 %all-to-all-start.1 = ((bf16[8,2,64,256]{3,2,1,0:T(8,128)(2,1)}), bf16[8,2,64,256]{3,2,1,0:T(8,128)(2,1)S(1)}, u32[]{:S(2)}, u32[]{:S(2)}) async-start(bf16[8,2,64,256]{3,2,1,0:T(8,128)(2,1)} %get-tuple-element.67), calls=%async_computation.1 | async-start | bytes 1048576 | tf_op jit(solution)/shard_map/all_to_all | solution.py:230
  148.3 7.0 copy-start.18
  158.5 30.8 %all-to-all-start.2 = ((bf16[8,2,2,64,256]{4,3,2,1,0:T(8,128)(2,1)}), bf16[8,2,2,64,256]{4,3,2,1,0:T(8,128)(2,1)S(1)}, u32[]{:S(2)}, u32[]{:S(2)}) async-start(bf16[8,2,2,64,256]{4,3,2,1,0:T(8,128)(2,1)} %pad_maximum_fusion.12), calls=%async_computation.2 | async-start | bytes 2097152 | tf_op jit(solution)/shard_map/all_to_all | solution.py:230
  162.7 22.0 %collective-permute-start.3 = (bf16[512,512]{1,0:T(8,128)(2,1)}, bf16[512,512]{1,0:T(8,128)(2,1)S(1)}, u32[]{:S(2)}, u32[]{:S(2)}) collective-permute-start(bf16[512,512]{1,0:T(8,128)(2,1)} %bitcast.334), channel_id=1, source_target_pairs={{0,8},{8,0},{1,9},{9,1},{2,10},{10,2},{3,11},{11,3},{4,12},{12,4},... | collective-permute-start | bytes 1572872 | tf_op jit(solution)/shard_map/ppermute | solution.py:394
  172.9 11.8 %copy-start.32 = (bf16[2,256,1024]{2,1,0:T(8,128)(2,1)S(1)}, bf16[2,256,1024]{2,1,0:T(8,128)(2,1)}, u32[]{:S(2)}) copy-start(bf16[2,256,1024]{2,1,0:T(8,128)(2,1)} %get-tuple-element.195) | copy-start | bytes 3145732
  172.9 11.8 %copy-start.37 = (bf16[64,8,2,256]{3,1,2,0:T(8,128)(2,1)S(1)}, bf16[64,8,2,256]{3,1,2,0:T(8,128)(2,1)}, u32[]{:S(2)}) copy-start(bf16[64,8,2,256]{3,1,2,0:T(8,128)(2,1)} %copy.140) | copy-start | bytes 1572868
  188.0 5.6 copy-start.74
  189.3 13.9 %all-to-all-start.3 = ((bf16[8,2,1,64,256]{4,3,2,1,0:T(8,128)(2,1)}), bf16[8,2,1,64,256]{4,3,2,1,0:T(8,128)(2,1)}, u32[]{:S(2)}, u32[]{:S(2)}) async-start(bf16[8,2,1,64,256]{4,3,2,1,0:T(8,128)(2,1)} %pad_maximum_fusion.18), calls=%async_computation.3 | async-start | bytes 1048576 | tf_op jit(solution)/shard_map/all_to_all | solution.py:230
  193.5 247.4 %reduce-scatter.4.cloned.1.call-start = ((), (), s32[]{:S(2)}) async-start(), calls=%async_computation.13 | async-start | bytes 8912896 | tf_op jit(solution)/shard_map/reduce_scatter | solution.py:585
  218.3 14.9 %copy-start.2 = (f32[8,2,64,256]{3,2,1,0:T(8,128)}, f32[8,2,64,256]{3,2,1,0:T(8,128)S(1)}, u32[]{:S(2)}) copy-start(f32[8,2,64,256]{3,2,1,0:T(8,128)S(1)} %get-tuple-element.80.wide_ref) | copy-start | bytes 3145732
  218.3 13.8 %copy-start.71 = (bf16[1024]{0:T(1024)(128)(2,1)S(1)}, bf16[1024]{0:T(1024)(128)(2,1)}, u32[]{:S(2)}) copy-start(bf16[1024]{0:T(1024)(128)(2,1)} %param.28) | copy-start | bytes 6148
  231.2 13.1 %copy-start.60 = (bf16[64,8,2,256]{3,1,2,0:T(8,128)(2,1)}, bf16[64,8,2,256]{3,1,2,0:T(8,128)(2,1)S(1)}, u32[]{:S(2)}) copy-start(bf16[64,8,2,256]{3,1,2,0:T(8,128)(2,1)S(1)} %copy.141) | copy-start | bytes 1572868
  231.2 13.1 %collective-permute-start.4 = (bf16[512,512]{1,0:T(8,128)(2,1)S(1)}, bf16[512,512]{1,0:T(8,128)(2,1)S(1)}, u32[]{:S(2)}, u32[]{:S(2)}) collective-permute-start(bf16[512,512]{1,0:T(8,128)(2,1)S(1)} %bitcast.368), channel_id=1, source_target_pairs={{0,8},{8,0},{1,9},{9,1},{2,10},{10,2},{3,11},{11,3},{4,12},{12,4},... | collective-permute-start | bytes 1572872 | tf_op jit(solution)/shard_map/ppermute | solution.py:394
  233.1 11.2 %copy-start.7 = (f32[512,1024]{1,0:T(8,128)S(1)}, f32[512,1024]{1,0:T(8,128)}, u32[]{:S(2)}) copy-start(f32[512,1024]{1,0:T(8,128)} %copy-done.6) | copy-start | bytes 6291460
  261.6 8.2 %copy-start.75 = (bf16[512,2048]{1,0:T(8,128)(2,1)}, bf16[512,2048]{1,0:T(8,128)(2,1)S(1)}, u32[]{:S(2)}) copy-start(bf16[512,2048]{1,0:T(8,128)(2,1)S(1)} %get-tuple-element.75) | copy-start | bytes 6291460
  282.0 32.8 %collective-permute-start.5 = (bf16[512,1024]{1,0:T(8,128)(2,1)}, bf16[512,1024]{1,0:T(8,128)(2,1)}, u32[]{:S(2)}, u32[]{:S(2)}) collective-permute-start(bf16[512,1024]{1,0:T(8,128)(2,1)} %fusion.19), channel_id=1, source_target_pairs={{0,8},{8,0},{1,9},{9,1},{2,10},{10,2},{3,11},{11,3},{4,12},{12,4},... | collective-permute-start | bytes 3145736 | tf_op jit(solution)/shard_map/ppermute | solution.py:394
  284.8 30.1 %copy-start.51 = (bf16[512,1024]{1,0:T(8,128)(2,1)S(1)}, bf16[512,1024]{1,0:T(8,128)(2,1)}, u32[]{:S(2)}) copy-start(bf16[512,1024]{1,0:T(8,128)(2,1)} %fusion.19) | copy-start | bytes 3145732
  289.4 27.1 %copy-start.41 = (f32[2,2,128,1024]{3,2,1,0:T(8,128)}, f32[2,2,128,1024]{3,2,1,0:T(8,128)S(1)}, u32[]{:S(2)}) copy-start(f32[2,2,128,1024]{3,2,1,0:T(8,128)S(1)} %fusion.78) | copy-start | bytes 6291460
  316.5 19.0 %collective-permute-start.6 = (bf16[256,1024]{1,0:T(8,128)(2,1)}, bf16[256,1024]{1,0:T(8,128)(2,1)}, u32[]{:S(2)}, u32[]{:S(2)}) collective-permute-start(bf16[256,1024]{1,0:T(8,128)(2,1)} %bitcast.39), channel_id=1, source_target_pairs={{0,8},{8,0},{1,9},{9,1},{2,10},{10,2},{3,11},{11,3},{4,12},{12,4},... | collective-permute-start | bytes 1572872 | tf_op jit(solution)/shard_map/ppermute | solution.py:394
  322.8 24.2 %all-to-all-start.5 = ((bf16[8,2,64,256]{3,2,1,0:T(8,128)(2,1)}), bf16[8,2,64,256]{3,2,1,0:T(8,128)(2,1)S(1)}, u32[]{:S(2)}, u32[]{:S(2)}) async-start(bf16[8,2,64,256]{3,2,1,0:T(8,128)(2,1)} %maximum_bitcast_fusion), calls=%async_computation.5 | async-start | bytes 1048576 | tf_op jit(solution)/shard_map/all_to_all | solution.py:230
  328.6 22.1 %copy-start.3 = (f32[8,2,64,256]{3,2,1,0:T(8,128)S(1)}, f32[8,2,64,256]{3,2,1,0:T(8,128)}, u32[]{:S(2)}) copy-start(f32[8,2,64,256]{3,2,1,0:T(8,128)} %copy-done.2) | copy-start | bytes 3145732
  347.0 35.2 %collective-permute-start.7 = (bf16[256,1024]{1,0:T(8,128)(2,1)}, bf16[256,1024]{1,0:T(8,128)(2,1)S(1)}, u32[]{:S(2)}, u32[]{:S(2)}) collective-permute-start(bf16[256,1024]{1,0:T(8,128)(2,1)} %fusion.40), channel_id=1, source_target_pairs={{0,16},{16,0},{1,17},{17,1},{2,18},{18,2},{3,19},{19,3},{4,20},{20... | collective-permute-start | bytes 1572872 | tf_op jit(solution)/shard_map/ppermute | solution.py:394
  384.3 36.9 %all-to-all-start.6 = ((bf16[8,2,3,64,256]{4,3,2,1,0:T(8,128)(2,1)}), bf16[8,2,3,64,256]{4,3,2,1,0:T(8,128)(2,1)S(1)}, u32[]{:S(2)}, u32[]{:S(2)}) async-start(bf16[8,2,3,64,256]{4,3,2,1,0:T(8,128)(2,1)} %pair_backward.2), calls=%async_computation.6 | async-start | bytes 3145728 | tf_op jit(solution)/shard_map/all_to_all | solution.py:230
  388.0 101.6 %reduce-scatter.6.cloned.1.call-start = ((), (), s32[]{:S(2)}) async-start(), calls=%async_computation.14 | async-start | bytes 4718592 | tf_op jit(solution)/shard_map/reduce_scatter | solution.py:567
  423.3 12.0 %collective-permute-start.8 = (bf16[512,512]{1,0:T(8,128)(2,1)S(1)}, bf16[512,512]{1,0:T(8,128)(2,1)S(1)}, u32[]{:S(2)}, u32[]{:S(2)}) collective-permute-start(bf16[512,512]{1,0:T(8,128)(2,1)S(1)} %bitcast.337), channel_id=1, source_target_pairs={{0,8},{8,0},{1,9},{9,1},{2,10},{10,2},{3,11},{11,3},{4,12},{12,4},... | collective-permute-start | bytes 1572872 | tf_op jit(solution)/shard_map/ppermute | solution.py:394
  436.1 92.8 %all-gather.12.cloned.1.call-start = ((), (), s32[]{:S(2)}) async-start(), calls=%async_computation.15 | async-start | bytes 4718592 | tf_op jit(solution)/shard_map/all_gather | solution.py:444
  444.6 22.3 %collective-permute-start.9 = (bf16[512,1024]{1,0:T(8,128)(2,1)S(1)}, bf16[512,1024]{1,0:T(8,128)(2,1)}, u32[]{:S(2)}, u32[]{:S(2)}) collective-permute-start(bf16[512,1024]{1,0:T(8,128)(2,1)S(1)} %convolution_convert_fusion.7), channel_id=1, source_target_pairs={{0,8},{8,0},{1,9},{9,1},{2,10},{10,2},{3,11},{11,3},{4,12},{12,4},... | collective-permute-start | bytes 3145736 | tf_op jit(solution)/shard_map/ppermute | solution.py:394
  449.6 17.3 %copy-start.34 = (bf16[512,1024]{1,0:T(8,128)(2,1)S(1)}, bf16[512,1024]{1,0:T(8,128)(2,1)}, u32[]{:S(2)}) copy-start(bf16[512,1024]{1,0:T(8,128)(2,1)} %copy-done.33) | copy-start | bytes 3145732
  451.0 38.7 %all-to-all-start.7 = ((bf16[8,2,64,256]{3,2,1,0:T(8,128)(2,1)}), bf16[8,2,64,256]{3,2,1,0:T(8,128)(2,1)S(1)}, u32[]{:S(2)}, u32[]{:S(2)}) async-start(bf16[8,2,64,256]{3,2,1,0:T(8,128)(2,1)} %maximum_bitcast_fusion.1), calls=%async_computation.8 | async-start | bytes 1048576 | tf_op jit(solution)/shard_map/all_to_all | solution.py:230
  454.5 14.1 %copy-start.73 = (bf16[768,1024]{1,0:T(8,128)(2,1)S(1)}, bf16[768,1024]{1,0:T(8,128)(2,1)}, u32[]{:S(2)}) copy-start(bf16[768,1024]{1,0:T(8,128)(2,1)} %param.27) | copy-start | bytes 4718596
  468.5 25.1 %copy-start.5 = (f32[8,2,64,256]{3,2,1,0:T(8,128)S(1)}, f32[8,2,64,256]{3,2,1,0:T(8,128)}, u32[]{:S(2)}) copy-start(f32[8,2,64,256]{3,2,1,0:T(8,128)} %copy-done.4) | copy-start | bytes 3145732
  470.0 55.9 %collective-permute-start.12 = (bf16[2,256,1024]{2,1,0:T(8,128)(2,1)}, bf16[2,256,1024]{2,1,0:T(8,128)(2,1)}, u32[]{:S(2)}, u32[]{:S(2)}) collective-permute-start(bf16[2,256,1024]{2,1,0:T(8,128)(2,1)} %pad_maximum_fusion.13), channel_id=1, source_target_pairs={{0,8},{8,0},{1,9},{9,1},{2,10},{10,2},{3,11},{11,3},{4,12},{12,4},... | collective-permute-start | bytes 3145736 | tf_op jit(solution)/shard_map/ppermute | solution.py:394
  490.6 38.3 %collective-permute-start.11 = (bf16[128,1024]{1,0:T(8,128)(2,1)S(1)}, bf16[128,1024]{1,0:T(8,128)(2,1)S(1)}, u32[]{:S(2)}, u32[]{:S(2)}) collective-permute-start(bf16[128,1024]{1,0:T(8,128)(2,1)S(1)} %dynamic-slice_bitcast_fusion.1), channel_id=1, source_target_pairs={{0,16},{16,0},{1,17},{17,1},{2,18},{18,2},{3,19},{19,3},{4,20},{20... | collective-permute-start | bytes 786440 | tf_op jit(solution)/shard_map/ppermute | solution.py:394
  493.1 32.7 %collective-permute-start.10 = (bf16[256,768]{1,0:T(8,128)(2,1)}, bf16[256,768]{1,0:T(8,128)(2,1)S(1)}, u32[]{:S(2)}, u32[]{:S(2)}) collective-permute-start(bf16[256,768]{1,0:T(8,128)(2,1)} %convolution_convert_fusion.15), channel_id=1, source_target_pairs={{0,16},{16,0},{1,17},{17,1},{2,18},{18,2},{3,19},{19,3},{4,20},{20... | collective-permute-start | bytes 1179656 | tf_op jit(solution)/shard_map/ppermute | solution.py:394
  493.6 32.1 %copy-start.62 = (bf16[256,768]{1,0:T(8,128)(2,1)S(1)}, bf16[256,768]{1,0:T(8,128)(2,1)}, u32[]{:S(2)}) copy-start(bf16[256,768]{1,0:T(8,128)(2,1)} %convolution_convert_fusion.15) | copy-start | bytes 1179652
  528.9 6.5 copy-start.25
  528.9 27.3 %all-to-all-start.8 = ((bf16[8,2,3,64,256]{4,3,2,1,0:T(8,128)(2,1)}), bf16[8,2,3,64,256]{4,3,2,1,0:T(8,128)(2,1)}, u32[]{:S(2)}, u32[]{:S(2)}) async-start(bf16[8,2,3,64,256]{4,3,2,1,0:T(8,128)(2,1)} %pair_backward.3), calls=%async_computation.10 | async-start | bytes 3145728 | tf_op jit(solution)/shard_map/all_to_all | solution.py:230
  533.4 94.7 %reduce-scatter.8.cloned.1.call-start = ((), (), s32[]{:S(2)}) async-start(), calls=%async_computation.16 | async-start | bytes 5898240 | tf_op jit(solution)/shard_map/reduce_scatter | solution.py:567
  533.9 20.0 %collective-permute-start.13 = (bf16[2,256,768]{2,1,0:T(8,128)(2,1)S(1)}, bf16[2,256,768]{2,1,0:T(8,128)(2,1)}, u32[]{:S(2)}, u32[]{:S(2)}) collective-permute-start(bf16[2,256,768]{2,1,0:T(8,128)(2,1)S(1)} %pad_maximum_fusion.17), channel_id=1, source_target_pairs={{0,8},{8,0},{1,9},{9,1},{2,10},{10,2},{3,11},{11,3},{4,12},{12,4},... | collective-permute-start | bytes 2359304 | tf_op jit(solution)/shard_map/ppermute | solution.py:394
  570.2 94.7 %all-gather.16.cloned.1.call-start = ((), (), s32[]{:S(2)}) async-start(), calls=%async_computation.18 | async-start | bytes 2359296 | tf_op jit(solution)/shard_map/all_gather | solution.py:444
  573.7 124.1 %all-gather.14.cloned.1.call-start = ((), (), s32[]{:S(2)}) async-start(), calls=%async_computation.17 | async-start | bytes 2949120 | tf_op jit(solution)/shard_map/all_gather | solution.py:444
  576.5 6.3 copy-start.28
  581.0 13.8 %collective-permute-start.14 = (bf16[256,1024]{1,0:T(8,128)(2,1)S(1)}, bf16[256,1024]{1,0:T(8,128)(2,1)S(1)}, u32[]{:S(2)}, u32[]{:S(2)}) collective-permute-start(bf16[256,1024]{1,0:T(8,128)(2,1)S(1)} %bitcast.371), channel_id=1, source_target_pairs={{0,8},{8,0},{1,9},{9,1},{2,10},{10,2},{3,11},{11,3},{4,12},{12,4},... | collective-permute-start | bytes 1572872 | tf_op jit(solution)/shard_map/ppermute | solution.py:394
  595.7 25.0 %collective-permute-start.15 = (bf16[256,1024]{1,0:T(8,128)(2,1)S(1)}, bf16[256,1024]{1,0:T(8,128)(2,1)S(1)}, u32[]{:S(2)}, u32[]{:S(2)}) collective-permute-start(bf16[256,1024]{1,0:T(8,128)(2,1)S(1)} %fusion.38), channel_id=1, source_target_pairs={{0,16},{16,0},{1,17},{17,1},{2,18},{18,2},{3,19},{19,3},{4,20},{20... | collective-permute-start | bytes 1572872 | tf_op jit(solution)/shard_map/ppermute | solution.py:394
  598.6 33.0 %copy-start.14 = (bf16[2,2,256,1024]{3,2,1,0:T(8,128)(2,1)S(1)}, bf16[2,2,256,1024]{3,2,1,0:T(8,128)(2,1)}, u32[]{:S(2)}) copy-start(bf16[2,2,256,1024]{3,2,1,0:T(8,128)(2,1)} %pad_maximum_fusion.6) | copy-start | bytes 6291460
  629.1 17.4 %collective-permute-start.19 = (bf16[160,1024]{1,0:T(8,128)(2,1)S(1)}, bf16[160,1024]{1,0:T(8,128)(2,1)S(1)}, u32[]{:S(2)}, u32[]{:S(2)}) collective-permute-start(bf16[160,1024]{1,0:T(8,128)(2,1)S(1)} %dynamic-slice_bitcast_fusion), channel_id=1, source_target_pairs={{0,16},{16,0},{1,17},{17,1},{2,18},{18,2},{3,19},{19,3},{4,20},{20... | collective-permute-start | bytes 983048 | tf_op jit(solution)/shard_map/ppermute | solution.py:394
  631.7 14.9 %copy-start.55 = (bf16[2,160,1024]{2,1,0:T(8,128)(2,1)S(1)}, bf16[2,160,1024]{2,1,0:T(8,128)(2,1)}, u32[]{:S(2)}) copy-start(bf16[2,160,1024]{2,1,0:T(8,128)(2,1)} %reduce-scatter.8.cloned.1.call-done) | copy-start | bytes 1966084
  664.9 6.3 collective-permute-start.17
  666.4 26.5 %collective-permute-start.16 = (bf16[2,256,1024]{2,1,0:T(8,128)(2,1)}, bf16[2,256,1024]{2,1,0:T(8,128)(2,1)}, u32[]{:S(2)}, u32[]{:S(2)}) collective-permute-start(bf16[2,256,1024]{2,1,0:T(8,128)(2,1)} %pad_maximum_fusion.14), channel_id=1, source_target_pairs={{0,8},{8,0},{1,9},{9,1},{2,10},{10,2},{3,11},{11,3},{4,12},{12,4},... | collective-permute-start | bytes 3145736 | tf_op jit(solution)/shard_map/ppermute | solution.py:394
  681.4 10.0 %collective-permute-start.18 = (bf16[80,256]{1,0:T(8,128)(2,1)S(1)}, bf16[80,256]{1,0:T(8,128)(2,1)S(1)}, u32[]{:S(2)}, u32[]{:S(2)}) collective-permute-start(bf16[80,256]{1,0:T(8,128)(2,1)S(1)} %dynamic-slice_bitcast_fusion.2), channel_id=1, source_target_pairs={{0,16},{16,0},{1,17},{17,1},{2,18},{18,2},{3,19},{19,3},{4,20},{20... | collective-permute-start | bytes 122888 | tf_op jit(solution)/shard_map/ppermute | solution.py:394
  702.9 5.8 copy-start.1
  (54 other events, 117.9 us)
Sparse Core Ops, SparseCore 0:
  28.5 26.8 all-gather.9
  69.5 59.3 all-gather.17
  131.9 82.0 all-gather.19
  282.1 124.7 reduce-scatter.3
  435.4 54.1 reduce-scatter.5
  491.6 36.6 all-gather.11
  570.4 57.6 reduce-scatter.7
  630.5 27.8 all-gather.15
  660.9 30.4 all-gather.13

commit v9 on v8

--- a/solution.py
+++ b/solution.py
@@ -624,19 +624,23 @@
     patch_terms = jnp.pad(patch_terms, ((0, 0), (0, 0), (0, width - patch_width)))
     grad_mixed, grad_self_low = tie(to_pairs(self_whole[: 2 * cols], grad_self_low, 1)[:, :, 0], grad_self_low)
     output_terms = by_shard(self_mixed_t, grad_self_low)
-    grad_mixed, patch_half, middle_part = tie(exchange_rows(grad_mixed), patch_half, middle_part)
+    grad_mixed, patch_half = tie(exchange_rows(grad_mixed), patch_half)
     patch_two = jnp.stack([patch_half, swap(patch_half, "far")])
+    last_terms = jnp.pad(
+        jnp.concatenate([output_terms, patch_terms], axis=1), ((0, 0), (3 * cols, 0), (0, 0))
+    )
+    grads = pair_backward(qkv, qkv, 1, None, grad_mixed, self_wide, self_log)
+    grads, patch_two, middle_part, result_four, last_terms = tie(
+        grads, patch_two, middle_part, result_four, last_terms
+    )
     middle_own, middle_away = own_and_away(middle_part)
-    middle_away = swap(middle_away, "far")
-    grads = pair_backward(qkv, qkv, 1, None, grad_mixed, self_wide, self_log)
-    grads, patch_two, hidden_total, middle_away, result_four = tie(
-        grads, patch_two, hidden_total, middle_away, result_four
-    )
     patch_four = jnp.stack([patch_two, swap(patch_two, "near")])
+    grads, patch_four, middle_away, hidden_total = tie(
+        exchange_rows(grads), patch_four, swap(middle_away, "far"), hidden_total
+    )
     middle_total = join_rows(add_far(middle_own, middle_away))
-    grads, patch_four = tie(exchange_rows(grads), patch_four)
     grad_qkv_t = from_pairs(grads)
-    last_terms = jnp.concatenate([by_shard(grad_qkv_t, normed_one), output_terms, patch_terms], axis=1)
+    last_terms = lax.dynamic_update_slice_in_dim(last_terms, by_shard(grad_qkv_t, normed_one), 0, 1)
     last_part = part_rows(last_terms)
     grad_one = half_sum_near(mul(grad_qkv_t, qkv_both, TN))
     gain_half, unit_half, rate_half, self_half = (
@@ -653,7 +657,9 @@
         axis=0,
     )
     input_two = jnp.stack([input_half, swap(input_half, "far")])
-    last_part, input_two, table_term = tie(last_part, input_two, table_term)
+    last_part, input_two = tie(last_part, input_two)
+    input_four = jnp.stack([input_two, swap(input_two, "near")])
+    input_four, table_term = tie(input_four, table_term)
     small = [sum_near(table_term), hidden_gain_term[None], cross_gain_term[None], jnp.zeros((14, width), WIDE)]
     small = jnp.stack(both_columns(jnp.concatenate(small, axis=0).astype(LOW)))
     small = jnp.sum(lax.all_gather(small, "rows", axis=0).astype(WIDE), axis=0).astype(LOW)
@@ -661,7 +667,7 @@
         lax.dynamic_index_in_dim(small, index, 0, keepdims=False) for index in (far, 1 - far)
     )
     small = small_own.astype(WIDE) + swap(small_away, "far").astype(WIDE)
-    input_grads = over_heads(jnp.stack([input_two, swap(input_two, "near")]))
+    input_grads = over_heads(input_four)
     outputs, patch_grads = over_heads(result_four), over_heads(patch_four)
     last_own, last_away = own_and_away(last_part)
     last_total = join_rows(add_far(last_own, swap(last_away, "far")))

time: 726 us -> 735 us (1.012)
  waiting for transfers between devices: 279 us -> 287 us
    ppermute x20, waiting for transfers between devices: 181 us -> 200 us  [swap(): return lax.ppermute(value, axis, [(0, 1), (1, 0)])]
    reduce_scatter x2, waiting for transfers between devices: 24.3 us -> 7.85 us  [part_rows(): return lax.psum_scatter(both, 'rows', scatter_dimension=1, tiled=True)]
    unnamed x177 -> x175, local copies, waits for them, and re-layouts: 39.5 us -> 43.6 us
  transfers between devices with their start and end apart: 37 -> 37, of which waited for: 22 -> 22; matrix products, arithmetic and copies ran while one was open for 23% -> 24% of each run, Pallas kernels for 12% -> 12%
where the time goes in v9:
time: 735 us; the launch traced here: 725 us
  waiting for transfers between devices  287 us (39%)
  local copies, waits for them, and re-layouts  106 us (14%)
  Pallas kernels  88.9 us (12%)
  other arithmetic  81.7 us (11%)
  starting transfers between devices  62.1 us (8%)
  matrix products  60 us (8%)
  blocking collectives  22.7 us (3%)
  between operations  15.5 us (2%)
    ppermute x20, waiting for transfers between devices, swap(): return lax.ppermute(value, axis, [(0, 1), (1, 0)])  200 us
    all_to_all x8, waiting for transfers between devices, exchange_rows(): return lax.all_to_all(value, 'rows', 0, 0, tiled=True)  79.9 us
    dot_general x31, matrix products, mul(): return lax.dot_general(left, right, dims, preferred_element_type=WIDE)  59 us
    pallas_call x2, Pallas kernels, pair_backward(): pl.pallas_call(kernel, grid_spec=pltpu.PrefetchScalarGridSpec(num_scalar_...  55 us
    unnamed x175, local copies, waits for them, and re-layouts  43.6 us
    pallas_call x2, Pallas kernels, pair_forward(): pl.pallas_call(kernel, grid_spec=pltpu.PrefetchScalarGridSpec(num_scalar_...  33.9 us
    all_to_all x8, starting transfers between devices, exchange_rows(): return lax.all_to_all(value, 'rows', 0, 0, tiled=True)  32 us
    ppermute x20, starting transfers between devices, swap(): return lax.ppermute(value, axis, [(0, 1), (1, 0)])  29.2 us
  transfers between devices with their start and end apart: 37, of which 22 were waited for; matrix products, arithmetic and copies ran while one was open for 24% of the time, Pallas kernels for 12%

profile of v9, /device:TPU:0, one launch (start us, length us, event | category | flops | bytes accessed | tf_op | source)
XLA Modules:
  0.0 724.5 jit_solution(6741831340697535392)
XLA Ops:
  7.2 2.7 copy.97
  10.0 2.7 copy.98
  14.4 4.0 collective-permute-start
  19.9 7.8 %collective-permute-done = bf16[96,1024]{1,0:T(8,128)(2,1)S(1)} collective-permute-done((bf16[96,1024]{1,0:T(8,128)(2,1)}, bf16[96,1024]{1,0:T(8,128)(2,1)S(1)}, u32[]{:S(2)}, u32[]{:S(2)}) %collective-permute-start) | collective-permute-done | bytes 196640 | tf_op jit(solution)/shard_map/ppermute | solution.py:394
  40.9 17.1 %collective-permute-done.1 = bf16[160,1024]{1,0:T(8,128)(2,1)} collective-permute-done((bf16[160,1024]{1,0:T(8,128)(2,1)}, bf16[160,1024]{1,0:T(8,128)(2,1)}, u32[]{:S(2)}, u32[]{:S(2)}) %collective-permute-start.1) | collective-permute-done | bytes 327712 | tf_op jit(solution)/shard_map/ppermute | solution.py:394
  59.9 8.5 %collective-permute-done.2 = bf16[2,96,1024]{2,1,0:T(8,128)(2,1)S(1)} collective-permute-done((bf16[2,96,1024]{2,1,0:T(8,128)(2,1)S(1)}, bf16[2,96,1024]{2,1,0:T(8,128)(2,1)S(1)}, u32[]{:S(2)}, u32[]{:S(2)}) %collective-permute-start.2) | collective-permute-done | bytes 393248 | tf_op jit(solution)/shard_map/ppermute | solution.py:394
  72.8 2.8 constant_dynamic-update-slice_fusion.3
  75.5 3.3 convolution_convert_fusion.3
  78.8 2.9 convolution_convert_fusion.4
  83.0 4.3 all-to-all-start
  89.2 23.7 %all-to-all-done.q_ref.k_ref.v_ref = bf16[8,2,3,64,256]{4,3,2,1,0:T(8,128)(2,1)} async-done(((bf16[8,2,3,64,256]{4,3,2,1,0:T(8,128)(2,1)}), bf16[8,2,3,64,256]{4,3,2,1,0:T(8,128)(2,1)}, u32[]{:S(2)}, u32[]{:S(2)}) %all-to-all-start) | async-done | bytes 1572896 | tf_op jit(solution)/shard_map/all_to_all | solution.py:230
  122.4 19.0 %pair_forward.2 = (bf16[8,2,64,256]{3,2,1,0:T(8,128)(2,1)}, f32[8,2,64,256]{3,2,1,0:T(8,128)S(1)}, f32[8,2,1,256]{3,2,1,0:T(1,128)S(1)}) custom-call(s32[2]{0:T(128)S(1)} %broadcast_13_len_ref.2.len_ref, bf16[8,2,3,64,256]{4,3,2,1,0:T(8,128)(2,1)} %all-to-all-done.q_ref.k_ref.v_ref, bf16[8,2,3,64,256]{4,3,2,1,0:T(8,128)(2,1)} %all-to-all-done.q_ref.k_ref.v_ref, ...), custom_call_target="tpu_custom_call" | custom-call | flops 20132659200 | bytes 8388608 | tf_op jit(solution)/shard_map/pair_forward/pallas_call | solution.py:282
  142.4 3.7 all-to-all-start.1
  149.0 2.9 copy-done.22
  151.9 3.3 slice.169
  158.5 4.2 all-to-all-start.2
  162.9 3.7 fusion.75
  166.7 6.2 fusion.76
  173.1 11.6 %collective-permute-done.3 = bf16[512,512]{1,0:T(8,128)(2,1)S(1)} collective-permute-done((bf16[512,512]{1,0:T(8,128)(2,1)}, bf16[512,512]{1,0:T(8,128)(2,1)S(1)}, u32[]{:S(2)}, u32[]{:S(2)}) %collective-permute-start.3) | collective-permute-done | bytes 524320 | tf_op jit(solution)/shard_map/ppermute | solution.py:394
  189.3 4.2 all-to-all-start.3
  193.6 9.6 %all-to-all-done.3.q_ref = bf16[8,2,1,64,256]{4,3,2,1,0:T(8,128)(2,1)} async-done(((bf16[8,2,1,64,256]{4,3,2,1,0:T(8,128)(2,1)}), bf16[8,2,1,64,256]{4,3,2,1,0:T(8,128)(2,1)}, u32[]{:S(2)}, u32[]{:S(2)}) %all-to-all-start.3) | async-done | bytes 524320 | tf_op jit(solution)/shard_map/all_to_all | solution.py:230
  203.3 15.0 %pair_forward.3 = (bf16[8,2,64,256]{3,2,1,0:T(8,128)(2,1)S(1)}, f32[8,2,64,256]{3,2,1,0:T(8,128)S(1)}, f32[8,2,1,256]{3,2,1,0:T(1,128)S(1)}) custom-call(s32[2]{0:T(128)S(1)} %dynamic_slice.117.len_ref, bf16[8,2,1,64,256]{4,3,2,1,0:T(8,128)(2,1)} %all-to-all-done.3.q_ref, bf16[8,2,2,64,256]{4,3,2,1,0:T(8,128)(2,1)S(1)} %all-to-all-done.2.k_ref.v_ref, ...), custom_call_target="tpu_custom_call" | custom-call | flops 14092861440 | bytes 8388608 | tf_op jit(solution)/shard_map/pair_forward/pallas_call | solution.py:282
  218.3 12.3 %all_to_all.45 = bf16[8,2,64,256]{3,2,1,0:T(8,128)(2,1)S(1)} all-to-all(bf16[8,2,64,256]{3,2,1,0:T(8,128)(2,1)S(1)} %get-tuple-element.74), channel_id=1, replica_groups=mesh['far'=2,'near'=2,'rows'=8] {'rows'}, dimensions={0} | all-to-all | bytes 1048576 | tf_op jit(solution)/shard_map/all_to_all | solution.py:230
  233.4 10.9 %collective-permute-done.4 = bf16[512,512]{1,0:T(8,128)(2,1)S(1)} collective-permute-done((bf16[512,512]{1,0:T(8,128)(2,1)S(1)}, bf16[512,512]{1,0:T(8,128)(2,1)S(1)}, u32[]{:S(2)}, u32[]{:S(2)}) %collective-permute-start.4) | collective-permute-done | bytes 524320 | tf_op jit(solution)/shard_map/ppermute | solution.py:394
  247.3 2.8 slice.177
  256.5 5.1 multiply_convert_fusion
  261.6 3.5 fusion.22
  265.0 4.7 convolution_convert_fusion.1
  269.8 4.4 convolution_convert_fusion.2
  274.2 7.8 %pad_maximum_fusion = bf16[2,2048,1024]{2,1,0:T(8,128)(2,1)} fusion(bf16[2,1024,1024]{2,1,0:T(8,128)(2,1)} %bitcast.326, bf16[2,1024,1024]{2,1,0:T(8,128)(2,1)} %bitcast.327), kind=kLoop, calls=%fused_computation.3 | loop fusion | flops 16777216 | bytes 16777216 | tf_op jit(solution)/shard_map/concatenate | solution.py:578
  284.8 4.6 fusion.81
  290.4 24.3 %collective-permute-done.5 = bf16[512,1024]{1,0:T(8,128)(2,1)} collective-permute-done((bf16[512,1024]{1,0:T(8,128)(2,1)}, bf16[512,1024]{1,0:T(8,128)(2,1)}, u32[]{:S(2)}, u32[]{:S(2)}) %collective-permute-start.5) | collective-permute-done | bytes 1048608 | tf_op jit(solution)/shard_map/ppermute | solution.py:394
  322.7 3.7 all-to-all-start.5
  328.5 7.0 collective-permute-done.6
  337.7 8.6 %all-to-all-done.5.g_ref = bf16[8,2,64,256]{3,2,1,0:T(8,128)(2,1)S(1)} async-done(((bf16[8,2,64,256]{3,2,1,0:T(8,128)(2,1)}), bf16[8,2,64,256]{3,2,1,0:T(8,128)(2,1)S(1)}, u32[]{:S(2)}, u32[]{:S(2)}) %all-to-all-start.5) | async-done | bytes 524320 | tf_op jit(solution)/shard_map/all_to_all | solution.py:230
  346.3 4.4 collective-permute-start.7
  350.7 22.8 %pair_backward.2 = bf16[8,2,3,64,256]{4,3,2,1,0:T(8,128)(2,1)} custom-call(s32[2]{0:T(128)S(1)} %dynamic_slice.117.len_ref, bf16[8,2,1,64,256]{4,3,2,1,0:T(8,128)(2,1)} %all-to-all-done.3.q_ref, bf16[8,2,2,64,256]{4,3,2,1,0:T(8,128)(2,1)S(1)} %all-to-all-done.2.k_ref.v_ref, bf16[8,2,2,64,256]{4,3,2,1,0:T(8,128)(2,1)S(1)} %all-to-all-done.2.k_ref.v_ref, ...), custom_call_target="tpu_custom_call" | custom-call | flops 20132659200 | bytes 8388608 | tf_op jit(solution)/shard_map/pair_backward/pallas_call | solution.py:364
  373.5 8.7 %collective-permute-done.7 = bf16[256,1024]{1,0:T(8,128)(2,1)S(1)} collective-permute-done((bf16[256,1024]{1,0:T(8,128)(2,1)}, bf16[256,1024]{1,0:T(8,128)(2,1)S(1)}, u32[]{:S(2)}, u32[]{:S(2)}) %collective-permute-start.7) | collective-permute-done | bytes 524320 | tf_op jit(solution)/shard_map/ppermute | solution.py:394
  384.3 3.7 all-to-all-start.6
  389.8 31.4 %all-to-all-done.6 = bf16[8,2,3,64,256]{4,3,2,1,0:T(8,128)(2,1)S(1)} async-done(((bf16[8,2,3,64,256]{4,3,2,1,0:T(8,128)(2,1)}), bf16[8,2,3,64,256]{4,3,2,1,0:T(8,128)(2,1)S(1)}, u32[]{:S(2)}, u32[]{:S(2)}) %all-to-all-start.6) | async-done | bytes 1572896 | tf_op jit(solution)/shard_map/all_to_all | solution.py:230
  429.3 6.0 collective-permute-done.8
  446.9 14.6 %collective-permute-done.9 = bf16[512,1024]{1,0:T(8,128)(2,1)} collective-permute-done((bf16[512,1024]{1,0:T(8,128)(2,1)S(1)}, bf16[512,1024]{1,0:T(8,128)(2,1)}, u32[]{:S(2)}, u32[]{:S(2)}) %collective-permute-start.9) | collective-permute-done | bytes 1048608 | tf_op jit(solution)/shard_map/ppermute | solution.py:394
  466.1 2.6 multiply_reduce_fusion
  472.9 4.5 all-to-all-start.7
  479.3 6.1 fusion.2
  485.4 6.6 all-to-all-done.7.g_ref
  494.4 32.1 %pair_backward.3 = bf16[8,2,3,64,256]{4,3,2,1,0:T(8,128)(2,1)} custom-call(s32[2]{0:T(128)S(1)} %broadcast_13_len_ref.2.len_ref, bf16[8,2,3,64,256]{4,3,2,1,0:T(8,128)(2,1)} %all-to-all-done.q_ref.k_ref.v_ref, bf16[8,2,3,64,256]{4,3,2,1,0:T(8,128)(2,1)} %all-to-all-done.q_ref.k_ref.v_ref, bf16[8,2,3,64,256]{4,3,2,1,0:T(8,128)(2,1)} %all-to-all-done.q_ref.k_ref.v_ref, ...), custom_call_target="tpu_custom_call" | custom-call | flops 30198988800 | bytes 8388608 | tf_op jit(solution)/shard_map/pair_backward/pallas_call | solution.py:364
  526.6 3.1 pad_maximum_fusion.5
  529.8 3.7 all-to-all-start.8
  535.8 23.4 %collective-permute-done.12 = bf16[2,256,768]{2,1,0:T(8,128)(2,1)S(1)} collective-permute-done((bf16[2,256,768]{2,1,0:T(8,128)(2,1)S(1)}, bf16[2,256,768]{2,1,0:T(8,128)(2,1)S(1)}, u32[]{:S(2)}, u32[]{:S(2)}) %collective-permute-start.12) | collective-permute-done | bytes 786464 | tf_op jit(solution)/shard_map/ppermute | solution.py:394
  570.5 4.7 fusion.10
  577.5 11.2 %collective-permute-done.14 = bf16[256,1024]{1,0:T(8,128)(2,1)S(1)} collective-permute-done((bf16[256,1024]{1,0:T(8,128)(2,1)S(1)}, bf16[256,1024]{1,0:T(8,128)(2,1)S(1)}, u32[]{:S(2)}, u32[]{:S(2)}) %collective-permute-start.14) | collective-permute-done | bytes 524320 | tf_op jit(solution)/shard_map/ppermute | solution.py:394
  593.4 20.8 %collective-permute-done.15 = bf16[256,1024]{1,0:T(8,128)(2,1)S(1)} collective-permute-done((bf16[256,1024]{1,0:T(8,128)(2,1)S(1)}, bf16[256,1024]{1,0:T(8,128)(2,1)S(1)}, u32[]{:S(2)}, u32[]{:S(2)}) %collective-permute-start.15) | collective-permute-done | bytes 524320 | tf_op jit(solution)/shard_map/ppermute | solution.py:394
  615.3 7.9 %reduce-scatter.8.cloned.1.call-done = bf16[2,160,1024]{2,1,0:T(8,128)(2,1)} async-done(((bf16[2,1280,1024]{2,1,0:T(8,128)(2,1)}), bf16[2,160,1024]{2,1,0:T(8,128)(2,1)}) %reduce-scatter.8.cloned.1.call-update) | async-done | bytes 655376 | tf_op jit(solution)/shard_map/reduce_scatter | solution.py:567
  626.6 4.6 reverse_select_fusion.2
  631.2 10.4 %collective-permute-done.19 = bf16[160,1024]{1,0:T(8,128)(2,1)S(1)} collective-permute-done((bf16[160,1024]{1,0:T(8,128)(2,1)S(1)}, bf16[160,1024]{1,0:T(8,128)(2,1)S(1)}, u32[]{:S(2)}, u32[]{:S(2)}) %collective-permute-start.19) | collective-permute-done | bytes 327712 | tf_op jit(solution)/shard_map/ppermute | solution.py:394
  648.3 4.4 slice_convert_fusion
  652.8 5.3 copy.127
  665.4 2.9 copy.125
  668.3 14.4 %collective-permute-done.16 = bf16[2,256,1024]{2,1,0:T(8,128)(2,1)} collective-permute-done((bf16[2,256,1024]{2,1,0:T(8,128)(2,1)}, bf16[2,256,1024]{2,1,0:T(8,128)(2,1)}, u32[]{:S(2)}, u32[]{:S(2)}) %collective-permute-start.16) | collective-permute-done | bytes 1048608 | tf_op jit(solution)/shard_map/ppermute | solution.py:394
  686.8 2.8 collective-permute-done.17
  689.8 10.4 %all-gather.2 = bf16[16,80,256]{2,1,0:T(8,128)(2,1)S(1)} all-gather(bf16[2,80,256]{2,1,0:T(8,128)(2,1)S(1)} %pad_maximum_fusion.21), channel_id=4, replica_groups=mesh['far'=2,'near'=2,'rows'=8] {'rows'}, dimensions={0}, use_global_device_ids=true | all-gather | bytes 737280 | tf_op jit(solution)/shard_map/all_gather | solution.py:665
  700.3 2.9 collective-permute-start.18
  711.9 3.7 copy.123
  (381 shorter events, 165.9 us)
Async XLA Ops:
  7.2 224.9 %copy-start = (bf16[4,256,1024]{2,1,0:T(8,128)(2,1)S(1)}, bf16[4,256,1024]{2,1,0:T(8,128)(2,1)}, u32[]{:S(2)}) copy-start(bf16[4,256,1024]{2,1,0:T(8,128)(2,1)} %param.31) | copy-start | bytes 6291460
  7.2 65.6 %all-gather.10.cloned.1.call-start = ((), (), s32[]{:S(2)}) async-start(), calls=%async_computation.12 | async-start | bytes 1769472 | tf_op jit(solution)/shard_map/all_gather | solution.py:444
  10.0 8.4 %copy-start.67 = (s32[4,256]{1,0:T(4,128)S(1)}, s32[4,256]{1,0:T(4,128)}, u32[]{:S(2)}) copy-start(s32[4,256]{1,0:T(4,128)} %param.17) | copy-start | bytes 12292
  12.7 18.1 %copy-start.63 = (bf16[32,2,1024]{2,1,0:T(2,128)(2,1)S(1)}, bf16[32,2,1024]{2,1,0:T(2,128)(2,1)}, u32[]{:S(2)}) copy-start(bf16[32,2,1024]{2,1,0:T(2,128)(2,1)} %param.20) | copy-start | bytes 393220
  12.7 20.0 %copy-start.48 = (bf16[2,1024,256]{2,1,0:T(8,128)(2,1)S(1)}, bf16[2,1024,256]{2,1,0:T(8,128)(2,1)}, u32[]{:S(2)}) copy-start(bf16[2,1024,256]{2,1,0:T(8,128)(2,1)} %param.25) | copy-start | bytes 3145732
  14.4 13.4 %collective-permute-start = (bf16[96,1024]{1,0:T(8,128)(2,1)}, bf16[96,1024]{1,0:T(8,128)(2,1)S(1)}, u32[]{:S(2)}, u32[]{:S(2)}) collective-permute-start(bf16[96,1024]{1,0:T(8,128)(2,1)} %constant_dynamic-slice_fusion.20), channel_id=1, source_target_pairs={{0,16},{16,0},{1,17},{17,1},{2,18},{18,2},{3,19},{19,3},{4,20},{20... | collective-permute-start | bytes 589832 | tf_op jit(solution)/shard_map/ppermute | solution.py:394
  19.9 11.5 %copy-start.64 = (f32[2,256]{1,0:T(2,128)}, f32[2,256]{1,0:T(2,128)S(1)}, u32[]{:S(2)}) copy-start(f32[2,256]{1,0:T(2,128)S(1)} %get-tuple-element.207) | copy-start | bytes 6148
  28.4 117.7 %all-gather.18.cloned.1.call-start = ((), (), s32[]{:S(2)}) async-start(), calls=%async_computation.19 | async-start | bytes 8257536 | tf_op jit(solution)/shard_map/all_gather | solution.py:522
  40.8 17.1 %collective-permute-start.1 = (bf16[160,1024]{1,0:T(8,128)(2,1)}, bf16[160,1024]{1,0:T(8,128)(2,1)}, u32[]{:S(2)}, u32[]{:S(2)}) collective-permute-start(bf16[160,1024]{1,0:T(8,128)(2,1)} %pad_maximum_fusion.19), channel_id=1, source_target_pairs={{0,16},{16,0},{1,17},{17,1},{2,18},{18,2},{3,19},{19,3},{4,20},{20... | collective-permute-start | bytes 983048 | tf_op jit(solution)/shard_map/ppermute | solution.py:394
  58.9 9.4 %collective-permute-start.2 = (bf16[2,96,1024]{2,1,0:T(8,128)(2,1)S(1)}, bf16[2,96,1024]{2,1,0:T(8,128)(2,1)S(1)}, u32[]{:S(2)}, u32[]{:S(2)}) collective-permute-start(bf16[2,96,1024]{2,1,0:T(8,128)(2,1)S(1)} %fusion.59), channel_id=1, source_target_pairs={{0,8},{8,0},{1,9},{9,1},{2,10},{10,2},{3,11},{11,3},{4,12},{12,4},... | collective-permute-start | bytes 1179656 | tf_op jit(solution)/shard_map/ppermute | solution.py:394
  83.0 29.9 %all-to-all-start = ((bf16[8,2,3,64,256]{4,3,2,1,0:T(8,128)(2,1)}), bf16[8,2,3,64,256]{4,3,2,1,0:T(8,128)(2,1)}, u32[]{:S(2)}, u32[]{:S(2)}) async-start(bf16[8,2,3,64,256]{4,3,2,1,0:T(8,128)(2,1)} %pad_maximum_fusion.7), calls=%async_computation | async-start | bytes 3145728 | tf_op jit(solution)/shard_map/all_to_all | solution.py:230
  87.3 27.4 %copy-start.69 = (bf16[1024]{0:T(1024)(128)(2,1)S(1)}, bf16[1024]{0:T(1024)(128)(2,1)}, u32[]{:S(2)}) copy-start(bf16[1024]{0:T(1024)(128)(2,1)} %param.23) | copy-start | bytes 6148
  87.3 160.0 %all-gather.20.cloned.1.call-start = ((), (), s32[]{:S(2)}) async-start(), calls=%async_computation.20 | async-start | bytes 8912896 | tf_op jit(solution)/shard_map/all_gather | solution.py:536
  142.4 14.7 %all-to-all-start.1 = ((bf16[8,2,64,256]{3,2,1,0:T(8,128)(2,1)}), bf16[8,2,64,256]{3,2,1,0:T(8,128)(2,1)S(1)}, u32[]{:S(2)}, u32[]{:S(2)}) async-start(bf16[8,2,64,256]{3,2,1,0:T(8,128)(2,1)} %get-tuple-element.69), calls=%async_computation.1 | async-start | bytes 1048576 | tf_op jit(solution)/shard_map/all_to_all | solution.py:230
  148.3 7.0 copy-start.17
  158.5 30.8 %all-to-all-start.2 = ((bf16[8,2,2,64,256]{4,3,2,1,0:T(8,128)(2,1)}), bf16[8,2,2,64,256]{4,3,2,1,0:T(8,128)(2,1)S(1)}, u32[]{:S(2)}, u32[]{:S(2)}) async-start(bf16[8,2,2,64,256]{4,3,2,1,0:T(8,128)(2,1)} %pad_maximum_fusion.11), calls=%async_computation.2 | async-start | bytes 2097152 | tf_op jit(solution)/shard_map/all_to_all | solution.py:230
  162.7 22.0 %collective-permute-start.3 = (bf16[512,512]{1,0:T(8,128)(2,1)}, bf16[512,512]{1,0:T(8,128)(2,1)S(1)}, u32[]{:S(2)}, u32[]{:S(2)}) collective-permute-start(bf16[512,512]{1,0:T(8,128)(2,1)} %bitcast.333), channel_id=1, source_target_pairs={{0,8},{8,0},{1,9},{9,1},{2,10},{10,2},{3,11},{11,3},{4,12},{12,4},... | collective-permute-start | bytes 1572872 | tf_op jit(solution)/shard_map/ppermute | solution.py:394
  172.9 11.8 %copy-start.33 = (bf16[2,256,1024]{2,1,0:T(8,128)(2,1)S(1)}, bf16[2,256,1024]{2,1,0:T(8,128)(2,1)}, u32[]{:S(2)}) copy-start(bf16[2,256,1024]{2,1,0:T(8,128)(2,1)} %get-tuple-element.199) | copy-start | bytes 3145732
  172.9 11.8 %copy-start.36 = (bf16[64,8,2,256]{3,1,2,0:T(8,128)(2,1)S(1)}, bf16[64,8,2,256]{3,1,2,0:T(8,128)(2,1)}, u32[]{:S(2)}) copy-start(bf16[64,8,2,256]{3,1,2,0:T(8,128)(2,1)} %copy.137) | copy-start | bytes 1572868
  188.0 5.6 copy-start.73
  189.3 13.9 %all-to-all-start.3 = ((bf16[8,2,1,64,256]{4,3,2,1,0:T(8,128)(2,1)}), bf16[8,2,1,64,256]{4,3,2,1,0:T(8,128)(2,1)}, u32[]{:S(2)}, u32[]{:S(2)}) async-start(bf16[8,2,1,64,256]{4,3,2,1,0:T(8,128)(2,1)} %pad_maximum_fusion.17), calls=%async_computation.3 | async-start | bytes 1048576 | tf_op jit(solution)/shard_map/all_to_all | solution.py:230
  193.5 272.5 %reduce-scatter.4.cloned.1.call-start = ((), (), s32[]{:S(2)}) async-start(), calls=%async_computation.13 | async-start | bytes 8912896 | tf_op jit(solution)/shard_map/reduce_scatter | solution.py:585
  218.2 14.9 %copy-start.2 = (f32[8,2,64,256]{3,2,1,0:T(8,128)}, f32[8,2,64,256]{3,2,1,0:T(8,128)S(1)}, u32[]{:S(2)}) copy-start(f32[8,2,64,256]{3,2,1,0:T(8,128)S(1)} %get-tuple-element.82.wide_ref) | copy-start | bytes 3145732
  218.2 13.8 %copy-start.70 = (bf16[1024]{0:T(1024)(128)(2,1)S(1)}, bf16[1024]{0:T(1024)(128)(2,1)}, u32[]{:S(2)}) copy-start(bf16[1024]{0:T(1024)(128)(2,1)} %param.28) | copy-start | bytes 6148
  231.2 13.1 %copy-start.59 = (bf16[64,8,2,256]{3,1,2,0:T(8,128)(2,1)}, bf16[64,8,2,256]{3,1,2,0:T(8,128)(2,1)S(1)}, u32[]{:S(2)}) copy-start(bf16[64,8,2,256]{3,1,2,0:T(8,128)(2,1)S(1)} %copy.138) | copy-start | bytes 1572868
  231.2 13.1 %collective-permute-start.4 = (bf16[512,512]{1,0:T(8,128)(2,1)S(1)}, bf16[512,512]{1,0:T(8,128)(2,1)S(1)}, u32[]{:S(2)}, u32[]{:S(2)}) collective-permute-start(bf16[512,512]{1,0:T(8,128)(2,1)S(1)} %bitcast.368), channel_id=1, source_target_pairs={{0,8},{8,0},{1,9},{9,1},{2,10},{10,2},{3,11},{11,3},{4,12},{12,4},... | collective-permute-start | bytes 1572872 | tf_op jit(solution)/shard_map/ppermute | solution.py:394
  233.1 11.2 %copy-start.7 = (f32[512,1024]{1,0:T(8,128)S(1)}, f32[512,1024]{1,0:T(8,128)}, u32[]{:S(2)}) copy-start(f32[512,1024]{1,0:T(8,128)} %copy-done.6) | copy-start | bytes 6291460
  261.6 8.2 %copy-start.74 = (bf16[512,2048]{1,0:T(8,128)(2,1)}, bf16[512,2048]{1,0:T(8,128)(2,1)S(1)}, u32[]{:S(2)}) copy-start(bf16[512,2048]{1,0:T(8,128)(2,1)S(1)} %get-tuple-element.77) | copy-start | bytes 6291460
  282.0 32.8 %collective-permute-start.5 = (bf16[512,1024]{1,0:T(8,128)(2,1)}, bf16[512,1024]{1,0:T(8,128)(2,1)}, u32[]{:S(2)}, u32[]{:S(2)}) collective-permute-start(bf16[512,1024]{1,0:T(8,128)(2,1)} %fusion.22), channel_id=1, source_target_pairs={{0,8},{8,0},{1,9},{9,1},{2,10},{10,2},{3,11},{11,3},{4,12},{12,4},... | collective-permute-start | bytes 3145736 | tf_op jit(solution)/shard_map/ppermute | solution.py:394
  284.8 30.0 %copy-start.50 = (bf16[512,1024]{1,0:T(8,128)(2,1)S(1)}, bf16[512,1024]{1,0:T(8,128)(2,1)}, u32[]{:S(2)}) copy-start(bf16[512,1024]{1,0:T(8,128)(2,1)} %fusion.22) | copy-start | bytes 3145732
  289.4 27.0 %copy-start.40 = (f32[2,2,128,1024]{3,2,1,0:T(8,128)}, f32[2,2,128,1024]{3,2,1,0:T(8,128)S(1)}, u32[]{:S(2)}) copy-start(f32[2,2,128,1024]{3,2,1,0:T(8,128)S(1)} %fusion.81) | copy-start | bytes 6291460
  316.4 19.1 %collective-permute-start.6 = (bf16[256,1024]{1,0:T(8,128)(2,1)}, bf16[256,1024]{1,0:T(8,128)(2,1)}, u32[]{:S(2)}, u32[]{:S(2)}) collective-permute-start(bf16[256,1024]{1,0:T(8,128)(2,1)} %bitcast.39), channel_id=1, source_target_pairs={{0,8},{8,0},{1,9},{9,1},{2,10},{10,2},{3,11},{11,3},{4,12},{12,4},... | collective-permute-start | bytes 1572872 | tf_op jit(solution)/shard_map/ppermute | solution.py:394
  322.7 23.5 %all-to-all-start.5 = ((bf16[8,2,64,256]{3,2,1,0:T(8,128)(2,1)}), bf16[8,2,64,256]{3,2,1,0:T(8,128)(2,1)S(1)}, u32[]{:S(2)}, u32[]{:S(2)}) async-start(bf16[8,2,64,256]{3,2,1,0:T(8,128)(2,1)} %maximum_bitcast_fusion), calls=%async_computation.5 | async-start | bytes 1048576 | tf_op jit(solution)/shard_map/all_to_all | solution.py:230
  328.5 22.1 %copy-start.3 = (f32[8,2,64,256]{3,2,1,0:T(8,128)S(1)}, f32[8,2,64,256]{3,2,1,0:T(8,128)}, u32[]{:S(2)}) copy-start(f32[8,2,64,256]{3,2,1,0:T(8,128)} %copy-done.2) | copy-start | bytes 3145732
  346.3 35.9 %collective-permute-start.7 = (bf16[256,1024]{1,0:T(8,128)(2,1)}, bf16[256,1024]{1,0:T(8,128)(2,1)S(1)}, u32[]{:S(2)}, u32[]{:S(2)}) collective-permute-start(bf16[256,1024]{1,0:T(8,128)(2,1)} %fusion.43), channel_id=1, source_target_pairs={{0,16},{16,0},{1,17},{17,1},{2,18},{18,2},{3,19},{19,3},{4,20},{20... | collective-permute-start | bytes 1572872 | tf_op jit(solution)/shard_map/ppermute | solution.py:394
  384.3 36.9 %all-to-all-start.6 = ((bf16[8,2,3,64,256]{4,3,2,1,0:T(8,128)(2,1)}), bf16[8,2,3,64,256]{4,3,2,1,0:T(8,128)(2,1)S(1)}, u32[]{:S(2)}, u32[]{:S(2)}) async-start(bf16[8,2,3,64,256]{4,3,2,1,0:T(8,128)(2,1)} %pair_backward.2), calls=%async_computation.6 | async-start | bytes 3145728 | tf_op jit(solution)/shard_map/all_to_all | solution.py:230
  388.0 141.7 %reduce-scatter.6.cloned.1.call-start = ((), (), s32[]{:S(2)}) async-start(), calls=%async_computation.14 | async-start | bytes 4718592 | tf_op jit(solution)/shard_map/reduce_scatter | solution.py:567
  423.3 12.0 %collective-permute-start.8 = (bf16[512,512]{1,0:T(8,128)(2,1)S(1)}, bf16[512,512]{1,0:T(8,128)(2,1)S(1)}, u32[]{:S(2)}, u32[]{:S(2)}) collective-permute-start(bf16[512,512]{1,0:T(8,128)(2,1)S(1)} %bitcast.336), channel_id=1, source_target_pairs={{0,8},{8,0},{1,9},{9,1},{2,10},{10,2},{3,11},{11,3},{4,12},{12,4},... | collective-permute-start | bytes 1572872 | tf_op jit(solution)/shard_map/ppermute | solution.py:394
  429.3 7.2 copy-start.18
  436.1 124.4 %all-gather.12.cloned.1.call-start = ((), (), s32[]{:S(2)}) async-start(), calls=%async_computation.15 | async-start | bytes 4718592 | tf_op jit(solution)/shard_map/all_gather | solution.py:444
  439.0 22.5 %collective-permute-start.9 = (bf16[512,1024]{1,0:T(8,128)(2,1)S(1)}, bf16[512,1024]{1,0:T(8,128)(2,1)}, u32[]{:S(2)}, u32[]{:S(2)}) collective-permute-start(bf16[512,1024]{1,0:T(8,128)(2,1)S(1)} %convolution_convert_fusion.7), channel_id=1, source_target_pairs={{0,8},{8,0},{1,9},{9,1},{2,10},{10,2},{3,11},{11,3},{4,12},{12,4},... | collective-permute-start | bytes 3145736 | tf_op jit(solution)/shard_map/ppermute | solution.py:394
  446.9 16.3 %copy-start.25 = (bf16[2,256,768]{2,1,0:T(8,128)(2,1)S(1)}, bf16[2,256,768]{2,1,0:T(8,128)(2,1)}, u32[]{:S(2)}) copy-start(bf16[2,256,768]{2,1,0:T(8,128)(2,1)} %copy-done.24) | copy-start | bytes 2359300
  471.5 7.0 copy-start.37
  472.0 6.5 copy-start.47
  472.9 19.1 %all-to-all-start.7 = ((bf16[8,2,64,256]{3,2,1,0:T(8,128)(2,1)}), bf16[8,2,64,256]{3,2,1,0:T(8,128)(2,1)S(1)}, u32[]{:S(2)}, u32[]{:S(2)}) async-start(bf16[8,2,64,256]{3,2,1,0:T(8,128)(2,1)} %maximum_bitcast_fusion.1), calls=%async_computation.8 | async-start | bytes 1048576 | tf_op jit(solution)/shard_map/all_to_all | solution.py:230
  477.4 49.3 %collective-permute-start.11 = (bf16[2,256,1024]{2,1,0:T(8,128)(2,1)}, bf16[2,256,1024]{2,1,0:T(8,128)(2,1)}, u32[]{:S(2)}, u32[]{:S(2)}) collective-permute-start(bf16[2,256,1024]{2,1,0:T(8,128)(2,1)} %pad_maximum_fusion.12), channel_id=1, source_target_pairs={{0,8},{8,0},{1,9},{9,1},{2,10},{10,2},{3,11},{11,3},{4,12},{12,4},... | collective-permute-start | bytes 3145736 | tf_op jit(solution)/shard_map/ppermute | solution.py:394
  479.3 12.7 %copy-start.61 = (bf16[256,768]{1,0:T(8,128)(2,1)S(1)}, bf16[256,768]{1,0:T(8,128)(2,1)}, u32[]{:S(2)}) copy-start(bf16[256,768]{1,0:T(8,128)(2,1)} %convolution_convert_fusion.15) | copy-start | bytes 1179652
  479.3 15.1 %copy-start.5 = (f32[8,2,64,256]{3,2,1,0:T(8,128)S(1)}, f32[8,2,64,256]{3,2,1,0:T(8,128)}, u32[]{:S(2)}) copy-start(f32[8,2,64,256]{3,2,1,0:T(8,128)} %copy-done.4) | copy-start | bytes 3145732
  492.0 34.5 %collective-permute-start.10 = (bf16[256,768]{1,0:T(8,128)(2,1)S(1)}, bf16[256,768]{1,0:T(8,128)(2,1)S(1)}, u32[]{:S(2)}, u32[]{:S(2)}) collective-permute-start(bf16[256,768]{1,0:T(8,128)(2,1)S(1)} %copy-done.61), channel_id=1, source_target_pairs={{0,16},{16,0},{1,17},{17,1},{2,18},{18,2},{3,19},{19,3},{4,20},{20... | collective-permute-start | bytes 1179656 | tf_op jit(solution)/shard_map/ppermute | solution.py:394
  529.8 5.5 copy-start.58
  529.8 30.7 %all-to-all-start.8 = ((bf16[8,2,3,64,256]{4,3,2,1,0:T(8,128)(2,1)}), bf16[8,2,3,64,256]{4,3,2,1,0:T(8,128)(2,1)S(1)}, u32[]{:S(2)}, u32[]{:S(2)}) async-start(bf16[8,2,3,64,256]{4,3,2,1,0:T(8,128)(2,1)} %pair_backward.3), calls=%async_computation.10 | async-start | bytes 3145728 | tf_op jit(solution)/shard_map/all_to_all | solution.py:230
  533.5 89.7 %reduce-scatter.8.cloned.1.call-start = ((), (), s32[]{:S(2)}) async-start(), calls=%async_computation.16 | async-start | bytes 5898240 | tf_op jit(solution)/shard_map/reduce_scatter | solution.py:567
  533.7 25.5 %collective-permute-start.12 = (bf16[2,256,768]{2,1,0:T(8,128)(2,1)S(1)}, bf16[2,256,768]{2,1,0:T(8,128)(2,1)S(1)}, u32[]{:S(2)}, u32[]{:S(2)}) collective-permute-start(bf16[2,256,768]{2,1,0:T(8,128)(2,1)S(1)} %pad_maximum_fusion.16), channel_id=1, source_target_pairs={{0,8},{8,0},{1,9},{9,1},{2,10},{10,2},{3,11},{11,3},{4,12},{12,4},... | collective-permute-start | bytes 2359304 | tf_op jit(solution)/shard_map/ppermute | solution.py:394
  535.3 25.2 %collective-permute-start.13 = (bf16[128,1024]{1,0:T(8,128)(2,1)S(1)}, bf16[128,1024]{1,0:T(8,128)(2,1)S(1)}, u32[]{:S(2)}, u32[]{:S(2)}) collective-permute-start(bf16[128,1024]{1,0:T(8,128)(2,1)S(1)} %dynamic-slice_bitcast_fusion.1), channel_id=1, source_target_pairs={{0,16},{16,0},{1,17},{17,1},{2,18},{18,2},{3,19},{19,3},{4,20},{20... | collective-permute-start | bytes 786440 | tf_op jit(solution)/shard_map/ppermute | solution.py:394
  567.2 92.6 %all-gather.16.cloned.1.call-start = ((), (), s32[]{:S(2)}) async-start(), calls=%async_computation.18 | async-start | bytes 2359296 | tf_op jit(solution)/shard_map/all_gather | solution.py:444
  570.5 136.7 %all-gather.14.cloned.1.call-start = ((), (), s32[]{:S(2)}) async-start(), calls=%async_computation.17 | async-start | bytes 2949120 | tf_op jit(solution)/shard_map/all_gather | solution.py:444
  575.4 13.3 %collective-permute-start.14 = (bf16[256,1024]{1,0:T(8,128)(2,1)S(1)}, bf16[256,1024]{1,0:T(8,128)(2,1)S(1)}, u32[]{:S(2)}, u32[]{:S(2)}) collective-permute-start(bf16[256,1024]{1,0:T(8,128)(2,1)S(1)} %bitcast.371), channel_id=1, source_target_pairs={{0,8},{8,0},{1,9},{9,1},{2,10},{10,2},{3,11},{11,3},{4,12},{12,4},... | collective-permute-start | bytes 1572872 | tf_op jit(solution)/shard_map/ppermute | solution.py:394
  589.7 24.5 %collective-permute-start.15 = (bf16[256,1024]{1,0:T(8,128)(2,1)S(1)}, bf16[256,1024]{1,0:T(8,128)(2,1)S(1)}, u32[]{:S(2)}, u32[]{:S(2)}) collective-permute-start(bf16[256,1024]{1,0:T(8,128)(2,1)S(1)} %fusion.41), channel_id=1, source_target_pairs={{0,16},{16,0},{1,17},{17,1},{2,18},{18,2},{3,19},{19,3},{4,20},{20... | collective-permute-start | bytes 1572872 | tf_op jit(solution)/shard_map/ppermute | solution.py:394
  624.1 17.4 %copy-start.54 = (bf16[2,160,1024]{2,1,0:T(8,128)(2,1)S(1)}, bf16[2,160,1024]{2,1,0:T(8,128)(2,1)}, u32[]{:S(2)}) copy-start(bf16[2,160,1024]{2,1,0:T(8,128)(2,1)} %reduce-scatter.8.cloned.1.call-done) | copy-start | bytes 1966084
  624.2 17.4 %collective-permute-start.19 = (bf16[160,1024]{1,0:T(8,128)(2,1)S(1)}, bf16[160,1024]{1,0:T(8,128)(2,1)S(1)}, u32[]{:S(2)}, u32[]{:S(2)}) collective-permute-start(bf16[160,1024]{1,0:T(8,128)(2,1)S(1)} %dynamic-slice_bitcast_fusion), channel_id=1, source_target_pairs={{0,16},{16,0},{1,17},{17,1},{2,18},{18,2},{3,19},{19,3},{4,20},{20... | collective-permute-start | bytes 983048 | tf_op jit(solution)/shard_map/ppermute | solution.py:394
  658.1 24.5 %collective-permute-start.16 = (bf16[2,256,1024]{2,1,0:T(8,128)(2,1)}, bf16[2,256,1024]{2,1,0:T(8,128)(2,1)}, u32[]{:S(2)}, u32[]{:S(2)}) collective-permute-start(bf16[2,256,1024]{2,1,0:T(8,128)(2,1)} %pad_maximum_fusion.13), channel_id=1, source_target_pairs={{0,8},{8,0},{1,9},{9,1},{2,10},{10,2},{3,11},{11,3},{4,12},{12,4},... | collective-permute-start | bytes 3145736 | tf_op jit(solution)/shard_map/ppermute | solution.py:394
  684.5 5.0 collective-permute-start.17
  700.3 5.6 collective-permute-start.18
  711.9 5.8 copy-start.1
  (53 other events, 113.3 us)
Sparse Core Ops, SparseCore 0:
  28.5 26.8 all-gather.9
  69.5 59.3 all-gather.17
  131.9 81.9 all-gather.19
  282.1 124.8 reduce-scatter.3
  435.4 56.4 reduce-scatter.5
  493.9 37.0 all-gather.11
  567.4 55.7 reduce-scatter.7
  625.6 27.8 all-gather.15
  656.0 30.1 all-gather.13

commit v10 on v9

--- a/solution.py
+++ b/solution.py
@@ -616,38 +616,42 @@
     cross_gain_term = jnp.sum(grad_two * unit_two, axis=0)
     grad_self = grad_cross + normed_back(grad_two * cross_gain_f, unit_two, rate_two)
     grad_self_low = grad_self.astype(LOW)
-    grad_mid = sum_near(
-        mul(grad_pair_t, pair_both, TN)
-    ).astype(LOW)
+    grad_mixed, grad_self_low, grad_mid = tie(
+        to_pairs(self_whole[: 2 * cols], grad_self_low, 1)[:, :, 0],
+        grad_self_low,
+        mul(grad_pair_t, pair_both, TN).astype(LOW),
+    )
+    grad_mid_away = swap(grad_mid, "near")
+    output_terms = by_shard(self_mixed_t, grad_self_low)
+    grads = pair_backward(qkv, qkv, 1, None, exchange_rows(grad_mixed), self_wide, self_log)
+    grads, grad_mid_away, result_four = tie(grads, grad_mid_away, result_four)
+    grad_mid = (grad_mid.astype(WIDE) + grad_mid_away.astype(WIDE)).astype(LOW)
     patch_half = mul(halves(grad_mid)[0], patch_weights, NT).astype(LOW)
+    patch_two = jnp.stack([patch_half, swap(patch_half, "far")])
     patch_terms = jnp.stack([mul(value, patch_in, TN).astype(LOW) for value in both_columns(grad_mid)])
     patch_terms = jnp.pad(patch_terms, ((0, 0), (0, 0), (0, width - patch_width)))
-    grad_mixed, grad_self_low = tie(to_pairs(self_whole[: 2 * cols], grad_self_low, 1)[:, :, 0], grad_self_low)
-    output_terms = by_shard(self_mixed_t, grad_self_low)
-    grad_mixed, patch_half = tie(exchange_rows(grad_mixed), patch_half)
-    patch_two = jnp.stack([patch_half, swap(patch_half, "far")])
     last_terms = jnp.pad(
         jnp.concatenate([output_terms, patch_terms], axis=1), ((0, 0), (3 * cols, 0), (0, 0))
     )
-    grads = pair_backward(qkv, qkv, 1, None, grad_mixed, self_wide, self_log)
-    grads, patch_two, middle_part, result_four, last_terms = tie(
-        grads, patch_two, middle_part, result_four, last_terms
-    )
-    middle_own, middle_away = own_and_away(middle_part)
-    patch_four = jnp.stack([patch_two, swap(patch_two, "near")])
-    grads, patch_four, middle_away, hidden_total = tie(
-        exchange_rows(grads), patch_four, swap(middle_away, "far"), hidden_total
-    )
-    middle_total = join_rows(add_far(middle_own, middle_away))
+    grads, patch_two, last_terms, hidden_total, middle_part = tie(
+        exchange_rows(grads), patch_two, last_terms, hidden_total, middle_part
+    )
     grad_qkv_t = from_pairs(grads)
     last_terms = lax.dynamic_update_slice_in_dim(last_terms, by_shard(grad_qkv_t, normed_one), 0, 1)
     last_part = part_rows(last_terms)
+    middle_own, middle_away = own_and_away(middle_part)
+    middle_total = join_rows(add_far(middle_own, swap(middle_away, "far")))
     grad_one = half_sum_near(mul(grad_qkv_t, qkv_both, TN))
     gain_half, unit_half, rate_half, self_half = (
         halves(value)[0] for value in (gain_one, unit_one, rate_one, grad_self)
     )
     input_half = self_half + normed_back(grad_one * gain_half, unit_half, rate_half)
     input_half = input_half.astype(LOW)
+    input_two = jnp.stack([input_half, swap(input_half, "far")])
+    input_two, patch_two = tie(input_two, patch_two)
+    input_four = jnp.stack([input_two, swap(input_two, "near")])
+    patch_four = jnp.stack([patch_two, swap(patch_two, "near")])
+    last_part, input_four = tie(last_part, input_four)
     onehot_half = halves(onehot)[0].astype(WIDE)
     table_term = jnp.concatenate(
         [
@@ -656,16 +660,10 @@
         ],
         axis=0,
     )
-    input_two = jnp.stack([input_half, swap(input_half, "far")])
-    last_part, input_two = tie(last_part, input_two)
-    input_four = jnp.stack([input_two, swap(input_two, "near")])
-    input_four, table_term = tie(input_four, table_term)
     small = [sum_near(table_term), hidden_gain_term[None], cross_gain_term[None], jnp.zeros((14, width), WIDE)]
     small = jnp.stack(both_columns(jnp.concatenate(small, axis=0).astype(LOW)))
     small = jnp.sum(lax.all_gather(small, "rows", axis=0).astype(WIDE), axis=0).astype(LOW)
-    small_own, small_away = (
-        lax.dynamic_index_in_dim(small, index, 0, keepdims=False) for index in (far, 1 - far)
-    )
+    small_own, small_away = own_and_away(small)
     small = small_own.astype(WIDE) + swap(small_away, "far").astype(WIDE)
     input_grads = over_heads(input_four)
     outputs, patch_grads = over_heads(result_four), over_heads(patch_four)

time: 735 us -> 736 us (level)
  waiting for transfers between devices: 287 us -> 275 us
    ppermute x20, waiting for transfers between devices: 200 us -> 185 us  [swap(): return lax.ppermute(value, axis, [(0, 1), (1, 0)])]
    all_to_all x8, waiting for transfers between devices: 79.9 us -> 89 us  [exchange_rows(): return lax.all_to_all(value, 'rows', 0, 0, tiled=True)]
    reduce_scatter x2, waiting for transfers between devices: 7.85 us -> 0.01 us  [part_rows(): return lax.psum_scatter(both, 'rows', scatter_dimension=1, tiled=True)]
    unnamed x175 -> x185, local copies, waits for them, and re-layouts: 43.6 us -> 42.4 us
  transfers between devices with their start and end apart: 37 -> 37, of which waited for: 22 -> 23; matrix products, arithmetic and copies ran while one was open for 24% -> 25% of each run, Pallas kernels for 12% -> 12%
where the time goes in v10:
time: 736 us; the launch traced here: 726 us
  waiting for transfers between devices  275 us (37%)
  local copies, waits for them, and re-layouts  111 us (15%)
  Pallas kernels  88.9 us (12%)
  other arithmetic  84.4 us (11%)
  starting transfers between devices  64.7 us (9%)
  matrix products  60.2 us (8%)
  blocking collectives  26.2 us (4%)
  between operations  15.7 us (2%)
    ppermute x20, waiting for transfers between devices, swap(): return lax.ppermute(value, axis, [(0, 1), (1, 0)])  185 us
    all_to_all x8, waiting for transfers between devices, exchange_rows(): return lax.all_to_all(value, 'rows', 0, 0, tiled=True)  89 us
    dot_general x31, matrix products, mul(): return lax.dot_general(left, right, dims, preferred_element_type=WIDE)  59.2 us
    pallas_call x2, Pallas kernels, pair_backward(): pl.pallas_call(kernel, grid_spec=pltpu.PrefetchScalarGridSpec(num_scalar_...  55 us
    unnamed x185, local copies, waits for them, and re-layouts  42.4 us
    pallas_call x2, Pallas kernels, pair_forward(): pl.pallas_call(kernel, grid_spec=pltpu.PrefetchScalarGridSpec(num_scalar_...  33.9 us
    all_to_all x8, starting transfers between devices, exchange_rows(): return lax.all_to_all(value, 'rows', 0, 0, tiled=True)  32.1 us
    ppermute x20, starting transfers between devices, swap(): return lax.ppermute(value, axis, [(0, 1), (1, 0)])  31.6 us
  transfers between devices with their start and end apart: 37, of which 23 were waited for; matrix products, arithmetic and copies ran while one was open for 25% of the time, Pallas kernels for 12%

profile of v10, /device:TPU:0, one launch (start us, length us, event | category | flops | bytes accessed | tf_op | source)
XLA Modules:
  0.0 725.9 jit_solution(7275638182740062178)
XLA Ops:
  14.4 4.0 collective-permute-start
  19.9 7.8 %collective-permute-done = bf16[96,1024]{1,0:T(8,128)(2,1)S(1)} collective-permute-done((bf16[96,1024]{1,0:T(8,128)(2,1)}, bf16[96,1024]{1,0:T(8,128)(2,1)S(1)}, u32[]{:S(2)}, u32[]{:S(2)}) %collective-permute-start) | collective-permute-done | bytes 196640 | tf_op jit(solution)/shard_map/ppermute | solution.py:394
  40.9 17.1 %collective-permute-done.1 = bf16[160,1024]{1,0:T(8,128)(2,1)} collective-permute-done((bf16[160,1024]{1,0:T(8,128)(2,1)}, bf16[160,1024]{1,0:T(8,128)(2,1)}, u32[]{:S(2)}, u32[]{:S(2)}) %collective-permute-start.1) | collective-permute-done | bytes 327712 | tf_op jit(solution)/shard_map/ppermute | solution.py:394
  59.9 8.5 %collective-permute-done.2 = bf16[2,96,1024]{2,1,0:T(8,128)(2,1)S(1)} collective-permute-done((bf16[2,96,1024]{2,1,0:T(8,128)(2,1)S(1)}, bf16[2,96,1024]{2,1,0:T(8,128)(2,1)S(1)}, u32[]{:S(2)}, u32[]{:S(2)}) %collective-permute-start.2) | collective-permute-done | bytes 393248 | tf_op jit(solution)/shard_map/ppermute | solution.py:394
  75.5 3.3 convolution_convert_fusion.3
  78.8 2.9 convolution_convert_fusion.4
  83.0 4.3 all-to-all-start
  89.2 23.8 %all-to-all-done.q_ref.k_ref.v_ref = bf16[8,2,3,64,256]{4,3,2,1,0:T(8,128)(2,1)} async-done(((bf16[8,2,3,64,256]{4,3,2,1,0:T(8,128)(2,1)}), bf16[8,2,3,64,256]{4,3,2,1,0:T(8,128)(2,1)}, u32[]{:S(2)}, u32[]{:S(2)}) %all-to-all-start) | async-done | bytes 1572896 | tf_op jit(solution)/shard_map/all_to_all | solution.py:230
  122.5 19.0 %pair_forward.2 = (bf16[8,2,64,256]{3,2,1,0:T(8,128)(2,1)}, f32[8,2,64,256]{3,2,1,0:T(8,128)S(1)}, f32[8,2,1,256]{3,2,1,0:T(1,128)S(1)}) custom-call(s32[2]{0:T(128)S(1)} %broadcast_13_len_ref.2.len_ref, bf16[8,2,3,64,256]{4,3,2,1,0:T(8,128)(2,1)} %all-to-all-done.q_ref.k_ref.v_ref, bf16[8,2,3,64,256]{4,3,2,1,0:T(8,128)(2,1)} %all-to-all-done.q_ref.k_ref.v_ref, ...), custom_call_target="tpu_custom_call" | custom-call | flops 20132659200 | bytes 8388608 | tf_op jit(solution)/shard_map/pair_forward/pallas_call | solution.py:282
  142.4 4.0 all-to-all-start.1
  149.3 2.9 copy-done.24
  152.2 3.3 slice.169
  158.8 4.2 all-to-all-start.2
  163.2 3.6 fusion.75
  166.9 6.2 fusion.76
  173.3 11.7 %collective-permute-done.3 = bf16[512,512]{1,0:T(8,128)(2,1)S(1)} collective-permute-done((bf16[512,512]{1,0:T(8,128)(2,1)}, bf16[512,512]{1,0:T(8,128)(2,1)S(1)}, u32[]{:S(2)}, u32[]{:S(2)}) %collective-permute-start.3) | collective-permute-done | bytes 524320 | tf_op jit(solution)/shard_map/ppermute | solution.py:394
  189.6 4.1 all-to-all-start.3
  193.9 9.6 %all-to-all-done.3.q_ref = bf16[8,2,1,64,256]{4,3,2,1,0:T(8,128)(2,1)} async-done(((bf16[8,2,1,64,256]{4,3,2,1,0:T(8,128)(2,1)}), bf16[8,2,1,64,256]{4,3,2,1,0:T(8,128)(2,1)}, u32[]{:S(2)}, u32[]{:S(2)}) %all-to-all-start.3) | async-done | bytes 524320 | tf_op jit(solution)/shard_map/all_to_all | solution.py:230
  203.5 15.0 %pair_forward.3 = (bf16[8,2,64,256]{3,2,1,0:T(8,128)(2,1)S(1)}, f32[8,2,64,256]{3,2,1,0:T(8,128)S(1)}, f32[8,2,1,256]{3,2,1,0:T(1,128)S(1)}) custom-call(s32[2]{0:T(128)S(1)} %dynamic_slice.117.len_ref, bf16[8,2,1,64,256]{4,3,2,1,0:T(8,128)(2,1)} %all-to-all-done.3.q_ref, bf16[8,2,2,64,256]{4,3,2,1,0:T(8,128)(2,1)S(1)} %all-to-all-done.2.k_ref.v_ref, ...), custom_call_target="tpu_custom_call" | custom-call | flops 14092861440 | bytes 8388608 | tf_op jit(solution)/shard_map/pair_forward/pallas_call | solution.py:282
  218.5 12.3 %all_to_all.45 = bf16[8,2,64,256]{3,2,1,0:T(8,128)(2,1)S(1)} all-to-all(bf16[8,2,64,256]{3,2,1,0:T(8,128)(2,1)S(1)} %get-tuple-element.72), channel_id=1, replica_groups=mesh['far'=2,'near'=2,'rows'=8] {'rows'}, dimensions={0} | all-to-all | bytes 1048576 | tf_op jit(solution)/shard_map/all_to_all | solution.py:230
  233.3 11.2 %collective-permute-done.4 = bf16[512,512]{1,0:T(8,128)(2,1)S(1)} collective-permute-done((bf16[512,512]{1,0:T(8,128)(2,1)S(1)}, bf16[512,512]{1,0:T(8,128)(2,1)S(1)}, u32[]{:S(2)}, u32[]{:S(2)}) %collective-permute-start.4) | collective-permute-done | bytes 524320 | tf_op jit(solution)/shard_map/ppermute | solution.py:394
  247.6 2.8 slice.177
  256.7 5.1 multiply_convert_fusion
  261.8 3.5 fusion.22
  265.3 4.8 convolution_convert_fusion.1
  270.1 4.4 convolution_convert_fusion.2
  274.5 7.8 %pad_maximum_fusion = bf16[2,2048,1024]{2,1,0:T(8,128)(2,1)} fusion(bf16[2,1024,1024]{2,1,0:T(8,128)(2,1)} %bitcast.325, bf16[2,1024,1024]{2,1,0:T(8,128)(2,1)} %bitcast.326), kind=kLoop, calls=%fused_computation.3 | loop fusion | flops 16777216 | bytes 16777216 | tf_op jit(solution)/shard_map/concatenate | solution.py:578
  284.8 4.6 fusion.81
  290.4 24.7 %collective-permute-done.5 = bf16[512,1024]{1,0:T(8,128)(2,1)} collective-permute-done((bf16[512,1024]{1,0:T(8,128)(2,1)}, bf16[512,1024]{1,0:T(8,128)(2,1)}, u32[]{:S(2)}, u32[]{:S(2)}) %collective-permute-start.5) | collective-permute-done | bytes 1048608 | tf_op jit(solution)/shard_map/ppermute | solution.py:394
  322.6 3.9 all-to-all-start.5
  328.6 7.2 collective-permute-done.6
  337.9 9.1 %all-to-all-done.5.g_ref = bf16[8,2,64,256]{3,2,1,0:T(8,128)(2,1)S(1)} async-done(((bf16[8,2,64,256]{3,2,1,0:T(8,128)(2,1)}), bf16[8,2,64,256]{3,2,1,0:T(8,128)(2,1)S(1)}, u32[]{:S(2)}, u32[]{:S(2)}) %all-to-all-start.5) | async-done | bytes 524320 | tf_op jit(solution)/shard_map/all_to_all | solution.py:230
  347.0 3.8 collective-permute-start.7
  350.8 22.8 %pair_backward.2 = bf16[8,2,3,64,256]{4,3,2,1,0:T(8,128)(2,1)} custom-call(s32[2]{0:T(128)S(1)} %dynamic_slice.117.len_ref, bf16[8,2,1,64,256]{4,3,2,1,0:T(8,128)(2,1)} %all-to-all-done.3.q_ref, bf16[8,2,2,64,256]{4,3,2,1,0:T(8,128)(2,1)S(1)} %all-to-all-done.2.k_ref.v_ref, bf16[8,2,2,64,256]{4,3,2,1,0:T(8,128)(2,1)S(1)} %all-to-all-done.2.k_ref.v_ref, ...), custom_call_target="tpu_custom_call" | custom-call | flops 20132659200 | bytes 8388608 | tf_op jit(solution)/shard_map/pair_backward/pallas_call | solution.py:364
  373.6 8.6 %collective-permute-done.7 = bf16[256,1024]{1,0:T(8,128)(2,1)S(1)} collective-permute-done((bf16[256,1024]{1,0:T(8,128)(2,1)}, bf16[256,1024]{1,0:T(8,128)(2,1)S(1)}, u32[]{:S(2)}, u32[]{:S(2)}) %collective-permute-start.7) | collective-permute-done | bytes 524320 | tf_op jit(solution)/shard_map/ppermute | solution.py:394
  384.3 3.7 all-to-all-start.6
  389.8 31.2 %all-to-all-done.6 = bf16[8,2,3,64,256]{4,3,2,1,0:T(8,128)(2,1)S(1)} async-done(((bf16[8,2,3,64,256]{4,3,2,1,0:T(8,128)(2,1)}), bf16[8,2,3,64,256]{4,3,2,1,0:T(8,128)(2,1)S(1)}, u32[]{:S(2)}, u32[]{:S(2)}) %all-to-all-start.6) | async-done | bytes 1572896 | tf_op jit(solution)/shard_map/all_to_all | solution.py:230
  429.1 6.1 collective-permute-done.8
  442.5 2.8 multiply_reduce_fusion
  449.9 3.6 all-to-all-start.7
  455.6 2.9 convolution_convert_fusion.8
  458.5 7.4 %all-to-all-done.7.g_ref = bf16[8,2,64,256]{3,2,1,0:T(8,128)(2,1)S(1)} async-done(((bf16[8,2,64,256]{3,2,1,0:T(8,128)(2,1)}), bf16[8,2,64,256]{3,2,1,0:T(8,128)(2,1)S(1)}, u32[]{:S(2)}, u32[]{:S(2)}) %all-to-all-start.7) | async-done | bytes 524320 | tf_op jit(solution)/shard_map/all_to_all | solution.py:230
  466.0 32.1 %pair_backward.3 = bf16[8,2,3,64,256]{4,3,2,1,0:T(8,128)(2,1)} custom-call(s32[2]{0:T(128)S(1)} %broadcast_13_len_ref.2.len_ref, bf16[8,2,3,64,256]{4,3,2,1,0:T(8,128)(2,1)} %all-to-all-done.q_ref.k_ref.v_ref, bf16[8,2,3,64,256]{4,3,2,1,0:T(8,128)(2,1)} %all-to-all-done.q_ref.k_ref.v_ref, bf16[8,2,3,64,256]{4,3,2,1,0:T(8,128)(2,1)} %all-to-all-done.q_ref.k_ref.v_ref, ...), custom_call_target="tpu_custom_call" | custom-call | flops 30198988800 | bytes 8388608 | tf_op jit(solution)/shard_map/pair_backward/pallas_call | solution.py:364
  498.1 3.5 collective-permute-done.10
  504.3 4.3 all-to-all-start.8
  514.5 6.1 fusion.2
  520.6 11.5 %collective-permute-done.11 = bf16[256,768]{1,0:T(8,128)(2,1)S(1)} collective-permute-done((bf16[256,768]{1,0:T(8,128)(2,1)S(1)}, bf16[256,768]{1,0:T(8,128)(2,1)S(1)}, u32[]{:S(2)}, u32[]{:S(2)}) %collective-permute-start.11) | collective-permute-done | bytes 393248 | tf_op jit(solution)/shard_map/ppermute | solution.py:394
  533.0 7.8 %all-to-all-done.8 = bf16[8,2,3,64,256]{4,3,2,1,0:T(8,128)(2,1)} async-done(((bf16[8,2,3,64,256]{4,3,2,1,0:T(8,128)(2,1)}), bf16[8,2,3,64,256]{4,3,2,1,0:T(8,128)(2,1)}, u32[]{:S(2)}, u32[]{:S(2)}) %all-to-all-start.8) | async-done | bytes 1572896 | tf_op jit(solution)/shard_map/all_to_all | solution.py:230
  540.8 3.0 copy.115
  554.1 4.7 fusion.10
  565.7 10.6 %collective-permute-done.19 = bf16[128,1024]{1,0:T(8,128)(2,1)S(1)} collective-permute-done((bf16[128,1024]{1,0:T(8,128)(2,1)S(1)}, bf16[128,1024]{1,0:T(8,128)(2,1)S(1)}, u32[]{:S(2)}, u32[]{:S(2)}) %collective-permute-start.19) | collective-permute-done | bytes 262176 | tf_op jit(solution)/shard_map/ppermute | solution.py:394
  582.5 3.5 collective-permute-start.13
  586.1 20.4 %collective-permute-done.13 = bf16[256,1024]{1,0:T(8,128)(2,1)S(1)} collective-permute-done((bf16[256,1024]{1,0:T(8,128)(2,1)S(1)}, bf16[256,1024]{1,0:T(8,128)(2,1)S(1)}, u32[]{:S(2)}, u32[]{:S(2)}) %collective-permute-start.13) | collective-permute-done | bytes 524320 | tf_op jit(solution)/shard_map/ppermute | solution.py:394
  607.4 3.1 copy.114
  610.5 20.0 %collective-permute-done.14 = bf16[2,256,1024]{2,1,0:T(8,128)(2,1)S(1)} collective-permute-done((bf16[2,256,1024]{2,1,0:T(8,128)(2,1)S(1)}, bf16[2,256,1024]{2,1,0:T(8,128)(2,1)S(1)}, u32[]{:S(2)}, u32[]{:S(2)}) %collective-permute-start.14) | collective-permute-done | bytes 1048608 | tf_op jit(solution)/shard_map/ppermute | solution.py:394
  633.0 3.4 collective-permute-start.18
  636.5 4.6 reverse_select_fusion.3
  641.6 9.4 %collective-permute-done.18 = bf16[160,1024]{1,0:T(8,128)(2,1)S(1)} collective-permute-done((bf16[160,1024]{1,0:T(8,128)(2,1)S(1)}, bf16[160,1024]{1,0:T(8,128)(2,1)S(1)}, u32[]{:S(2)}, u32[]{:S(2)}) %collective-permute-start.18) | collective-permute-done | bytes 327712 | tf_op jit(solution)/shard_map/ppermute | solution.py:394
  657.6 14.0 %all-gather.2 = bf16[16,80,256]{2,1,0:T(8,128)(2,1)S(1)} all-gather(bf16[2,80,256]{2,1,0:T(8,128)(2,1)S(1)} %pad_maximum_fusion.21), channel_id=4, replica_groups=mesh['far'=2,'near'=2,'rows'=8] {'rows'}, dimensions={0}, use_global_device_ids=true | all-gather | bytes 737280 | tf_op jit(solution)/shard_map/all_gather | solution.py:665
  675.3 6.7 slice_convert_fusion
  682.0 5.4 copy.127
  688.6 4.9 collective-permute-done.15
  701.8 3.0 copy.125
  713.1 3.7 copy.123
  (391 shorter events, 174.9 us)
Async XLA Ops:
  7.2 224.8 %copy-start = (bf16[4,256,1024]{2,1,0:T(8,128)(2,1)S(1)}, bf16[4,256,1024]{2,1,0:T(8,128)(2,1)}, u32[]{:S(2)}) copy-start(bf16[4,256,1024]{2,1,0:T(8,128)(2,1)} %param.31) | copy-start | bytes 6291460
  7.2 65.6 %all-gather.10.cloned.1.call-start = ((), (), s32[]{:S(2)}) async-start(), calls=%async_computation.12 | async-start | bytes 1769472 | tf_op jit(solution)/shard_map/all_gather | solution.py:444
  10.0 8.4 %copy-start.72 = (s32[4,256]{1,0:T(4,128)S(1)}, s32[4,256]{1,0:T(4,128)}, u32[]{:S(2)}) copy-start(s32[4,256]{1,0:T(4,128)} %param.17) | copy-start | bytes 12292
  12.7 18.1 %copy-start.68 = (bf16[32,2,1024]{2,1,0:T(2,128)(2,1)S(1)}, bf16[32,2,1024]{2,1,0:T(2,128)(2,1)}, u32[]{:S(2)}) copy-start(bf16[32,2,1024]{2,1,0:T(2,128)(2,1)} %param.20) | copy-start | bytes 393220
  12.7 20.0 %copy-start.53 = (bf16[2,1024,256]{2,1,0:T(8,128)(2,1)S(1)}, bf16[2,1024,256]{2,1,0:T(8,128)(2,1)}, u32[]{:S(2)}) copy-start(bf16[2,1024,256]{2,1,0:T(8,128)(2,1)} %param.25) | copy-start | bytes 3145732
  14.4 13.4 %collective-permute-start = (bf16[96,1024]{1,0:T(8,128)(2,1)}, bf16[96,1024]{1,0:T(8,128)(2,1)S(1)}, u32[]{:S(2)}, u32[]{:S(2)}) collective-permute-start(bf16[96,1024]{1,0:T(8,128)(2,1)} %constant_dynamic-slice_fusion.20), channel_id=1, source_target_pairs={{0,16},{16,0},{1,17},{17,1},{2,18},{18,2},{3,19},{19,3},{4,20},{20... | collective-permute-start | bytes 589832 | tf_op jit(solution)/shard_map/ppermute | solution.py:394
  19.9 11.5 %copy-start.69 = (f32[2,256]{1,0:T(2,128)}, f32[2,256]{1,0:T(2,128)S(1)}, u32[]{:S(2)}) copy-start(f32[2,256]{1,0:T(2,128)S(1)} %get-tuple-element.203) | copy-start | bytes 6148
  28.4 118.0 %all-gather.18.cloned.1.call-start = ((), (), s32[]{:S(2)}) async-start(), calls=%async_computation.19 | async-start | bytes 8257536 | tf_op jit(solution)/shard_map/all_gather | solution.py:522
  40.8 17.1 %collective-permute-start.1 = (bf16[160,1024]{1,0:T(8,128)(2,1)}, bf16[160,1024]{1,0:T(8,128)(2,1)}, u32[]{:S(2)}, u32[]{:S(2)}) collective-permute-start(bf16[160,1024]{1,0:T(8,128)(2,1)} %pad_maximum_fusion.19), channel_id=1, source_target_pairs={{0,16},{16,0},{1,17},{17,1},{2,18},{18,2},{3,19},{19,3},{4,20},{20... | collective-permute-start | bytes 983048 | tf_op jit(solution)/shard_map/ppermute | solution.py:394
  58.9 9.4 %collective-permute-start.2 = (bf16[2,96,1024]{2,1,0:T(8,128)(2,1)S(1)}, bf16[2,96,1024]{2,1,0:T(8,128)(2,1)S(1)}, u32[]{:S(2)}, u32[]{:S(2)}) collective-permute-start(bf16[2,96,1024]{2,1,0:T(8,128)(2,1)S(1)} %fusion.59), channel_id=1, source_target_pairs={{0,8},{8,0},{1,9},{9,1},{2,10},{10,2},{3,11},{11,3},{4,12},{12,4},... | collective-permute-start | bytes 1179656 | tf_op jit(solution)/shard_map/ppermute | solution.py:394
  83.0 29.9 %all-to-all-start = ((bf16[8,2,3,64,256]{4,3,2,1,0:T(8,128)(2,1)}), bf16[8,2,3,64,256]{4,3,2,1,0:T(8,128)(2,1)}, u32[]{:S(2)}, u32[]{:S(2)}) async-start(bf16[8,2,3,64,256]{4,3,2,1,0:T(8,128)(2,1)} %pad_maximum_fusion.7), calls=%async_computation | async-start | bytes 3145728 | tf_op jit(solution)/shard_map/all_to_all | solution.py:230
  87.3 27.4 %copy-start.74 = (bf16[1024]{0:T(1024)(128)(2,1)S(1)}, bf16[1024]{0:T(1024)(128)(2,1)}, u32[]{:S(2)}) copy-start(bf16[1024]{0:T(1024)(128)(2,1)} %param.23) | copy-start | bytes 6148
  87.3 160.2 %all-gather.20.cloned.1.call-start = ((), (), s32[]{:S(2)}) async-start(), calls=%async_computation.20 | async-start | bytes 8912896 | tf_op jit(solution)/shard_map/all_gather | solution.py:536
  142.4 14.9 %all-to-all-start.1 = ((bf16[8,2,64,256]{3,2,1,0:T(8,128)(2,1)}), bf16[8,2,64,256]{3,2,1,0:T(8,128)(2,1)S(1)}, u32[]{:S(2)}, u32[]{:S(2)}) async-start(bf16[8,2,64,256]{3,2,1,0:T(8,128)(2,1)} %get-tuple-element.67), calls=%async_computation.1 | async-start | bytes 1048576 | tf_op jit(solution)/shard_map/all_to_all | solution.py:230
  158.8 30.8 %all-to-all-start.2 = ((bf16[8,2,2,64,256]{4,3,2,1,0:T(8,128)(2,1)}), bf16[8,2,2,64,256]{4,3,2,1,0:T(8,128)(2,1)S(1)}, u32[]{:S(2)}, u32[]{:S(2)}) async-start(bf16[8,2,2,64,256]{4,3,2,1,0:T(8,128)(2,1)} %pad_maximum_fusion.11), calls=%async_computation.2 | async-start | bytes 2097152 | tf_op jit(solution)/shard_map/all_to_all | solution.py:230
  162.9 22.0 %collective-permute-start.3 = (bf16[512,512]{1,0:T(8,128)(2,1)}, bf16[512,512]{1,0:T(8,128)(2,1)S(1)}, u32[]{:S(2)}, u32[]{:S(2)}) collective-permute-start(bf16[512,512]{1,0:T(8,128)(2,1)} %bitcast.332), channel_id=1, source_target_pairs={{0,8},{8,0},{1,9},{9,1},{2,10},{10,2},{3,11},{11,3},{4,12},{12,4},... | collective-permute-start | bytes 1572872 | tf_op jit(solution)/shard_map/ppermute | solution.py:394
  173.1 11.9 %copy-start.34 = (bf16[2,256,1024]{2,1,0:T(8,128)(2,1)S(1)}, bf16[2,256,1024]{2,1,0:T(8,128)(2,1)}, u32[]{:S(2)}) copy-start(bf16[2,256,1024]{2,1,0:T(8,128)(2,1)} %get-tuple-element.195) | copy-start | bytes 3145732
  173.1 11.9 %copy-start.41 = (bf16[64,8,2,256]{3,1,2,0:T(8,128)(2,1)S(1)}, bf16[64,8,2,256]{3,1,2,0:T(8,128)(2,1)}, u32[]{:S(2)}) copy-start(bf16[64,8,2,256]{3,1,2,0:T(8,128)(2,1)} %copy.137) | copy-start | bytes 1572868
  189.6 13.9 %all-to-all-start.3 = ((bf16[8,2,1,64,256]{4,3,2,1,0:T(8,128)(2,1)}), bf16[8,2,1,64,256]{4,3,2,1,0:T(8,128)(2,1)}, u32[]{:S(2)}, u32[]{:S(2)}) async-start(bf16[8,2,1,64,256]{4,3,2,1,0:T(8,128)(2,1)} %pad_maximum_fusion.17), calls=%async_computation.3 | async-start | bytes 1048576 | tf_op jit(solution)/shard_map/all_to_all | solution.py:230
  193.8 248.7 %reduce-scatter.4.cloned.1.call-start = ((), (), s32[]{:S(2)}) async-start(), calls=%async_computation.13 | async-start | bytes 8912896 | tf_op jit(solution)/shard_map/reduce_scatter | solution.py:585
  218.5 14.6 %copy-start.2 = (f32[8,2,64,256]{3,2,1,0:T(8,128)}, f32[8,2,64,256]{3,2,1,0:T(8,128)S(1)}, u32[]{:S(2)}) copy-start(f32[8,2,64,256]{3,2,1,0:T(8,128)S(1)} %get-tuple-element.80.wide_ref) | copy-start | bytes 3145732
  218.5 13.5 %copy-start.75 = (bf16[1024]{0:T(1024)(128)(2,1)S(1)}, bf16[1024]{0:T(1024)(128)(2,1)}, u32[]{:S(2)}) copy-start(bf16[1024]{0:T(1024)(128)(2,1)} %param.28) | copy-start | bytes 6148
  231.4 13.1 %copy-start.65 = (bf16[64,8,2,256]{3,1,2,0:T(8,128)(2,1)}, bf16[64,8,2,256]{3,1,2,0:T(8,128)(2,1)S(1)}, u32[]{:S(2)}) copy-start(bf16[64,8,2,256]{3,1,2,0:T(8,128)(2,1)S(1)} %copy.138) | copy-start | bytes 1572868
  231.4 13.1 %collective-permute-start.4 = (bf16[512,512]{1,0:T(8,128)(2,1)S(1)}, bf16[512,512]{1,0:T(8,128)(2,1)S(1)}, u32[]{:S(2)}, u32[]{:S(2)}) collective-permute-start(bf16[512,512]{1,0:T(8,128)(2,1)S(1)} %bitcast.368), channel_id=1, source_target_pairs={{0,8},{8,0},{1,9},{9,1},{2,10},{10,2},{3,11},{11,3},{4,12},{12,4},... | collective-permute-start | bytes 1572872 | tf_op jit(solution)/shard_map/ppermute | solution.py:394
  233.1 11.5 %copy-start.7 = (f32[512,1024]{1,0:T(8,128)S(1)}, f32[512,1024]{1,0:T(8,128)}, u32[]{:S(2)}) copy-start(f32[512,1024]{1,0:T(8,128)} %copy-done.6) | copy-start | bytes 6291460
  261.8 8.2 %copy-start.79 = (bf16[512,2048]{1,0:T(8,128)(2,1)}, bf16[512,2048]{1,0:T(8,128)(2,1)S(1)}, u32[]{:S(2)}) copy-start(bf16[512,2048]{1,0:T(8,128)(2,1)S(1)} %get-tuple-element.75) | copy-start | bytes 6291460
  282.3 32.8 %collective-permute-start.5 = (bf16[512,1024]{1,0:T(8,128)(2,1)}, bf16[512,1024]{1,0:T(8,128)(2,1)}, u32[]{:S(2)}, u32[]{:S(2)}) collective-permute-start(bf16[512,1024]{1,0:T(8,128)(2,1)} %fusion.22), channel_id=1, source_target_pairs={{0,8},{8,0},{1,9},{9,1},{2,10},{10,2},{3,11},{11,3},{4,12},{12,4},... | collective-permute-start | bytes 3145736 | tf_op jit(solution)/shard_map/ppermute | solution.py:394
  284.8 30.4 %copy-start.55 = (bf16[512,1024]{1,0:T(8,128)(2,1)S(1)}, bf16[512,1024]{1,0:T(8,128)(2,1)}, u32[]{:S(2)}) copy-start(bf16[512,1024]{1,0:T(8,128)(2,1)} %fusion.22) | copy-start | bytes 3145732
  289.4 27.3 %copy-start.45 = (f32[2,2,128,1024]{3,2,1,0:T(8,128)}, f32[2,2,128,1024]{3,2,1,0:T(8,128)S(1)}, u32[]{:S(2)}) copy-start(f32[2,2,128,1024]{3,2,1,0:T(8,128)S(1)} %fusion.81) | copy-start | bytes 6291460
  316.8 19.0 %collective-permute-start.6 = (bf16[256,1024]{1,0:T(8,128)(2,1)}, bf16[256,1024]{1,0:T(8,128)(2,1)}, u32[]{:S(2)}, u32[]{:S(2)}) collective-permute-start(bf16[256,1024]{1,0:T(8,128)(2,1)} %bitcast.39), channel_id=1, source_target_pairs={{0,8},{8,0},{1,9},{9,1},{2,10},{10,2},{3,11},{11,3},{4,12},{12,4},... | collective-permute-start | bytes 1572872 | tf_op jit(solution)/shard_map/ppermute | solution.py:394
  322.6 24.5 %all-to-all-start.5 = ((bf16[8,2,64,256]{3,2,1,0:T(8,128)(2,1)}), bf16[8,2,64,256]{3,2,1,0:T(8,128)(2,1)S(1)}, u32[]{:S(2)}, u32[]{:S(2)}) async-start(bf16[8,2,64,256]{3,2,1,0:T(8,128)(2,1)} %maximum_bitcast_fusion), calls=%async_computation.5 | async-start | bytes 1048576 | tf_op jit(solution)/shard_map/all_to_all | solution.py:230
  328.5 22.3 %copy-start.3 = (f32[8,2,64,256]{3,2,1,0:T(8,128)S(1)}, f32[8,2,64,256]{3,2,1,0:T(8,128)}, u32[]{:S(2)}) copy-start(f32[8,2,64,256]{3,2,1,0:T(8,128)} %copy-done.2) | copy-start | bytes 3145732
  347.0 35.2 %collective-permute-start.7 = (bf16[256,1024]{1,0:T(8,128)(2,1)}, bf16[256,1024]{1,0:T(8,128)(2,1)S(1)}, u32[]{:S(2)}, u32[]{:S(2)}) collective-permute-start(bf16[256,1024]{1,0:T(8,128)(2,1)} %fusion.43), channel_id=1, source_target_pairs={{0,16},{16,0},{1,17},{17,1},{2,18},{18,2},{3,19},{19,3},{4,20},{20... | collective-permute-start | bytes 1572872 | tf_op jit(solution)/shard_map/ppermute | solution.py:394
  384.3 36.7 %all-to-all-start.6 = ((bf16[8,2,3,64,256]{4,3,2,1,0:T(8,128)(2,1)}), bf16[8,2,3,64,256]{4,3,2,1,0:T(8,128)(2,1)S(1)}, u32[]{:S(2)}, u32[]{:S(2)}) async-start(bf16[8,2,3,64,256]{4,3,2,1,0:T(8,128)(2,1)} %pair_backward.2), calls=%async_computation.6 | async-start | bytes 3145728 | tf_op jit(solution)/shard_map/all_to_all | solution.py:230
  388.1 145.0 %reduce-scatter.6.cloned.1.call-start = ((), (), s32[]{:S(2)}) async-start(), calls=%async_computation.15 | async-start | bytes 4718592 | tf_op jit(solution)/shard_map/reduce_scatter | solution.py:567
  423.2 12.0 %collective-permute-start.8 = (bf16[512,512]{1,0:T(8,128)(2,1)S(1)}, bf16[512,512]{1,0:T(8,128)(2,1)S(1)}, u32[]{:S(2)}, u32[]{:S(2)}) collective-permute-start(bf16[512,512]{1,0:T(8,128)(2,1)S(1)} %bitcast.335), channel_id=1, source_target_pairs={{0,8},{8,0},{1,9},{9,1},{2,10},{10,2},{3,11},{11,3},{4,12},{12,4},... | collective-permute-start | bytes 1572872 | tf_op jit(solution)/shard_map/ppermute | solution.py:394
  429.1 7.1 copy-start.22
  436.0 104.8 %all-gather.12.cloned.1.call-start = ((), (), s32[]{:S(2)}) async-start(), calls=%async_computation.14 | async-start | bytes 4718592 | tf_op jit(solution)/shard_map/all_gather | solution.py:444
  448.5 7.1 copy-start.42
  449.9 16.1 %copy-start.5 = (f32[8,2,64,256]{3,2,1,0:T(8,128)S(1)}, f32[8,2,64,256]{3,2,1,0:T(8,128)}, u32[]{:S(2)}) copy-start(f32[8,2,64,256]{3,2,1,0:T(8,128)} %copy-done.4) | copy-start | bytes 3145732
  449.9 16.1 %all-to-all-start.7 = ((bf16[8,2,64,256]{3,2,1,0:T(8,128)(2,1)}), bf16[8,2,64,256]{3,2,1,0:T(8,128)(2,1)S(1)}, u32[]{:S(2)}, u32[]{:S(2)}) async-start(bf16[8,2,64,256]{3,2,1,0:T(8,128)(2,1)} %maximum_bitcast_fusion.1), calls=%async_computation.8 | async-start | bytes 1048576 | tf_op jit(solution)/shard_map/all_to_all | solution.py:230
  453.5 50.8 %collective-permute-start.9 = (bf16[512,1024]{1,0:T(8,128)(2,1)S(1)}, bf16[512,1024]{1,0:T(8,128)(2,1)}, u32[]{:S(2)}, u32[]{:S(2)}) collective-permute-start(bf16[512,1024]{1,0:T(8,128)(2,1)S(1)} %convolution_convert_fusion.7), channel_id=1, source_target_pairs={{0,8},{8,0},{1,9},{9,1},{2,10},{10,2},{3,11},{11,3},{4,12},{12,4},... | collective-permute-start | bytes 3145736 | tf_op jit(solution)/shard_map/ppermute | solution.py:394
  455.1 46.4 %collective-permute-start.10 = (bf16[2,256,1024]{2,1,0:T(8,128)(2,1)}, bf16[2,256,1024]{2,1,0:T(8,128)(2,1)}, u32[]{:S(2)}, u32[]{:S(2)}) collective-permute-start(bf16[2,256,1024]{2,1,0:T(8,128)(2,1)} %pad_maximum_fusion.12), channel_id=1, source_target_pairs={{0,8},{8,0},{1,9},{9,1},{2,10},{10,2},{3,11},{11,3},{4,12},{12,4},... | collective-permute-start | bytes 3145736 | tf_op jit(solution)/shard_map/ppermute | solution.py:394
  466.0 35.6 %copy-start.36 = (bf16[2,256,1024]{2,1,0:T(8,128)(2,1)S(1)}, bf16[2,256,1024]{2,1,0:T(8,128)(2,1)}, u32[]{:S(2)}) copy-start(bf16[2,256,1024]{2,1,0:T(8,128)(2,1)} %pad_maximum_fusion.12) | copy-start | bytes 3145732
  504.3 36.5 %all-to-all-start.8 = ((bf16[8,2,3,64,256]{4,3,2,1,0:T(8,128)(2,1)}), bf16[8,2,3,64,256]{4,3,2,1,0:T(8,128)(2,1)}, u32[]{:S(2)}, u32[]{:S(2)}) async-start(bf16[8,2,3,64,256]{4,3,2,1,0:T(8,128)(2,1)} %pair_backward.3), calls=%async_computation.9 | async-start | bytes 3145728 | tf_op jit(solution)/shard_map/all_to_all | solution.py:230
  508.6 123.4 %reduce-scatter.8.cloned.1.call-start = ((), (), s32[]{:S(2)}) async-start(), calls=%async_computation.16 | async-start | bytes 5898240 | tf_op jit(solution)/shard_map/reduce_scatter | solution.py:567
  511.3 20.7 %collective-permute-start.11 = (bf16[256,768]{1,0:T(8,128)(2,1)S(1)}, bf16[256,768]{1,0:T(8,128)(2,1)S(1)}, u32[]{:S(2)}, u32[]{:S(2)}) collective-permute-start(bf16[256,768]{1,0:T(8,128)(2,1)S(1)} %convolution_convert_fusion.15), channel_id=1, source_target_pairs={{0,16},{16,0},{1,17},{17,1},{2,18},{18,2},{3,19},{19,3},{4,20},{20... | collective-permute-start | bytes 1179656 | tf_op jit(solution)/shard_map/ppermute | solution.py:394
  549.0 147.3 %all-gather.16.cloned.1.call-start = ((), (), s32[]{:S(2)}) async-start(), calls=%async_computation.18 | async-start | bytes 2359296 | tf_op jit(solution)/shard_map/all_gather | solution.py:444
  554.1 7.1 copy-start.64
  554.1 9.5 %copy-start.29 = (f32[512,1024]{1,0:T(8,128)S(1)}, f32[512,1024]{1,0:T(8,128)}, u32[]{:S(2)}) copy-start(f32[512,1024]{1,0:T(8,128)} %get-tuple-element.175) | copy-start | bytes 6291460
  559.7 17.7 %collective-permute-start.12 = (bf16[256,1024]{1,0:T(8,128)(2,1)}, bf16[256,1024]{1,0:T(8,128)(2,1)S(1)}, u32[]{:S(2)}, u32[]{:S(2)}) collective-permute-start(bf16[256,1024]{1,0:T(8,128)(2,1)} %bitcast.83), channel_id=1, source_target_pairs={{0,8},{8,0},{1,9},{9,1},{2,10},{10,2},{3,11},{11,3},{4,12},{12,4},... | collective-permute-start | bytes 1572872 | tf_op jit(solution)/shard_map/ppermute | solution.py:394
  561.3 15.0 %collective-permute-start.19 = (bf16[128,1024]{1,0:T(8,128)(2,1)S(1)}, bf16[128,1024]{1,0:T(8,128)(2,1)S(1)}, u32[]{:S(2)}, u32[]{:S(2)}) collective-permute-start(bf16[128,1024]{1,0:T(8,128)(2,1)S(1)} %dynamic-slice_bitcast_fusion.1), channel_id=1, source_target_pairs={{0,16},{16,0},{1,17},{17,1},{2,18},{18,2},{3,19},{19,3},{4,20},{20... | collective-permute-start | bytes 786440 | tf_op jit(solution)/shard_map/ppermute | solution.py:394
  577.1 131.1 %all-gather.14.cloned.1.call-start = ((), (), s32[]{:S(2)}) async-start(), calls=%async_computation.17 | async-start | bytes 2949120 | tf_op jit(solution)/shard_map/all_gather | solution.py:444
  582.5 24.7 %copy-start.73 = (s32[4,256]{1,0:T(4,128)S(1)}, s32[4,256]{1,0:T(4,128)}, u32[]{:S(2)}) copy-start(s32[4,256]{1,0:T(4,128)} %param.17) | copy-start | bytes 12292
  582.5 23.9 %collective-permute-start.13 = (bf16[256,1024]{1,0:T(8,128)(2,1)S(1)}, bf16[256,1024]{1,0:T(8,128)(2,1)S(1)}, u32[]{:S(2)}, u32[]{:S(2)}) collective-permute-start(bf16[256,1024]{1,0:T(8,128)(2,1)S(1)} %fusion.41), channel_id=1, source_target_pairs={{0,16},{16,0},{1,17},{17,1},{2,18},{18,2},{3,19},{19,3},{4,20},{20... | collective-permute-start | bytes 1572872 | tf_op jit(solution)/shard_map/ppermute | solution.py:394
  606.6 24.0 %collective-permute-start.14 = (bf16[2,256,1024]{2,1,0:T(8,128)(2,1)S(1)}, bf16[2,256,1024]{2,1,0:T(8,128)(2,1)S(1)}, u32[]{:S(2)}, u32[]{:S(2)}) collective-permute-start(bf16[2,256,1024]{2,1,0:T(8,128)(2,1)S(1)} %pad_maximum_fusion.13), channel_id=1, source_target_pairs={{0,8},{8,0},{1,9},{9,1},{2,10},{10,2},{3,11},{11,3},{4,12},{12,4},... | collective-permute-start | bytes 3145736 | tf_op jit(solution)/shard_map/ppermute | solution.py:394
  633.0 18.0 %copy-start.59 = (bf16[2,160,1024]{2,1,0:T(8,128)(2,1)S(1)}, bf16[2,160,1024]{2,1,0:T(8,128)(2,1)}, u32[]{:S(2)}) copy-start(bf16[2,160,1024]{2,1,0:T(8,128)(2,1)} %reduce-scatter.8.cloned.1.call-done) | copy-start | bytes 1966084
  633.0 17.9 %collective-permute-start.18 = (bf16[160,1024]{1,0:T(8,128)(2,1)S(1)}, bf16[160,1024]{1,0:T(8,128)(2,1)S(1)}, u32[]{:S(2)}, u32[]{:S(2)}) collective-permute-start(bf16[160,1024]{1,0:T(8,128)(2,1)S(1)} %dynamic-slice_bitcast_fusion), channel_id=1, source_target_pairs={{0,16},{16,0},{1,17},{17,1},{2,18},{18,2},{3,19},{19,3},{4,20},{20... | collective-permute-start | bytes 983048 | tf_op jit(solution)/shard_map/ppermute | solution.py:394
  641.0 10.8 %copy-start.37 = (f32[256,1024]{1,0:T(8,128)S(1)}, f32[256,1024]{1,0:T(8,128)}, u32[]{:S(2)}) copy-start(f32[256,1024]{1,0:T(8,128)} %get-tuple-element.172) | copy-start | bytes 3145732
  641.6 11.6 %copy-start.15 = (bf16[2,2,2,128,1024]{4,3,0,2,1:T(8,128)(2,1)S(1)}, bf16[2,2,2,128,1024]{4,3,0,2,1:T(8,128)(2,1)}, u32[]{:S(2)}) copy-start(bf16[2,2,2,128,1024]{4,3,0,2,1:T(8,128)(2,1)} %reverse_select_fusion.3) | copy-start | bytes 6291460
  652.4 5.0 collective-permute-start.16
  655.1 18.5 %copy-start.40 = (bf16[2,256,768]{2,1,0:T(8,128)(2,1)S(1)}, bf16[2,256,768]{2,1,0:T(8,128)(2,1)}, u32[]{:S(2)}) copy-start(bf16[2,256,768]{2,1,0:T(8,128)(2,1)} %pad_maximum_fusion.16) | copy-start | bytes 2359300
  671.7 15.7 %collective-permute-start.17 = (bf16[80,256]{1,0:T(8,128)(2,1)S(1)}, bf16[80,256]{1,0:T(8,128)(2,1)S(1)}, u32[]{:S(2)}, u32[]{:S(2)}) collective-permute-start(bf16[80,256]{1,0:T(8,128)(2,1)S(1)} %dynamic-slice_bitcast_fusion.2), channel_id=1, source_target_pairs={{0,16},{16,0},{1,17},{17,1},{2,18},{18,2},{3,19},{19,3},{4,20},{20... | collective-permute-start | bytes 122888 | tf_op jit(solution)/shard_map/ppermute | solution.py:394
  673.6 20.0 %collective-permute-start.15 = (bf16[2,256,768]{2,1,0:T(8,128)(2,1)S(1)}, bf16[2,256,768]{2,1,0:T(8,128)(2,1)S(1)}, u32[]{:S(2)}, u32[]{:S(2)}) collective-permute-start(bf16[2,256,768]{2,1,0:T(8,128)(2,1)S(1)} %copy-done.40), channel_id=1, source_target_pairs={{0,8},{8,0},{1,9},{9,1},{2,10},{10,2},{3,11},{11,3},{4,12},{12,4},... | collective-permute-start | bytes 2359304 | tf_op jit(solution)/shard_map/ppermute | solution.py:394
  (58 other events, 131.6 us)
Sparse Core Ops, SparseCore 0:
  28.5 26.8 all-gather.9
  69.5 59.3 all-gather.17
  131.9 81.9 all-gather.19
  282.4 124.5 reduce-scatter.3
  435.4 53.6 reduce-scatter.5
  491.0 47.8 all-gather.11
  549.1 57.2 reduce-scatter.7
  608.3 27.8 all-gather.15
  652.0 34.0 all-gather.13

commit v11 on v10

--- a/solution.py
+++ b/solution.py
@@ -582,9 +582,7 @@
         ],
         axis=1,
     )
-    hidden_part = lax.psum_scatter(
-        hidden_terms.reshape(-1, width), ("far", "rows"), scatter_dimension=0, tiled=True
-    )
+    hidden_part = part_rows(hidden_terms)
 
     hidden_gain_term = jnp.sum(grad_three * unit_three, axis=0)
     grad_cross = grad_low.astype(WIDE) + normed_back(
@@ -592,11 +590,14 @@
     )
     grad_cross_low = grad_cross.astype(LOW)
     grad_mixed = exchange_rows(to_pairs(cross_whole[: 2 * cols], grad_cross_low, 1)[:, :, 0])
-    grad_mixed, result = tie(grad_mixed, result)
+    grad_mixed, hidden_part = tie(grad_mixed, hidden_part)
+    hidden_own, hidden_away = own_and_away(hidden_part)
+    hidden_away = swap(hidden_away, "far")
+    grads = pair_backward(cross_q, pair, 0, length, grad_mixed, cross_wide, cross_log)
+    grads, hidden_away, result = tie(grads, hidden_away, result)
+    hidden_total = join_rows(add_far(hidden_own, hidden_away))
     result_two = jnp.stack([result, swap(result, "far")])
-    grads = pair_backward(cross_q, pair, 0, length, grad_mixed, cross_wide, cross_log)
-    grads, result_two = tie(grads, result_two)
-    grads = exchange_rows(grads)
+    grads, result_two = tie(exchange_rows(grads), result_two)
     grad_cq_t = from_pairs(grads[:, :, :1])
     grad_pair_t = from_pairs(grads[:, :, 1:])
     middle_terms = jnp.concatenate(
@@ -610,9 +611,8 @@
     grad_cq_away, middle_terms = tie(swap(grad_cq_t, "near"), middle_terms)
     middle_part = part_rows(middle_terms)
     grad_two = mul(jnp.concatenate([grad_cq_t, grad_cq_away]), query_whole, TN)
-    grad_two, result_two, hidden_part = tie(grad_two, result_two, hidden_part)
+    grad_two, result_two = tie(grad_two, result_two)
     result_four = jnp.stack([result_two, swap(result_two, "near")])
-    hidden_total = join_rows(hidden_part)
     cross_gain_term = jnp.sum(grad_two * unit_two, axis=0)
     grad_self = grad_cross + normed_back(grad_two * cross_gain_f, unit_two, rate_two)
     grad_self_low = grad_self.astype(LOW)
@@ -633,8 +633,9 @@
     last_terms = jnp.pad(
         jnp.concatenate([output_terms, patch_terms], axis=1), ((0, 0), (3 * cols, 0), (0, 0))
     )
-    grads, patch_two, last_terms, hidden_total, middle_part = tie(
-        exchange_rows(grads), patch_two, last_terms, hidden_total, middle_part
+    hidden_gradients = [hidden_total[hidden:].T.astype(WIDE), hidden_total[:hidden].astype(WIDE)]
+    grads, patch_two, last_terms, hidden_gradients, middle_part = tie(
+        exchange_rows(grads), patch_two, last_terms, hidden_gradients, middle_part
     )
     grad_qkv_t = from_pairs(grads)
     last_terms = lax.dynamic_update_slice_in_dim(last_terms, by_shard(grad_qkv_t, normed_one), 0, 1)
@@ -648,10 +649,9 @@
     input_half = self_half + normed_back(grad_one * gain_half, unit_half, rate_half)
     input_half = input_half.astype(LOW)
     input_two = jnp.stack([input_half, swap(input_half, "far")])
-    input_two, patch_two = tie(input_two, patch_two)
+    last_part, input_two, patch_two = tie(last_part, input_two, patch_two)
     input_four = jnp.stack([input_two, swap(input_two, "near")])
     patch_four = jnp.stack([patch_two, swap(patch_two, "near")])
-    last_part, input_four = tie(last_part, input_four)
     onehot_half = halves(onehot)[0].astype(WIDE)
     table_term = jnp.concatenate(
         [
@@ -685,8 +685,7 @@
         cross_output_total,
         patch_total.T,
         small[2 * codes],
-        hidden_total[hidden:].T,
-        hidden_total[:hidden],
+        *hidden_gradients,
     )
     return (outputs, input_grads.astype(WIDE), patch_grads.astype(WIDE)) + tuple(
         value.astype(WIDE) for value in gradients

time: 736 us -> 728 us (0.989)
  starting transfers between devices: 64.7 us -> 49 us
  waiting for transfers between devices: 275 us -> 283 us
    all_to_all x8, waiting for transfers between devices: 89 us -> 48.9 us  [exchange_rows(): return lax.all_to_all(value, 'rows', 0, 0, tiled=True)]
    reduce_scatter x2 -> x3, waiting for transfers between devices: 0.01 us -> 26 us  [part_rows(): return lax.psum_scatter(both, 'rows', scatter_dimension=1, tiled=True)]
    ppermute x20 -> x21, waiting for transfers between devices: 185 us -> 208 us  [swap(): return lax.ppermute(value, axis, [(0, 1), (1, 0)])]
    ppermute x20 -> x21, starting transfers between devices: 31.6 us -> 15.9 us  [swap(): return lax.ppermute(value, axis, [(0, 1), (1, 0)])]
    unnamed x185 -> x169, local copies, waits for them, and re-layouts: 42.4 us -> 41.2 us
  transfers between devices with their start and end apart: 37 -> 38, of which waited for: 23 -> 24; matrix products, arithmetic and copies ran while one was open for 25% -> 25% of each run, Pallas kernels for 12% -> 12%
where the time goes in v11:
time: 728 us; the launch traced here: 718 us
  waiting for transfers between devices  283 us (39%)
  local copies, waits for them, and re-layouts  111 us (15%)
  Pallas kernels  89.3 us (12%)
  other arithmetic  84.8 us (12%)
  matrix products  62.7 us (9%)
  starting transfers between devices  49 us (7%)
  blocking collectives  22.6 us (3%)
  between operations  15.6 us (2%)
    ppermute x21, waiting for transfers between devices, swap(): return lax.ppermute(value, axis, [(0, 1), (1, 0)])  208 us
    dot_general x31, matrix products, mul(): return lax.dot_general(left, right, dims, preferred_element_type=WIDE)  61.7 us
    pallas_call x2, Pallas kernels, pair_backward(): pl.pallas_call(kernel, grid_spec=pltpu.PrefetchScalarGridSpec(num_scalar_...  55.4 us
    all_to_all x8, waiting for transfers between devices, exchange_rows(): return lax.all_to_all(value, 'rows', 0, 0, tiled=True)  48.9 us
    unnamed x169, local copies, waits for them, and re-layouts  41.2 us
    pallas_call x2, Pallas kernels, pair_forward(): pl.pallas_call(kernel, grid_spec=pltpu.PrefetchScalarGridSpec(num_scalar_...  33.9 us
    all_to_all x8, starting transfers between devices, exchange_rows(): return lax.all_to_all(value, 'rows', 0, 0, tiled=True)  32.5 us
    reduce_scatter x3, waiting for transfers between devices, part_rows(): return lax.psum_scatter(both, 'rows', scatter_dimension=1, tiled=True)  26 us
  transfers between devices with their start and end apart: 38, of which 24 were waited for; matrix products, arithmetic and copies ran while one was open for 25% of the time, Pallas kernels for 12%

profile of v11, /device:TPU:0, one launch (start us, length us, event | category | flops | bytes accessed | tf_op | source)
XLA Modules:
  0.0 718.3 jit_solution(3319074210720761607)
XLA Ops:
  7.2 2.7 copy.97
  10.0 2.7 copy.98
  14.4 4.0 collective-permute-start
  19.9 7.8 %collective-permute-done = bf16[96,1024]{1,0:T(8,128)(2,1)S(1)} collective-permute-done((bf16[96,1024]{1,0:T(8,128)(2,1)}, bf16[96,1024]{1,0:T(8,128)(2,1)S(1)}, u32[]{:S(2)}, u32[]{:S(2)}) %collective-permute-start) | collective-permute-done | bytes 196640 | tf_op jit(solution)/shard_map/ppermute | solution.py:394
  40.9 17.1 %collective-permute-done.1 = bf16[160,1024]{1,0:T(8,128)(2,1)} collective-permute-done((bf16[160,1024]{1,0:T(8,128)(2,1)}, bf16[160,1024]{1,0:T(8,128)(2,1)}, u32[]{:S(2)}, u32[]{:S(2)}) %collective-permute-start.1) | collective-permute-done | bytes 327712 | tf_op jit(solution)/shard_map/ppermute | solution.py:394
  59.9 8.5 %collective-permute-done.2 = bf16[2,96,1024]{2,1,0:T(8,128)(2,1)S(1)} collective-permute-done((bf16[2,96,1024]{2,1,0:T(8,128)(2,1)S(1)}, bf16[2,96,1024]{2,1,0:T(8,128)(2,1)S(1)}, u32[]{:S(2)}, u32[]{:S(2)}) %collective-permute-start.2) | collective-permute-done | bytes 393248 | tf_op jit(solution)/shard_map/ppermute | solution.py:394
  72.8 2.8 constant_dynamic-update-slice_fusion.3
  75.5 3.3 convolution_convert_fusion.3
  78.8 2.9 convolution_convert_fusion.4
  83.0 4.3 all-to-all-start
  89.2 23.8 %all-to-all-done.q_ref.k_ref.v_ref = bf16[8,2,3,64,256]{4,3,2,1,0:T(8,128)(2,1)} async-done(((bf16[8,2,3,64,256]{4,3,2,1,0:T(8,128)(2,1)}), bf16[8,2,3,64,256]{4,3,2,1,0:T(8,128)(2,1)}, u32[]{:S(2)}, u32[]{:S(2)}) %all-to-all-start) | async-done | bytes 1572896 | tf_op jit(solution)/shard_map/all_to_all | solution.py:230
  122.4 19.0 %pair_forward.2 = (bf16[8,2,64,256]{3,2,1,0:T(8,128)(2,1)}, f32[8,2,64,256]{3,2,1,0:T(8,128)S(1)}, f32[8,2,1,256]{3,2,1,0:T(1,128)S(1)}) custom-call(s32[2]{0:T(128)S(1)} %broadcast_13_len_ref.2.len_ref, bf16[8,2,3,64,256]{4,3,2,1,0:T(8,128)(2,1)} %all-to-all-done.q_ref.k_ref.v_ref, bf16[8,2,3,64,256]{4,3,2,1,0:T(8,128)(2,1)} %all-to-all-done.q_ref.k_ref.v_ref, ...), custom_call_target="tpu_custom_call" | custom-call | flops 20132659200 | bytes 8388608 | tf_op jit(solution)/shard_map/pair_forward/pallas_call | solution.py:282
  142.4 4.0 all-to-all-start.1
  149.3 2.9 copy-done.22
  152.2 3.3 slice.169
  158.8 4.2 all-to-all-start.2
  163.2 3.7 fusion.76
  166.9 6.2 fusion.77
  173.3 11.7 %collective-permute-done.3 = bf16[512,512]{1,0:T(8,128)(2,1)S(1)} collective-permute-done((bf16[512,512]{1,0:T(8,128)(2,1)}, bf16[512,512]{1,0:T(8,128)(2,1)S(1)}, u32[]{:S(2)}, u32[]{:S(2)}) %collective-permute-start.3) | collective-permute-done | bytes 524320 | tf_op jit(solution)/shard_map/ppermute | solution.py:394
  189.6 4.2 all-to-all-start.3
  193.9 9.6 %all-to-all-done.3.q_ref = bf16[8,2,1,64,256]{4,3,2,1,0:T(8,128)(2,1)} async-done(((bf16[8,2,1,64,256]{4,3,2,1,0:T(8,128)(2,1)}), bf16[8,2,1,64,256]{4,3,2,1,0:T(8,128)(2,1)}, u32[]{:S(2)}, u32[]{:S(2)}) %all-to-all-start.3) | async-done | bytes 524320 | tf_op jit(solution)/shard_map/all_to_all | solution.py:230
  203.5 15.0 %pair_forward.3 = (bf16[8,2,64,256]{3,2,1,0:T(8,128)(2,1)S(1)}, f32[8,2,64,256]{3,2,1,0:T(8,128)S(1)}, f32[8,2,1,256]{3,2,1,0:T(1,128)S(1)}) custom-call(s32[2]{0:T(128)S(1)} %dynamic_slice.124.len_ref, bf16[8,2,1,64,256]{4,3,2,1,0:T(8,128)(2,1)} %all-to-all-done.3.q_ref, bf16[8,2,2,64,256]{4,3,2,1,0:T(8,128)(2,1)S(1)} %all-to-all-done.2.k_ref.v_ref, ...), custom_call_target="tpu_custom_call" | custom-call | flops 14092861440 | bytes 8388608 | tf_op jit(solution)/shard_map/pair_forward/pallas_call | solution.py:282
  218.5 12.3 %all_to_all.45 = bf16[8,2,64,256]{3,2,1,0:T(8,128)(2,1)S(1)} all-to-all(bf16[8,2,64,256]{3,2,1,0:T(8,128)(2,1)S(1)} %get-tuple-element.74), channel_id=1, replica_groups=mesh['far'=2,'near'=2,'rows'=8] {'rows'}, dimensions={0} | all-to-all | bytes 1048576 | tf_op jit(solution)/shard_map/all_to_all | solution.py:230
  233.4 11.2 %collective-permute-done.4 = bf16[512,512]{1,0:T(8,128)(2,1)S(1)} collective-permute-done((bf16[512,512]{1,0:T(8,128)(2,1)S(1)}, bf16[512,512]{1,0:T(8,128)(2,1)S(1)}, u32[]{:S(2)}, u32[]{:S(2)}) %collective-permute-start.4) | collective-permute-done | bytes 524320 | tf_op jit(solution)/shard_map/ppermute | solution.py:394
  247.6 2.8 slice.177
  256.7 5.1 multiply_convert_fusion
  261.8 3.4 fusion.22
  265.2 4.8 convolution_convert_fusion.1
  270.0 4.4 convolution_convert_fusion.2
  274.4 7.8 %pad_maximum_fusion = bf16[2,2048,1024]{2,1,0:T(8,128)(2,1)} fusion(bf16[2,1024,1024]{2,1,0:T(8,128)(2,1)} %bitcast.329, bf16[2,1024,1024]{2,1,0:T(8,128)(2,1)} %bitcast.330), kind=kLoop, calls=%fused_computation.3 | loop fusion | flops 16777216 | bytes 16777216 | tf_op jit(solution)/shard_map/concatenate | solution.py:578
  284.7 5.0 fusion.82
  290.7 15.2 %collective-permute-done.5 = bf16[512,1024]{1,0:T(8,128)(2,1)} collective-permute-done((bf16[512,1024]{1,0:T(8,128)(2,1)}, bf16[512,1024]{1,0:T(8,128)(2,1)}, u32[]{:S(2)}, u32[]{:S(2)}) %collective-permute-start.5) | collective-permute-done | bytes 1048608 | tf_op jit(solution)/shard_map/ppermute | solution.py:394
  313.0 3.5 all-to-all-start.5
  321.2 10.9 %all-to-all-done.5.g_ref = bf16[8,2,64,256]{3,2,1,0:T(8,128)(2,1)S(1)} async-done(((bf16[8,2,64,256]{3,2,1,0:T(8,128)(2,1)}), bf16[8,2,64,256]{3,2,1,0:T(8,128)(2,1)S(1)}, u32[]{:S(2)}, u32[]{:S(2)}) %all-to-all-start.5) | async-done | bytes 524320 | tf_op jit(solution)/shard_map/all_to_all | solution.py:230
  332.1 26.0 %reduce-scatter.4.cloned.1.call-done = bf16[2,256,1024]{2,1,0:T(8,128)(2,1)} async-done(((bf16[2,2048,1024]{2,1,0:T(8,128)(2,1)}), bf16[2,256,1024]{2,1,0:T(8,128)(2,1)}) %reduce-scatter.4.cloned.1.call-update) | async-done | bytes 1048592 | tf_op jit(solution)/shard_map/reduce_scatter | solution.py:567
  361.7 23.3 %pair_backward.2 = bf16[8,2,3,64,256]{4,3,2,1,0:T(8,128)(2,1)} custom-call(s32[2]{0:T(128)S(1)} %dynamic_slice.124.len_ref, bf16[8,2,1,64,256]{4,3,2,1,0:T(8,128)(2,1)} %all-to-all-done.3.q_ref, bf16[8,2,2,64,256]{4,3,2,1,0:T(8,128)(2,1)S(1)} %all-to-all-done.2.k_ref.v_ref, bf16[8,2,2,64,256]{4,3,2,1,0:T(8,128)(2,1)S(1)} %all-to-all-done.2.k_ref.v_ref, ...), custom_call_target="tpu_custom_call" | custom-call | flops 20132659200 | bytes 8388608 | tf_op jit(solution)/shard_map/pair_backward/pallas_call | solution.py:364
  386.1 4.4 all-to-all-start.6
  396.2 20.8 %collective-permute-done.8 = bf16[256,1024]{1,0:T(8,128)(2,1)S(1)} collective-permute-done((bf16[256,1024]{1,0:T(8,128)(2,1)S(1)}, bf16[256,1024]{1,0:T(8,128)(2,1)S(1)}, u32[]{:S(2)}, u32[]{:S(2)}) %collective-permute-start.8) | collective-permute-done | bytes 524320 | tf_op jit(solution)/shard_map/ppermute | solution.py:394
  432.2 5.1 collective-permute-done.9
  441.4 4.3 fusion.73
  447.6 3.7 all-to-all-start.7
  453.4 3.0 convolution_convert_fusion.8
  456.4 4.7 all-to-all-done.7.g_ref
  461.0 32.1 %pair_backward.3 = bf16[8,2,3,64,256]{4,3,2,1,0:T(8,128)(2,1)} custom-call(s32[2]{0:T(128)S(1)} %broadcast_13_len_ref.2.len_ref, bf16[8,2,3,64,256]{4,3,2,1,0:T(8,128)(2,1)} %all-to-all-done.q_ref.k_ref.v_ref, bf16[8,2,3,64,256]{4,3,2,1,0:T(8,128)(2,1)} %all-to-all-done.q_ref.k_ref.v_ref, bf16[8,2,3,64,256]{4,3,2,1,0:T(8,128)(2,1)} %all-to-all-done.q_ref.k_ref.v_ref, ...), custom_call_target="tpu_custom_call" | custom-call | flops 30198988800 | bytes 8388608 | tf_op jit(solution)/shard_map/pair_backward/pallas_call | solution.py:364
  493.2 6.2 collective-permute-done.11
  499.4 2.7 pad_maximum_fusion.5
  502.2 4.3 all-to-all-start.8
  510.9 6.3 fusion.2
  517.3 12.2 %collective-permute-done.12 = bf16[256,768]{1,0:T(8,128)(2,1)S(1)} collective-permute-done((bf16[256,768]{1,0:T(8,128)(2,1)S(1)}, bf16[256,768]{1,0:T(8,128)(2,1)S(1)}, u32[]{:S(2)}, u32[]{:S(2)}) %collective-permute-start.12) | collective-permute-done | bytes 393248 | tf_op jit(solution)/shard_map/ppermute | solution.py:394
  530.4 6.7 slice_convert_fusion
  537.1 3.0 copy.115
  548.0 12.6 %collective-permute-done.20 = bf16[128,1024]{1,0:T(8,128)(2,1)S(1)} collective-permute-done((bf16[128,1024]{1,0:T(8,128)(2,1)S(1)}, bf16[128,1024]{1,0:T(8,128)(2,1)S(1)}, u32[]{:S(2)}, u32[]{:S(2)}) %collective-permute-start.20) | collective-permute-done | bytes 262176 | tf_op jit(solution)/shard_map/ppermute | solution.py:394
  561.7 4.3 fusion.10
  567.9 12.0 %collective-permute-done.13 = bf16[256,1024]{1,0:T(8,128)(2,1)S(1)} collective-permute-done((bf16[256,1024]{1,0:T(8,128)(2,1)S(1)}, bf16[256,1024]{1,0:T(8,128)(2,1)S(1)}, u32[]{:S(2)}, u32[]{:S(2)}) %collective-permute-start.13) | collective-permute-done | bytes 524320 | tf_op jit(solution)/shard_map/ppermute | solution.py:394
  582.5 24.8 %collective-permute-done.14 = bf16[256,1024]{1,0:T(8,128)(2,1)S(1)} collective-permute-done((bf16[256,1024]{1,0:T(8,128)(2,1)}, bf16[256,1024]{1,0:T(8,128)(2,1)S(1)}, u32[]{:S(2)}, u32[]{:S(2)}) %collective-permute-start.14) | collective-permute-done | bytes 524320 | tf_op jit(solution)/shard_map/ppermute | solution.py:394
  610.7 3.2 copy.114
  614.4 12.7 %collective-permute-done.19 = bf16[160,1024]{1,0:T(8,128)(2,1)S(1)} collective-permute-done((bf16[160,1024]{1,0:T(8,128)(2,1)S(1)}, bf16[160,1024]{1,0:T(8,128)(2,1)S(1)}, u32[]{:S(2)}, u32[]{:S(2)}) %collective-permute-start.19) | collective-permute-done | bytes 327712 | tf_op jit(solution)/shard_map/ppermute | solution.py:394
  628.6 3.3 reverse_select_fusion.3
  634.2 10.3 %all-gather.2 = bf16[16,80,256]{2,1,0:T(8,128)(2,1)S(1)} all-gather(bf16[2,80,256]{2,1,0:T(8,128)(2,1)S(1)} %pad_maximum_fusion.21), channel_id=4, replica_groups=mesh['far'=2,'near'=2,'rows'=8] {'rows'}, dimensions={0}, use_global_device_ids=true | all-gather | bytes 737280 | tf_op jit(solution)/shard_map/all_gather | solution.py:665
  647.4 5.3 copy.127
  661.6 2.9 copy.125
  664.5 9.7 %collective-permute-done.16 = bf16[2,256,768]{2,1,0:T(8,128)(2,1)} collective-permute-done((bf16[2,256,768]{2,1,0:T(8,128)(2,1)}, bf16[2,256,768]{2,1,0:T(8,128)(2,1)}, u32[]{:S(2)}, u32[]{:S(2)}) %collective-permute-start.16) | collective-permute-done | bytes 786464 | tf_op jit(solution)/shard_map/ppermute | solution.py:394
  678.3 17.5 %collective-permute-done.15 = bf16[2,256,1024]{2,1,0:T(8,128)(2,1)} collective-permute-done((bf16[2,256,1024]{2,1,0:T(8,128)(2,1)}, bf16[2,256,1024]{2,1,0:T(8,128)(2,1)}, u32[]{:S(2)}, u32[]{:S(2)}) %collective-permute-start.15) | collective-permute-done | bytes 1048608 | tf_op jit(solution)/shard_map/ppermute | solution.py:394
  705.5 3.7 copy.123
  (378 shorter events, 161.7 us)
Async XLA Ops:
  7.2 224.9 %copy-start = (bf16[4,256,1024]{2,1,0:T(8,128)(2,1)S(1)}, bf16[4,256,1024]{2,1,0:T(8,128)(2,1)}, u32[]{:S(2)}) copy-start(bf16[4,256,1024]{2,1,0:T(8,128)(2,1)} %param.31) | copy-start | bytes 6291460
  7.2 65.6 %all-gather.10.cloned.1.call-start = ((), (), s32[]{:S(2)}) async-start(), calls=%async_computation.12 | async-start | bytes 1769472 | tf_op jit(solution)/shard_map/all_gather | solution.py:444
  10.0 8.4 %copy-start.64 = (s32[4,256]{1,0:T(4,128)S(1)}, s32[4,256]{1,0:T(4,128)}, u32[]{:S(2)}) copy-start(s32[4,256]{1,0:T(4,128)} %param.17) | copy-start | bytes 12292
  12.7 18.1 %copy-start.60 = (bf16[32,2,1024]{2,1,0:T(2,128)(2,1)S(1)}, bf16[32,2,1024]{2,1,0:T(2,128)(2,1)}, u32[]{:S(2)}) copy-start(bf16[32,2,1024]{2,1,0:T(2,128)(2,1)} %param.20) | copy-start | bytes 393220
  12.7 20.0 %copy-start.47 = (bf16[2,1024,256]{2,1,0:T(8,128)(2,1)S(1)}, bf16[2,1024,256]{2,1,0:T(8,128)(2,1)}, u32[]{:S(2)}) copy-start(bf16[2,1024,256]{2,1,0:T(8,128)(2,1)} %param.25) | copy-start | bytes 3145732
  14.4 13.4 %collective-permute-start = (bf16[96,1024]{1,0:T(8,128)(2,1)}, bf16[96,1024]{1,0:T(8,128)(2,1)S(1)}, u32[]{:S(2)}, u32[]{:S(2)}) collective-permute-start(bf16[96,1024]{1,0:T(8,128)(2,1)} %constant_dynamic-slice_fusion.20), channel_id=1, source_target_pairs={{0,16},{16,0},{1,17},{17,1},{2,18},{18,2},{3,19},{19,3},{4,20},{20... | collective-permute-start | bytes 589832 | tf_op jit(solution)/shard_map/ppermute | solution.py:394
  19.9 11.5 %copy-start.61 = (f32[2,256]{1,0:T(2,128)}, f32[2,256]{1,0:T(2,128)S(1)}, u32[]{:S(2)}) copy-start(f32[2,256]{1,0:T(2,128)S(1)} %get-tuple-element.207) | copy-start | bytes 6148
  28.4 118.0 %all-gather.18.cloned.1.call-start = ((), (), s32[]{:S(2)}) async-start(), calls=%async_computation.19 | async-start | bytes 8257536 | tf_op jit(solution)/shard_map/all_gather | solution.py:522
  40.8 17.1 %collective-permute-start.1 = (bf16[160,1024]{1,0:T(8,128)(2,1)}, bf16[160,1024]{1,0:T(8,128)(2,1)}, u32[]{:S(2)}, u32[]{:S(2)}) collective-permute-start(bf16[160,1024]{1,0:T(8,128)(2,1)} %pad_maximum_fusion.19), channel_id=1, source_target_pairs={{0,16},{16,0},{1,17},{17,1},{2,18},{18,2},{3,19},{19,3},{4,20},{20... | collective-permute-start | bytes 983048 | tf_op jit(solution)/shard_map/ppermute | solution.py:394
  58.9 9.4 %collective-permute-start.2 = (bf16[2,96,1024]{2,1,0:T(8,128)(2,1)S(1)}, bf16[2,96,1024]{2,1,0:T(8,128)(2,1)S(1)}, u32[]{:S(2)}, u32[]{:S(2)}) collective-permute-start(bf16[2,96,1024]{2,1,0:T(8,128)(2,1)S(1)} %fusion.60), channel_id=1, source_target_pairs={{0,8},{8,0},{1,9},{9,1},{2,10},{10,2},{3,11},{11,3},{4,12},{12,4},... | collective-permute-start | bytes 1179656 | tf_op jit(solution)/shard_map/ppermute | solution.py:394
  83.0 29.9 %all-to-all-start = ((bf16[8,2,3,64,256]{4,3,2,1,0:T(8,128)(2,1)}), bf16[8,2,3,64,256]{4,3,2,1,0:T(8,128)(2,1)}, u32[]{:S(2)}, u32[]{:S(2)}) async-start(bf16[8,2,3,64,256]{4,3,2,1,0:T(8,128)(2,1)} %pad_maximum_fusion.7), calls=%async_computation | async-start | bytes 3145728 | tf_op jit(solution)/shard_map/all_to_all | solution.py:230
  87.3 27.4 %copy-start.66 = (bf16[1024]{0:T(1024)(128)(2,1)S(1)}, bf16[1024]{0:T(1024)(128)(2,1)}, u32[]{:S(2)}) copy-start(bf16[1024]{0:T(1024)(128)(2,1)} %param.23) | copy-start | bytes 6148
  87.3 160.2 %all-gather.20.cloned.1.call-start = ((), (), s32[]{:S(2)}) async-start(), calls=%async_computation.20 | async-start | bytes 8912896 | tf_op jit(solution)/shard_map/all_gather | solution.py:536
  142.4 14.9 %all-to-all-start.1 = ((bf16[8,2,64,256]{3,2,1,0:T(8,128)(2,1)}), bf16[8,2,64,256]{3,2,1,0:T(8,128)(2,1)S(1)}, u32[]{:S(2)}, u32[]{:S(2)}) async-start(bf16[8,2,64,256]{3,2,1,0:T(8,128)(2,1)} %get-tuple-element.69), calls=%async_computation.1 | async-start | bytes 1048576 | tf_op jit(solution)/shard_map/all_to_all | solution.py:230
  148.6 7.0 copy-start.16
  158.8 30.8 %all-to-all-start.2 = ((bf16[8,2,2,64,256]{4,3,2,1,0:T(8,128)(2,1)}), bf16[8,2,2,64,256]{4,3,2,1,0:T(8,128)(2,1)S(1)}, u32[]{:S(2)}, u32[]{:S(2)}) async-start(bf16[8,2,2,64,256]{4,3,2,1,0:T(8,128)(2,1)} %pad_maximum_fusion.11), calls=%async_computation.2 | async-start | bytes 2097152 | tf_op jit(solution)/shard_map/all_to_all | solution.py:230
  162.9 22.0 %collective-permute-start.3 = (bf16[512,512]{1,0:T(8,128)(2,1)}, bf16[512,512]{1,0:T(8,128)(2,1)S(1)}, u32[]{:S(2)}, u32[]{:S(2)}) collective-permute-start(bf16[512,512]{1,0:T(8,128)(2,1)} %bitcast.335), channel_id=1, source_target_pairs={{0,8},{8,0},{1,9},{9,1},{2,10},{10,2},{3,11},{11,3},{4,12},{12,4},... | collective-permute-start | bytes 1572872 | tf_op jit(solution)/shard_map/ppermute | solution.py:394
  173.1 11.8 %copy-start.32 = (bf16[2,256,1024]{2,1,0:T(8,128)(2,1)S(1)}, bf16[2,256,1024]{2,1,0:T(8,128)(2,1)}, u32[]{:S(2)}) copy-start(bf16[2,256,1024]{2,1,0:T(8,128)(2,1)} %get-tuple-element.199) | copy-start | bytes 3145732
  173.1 11.8 %copy-start.36 = (bf16[64,8,2,256]{3,1,2,0:T(8,128)(2,1)S(1)}, bf16[64,8,2,256]{3,1,2,0:T(8,128)(2,1)}, u32[]{:S(2)}) copy-start(bf16[64,8,2,256]{3,1,2,0:T(8,128)(2,1)} %copy.137) | copy-start | bytes 1572868
  188.2 5.6 copy-start.70
  189.6 13.9 %all-to-all-start.3 = ((bf16[8,2,1,64,256]{4,3,2,1,0:T(8,128)(2,1)}), bf16[8,2,1,64,256]{4,3,2,1,0:T(8,128)(2,1)}, u32[]{:S(2)}, u32[]{:S(2)}) async-start(bf16[8,2,1,64,256]{4,3,2,1,0:T(8,128)(2,1)} %pad_maximum_fusion.17), calls=%async_computation.3 | async-start | bytes 1048576 | tf_op jit(solution)/shard_map/all_to_all | solution.py:230
  193.8 164.3 %reduce-scatter.4.cloned.1.call-start = ((), (), s32[]{:S(2)}) async-start(), calls=%async_computation.13 | async-start | bytes 9437184 | tf_op jit(solution)/shard_map/reduce_scatter | solution.py:567
  218.5 14.6 %copy-start.2 = (f32[8,2,64,256]{3,2,1,0:T(8,128)}, f32[8,2,64,256]{3,2,1,0:T(8,128)S(1)}, u32[]{:S(2)}) copy-start(f32[8,2,64,256]{3,2,1,0:T(8,128)S(1)} %get-tuple-element.82.wide_ref) | copy-start | bytes 3145732
  218.5 13.5 %copy-start.67 = (bf16[1024]{0:T(1024)(128)(2,1)S(1)}, bf16[1024]{0:T(1024)(128)(2,1)}, u32[]{:S(2)}) copy-start(bf16[1024]{0:T(1024)(128)(2,1)} %param.28) | copy-start | bytes 6148
  231.4 13.1 %copy-start.56 = (bf16[64,8,2,256]{3,1,2,0:T(8,128)(2,1)}, bf16[64,8,2,256]{3,1,2,0:T(8,128)(2,1)S(1)}, u32[]{:S(2)}) copy-start(bf16[64,8,2,256]{3,1,2,0:T(8,128)(2,1)S(1)} %copy.138) | copy-start | bytes 1572868
  231.5 13.1 %collective-permute-start.4 = (bf16[512,512]{1,0:T(8,128)(2,1)S(1)}, bf16[512,512]{1,0:T(8,128)(2,1)S(1)}, u32[]{:S(2)}, u32[]{:S(2)}) collective-permute-start(bf16[512,512]{1,0:T(8,128)(2,1)S(1)} %bitcast.366), channel_id=1, source_target_pairs={{0,8},{8,0},{1,9},{9,1},{2,10},{10,2},{3,11},{11,3},{4,12},{12,4},... | collective-permute-start | bytes 1572872 | tf_op jit(solution)/shard_map/ppermute | solution.py:394
  233.1 11.4 %copy-start.7 = (f32[512,1024]{1,0:T(8,128)S(1)}, f32[512,1024]{1,0:T(8,128)}, u32[]{:S(2)}) copy-start(f32[512,1024]{1,0:T(8,128)} %copy-done.6) | copy-start | bytes 6291460
  261.8 8.2 %copy-start.71 = (bf16[512,2048]{1,0:T(8,128)(2,1)}, bf16[512,2048]{1,0:T(8,128)(2,1)S(1)}, u32[]{:S(2)}) copy-start(bf16[512,2048]{1,0:T(8,128)(2,1)S(1)} %get-tuple-element.77) | copy-start | bytes 6291460
  282.2 23.7 %collective-permute-start.5 = (bf16[512,1024]{1,0:T(8,128)(2,1)}, bf16[512,1024]{1,0:T(8,128)(2,1)}, u32[]{:S(2)}, u32[]{:S(2)}) collective-permute-start(bf16[512,1024]{1,0:T(8,128)(2,1)} %fusion.22), channel_id=1, source_target_pairs={{0,8},{8,0},{1,9},{9,1},{2,10},{10,2},{3,11},{11,3},{4,12},{12,4},... | collective-permute-start | bytes 3145736 | tf_op jit(solution)/shard_map/ppermute | solution.py:394
  284.7 21.2 %copy-start.50 = (bf16[512,1024]{1,0:T(8,128)(2,1)S(1)}, bf16[512,1024]{1,0:T(8,128)(2,1)}, u32[]{:S(2)}) copy-start(bf16[512,1024]{1,0:T(8,128)(2,1)} %fusion.22) | copy-start | bytes 3145732
  289.8 18.1 %copy-start.39 = (f32[2,2,128,1024]{3,2,1,0:T(8,128)}, f32[2,2,128,1024]{3,2,1,0:T(8,128)S(1)}, u32[]{:S(2)}) copy-start(f32[2,2,128,1024]{3,2,1,0:T(8,128)S(1)} %fusion.82) | copy-start | bytes 6291460
  307.9 11.2 %collective-permute-start.7 = (bf16[256,1024]{1,0:T(8,128)(2,1)}, bf16[256,1024]{1,0:T(8,128)(2,1)}, u32[]{:S(2)}, u32[]{:S(2)}) collective-permute-start(bf16[256,1024]{1,0:T(8,128)(2,1)} %bitcast.39), channel_id=1, source_target_pairs={{0,8},{8,0},{1,9},{9,1},{2,10},{10,2},{3,11},{11,3},{4,12},{12,4},... | collective-permute-start | bytes 1572872 | tf_op jit(solution)/shard_map/ppermute | solution.py:394
  313.0 19.1 %all-to-all-start.5 = ((bf16[8,2,64,256]{3,2,1,0:T(8,128)(2,1)}), bf16[8,2,64,256]{3,2,1,0:T(8,128)(2,1)S(1)}, u32[]{:S(2)}, u32[]{:S(2)}) async-start(bf16[8,2,64,256]{3,2,1,0:T(8,128)(2,1)} %maximum_bitcast_fusion), calls=%async_computation.5 | async-start | bytes 1048576 | tf_op jit(solution)/shard_map/all_to_all | solution.py:230
  316.5 213.9 %all-gather.12.cloned.1.call-start = ((), (), s32[]{:S(2)}) async-start(), calls=%async_computation.14 | async-start | bytes 4718592 | tf_op jit(solution)/shard_map/all_gather | solution.py:444
  318.6 43.1 %copy-start.3 = (f32[8,2,64,256]{3,2,1,0:T(8,128)S(1)}, f32[8,2,64,256]{3,2,1,0:T(8,128)}, u32[]{:S(2)}) copy-start(f32[8,2,64,256]{3,2,1,0:T(8,128)} %copy-done.2) | copy-start | bytes 3145732
  359.2 25.8 %collective-permute-start.6 = (bf16[256,1024]{1,0:T(8,128)(2,1)S(1)}, bf16[256,1024]{1,0:T(8,128)(2,1)S(1)}, u32[]{:S(2)}, u32[]{:S(2)}) collective-permute-start(bf16[256,1024]{1,0:T(8,128)(2,1)S(1)} %dynamic-slice_bitcast_fusion), channel_id=1, source_target_pairs={{0,16},{16,0},{1,17},{17,1},{2,18},{18,2},{3,19},{19,3},{4,20},{20... | collective-permute-start | bytes 1572872 | tf_op jit(solution)/shard_map/ppermute | solution.py:394
  361.7 23.4 %copy-start.49 = (bf16[2,256,1024]{2,1,0:T(8,128)(2,1)S(1)}, bf16[2,256,1024]{2,1,0:T(8,128)(2,1)}, u32[]{:S(2)}) copy-start(bf16[2,256,1024]{2,1,0:T(8,128)(2,1)} %reduce-scatter.4.cloned.1.call-done) | copy-start | bytes 3145732
  386.1 31.9 %all-to-all-start.6 = ((bf16[8,2,3,64,256]{4,3,2,1,0:T(8,128)(2,1)}), bf16[8,2,3,64,256]{4,3,2,1,0:T(8,128)(2,1)}, u32[]{:S(2)}, u32[]{:S(2)}) async-start(bf16[8,2,3,64,256]{4,3,2,1,0:T(8,128)(2,1)} %pair_backward.2), calls=%async_computation.7 | async-start | bytes 3145728 | tf_op jit(solution)/shard_map/all_to_all | solution.py:230
  390.5 146.6 %reduce-scatter.6.cloned.1.call-start = ((), (), s32[]{:S(2)}) async-start(), calls=%async_computation.15 | async-start | bytes 4718592 | tf_op jit(solution)/shard_map/reduce_scatter | solution.py:567
  390.6 26.4 %collective-permute-start.8 = (bf16[256,1024]{1,0:T(8,128)(2,1)S(1)}, bf16[256,1024]{1,0:T(8,128)(2,1)S(1)}, u32[]{:S(2)}, u32[]{:S(2)}) collective-permute-start(bf16[256,1024]{1,0:T(8,128)(2,1)S(1)} %copy-done.38), channel_id=1, source_target_pairs={{0,16},{16,0},{1,17},{17,1},{2,18},{18,2},{3,19},{19,3},{4,20},{20... | collective-permute-start | bytes 1572872 | tf_op jit(solution)/shard_map/ppermute | solution.py:394
  420.8 5.0 copy-start.35
  423.8 13.6 %collective-permute-start.9 = (bf16[512,512]{1,0:T(8,128)(2,1)}, bf16[512,512]{1,0:T(8,128)(2,1)}, u32[]{:S(2)}, u32[]{:S(2)}) collective-permute-start(bf16[512,512]{1,0:T(8,128)(2,1)} %bitcast.165), channel_id=1, source_target_pairs={{0,8},{8,0},{1,9},{9,1},{2,10},{10,2},{3,11},{11,3},{4,12},{12,4},... | collective-permute-start | bytes 1572872 | tf_op jit(solution)/shard_map/ppermute | solution.py:394
  429.6 7.8 %copy-start.13 = (bf16[1,4,8,32,1024]{4,3,2,1,0:T(8,128)(2,1)S(1)}, bf16[1,4,8,32,1024]{4,3,2,1,0:T(8,128)(2,1)}, u32[]{:S(2)}) copy-start(bf16[1,4,8,32,1024]{4,3,2,1,0:T(8,128)(2,1)} %copy.112) | copy-start | bytes 6291460
  446.2 7.1 copy-start.37
  447.6 13.5 %copy-start.5 = (f32[8,2,64,256]{3,2,1,0:T(8,128)S(1)}, f32[8,2,64,256]{3,2,1,0:T(8,128)}, u32[]{:S(2)}) copy-start(f32[8,2,64,256]{3,2,1,0:T(8,128)} %copy-done.4) | copy-start | bytes 3145732
  447.6 13.5 %all-to-all-start.7 = ((bf16[8,2,64,256]{3,2,1,0:T(8,128)(2,1)}), bf16[8,2,64,256]{3,2,1,0:T(8,128)(2,1)S(1)}, u32[]{:S(2)}, u32[]{:S(2)}) async-start(bf16[8,2,64,256]{3,2,1,0:T(8,128)(2,1)} %maximum_bitcast_fusion.1), calls=%async_computation.8 | async-start | bytes 1048576 | tf_op jit(solution)/shard_map/all_to_all | solution.py:230
  451.3 50.9 %collective-permute-start.10 = (bf16[512,1024]{1,0:T(8,128)(2,1)S(1)}, bf16[512,1024]{1,0:T(8,128)(2,1)}, u32[]{:S(2)}, u32[]{:S(2)}) collective-permute-start(bf16[512,1024]{1,0:T(8,128)(2,1)S(1)} %convolution_convert_fusion.7), channel_id=1, source_target_pairs={{0,8},{8,0},{1,9},{9,1},{2,10},{10,2},{3,11},{11,3},{4,12},{12,4},... | collective-permute-start | bytes 3145736 | tf_op jit(solution)/shard_map/ppermute | solution.py:394
  451.6 47.8 %collective-permute-start.11 = (bf16[2,256,1024]{2,1,0:T(8,128)(2,1)}, bf16[2,256,1024]{2,1,0:T(8,128)(2,1)}, u32[]{:S(2)}, u32[]{:S(2)}) collective-permute-start(bf16[2,256,1024]{2,1,0:T(8,128)(2,1)} %pad_maximum_fusion.12), channel_id=1, source_target_pairs={{0,8},{8,0},{1,9},{9,1},{2,10},{10,2},{3,11},{11,3},{4,12},{12,4},... | collective-permute-start | bytes 3145736 | tf_op jit(solution)/shard_map/ppermute | solution.py:394
  461.0 38.4 %copy-start.34 = (bf16[2,256,1024]{2,1,0:T(8,128)(2,1)S(1)}, bf16[2,256,1024]{2,1,0:T(8,128)(2,1)}, u32[]{:S(2)}) copy-start(bf16[2,256,1024]{2,1,0:T(8,128)(2,1)} %pad_maximum_fusion.12) | copy-start | bytes 3145732
  502.2 34.9 %all-to-all-start.8 = ((bf16[8,2,3,64,256]{4,3,2,1,0:T(8,128)(2,1)}), bf16[8,2,3,64,256]{4,3,2,1,0:T(8,128)(2,1)}, u32[]{:S(2)}, u32[]{:S(2)}) async-start(bf16[8,2,3,64,256]{4,3,2,1,0:T(8,128)(2,1)} %pair_backward.3), calls=%async_computation.9 | async-start | bytes 3145728 | tf_op jit(solution)/shard_map/all_to_all | solution.py:230
  506.5 102.9 %reduce-scatter.8.cloned.1.call-start = ((), (), s32[]{:S(2)}) async-start(), calls=%async_computation.16 | async-start | bytes 5898240 | tf_op jit(solution)/shard_map/reduce_scatter | solution.py:567
  509.0 20.5 %collective-permute-start.12 = (bf16[256,768]{1,0:T(8,128)(2,1)S(1)}, bf16[256,768]{1,0:T(8,128)(2,1)S(1)}, u32[]{:S(2)}, u32[]{:S(2)}) collective-permute-start(bf16[256,768]{1,0:T(8,128)(2,1)S(1)} %convolution_convert_fusion.15), channel_id=1, source_target_pairs={{0,16},{16,0},{1,17},{17,1},{2,18},{18,2},{3,19},{19,3},{4,20},{20... | collective-permute-start | bytes 1179656 | tf_op jit(solution)/shard_map/ppermute | solution.py:394
  545.2 110.6 %all-gather.16.cloned.1.call-start = ((), (), s32[]{:S(2)}) async-start(), calls=%async_computation.18 | async-start | bytes 2359296 | tf_op jit(solution)/shard_map/all_gather | solution.py:444
  546.2 14.3 %collective-permute-start.20 = (bf16[128,1024]{1,0:T(8,128)(2,1)S(1)}, bf16[128,1024]{1,0:T(8,128)(2,1)S(1)}, u32[]{:S(2)}, u32[]{:S(2)}) collective-permute-start(bf16[128,1024]{1,0:T(8,128)(2,1)S(1)} %dynamic-slice_bitcast_fusion.2), channel_id=1, source_target_pairs={{0,16},{16,0},{1,17},{17,1},{2,18},{18,2},{3,19},{19,3},{4,20},{20... | collective-permute-start | bytes 786440 | tf_op jit(solution)/shard_map/ppermute | solution.py:394
  561.3 139.4 %all-gather.14.cloned.1.call-start = ((), (), s32[]{:S(2)}) async-start(), calls=%async_computation.17 | async-start | bytes 2949120 | tf_op jit(solution)/shard_map/all_gather | solution.py:444
  566.1 13.9 %collective-permute-start.13 = (bf16[256,1024]{1,0:T(8,128)(2,1)S(1)}, bf16[256,1024]{1,0:T(8,128)(2,1)S(1)}, u32[]{:S(2)}, u32[]{:S(2)}) collective-permute-start(bf16[256,1024]{1,0:T(8,128)(2,1)S(1)} %bitcast.369), channel_id=1, source_target_pairs={{0,8},{8,0},{1,9},{9,1},{2,10},{10,2},{3,11},{11,3},{4,12},{12,4},... | collective-permute-start | bytes 1572872 | tf_op jit(solution)/shard_map/ppermute | solution.py:394
  581.8 25.5 %collective-permute-start.14 = (bf16[256,1024]{1,0:T(8,128)(2,1)}, bf16[256,1024]{1,0:T(8,128)(2,1)S(1)}, u32[]{:S(2)}, u32[]{:S(2)}) collective-permute-start(bf16[256,1024]{1,0:T(8,128)(2,1)} %fusion.42), channel_id=1, source_target_pairs={{0,16},{16,0},{1,17},{17,1},{2,18},{18,2},{3,19},{19,3},{4,20},{20... | collective-permute-start | bytes 1572872 | tf_op jit(solution)/shard_map/ppermute | solution.py:394
  610.4 16.8 %collective-permute-start.19 = (bf16[160,1024]{1,0:T(8,128)(2,1)S(1)}, bf16[160,1024]{1,0:T(8,128)(2,1)S(1)}, u32[]{:S(2)}, u32[]{:S(2)}) collective-permute-start(bf16[160,1024]{1,0:T(8,128)(2,1)S(1)} %dynamic-slice_bitcast_fusion.1), channel_id=1, source_target_pairs={{0,16},{16,0},{1,17},{17,1},{2,18},{18,2},{3,19},{19,3},{4,20},{20... | collective-permute-start | bytes 983048 | tf_op jit(solution)/shard_map/ppermute | solution.py:394
  610.7 16.5 %copy-start.54 = (bf16[2,160,1024]{2,1,0:T(8,128)(2,1)S(1)}, bf16[2,160,1024]{2,1,0:T(8,128)(2,1)}, u32[]{:S(2)}) copy-start(bf16[2,160,1024]{2,1,0:T(8,128)(2,1)} %reduce-scatter.8.cloned.1.call-done) | copy-start | bytes 1966084
  628.5 5.5 collective-permute-start.17
  644.6 8.2 %collective-permute-start.18 = (bf16[80,256]{1,0:T(8,128)(2,1)S(1)}, bf16[80,256]{1,0:T(8,128)(2,1)S(1)}, u32[]{:S(2)}, u32[]{:S(2)}) collective-permute-start(bf16[80,256]{1,0:T(8,128)(2,1)S(1)} %dynamic-slice_bitcast_fusion.3), channel_id=1, source_target_pairs={{0,16},{16,0},{1,17},{17,1},{2,18},{18,2},{3,19},{19,3},{4,20},{20... | collective-permute-start | bytes 122888 | tf_op jit(solution)/shard_map/ppermute | solution.py:394
  653.5 20.7 %collective-permute-start.16 = (bf16[2,256,768]{2,1,0:T(8,128)(2,1)}, bf16[2,256,768]{2,1,0:T(8,128)(2,1)}, u32[]{:S(2)}, u32[]{:S(2)}) collective-permute-start(bf16[2,256,768]{2,1,0:T(8,128)(2,1)} %pad_maximum_fusion.16), channel_id=1, source_target_pairs={{0,8},{8,0},{1,9},{9,1},{2,10},{10,2},{3,11},{11,3},{4,12},{12,4},... | collective-permute-start | bytes 2359304 | tf_op jit(solution)/shard_map/ppermute | solution.py:394
  659.5 36.3 %collective-permute-start.15 = (bf16[2,256,1024]{2,1,0:T(8,128)(2,1)}, bf16[2,256,1024]{2,1,0:T(8,128)(2,1)}, u32[]{:S(2)}, u32[]{:S(2)}) collective-permute-start(bf16[2,256,1024]{2,1,0:T(8,128)(2,1)} %pad_maximum_fusion.13), channel_id=1, source_target_pairs={{0,8},{8,0},{1,9},{9,1},{2,10},{10,2},{3,11},{11,3},{4,12},{12,4},... | collective-permute-start | bytes 3145736 | tf_op jit(solution)/shard_map/ppermute | solution.py:394
  705.5 5.8 copy-start.1
  (51 other events, 111.8 us)
Sparse Core Ops, SparseCore 0:
  28.5 26.8 all-gather.9
  69.5 59.3 all-gather.17
  131.8 82.0 all-gather.19
  282.3 75.7 reduce-scatter.3
  386.2 47.7 all-gather.11
  441.5 50.9 reduce-scatter.5
  545.3 56.4 reduce-scatter.7
  604.5 27.8 all-gather.15
  634.4 30.1 all-gather.13

commit v12 on v11

--- a/solution.py
+++ b/solution.py
@@ -590,14 +590,13 @@
     )
     grad_cross_low = grad_cross.astype(LOW)
     grad_mixed = exchange_rows(to_pairs(cross_whole[: 2 * cols], grad_cross_low, 1)[:, :, 0])
-    grad_mixed, hidden_part = tie(grad_mixed, hidden_part)
+    grad_mixed, result = tie(grad_mixed, result)
+    result_two = jnp.stack([result, swap(result, "far")])
+    grads = pair_backward(cross_q, pair, 0, length, grad_mixed, cross_wide, cross_log)
+    grads, result_two, hidden_part = tie(grads, result_two, hidden_part)
     hidden_own, hidden_away = own_and_away(hidden_part)
-    hidden_away = swap(hidden_away, "far")
-    grads = pair_backward(cross_q, pair, 0, length, grad_mixed, cross_wide, cross_log)
-    grads, hidden_away, result = tie(grads, hidden_away, result)
+    grads, hidden_away = tie(exchange_rows(grads), swap(hidden_away, "far"))
     hidden_total = join_rows(add_far(hidden_own, hidden_away))
-    result_two = jnp.stack([result, swap(result, "far")])
-    grads, result_two = tie(exchange_rows(grads), result_two)
     grad_cq_t = from_pairs(grads[:, :, :1])
     grad_pair_t = from_pairs(grads[:, :, 1:])
     middle_terms = jnp.concatenate(
@@ -641,8 +640,10 @@
     last_terms = lax.dynamic_update_slice_in_dim(last_terms, by_shard(grad_qkv_t, normed_one), 0, 1)
     last_part = part_rows(last_terms)
     middle_own, middle_away = own_and_away(middle_part)
+    first_mine, first_away = halves(mul(grad_qkv_t, qkv_both, TN))
+    first_away, middle_away = tie(first_away.astype(LOW), middle_away)
     middle_total = join_rows(add_far(middle_own, swap(middle_away, "far")))
-    grad_one = half_sum_near(mul(grad_qkv_t, qkv_both, TN))
+    grad_one = first_mine + swap(first_away, "near").astype(WIDE)
     gain_half, unit_half, rate_half, self_half = (
         halves(value)[0] for value in (gain_one, unit_one, rate_one, grad_self)
     )
@@ -664,11 +665,13 @@
     small = jnp.stack(both_columns(jnp.concatenate(small, axis=0).astype(LOW)))
     small = jnp.sum(lax.all_gather(small, "rows", axis=0).astype(WIDE), axis=0).astype(LOW)
     small_own, small_away = own_and_away(small)
+    small_away, patch_four = tie(small_away, patch_four)
     small = small_own.astype(WIDE) + swap(small_away, "far").astype(WIDE)
+    last_own, last_away = own_and_away(last_part)
+    last_sum, input_four = tie(add_far(last_own, swap(last_away, "far")), input_four)
+    last_total = join_rows(last_sum)
     input_grads = over_heads(input_four)
     outputs, patch_grads = over_heads(result_four), over_heads(patch_four)
-    last_own, last_away = own_and_away(last_part)
-    last_total = join_rows(add_far(last_own, swap(last_away, "far")))
 
     cross_output_total, query_total = middle_total[:cols], middle_total[cols : 2 * cols]
     pair_total = middle_total[2 * cols :].reshape(heads, 2, HEAD_DIM, width)

time: 728 us -> 699 us (0.960)
  waiting for transfers between devices: 283 us -> 234 us
  Pallas kernels: 89.3 us -> 101 us
    ppermute x21, waiting for transfers between devices: 208 us -> 183 us  [swap(): return lax.ppermute(value, axis, [(0, 1), (1, 0)])]
    reduce_scatter x3, waiting for transfers between devices: 26 us -> 1.27 us  [part_rows(): return lax.psum_scatter(both, 'rows', scatter_dimension=1, tiled=True)]
    pallas_call x2, Pallas kernels: 55.4 us -> 64 us  [pair_backward(): pl.pallas_call(kernel, grid_spec=pltpu.PrefetchScalarGridSpec(num_scalar_...]
    unnamed x169 -> x167, local copies, waits for them, and re-layouts: 41.2 us -> 39.2 us
  transfers between devices with their start and end apart: 38 -> 38, of which waited for: 24 -> 22; matrix products, arithmetic and copies ran while one was open for 25% -> 27% of each run, Pallas kernels for 12% -> 15%
where the time goes in v12:
time: 699 us; the launch traced here: 688 us
  waiting for transfers between devices  234 us (33%)
  local copies, waits for them, and re-layouts  111 us (16%)
  Pallas kernels  101 us (14%)
  other arithmetic  87.7 us (13%)
  matrix products  61.1 us (9%)
  starting transfers between devices  54.4 us (8%)
  blocking collectives  24.2 us (3%)
  between operations  15.6 us (2%)
    ppermute x21, waiting for transfers between devices, swap(): return lax.ppermute(value, axis, [(0, 1), (1, 0)])  183 us
    pallas_call x2, Pallas kernels, pair_backward(): pl.pallas_call(kernel, grid_spec=pltpu.PrefetchScalarGridSpec(num_scalar_...  64 us
    dot_general x31, matrix products, mul(): return lax.dot_general(left, right, dims, preferred_element_type=WIDE)  60.1 us
    all_to_all x8, waiting for transfers between devices, exchange_rows(): return lax.all_to_all(value, 'rows', 0, 0, tiled=True)  49.2 us
    unnamed x167, local copies, waits for them, and re-layouts  39.2 us
    pallas_call x2, Pallas kernels, pair_forward(): pl.pallas_call(kernel, grid_spec=pltpu.PrefetchScalarGridSpec(num_scalar_...  37 us
    all_to_all x8, starting transfers between devices, exchange_rows(): return lax.all_to_all(value, 'rows', 0, 0, tiled=True)  33.1 us
    ppermute x21, starting transfers between devices, swap(): return lax.ppermute(value, axis, [(0, 1), (1, 0)])  20.7 us
  transfers between devices with their start and end apart: 38, of which 22 were waited for; matrix products, arithmetic and copies ran while one was open for 27% of the time, Pallas kernels for 15%

profile of v12, /device:TPU:0, one launch (start us, length us, event | category | flops | bytes accessed | tf_op | source)
XLA Modules:
  0.0 688.2 jit_solution(8005952566065240124)
XLA Ops:
  7.2 2.7 copy.97
  10.0 2.7 copy.98
  14.4 4.0 collective-permute-start
  19.9 7.8 %collective-permute-done = bf16[96,1024]{1,0:T(8,128)(2,1)S(1)} collective-permute-done((bf16[96,1024]{1,0:T(8,128)(2,1)}, bf16[96,1024]{1,0:T(8,128)(2,1)S(1)}, u32[]{:S(2)}, u32[]{:S(2)}) %collective-permute-start) | collective-permute-done | bytes 196640 | tf_op jit(solution)/shard_map/ppermute | solution.py:394
  40.9 17.1 %collective-permute-done.1 = bf16[160,1024]{1,0:T(8,128)(2,1)} collective-permute-done((bf16[160,1024]{1,0:T(8,128)(2,1)}, bf16[160,1024]{1,0:T(8,128)(2,1)}, u32[]{:S(2)}, u32[]{:S(2)}) %collective-permute-start.1) | collective-permute-done | bytes 327712 | tf_op jit(solution)/shard_map/ppermute | solution.py:394
  59.9 8.5 %collective-permute-done.2 = bf16[2,96,1024]{2,1,0:T(8,128)(2,1)S(1)} collective-permute-done((bf16[2,96,1024]{2,1,0:T(8,128)(2,1)S(1)}, bf16[2,96,1024]{2,1,0:T(8,128)(2,1)S(1)}, u32[]{:S(2)}, u32[]{:S(2)}) %collective-permute-start.2) | collective-permute-done | bytes 393248 | tf_op jit(solution)/shard_map/ppermute | solution.py:394
  72.8 2.8 constant_dynamic-update-slice_fusion.3
  75.5 3.3 convolution_convert_fusion.3
  78.8 2.9 convolution_convert_fusion.4
  83.0 4.3 all-to-all-start
  89.2 23.7 %all-to-all-done.q_ref.k_ref.v_ref = bf16[8,2,3,64,256]{4,3,2,1,0:T(8,128)(2,1)} async-done(((bf16[8,2,3,64,256]{4,3,2,1,0:T(8,128)(2,1)}), bf16[8,2,3,64,256]{4,3,2,1,0:T(8,128)(2,1)}, u32[]{:S(2)}, u32[]{:S(2)}) %all-to-all-start) | async-done | bytes 1572896 | tf_op jit(solution)/shard_map/all_to_all | solution.py:230
  122.4 19.0 %pair_forward.2 = (bf16[8,2,64,256]{3,2,1,0:T(8,128)(2,1)}, f32[8,2,64,256]{3,2,1,0:T(8,128)S(1)}, f32[8,2,1,256]{3,2,1,0:T(1,128)S(1)}) custom-call(s32[2]{0:T(128)S(1)} %broadcast_13_len_ref.2.len_ref, bf16[8,2,3,64,256]{4,3,2,1,0:T(8,128)(2,1)} %all-to-all-done.q_ref.k_ref.v_ref, bf16[8,2,3,64,256]{4,3,2,1,0:T(8,128)(2,1)} %all-to-all-done.q_ref.k_ref.v_ref, ...), custom_call_target="tpu_custom_call" | custom-call | flops 20132659200 | bytes 8388608 | tf_op jit(solution)/shard_map/pair_forward/pallas_call | solution.py:282
  142.4 4.0 all-to-all-start.1
  149.3 2.9 copy-done.23
  152.2 3.3 slice.169
  158.8 4.2 all-to-all-start.2
  163.2 3.6 fusion.76
  166.9 6.2 fusion.77
  173.3 11.7 %collective-permute-done.3 = bf16[512,512]{1,0:T(8,128)(2,1)S(1)} collective-permute-done((bf16[512,512]{1,0:T(8,128)(2,1)}, bf16[512,512]{1,0:T(8,128)(2,1)S(1)}, u32[]{:S(2)}, u32[]{:S(2)}) %collective-permute-start.3) | collective-permute-done | bytes 524320 | tf_op jit(solution)/shard_map/ppermute | solution.py:394
  189.6 4.2 all-to-all-start.3
  193.9 9.6 %all-to-all-done.3.q_ref = bf16[8,2,1,64,256]{4,3,2,1,0:T(8,128)(2,1)} async-done(((bf16[8,2,1,64,256]{4,3,2,1,0:T(8,128)(2,1)}), bf16[8,2,1,64,256]{4,3,2,1,0:T(8,128)(2,1)}, u32[]{:S(2)}, u32[]{:S(2)}) %all-to-all-start.3) | async-done | bytes 524320 | tf_op jit(solution)/shard_map/all_to_all | solution.py:230
  203.5 18.0 %pair_forward.3 = (bf16[8,2,64,256]{3,2,1,0:T(8,128)(2,1)S(1)}, f32[8,2,64,256]{3,2,1,0:T(8,128)S(1)}, f32[8,2,1,256]{3,2,1,0:T(1,128)S(1)}) custom-call(s32[2]{0:T(128)S(1)} %dynamic_slice.124.len_ref, bf16[8,2,1,64,256]{4,3,2,1,0:T(8,128)(2,1)} %all-to-all-done.3.q_ref, bf16[8,2,2,64,256]{4,3,2,1,0:T(8,128)(2,1)S(1)} %all-to-all-done.2.k_ref.v_ref, ...), custom_call_target="tpu_custom_call" | custom-call | flops 14092861440 | bytes 8388608 | tf_op jit(solution)/shard_map/pair_forward/pallas_call | solution.py:282
  221.6 12.3 %all_to_all.45 = bf16[8,2,64,256]{3,2,1,0:T(8,128)(2,1)S(1)} all-to-all(bf16[8,2,64,256]{3,2,1,0:T(8,128)(2,1)S(1)} %get-tuple-element.80), channel_id=1, replica_groups=mesh['far'=2,'near'=2,'rows'=8] {'rows'}, dimensions={0} | all-to-all | bytes 1048576 | tf_op jit(solution)/shard_map/all_to_all | solution.py:230
  236.4 11.2 %collective-permute-done.4 = bf16[512,512]{1,0:T(8,128)(2,1)S(1)} collective-permute-done((bf16[512,512]{1,0:T(8,128)(2,1)S(1)}, bf16[512,512]{1,0:T(8,128)(2,1)S(1)}, u32[]{:S(2)}, u32[]{:S(2)}) %collective-permute-start.4) | collective-permute-done | bytes 524320 | tf_op jit(solution)/shard_map/ppermute | solution.py:394
  250.7 2.8 slice.177
  259.8 5.1 multiply_convert_fusion
  264.9 3.4 fusion.22
  268.3 4.8 convolution_convert_fusion.1
  273.0 4.4 convolution_convert_fusion.2
  277.4 7.8 %pad_maximum_fusion = bf16[2,2048,1024]{2,1,0:T(8,128)(2,1)} fusion(bf16[2,1024,1024]{2,1,0:T(8,128)(2,1)} %bitcast.330, bf16[2,1024,1024]{2,1,0:T(8,128)(2,1)} %bitcast.331), kind=kLoop, calls=%fused_computation.3 | loop fusion | flops 16777216 | bytes 16777216 | tf_op jit(solution)/shard_map/concatenate | solution.py:578
  287.7 4.7 fusion.82
  293.4 15.6 %collective-permute-done.5 = bf16[512,1024]{1,0:T(8,128)(2,1)} collective-permute-done((bf16[512,1024]{1,0:T(8,128)(2,1)}, bf16[512,1024]{1,0:T(8,128)(2,1)}, u32[]{:S(2)}, u32[]{:S(2)}) %collective-permute-start.5) | collective-permute-done | bytes 1048608 | tf_op jit(solution)/shard_map/ppermute | solution.py:394
  316.0 3.9 all-to-all-start.5
  324.4 11.0 %all-to-all-done.5.g_ref = bf16[8,2,64,256]{3,2,1,0:T(8,128)(2,1)S(1)} async-done(((bf16[8,2,64,256]{3,2,1,0:T(8,128)(2,1)}), bf16[8,2,64,256]{3,2,1,0:T(8,128)(2,1)S(1)}, u32[]{:S(2)}, u32[]{:S(2)}) %all-to-all-start.5) | async-done | bytes 524320 | tf_op jit(solution)/shard_map/all_to_all | solution.py:230
  335.5 31.8 %pair_backward.2 = bf16[8,2,3,64,256]{4,3,2,1,0:T(8,128)(2,1)} custom-call(s32[2]{0:T(128)S(1)} %dynamic_slice.124.len_ref, bf16[8,2,1,64,256]{4,3,2,1,0:T(8,128)(2,1)} %all-to-all-done.3.q_ref, bf16[8,2,2,64,256]{4,3,2,1,0:T(8,128)(2,1)S(1)} %all-to-all-done.2.k_ref.v_ref, bf16[8,2,2,64,256]{4,3,2,1,0:T(8,128)(2,1)S(1)} %all-to-all-done.2.k_ref.v_ref, ...), custom_call_target="tpu_custom_call" | custom-call | flops 20132659200 | bytes 8388608 | tf_op jit(solution)/shard_map/pair_backward/pallas_call | solution.py:364
  369.4 4.4 all-to-all-start.6
  374.1 26.4 %collective-permute-done.8 = bf16[256,1024]{1,0:T(8,128)(2,1)} collective-permute-done((bf16[256,1024]{1,0:T(8,128)(2,1)S(1)}, bf16[256,1024]{1,0:T(8,128)(2,1)}, u32[]{:S(2)}, u32[]{:S(2)}) %collective-permute-start.8) | collective-permute-done | bytes 524320 | tf_op jit(solution)/shard_map/ppermute | solution.py:394
  417.7 2.6 convolution_convert_fusion.7
  420.4 5.5 collective-permute-done.9
  425.9 2.6 fusion.33
  429.9 4.4 fusion.73
  436.1 3.9 all-to-all-start.7
  442.0 2.9 convolution_convert_fusion.8
  444.9 4.8 all-to-all-done.7.g_ref
  449.7 32.2 %pair_backward.3 = bf16[8,2,3,64,256]{4,3,2,1,0:T(8,128)(2,1)} custom-call(s32[2]{0:T(128)S(1)} %broadcast_13_len_ref.2.len_ref, bf16[8,2,3,64,256]{4,3,2,1,0:T(8,128)(2,1)} %all-to-all-done.q_ref.k_ref.v_ref, bf16[8,2,3,64,256]{4,3,2,1,0:T(8,128)(2,1)} %all-to-all-done.q_ref.k_ref.v_ref, bf16[8,2,3,64,256]{4,3,2,1,0:T(8,128)(2,1)} %all-to-all-done.q_ref.k_ref.v_ref, ...), custom_call_target="tpu_custom_call" | custom-call | flops 30198988800 | bytes 8388608 | tf_op jit(solution)/shard_map/pair_backward/pallas_call | solution.py:364
  482.0 6.2 collective-permute-done.11
  488.1 2.7 pad_maximum_fusion.5
  490.9 4.3 all-to-all-start.8
  499.5 6.4 fusion.2
  505.8 12.4 %collective-permute-done.12 = bf16[256,768]{1,0:T(8,128)(2,1)S(1)} collective-permute-done((bf16[256,768]{1,0:T(8,128)(2,1)S(1)}, bf16[256,768]{1,0:T(8,128)(2,1)S(1)}, u32[]{:S(2)}, u32[]{:S(2)}) %collective-permute-start.12) | collective-permute-done | bytes 393248 | tf_op jit(solution)/shard_map/ppermute | solution.py:394
  519.1 6.7 slice_convert_fusion
  525.8 3.0 copy.115
  535.6 4.2 fusion.10
  543.3 11.6 %collective-permute-done.20 = bf16[128,1024]{1,0:T(8,128)(2,1)S(1)} collective-permute-done((bf16[128,1024]{1,0:T(8,128)(2,1)S(1)}, bf16[128,1024]{1,0:T(8,128)(2,1)S(1)}, u32[]{:S(2)}, u32[]{:S(2)}) %collective-permute-start.20) | collective-permute-done | bytes 262176 | tf_op jit(solution)/shard_map/ppermute | solution.py:394
  564.2 24.8 %collective-permute-done.14 = bf16[256,1024]{1,0:T(8,128)(2,1)S(1)} collective-permute-done((bf16[256,1024]{1,0:T(8,128)(2,1)S(1)}, bf16[256,1024]{1,0:T(8,128)(2,1)S(1)}, u32[]{:S(2)}, u32[]{:S(2)}) %collective-permute-start.14) | collective-permute-done | bytes 524320 | tf_op jit(solution)/shard_map/ppermute | solution.py:394
  595.5 3.1 copy.114
  598.7 22.6 %collective-permute-done.15 = bf16[160,1024]{1,0:T(8,128)(2,1)S(1)} collective-permute-done((bf16[160,1024]{1,0:T(8,128)(2,1)S(1)}, bf16[160,1024]{1,0:T(8,128)(2,1)S(1)}, u32[]{:S(2)}, u32[]{:S(2)}) %collective-permute-start.15) | collective-permute-done | bytes 327712 | tf_op jit(solution)/shard_map/ppermute | solution.py:394
  623.8 3.3 reverse_select_fusion.3
  628.1 3.3 collective-permute-start.17
  633.3 5.3 copy.127
  639.0 11.9 %all-gather.2 = bf16[16,80,256]{2,1,0:T(8,128)(2,1)S(1)} all-gather(bf16[2,80,256]{2,1,0:T(8,128)(2,1)S(1)} %pad_maximum_fusion.21), channel_id=4, replica_groups=mesh['far'=2,'near'=2,'rows'=8] {'rows'}, dimensions={0}, use_global_device_ids=true | all-gather | bytes 737280 | tf_op jit(solution)/shard_map/all_gather | solution.py:666
  656.6 2.9 copy.125
  668.0 2.6 fusion.14
  675.4 3.7 copy.123
  (377 shorter events, 156.9 us)
Async XLA Ops:
  7.2 227.9 %copy-start = (bf16[4,256,1024]{2,1,0:T(8,128)(2,1)S(1)}, bf16[4,256,1024]{2,1,0:T(8,128)(2,1)}, u32[]{:S(2)}) copy-start(bf16[4,256,1024]{2,1,0:T(8,128)(2,1)} %param.31) | copy-start | bytes 6291460
  7.2 65.6 %all-gather.10.cloned.1.call-start = ((), (), s32[]{:S(2)}) async-start(), calls=%async_computation.12 | async-start | bytes 1769472 | tf_op jit(solution)/shard_map/all_gather | solution.py:444
  10.0 8.4 %copy-start.63 = (s32[4,256]{1,0:T(4,128)S(1)}, s32[4,256]{1,0:T(4,128)}, u32[]{:S(2)}) copy-start(s32[4,256]{1,0:T(4,128)} %param.17) | copy-start | bytes 12292
  12.7 18.1 %copy-start.59 = (bf16[32,2,1024]{2,1,0:T(2,128)(2,1)S(1)}, bf16[32,2,1024]{2,1,0:T(2,128)(2,1)}, u32[]{:S(2)}) copy-start(bf16[32,2,1024]{2,1,0:T(2,128)(2,1)} %param.20) | copy-start | bytes 393220
  12.7 20.0 %copy-start.47 = (bf16[2,1024,256]{2,1,0:T(8,128)(2,1)S(1)}, bf16[2,1024,256]{2,1,0:T(8,128)(2,1)}, u32[]{:S(2)}) copy-start(bf16[2,1024,256]{2,1,0:T(8,128)(2,1)} %param.25) | copy-start | bytes 3145732
  14.4 13.4 %collective-permute-start = (bf16[96,1024]{1,0:T(8,128)(2,1)}, bf16[96,1024]{1,0:T(8,128)(2,1)S(1)}, u32[]{:S(2)}, u32[]{:S(2)}) collective-permute-start(bf16[96,1024]{1,0:T(8,128)(2,1)} %constant_dynamic-slice_fusion.20), channel_id=1, source_target_pairs={{0,16},{16,0},{1,17},{17,1},{2,18},{18,2},{3,19},{19,3},{4,20},{20... | collective-permute-start | bytes 589832 | tf_op jit(solution)/shard_map/ppermute | solution.py:394
  19.9 11.5 %copy-start.60 = (f32[2,256]{1,0:T(2,128)}, f32[2,256]{1,0:T(2,128)S(1)}, u32[]{:S(2)}) copy-start(f32[2,256]{1,0:T(2,128)S(1)} %get-tuple-element.219) | copy-start | bytes 6148
  28.4 118.0 %all-gather.18.cloned.1.call-start = ((), (), s32[]{:S(2)}) async-start(), calls=%async_computation.19 | async-start | bytes 8257536 | tf_op jit(solution)/shard_map/all_gather | solution.py:522
  40.8 17.1 %collective-permute-start.1 = (bf16[160,1024]{1,0:T(8,128)(2,1)}, bf16[160,1024]{1,0:T(8,128)(2,1)}, u32[]{:S(2)}, u32[]{:S(2)}) collective-permute-start(bf16[160,1024]{1,0:T(8,128)(2,1)} %pad_maximum_fusion.19), channel_id=1, source_target_pairs={{0,16},{16,0},{1,17},{17,1},{2,18},{18,2},{3,19},{19,3},{4,20},{20... | collective-permute-start | bytes 983048 | tf_op jit(solution)/shard_map/ppermute | solution.py:394
  58.9 9.4 %collective-permute-start.2 = (bf16[2,96,1024]{2,1,0:T(8,128)(2,1)S(1)}, bf16[2,96,1024]{2,1,0:T(8,128)(2,1)S(1)}, u32[]{:S(2)}, u32[]{:S(2)}) collective-permute-start(bf16[2,96,1024]{2,1,0:T(8,128)(2,1)S(1)} %fusion.60), channel_id=1, source_target_pairs={{0,8},{8,0},{1,9},{9,1},{2,10},{10,2},{3,11},{11,3},{4,12},{12,4},... | collective-permute-start | bytes 1179656 | tf_op jit(solution)/shard_map/ppermute | solution.py:394
  83.0 29.9 %all-to-all-start = ((bf16[8,2,3,64,256]{4,3,2,1,0:T(8,128)(2,1)}), bf16[8,2,3,64,256]{4,3,2,1,0:T(8,128)(2,1)}, u32[]{:S(2)}, u32[]{:S(2)}) async-start(bf16[8,2,3,64,256]{4,3,2,1,0:T(8,128)(2,1)} %pad_maximum_fusion.7), calls=%async_computation | async-start | bytes 3145728 | tf_op jit(solution)/shard_map/all_to_all | solution.py:230
  87.3 27.4 %copy-start.65 = (bf16[1024]{0:T(1024)(128)(2,1)S(1)}, bf16[1024]{0:T(1024)(128)(2,1)}, u32[]{:S(2)}) copy-start(bf16[1024]{0:T(1024)(128)(2,1)} %param.23) | copy-start | bytes 6148
  87.3 163.3 %all-gather.20.cloned.1.call-start = ((), (), s32[]{:S(2)}) async-start(), calls=%async_computation.20 | async-start | bytes 8912896 | tf_op jit(solution)/shard_map/all_gather | solution.py:536
  142.4 14.9 %all-to-all-start.1 = ((bf16[8,2,64,256]{3,2,1,0:T(8,128)(2,1)}), bf16[8,2,64,256]{3,2,1,0:T(8,128)(2,1)S(1)}, u32[]{:S(2)}, u32[]{:S(2)}) async-start(bf16[8,2,64,256]{3,2,1,0:T(8,128)(2,1)} %get-tuple-element.75), calls=%async_computation.1 | async-start | bytes 1048576 | tf_op jit(solution)/shard_map/all_to_all | solution.py:230
  148.6 6.9 %copy-start.17 = (bf16[1024,1024]{1,0:T(8,128)(2,1)}, bf16[1024,1024]{1,0:T(8,128)(2,1)S(1)}, u32[]{:S(2)}) copy-start(bf16[1024,1024]{1,0:T(8,128)(2,1)S(1)} %constant_dynamic-update-slice_fusion.1) | copy-start | bytes 6291460
  158.8 30.8 %all-to-all-start.2 = ((bf16[8,2,2,64,256]{4,3,2,1,0:T(8,128)(2,1)}), bf16[8,2,2,64,256]{4,3,2,1,0:T(8,128)(2,1)S(1)}, u32[]{:S(2)}, u32[]{:S(2)}) async-start(bf16[8,2,2,64,256]{4,3,2,1,0:T(8,128)(2,1)} %pad_maximum_fusion.11), calls=%async_computation.2 | async-start | bytes 2097152 | tf_op jit(solution)/shard_map/all_to_all | solution.py:230
  162.9 22.0 %collective-permute-start.3 = (bf16[512,512]{1,0:T(8,128)(2,1)}, bf16[512,512]{1,0:T(8,128)(2,1)S(1)}, u32[]{:S(2)}, u32[]{:S(2)}) collective-permute-start(bf16[512,512]{1,0:T(8,128)(2,1)} %bitcast.336), channel_id=1, source_target_pairs={{0,8},{8,0},{1,9},{9,1},{2,10},{10,2},{3,11},{11,3},{4,12},{12,4},... | collective-permute-start | bytes 1572872 | tf_op jit(solution)/shard_map/ppermute | solution.py:394
  173.1 11.9 %copy-start.30 = (bf16[2,256,1024]{2,1,0:T(8,128)(2,1)S(1)}, bf16[2,256,1024]{2,1,0:T(8,128)(2,1)}, u32[]{:S(2)}) copy-start(bf16[2,256,1024]{2,1,0:T(8,128)(2,1)} %get-tuple-element.211) | copy-start | bytes 3145732
  173.1 11.9 %copy-start.35 = (bf16[64,8,2,256]{3,1,2,0:T(8,128)(2,1)S(1)}, bf16[64,8,2,256]{3,1,2,0:T(8,128)(2,1)}, u32[]{:S(2)}) copy-start(bf16[64,8,2,256]{3,1,2,0:T(8,128)(2,1)} %copy.137) | copy-start | bytes 1572868
  189.6 13.9 %all-to-all-start.3 = ((bf16[8,2,1,64,256]{4,3,2,1,0:T(8,128)(2,1)}), bf16[8,2,1,64,256]{4,3,2,1,0:T(8,128)(2,1)}, u32[]{:S(2)}, u32[]{:S(2)}) async-start(bf16[8,2,1,64,256]{4,3,2,1,0:T(8,128)(2,1)} %pad_maximum_fusion.17), calls=%async_computation.3 | async-start | bytes 1048576 | tf_op jit(solution)/shard_map/all_to_all | solution.py:230
  193.8 175.6 %reduce-scatter.4.cloned.1.call-start = ((), (), s32[]{:S(2)}) async-start(), calls=%async_computation.13 | async-start | bytes 9437184 | tf_op jit(solution)/shard_map/reduce_scatter | solution.py:567
  221.5 14.6 %copy-start.2 = (f32[8,2,64,256]{3,2,1,0:T(8,128)}, f32[8,2,64,256]{3,2,1,0:T(8,128)S(1)}, u32[]{:S(2)}) copy-start(f32[8,2,64,256]{3,2,1,0:T(8,128)S(1)} %get-tuple-element.88.wide_ref) | copy-start | bytes 3145732
  221.6 13.5 %copy-start.66 = (bf16[1024]{0:T(1024)(128)(2,1)S(1)}, bf16[1024]{0:T(1024)(128)(2,1)}, u32[]{:S(2)}) copy-start(bf16[1024]{0:T(1024)(128)(2,1)} %param.28) | copy-start | bytes 6148
  234.5 13.1 %copy-start.55 = (bf16[64,8,2,256]{3,1,2,0:T(8,128)(2,1)}, bf16[64,8,2,256]{3,1,2,0:T(8,128)(2,1)S(1)}, u32[]{:S(2)}) copy-start(bf16[64,8,2,256]{3,1,2,0:T(8,128)(2,1)S(1)} %copy.138) | copy-start | bytes 1572868
  234.5 13.1 %collective-permute-start.4 = (bf16[512,512]{1,0:T(8,128)(2,1)S(1)}, bf16[512,512]{1,0:T(8,128)(2,1)S(1)}, u32[]{:S(2)}, u32[]{:S(2)}) collective-permute-start(bf16[512,512]{1,0:T(8,128)(2,1)S(1)} %bitcast.368), channel_id=1, source_target_pairs={{0,8},{8,0},{1,9},{9,1},{2,10},{10,2},{3,11},{11,3},{4,12},{12,4},... | collective-permute-start | bytes 1572872 | tf_op jit(solution)/shard_map/ppermute | solution.py:394
  236.1 11.5 %copy-start.7 = (f32[512,1024]{1,0:T(8,128)S(1)}, f32[512,1024]{1,0:T(8,128)}, u32[]{:S(2)}) copy-start(f32[512,1024]{1,0:T(8,128)} %copy-done.6) | copy-start | bytes 6291460
  264.9 8.1 %copy-start.70 = (bf16[512,2048]{1,0:T(8,128)(2,1)}, bf16[512,2048]{1,0:T(8,128)(2,1)S(1)}, u32[]{:S(2)}) copy-start(bf16[512,2048]{1,0:T(8,128)(2,1)S(1)} %get-tuple-element.83) | copy-start | bytes 6291460
  285.3 23.7 %collective-permute-start.5 = (bf16[512,1024]{1,0:T(8,128)(2,1)}, bf16[512,1024]{1,0:T(8,128)(2,1)}, u32[]{:S(2)}, u32[]{:S(2)}) collective-permute-start(bf16[512,1024]{1,0:T(8,128)(2,1)} %fusion.22), channel_id=1, source_target_pairs={{0,8},{8,0},{1,9},{9,1},{2,10},{10,2},{3,11},{11,3},{4,12},{12,4},... | collective-permute-start | bytes 3145736 | tf_op jit(solution)/shard_map/ppermute | solution.py:394
  287.7 21.2 %copy-start.50 = (bf16[512,1024]{1,0:T(8,128)(2,1)S(1)}, bf16[512,1024]{1,0:T(8,128)(2,1)}, u32[]{:S(2)}) copy-start(bf16[512,1024]{1,0:T(8,128)(2,1)} %fusion.22) | copy-start | bytes 3145732
  292.4 18.1 %copy-start.39 = (f32[2,2,128,1024]{3,2,1,0:T(8,128)}, f32[2,2,128,1024]{3,2,1,0:T(8,128)S(1)}, u32[]{:S(2)}) copy-start(f32[2,2,128,1024]{3,2,1,0:T(8,128)S(1)} %fusion.82) | copy-start | bytes 6291460
  310.6 11.5 %collective-permute-start.6 = (bf16[256,1024]{1,0:T(8,128)(2,1)}, bf16[256,1024]{1,0:T(8,128)(2,1)}, u32[]{:S(2)}, u32[]{:S(2)}) collective-permute-start(bf16[256,1024]{1,0:T(8,128)(2,1)} %bitcast.39), channel_id=1, source_target_pairs={{0,8},{8,0},{1,9},{9,1},{2,10},{10,2},{3,11},{11,3},{4,12},{12,4},... | collective-permute-start | bytes 1572872 | tf_op jit(solution)/shard_map/ppermute | solution.py:394
  316.0 19.5 %all-to-all-start.5 = ((bf16[8,2,64,256]{3,2,1,0:T(8,128)(2,1)}), bf16[8,2,64,256]{3,2,1,0:T(8,128)(2,1)S(1)}, u32[]{:S(2)}, u32[]{:S(2)}) async-start(bf16[8,2,64,256]{3,2,1,0:T(8,128)(2,1)} %maximum_bitcast_fusion), calls=%async_computation.5 | async-start | bytes 1048576 | tf_op jit(solution)/shard_map/all_to_all | solution.py:230
  321.9 13.6 %copy-start.3 = (f32[8,2,64,256]{3,2,1,0:T(8,128)S(1)}, f32[8,2,64,256]{3,2,1,0:T(8,128)}, u32[]{:S(2)}) copy-start(f32[8,2,64,256]{3,2,1,0:T(8,128)} %copy-done.2) | copy-start | bytes 3145732
  335.5 31.8 %collective-permute-start.7 = (bf16[256,1024]{1,0:T(8,128)(2,1)}, bf16[256,1024]{1,0:T(8,128)(2,1)S(1)}, u32[]{:S(2)}, u32[]{:S(2)}) collective-permute-start(bf16[256,1024]{1,0:T(8,128)(2,1)} %fusion.44), channel_id=1, source_target_pairs={{0,16},{16,0},{1,17},{17,1},{2,18},{18,2},{3,19},{19,3},{4,20},{20... | collective-permute-start | bytes 1572872 | tf_op jit(solution)/shard_map/ppermute | solution.py:394
  369.4 31.0 %all-to-all-start.6 = ((bf16[8,2,3,64,256]{4,3,2,1,0:T(8,128)(2,1)}), bf16[8,2,3,64,256]{4,3,2,1,0:T(8,128)(2,1)}, u32[]{:S(2)}, u32[]{:S(2)}) async-start(bf16[8,2,3,64,256]{4,3,2,1,0:T(8,128)(2,1)} %pair_backward.2), calls=%async_computation.7 | async-start | bytes 3145728 | tf_op jit(solution)/shard_map/all_to_all | solution.py:230
  373.9 28.7 %copy-start.21 = (bf16[1,4,8,32,1024]{4,3,0,1,2:T(8,128)(2,1)S(1)}, bf16[1,4,8,32,1024]{4,3,0,1,2:T(8,128)(2,1)}, u32[]{:S(2)}) copy-start(bf16[1,4,8,32,1024]{4,3,0,1,2:T(8,128)(2,1)} %get-tuple-element.199) | copy-start | bytes 6291460
  373.9 145.2 %all-gather.12.cloned.1.call-start = ((), (), s32[]{:S(2)}) async-start(), calls=%async_computation.14 | async-start | bytes 4718592 | tf_op jit(solution)/shard_map/all_gather | solution.py:444
  374.0 26.5 %collective-permute-start.8 = (bf16[256,1024]{1,0:T(8,128)(2,1)S(1)}, bf16[256,1024]{1,0:T(8,128)(2,1)}, u32[]{:S(2)}, u32[]{:S(2)}) collective-permute-start(bf16[256,1024]{1,0:T(8,128)(2,1)S(1)} %dynamic-slice_bitcast_fusion), channel_id=1, source_target_pairs={{0,16},{16,0},{1,17},{17,1},{2,18},{18,2},{3,19},{19,3},{4,20},{20... | collective-permute-start | bytes 1572872 | tf_op jit(solution)/shard_map/ppermute | solution.py:394
  402.5 123.3 %reduce-scatter.6.cloned.1.call-start = ((), (), s32[]{:S(2)}) async-start(), calls=%async_computation.15 | async-start | bytes 4718592 | tf_op jit(solution)/shard_map/reduce_scatter | solution.py:567
  412.3 13.6 %collective-permute-start.9 = (bf16[512,512]{1,0:T(8,128)(2,1)}, bf16[512,512]{1,0:T(8,128)(2,1)}, u32[]{:S(2)}, u32[]{:S(2)}) collective-permute-start(bf16[512,512]{1,0:T(8,128)(2,1)} %bitcast.163), channel_id=1, source_target_pairs={{0,8},{8,0},{1,9},{9,1},{2,10},{10,2},{3,11},{11,3},{4,12},{12,4},... | collective-permute-start | bytes 1572872 | tf_op jit(solution)/shard_map/ppermute | solution.py:394
  417.7 8.2 %copy-start.14 = (bf16[1,4,8,32,1024]{4,3,2,1,0:T(8,128)(2,1)S(1)}, bf16[1,4,8,32,1024]{4,3,2,1,0:T(8,128)(2,1)}, u32[]{:S(2)}) copy-start(bf16[1,4,8,32,1024]{4,3,2,1,0:T(8,128)(2,1)} %copy.112) | copy-start | bytes 6291460
  434.8 7.2 %copy-start.36 = (bf16[64,8,2,256]{3,1,2,0:T(8,128)(2,1)S(1)}, bf16[64,8,2,256]{3,1,2,0:T(8,128)(2,1)}, u32[]{:S(2)}) copy-start(bf16[64,8,2,256]{3,1,2,0:T(8,128)(2,1)} %copy.137) | copy-start | bytes 1572868
  436.1 13.6 %copy-start.5 = (f32[8,2,64,256]{3,2,1,0:T(8,128)S(1)}, f32[8,2,64,256]{3,2,1,0:T(8,128)}, u32[]{:S(2)}) copy-start(f32[8,2,64,256]{3,2,1,0:T(8,128)} %copy-done.4) | copy-start | bytes 3145732
  436.1 13.6 %all-to-all-start.7 = ((bf16[8,2,64,256]{3,2,1,0:T(8,128)(2,1)}), bf16[8,2,64,256]{3,2,1,0:T(8,128)(2,1)S(1)}, u32[]{:S(2)}, u32[]{:S(2)}) async-start(bf16[8,2,64,256]{3,2,1,0:T(8,128)(2,1)} %maximum_bitcast_fusion.1), calls=%async_computation.8 | async-start | bytes 1048576 | tf_op jit(solution)/shard_map/all_to_all | solution.py:230
  440.0 50.9 %collective-permute-start.10 = (bf16[512,1024]{1,0:T(8,128)(2,1)S(1)}, bf16[512,1024]{1,0:T(8,128)(2,1)}, u32[]{:S(2)}, u32[]{:S(2)}) collective-permute-start(bf16[512,1024]{1,0:T(8,128)(2,1)S(1)} %convolution_convert_fusion.7), channel_id=1, source_target_pairs={{0,8},{8,0},{1,9},{9,1},{2,10},{10,2},{3,11},{11,3},{4,12},{12,4},... | collective-permute-start | bytes 3145736 | tf_op jit(solution)/shard_map/ppermute | solution.py:394
  440.2 47.9 %collective-permute-start.11 = (bf16[2,256,1024]{2,1,0:T(8,128)(2,1)}, bf16[2,256,1024]{2,1,0:T(8,128)(2,1)}, u32[]{:S(2)}, u32[]{:S(2)}) collective-permute-start(bf16[2,256,1024]{2,1,0:T(8,128)(2,1)} %pad_maximum_fusion.12), channel_id=1, source_target_pairs={{0,8},{8,0},{1,9},{9,1},{2,10},{10,2},{3,11},{11,3},{4,12},{12,4},... | collective-permute-start | bytes 3145736 | tf_op jit(solution)/shard_map/ppermute | solution.py:394
  449.7 38.4 %copy-start.32 = (bf16[2,256,1024]{2,1,0:T(8,128)(2,1)S(1)}, bf16[2,256,1024]{2,1,0:T(8,128)(2,1)}, u32[]{:S(2)}) copy-start(bf16[2,256,1024]{2,1,0:T(8,128)(2,1)} %pad_maximum_fusion.12) | copy-start | bytes 3145732
  490.9 34.9 %all-to-all-start.8 = ((bf16[8,2,3,64,256]{4,3,2,1,0:T(8,128)(2,1)}), bf16[8,2,3,64,256]{4,3,2,1,0:T(8,128)(2,1)}, u32[]{:S(2)}, u32[]{:S(2)}) async-start(bf16[8,2,3,64,256]{4,3,2,1,0:T(8,128)(2,1)} %pair_backward.3), calls=%async_computation.9 | async-start | bytes 3145728 | tf_op jit(solution)/shard_map/all_to_all | solution.py:230
  495.2 95.1 %reduce-scatter.8.cloned.1.call-start = ((), (), s32[]{:S(2)}) async-start(), calls=%async_computation.16 | async-start | bytes 5898240 | tf_op jit(solution)/shard_map/reduce_scatter | solution.py:567
  497.7 20.5 %collective-permute-start.12 = (bf16[256,768]{1,0:T(8,128)(2,1)S(1)}, bf16[256,768]{1,0:T(8,128)(2,1)S(1)}, u32[]{:S(2)}, u32[]{:S(2)}) collective-permute-start(bf16[256,768]{1,0:T(8,128)(2,1)S(1)} %convolution_convert_fusion.15), channel_id=1, source_target_pairs={{0,16},{16,0},{1,17},{17,1},{2,18},{18,2},{3,19},{19,3},{4,20},{20... | collective-permute-start | bytes 1179656 | tf_op jit(solution)/shard_map/ppermute | solution.py:394
  533.9 117.1 %all-gather.16.cloned.1.call-start = ((), (), s32[]{:S(2)}) async-start(), calls=%async_computation.18 | async-start | bytes 2359296 | tf_op jit(solution)/shard_map/all_gather | solution.py:444
  539.7 16.2 %copy-start.37 = (f32[2,2,128,1024]{3,2,1,0:T(8,128)}, f32[2,2,128,1024]{3,2,1,0:T(8,128)S(1)}, u32[]{:S(2)}) copy-start(f32[2,2,128,1024]{3,2,1,0:T(8,128)S(1)} %fusion.10) | copy-start | bytes 6291460
  540.7 14.1 %collective-permute-start.20 = (bf16[128,1024]{1,0:T(8,128)(2,1)S(1)}, bf16[128,1024]{1,0:T(8,128)(2,1)S(1)}, u32[]{:S(2)}, u32[]{:S(2)}) collective-permute-start(bf16[128,1024]{1,0:T(8,128)(2,1)S(1)} %dynamic-slice_bitcast_fusion.2), channel_id=1, source_target_pairs={{0,16},{16,0},{1,17},{17,1},{2,18},{18,2},{3,19},{19,3},{4,20},{20... | collective-permute-start | bytes 786440 | tf_op jit(solution)/shard_map/ppermute | solution.py:394
  540.8 20.3 %collective-permute-start.13 = (bf16[256,1024]{1,0:T(8,128)(2,1)}, bf16[256,1024]{1,0:T(8,128)(2,1)}, u32[]{:S(2)}, u32[]{:S(2)}) collective-permute-start(bf16[256,1024]{1,0:T(8,128)(2,1)} %bitcast.85), channel_id=1, source_target_pairs={{0,8},{8,0},{1,9},{9,1},{2,10},{10,2},{3,11},{11,3},{4,12},{12,4},... | collective-permute-start | bytes 1572872 | tf_op jit(solution)/shard_map/ppermute | solution.py:394
  555.7 115.0 %all-gather.14.cloned.1.call-start = ((), (), s32[]{:S(2)}) async-start(), calls=%async_computation.17 | async-start | bytes 2949120 | tf_op jit(solution)/shard_map/all_gather | solution.py:444
  564.1 27.7 %copy-start.64 = (s32[4,256]{1,0:T(4,128)S(1)}, s32[4,256]{1,0:T(4,128)}, u32[]{:S(2)}) copy-start(s32[4,256]{1,0:T(4,128)} %param.17) | copy-start | bytes 12292
  564.1 24.8 %collective-permute-start.14 = (bf16[256,1024]{1,0:T(8,128)(2,1)S(1)}, bf16[256,1024]{1,0:T(8,128)(2,1)S(1)}, u32[]{:S(2)}, u32[]{:S(2)}) collective-permute-start(bf16[256,1024]{1,0:T(8,128)(2,1)S(1)} %fusion.42), channel_id=1, source_target_pairs={{0,16},{16,0},{1,17},{17,1},{2,18},{18,2},{3,19},{19,3},{4,20},{20... | collective-permute-start | bytes 1572872 | tf_op jit(solution)/shard_map/ppermute | solution.py:394
  590.3 31.9 %collective-permute-start.16 = (bf16[2,256,1024]{2,1,0:T(8,128)(2,1)S(1)}, bf16[2,256,1024]{2,1,0:T(8,128)(2,1)S(1)}, u32[]{:S(2)}, u32[]{:S(2)}) collective-permute-start(bf16[2,256,1024]{2,1,0:T(8,128)(2,1)S(1)} %pad_maximum_fusion.13), channel_id=1, source_target_pairs={{0,8},{8,0},{1,9},{9,1},{2,10},{10,2},{3,11},{11,3},{4,12},{12,4},... | collective-permute-start | bytes 3145736 | tf_op jit(solution)/shard_map/ppermute | solution.py:394
  592.9 28.3 %collective-permute-start.15 = (bf16[160,1024]{1,0:T(8,128)(2,1)S(1)}, bf16[160,1024]{1,0:T(8,128)(2,1)S(1)}, u32[]{:S(2)}, u32[]{:S(2)}) collective-permute-start(bf16[160,1024]{1,0:T(8,128)(2,1)S(1)} %dynamic-slice_bitcast_fusion.1), channel_id=1, source_target_pairs={{0,16},{16,0},{1,17},{17,1},{2,18},{18,2},{3,19},{19,3},{4,20},{20... | collective-permute-start | bytes 983048 | tf_op jit(solution)/shard_map/ppermute | solution.py:394
  595.5 25.7 %copy-start.53 = (bf16[2,160,1024]{2,1,0:T(8,128)(2,1)S(1)}, bf16[2,160,1024]{2,1,0:T(8,128)(2,1)}, u32[]{:S(2)}) copy-start(bf16[2,160,1024]{2,1,0:T(8,128)(2,1)} %reduce-scatter.8.cloned.1.call-done) | copy-start | bytes 1966084
  628.1 10.5 %collective-permute-start.17 = (bf16[64,1024]{1,0:T(8,128)(2,1)S(1)}, bf16[64,1024]{1,0:T(8,128)(2,1)S(1)}, u32[]{:S(2)}, u32[]{:S(2)}) collective-permute-start(bf16[64,1024]{1,0:T(8,128)(2,1)S(1)} %pad_maximum_fusion.20), channel_id=1, source_target_pairs={{0,8},{8,0},{1,9},{9,1},{2,10},{10,2},{3,11},{11,3},{4,12},{12,4},... | collective-permute-start | bytes 393224 | tf_op jit(solution)/shard_map/ppermute | solution.py:394
  638.8 20.6 %collective-permute-start.18 = (bf16[2,256,768]{2,1,0:T(8,128)(2,1)}, bf16[2,256,768]{2,1,0:T(8,128)(2,1)}, u32[]{:S(2)}, u32[]{:S(2)}) collective-permute-start(bf16[2,256,768]{2,1,0:T(8,128)(2,1)} %pad_maximum_fusion.16), channel_id=1, source_target_pairs={{0,8},{8,0},{1,9},{9,1},{2,10},{10,2},{3,11},{11,3},{4,12},{12,4},... | collective-permute-start | bytes 2359304 | tf_op jit(solution)/shard_map/ppermute | solution.py:394
  661.0 5.0 collective-permute-start.19
  675.4 5.8 copy-start.1
  (50 other events, 121.1 us)
Sparse Core Ops, SparseCore 0:
  28.5 26.8 all-gather.9
  69.5 59.3 all-gather.17
  131.9 81.9 all-gather.19
  285.4 73.8 reduce-scatter.3
  402.6 35.6 all-gather.11
  442.5 51.3 reduce-scatter.5
  534.0 56.2 reduce-scatter.7
  593.0 27.8 all-gather.15
  623.9 31.2 all-gather.13

commit v13 on v12

--- a/solution.py
+++ b/solution.py
@@ -632,9 +632,8 @@
     last_terms = jnp.pad(
         jnp.concatenate([output_terms, patch_terms], axis=1), ((0, 0), (3 * cols, 0), (0, 0))
     )
-    hidden_gradients = [hidden_total[hidden:].T.astype(WIDE), hidden_total[:hidden].astype(WIDE)]
-    grads, patch_two, last_terms, hidden_gradients, middle_part = tie(
-        exchange_rows(grads), patch_two, last_terms, hidden_gradients, middle_part
+    grads, patch_two, last_terms, hidden_total, middle_part = tie(
+        exchange_rows(grads), patch_two, last_terms, hidden_total, middle_part
     )
     grad_qkv_t = from_pairs(grads)
     last_terms = lax.dynamic_update_slice_in_dim(last_terms, by_shard(grad_qkv_t, normed_one), 0, 1)
@@ -650,9 +649,6 @@
     input_half = self_half + normed_back(grad_one * gain_half, unit_half, rate_half)
     input_half = input_half.astype(LOW)
     input_two = jnp.stack([input_half, swap(input_half, "far")])
-    last_part, input_two, patch_two = tie(last_part, input_two, patch_two)
-    input_four = jnp.stack([input_two, swap(input_two, "near")])
-    patch_four = jnp.stack([patch_two, swap(patch_two, "near")])
     onehot_half = halves(onehot)[0].astype(WIDE)
     table_term = jnp.concatenate(
         [
@@ -665,13 +661,19 @@
     small = jnp.stack(both_columns(jnp.concatenate(small, axis=0).astype(LOW)))
     small = jnp.sum(lax.all_gather(small, "rows", axis=0).astype(WIDE), axis=0).astype(LOW)
     small_own, small_away = own_and_away(small)
-    small_away, patch_four = tie(small_away, patch_four)
     small = small_own.astype(WIDE) + swap(small_away, "far").astype(WIDE)
+    last_part, input_two, patch_two, small = tie(last_part, input_two, patch_two, small)
+    input_four = jnp.stack([input_two, swap(input_two, "near")])
+    patch_four = jnp.stack([patch_two, swap(patch_two, "near")])
+    outputs = over_heads(result_four)
+    hidden_gradients = [hidden_total[hidden:].T.astype(WIDE), hidden_total[:hidden].astype(WIDE)]
     last_own, last_away = own_and_away(last_part)
-    last_sum, input_four = tie(add_far(last_own, swap(last_away, "far")), input_four)
+    last_sum, input_four, outputs, hidden_gradients = tie(
+        add_far(last_own, swap(last_away, "far")), input_four, outputs, hidden_gradients
+    )
     last_total = join_rows(last_sum)
-    input_grads = over_heads(input_four)
-    outputs, patch_grads = over_heads(result_four), over_heads(patch_four)
+    middle_total, patch_four = tie(middle_total, patch_four)
+    input_grads, patch_grads = over_heads(input_four), over_heads(patch_four)
 
     cross_output_total, query_total = middle_total[:cols], middle_total[cols : 2 * cols]
     pair_total = middle_total[2 * cols :].reshape(heads, 2, HEAD_DIM, width)

time: 699 us -> 703 us (level)
  Pallas kernels: 101 us -> 88.9 us
    ppermute x21, waiting for transfers between devices: 183 us -> 166 us  [swap(): return lax.ppermute(value, axis, [(0, 1), (1, 0)])]
    all_to_all x8, waiting for transfers between devices: 49.2 us -> 62.9 us  [exchange_rows(): return lax.all_to_all(value, 'rows', 0, 0, tiled=True)]
    pallas_call x2, Pallas kernels: 64 us -> 55 us  [pair_backward(): pl.pallas_call(kernel, grid_spec=pltpu.PrefetchScalarGridSpec(num_scalar_...]
    unnamed x167 -> x185, local copies, waits for them, and re-layouts: 39.2 us -> 46.2 us
  transfers between devices with their start and end apart: 38 -> 38, of which waited for: 22 -> 23; matrix products, arithmetic and copies ran while one was open for 27% -> 27% of each run, Pallas kernels for 15% -> 13%
where the time goes in v13:
time: 703 us; the launch traced here: 689 us
  waiting for transfers between devices  229 us (33%)
  local copies, waits for them, and re-layouts  118 us (17%)
  Pallas kernels  88.9 us (13%)
  other arithmetic  87.1 us (12%)
  matrix products  62.9 us (9%)
  starting transfers between devices  59.9 us (9%)
  blocking collectives  27.1 us (4%)
  between operations  15.6 us (2%)
    ppermute x21, waiting for transfers between devices, swap(): return lax.ppermute(value, axis, [(0, 1), (1, 0)])  166 us
    all_to_all x8, waiting for transfers between devices, exchange_rows(): return lax.all_to_all(value, 'rows', 0, 0, tiled=True)  62.9 us
    dot_general x31, matrix products, mul(): return lax.dot_general(left, right, dims, preferred_element_type=WIDE)  61.9 us
    pallas_call x2, Pallas kernels, pair_backward(): pl.pallas_call(kernel, grid_spec=pltpu.PrefetchScalarGridSpec(num_scalar_...  55 us
    unnamed x185, local copies, waits for them, and re-layouts  46.2 us
    pallas_call x2, Pallas kernels, pair_forward(): pl.pallas_call(kernel, grid_spec=pltpu.PrefetchScalarGridSpec(num_scalar_...  33.9 us
    all_to_all x8, starting transfers between devices, exchange_rows(): return lax.all_to_all(value, 'rows', 0, 0, tiled=True)  32.5 us
    ppermute x21, starting transfers between devices, swap(): return lax.ppermute(value, axis, [(0, 1), (1, 0)])  26.5 us
  transfers between devices with their start and end apart: 38, of which 23 were waited for; matrix products, arithmetic and copies ran while one was open for 27% of the time, Pallas kernels for 13%

profile of v13, /device:TPU:0, one launch (start us, length us, event | category | flops | bytes accessed | tf_op | source)
XLA Modules:
  0.0 688.9 jit_solution(5070806702393067249)
XLA Ops:
  7.2 2.7 copy.97
  10.0 2.7 copy.98
  14.4 4.0 collective-permute-start
  19.9 7.8 %collective-permute-done = bf16[96,1024]{1,0:T(8,128)(2,1)S(1)} collective-permute-done((bf16[96,1024]{1,0:T(8,128)(2,1)}, bf16[96,1024]{1,0:T(8,128)(2,1)S(1)}, u32[]{:S(2)}, u32[]{:S(2)}) %collective-permute-start) | collective-permute-done | bytes 196640 | tf_op jit(solution)/shard_map/ppermute | solution.py:394
  40.9 17.1 %collective-permute-done.1 = bf16[160,1024]{1,0:T(8,128)(2,1)} collective-permute-done((bf16[160,1024]{1,0:T(8,128)(2,1)}, bf16[160,1024]{1,0:T(8,128)(2,1)}, u32[]{:S(2)}, u32[]{:S(2)}) %collective-permute-start.1) | collective-permute-done | bytes 327712 | tf_op jit(solution)/shard_map/ppermute | solution.py:394
  59.9 8.5 %collective-permute-done.2 = bf16[2,96,1024]{2,1,0:T(8,128)(2,1)S(1)} collective-permute-done((bf16[2,96,1024]{2,1,0:T(8,128)(2,1)S(1)}, bf16[2,96,1024]{2,1,0:T(8,128)(2,1)S(1)}, u32[]{:S(2)}, u32[]{:S(2)}) %collective-permute-start.2) | collective-permute-done | bytes 393248 | tf_op jit(solution)/shard_map/ppermute | solution.py:394
  72.8 2.8 constant_dynamic-update-slice_fusion.3
  75.5 3.3 convolution_convert_fusion.3
  78.8 2.9 convolution_convert_fusion.4
  83.0 4.3 all-to-all-start
  89.2 23.7 %all-to-all-done.q_ref.k_ref.v_ref = bf16[8,2,3,64,256]{4,3,2,1,0:T(8,128)(2,1)} async-done(((bf16[8,2,3,64,256]{4,3,2,1,0:T(8,128)(2,1)}), bf16[8,2,3,64,256]{4,3,2,1,0:T(8,128)(2,1)}, u32[]{:S(2)}, u32[]{:S(2)}) %all-to-all-start) | async-done | bytes 1572896 | tf_op jit(solution)/shard_map/all_to_all | solution.py:230
  122.5 19.0 %pair_forward.2 = (bf16[8,2,64,256]{3,2,1,0:T(8,128)(2,1)}, f32[8,2,64,256]{3,2,1,0:T(8,128)S(1)}, f32[8,2,1,256]{3,2,1,0:T(1,128)S(1)}) custom-call(s32[2]{0:T(128)S(1)} %broadcast_13_len_ref.2.len_ref, bf16[8,2,3,64,256]{4,3,2,1,0:T(8,128)(2,1)} %all-to-all-done.q_ref.k_ref.v_ref, bf16[8,2,3,64,256]{4,3,2,1,0:T(8,128)(2,1)} %all-to-all-done.q_ref.k_ref.v_ref, ...), custom_call_target="tpu_custom_call" | custom-call | flops 20132659200 | bytes 8388608 | tf_op jit(solution)/shard_map/pair_forward/pallas_call | solution.py:282
  142.4 4.0 all-to-all-start.1
  149.3 2.9 copy-done.24
  152.2 3.3 slice.169
  158.8 4.2 all-to-all-start.2
  163.2 3.6 fusion.76
  166.9 6.2 fusion.77
  173.3 11.7 %collective-permute-done.3 = bf16[512,512]{1,0:T(8,128)(2,1)S(1)} collective-permute-done((bf16[512,512]{1,0:T(8,128)(2,1)}, bf16[512,512]{1,0:T(8,128)(2,1)S(1)}, u32[]{:S(2)}, u32[]{:S(2)}) %collective-permute-start.3) | collective-permute-done | bytes 524320 | tf_op jit(solution)/shard_map/ppermute | solution.py:394
  189.6 4.2 all-to-all-start.3
  193.9 9.6 %all-to-all-done.3.q_ref = bf16[8,2,1,64,256]{4,3,2,1,0:T(8,128)(2,1)} async-done(((bf16[8,2,1,64,256]{4,3,2,1,0:T(8,128)(2,1)}), bf16[8,2,1,64,256]{4,3,2,1,0:T(8,128)(2,1)}, u32[]{:S(2)}, u32[]{:S(2)}) %all-to-all-start.3) | async-done | bytes 524320 | tf_op jit(solution)/shard_map/all_to_all | solution.py:230
  203.5 15.0 %pair_forward.3 = (bf16[8,2,64,256]{3,2,1,0:T(8,128)(2,1)S(1)}, f32[8,2,64,256]{3,2,1,0:T(8,128)S(1)}, f32[8,2,1,256]{3,2,1,0:T(1,128)S(1)}) custom-call(s32[2]{0:T(128)S(1)} %dynamic_slice.124.len_ref, bf16[8,2,1,64,256]{4,3,2,1,0:T(8,128)(2,1)} %all-to-all-done.3.q_ref, bf16[8,2,2,64,256]{4,3,2,1,0:T(8,128)(2,1)S(1)} %all-to-all-done.2.k_ref.v_ref, ...), custom_call_target="tpu_custom_call" | custom-call | flops 14092861440 | bytes 8388608 | tf_op jit(solution)/shard_map/pair_forward/pallas_call | solution.py:282
  218.5 12.3 %all_to_all.45 = bf16[8,2,64,256]{3,2,1,0:T(8,128)(2,1)S(1)} all-to-all(bf16[8,2,64,256]{3,2,1,0:T(8,128)(2,1)S(1)} %get-tuple-element.83), channel_id=1, replica_groups=mesh['far'=2,'near'=2,'rows'=8] {'rows'}, dimensions={0} | all-to-all | bytes 1048576 | tf_op jit(solution)/shard_map/all_to_all | solution.py:230
  233.3 11.2 %collective-permute-done.4 = bf16[512,512]{1,0:T(8,128)(2,1)S(1)} collective-permute-done((bf16[512,512]{1,0:T(8,128)(2,1)S(1)}, bf16[512,512]{1,0:T(8,128)(2,1)S(1)}, u32[]{:S(2)}, u32[]{:S(2)}) %collective-permute-start.4) | collective-permute-done | bytes 524320 | tf_op jit(solution)/shard_map/ppermute | solution.py:394
  247.6 2.8 slice.177
  256.7 5.1 multiply_convert_fusion
  261.8 3.4 fusion.22
  265.2 4.8 convolution_convert_fusion.1
  270.0 4.4 convolution_convert_fusion.2
  274.4 7.8 %pad_maximum_fusion = bf16[2,2048,1024]{2,1,0:T(8,128)(2,1)} fusion(bf16[2,1024,1024]{2,1,0:T(8,128)(2,1)} %bitcast.330, bf16[2,1024,1024]{2,1,0:T(8,128)(2,1)} %bitcast.331), kind=kLoop, calls=%fused_computation.3 | loop fusion | flops 16777216 | bytes 16777216 | tf_op jit(solution)/shard_map/concatenate | solution.py:578
  284.7 5.0 fusion.82
  290.7 15.2 %collective-permute-done.5 = bf16[512,1024]{1,0:T(8,128)(2,1)} collective-permute-done((bf16[512,1024]{1,0:T(8,128)(2,1)}, bf16[512,1024]{1,0:T(8,128)(2,1)}, u32[]{:S(2)}, u32[]{:S(2)}) %collective-permute-start.5) | collective-permute-done | bytes 1048608 | tf_op jit(solution)/shard_map/ppermute | solution.py:394
  312.9 3.9 all-to-all-start.5
  321.3 11.2 %all-to-all-done.5.g_ref = bf16[8,2,64,256]{3,2,1,0:T(8,128)(2,1)S(1)} async-done(((bf16[8,2,64,256]{3,2,1,0:T(8,128)(2,1)}), bf16[8,2,64,256]{3,2,1,0:T(8,128)(2,1)S(1)}, u32[]{:S(2)}, u32[]{:S(2)}) %all-to-all-start.5) | async-done | bytes 524320 | tf_op jit(solution)/shard_map/all_to_all | solution.py:230
  334.9 22.9 %pair_backward.2 = bf16[8,2,3,64,256]{4,3,2,1,0:T(8,128)(2,1)} custom-call(s32[2]{0:T(128)S(1)} %dynamic_slice.124.len_ref, bf16[8,2,1,64,256]{4,3,2,1,0:T(8,128)(2,1)} %all-to-all-done.3.q_ref, bf16[8,2,2,64,256]{4,3,2,1,0:T(8,128)(2,1)S(1)} %all-to-all-done.2.k_ref.v_ref, bf16[8,2,2,64,256]{4,3,2,1,0:T(8,128)(2,1)S(1)} %all-to-all-done.2.k_ref.v_ref, ...), custom_call_target="tpu_custom_call" | custom-call | flops 20132659200 | bytes 8388608 | tf_op jit(solution)/shard_map/pair_backward/pallas_call | solution.py:364
  359.9 3.7 all-to-all-start.6
  367.1 24.0 %collective-permute-done.8 = bf16[256,1024]{1,0:T(8,128)(2,1)} collective-permute-done((bf16[256,1024]{1,0:T(8,128)(2,1)S(1)}, bf16[256,1024]{1,0:T(8,128)(2,1)}, u32[]{:S(2)}, u32[]{:S(2)}) %collective-permute-start.8) | collective-permute-done | bytes 524320 | tf_op jit(solution)/shard_map/ppermute | solution.py:394
  398.2 10.3 %collective-permute-done.9 = bf16[512,512]{1,0:T(8,128)(2,1)S(1)} collective-permute-done((bf16[512,512]{1,0:T(8,128)(2,1)S(1)}, bf16[512,512]{1,0:T(8,128)(2,1)S(1)}, u32[]{:S(2)}, u32[]{:S(2)}) %collective-permute-start.9) | collective-permute-done | bytes 524320 | tf_op jit(solution)/shard_map/ppermute | solution.py:394
  416.7 3.6 fusion.33
  426.0 4.0 all-to-all-start.7
  432.0 2.9 convolution_convert_fusion.8
  434.9 10.4 %all-to-all-done.7.g_ref = bf16[8,2,64,256]{3,2,1,0:T(8,128)(2,1)S(1)} async-done(((bf16[8,2,64,256]{3,2,1,0:T(8,128)(2,1)}), bf16[8,2,64,256]{3,2,1,0:T(8,128)(2,1)S(1)}, u32[]{:S(2)}, u32[]{:S(2)}) %all-to-all-start.7) | async-done | bytes 524320 | tf_op jit(solution)/shard_map/all_to_all | solution.py:230
  445.4 32.1 %pair_backward.3 = bf16[8,2,3,64,256]{4,3,2,1,0:T(8,128)(2,1)} custom-call(s32[2]{0:T(128)S(1)} %broadcast_13_len_ref.2.len_ref, bf16[8,2,3,64,256]{4,3,2,1,0:T(8,128)(2,1)} %all-to-all-done.q_ref.k_ref.v_ref, bf16[8,2,3,64,256]{4,3,2,1,0:T(8,128)(2,1)} %all-to-all-done.q_ref.k_ref.v_ref, bf16[8,2,3,64,256]{4,3,2,1,0:T(8,128)(2,1)} %all-to-all-done.q_ref.k_ref.v_ref, ...), custom_call_target="tpu_custom_call" | custom-call | flops 30198988800 | bytes 8388608 | tf_op jit(solution)/shard_map/pair_backward/pallas_call | solution.py:364
  478.1 2.7 pad_maximum_fusion.5
  480.9 4.3 all-to-all-start.8
  489.5 6.1 fusion.2
  495.6 12.8 %collective-permute-done.12 = bf16[256,768]{1,0:T(8,128)(2,1)S(1)} collective-permute-done((bf16[256,768]{1,0:T(8,128)(2,1)S(1)}, bf16[256,768]{1,0:T(8,128)(2,1)S(1)}, u32[]{:S(2)}, u32[]{:S(2)}) %collective-permute-start.12) | collective-permute-done | bytes 393248 | tf_op jit(solution)/shard_map/ppermute | solution.py:394
  509.4 8.0 %all-to-all-done.8 = bf16[8,2,3,64,256]{4,3,2,1,0:T(8,128)(2,1)} async-done(((bf16[8,2,3,64,256]{4,3,2,1,0:T(8,128)(2,1)}), bf16[8,2,3,64,256]{4,3,2,1,0:T(8,128)(2,1)}, u32[]{:S(2)}, u32[]{:S(2)}) %all-to-all-start.8) | async-done | bytes 1572896 | tf_op jit(solution)/shard_map/all_to_all | solution.py:230
  517.4 3.0 copy.113
  528.3 2.6 copy.130
  530.9 4.7 fusion.10
  545.9 6.7 collective-permute-done.19
  557.6 3.4 collective-permute-start.15
  565.0 14.9 %all-gather.2 = bf16[16,80,256]{2,1,0:T(8,128)(2,1)S(1)} all-gather(bf16[2,80,256]{2,1,0:T(8,128)(2,1)S(1)} %pad_maximum_fusion.21), channel_id=4, replica_groups=mesh['far'=2,'near'=2,'rows'=8] {'rows'}, dimensions={0}, use_global_device_ids=true | all-gather | bytes 737280 | tf_op jit(solution)/shard_map/all_gather | solution.py:662
  580.0 4.0 collective-permute-start.16
  594.2 4.4 slice_convert_fusion
  598.7 20.1 %collective-permute-done.17 = bf16[160,1024]{1,0:T(8,128)(2,1)S(1)} collective-permute-done((bf16[160,1024]{1,0:T(8,128)(2,1)S(1)}, bf16[160,1024]{1,0:T(8,128)(2,1)S(1)}, u32[]{:S(2)}, u32[]{:S(2)}) %collective-permute-start.17) | collective-permute-done | bytes 327712 | tf_op jit(solution)/shard_map/ppermute | solution.py:394
  626.1 15.2 %collective-permute-done.20 = bf16[2,256,768]{2,1,0:T(8,128)(2,1)S(1)} collective-permute-done((bf16[2,256,768]{2,1,0:T(8,128)(2,1)}, bf16[2,256,768]{2,1,0:T(8,128)(2,1)S(1)}, u32[]{:S(2)}, u32[]{:S(2)}) %collective-permute-start.20) | collective-permute-done | bytes 786464 | tf_op jit(solution)/shard_map/ppermute | solution.py:394
  646.9 2.5 copy.124
  651.1 2.9 copy.125
  660.1 5.3 copy.127
  665.4 3.2 reverse_select_fusion.1
  668.6 2.6 fusion.14
  676.1 3.7 copy.123
  (395 shorter events, 175.6 us)
Async XLA Ops:
  7.2 224.8 %copy-start = (bf16[4,256,1024]{2,1,0:T(8,128)(2,1)S(1)}, bf16[4,256,1024]{2,1,0:T(8,128)(2,1)}, u32[]{:S(2)}) copy-start(bf16[4,256,1024]{2,1,0:T(8,128)(2,1)} %param.31) | copy-start | bytes 6291460
  7.2 65.6 %all-gather.10.cloned.1.call-start = ((), (), s32[]{:S(2)}) async-start(), calls=%async_computation.12 | async-start | bytes 1769472 | tf_op jit(solution)/shard_map/all_gather | solution.py:444
  10.0 8.4 %copy-start.72 = (s32[4,256]{1,0:T(4,128)S(1)}, s32[4,256]{1,0:T(4,128)}, u32[]{:S(2)}) copy-start(s32[4,256]{1,0:T(4,128)} %param.17) | copy-start | bytes 12292
  12.7 18.1 %copy-start.68 = (bf16[32,2,1024]{2,1,0:T(2,128)(2,1)S(1)}, bf16[32,2,1024]{2,1,0:T(2,128)(2,1)}, u32[]{:S(2)}) copy-start(bf16[32,2,1024]{2,1,0:T(2,128)(2,1)} %param.20) | copy-start | bytes 393220
  12.7 20.0 %copy-start.52 = (bf16[2,1024,256]{2,1,0:T(8,128)(2,1)S(1)}, bf16[2,1024,256]{2,1,0:T(8,128)(2,1)}, u32[]{:S(2)}) copy-start(bf16[2,1024,256]{2,1,0:T(8,128)(2,1)} %param.25) | copy-start | bytes 3145732
  14.4 13.4 %collective-permute-start = (bf16[96,1024]{1,0:T(8,128)(2,1)}, bf16[96,1024]{1,0:T(8,128)(2,1)S(1)}, u32[]{:S(2)}, u32[]{:S(2)}) collective-permute-start(bf16[96,1024]{1,0:T(8,128)(2,1)} %constant_dynamic-slice_fusion.20), channel_id=1, source_target_pairs={{0,16},{16,0},{1,17},{17,1},{2,18},{18,2},{3,19},{19,3},{4,20},{20... | collective-permute-start | bytes 589832 | tf_op jit(solution)/shard_map/ppermute | solution.py:394
  19.9 11.5 %copy-start.69 = (f32[2,256]{1,0:T(2,128)}, f32[2,256]{1,0:T(2,128)S(1)}, u32[]{:S(2)}) copy-start(f32[2,256]{1,0:T(2,128)S(1)} %get-tuple-element.225) | copy-start | bytes 6148
  28.4 118.0 %all-gather.18.cloned.1.call-start = ((), (), s32[]{:S(2)}) async-start(), calls=%async_computation.19 | async-start | bytes 8257536 | tf_op jit(solution)/shard_map/all_gather | solution.py:522
  40.8 17.1 %collective-permute-start.1 = (bf16[160,1024]{1,0:T(8,128)(2,1)}, bf16[160,1024]{1,0:T(8,128)(2,1)}, u32[]{:S(2)}, u32[]{:S(2)}) collective-permute-start(bf16[160,1024]{1,0:T(8,128)(2,1)} %pad_maximum_fusion.19), channel_id=1, source_target_pairs={{0,16},{16,0},{1,17},{17,1},{2,18},{18,2},{3,19},{19,3},{4,20},{20... | collective-permute-start | bytes 983048 | tf_op jit(solution)/shard_map/ppermute | solution.py:394
  58.9 9.4 %collective-permute-start.2 = (bf16[2,96,1024]{2,1,0:T(8,128)(2,1)S(1)}, bf16[2,96,1024]{2,1,0:T(8,128)(2,1)S(1)}, u32[]{:S(2)}, u32[]{:S(2)}) collective-permute-start(bf16[2,96,1024]{2,1,0:T(8,128)(2,1)S(1)} %fusion.60), channel_id=1, source_target_pairs={{0,8},{8,0},{1,9},{9,1},{2,10},{10,2},{3,11},{11,3},{4,12},{12,4},... | collective-permute-start | bytes 1179656 | tf_op jit(solution)/shard_map/ppermute | solution.py:394
  83.0 29.9 %all-to-all-start = ((bf16[8,2,3,64,256]{4,3,2,1,0:T(8,128)(2,1)}), bf16[8,2,3,64,256]{4,3,2,1,0:T(8,128)(2,1)}, u32[]{:S(2)}, u32[]{:S(2)}) async-start(bf16[8,2,3,64,256]{4,3,2,1,0:T(8,128)(2,1)} %pad_maximum_fusion.7), calls=%async_computation | async-start | bytes 3145728 | tf_op jit(solution)/shard_map/all_to_all | solution.py:230
  87.3 27.4 %copy-start.74 = (bf16[1024]{0:T(1024)(128)(2,1)S(1)}, bf16[1024]{0:T(1024)(128)(2,1)}, u32[]{:S(2)}) copy-start(bf16[1024]{0:T(1024)(128)(2,1)} %param.23) | copy-start | bytes 6148
  87.3 160.2 %all-gather.20.cloned.1.call-start = ((), (), s32[]{:S(2)}) async-start(), calls=%async_computation.20 | async-start | bytes 8912896 | tf_op jit(solution)/shard_map/all_gather | solution.py:536
  142.4 14.9 %all-to-all-start.1 = ((bf16[8,2,64,256]{3,2,1,0:T(8,128)(2,1)}), bf16[8,2,64,256]{3,2,1,0:T(8,128)(2,1)S(1)}, u32[]{:S(2)}, u32[]{:S(2)}) async-start(bf16[8,2,64,256]{3,2,1,0:T(8,128)(2,1)} %get-tuple-element.78), calls=%async_computation.1 | async-start | bytes 1048576 | tf_op jit(solution)/shard_map/all_to_all | solution.py:230
  148.6 6.9 %copy-start.18 = (bf16[1024,1024]{1,0:T(8,128)(2,1)}, bf16[1024,1024]{1,0:T(8,128)(2,1)S(1)}, u32[]{:S(2)}) copy-start(bf16[1024,1024]{1,0:T(8,128)(2,1)S(1)} %constant_dynamic-update-slice_fusion.1) | copy-start | bytes 6291460
  158.8 30.8 %all-to-all-start.2 = ((bf16[8,2,2,64,256]{4,3,2,1,0:T(8,128)(2,1)}), bf16[8,2,2,64,256]{4,3,2,1,0:T(8,128)(2,1)S(1)}, u32[]{:S(2)}, u32[]{:S(2)}) async-start(bf16[8,2,2,64,256]{4,3,2,1,0:T(8,128)(2,1)} %pad_maximum_fusion.11), calls=%async_computation.2 | async-start | bytes 2097152 | tf_op jit(solution)/shard_map/all_to_all | solution.py:230
  162.9 22.0 %collective-permute-start.3 = (bf16[512,512]{1,0:T(8,128)(2,1)}, bf16[512,512]{1,0:T(8,128)(2,1)S(1)}, u32[]{:S(2)}, u32[]{:S(2)}) collective-permute-start(bf16[512,512]{1,0:T(8,128)(2,1)} %bitcast.337), channel_id=1, source_target_pairs={{0,8},{8,0},{1,9},{9,1},{2,10},{10,2},{3,11},{11,3},{4,12},{12,4},... | collective-permute-start | bytes 1572872 | tf_op jit(solution)/shard_map/ppermute | solution.py:394
  173.1 11.9 %copy-start.35 = (bf16[2,256,1024]{2,1,0:T(8,128)(2,1)S(1)}, bf16[2,256,1024]{2,1,0:T(8,128)(2,1)}, u32[]{:S(2)}) copy-start(bf16[2,256,1024]{2,1,0:T(8,128)(2,1)} %get-tuple-element.217) | copy-start | bytes 3145732
  173.1 11.9 %copy-start.39 = (bf16[64,8,2,256]{3,1,2,0:T(8,128)(2,1)S(1)}, bf16[64,8,2,256]{3,1,2,0:T(8,128)(2,1)}, u32[]{:S(2)}) copy-start(bf16[64,8,2,256]{3,1,2,0:T(8,128)(2,1)} %copy.137) | copy-start | bytes 1572868
  188.2 5.6 copy-start.78
  189.6 13.9 %all-to-all-start.3 = ((bf16[8,2,1,64,256]{4,3,2,1,0:T(8,128)(2,1)}), bf16[8,2,1,64,256]{4,3,2,1,0:T(8,128)(2,1)}, u32[]{:S(2)}, u32[]{:S(2)}) async-start(bf16[8,2,1,64,256]{4,3,2,1,0:T(8,128)(2,1)} %pad_maximum_fusion.17), calls=%async_computation.3 | async-start | bytes 1048576 | tf_op jit(solution)/shard_map/all_to_all | solution.py:230
  193.8 166.1 %reduce-scatter.4.cloned.1.call-start = ((), (), s32[]{:S(2)}) async-start(), calls=%async_computation.13 | async-start | bytes 9437184 | tf_op jit(solution)/shard_map/reduce_scatter | solution.py:567
  218.5 14.6 %copy-start.2 = (f32[8,2,64,256]{3,2,1,0:T(8,128)}, f32[8,2,64,256]{3,2,1,0:T(8,128)S(1)}, u32[]{:S(2)}) copy-start(f32[8,2,64,256]{3,2,1,0:T(8,128)S(1)} %get-tuple-element.91.wide_ref) | copy-start | bytes 3145732
  218.5 13.5 %copy-start.75 = (bf16[1024]{0:T(1024)(128)(2,1)S(1)}, bf16[1024]{0:T(1024)(128)(2,1)}, u32[]{:S(2)}) copy-start(bf16[1024]{0:T(1024)(128)(2,1)} %param.28) | copy-start | bytes 6148
  231.4 13.1 %copy-start.64 = (bf16[64,8,2,256]{3,1,2,0:T(8,128)(2,1)}, bf16[64,8,2,256]{3,1,2,0:T(8,128)(2,1)S(1)}, u32[]{:S(2)}) copy-start(bf16[64,8,2,256]{3,1,2,0:T(8,128)(2,1)S(1)} %copy.138) | copy-start | bytes 1572868
  231.4 13.1 %collective-permute-start.4 = (bf16[512,512]{1,0:T(8,128)(2,1)S(1)}, bf16[512,512]{1,0:T(8,128)(2,1)S(1)}, u32[]{:S(2)}, u32[]{:S(2)}) collective-permute-start(bf16[512,512]{1,0:T(8,128)(2,1)S(1)} %bitcast.371), channel_id=1, source_target_pairs={{0,8},{8,0},{1,9},{9,1},{2,10},{10,2},{3,11},{11,3},{4,12},{12,4},... | collective-permute-start | bytes 1572872 | tf_op jit(solution)/shard_map/ppermute | solution.py:394
  233.1 11.5 %copy-start.7 = (f32[512,1024]{1,0:T(8,128)S(1)}, f32[512,1024]{1,0:T(8,128)}, u32[]{:S(2)}) copy-start(f32[512,1024]{1,0:T(8,128)} %copy-done.6) | copy-start | bytes 6291460
  261.8 8.2 %copy-start.79 = (bf16[512,2048]{1,0:T(8,128)(2,1)}, bf16[512,2048]{1,0:T(8,128)(2,1)S(1)}, u32[]{:S(2)}) copy-start(bf16[512,2048]{1,0:T(8,128)(2,1)S(1)} %get-tuple-element.86) | copy-start | bytes 6291460
  282.2 23.7 %collective-permute-start.5 = (bf16[512,1024]{1,0:T(8,128)(2,1)}, bf16[512,1024]{1,0:T(8,128)(2,1)}, u32[]{:S(2)}, u32[]{:S(2)}) collective-permute-start(bf16[512,1024]{1,0:T(8,128)(2,1)} %fusion.22), channel_id=1, source_target_pairs={{0,8},{8,0},{1,9},{9,1},{2,10},{10,2},{3,11},{11,3},{4,12},{12,4},... | collective-permute-start | bytes 3145736 | tf_op jit(solution)/shard_map/ppermute | solution.py:394
  284.7 21.2 %copy-start.55 = (bf16[512,1024]{1,0:T(8,128)(2,1)S(1)}, bf16[512,1024]{1,0:T(8,128)(2,1)}, u32[]{:S(2)}) copy-start(bf16[512,1024]{1,0:T(8,128)(2,1)} %fusion.22) | copy-start | bytes 3145732
  289.7 18.1 %copy-start.42 = (f32[2,2,128,1024]{3,2,1,0:T(8,128)}, f32[2,2,128,1024]{3,2,1,0:T(8,128)S(1)}, u32[]{:S(2)}) copy-start(f32[2,2,128,1024]{3,2,1,0:T(8,128)S(1)} %fusion.82) | copy-start | bytes 6291460
  307.8 11.3 %collective-permute-start.6 = (bf16[256,1024]{1,0:T(8,128)(2,1)}, bf16[256,1024]{1,0:T(8,128)(2,1)}, u32[]{:S(2)}, u32[]{:S(2)}) collective-permute-start(bf16[256,1024]{1,0:T(8,128)(2,1)} %bitcast.39), channel_id=1, source_target_pairs={{0,8},{8,0},{1,9},{9,1},{2,10},{10,2},{3,11},{11,3},{4,12},{12,4},... | collective-permute-start | bytes 1572872 | tf_op jit(solution)/shard_map/ppermute | solution.py:394
  312.9 19.5 %all-to-all-start.5 = ((bf16[8,2,64,256]{3,2,1,0:T(8,128)(2,1)}), bf16[8,2,64,256]{3,2,1,0:T(8,128)(2,1)S(1)}, u32[]{:S(2)}, u32[]{:S(2)}) async-start(bf16[8,2,64,256]{3,2,1,0:T(8,128)(2,1)} %maximum_bitcast_fusion), calls=%async_computation.5 | async-start | bytes 1048576 | tf_op jit(solution)/shard_map/all_to_all | solution.py:230
  319.0 16.0 %copy-start.3 = (f32[8,2,64,256]{3,2,1,0:T(8,128)S(1)}, f32[8,2,64,256]{3,2,1,0:T(8,128)}, u32[]{:S(2)}) copy-start(f32[8,2,64,256]{3,2,1,0:T(8,128)} %copy-done.2) | copy-start | bytes 3145732
  332.5 25.3 %collective-permute-start.7 = (bf16[256,1024]{1,0:T(8,128)(2,1)}, bf16[256,1024]{1,0:T(8,128)(2,1)S(1)}, u32[]{:S(2)}, u32[]{:S(2)}) collective-permute-start(bf16[256,1024]{1,0:T(8,128)(2,1)} %fusion.44), channel_id=1, source_target_pairs={{0,16},{16,0},{1,17},{17,1},{2,18},{18,2},{3,19},{19,3},{4,20},{20... | collective-permute-start | bytes 1572872 | tf_op jit(solution)/shard_map/ppermute | solution.py:394
  359.9 5.5 copy-start.65
  359.9 31.2 %all-to-all-start.6 = ((bf16[8,2,3,64,256]{4,3,2,1,0:T(8,128)(2,1)}), bf16[8,2,3,64,256]{4,3,2,1,0:T(8,128)(2,1)S(1)}, u32[]{:S(2)}, u32[]{:S(2)}) async-start(bf16[8,2,3,64,256]{4,3,2,1,0:T(8,128)(2,1)} %pair_backward.2), calls=%async_computation.7 | async-start | bytes 3145728 | tf_op jit(solution)/shard_map/all_to_all | solution.py:230
  363.6 153.8 %reduce-scatter.6.cloned.1.call-start = ((), (), s32[]{:S(2)}) async-start(), calls=%async_computation.15 | async-start | bytes 4718592 | tf_op jit(solution)/shard_map/reduce_scatter | solution.py:567
  364.7 26.4 %collective-permute-start.8 = (bf16[256,1024]{1,0:T(8,128)(2,1)S(1)}, bf16[256,1024]{1,0:T(8,128)(2,1)}, u32[]{:S(2)}, u32[]{:S(2)}) collective-permute-start(bf16[256,1024]{1,0:T(8,128)(2,1)S(1)} %dynamic-slice_bitcast_fusion), channel_id=1, source_target_pairs={{0,16},{16,0},{1,17},{17,1},{2,18},{18,2},{3,19},{19,3},{4,20},{20... | collective-permute-start | bytes 1572872 | tf_op jit(solution)/shard_map/ppermute | solution.py:394
  394.5 13.9 %collective-permute-start.9 = (bf16[512,512]{1,0:T(8,128)(2,1)S(1)}, bf16[512,512]{1,0:T(8,128)(2,1)S(1)}, u32[]{:S(2)}, u32[]{:S(2)}) collective-permute-start(bf16[512,512]{1,0:T(8,128)(2,1)S(1)} %bitcast.340), channel_id=1, source_target_pairs={{0,8},{8,0},{1,9},{9,1},{2,10},{10,2},{3,11},{11,3},{4,12},{12,4},... | collective-permute-start | bytes 1572872 | tf_op jit(solution)/shard_map/ppermute | solution.py:394
  398.2 11.3 %copy-start.22 = (bf16[1,4,8,32,1024]{4,3,0,1,2:T(8,128)(2,1)S(1)}, bf16[1,4,8,32,1024]{4,3,0,1,2:T(8,128)(2,1)}, u32[]{:S(2)}) copy-start(bf16[1,4,8,32,1024]{4,3,0,1,2:T(8,128)(2,1)} %get-tuple-element.205) | copy-start | bytes 6291460
  409.3 108.1 %all-gather.12.cloned.1.call-start = ((), (), s32[]{:S(2)}) async-start(), calls=%async_computation.14 | async-start | bytes 4718592 | tf_op jit(solution)/shard_map/all_gather | solution.py:444
  424.6 7.4 %copy-start.40 = (bf16[64,8,2,256]{3,1,2,0:T(8,128)(2,1)S(1)}, bf16[64,8,2,256]{3,1,2,0:T(8,128)(2,1)}, u32[]{:S(2)}) copy-start(bf16[64,8,2,256]{3,1,2,0:T(8,128)(2,1)} %copy.137) | copy-start | bytes 1572868
  426.0 19.4 %copy-start.5 = (f32[8,2,64,256]{3,2,1,0:T(8,128)S(1)}, f32[8,2,64,256]{3,2,1,0:T(8,128)}, u32[]{:S(2)}) copy-start(f32[8,2,64,256]{3,2,1,0:T(8,128)} %copy-done.4) | copy-start | bytes 3145732
  426.0 19.4 %all-to-all-start.7 = ((bf16[8,2,64,256]{3,2,1,0:T(8,128)(2,1)}), bf16[8,2,64,256]{3,2,1,0:T(8,128)(2,1)S(1)}, u32[]{:S(2)}, u32[]{:S(2)}) async-start(bf16[8,2,64,256]{3,2,1,0:T(8,128)(2,1)} %maximum_bitcast_fusion.1), calls=%async_computation.8 | async-start | bytes 1048576 | tf_op jit(solution)/shard_map/all_to_all | solution.py:230
  430.0 50.9 %collective-permute-start.10 = (bf16[512,1024]{1,0:T(8,128)(2,1)S(1)}, bf16[512,1024]{1,0:T(8,128)(2,1)}, u32[]{:S(2)}, u32[]{:S(2)}) collective-permute-start(bf16[512,1024]{1,0:T(8,128)(2,1)S(1)} %convolution_convert_fusion.7), channel_id=1, source_target_pairs={{0,8},{8,0},{1,9},{9,1},{2,10},{10,2},{3,11},{11,3},{4,12},{12,4},... | collective-permute-start | bytes 3145736 | tf_op jit(solution)/shard_map/ppermute | solution.py:394
  430.4 47.7 %collective-permute-start.11 = (bf16[2,256,1024]{2,1,0:T(8,128)(2,1)}, bf16[2,256,1024]{2,1,0:T(8,128)(2,1)}, u32[]{:S(2)}, u32[]{:S(2)}) collective-permute-start(bf16[2,256,1024]{2,1,0:T(8,128)(2,1)} %pad_maximum_fusion.12), channel_id=1, source_target_pairs={{0,8},{8,0},{1,9},{9,1},{2,10},{10,2},{3,11},{11,3},{4,12},{12,4},... | collective-permute-start | bytes 3145736 | tf_op jit(solution)/shard_map/ppermute | solution.py:394
  445.4 32.8 %copy-start.37 = (bf16[2,256,1024]{2,1,0:T(8,128)(2,1)S(1)}, bf16[2,256,1024]{2,1,0:T(8,128)(2,1)}, u32[]{:S(2)}) copy-start(bf16[2,256,1024]{2,1,0:T(8,128)(2,1)} %pad_maximum_fusion.12) | copy-start | bytes 3145732
  480.9 36.5 %all-to-all-start.8 = ((bf16[8,2,3,64,256]{4,3,2,1,0:T(8,128)(2,1)}), bf16[8,2,3,64,256]{4,3,2,1,0:T(8,128)(2,1)}, u32[]{:S(2)}, u32[]{:S(2)}) async-start(bf16[8,2,3,64,256]{4,3,2,1,0:T(8,128)(2,1)} %pair_backward.3), calls=%async_computation.9 | async-start | bytes 3145728 | tf_op jit(solution)/shard_map/all_to_all | solution.py:230
  485.2 103.7 %reduce-scatter.8.cloned.1.call-start = ((), (), s32[]{:S(2)}) async-start(), calls=%async_computation.16 | async-start | bytes 5898240 | tf_op jit(solution)/shard_map/reduce_scatter | solution.py:567
  487.9 20.6 %collective-permute-start.12 = (bf16[256,768]{1,0:T(8,128)(2,1)S(1)}, bf16[256,768]{1,0:T(8,128)(2,1)S(1)}, u32[]{:S(2)}, u32[]{:S(2)}) collective-permute-start(bf16[256,768]{1,0:T(8,128)(2,1)S(1)} %convolution_convert_fusion.15), channel_id=1, source_target_pairs={{0,16},{16,0},{1,17},{17,1},{2,18},{18,2},{3,19},{19,3},{4,20},{20... | collective-permute-start | bytes 1179656 | tf_op jit(solution)/shard_map/ppermute | solution.py:394
  525.6 118.1 %all-gather.14.cloned.1.call-start = ((), (), s32[]{:S(2)}) async-start(), calls=%async_computation.17 | async-start | bytes 2359296 | tf_op jit(solution)/shard_map/all_gather | solution.py:444
  537.8 16.0 %collective-permute-start.13 = (bf16[256,1024]{1,0:T(8,128)(2,1)}, bf16[256,1024]{1,0:T(8,128)(2,1)S(1)}, u32[]{:S(2)}, u32[]{:S(2)}) collective-permute-start(bf16[256,1024]{1,0:T(8,128)(2,1)} %bitcast.81), channel_id=1, source_target_pairs={{0,8},{8,0},{1,9},{9,1},{2,10},{10,2},{3,11},{11,3},{4,12},{12,4},... | collective-permute-start | bytes 1572872 | tf_op jit(solution)/shard_map/ppermute | solution.py:394
  538.1 14.5 %collective-permute-start.19 = (bf16[128,1024]{1,0:T(8,128)(2,1)S(1)}, bf16[128,1024]{1,0:T(8,128)(2,1)S(1)}, u32[]{:S(2)}, u32[]{:S(2)}) collective-permute-start(bf16[128,1024]{1,0:T(8,128)(2,1)S(1)} %dynamic-slice_bitcast_fusion.2), channel_id=1, source_target_pairs={{0,16},{16,0},{1,17},{17,1},{2,18},{18,2},{3,19},{19,3},{4,20},{20... | collective-permute-start | bytes 786440 | tf_op jit(solution)/shard_map/ppermute | solution.py:394
  553.4 117.9 %all-gather.16.cloned.1.call-start = ((), (), s32[]{:S(2)}) async-start(), calls=%async_computation.18 | async-start | bytes 2949120 | tf_op jit(solution)/shard_map/all_gather | solution.py:444
  557.6 7.2 %collective-permute-start.15 = (bf16[64,1024]{1,0:T(8,128)(2,1)S(1)}, bf16[64,1024]{1,0:T(8,128)(2,1)S(1)}, u32[]{:S(2)}, u32[]{:S(2)}) collective-permute-start(bf16[64,1024]{1,0:T(8,128)(2,1)S(1)} %pad_maximum_fusion.20), channel_id=1, source_target_pairs={{0,8},{8,0},{1,9},{9,1},{2,10},{10,2},{3,11},{11,3},{4,12},{12,4},... | collective-permute-start | bytes 393224 | tf_op jit(solution)/shard_map/ppermute | solution.py:394
  562.1 21.9 %copy-start.14 = (bf16[2,2,2,128,1024]{4,3,0,2,1:T(8,128)(2,1)S(1)}, bf16[2,2,2,128,1024]{4,3,0,2,1:T(8,128)(2,1)}, u32[]{:S(2)}) copy-start(bf16[2,2,2,128,1024]{4,3,0,2,1:T(8,128)(2,1)} %copy.116) | copy-start | bytes 6291460
  562.1 24.6 %collective-permute-start.14 = (bf16[256,1024]{1,0:T(8,128)(2,1)}, bf16[256,1024]{1,0:T(8,128)(2,1)S(1)}, u32[]{:S(2)}, u32[]{:S(2)}) collective-permute-start(bf16[256,1024]{1,0:T(8,128)(2,1)} %fusion.42), channel_id=1, source_target_pairs={{0,16},{16,0},{1,17},{17,1},{2,18},{18,2},{3,19},{19,3},{4,20},{20... | collective-permute-start | bytes 1572872 | tf_op jit(solution)/shard_map/ppermute | solution.py:394
  580.0 6.7 collective-permute-start.16
  588.8 32.2 %collective-permute-start.18 = (bf16[2,256,1024]{2,1,0:T(8,128)(2,1)S(1)}, bf16[2,256,1024]{2,1,0:T(8,128)(2,1)}, u32[]{:S(2)}, u32[]{:S(2)}) collective-permute-start(bf16[2,256,1024]{2,1,0:T(8,128)(2,1)S(1)} %pad_maximum_fusion.13), channel_id=1, source_target_pairs={{0,8},{8,0},{1,9},{9,1},{2,10},{10,2},{3,11},{11,3},{4,12},{12,4},... | collective-permute-start | bytes 3145736 | tf_op jit(solution)/shard_map/ppermute | solution.py:394
  591.9 26.9 %copy-start.59 = (bf16[2,160,1024]{2,1,0:T(8,128)(2,1)S(1)}, bf16[2,160,1024]{2,1,0:T(8,128)(2,1)}, u32[]{:S(2)}) copy-start(bf16[2,160,1024]{2,1,0:T(8,128)(2,1)} %reduce-scatter.8.cloned.1.call-done) | copy-start | bytes 1966084
  591.9 26.8 %collective-permute-start.17 = (bf16[160,1024]{1,0:T(8,128)(2,1)S(1)}, bf16[160,1024]{1,0:T(8,128)(2,1)S(1)}, u32[]{:S(2)}, u32[]{:S(2)}) collective-permute-start(bf16[160,1024]{1,0:T(8,128)(2,1)S(1)} %dynamic-slice_bitcast_fusion.1), channel_id=1, source_target_pairs={{0,16},{16,0},{1,17},{17,1},{2,18},{18,2},{3,19},{19,3},{4,20},{20... | collective-permute-start | bytes 983048 | tf_op jit(solution)/shard_map/ppermute | solution.py:394
  622.5 18.8 %collective-permute-start.20 = (bf16[2,256,768]{2,1,0:T(8,128)(2,1)}, bf16[2,256,768]{2,1,0:T(8,128)(2,1)S(1)}, u32[]{:S(2)}, u32[]{:S(2)}) collective-permute-start(bf16[2,256,768]{2,1,0:T(8,128)(2,1)} %pad_maximum_fusion.16), channel_id=1, source_target_pairs={{0,8},{8,0},{1,9},{9,1},{2,10},{10,2},{3,11},{11,3},{4,12},{12,4},... | collective-permute-start | bytes 2359304 | tf_op jit(solution)/shard_map/ppermute | solution.py:394
  676.1 5.8 copy-start.1
  (59 other events, 126.9 us)
Sparse Core Ops, SparseCore 0:
  28.5 26.8 all-gather.9
  69.5 59.3 all-gather.17
  131.9 81.9 all-gather.19
  282.3 75.6 reduce-scatter.3
  408.6 55.4 reduce-scatter.5
  465.9 47.9 all-gather.11
  525.7 57.3 reduce-scatter.7
  585.7 27.9 all-gather.13
  622.6 34.8 all-gather.15

commit v14 on v13

--- a/solution.py
+++ b/solution.py
@@ -623,7 +623,7 @@
     grad_mid_away = swap(grad_mid, "near")
     output_terms = by_shard(self_mixed_t, grad_self_low)
     grads = pair_backward(qkv, qkv, 1, None, exchange_rows(grad_mixed), self_wide, self_log)
-    grads, grad_mid_away, result_four = tie(grads, grad_mid_away, result_four)
+    grads, grad_mid_away, result_four, hidden_total = tie(grads, grad_mid_away, result_four, hidden_total)
     grad_mid = (grad_mid.astype(WIDE) + grad_mid_away.astype(WIDE)).astype(LOW)
     patch_half = mul(halves(grad_mid)[0], patch_weights, NT).astype(LOW)
     patch_two = jnp.stack([patch_half, swap(patch_half, "far")])
@@ -632,9 +632,7 @@
     last_terms = jnp.pad(
         jnp.concatenate([output_terms, patch_terms], axis=1), ((0, 0), (3 * cols, 0), (0, 0))
     )
-    grads, patch_two, last_terms, hidden_total, middle_part = tie(
-        exchange_rows(grads), patch_two, last_terms, hidden_total, middle_part
-    )
+    grads, patch_two, last_terms, middle_part = tie(exchange_rows(grads), patch_two, last_terms, middle_part)
     grad_qkv_t = from_pairs(grads)
     last_terms = lax.dynamic_update_slice_in_dim(last_terms, by_shard(grad_qkv_t, normed_one), 0, 1)
     last_part = part_rows(last_terms)
@@ -672,7 +670,7 @@
         add_far(last_own, swap(last_away, "far")), input_four, outputs, hidden_gradients
     )
     last_total = join_rows(last_sum)
-    middle_total, patch_four = tie(middle_total, patch_four)
+    input_four, patch_four = tie(input_four, patch_four)
     input_grads, patch_grads = over_heads(input_four), over_heads(patch_four)
 
     cross_output_total, query_total = middle_total[:cols], middle_total[cols : 2 * cols]

time: 703 us -> 680 us (0.967)
  waiting for transfers between devices: 229 us -> 220 us
    all_to_all x8, waiting for transfers between devices: 62.9 us -> 49.4 us  [exchange_rows(): return lax.all_to_all(value, 'rows', 0, 0, tiled=True)]
    unnamed x185 -> x171, local copies, waits for them, and re-layouts: 46.2 us -> 40.8 us
  transfers between devices with their start and end apart: 38 -> 38, of which waited for: 23 -> 22; matrix products, arithmetic and copies ran while one was open for 27% -> 28% of each run, Pallas kernels for 13% -> 13%
where the time goes in v14:
time: 680 us; the launch traced here: 670 us
  waiting for transfers between devices  220 us (32%)
  local copies, waits for them, and re-layouts  112 us (16%)
  Pallas kernels  89 us (13%)
  other arithmetic  88.7 us (13%)
  matrix products  62.1 us (9%)
  starting transfers between devices  57.9 us (9%)
  blocking collectives  24.3 us (4%)
  between operations  15.6 us (2%)
    ppermute x21, waiting for transfers between devices, swap(): return lax.ppermute(value, axis, [(0, 1), (1, 0)])  170 us
    dot_general x31, matrix products, mul(): return lax.dot_general(left, right, dims, preferred_element_type=WIDE)  61.1 us
    pallas_call x2, Pallas kernels, pair_backward(): pl.pallas_call(kernel, grid_spec=pltpu.PrefetchScalarGridSpec(num_scalar_...  55 us
    all_to_all x8, waiting for transfers between devices, exchange_rows(): return lax.all_to_all(value, 'rows', 0, 0, tiled=True)  49.4 us
    unnamed x171, local copies, waits for them, and re-layouts  40.8 us
    pallas_call x2, Pallas kernels, pair_forward(): pl.pallas_call(kernel, grid_spec=pltpu.PrefetchScalarGridSpec(num_scalar_...  33.9 us
    all_to_all x8, starting transfers between devices, exchange_rows(): return lax.all_to_all(value, 'rows', 0, 0, tiled=True)  33.3 us
    ppermute x21, starting transfers between devices, swap(): return lax.ppermute(value, axis, [(0, 1), (1, 0)])  24.3 us
  transfers between devices with their start and end apart: 38, of which 22 were waited for; matrix products, arithmetic and copies ran while one was open for 28% of the time, Pallas kernels for 13%

profile of v14, /device:TPU:0, one launch (start us, length us, event | category | flops | bytes accessed | tf_op | source)
XLA Modules:
  0.0 669.9 jit_solution(12367038911914788965)
XLA Ops:
  7.2 2.7 copy.97
  10.0 2.7 copy.98
  14.4 4.0 collective-permute-start
  19.9 7.8 %collective-permute-done = bf16[96,1024]{1,0:T(8,128)(2,1)S(1)} collective-permute-done((bf16[96,1024]{1,0:T(8,128)(2,1)}, bf16[96,1024]{1,0:T(8,128)(2,1)S(1)}, u32[]{:S(2)}, u32[]{:S(2)}) %collective-permute-start) | collective-permute-done | bytes 196640 | tf_op jit(solution)/shard_map/ppermute | solution.py:394
  40.9 17.1 %collective-permute-done.1 = bf16[160,1024]{1,0:T(8,128)(2,1)} collective-permute-done((bf16[160,1024]{1,0:T(8,128)(2,1)}, bf16[160,1024]{1,0:T(8,128)(2,1)}, u32[]{:S(2)}, u32[]{:S(2)}) %collective-permute-start.1) | collective-permute-done | bytes 327712 | tf_op jit(solution)/shard_map/ppermute | solution.py:394
  59.9 8.5 %collective-permute-done.2 = bf16[2,96,1024]{2,1,0:T(8,128)(2,1)S(1)} collective-permute-done((bf16[2,96,1024]{2,1,0:T(8,128)(2,1)S(1)}, bf16[2,96,1024]{2,1,0:T(8,128)(2,1)S(1)}, u32[]{:S(2)}, u32[]{:S(2)}) %collective-permute-start.2) | collective-permute-done | bytes 393248 | tf_op jit(solution)/shard_map/ppermute | solution.py:394
  72.8 2.8 constant_dynamic-update-slice_fusion.3
  75.5 3.3 convolution_convert_fusion.3
  78.8 2.9 convolution_convert_fusion.4
  83.0 4.3 all-to-all-start
  89.2 23.7 %all-to-all-done.q_ref.k_ref.v_ref = bf16[8,2,3,64,256]{4,3,2,1,0:T(8,128)(2,1)} async-done(((bf16[8,2,3,64,256]{4,3,2,1,0:T(8,128)(2,1)}), bf16[8,2,3,64,256]{4,3,2,1,0:T(8,128)(2,1)}, u32[]{:S(2)}, u32[]{:S(2)}) %all-to-all-start) | async-done | bytes 1572896 | tf_op jit(solution)/shard_map/all_to_all | solution.py:230
  122.4 19.0 %pair_forward.2 = (bf16[8,2,64,256]{3,2,1,0:T(8,128)(2,1)}, f32[8,2,64,256]{3,2,1,0:T(8,128)S(1)}, f32[8,2,1,256]{3,2,1,0:T(1,128)S(1)}) custom-call(s32[2]{0:T(128)S(1)} %broadcast_13_len_ref.2.len_ref, bf16[8,2,3,64,256]{4,3,2,1,0:T(8,128)(2,1)} %all-to-all-done.q_ref.k_ref.v_ref, bf16[8,2,3,64,256]{4,3,2,1,0:T(8,128)(2,1)} %all-to-all-done.q_ref.k_ref.v_ref, ...), custom_call_target="tpu_custom_call" | custom-call | flops 20132659200 | bytes 8388608 | tf_op jit(solution)/shard_map/pair_forward/pallas_call | solution.py:282
  142.4 4.0 all-to-all-start.1
  149.3 2.9 copy-done.23
  152.2 3.3 slice.169
  158.7 4.2 all-to-all-start.2
  163.2 3.7 fusion.76
  166.9 6.2 fusion.77
  173.3 11.7 %collective-permute-done.3 = bf16[512,512]{1,0:T(8,128)(2,1)S(1)} collective-permute-done((bf16[512,512]{1,0:T(8,128)(2,1)}, bf16[512,512]{1,0:T(8,128)(2,1)S(1)}, u32[]{:S(2)}, u32[]{:S(2)}) %collective-permute-start.3) | collective-permute-done | bytes 524320 | tf_op jit(solution)/shard_map/ppermute | solution.py:394
  189.6 4.1 all-to-all-start.3
  193.9 9.6 %all-to-all-done.3.q_ref = bf16[8,2,1,64,256]{4,3,2,1,0:T(8,128)(2,1)} async-done(((bf16[8,2,1,64,256]{4,3,2,1,0:T(8,128)(2,1)}), bf16[8,2,1,64,256]{4,3,2,1,0:T(8,128)(2,1)}, u32[]{:S(2)}, u32[]{:S(2)}) %all-to-all-start.3) | async-done | bytes 524320 | tf_op jit(solution)/shard_map/all_to_all | solution.py:230
  203.5 15.0 %pair_forward.3 = (bf16[8,2,64,256]{3,2,1,0:T(8,128)(2,1)S(1)}, f32[8,2,64,256]{3,2,1,0:T(8,128)S(1)}, f32[8,2,1,256]{3,2,1,0:T(1,128)S(1)}) custom-call(s32[2]{0:T(128)S(1)} %dynamic_slice.124.len_ref, bf16[8,2,1,64,256]{4,3,2,1,0:T(8,128)(2,1)} %all-to-all-done.3.q_ref, bf16[8,2,2,64,256]{4,3,2,1,0:T(8,128)(2,1)S(1)} %all-to-all-done.2.k_ref.v_ref, ...), custom_call_target="tpu_custom_call" | custom-call | flops 14092861440 | bytes 8388608 | tf_op jit(solution)/shard_map/pair_forward/pallas_call | solution.py:282
  218.5 12.3 %all_to_all.45 = bf16[8,2,64,256]{3,2,1,0:T(8,128)(2,1)S(1)} all-to-all(bf16[8,2,64,256]{3,2,1,0:T(8,128)(2,1)S(1)} %get-tuple-element.83), channel_id=1, replica_groups=mesh['far'=2,'near'=2,'rows'=8] {'rows'}, dimensions={0} | all-to-all | bytes 1048576 | tf_op jit(solution)/shard_map/all_to_all | solution.py:230
  233.4 11.1 %collective-permute-done.4 = bf16[512,512]{1,0:T(8,128)(2,1)S(1)} collective-permute-done((bf16[512,512]{1,0:T(8,128)(2,1)S(1)}, bf16[512,512]{1,0:T(8,128)(2,1)S(1)}, u32[]{:S(2)}, u32[]{:S(2)}) %collective-permute-start.4) | collective-permute-done | bytes 524320 | tf_op jit(solution)/shard_map/ppermute | solution.py:394
  247.6 2.8 slice.177
  256.7 5.1 multiply_convert_fusion
  261.8 3.4 fusion.22
  265.2 4.8 convolution_convert_fusion.1
  269.9 4.4 convolution_convert_fusion.2
  274.4 7.8 %pad_maximum_fusion = bf16[2,2048,1024]{2,1,0:T(8,128)(2,1)} fusion(bf16[2,1024,1024]{2,1,0:T(8,128)(2,1)} %bitcast.330, bf16[2,1024,1024]{2,1,0:T(8,128)(2,1)} %bitcast.331), kind=kLoop, calls=%fused_computation.3 | loop fusion | flops 16777216 | bytes 16777216 | tf_op jit(solution)/shard_map/concatenate | solution.py:578
  284.7 5.0 fusion.82
  290.7 15.1 %collective-permute-done.5 = bf16[512,1024]{1,0:T(8,128)(2,1)} collective-permute-done((bf16[512,1024]{1,0:T(8,128)(2,1)}, bf16[512,1024]{1,0:T(8,128)(2,1)}, u32[]{:S(2)}, u32[]{:S(2)}) %collective-permute-start.5) | collective-permute-done | bytes 1048608 | tf_op jit(solution)/shard_map/ppermute | solution.py:394
  313.0 3.9 all-to-all-start.5
  321.3 11.2 %all-to-all-done.5.g_ref = bf16[8,2,64,256]{3,2,1,0:T(8,128)(2,1)S(1)} async-done(((bf16[8,2,64,256]{3,2,1,0:T(8,128)(2,1)}), bf16[8,2,64,256]{3,2,1,0:T(8,128)(2,1)S(1)}, u32[]{:S(2)}, u32[]{:S(2)}) %all-to-all-start.5) | async-done | bytes 524320 | tf_op jit(solution)/shard_map/all_to_all | solution.py:230
  334.9 22.9 %pair_backward.2 = bf16[8,2,3,64,256]{4,3,2,1,0:T(8,128)(2,1)} custom-call(s32[2]{0:T(128)S(1)} %dynamic_slice.124.len_ref, bf16[8,2,1,64,256]{4,3,2,1,0:T(8,128)(2,1)} %all-to-all-done.3.q_ref, bf16[8,2,2,64,256]{4,3,2,1,0:T(8,128)(2,1)S(1)} %all-to-all-done.2.k_ref.v_ref, bf16[8,2,2,64,256]{4,3,2,1,0:T(8,128)(2,1)S(1)} %all-to-all-done.2.k_ref.v_ref, ...), custom_call_target="tpu_custom_call" | custom-call | flops 20132659200 | bytes 8388608 | tf_op jit(solution)/shard_map/pair_backward/pallas_call | solution.py:364
  359.9 4.4 all-to-all-start.6
  365.1 25.7 %collective-permute-done.8 = bf16[256,1024]{1,0:T(8,128)(2,1)} collective-permute-done((bf16[256,1024]{1,0:T(8,128)(2,1)S(1)}, bf16[256,1024]{1,0:T(8,128)(2,1)}, u32[]{:S(2)}, u32[]{:S(2)}) %collective-permute-start.8) | collective-permute-done | bytes 524320 | tf_op jit(solution)/shard_map/ppermute | solution.py:394
  408.1 2.6 convolution_convert_fusion.7
  410.8 6.1 collective-permute-done.9
  416.8 2.6 fusion.33
  420.9 4.4 fusion.73
  427.1 4.1 all-to-all-start.7
  433.1 2.9 convolution_convert_fusion.8
  436.0 4.8 all-to-all-done.7.g_ref
  440.9 32.2 %pair_backward.3 = bf16[8,2,3,64,256]{4,3,2,1,0:T(8,128)(2,1)} custom-call(s32[2]{0:T(128)S(1)} %broadcast_13_len_ref.2.len_ref, bf16[8,2,3,64,256]{4,3,2,1,0:T(8,128)(2,1)} %all-to-all-done.q_ref.k_ref.v_ref, bf16[8,2,3,64,256]{4,3,2,1,0:T(8,128)(2,1)} %all-to-all-done.q_ref.k_ref.v_ref, bf16[8,2,3,64,256]{4,3,2,1,0:T(8,128)(2,1)} %all-to-all-done.q_ref.k_ref.v_ref, ...), custom_call_target="tpu_custom_call" | custom-call | flops 30198988800 | bytes 8388608 | tf_op jit(solution)/shard_map/pair_backward/pallas_call | solution.py:364
  473.0 6.2 collective-permute-done.11
  479.3 2.7 pad_maximum_fusion.5
  482.0 4.3 all-to-all-start.8
  490.2 6.3 fusion.2
  496.5 12.7 %collective-permute-done.12 = bf16[256,768]{1,0:T(8,128)(2,1)S(1)} collective-permute-done((bf16[256,768]{1,0:T(8,128)(2,1)S(1)}, bf16[256,768]{1,0:T(8,128)(2,1)S(1)}, u32[]{:S(2)}, u32[]{:S(2)}) %collective-permute-start.12) | collective-permute-done | bytes 393248 | tf_op jit(solution)/shard_map/ppermute | solution.py:394
  510.2 3.0 copy.113
  521.1 2.6 copy.130
  523.8 4.8 fusion.10
  533.7 13.1 %collective-permute-done.20 = bf16[128,1024]{1,0:T(8,128)(2,1)S(1)} collective-permute-done((bf16[128,1024]{1,0:T(8,128)(2,1)S(1)}, bf16[128,1024]{1,0:T(8,128)(2,1)S(1)}, u32[]{:S(2)}, u32[]{:S(2)}) %collective-permute-start.20) | collective-permute-done | bytes 262176 | tf_op jit(solution)/shard_map/ppermute | solution.py:394
  558.1 12.0 %all-gather.2 = bf16[16,80,256]{2,1,0:T(8,128)(2,1)S(1)} all-gather(bf16[2,80,256]{2,1,0:T(8,128)(2,1)S(1)} %pad_maximum_fusion.21), channel_id=4, replica_groups=mesh['far'=2,'near'=2,'rows'=8] {'rows'}, dimensions={0}, use_global_device_ids=true | all-gather | bytes 737280 | tf_op jit(solution)/shard_map/all_gather | solution.py:660
  570.3 3.6 collective-permute-start.16
  573.9 8.6 %collective-permute-done.16 = bf16[80,256]{1,0:T(8,128)(2,1)S(1)} collective-permute-done((bf16[80,256]{1,0:T(8,128)(2,1)S(1)}, bf16[80,256]{1,0:T(8,128)(2,1)S(1)}, u32[]{:S(2)}, u32[]{:S(2)}) %collective-permute-start.16) | collective-permute-done | bytes 40992 | tf_op jit(solution)/shard_map/ppermute | solution.py:394
  583.8 6.9 %slice_convert_fusion = (f32[1024,1024]{1,0:T(8,128)}, f32[1024,1024]{0,1:T(8,128)}) fusion(bf16[2048,1024]{1,0:T(8,128)(2,1)} %all-gather.12.cloned.1.call-done), kind=kLoop, calls=%fused_computation.52 | loop fusion | flops 2097152 | bytes 12582912 | tf_op jit(solution)/shard_map/convert_element_type | solution.py:667
  596.6 16.2 %collective-permute-done.17 = bf16[160,1024]{1,0:T(8,128)(2,1)S(1)} collective-permute-done((bf16[160,1024]{1,0:T(8,128)(2,1)S(1)}, bf16[160,1024]{1,0:T(8,128)(2,1)S(1)}, u32[]{:S(2)}, u32[]{:S(2)}) %collective-permute-start.17) | collective-permute-done | bytes 327712 | tf_op jit(solution)/shard_map/ppermute | solution.py:394
  625.3 3.0 copy.125
  629.5 6.0 collective-permute-done.19
  641.1 5.4 copy.127
  646.5 3.2 reverse_select_fusion.1
  657.1 3.7 copy.123
  (381 shorter events, 166.8 us)
Async XLA Ops:
  7.2 224.9 %copy-start = (bf16[4,256,1024]{2,1,0:T(8,128)(2,1)S(1)}, bf16[4,256,1024]{2,1,0:T(8,128)(2,1)}, u32[]{:S(2)}) copy-start(bf16[4,256,1024]{2,1,0:T(8,128)(2,1)} %param.31) | copy-start | bytes 6291460
  7.2 65.6 %all-gather.10.cloned.1.call-start = ((), (), s32[]{:S(2)}) async-start(), calls=%async_computation.12 | async-start | bytes 1769472 | tf_op jit(solution)/shard_map/all_gather | solution.py:444
  10.0 8.4 %copy-start.65 = (s32[4,256]{1,0:T(4,128)S(1)}, s32[4,256]{1,0:T(4,128)}, u32[]{:S(2)}) copy-start(s32[4,256]{1,0:T(4,128)} %param.17) | copy-start | bytes 12292
  12.7 18.1 %copy-start.61 = (bf16[32,2,1024]{2,1,0:T(2,128)(2,1)S(1)}, bf16[32,2,1024]{2,1,0:T(2,128)(2,1)}, u32[]{:S(2)}) copy-start(bf16[32,2,1024]{2,1,0:T(2,128)(2,1)} %param.20) | copy-start | bytes 393220
  12.7 20.0 %copy-start.48 = (bf16[2,1024,256]{2,1,0:T(8,128)(2,1)S(1)}, bf16[2,1024,256]{2,1,0:T(8,128)(2,1)}, u32[]{:S(2)}) copy-start(bf16[2,1024,256]{2,1,0:T(8,128)(2,1)} %param.25) | copy-start | bytes 3145732
  14.4 13.4 %collective-permute-start = (bf16[96,1024]{1,0:T(8,128)(2,1)}, bf16[96,1024]{1,0:T(8,128)(2,1)S(1)}, u32[]{:S(2)}, u32[]{:S(2)}) collective-permute-start(bf16[96,1024]{1,0:T(8,128)(2,1)} %constant_dynamic-slice_fusion.20), channel_id=1, source_target_pairs={{0,16},{16,0},{1,17},{17,1},{2,18},{18,2},{3,19},{19,3},{4,20},{20... | collective-permute-start | bytes 589832 | tf_op jit(solution)/shard_map/ppermute | solution.py:394
  19.9 11.5 %copy-start.62 = (f32[2,256]{1,0:T(2,128)}, f32[2,256]{1,0:T(2,128)S(1)}, u32[]{:S(2)}) copy-start(f32[2,256]{1,0:T(2,128)S(1)} %get-tuple-element.225) | copy-start | bytes 6148
  28.4 117.9 %all-gather.18.cloned.1.call-start = ((), (), s32[]{:S(2)}) async-start(), calls=%async_computation.19 | async-start | bytes 8257536 | tf_op jit(solution)/shard_map/all_gather | solution.py:522
  40.8 17.1 %collective-permute-start.1 = (bf16[160,1024]{1,0:T(8,128)(2,1)}, bf16[160,1024]{1,0:T(8,128)(2,1)}, u32[]{:S(2)}, u32[]{:S(2)}) collective-permute-start(bf16[160,1024]{1,0:T(8,128)(2,1)} %pad_maximum_fusion.19), channel_id=1, source_target_pairs={{0,16},{16,0},{1,17},{17,1},{2,18},{18,2},{3,19},{19,3},{4,20},{20... | collective-permute-start | bytes 983048 | tf_op jit(solution)/shard_map/ppermute | solution.py:394
  58.9 9.4 %collective-permute-start.2 = (bf16[2,96,1024]{2,1,0:T(8,128)(2,1)S(1)}, bf16[2,96,1024]{2,1,0:T(8,128)(2,1)S(1)}, u32[]{:S(2)}, u32[]{:S(2)}) collective-permute-start(bf16[2,96,1024]{2,1,0:T(8,128)(2,1)S(1)} %fusion.60), channel_id=1, source_target_pairs={{0,8},{8,0},{1,9},{9,1},{2,10},{10,2},{3,11},{11,3},{4,12},{12,4},... | collective-permute-start | bytes 1179656 | tf_op jit(solution)/shard_map/ppermute | solution.py:394
  83.0 29.9 %all-to-all-start = ((bf16[8,2,3,64,256]{4,3,2,1,0:T(8,128)(2,1)}), bf16[8,2,3,64,256]{4,3,2,1,0:T(8,128)(2,1)}, u32[]{:S(2)}, u32[]{:S(2)}) async-start(bf16[8,2,3,64,256]{4,3,2,1,0:T(8,128)(2,1)} %pad_maximum_fusion.7), calls=%async_computation | async-start | bytes 3145728 | tf_op jit(solution)/shard_map/all_to_all | solution.py:230
  87.3 27.4 %copy-start.67 = (bf16[1024]{0:T(1024)(128)(2,1)S(1)}, bf16[1024]{0:T(1024)(128)(2,1)}, u32[]{:S(2)}) copy-start(bf16[1024]{0:T(1024)(128)(2,1)} %param.23) | copy-start | bytes 6148
  87.3 160.2 %all-gather.20.cloned.1.call-start = ((), (), s32[]{:S(2)}) async-start(), calls=%async_computation.20 | async-start | bytes 8912896 | tf_op jit(solution)/shard_map/all_gather | solution.py:536
  142.4 14.9 %all-to-all-start.1 = ((bf16[8,2,64,256]{3,2,1,0:T(8,128)(2,1)}), bf16[8,2,64,256]{3,2,1,0:T(8,128)(2,1)S(1)}, u32[]{:S(2)}, u32[]{:S(2)}) async-start(bf16[8,2,64,256]{3,2,1,0:T(8,128)(2,1)} %get-tuple-element.78), calls=%async_computation.1 | async-start | bytes 1048576 | tf_op jit(solution)/shard_map/all_to_all | solution.py:230
  148.6 6.9 %copy-start.17 = (bf16[1024,1024]{1,0:T(8,128)(2,1)}, bf16[1024,1024]{1,0:T(8,128)(2,1)S(1)}, u32[]{:S(2)}) copy-start(bf16[1024,1024]{1,0:T(8,128)(2,1)S(1)} %constant_dynamic-update-slice_fusion.1) | copy-start | bytes 6291460
  158.7 30.8 %all-to-all-start.2 = ((bf16[8,2,2,64,256]{4,3,2,1,0:T(8,128)(2,1)}), bf16[8,2,2,64,256]{4,3,2,1,0:T(8,128)(2,1)S(1)}, u32[]{:S(2)}, u32[]{:S(2)}) async-start(bf16[8,2,2,64,256]{4,3,2,1,0:T(8,128)(2,1)} %pad_maximum_fusion.11), calls=%async_computation.2 | async-start | bytes 2097152 | tf_op jit(solution)/shard_map/all_to_all | solution.py:230
  162.9 22.0 %collective-permute-start.3 = (bf16[512,512]{1,0:T(8,128)(2,1)}, bf16[512,512]{1,0:T(8,128)(2,1)S(1)}, u32[]{:S(2)}, u32[]{:S(2)}) collective-permute-start(bf16[512,512]{1,0:T(8,128)(2,1)} %bitcast.337), channel_id=1, source_target_pairs={{0,8},{8,0},{1,9},{9,1},{2,10},{10,2},{3,11},{11,3},{4,12},{12,4},... | collective-permute-start | bytes 1572872 | tf_op jit(solution)/shard_map/ppermute | solution.py:394
  173.1 11.8 %copy-start.33 = (bf16[2,256,1024]{2,1,0:T(8,128)(2,1)S(1)}, bf16[2,256,1024]{2,1,0:T(8,128)(2,1)}, u32[]{:S(2)}) copy-start(bf16[2,256,1024]{2,1,0:T(8,128)(2,1)} %get-tuple-element.217) | copy-start | bytes 3145732
  173.1 11.8 %copy-start.38 = (bf16[64,8,2,256]{3,1,2,0:T(8,128)(2,1)S(1)}, bf16[64,8,2,256]{3,1,2,0:T(8,128)(2,1)}, u32[]{:S(2)}) copy-start(bf16[64,8,2,256]{3,1,2,0:T(8,128)(2,1)} %copy.137) | copy-start | bytes 1572868
  189.6 13.9 %all-to-all-start.3 = ((bf16[8,2,1,64,256]{4,3,2,1,0:T(8,128)(2,1)}), bf16[8,2,1,64,256]{4,3,2,1,0:T(8,128)(2,1)}, u32[]{:S(2)}, u32[]{:S(2)}) async-start(bf16[8,2,1,64,256]{4,3,2,1,0:T(8,128)(2,1)} %pad_maximum_fusion.17), calls=%async_computation.3 | async-start | bytes 1048576 | tf_op jit(solution)/shard_map/all_to_all | solution.py:230
  193.7 166.2 %reduce-scatter.4.cloned.1.call-start = ((), (), s32[]{:S(2)}) async-start(), calls=%async_computation.13 | async-start | bytes 9437184 | tf_op jit(solution)/shard_map/reduce_scatter | solution.py:567
  218.5 14.6 %copy-start.2 = (f32[8,2,64,256]{3,2,1,0:T(8,128)}, f32[8,2,64,256]{3,2,1,0:T(8,128)S(1)}, u32[]{:S(2)}) copy-start(f32[8,2,64,256]{3,2,1,0:T(8,128)S(1)} %get-tuple-element.91.wide_ref) | copy-start | bytes 3145732
  218.5 13.6 %copy-start.68 = (bf16[1024]{0:T(1024)(128)(2,1)S(1)}, bf16[1024]{0:T(1024)(128)(2,1)}, u32[]{:S(2)}) copy-start(bf16[1024]{0:T(1024)(128)(2,1)} %param.28) | copy-start | bytes 6148
  231.4 13.1 %copy-start.57 = (bf16[64,8,2,256]{3,1,2,0:T(8,128)(2,1)}, bf16[64,8,2,256]{3,1,2,0:T(8,128)(2,1)S(1)}, u32[]{:S(2)}) copy-start(bf16[64,8,2,256]{3,1,2,0:T(8,128)(2,1)S(1)} %copy.138) | copy-start | bytes 1572868
  231.4 13.1 %collective-permute-start.4 = (bf16[512,512]{1,0:T(8,128)(2,1)S(1)}, bf16[512,512]{1,0:T(8,128)(2,1)S(1)}, u32[]{:S(2)}, u32[]{:S(2)}) collective-permute-start(bf16[512,512]{1,0:T(8,128)(2,1)S(1)} %bitcast.367), channel_id=1, source_target_pairs={{0,8},{8,0},{1,9},{9,1},{2,10},{10,2},{3,11},{11,3},{4,12},{12,4},... | collective-permute-start | bytes 1572872 | tf_op jit(solution)/shard_map/ppermute | solution.py:394
  233.1 11.4 %copy-start.7 = (f32[512,1024]{1,0:T(8,128)S(1)}, f32[512,1024]{1,0:T(8,128)}, u32[]{:S(2)}) copy-start(f32[512,1024]{1,0:T(8,128)} %copy-done.6) | copy-start | bytes 6291460
  261.8 8.1 %copy-start.72 = (bf16[512,2048]{1,0:T(8,128)(2,1)}, bf16[512,2048]{1,0:T(8,128)(2,1)S(1)}, u32[]{:S(2)}) copy-start(bf16[512,2048]{1,0:T(8,128)(2,1)S(1)} %get-tuple-element.86) | copy-start | bytes 6291460
  282.2 23.7 %collective-permute-start.5 = (bf16[512,1024]{1,0:T(8,128)(2,1)}, bf16[512,1024]{1,0:T(8,128)(2,1)}, u32[]{:S(2)}, u32[]{:S(2)}) collective-permute-start(bf16[512,1024]{1,0:T(8,128)(2,1)} %fusion.22), channel_id=1, source_target_pairs={{0,8},{8,0},{1,9},{9,1},{2,10},{10,2},{3,11},{11,3},{4,12},{12,4},... | collective-permute-start | bytes 3145736 | tf_op jit(solution)/shard_map/ppermute | solution.py:394
  284.7 21.2 %copy-start.51 = (bf16[512,1024]{1,0:T(8,128)(2,1)S(1)}, bf16[512,1024]{1,0:T(8,128)(2,1)}, u32[]{:S(2)}) copy-start(bf16[512,1024]{1,0:T(8,128)(2,1)} %fusion.22) | copy-start | bytes 3145732
  289.8 18.0 %copy-start.40 = (f32[2,2,128,1024]{3,2,1,0:T(8,128)}, f32[2,2,128,1024]{3,2,1,0:T(8,128)S(1)}, u32[]{:S(2)}) copy-start(f32[2,2,128,1024]{3,2,1,0:T(8,128)S(1)} %fusion.82) | copy-start | bytes 6291460
  307.8 11.2 %collective-permute-start.6 = (bf16[256,1024]{1,0:T(8,128)(2,1)}, bf16[256,1024]{1,0:T(8,128)(2,1)}, u32[]{:S(2)}, u32[]{:S(2)}) collective-permute-start(bf16[256,1024]{1,0:T(8,128)(2,1)} %bitcast.39), channel_id=1, source_target_pairs={{0,8},{8,0},{1,9},{9,1},{2,10},{10,2},{3,11},{11,3},{4,12},{12,4},... | collective-permute-start | bytes 1572872 | tf_op jit(solution)/shard_map/ppermute | solution.py:394
  313.0 19.6 %all-to-all-start.5 = ((bf16[8,2,64,256]{3,2,1,0:T(8,128)(2,1)}), bf16[8,2,64,256]{3,2,1,0:T(8,128)(2,1)S(1)}, u32[]{:S(2)}, u32[]{:S(2)}) async-start(bf16[8,2,64,256]{3,2,1,0:T(8,128)(2,1)} %maximum_bitcast_fusion), calls=%async_computation.5 | async-start | bytes 1048576 | tf_op jit(solution)/shard_map/all_to_all | solution.py:230
  319.0 16.0 %copy-start.3 = (f32[8,2,64,256]{3,2,1,0:T(8,128)S(1)}, f32[8,2,64,256]{3,2,1,0:T(8,128)}, u32[]{:S(2)}) copy-start(f32[8,2,64,256]{3,2,1,0:T(8,128)} %copy-done.2) | copy-start | bytes 3145732
  332.5 25.3 %collective-permute-start.7 = (bf16[256,1024]{1,0:T(8,128)(2,1)}, bf16[256,1024]{1,0:T(8,128)(2,1)S(1)}, u32[]{:S(2)}, u32[]{:S(2)}) collective-permute-start(bf16[256,1024]{1,0:T(8,128)(2,1)} %fusion.44), channel_id=1, source_target_pairs={{0,16},{16,0},{1,17},{17,1},{2,18},{18,2},{3,19},{19,3},{4,20},{20... | collective-permute-start | bytes 1572872 | tf_op jit(solution)/shard_map/ppermute | solution.py:394
  359.9 30.9 %all-to-all-start.6 = ((bf16[8,2,3,64,256]{4,3,2,1,0:T(8,128)(2,1)}), bf16[8,2,3,64,256]{4,3,2,1,0:T(8,128)(2,1)}, u32[]{:S(2)}, u32[]{:S(2)}) async-start(bf16[8,2,3,64,256]{4,3,2,1,0:T(8,128)(2,1)} %pair_backward.2), calls=%async_computation.7 | async-start | bytes 3145728 | tf_op jit(solution)/shard_map/all_to_all | solution.py:230
  364.4 28.6 %copy-start.21 = (bf16[1,4,8,32,1024]{4,3,0,1,2:T(8,128)(2,1)S(1)}, bf16[1,4,8,32,1024]{4,3,0,1,2:T(8,128)(2,1)}, u32[]{:S(2)}) copy-start(bf16[1,4,8,32,1024]{4,3,0,1,2:T(8,128)(2,1)} %get-tuple-element.205) | copy-start | bytes 6291460
  364.4 117.6 %all-gather.12.cloned.1.call-start = ((), (), s32[]{:S(2)}) async-start(), calls=%async_computation.14 | async-start | bytes 4718592 | tf_op jit(solution)/shard_map/all_gather | solution.py:444
  364.5 26.4 %collective-permute-start.8 = (bf16[256,1024]{1,0:T(8,128)(2,1)S(1)}, bf16[256,1024]{1,0:T(8,128)(2,1)}, u32[]{:S(2)}, u32[]{:S(2)}) collective-permute-start(bf16[256,1024]{1,0:T(8,128)(2,1)S(1)} %dynamic-slice_bitcast_fusion), channel_id=1, source_target_pairs={{0,16},{16,0},{1,17},{17,1},{2,18},{18,2},{3,19},{19,3},{4,20},{20... | collective-permute-start | bytes 1572872 | tf_op jit(solution)/shard_map/ppermute | solution.py:394
  392.9 117.3 %reduce-scatter.6.cloned.1.call-start = ((), (), s32[]{:S(2)}) async-start(), calls=%async_computation.15 | async-start | bytes 4718592 | tf_op jit(solution)/shard_map/reduce_scatter | solution.py:567
  402.6 14.2 %collective-permute-start.9 = (bf16[512,512]{1,0:T(8,128)(2,1)}, bf16[512,512]{1,0:T(8,128)(2,1)}, u32[]{:S(2)}, u32[]{:S(2)}) collective-permute-start(bf16[512,512]{1,0:T(8,128)(2,1)} %bitcast.163), channel_id=1, source_target_pairs={{0,8},{8,0},{1,9},{9,1},{2,10},{10,2},{3,11},{11,3},{4,12},{12,4},... | collective-permute-start | bytes 1572872 | tf_op jit(solution)/shard_map/ppermute | solution.py:394
  408.1 8.7 %copy-start.14 = (bf16[1,4,8,32,1024]{4,3,2,1,0:T(8,128)(2,1)S(1)}, bf16[1,4,8,32,1024]{4,3,2,1,0:T(8,128)(2,1)}, u32[]{:S(2)}) copy-start(bf16[1,4,8,32,1024]{4,3,2,1,0:T(8,128)(2,1)} %copy.112) | copy-start | bytes 6291460
  425.7 7.4 %copy-start.39 = (bf16[64,8,2,256]{3,1,2,0:T(8,128)(2,1)S(1)}, bf16[64,8,2,256]{3,1,2,0:T(8,128)(2,1)}, u32[]{:S(2)}) copy-start(bf16[64,8,2,256]{3,1,2,0:T(8,128)(2,1)} %copy.137) | copy-start | bytes 1572868
  427.1 13.8 %copy-start.5 = (f32[8,2,64,256]{3,2,1,0:T(8,128)S(1)}, f32[8,2,64,256]{3,2,1,0:T(8,128)}, u32[]{:S(2)}) copy-start(f32[8,2,64,256]{3,2,1,0:T(8,128)} %copy-done.4) | copy-start | bytes 3145732
  427.1 13.8 %all-to-all-start.7 = ((bf16[8,2,64,256]{3,2,1,0:T(8,128)(2,1)}), bf16[8,2,64,256]{3,2,1,0:T(8,128)(2,1)S(1)}, u32[]{:S(2)}, u32[]{:S(2)}) async-start(bf16[8,2,64,256]{3,2,1,0:T(8,128)(2,1)} %maximum_bitcast_fusion.1), calls=%async_computation.8 | async-start | bytes 1048576 | tf_op jit(solution)/shard_map/all_to_all | solution.py:230
  431.1 50.9 %collective-permute-start.10 = (bf16[512,1024]{1,0:T(8,128)(2,1)S(1)}, bf16[512,1024]{1,0:T(8,128)(2,1)}, u32[]{:S(2)}, u32[]{:S(2)}) collective-permute-start(bf16[512,1024]{1,0:T(8,128)(2,1)S(1)} %convolution_convert_fusion.7), channel_id=1, source_target_pairs={{0,8},{8,0},{1,9},{9,1},{2,10},{10,2},{3,11},{11,3},{4,12},{12,4},... | collective-permute-start | bytes 3145736 | tf_op jit(solution)/shard_map/ppermute | solution.py:394
  431.3 47.9 %collective-permute-start.11 = (bf16[2,256,1024]{2,1,0:T(8,128)(2,1)}, bf16[2,256,1024]{2,1,0:T(8,128)(2,1)}, u32[]{:S(2)}, u32[]{:S(2)}) collective-permute-start(bf16[2,256,1024]{2,1,0:T(8,128)(2,1)} %pad_maximum_fusion.12), channel_id=1, source_target_pairs={{0,8},{8,0},{1,9},{9,1},{2,10},{10,2},{3,11},{11,3},{4,12},{12,4},... | collective-permute-start | bytes 3145736 | tf_op jit(solution)/shard_map/ppermute | solution.py:394
  440.9 38.4 %copy-start.35 = (bf16[2,256,1024]{2,1,0:T(8,128)(2,1)S(1)}, bf16[2,256,1024]{2,1,0:T(8,128)(2,1)}, u32[]{:S(2)}) copy-start(bf16[2,256,1024]{2,1,0:T(8,128)(2,1)} %pad_maximum_fusion.12) | copy-start | bytes 3145732
  482.0 28.2 %all-to-all-start.8 = ((bf16[8,2,3,64,256]{4,3,2,1,0:T(8,128)(2,1)}), bf16[8,2,3,64,256]{4,3,2,1,0:T(8,128)(2,1)}, u32[]{:S(2)}, u32[]{:S(2)}) async-start(bf16[8,2,3,64,256]{4,3,2,1,0:T(8,128)(2,1)} %pair_backward.3), calls=%async_computation.9 | async-start | bytes 3145728 | tf_op jit(solution)/shard_map/all_to_all | solution.py:230
  486.3 97.4 %reduce-scatter.8.cloned.1.call-start = ((), (), s32[]{:S(2)}) async-start(), calls=%async_computation.16 | async-start | bytes 5898240 | tf_op jit(solution)/shard_map/reduce_scatter | solution.py:567
  488.8 20.5 %collective-permute-start.12 = (bf16[256,768]{1,0:T(8,128)(2,1)S(1)}, bf16[256,768]{1,0:T(8,128)(2,1)S(1)}, u32[]{:S(2)}, u32[]{:S(2)}) collective-permute-start(bf16[256,768]{1,0:T(8,128)(2,1)S(1)} %convolution_convert_fusion.15), channel_id=1, source_target_pairs={{0,16},{16,0},{1,17},{17,1},{2,18},{18,2},{3,19},{19,3},{4,20},{20... | collective-permute-start | bytes 1179656 | tf_op jit(solution)/shard_map/ppermute | solution.py:394
  518.4 100.2 %all-gather.16.cloned.1.call-start = ((), (), s32[]{:S(2)}) async-start(), calls=%async_computation.18 | async-start | bytes 2359296 | tf_op jit(solution)/shard_map/all_gather | solution.py:444
  523.8 7.9 %copy-start.28 = (f32[512,1024]{1,0:T(8,128)S(1)}, f32[512,1024]{1,0:T(8,128)}, u32[]{:S(2)}) copy-start(f32[512,1024]{1,0:T(8,128)} %get-tuple-element.197) | copy-start | bytes 6291460
  529.5 19.6 %collective-permute-start.13 = (bf16[256,1024]{1,0:T(8,128)(2,1)}, bf16[256,1024]{1,0:T(8,128)(2,1)S(1)}, u32[]{:S(2)}, u32[]{:S(2)}) collective-permute-start(bf16[256,1024]{1,0:T(8,128)(2,1)} %bitcast.81), channel_id=1, source_target_pairs={{0,8},{8,0},{1,9},{9,1},{2,10},{10,2},{3,11},{11,3},{4,12},{12,4},... | collective-permute-start | bytes 1572872 | tf_op jit(solution)/shard_map/ppermute | solution.py:394
  529.6 17.3 %collective-permute-start.20 = (bf16[128,1024]{1,0:T(8,128)(2,1)S(1)}, bf16[128,1024]{1,0:T(8,128)(2,1)S(1)}, u32[]{:S(2)}, u32[]{:S(2)}) collective-permute-start(bf16[128,1024]{1,0:T(8,128)(2,1)S(1)} %dynamic-slice_bitcast_fusion.2), channel_id=1, source_target_pairs={{0,16},{16,0},{1,17},{17,1},{2,18},{18,2},{3,19},{19,3},{4,20},{20... | collective-permute-start | bytes 786440 | tf_op jit(solution)/shard_map/ppermute | solution.py:394
  547.7 104.7 %all-gather.14.cloned.1.call-start = ((), (), s32[]{:S(2)}) async-start(), calls=%async_computation.17 | async-start | bytes 2949120 | tf_op jit(solution)/shard_map/all_gather | solution.py:444
  552.9 5.0 collective-permute-start.15
  555.3 27.2 %collective-permute-start.14 = (bf16[256,1024]{1,0:T(8,128)(2,1)}, bf16[256,1024]{1,0:T(8,128)(2,1)S(1)}, u32[]{:S(2)}, u32[]{:S(2)}) collective-permute-start(bf16[256,1024]{1,0:T(8,128)(2,1)} %fusion.42), channel_id=1, source_target_pairs={{0,16},{16,0},{1,17},{17,1},{2,18},{18,2},{3,19},{19,3},{4,20},{20... | collective-permute-start | bytes 1572872 | tf_op jit(solution)/shard_map/ppermute | solution.py:394
  570.3 12.2 %collective-permute-start.16 = (bf16[80,256]{1,0:T(8,128)(2,1)S(1)}, bf16[80,256]{1,0:T(8,128)(2,1)S(1)}, u32[]{:S(2)}, u32[]{:S(2)}) collective-permute-start(bf16[80,256]{1,0:T(8,128)(2,1)S(1)} %dynamic-slice_bitcast_fusion.3), channel_id=1, source_target_pairs={{0,16},{16,0},{1,17},{17,1},{2,18},{18,2},{3,19},{19,3},{4,20},{20... | collective-permute-start | bytes 122888 | tf_op jit(solution)/shard_map/ppermute | solution.py:394
  583.7 7.1 %copy-start.13 = (bf16[2,2,256,1024]{3,2,1,0:T(8,128)(2,1)S(1)}, bf16[2,2,256,1024]{3,2,1,0:T(8,128)(2,1)}, u32[]{:S(2)}) copy-start(bf16[2,2,256,1024]{3,2,1,0:T(8,128)(2,1)} %pad_maximum_fusion.5) | copy-start | bytes 6291460
  583.7 31.4 %collective-permute-start.18 = (bf16[2,256,1024]{2,1,0:T(8,128)(2,1)S(1)}, bf16[2,256,1024]{2,1,0:T(8,128)(2,1)}, u32[]{:S(2)}, u32[]{:S(2)}) collective-permute-start(bf16[2,256,1024]{2,1,0:T(8,128)(2,1)S(1)} %pad_maximum_fusion.13), channel_id=1, source_target_pairs={{0,8},{8,0},{1,9},{9,1},{2,10},{10,2},{3,11},{11,3},{4,12},{12,4},... | collective-permute-start | bytes 3145736 | tf_op jit(solution)/shard_map/ppermute | solution.py:394
  592.0 20.8 %collective-permute-start.17 = (bf16[160,1024]{1,0:T(8,128)(2,1)S(1)}, bf16[160,1024]{1,0:T(8,128)(2,1)S(1)}, u32[]{:S(2)}, u32[]{:S(2)}) collective-permute-start(bf16[160,1024]{1,0:T(8,128)(2,1)S(1)} %dynamic-slice_bitcast_fusion.1), channel_id=1, source_target_pairs={{0,16},{16,0},{1,17},{17,1},{2,18},{18,2},{3,19},{19,3},{4,20},{20... | collective-permute-start | bytes 983048 | tf_op jit(solution)/shard_map/ppermute | solution.py:394
  616.6 19.0 %collective-permute-start.19 = (bf16[2,256,768]{2,1,0:T(8,128)(2,1)}, bf16[2,256,768]{2,1,0:T(8,128)(2,1)}, u32[]{:S(2)}, u32[]{:S(2)}) collective-permute-start(bf16[2,256,768]{2,1,0:T(8,128)(2,1)} %pad_maximum_fusion.16), channel_id=1, source_target_pairs={{0,8},{8,0},{1,9},{9,1},{2,10},{10,2},{3,11},{11,3},{4,12},{12,4},... | collective-permute-start | bytes 2359304 | tf_op jit(solution)/shard_map/ppermute | solution.py:394
  625.3 10.2 %copy-start.37 = (bf16[2,256,768]{2,1,0:T(8,128)(2,1)S(1)}, bf16[2,256,768]{2,1,0:T(8,128)(2,1)}, u32[]{:S(2)}) copy-start(bf16[2,256,768]{2,1,0:T(8,128)(2,1)} %pad_maximum_fusion.16) | copy-start | bytes 2359300
  657.1 5.8 copy-start.1
  (52 other events, 110.0 us)
Sparse Core Ops, SparseCore 0:
  28.5 26.8 all-gather.9
  69.5 59.3 all-gather.17
  131.9 82.0 all-gather.19
  282.3 75.7 reduce-scatter.3
  393.0 36.0 all-gather.11
  433.3 51.3 reduce-scatter.5
  518.5 57.1 reduce-scatter.7
  578.3 27.4 all-gather.15
  616.7 30.1 all-gather.13

commit v15 on v14

--- a/solution.py
+++ b/solution.py
@@ -577,8 +577,10 @@
 
     hidden_terms = jnp.concatenate(
         [
-            mul(value, against, TN).astype(LOW).reshape(2, hidden, width)
-            for value, against in ((activated, grad_low), (grad_pre, normed_three))
+            mul(activated, grad_low, TN).astype(LOW).reshape(2, hidden, width),
+            jnp.stack(
+                [mul(normed_three, value, TN).astype(LOW) for value in jnp.split(grad_pre, 2, axis=1)]
+            ),
         ],
         axis=1,
     )
@@ -664,12 +666,11 @@
     input_four = jnp.stack([input_two, swap(input_two, "near")])
     patch_four = jnp.stack([patch_two, swap(patch_two, "near")])
     outputs = over_heads(result_four)
-    hidden_gradients = [hidden_total[hidden:].T.astype(WIDE), hidden_total[:hidden].astype(WIDE)]
+    hidden_gradients = [hidden_total[hidden:].astype(WIDE), hidden_total[:hidden].astype(WIDE)]
     last_own, last_away = own_and_away(last_part)
-    last_sum, input_four, outputs, hidden_gradients = tie(
-        add_far(last_own, swap(last_away, "far")), input_four, outputs, hidden_gradients
-    )
+    last_sum, input_four = tie(add_far(last_own, swap(last_away, "far")), input_four)
     last_total = join_rows(last_sum)
+    middle_total, outputs, hidden_gradients = tie(middle_total, outputs, hidden_gradients)
     input_four, patch_four = tie(input_four, patch_four)
     input_grads, patch_grads = over_heads(input_four), over_heads(patch_four)
 

time: 680 us -> 681 us (level)
  Pallas kernels: 89 us -> 101 us
  waiting for transfers between devices: 220 us -> 230 us
    ppermute x21, waiting for transfers between devices: 170 us -> 181 us  [swap(): return lax.ppermute(value, axis, [(0, 1), (1, 0)])]
    pallas_call x2, Pallas kernels: 55 us -> 64 us  [pair_backward(): pl.pallas_call(kernel, grid_spec=pltpu.PrefetchScalarGridSpec(num_scalar_...]
    dot_general x31 -> x32, matrix products: 61.1 us -> 57.4 us  [mul(): return lax.dot_general(left, right, dims, preferred_element_type=WIDE)]
    unnamed x171 -> x178, local copies, waits for them, and re-layouts: 40.8 us -> 40 us
  transfers between devices with their start and end apart: 38 -> 38, of which waited for: 22 -> 22; matrix products, arithmetic and copies ran while one was open for 28% -> 26% of each run, Pallas kernels for 13% -> 15%
where the time goes in v15:
time: 681 us; the launch traced here: 674 us
  waiting for transfers between devices  230 us (34%)
  local copies, waits for them, and re-layouts  109 us (16%)
  Pallas kernels  101 us (15%)
  other arithmetic  83 us (12%)
  matrix products  58.4 us (9%)
  starting transfers between devices  52.9 us (8%)
  blocking collectives  25.1 us (4%)
  between operations  15.5 us (2%)
    ppermute x21, waiting for transfers between devices, swap(): return lax.ppermute(value, axis, [(0, 1), (1, 0)])  181 us
    pallas_call x2, Pallas kernels, pair_backward(): pl.pallas_call(kernel, grid_spec=pltpu.PrefetchScalarGridSpec(num_scalar_...  64 us
    dot_general x32, matrix products, mul(): return lax.dot_general(left, right, dims, preferred_element_type=WIDE)  57.4 us
    all_to_all x8, waiting for transfers between devices, exchange_rows(): return lax.all_to_all(value, 'rows', 0, 0, tiled=True)  49.3 us
    unnamed x178, local copies, waits for them, and re-layouts  40 us
    pallas_call x2, Pallas kernels, pair_forward(): pl.pallas_call(kernel, grid_spec=pltpu.PrefetchScalarGridSpec(num_scalar_...  37 us
    all_to_all x8, starting transfers between devices, exchange_rows(): return lax.all_to_all(value, 'rows', 0, 0, tiled=True)  32.7 us
    ppermute x21, starting transfers between devices, swap(): return lax.ppermute(value, axis, [(0, 1), (1, 0)])  19.8 us
  transfers between devices with their start and end apart: 38, of which 22 were waited for; matrix products, arithmetic and copies ran while one was open for 26% of the time, Pallas kernels for 15%

profile of v15, /device:TPU:0, one launch (start us, length us, event | category | flops | bytes accessed | tf_op | source)
XLA Modules:
  0.0 674.5 jit_solution(5783349965999781092)
XLA Ops:
  7.2 2.7 copy.94
  10.0 2.7 copy.95
  14.4 4.0 collective-permute-start
  19.9 7.8 %collective-permute-done = bf16[96,1024]{1,0:T(8,128)(2,1)S(1)} collective-permute-done((bf16[96,1024]{1,0:T(8,128)(2,1)}, bf16[96,1024]{1,0:T(8,128)(2,1)S(1)}, u32[]{:S(2)}, u32[]{:S(2)}) %collective-permute-start) | collective-permute-done | bytes 196640 | tf_op jit(solution)/shard_map/ppermute | solution.py:394
  40.9 17.1 %collective-permute-done.1 = bf16[160,1024]{1,0:T(8,128)(2,1)} collective-permute-done((bf16[160,1024]{1,0:T(8,128)(2,1)}, bf16[160,1024]{1,0:T(8,128)(2,1)}, u32[]{:S(2)}, u32[]{:S(2)}) %collective-permute-start.1) | collective-permute-done | bytes 327712 | tf_op jit(solution)/shard_map/ppermute | solution.py:394
  59.9 8.5 %collective-permute-done.2 = bf16[2,96,1024]{2,1,0:T(8,128)(2,1)S(1)} collective-permute-done((bf16[2,96,1024]{2,1,0:T(8,128)(2,1)S(1)}, bf16[2,96,1024]{2,1,0:T(8,128)(2,1)S(1)}, u32[]{:S(2)}, u32[]{:S(2)}) %collective-permute-start.2) | collective-permute-done | bytes 393248 | tf_op jit(solution)/shard_map/ppermute | solution.py:394
  72.8 2.8 constant_dynamic-update-slice_fusion.3
  75.5 3.3 convolution_convert_fusion.2
  78.8 2.9 convolution_convert_fusion.3
  83.0 4.3 all-to-all-start
  89.2 23.8 %all-to-all-done.q_ref.k_ref.v_ref = bf16[8,2,3,64,256]{4,3,2,1,0:T(8,128)(2,1)} async-done(((bf16[8,2,3,64,256]{4,3,2,1,0:T(8,128)(2,1)}), bf16[8,2,3,64,256]{4,3,2,1,0:T(8,128)(2,1)}, u32[]{:S(2)}, u32[]{:S(2)}) %all-to-all-start) | async-done | bytes 1572896 | tf_op jit(solution)/shard_map/all_to_all | solution.py:230
  122.4 19.0 %pair_forward.2 = (bf16[8,2,64,256]{3,2,1,0:T(8,128)(2,1)}, f32[8,2,64,256]{3,2,1,0:T(8,128)S(1)}, f32[8,2,1,256]{3,2,1,0:T(1,128)S(1)}) custom-call(s32[2]{0:T(128)S(1)} %broadcast_13_len_ref.2.len_ref, bf16[8,2,3,64,256]{4,3,2,1,0:T(8,128)(2,1)} %all-to-all-done.q_ref.k_ref.v_ref, bf16[8,2,3,64,256]{4,3,2,1,0:T(8,128)(2,1)} %all-to-all-done.q_ref.k_ref.v_ref, ...), custom_call_target="tpu_custom_call" | custom-call | flops 20132659200 | bytes 8388608 | tf_op jit(solution)/shard_map/pair_forward/pallas_call | solution.py:282
  142.3 3.8 all-to-all-start.1
  149.1 2.9 copy-done.24
  152.0 3.3 slice.169
  158.5 4.2 all-to-all-start.2
  162.9 3.7 fusion.78
  166.7 6.2 fusion.79
  173.1 11.7 %collective-permute-done.3 = bf16[512,512]{1,0:T(8,128)(2,1)S(1)} collective-permute-done((bf16[512,512]{1,0:T(8,128)(2,1)}, bf16[512,512]{1,0:T(8,128)(2,1)S(1)}, u32[]{:S(2)}, u32[]{:S(2)}) %collective-permute-start.3) | collective-permute-done | bytes 524320 | tf_op jit(solution)/shard_map/ppermute | solution.py:394
  189.3 4.1 all-to-all-start.3
  193.5 9.6 %all-to-all-done.3.q_ref = bf16[8,2,1,64,256]{4,3,2,1,0:T(8,128)(2,1)} async-done(((bf16[8,2,1,64,256]{4,3,2,1,0:T(8,128)(2,1)}), bf16[8,2,1,64,256]{4,3,2,1,0:T(8,128)(2,1)}, u32[]{:S(2)}, u32[]{:S(2)}) %all-to-all-start.3) | async-done | bytes 524320 | tf_op jit(solution)/shard_map/all_to_all | solution.py:230
  203.2 18.0 %pair_forward.3 = (bf16[8,2,64,256]{3,2,1,0:T(8,128)(2,1)S(1)}, f32[8,2,64,256]{3,2,1,0:T(8,128)S(1)}, f32[8,2,1,256]{3,2,1,0:T(1,128)S(1)}) custom-call(s32[2]{0:T(128)S(1)} %dynamic_slice.124.len_ref, bf16[8,2,1,64,256]{4,3,2,1,0:T(8,128)(2,1)} %all-to-all-done.3.q_ref, bf16[8,2,2,64,256]{4,3,2,1,0:T(8,128)(2,1)S(1)} %all-to-all-done.2.k_ref.v_ref, ...), custom_call_target="tpu_custom_call" | custom-call | flops 14092861440 | bytes 8388608 | tf_op jit(solution)/shard_map/pair_forward/pallas_call | solution.py:282
  221.2 12.8 %all_to_all.45 = bf16[8,2,64,256]{3,2,1,0:T(8,128)(2,1)S(1)} all-to-all(bf16[8,2,64,256]{3,2,1,0:T(8,128)(2,1)S(1)} %get-tuple-element.84), channel_id=1, replica_groups=mesh['far'=2,'near'=2,'rows'=8] {'rows'}, dimensions={0} | all-to-all | bytes 1048576 | tf_op jit(solution)/shard_map/all_to_all | solution.py:230
  236.3 11.4 %collective-permute-done.4 = bf16[512,512]{1,0:T(8,128)(2,1)S(1)} collective-permute-done((bf16[512,512]{1,0:T(8,128)(2,1)S(1)}, bf16[512,512]{1,0:T(8,128)(2,1)S(1)}, u32[]{:S(2)}, u32[]{:S(2)}) %collective-permute-start.4) | collective-permute-done | bytes 524320 | tf_op jit(solution)/shard_map/ppermute | solution.py:394
  251.7 2.8 slice.177
  260.8 6.0 multiply_convert_fusion
  266.8 3.3 fusion.22
  275.2 4.3 maximum_maximum_fusion
  281.5 4.9 fusion.84
  288.6 14.5 %collective-permute-done.5 = bf16[512,1024]{1,0:T(8,128)(2,1)} collective-permute-done((bf16[512,1024]{1,0:T(8,128)(2,1)}, bf16[512,1024]{1,0:T(8,128)(2,1)}, u32[]{:S(2)}, u32[]{:S(2)}) %collective-permute-start.5) | collective-permute-done | bytes 1048608 | tf_op jit(solution)/shard_map/ppermute | solution.py:394
  310.6 3.7 all-to-all-start.5
  318.8 11.1 %all-to-all-done.5.g_ref = bf16[8,2,64,256]{3,2,1,0:T(8,128)(2,1)S(1)} async-done(((bf16[8,2,64,256]{3,2,1,0:T(8,128)(2,1)}), bf16[8,2,64,256]{3,2,1,0:T(8,128)(2,1)S(1)}, u32[]{:S(2)}, u32[]{:S(2)}) %all-to-all-start.5) | async-done | bytes 524320 | tf_op jit(solution)/shard_map/all_to_all | solution.py:230
  329.9 31.8 %pair_backward.2 = bf16[8,2,3,64,256]{4,3,2,1,0:T(8,128)(2,1)} custom-call(s32[2]{0:T(128)S(1)} %dynamic_slice.124.len_ref, bf16[8,2,1,64,256]{4,3,2,1,0:T(8,128)(2,1)} %all-to-all-done.3.q_ref, bf16[8,2,2,64,256]{4,3,2,1,0:T(8,128)(2,1)S(1)} %all-to-all-done.2.k_ref.v_ref, bf16[8,2,2,64,256]{4,3,2,1,0:T(8,128)(2,1)S(1)} %all-to-all-done.2.k_ref.v_ref, ...), custom_call_target="tpu_custom_call" | custom-call | flops 20132659200 | bytes 8388608 | tf_op jit(solution)/shard_map/pair_backward/pallas_call | solution.py:364
  363.9 4.4 all-to-all-start.6
  368.5 26.4 %collective-permute-done.8 = bf16[256,1024]{1,0:T(8,128)(2,1)} collective-permute-done((bf16[256,1024]{1,0:T(8,128)(2,1)S(1)}, bf16[256,1024]{1,0:T(8,128)(2,1)}, u32[]{:S(2)}, u32[]{:S(2)}) %collective-permute-start.8) | collective-permute-done | bytes 524320 | tf_op jit(solution)/shard_map/ppermute | solution.py:394
  409.8 2.6 pad_maximum_fusion.1
  412.4 2.6 convolution_convert_fusion.6
  415.1 5.3 collective-permute-done.9
  420.4 2.6 fusion.33
  424.4 4.4 fusion.75
  430.6 3.9 all-to-all-start.7
  436.5 2.9 convolution_convert_fusion.7
  439.4 4.8 all-to-all-done.7.g_ref
  444.2 32.2 %pair_backward.3 = bf16[8,2,3,64,256]{4,3,2,1,0:T(8,128)(2,1)} custom-call(s32[2]{0:T(128)S(1)} %broadcast_13_len_ref.2.len_ref, bf16[8,2,3,64,256]{4,3,2,1,0:T(8,128)(2,1)} %all-to-all-done.q_ref.k_ref.v_ref, bf16[8,2,3,64,256]{4,3,2,1,0:T(8,128)(2,1)} %all-to-all-done.q_ref.k_ref.v_ref, bf16[8,2,3,64,256]{4,3,2,1,0:T(8,128)(2,1)} %all-to-all-done.q_ref.k_ref.v_ref, ...), custom_call_target="tpu_custom_call" | custom-call | flops 30198988800 | bytes 8388608 | tf_op jit(solution)/shard_map/pair_backward/pallas_call | solution.py:364
  476.4 6.2 collective-permute-done.11
  482.6 2.7 pad_maximum_fusion.4
  485.3 4.3 all-to-all-start.8
  493.9 6.3 fusion.2
  500.2 12.4 %collective-permute-done.12 = bf16[256,768]{1,0:T(8,128)(2,1)S(1)} collective-permute-done((bf16[256,768]{1,0:T(8,128)(2,1)S(1)}, bf16[256,768]{1,0:T(8,128)(2,1)S(1)}, u32[]{:S(2)}, u32[]{:S(2)}) %collective-permute-start.12) | collective-permute-done | bytes 393248 | tf_op jit(solution)/shard_map/ppermute | solution.py:394
  513.6 3.0 copy.110
  524.4 2.6 copy.126
  527.1 4.6 fusion.10
  532.7 2.6 collective-permute-start.13
  537.4 12.6 %collective-permute-done.13 = bf16[128,1024]{1,0:T(8,128)(2,1)S(1)} collective-permute-done((bf16[128,1024]{1,0:T(8,128)(2,1)S(1)}, bf16[128,1024]{1,0:T(8,128)(2,1)S(1)}, u32[]{:S(2)}, u32[]{:S(2)}) %collective-permute-start.13) | collective-permute-done | bytes 262176 | tf_op jit(solution)/shard_map/ppermute | solution.py:394
  561.0 12.3 %all-gather.2 = bf16[16,80,256]{2,1,0:T(8,128)(2,1)S(1)} all-gather(bf16[2,80,256]{2,1,0:T(8,128)(2,1)S(1)} %pad_maximum_fusion.20), channel_id=4, replica_groups=mesh['far'=2,'near'=2,'rows'=8] {'rows'}, dimensions={0}, use_global_device_ids=true | all-gather | bytes 737280 | tf_op jit(solution)/shard_map/all_gather | solution.py:662
  575.2 11.0 %collective-permute-done.17 = bf16[80,256]{1,0:T(8,128)(2,1)S(1)} collective-permute-done((bf16[80,256]{1,0:T(8,128)(2,1)S(1)}, bf16[80,256]{1,0:T(8,128)(2,1)S(1)}, u32[]{:S(2)}, u32[]{:S(2)}) %collective-permute-start.17) | collective-permute-done | bytes 40992 | tf_op jit(solution)/shard_map/ppermute | solution.py:394
  590.7 26.3 %collective-permute-done.18 = bf16[160,1024]{1,0:T(8,128)(2,1)S(1)} collective-permute-done((bf16[160,1024]{1,0:T(8,128)(2,1)S(1)}, bf16[160,1024]{1,0:T(8,128)(2,1)S(1)}, u32[]{:S(2)}, u32[]{:S(2)}) %collective-permute-start.18) | collective-permute-done | bytes 327712 | tf_op jit(solution)/shard_map/ppermute | solution.py:394
  620.2 2.9 pad_maximum_fusion.5
  626.8 4.4 slice_convert_fusion
  634.7 2.5 copy.121
  639.1 3.0 copy.122
  643.3 6.5 collective-permute-done.20
  654.5 2.6 fusion.14
  661.9 3.7 copy.120
  (390 shorter events, 161.3 us)
Async XLA Ops:
  7.2 227.8 %copy-start = (bf16[4,256,1024]{2,1,0:T(8,128)(2,1)S(1)}, bf16[4,256,1024]{2,1,0:T(8,128)(2,1)}, u32[]{:S(2)}) copy-start(bf16[4,256,1024]{2,1,0:T(8,128)(2,1)} %param.31) | copy-start | bytes 6291460
  7.2 65.6 %all-gather.10.cloned.1.call-start = ((), (), s32[]{:S(2)}) async-start(), calls=%async_computation.12 | async-start | bytes 1769472 | tf_op jit(solution)/shard_map/all_gather | solution.py:444
  10.0 8.4 %copy-start.69 = (s32[4,256]{1,0:T(4,128)S(1)}, s32[4,256]{1,0:T(4,128)}, u32[]{:S(2)}) copy-start(s32[4,256]{1,0:T(4,128)} %param.17) | copy-start | bytes 12292
  12.7 18.1 %copy-start.65 = (bf16[32,2,1024]{2,1,0:T(2,128)(2,1)S(1)}, bf16[32,2,1024]{2,1,0:T(2,128)(2,1)}, u32[]{:S(2)}) copy-start(bf16[32,2,1024]{2,1,0:T(2,128)(2,1)} %param.20) | copy-start | bytes 393220
  12.7 20.0 %copy-start.53 = (bf16[2,1024,256]{2,1,0:T(8,128)(2,1)S(1)}, bf16[2,1024,256]{2,1,0:T(8,128)(2,1)}, u32[]{:S(2)}) copy-start(bf16[2,1024,256]{2,1,0:T(8,128)(2,1)} %param.25) | copy-start | bytes 3145732
  14.4 13.4 %collective-permute-start = (bf16[96,1024]{1,0:T(8,128)(2,1)}, bf16[96,1024]{1,0:T(8,128)(2,1)S(1)}, u32[]{:S(2)}, u32[]{:S(2)}) collective-permute-start(bf16[96,1024]{1,0:T(8,128)(2,1)} %constant_dynamic-slice_fusion.20), channel_id=1, source_target_pairs={{0,16},{16,0},{1,17},{17,1},{2,18},{18,2},{3,19},{19,3},{4,20},{20... | collective-permute-start | bytes 589832 | tf_op jit(solution)/shard_map/ppermute | solution.py:394
  19.9 11.5 %copy-start.66 = (f32[2,256]{1,0:T(2,128)}, f32[2,256]{1,0:T(2,128)S(1)}, u32[]{:S(2)}) copy-start(f32[2,256]{1,0:T(2,128)S(1)} %get-tuple-element.227) | copy-start | bytes 6148
  28.4 117.7 %all-gather.18.cloned.1.call-start = ((), (), s32[]{:S(2)}) async-start(), calls=%async_computation.19 | async-start | bytes 8257536 | tf_op jit(solution)/shard_map/all_gather | solution.py:522
  40.8 17.1 %collective-permute-start.1 = (bf16[160,1024]{1,0:T(8,128)(2,1)}, bf16[160,1024]{1,0:T(8,128)(2,1)}, u32[]{:S(2)}, u32[]{:S(2)}) collective-permute-start(bf16[160,1024]{1,0:T(8,128)(2,1)} %pad_maximum_fusion.18), channel_id=1, source_target_pairs={{0,16},{16,0},{1,17},{17,1},{2,18},{18,2},{3,19},{19,3},{4,20},{20... | collective-permute-start | bytes 983048 | tf_op jit(solution)/shard_map/ppermute | solution.py:394
  58.9 9.4 %collective-permute-start.2 = (bf16[2,96,1024]{2,1,0:T(8,128)(2,1)S(1)}, bf16[2,96,1024]{2,1,0:T(8,128)(2,1)S(1)}, u32[]{:S(2)}, u32[]{:S(2)}) collective-permute-start(bf16[2,96,1024]{2,1,0:T(8,128)(2,1)S(1)} %fusion.62), channel_id=1, source_target_pairs={{0,8},{8,0},{1,9},{9,1},{2,10},{10,2},{3,11},{11,3},{4,12},{12,4},... | collective-permute-start | bytes 1179656 | tf_op jit(solution)/shard_map/ppermute | solution.py:394
  83.0 29.9 %all-to-all-start = ((bf16[8,2,3,64,256]{4,3,2,1,0:T(8,128)(2,1)}), bf16[8,2,3,64,256]{4,3,2,1,0:T(8,128)(2,1)}, u32[]{:S(2)}, u32[]{:S(2)}) async-start(bf16[8,2,3,64,256]{4,3,2,1,0:T(8,128)(2,1)} %pad_maximum_fusion.6), calls=%async_computation | async-start | bytes 3145728 | tf_op jit(solution)/shard_map/all_to_all | solution.py:230
  87.3 27.4 %copy-start.71 = (bf16[1024]{0:T(1024)(128)(2,1)S(1)}, bf16[1024]{0:T(1024)(128)(2,1)}, u32[]{:S(2)}) copy-start(bf16[1024]{0:T(1024)(128)(2,1)} %param.23) | copy-start | bytes 6148
  87.3 164.3 %all-gather.20.cloned.1.call-start = ((), (), s32[]{:S(2)}) async-start(), calls=%async_computation.20 | async-start | bytes 8912896 | tf_op jit(solution)/shard_map/all_gather | solution.py:536
  142.3 14.8 %all-to-all-start.1 = ((bf16[8,2,64,256]{3,2,1,0:T(8,128)(2,1)}), bf16[8,2,64,256]{3,2,1,0:T(8,128)(2,1)S(1)}, u32[]{:S(2)}, u32[]{:S(2)}) async-start(bf16[8,2,64,256]{3,2,1,0:T(8,128)(2,1)} %get-tuple-element.79), calls=%async_computation.1 | async-start | bytes 1048576 | tf_op jit(solution)/shard_map/all_to_all | solution.py:230
  148.3 6.9 %copy-start.18 = (bf16[1024,1024]{1,0:T(8,128)(2,1)}, bf16[1024,1024]{1,0:T(8,128)(2,1)S(1)}, u32[]{:S(2)}) copy-start(bf16[1024,1024]{1,0:T(8,128)(2,1)S(1)} %constant_dynamic-update-slice_fusion.1) | copy-start | bytes 6291460
  158.5 30.7 %all-to-all-start.2 = ((bf16[8,2,2,64,256]{4,3,2,1,0:T(8,128)(2,1)}), bf16[8,2,2,64,256]{4,3,2,1,0:T(8,128)(2,1)S(1)}, u32[]{:S(2)}, u32[]{:S(2)}) async-start(bf16[8,2,2,64,256]{4,3,2,1,0:T(8,128)(2,1)} %pad_maximum_fusion.10), calls=%async_computation.2 | async-start | bytes 2097152 | tf_op jit(solution)/shard_map/all_to_all | solution.py:230
  162.7 22.0 %collective-permute-start.3 = (bf16[512,512]{1,0:T(8,128)(2,1)}, bf16[512,512]{1,0:T(8,128)(2,1)S(1)}, u32[]{:S(2)}, u32[]{:S(2)}) collective-permute-start(bf16[512,512]{1,0:T(8,128)(2,1)} %bitcast.339), channel_id=1, source_target_pairs={{0,8},{8,0},{1,9},{9,1},{2,10},{10,2},{3,11},{11,3},{4,12},{12,4},... | collective-permute-start | bytes 1572872 | tf_op jit(solution)/shard_map/ppermute | solution.py:394
  172.9 11.8 %copy-start.36 = (bf16[2,256,1024]{2,1,0:T(8,128)(2,1)S(1)}, bf16[2,256,1024]{2,1,0:T(8,128)(2,1)}, u32[]{:S(2)}) copy-start(bf16[2,256,1024]{2,1,0:T(8,128)(2,1)} %get-tuple-element.219) | copy-start | bytes 3145732
  172.9 11.8 %copy-start.42 = (bf16[64,8,2,256]{3,1,2,0:T(8,128)(2,1)S(1)}, bf16[64,8,2,256]{3,1,2,0:T(8,128)(2,1)}, u32[]{:S(2)}) copy-start(bf16[64,8,2,256]{3,1,2,0:T(8,128)(2,1)} %copy.133) | copy-start | bytes 1572868
  189.3 13.9 %all-to-all-start.3 = ((bf16[8,2,1,64,256]{4,3,2,1,0:T(8,128)(2,1)}), bf16[8,2,1,64,256]{4,3,2,1,0:T(8,128)(2,1)}, u32[]{:S(2)}, u32[]{:S(2)}) async-start(bf16[8,2,1,64,256]{4,3,2,1,0:T(8,128)(2,1)} %pad_maximum_fusion.16), calls=%async_computation.3 | async-start | bytes 1048576 | tf_op jit(solution)/shard_map/all_to_all | solution.py:230
  193.4 170.5 %reduce-scatter.4.cloned.1.call-start = ((), (), s32[]{:S(2)}) async-start(), calls=%async_computation.13 | async-start | bytes 9437184 | tf_op jit(solution)/shard_map/reduce_scatter | solution.py:567
  221.2 14.9 %copy-start.2 = (f32[8,2,64,256]{3,2,1,0:T(8,128)}, f32[8,2,64,256]{3,2,1,0:T(8,128)S(1)}, u32[]{:S(2)}) copy-start(f32[8,2,64,256]{3,2,1,0:T(8,128)S(1)} %get-tuple-element.92.wide_ref) | copy-start | bytes 3145732
  221.2 13.8 %copy-start.72 = (bf16[1024]{0:T(1024)(128)(2,1)S(1)}, bf16[1024]{0:T(1024)(128)(2,1)}, u32[]{:S(2)}) copy-start(bf16[1024]{0:T(1024)(128)(2,1)} %param.28) | copy-start | bytes 6148
  234.7 13.1 %copy-start.61 = (bf16[64,8,2,256]{3,1,2,0:T(8,128)(2,1)}, bf16[64,8,2,256]{3,1,2,0:T(8,128)(2,1)S(1)}, u32[]{:S(2)}) copy-start(bf16[64,8,2,256]{3,1,2,0:T(8,128)(2,1)S(1)} %copy.134) | copy-start | bytes 1572868
  234.7 13.0 %collective-permute-start.4 = (bf16[512,512]{1,0:T(8,128)(2,1)S(1)}, bf16[512,512]{1,0:T(8,128)(2,1)S(1)}, u32[]{:S(2)}, u32[]{:S(2)}) collective-permute-start(bf16[512,512]{1,0:T(8,128)(2,1)S(1)} %bitcast.370), channel_id=1, source_target_pairs={{0,8},{8,0},{1,9},{9,1},{2,10},{10,2},{3,11},{11,3},{4,12},{12,4},... | collective-permute-start | bytes 1572872 | tf_op jit(solution)/shard_map/ppermute | solution.py:394
  236.1 11.7 %copy-start.7 = (f32[512,1024]{1,0:T(8,128)S(1)}, f32[512,1024]{1,0:T(8,128)}, u32[]{:S(2)}) copy-start(f32[512,1024]{1,0:T(8,128)} %copy-done.6) | copy-start | bytes 6291460
  266.8 6.0 copy-start.76
  279.5 23.7 %collective-permute-start.5 = (bf16[512,1024]{1,0:T(8,128)(2,1)}, bf16[512,1024]{1,0:T(8,128)(2,1)}, u32[]{:S(2)}, u32[]{:S(2)}) collective-permute-start(bf16[512,1024]{1,0:T(8,128)(2,1)} %fusion.22), channel_id=1, source_target_pairs={{0,8},{8,0},{1,9},{9,1},{2,10},{10,2},{3,11},{11,3},{4,12},{12,4},... | collective-permute-start | bytes 3145736 | tf_op jit(solution)/shard_map/ppermute | solution.py:394
  288.6 17.0 %copy-start.10 = (f32[512,1024]{1,0:T(8,128)S(1)}, f32[512,1024]{1,0:T(8,128)}, u32[]{:S(2)}) copy-start(f32[512,1024]{1,0:T(8,128)} %copy-done.9) | copy-start | bytes 6291460
  305.1 11.5 %collective-permute-start.6 = (bf16[256,1024]{1,0:T(8,128)(2,1)}, bf16[256,1024]{1,0:T(8,128)(2,1)}, u32[]{:S(2)}, u32[]{:S(2)}) collective-permute-start(bf16[256,1024]{1,0:T(8,128)(2,1)} %bitcast.39), channel_id=1, source_target_pairs={{0,8},{8,0},{1,9},{9,1},{2,10},{10,2},{3,11},{11,3},{4,12},{12,4},... | collective-permute-start | bytes 1572872 | tf_op jit(solution)/shard_map/ppermute | solution.py:394
  310.6 19.4 %all-to-all-start.5 = ((bf16[8,2,64,256]{3,2,1,0:T(8,128)(2,1)}), bf16[8,2,64,256]{3,2,1,0:T(8,128)(2,1)S(1)}, u32[]{:S(2)}, u32[]{:S(2)}) async-start(bf16[8,2,64,256]{3,2,1,0:T(8,128)(2,1)} %maximum_bitcast_fusion), calls=%async_computation.5 | async-start | bytes 1048576 | tf_op jit(solution)/shard_map/all_to_all | solution.py:230
  316.3 13.6 %copy-start.3 = (f32[8,2,64,256]{3,2,1,0:T(8,128)S(1)}, f32[8,2,64,256]{3,2,1,0:T(8,128)}, u32[]{:S(2)}) copy-start(f32[8,2,64,256]{3,2,1,0:T(8,128)} %copy-done.2) | copy-start | bytes 3145732
  329.9 31.8 %collective-permute-start.7 = (bf16[256,1024]{1,0:T(8,128)(2,1)}, bf16[256,1024]{1,0:T(8,128)(2,1)S(1)}, u32[]{:S(2)}, u32[]{:S(2)}) collective-permute-start(bf16[256,1024]{1,0:T(8,128)(2,1)} %fusion.44), channel_id=1, source_target_pairs={{0,16},{16,0},{1,17},{17,1},{2,18},{18,2},{3,19},{19,3},{4,20},{20... | collective-permute-start | bytes 1572872 | tf_op jit(solution)/shard_map/ppermute | solution.py:394
  363.9 31.0 %all-to-all-start.6 = ((bf16[8,2,3,64,256]{4,3,2,1,0:T(8,128)(2,1)}), bf16[8,2,3,64,256]{4,3,2,1,0:T(8,128)(2,1)}, u32[]{:S(2)}, u32[]{:S(2)}) async-start(bf16[8,2,3,64,256]{4,3,2,1,0:T(8,128)(2,1)} %pair_backward.2), calls=%async_computation.7 | async-start | bytes 3145728 | tf_op jit(solution)/shard_map/all_to_all | solution.py:230
  368.3 28.7 %copy-start.22 = (bf16[1,4,8,32,1024]{4,3,0,1,2:T(8,128)(2,1)S(1)}, bf16[1,4,8,32,1024]{4,3,0,1,2:T(8,128)(2,1)}, u32[]{:S(2)}) copy-start(bf16[1,4,8,32,1024]{4,3,0,1,2:T(8,128)(2,1)} %get-tuple-element.207) | copy-start | bytes 6291460
  368.3 117.0 %all-gather.12.cloned.1.call-start = ((), (), s32[]{:S(2)}) async-start(), calls=%async_computation.14 | async-start | bytes 4718592 | tf_op jit(solution)/shard_map/all_gather | solution.py:444
  368.4 26.5 %collective-permute-start.8 = (bf16[256,1024]{1,0:T(8,128)(2,1)S(1)}, bf16[256,1024]{1,0:T(8,128)(2,1)}, u32[]{:S(2)}, u32[]{:S(2)}) collective-permute-start(bf16[256,1024]{1,0:T(8,128)(2,1)S(1)} %dynamic-slice_bitcast_fusion), channel_id=1, source_target_pairs={{0,16},{16,0},{1,17},{17,1},{2,18},{18,2},{3,19},{19,3},{4,20},{20... | collective-permute-start | bytes 1572872 | tf_op jit(solution)/shard_map/ppermute | solution.py:394
  397.0 116.6 %reduce-scatter.6.cloned.1.call-start = ((), (), s32[]{:S(2)}) async-start(), calls=%async_computation.15 | async-start | bytes 4718592 | tf_op jit(solution)/shard_map/reduce_scatter | solution.py:567
  406.7 13.6 %collective-permute-start.9 = (bf16[512,512]{1,0:T(8,128)(2,1)}, bf16[512,512]{1,0:T(8,128)(2,1)}, u32[]{:S(2)}, u32[]{:S(2)}) collective-permute-start(bf16[512,512]{1,0:T(8,128)(2,1)} %bitcast.163), channel_id=1, source_target_pairs={{0,8},{8,0},{1,9},{9,1},{2,10},{10,2},{3,11},{11,3},{4,12},{12,4},... | collective-permute-start | bytes 1572872 | tf_op jit(solution)/shard_map/ppermute | solution.py:394
  412.4 7.9 %copy-start.15 = (bf16[1,4,8,32,1024]{4,3,2,1,0:T(8,128)(2,1)S(1)}, bf16[1,4,8,32,1024]{4,3,2,1,0:T(8,128)(2,1)}, u32[]{:S(2)}) copy-start(bf16[1,4,8,32,1024]{4,3,2,1,0:T(8,128)(2,1)} %copy.109) | copy-start | bytes 6291460
  429.2 7.2 %copy-start.43 = (bf16[64,8,2,256]{3,1,2,0:T(8,128)(2,1)S(1)}, bf16[64,8,2,256]{3,1,2,0:T(8,128)(2,1)}, u32[]{:S(2)}) copy-start(bf16[64,8,2,256]{3,1,2,0:T(8,128)(2,1)} %copy.133) | copy-start | bytes 1572868
  430.6 13.6 %copy-start.5 = (f32[8,2,64,256]{3,2,1,0:T(8,128)S(1)}, f32[8,2,64,256]{3,2,1,0:T(8,128)}, u32[]{:S(2)}) copy-start(f32[8,2,64,256]{3,2,1,0:T(8,128)} %copy-done.4) | copy-start | bytes 3145732
  430.6 13.6 %all-to-all-start.7 = ((bf16[8,2,64,256]{3,2,1,0:T(8,128)(2,1)}), bf16[8,2,64,256]{3,2,1,0:T(8,128)(2,1)S(1)}, u32[]{:S(2)}, u32[]{:S(2)}) async-start(bf16[8,2,64,256]{3,2,1,0:T(8,128)(2,1)} %maximum_bitcast_fusion.1), calls=%async_computation.8 | async-start | bytes 1048576 | tf_op jit(solution)/shard_map/all_to_all | solution.py:230
  434.4 50.9 %collective-permute-start.10 = (bf16[512,1024]{1,0:T(8,128)(2,1)S(1)}, bf16[512,1024]{1,0:T(8,128)(2,1)}, u32[]{:S(2)}, u32[]{:S(2)}) collective-permute-start(bf16[512,1024]{1,0:T(8,128)(2,1)S(1)} %convolution_convert_fusion.6), channel_id=1, source_target_pairs={{0,8},{8,0},{1,9},{9,1},{2,10},{10,2},{3,11},{11,3},{4,12},{12,4},... | collective-permute-start | bytes 3145736 | tf_op jit(solution)/shard_map/ppermute | solution.py:394
  434.7 47.9 %collective-permute-start.11 = (bf16[2,256,1024]{2,1,0:T(8,128)(2,1)}, bf16[2,256,1024]{2,1,0:T(8,128)(2,1)}, u32[]{:S(2)}, u32[]{:S(2)}) collective-permute-start(bf16[2,256,1024]{2,1,0:T(8,128)(2,1)} %pad_maximum_fusion.11), channel_id=1, source_target_pairs={{0,8},{8,0},{1,9},{9,1},{2,10},{10,2},{3,11},{11,3},{4,12},{12,4},... | collective-permute-start | bytes 3145736 | tf_op jit(solution)/shard_map/ppermute | solution.py:394
  444.2 38.4 %copy-start.38 = (bf16[2,256,1024]{2,1,0:T(8,128)(2,1)S(1)}, bf16[2,256,1024]{2,1,0:T(8,128)(2,1)}, u32[]{:S(2)}) copy-start(bf16[2,256,1024]{2,1,0:T(8,128)(2,1)} %pad_maximum_fusion.11) | copy-start | bytes 3145732
  485.3 28.2 %all-to-all-start.8 = ((bf16[8,2,3,64,256]{4,3,2,1,0:T(8,128)(2,1)}), bf16[8,2,3,64,256]{4,3,2,1,0:T(8,128)(2,1)}, u32[]{:S(2)}, u32[]{:S(2)}) async-start(bf16[8,2,3,64,256]{4,3,2,1,0:T(8,128)(2,1)} %pair_backward.3), calls=%async_computation.9 | async-start | bytes 3145728 | tf_op jit(solution)/shard_map/all_to_all | solution.py:230
  489.6 97.8 %reduce-scatter.8.cloned.1.call-start = ((), (), s32[]{:S(2)}) async-start(), calls=%async_computation.17 | async-start | bytes 5898240 | tf_op jit(solution)/shard_map/reduce_scatter | solution.py:567
  492.2 20.5 %collective-permute-start.12 = (bf16[256,768]{1,0:T(8,128)(2,1)S(1)}, bf16[256,768]{1,0:T(8,128)(2,1)S(1)}, u32[]{:S(2)}, u32[]{:S(2)}) collective-permute-start(bf16[256,768]{1,0:T(8,128)(2,1)S(1)} %convolution_convert_fusion.14), channel_id=1, source_target_pairs={{0,16},{16,0},{1,17},{17,1},{2,18},{18,2},{3,19},{19,3},{4,20},{20... | collective-permute-start | bytes 1179656 | tf_op jit(solution)/shard_map/ppermute | solution.py:394
  521.7 109.5 %all-gather.14.cloned.1.call-start = ((), (), s32[]{:S(2)}) async-start(), calls=%async_computation.16 | async-start | bytes 2359296 | tf_op jit(solution)/shard_map/all_gather | solution.py:444
  527.1 8.3 %copy-start.29 = (f32[512,1024]{1,0:T(8,128)S(1)}, f32[512,1024]{1,0:T(8,128)}, u32[]{:S(2)}) copy-start(f32[512,1024]{1,0:T(8,128)} %get-tuple-element.199) | copy-start | bytes 6291460
  532.6 19.6 %collective-permute-start.14 = (bf16[256,1024]{1,0:T(8,128)(2,1)}, bf16[256,1024]{1,0:T(8,128)(2,1)S(1)}, u32[]{:S(2)}, u32[]{:S(2)}) collective-permute-start(bf16[256,1024]{1,0:T(8,128)(2,1)} %bitcast.78), channel_id=1, source_target_pairs={{0,8},{8,0},{1,9},{9,1},{2,10},{10,2},{3,11},{11,3},{4,12},{12,4},... | collective-permute-start | bytes 1572872 | tf_op jit(solution)/shard_map/ppermute | solution.py:394
  532.7 17.3 %collective-permute-start.13 = (bf16[128,1024]{1,0:T(8,128)(2,1)S(1)}, bf16[128,1024]{1,0:T(8,128)(2,1)S(1)}, u32[]{:S(2)}, u32[]{:S(2)}) collective-permute-start(bf16[128,1024]{1,0:T(8,128)(2,1)S(1)} %dynamic-slice_bitcast_fusion.2), channel_id=1, source_target_pairs={{0,16},{16,0},{1,17},{17,1},{2,18},{18,2},{3,19},{19,3},{4,20},{20... | collective-permute-start | bytes 786440 | tf_op jit(solution)/shard_map/ppermute | solution.py:394
  550.8 106.3 %all-gather.16.cloned.1.call-start = ((), (), s32[]{:S(2)}) async-start(), calls=%async_computation.18 | async-start | bytes 2949120 | tf_op jit(solution)/shard_map/all_gather | solution.py:444
  555.8 5.1 collective-permute-start.16
  559.0 27.2 %collective-permute-start.15 = (bf16[256,1024]{1,0:T(8,128)(2,1)}, bf16[256,1024]{1,0:T(8,128)(2,1)S(1)}, u32[]{:S(2)}, u32[]{:S(2)}) collective-permute-start(bf16[256,1024]{1,0:T(8,128)(2,1)} %fusion.42), channel_id=1, source_target_pairs={{0,16},{16,0},{1,17},{17,1},{2,18},{18,2},{3,19},{19,3},{4,20},{20... | collective-permute-start | bytes 1572872 | tf_op jit(solution)/shard_map/ppermute | solution.py:394
  573.4 12.8 %collective-permute-start.17 = (bf16[80,256]{1,0:T(8,128)(2,1)S(1)}, bf16[80,256]{1,0:T(8,128)(2,1)S(1)}, u32[]{:S(2)}, u32[]{:S(2)}) collective-permute-start(bf16[80,256]{1,0:T(8,128)(2,1)S(1)} %dynamic-slice_bitcast_fusion.3), channel_id=1, source_target_pairs={{0,16},{16,0},{1,17},{17,1},{2,18},{18,2},{3,19},{19,3},{4,20},{20... | collective-permute-start | bytes 122888 | tf_op jit(solution)/shard_map/ppermute | solution.py:394
  587.4 31.8 %collective-permute-start.19 = (bf16[2,256,1024]{2,1,0:T(8,128)(2,1)S(1)}, bf16[2,256,1024]{2,1,0:T(8,128)(2,1)S(1)}, u32[]{:S(2)}, u32[]{:S(2)}) collective-permute-start(bf16[2,256,1024]{2,1,0:T(8,128)(2,1)S(1)} %pad_maximum_fusion.12), channel_id=1, source_target_pairs={{0,8},{8,0},{1,9},{9,1},{2,10},{10,2},{3,11},{11,3},{4,12},{12,4},... | collective-permute-start | bytes 3145736 | tf_op jit(solution)/shard_map/ppermute | solution.py:394
  588.5 28.5 %collective-permute-start.18 = (bf16[160,1024]{1,0:T(8,128)(2,1)S(1)}, bf16[160,1024]{1,0:T(8,128)(2,1)S(1)}, u32[]{:S(2)}, u32[]{:S(2)}) collective-permute-start(bf16[160,1024]{1,0:T(8,128)(2,1)S(1)} %dynamic-slice_bitcast_fusion.1), channel_id=1, source_target_pairs={{0,16},{16,0},{1,17},{17,1},{2,18},{18,2},{3,19},{19,3},{4,20},{20... | collective-permute-start | bytes 983048 | tf_op jit(solution)/shard_map/ppermute | solution.py:394
  631.2 6.0 slice-start.1
  631.2 18.6 %collective-permute-start.20 = (bf16[2,256,768]{2,1,0:T(8,128)(2,1)}, bf16[2,256,768]{2,1,0:T(8,128)(2,1)}, u32[]{:S(2)}, u32[]{:S(2)}) collective-permute-start(bf16[2,256,768]{2,1,0:T(8,128)(2,1)} %pad_maximum_fusion.15), channel_id=1, source_target_pairs={{0,8},{8,0},{1,9},{9,1},{2,10},{10,2},{3,11},{11,3},{4,12},{12,4},... | collective-permute-start | bytes 2359304 | tf_op jit(solution)/shard_map/ppermute | solution.py:394
  639.1 10.8 %copy-start.41 = (bf16[2,256,768]{2,1,0:T(8,128)(2,1)S(1)}, bf16[2,256,768]{2,1,0:T(8,128)(2,1)}, u32[]{:S(2)}) copy-start(bf16[2,256,768]{2,1,0:T(8,128)(2,1)} %pad_maximum_fusion.15) | copy-start | bytes 2359300
  642.0 9.1 %copy-start.14 = (bf16[2,2,256,1024]{3,2,1,0:T(8,128)(2,1)S(1)}, bf16[2,2,256,1024]{3,2,1,0:T(8,128)(2,1)}, u32[]{:S(2)}) copy-start(bf16[2,2,256,1024]{3,2,1,0:T(8,128)(2,1)} %pad_maximum_fusion.5) | copy-start | bytes 6291460
  661.9 5.8 copy-start.1
  (56 other events, 119.9 us)
Sparse Core Ops, SparseCore 0:
  28.5 26.8 all-gather.9
  69.5 59.3 all-gather.17
  131.3 81.9 all-gather.19
  279.6 73.9 reduce-scatter.3
  397.1 35.6 all-gather.11
  437.0 51.3 reduce-scatter.5
  521.8 57.1 reduce-scatter.7
  581.6 26.9 all-gather.13
  623.2 31.0 all-gather.15
